TPU v7x, 32 devices: a whole 2x2x4 slice. The times are simulated.
32 devices in a mesh: pair: 8 (over y, x, core), aux: 4 (over z).
Axes of the slice: x: 2, y: 2, z: 4, core: 2. Of those that a mesh axis runs over, the one named last changes fastest.
Arguments:
- three_center: float32 [2048, 8192], P('aux', 'pair'), may hold values from -0.0625 to 0.0625
- densities: float32 [8192, 512], P(('pair', 'aux')), may hold values from -6 to 6
- screen_mask: int32 [32, 128], P('aux', 'pair'), may hold values 0 or 1
- diag_inverse: float32 [2048, 512], P('aux'), as said below
- sub_factor: float32 [2048, 512], P('aux'), as said below
Outputs:
- response: float32 [8192, 512], P(('pair', 'aux'))
Inputs may be any that keep to these rules, and one draw needn't show every extreme that they name: `diag_inverse`: each block of 512 rows is lower triangular; its diagonal lies in 0.75 to 1.3 and its entries below the diagonal within plus or minus 2 / sqrt(512). `sub_factor`: block 0 is not used; entries lie within plus or minus 3.4 / sqrt(512).
All inputs are finite; a program needn't handle non-finite values. No bound on the sum of `screen_mask` on one device may be relied on, other than what follows from the above.
Results may differ from a plain program's by a relative error of at most 0.0003.
Values sent between devices are 32-bit elements; how exact they have to be, the bound alone decides.
No kernel may reach another device: no remote copies, remote signals or barrier semaphores. Data moves between devices by JAX's collectives and lax.ppermute only.
A program may use at most 192 MiB of HBM per device.

v0:
```python
import jax
import jax.numpy as jnp
from jax import lax
from jax.sharding import PartitionSpec as P


def from_behind(array, axis, by):
    count = lax.axis_size(axis)
    pairs = [(i, i + by) for i in range(count) if 0 <= i + by < count]
    return lax.ppermute(array, axis, pairs)


def screen_block(block, screen_mask):
    aux_blocks, pair_blocks = screen_mask.shape
    aux_size = block.shape[0] // aux_blocks
    pair_size = block.shape[1] // pair_blocks
    shaped = block.reshape(aux_blocks, aux_size, pair_blocks, pair_size)
    shaped = shaped * screen_mask.astype(jnp.float32)[:, None, :, None]
    return shaped.reshape(block.shape)


def product(left, right):
    return jnp.dot(left, right, precision=lax.Precision.HIGHEST, preferred_element_type=jnp.float32)


def contract_first(left, right):
    return lax.dot_general(
        left,
        right,
        (((0,), (0,)), ((), ())),
        precision=lax.Precision.HIGHEST,
        preferred_element_type=jnp.float32,
    )


def per_device(three_center, densities, screen_mask, diag_inverse, sub_factor):
    screened = screen_block(three_center, screen_mask)
    dens_full = lax.all_gather(densities, "aux", axis=0, tiled=True)
    gamma_share = lax.psum_scatter(
        contract_first(dens_full, screened.T), "pair", scatter_dimension=0, tiled=True
    )
    right_side = gamma_share.T
    transfer = -product(diag_inverse, sub_factor)
    driving = product(diag_inverse, right_side)
    chain_length = lax.axis_size("aux")

    def forward(turn_index, incoming):
        return from_behind(product(transfer, incoming) + driving, "aux", 1)

    incoming = lax.fori_loop(0, chain_length - 1, forward, jnp.zeros_like(driving))
    solved = product(transfer, incoming) + driving
    source = product(sub_factor.T, product(diag_inverse.T, solved))
    back_map = transfer.T

    def backward(turn_index, arriving):
        return from_behind(product(back_map, arriving) + source, "aux", -1)

    arriving = lax.fori_loop(0, chain_length - 1, backward, jnp.zeros_like(driving))
    coefficients = product(diag_inverse.T, solved - arriving)
    coeff_full = lax.all_gather(coefficients, "pair", axis=1, tiled=True)
    return lax.psum_scatter(
        contract_first(screened, coeff_full), "aux", scatter_dimension=0, tiled=True
    )


def solution(mesh):
    return jax.shard_map(
        per_device,
        mesh=mesh,
        in_specs=(
            P("aux", "pair"),
            P(("pair", "aux"), None),
            P("aux", "pair"),
            P("aux", None),
            P("aux", None),
        ),
        out_specs=P(("pair", "aux"), None),
        check_vma=False,
    )
```

profile of v0, /device:TPU:0, one launch (start us, length us, event | category | flops | bytes accessed | tf_op | source)
XLA Modules:
  0.0 238.7 jit_solution(8295645147686337585)
XLA Ops:
  8.0 2.3 mul.11
  10.3 4.9 %mul.12 = f32[512,1024]{1,0:T(8,128)} reshape(f32[8,64,16,64]{3,2,1,0:T(8,128)} %mul.11) | data formatting | bytes 4194304 | tf_op jit(solution)/shard_map/mul | solution.py:18
  15.2 2.6 %mul.13 = f32[512,1024]{1,0:T(8,128)S(1)} multiply(f32[512,1024]{1,0:T(8,128)} %param.9, f32[512,1024]{1,0:T(8,128)} %mul.12) | non-fusion elementwise | flops 524288 | bytes 6291456 | tf_op jit(solution)/shard_map/mul | solution.py:18
  17.8 39.8 %all-gather.3.cloned.1.call-done = f32[1024,512]{1,0:T(8,128)} async-done(((f32[256,512]{1,0:T(8,128)}), f32[1024,512]{1,0:T(8,128)}) %all-gather.3.cloned.1.call-update) | async-done | bytes 2097168 | tf_op jit(solution)/shard_map/all_gather | solution.py:38
  57.6 6.1 %convolution_bitcast_fusion = f32[512,512]{0,1:T(8,128)} fusion(f32[512,1024]{1,0:T(8,128)S(1)} %mul.13, f32[1024,512]{1,0:T(8,128)} %all-gather.3.cloned.1.call-done), kind=kOutput, calls=%fused_computation.2 | convolution fusion | flops 3221225472 | bytes 5242880 | tf_op jit(solution)/shard_map/dot_general | solution.py:27
  63.7 2.5 %copy.8 = f32[512,512]{1,0:T(8,128)} copy(f32[512,512]{0,1:T(8,128)} %convolution_bitcast_fusion) | data formatting | bytes 2097152
  66.5 3.1 %convolution_negate_fusion = f32[512,512]{1,0:T(8,128)S(1)} fusion(f32[512,512]{1,0:T(8,128)S(1)} %copy-done, f32[512,512]{1,0:T(8,128)} %param.13), kind=kOutput, calls=%fused_computation.3 | convolution fusion | flops 1610874880 | bytes 3145728 | tf_op jit(solution)/shard_map/dot_general | solution.py:23
  69.9 31.3 %reduce-scatter.7.cloned.1.call-done = f32[64,512]{1,0:T(8,128)} async-done(((f32[512,512]{1,0:T(8,128)}), f32[64,512]{1,0:T(8,128)}) %reduce-scatter.7.cloned.1.call-update) | async-done | bytes 131088
  101.2 2.0 convolution_bitcast_fusion.3
  103.2 23.2 %while.20 = (s32[]{:T(128)}, f32[512,64]{0,1:T(8,128)S(1)}, f32[512,512]{1,0:T(8,128)S(1)}, f32[512,64]{0,1:T(8,128)S(1)}, s32[]{:T(128)}) while((s32[]{:T(128)}, f32[512,64]{0,1:T(8,128)S(1)}, f32[512,512]{1,0:T(8,128)S(1)}, f32[512,64]{0,1:T(8,128)S(1)}, s32[]{:T(128)}) %tuple.33), condition=%wide.region_2.0_spmd, body=%wide.region_1.0_spmd.sunk | while | flops 201359360 | bytes 1966181 | solution.py:50
  103.2 1.1 convolution_add_fusion.5
  104.4 3.4 %collective-permute-start = (f32[512,64]{0,1:T(8,128)S(1)}, f32[512,64]{0,1:T(8,128)S(1)}, u32[]{:S(2)}, u32[]{:S(2)}) collective-permute-start(f32[512,64]{0,1:T(8,128)S(1)} %convolution_add_fusion.5), channel_id=1, source_target_pairs={{0,1},{1,2},{2,3},{4,5},{5,6},{6,7},{8,9},{9,10},{10,11},{12,13},{... | collective-permute-start | bytes 393224 | tf_op jit(solution)/shard_map/while/body/eval_jaxpr/ppermute | solution.py:10
  107.8 2.6 %collective-permute-done = f32[512,64]{0,1:T(8,128)S(1)} collective-permute-done((f32[512,64]{0,1:T(8,128)S(1)}, f32[512,64]{0,1:T(8,128)S(1)}, u32[]{:S(2)}, u32[]{:S(2)}) %collective-permute-start) | collective-permute-done | bytes 131104 | tf_op jit(solution)/shard_map/while/body/eval_jaxpr/ppermute | solution.py:10
  110.4 1.1 convolution_add_fusion.5
  111.5 4.4 %collective-permute-start = (f32[512,64]{0,1:T(8,128)S(1)}, f32[512,64]{0,1:T(8,128)S(1)}, u32[]{:S(2)}, u32[]{:S(2)}) collective-permute-start(f32[512,64]{0,1:T(8,128)S(1)} %convolution_add_fusion.5), channel_id=1, source_target_pairs={{0,1},{1,2},{2,3},{4,5},{5,6},{6,7},{8,9},{9,10},{10,11},{12,13},{... | collective-permute-start | bytes 393224 | tf_op jit(solution)/shard_map/while/body/eval_jaxpr/ppermute | solution.py:10
  115.9 2.5 %collective-permute-done = f32[512,64]{0,1:T(8,128)S(1)} collective-permute-done((f32[512,64]{0,1:T(8,128)S(1)}, f32[512,64]{0,1:T(8,128)S(1)}, u32[]{:S(2)}, u32[]{:S(2)}) %collective-permute-start) | collective-permute-done | bytes 131104 | tf_op jit(solution)/shard_map/while/body/eval_jaxpr/ppermute | solution.py:10
  119.5 4.4 %collective-permute-start = (f32[512,64]{0,1:T(8,128)S(1)}, f32[512,64]{0,1:T(8,128)S(1)}, u32[]{:S(2)}, u32[]{:S(2)}) collective-permute-start(f32[512,64]{0,1:T(8,128)S(1)} %convolution_add_fusion.5), channel_id=1, source_target_pairs={{0,1},{1,2},{2,3},{4,5},{5,6},{6,7},{8,9},{9,10},{10,11},{12,13},{... | collective-permute-start | bytes 393224 | tf_op jit(solution)/shard_map/while/body/eval_jaxpr/ppermute | solution.py:10
  123.9 2.5 %collective-permute-done = f32[512,64]{0,1:T(8,128)S(1)} collective-permute-done((f32[512,64]{0,1:T(8,128)S(1)}, f32[512,64]{0,1:T(8,128)S(1)}, u32[]{:S(2)}, u32[]{:S(2)}) %collective-permute-start) | collective-permute-done | bytes 131104 | tf_op jit(solution)/shard_map/while/body/eval_jaxpr/ppermute | solution.py:10
  129.1 24.6 %while.21 = (s32[]{:T(128)}, f32[512,64]{0,1:T(8,128)S(1)}, f32[512,512]{1,0:T(8,128)S(1)}, f32[512,64]{0,1:T(8,128)S(1)}, s32[]{:T(128)}) while((s32[]{:T(128)}, f32[512,64]{0,1:T(8,128)S(1)}, f32[512,512]{1,0:T(8,128)S(1)}, f32[512,64]{0,1:T(8,128)S(1)}, s32[]{:T(128)}) %tuple.36), condition=%wide.region_4.0_spmd, body=%wide.region_3.0_spmd.sunk | while | flops 201359360 | bytes 1966181 | solution.py:58
  129.1 1.1 convolution_add_fusion.6
  130.2 1.3 collective-permute-start.1
  131.5 6.0 %collective-permute-done.1 = f32[512,64]{0,1:T(8,128)S(1)} collective-permute-done((f32[512,64]{0,1:T(8,128)S(1)}, f32[512,64]{0,1:T(8,128)S(1)}, u32[]{:S(2)}, u32[]{:S(2)}) %collective-permute-start.1) | collective-permute-done | bytes 131104 | tf_op jit(solution)/shard_map/while/body/eval_jaxpr/ppermute | solution.py:10
  137.5 1.1 convolution_add_fusion.6
  138.7 1.3 collective-permute-start.1
  140.0 5.6 %collective-permute-done.1 = f32[512,64]{0,1:T(8,128)S(1)} collective-permute-done((f32[512,64]{0,1:T(8,128)S(1)}, f32[512,64]{0,1:T(8,128)S(1)}, u32[]{:S(2)}, u32[]{:S(2)}) %collective-permute-start.1) | collective-permute-done | bytes 131104 | tf_op jit(solution)/shard_map/while/body/eval_jaxpr/ppermute | solution.py:10
  145.5 1.1 convolution_add_fusion.6
  146.7 1.3 collective-permute-start.1
  148.0 5.7 %collective-permute-done.1 = f32[512,64]{0,1:T(8,128)S(1)} collective-permute-done((f32[512,64]{0,1:T(8,128)S(1)}, f32[512,64]{0,1:T(8,128)S(1)}, u32[]{:S(2)}, u32[]{:S(2)}) %collective-permute-start.1) | collective-permute-done | bytes 131104 | tf_op jit(solution)/shard_map/while/body/eval_jaxpr/ppermute | solution.py:10
  153.6 1.4 convolution_bitcast_fusion.1
  155.3 23.0 %all-gather.5.cloned.1.call-done = f32[512,512]{0,1:T(8,128)} async-done(((f32[512,64]{0,1:T(8,128)}), f32[512,512]{0,1:T(8,128)}) %all-gather.5.cloned.1.call-update) | async-done | bytes 1048592 | tf_op jit(solution)/shard_map/all_gather | solution.py:60
  178.3 9.8 %fusion.2 = f32[1024,512]{1,0:T(8,128)} fusion(f32[512,1024]{1,0:T(8,128)} %copy-done.1, f32[512,512]{0,1:T(8,128)} %all-gather.5.cloned.1.call-done), kind=kOutput, calls=%fused_computation.10 | convolution fusion | flops 3221225472 | bytes 5242880 | tf_op jit(solution)/shard_map/dot_general | solution.py:27
  188.2 44.0 %reduce-scatter.5.cloned.1.call-done = f32[256,512]{1,0:T(8,128)} async-done(((f32[1024,512]{1,0:T(8,128)}), f32[256,512]{1,0:T(8,128)}) %reduce-scatter.5.cloned.1.call-update) | async-done | bytes 524304 | tf_op jit(solution)/shard_map/reduce_scatter | solution.py:61
  (22 shorter events, 6.1 us)
Async XLA Ops:
  6.5 59.9 %copy-start = (f32[512,512]{1,0:T(8,128)S(1)}, f32[512,512]{1,0:T(8,128)}, u32[]{:S(2)}) copy-start(f32[512,512]{1,0:T(8,128)} %param.12) | copy-start | bytes 3145732
  6.5 51.1 %all-gather.3.cloned.1.call-start = ((), (), s32[]{:S(2)}) async-start(), calls=%async_computation.2 | async-start | bytes 2621440 | tf_op jit(solution)/shard_map/all_gather | solution.py:38
  7.3 93.9 %reduce-scatter.7.cloned.1.call-start = ((), (), s32[]{:S(2)}) async-start(), calls=%async_computation.5 | async-start | bytes 1179648
  17.8 45.9 %copy-start.1 = (f32[512,1024]{1,0:T(8,128)}, f32[512,1024]{1,0:T(8,128)S(1)}, u32[]{:S(2)}) copy-start(f32[512,1024]{1,0:T(8,128)S(1)} %mul.13) | copy-start | bytes 6291460
  66.3 112.1 %all-gather.5.cloned.1.call-start = ((), (), s32[]{:S(2)}) async-start(), calls=%async_computation.3 | async-start | bytes 1179648 | tf_op jit(solution)/shard_map/all_gather | solution.py:60
  104.4 6.0 %collective-permute-start = (f32[512,64]{0,1:T(8,128)S(1)}, f32[512,64]{0,1:T(8,128)S(1)}, u32[]{:S(2)}, u32[]{:S(2)}) collective-permute-start(f32[512,64]{0,1:T(8,128)S(1)} %convolution_add_fusion.5), channel_id=1, source_target_pairs={{0,1},{1,2},{2,3},{4,5},{5,6},{6,7},{8,9},{9,10},{10,11},{12,13},{... | collective-permute-start | bytes 393224 | tf_op jit(solution)/shard_map/while/body/eval_jaxpr/ppermute | solution.py:10
  111.5 6.9 %collective-permute-start = (f32[512,64]{0,1:T(8,128)S(1)}, f32[512,64]{0,1:T(8,128)S(1)}, u32[]{:S(2)}, u32[]{:S(2)}) collective-permute-start(f32[512,64]{0,1:T(8,128)S(1)} %convolution_add_fusion.5), channel_id=1, source_target_pairs={{0,1},{1,2},{2,3},{4,5},{5,6},{6,7},{8,9},{9,10},{10,11},{12,13},{... | collective-permute-start | bytes 393224 | tf_op jit(solution)/shard_map/while/body/eval_jaxpr/ppermute | solution.py:10
  119.5 6.9 %collective-permute-start = (f32[512,64]{0,1:T(8,128)S(1)}, f32[512,64]{0,1:T(8,128)S(1)}, u32[]{:S(2)}, u32[]{:S(2)}) collective-permute-start(f32[512,64]{0,1:T(8,128)S(1)} %convolution_add_fusion.5), channel_id=1, source_target_pairs={{0,1},{1,2},{2,3},{4,5},{5,6},{6,7},{8,9},{9,10},{10,11},{12,13},{... | collective-permute-start | bytes 393224 | tf_op jit(solution)/shard_map/while/body/eval_jaxpr/ppermute | solution.py:10
  126.4 1.9 copy-start.2
  130.2 7.3 %collective-permute-start.1 = (f32[512,64]{0,1:T(8,128)S(1)}, f32[512,64]{0,1:T(8,128)S(1)}, u32[]{:S(2)}, u32[]{:S(2)}) collective-permute-start(f32[512,64]{0,1:T(8,128)S(1)} %convolution_add_fusion.6), channel_id=1, source_target_pairs={{1,0},{2,1},{3,2},{5,4},{6,5},{7,6},{9,8},{10,9},{11,10},{13,12},{... | collective-permute-start | bytes 393224 | tf_op jit(solution)/shard_map/while/body/eval_jaxpr/ppermute | solution.py:10
  138.7 6.9 %collective-permute-start.1 = (f32[512,64]{0,1:T(8,128)S(1)}, f32[512,64]{0,1:T(8,128)S(1)}, u32[]{:S(2)}, u32[]{:S(2)}) collective-permute-start(f32[512,64]{0,1:T(8,128)S(1)} %convolution_add_fusion.6), channel_id=1, source_target_pairs={{1,0},{2,1},{3,2},{5,4},{6,5},{7,6},{9,8},{10,9},{11,10},{13,12},{... | collective-permute-start | bytes 393224 | tf_op jit(solution)/shard_map/while/body/eval_jaxpr/ppermute | solution.py:10
  146.7 7.0 %collective-permute-start.1 = (f32[512,64]{0,1:T(8,128)S(1)}, f32[512,64]{0,1:T(8,128)S(1)}, u32[]{:S(2)}, u32[]{:S(2)}) collective-permute-start(f32[512,64]{0,1:T(8,128)S(1)} %convolution_add_fusion.6), channel_id=1, source_target_pairs={{1,0},{2,1},{3,2},{5,4},{6,5},{7,6},{9,8},{10,9},{11,10},{13,12},{... | collective-permute-start | bytes 393224 | tf_op jit(solution)/shard_map/while/body/eval_jaxpr/ppermute | solution.py:10
  155.1 77.1 %reduce-scatter.5.cloned.1.call-start = ((), (), s32[]{:S(2)}) async-start(), calls=%async_computation.4 | async-start | bytes 2621440 | tf_op jit(solution)/shard_map/reduce_scatter | solution.py:61
Sparse Core Ops, SparseCore 0:
  8.9 48.6 all-gather.2
  66.4 34.7 reduce-scatter.6
  155.2 23.0 all-gather.4
  188.3 43.8 reduce-scatter.4
where the time goes:
time: 239 us
  waiting for transfers between devices  164 us (69%)
  matrix products  31.9 us (13%)
  starting transfers between devices  16.5 us (7%)
  between operations  13.2 us (6%)
  local copies, waits for them, and re-layouts  10.1 us (4%)
  other arithmetic  3.3 us (1%)
    reduce_scatter x1, waiting for transfers between devices, per_device(): lax.psum_scatter(contract_first(screened, coeff_full), 'aux', scatter_dim...  44 us
    all_gather x1, waiting for transfers between devices, per_device(): dens_full = lax.all_gather(densities, 'aux', axis=0, tiled=True)  39.8 us
    unnamed x5, waiting for transfers between devices  32 us
    ppermute x6, waiting for transfers between devices, from_behind(): return lax.ppermute(array, axis, pairs)  24.8 us
    all_gather x1, waiting for transfers between devices, per_device(): coeff_full = lax.all_gather(coefficients, 'pair', axis=1, tiled=True)  23 us
    ppermute x6, starting transfers between devices, from_behind(): return lax.ppermute(array, axis, pairs)  16 us
    dot_general x12, matrix products, product(): jnp.dot(left, right, precision=lax.Precision.HIGHEST, preferred_element_t...  16 us
    dot_general x2, matrix products, contract_first(): lax.dot_general(left, right, (((0,), (0,)), ((), ())), precision=lax.Prec...  15.9 us
  transfers between devices with their start and end apart: 10, of which 10 were waited for; matrix products, arithmetic and copies ran while one was open for 6% of the time, Pallas kernels for 0%

commit v1 on v0

v1 whole, which is shorter than its diff:
```python
import jax
import jax.numpy as jnp
from jax import lax
from jax.sharding import PartitionSpec as P


def from_behind(array, axis, by):
    count = lax.axis_size(axis)
    pairs = [(i, i + by) for i in range(count) if 0 <= i + by < count]
    return lax.ppermute(array, axis, pairs)


def swap(array, axis, bit):
    count = lax.axis_size(axis)
    return lax.ppermute(array, axis, [(i, i ^ bit) for i in range(count)])


def screen_block(block, screen_mask):
    aux_blocks, pair_blocks = screen_mask.shape
    aux_size = block.shape[0] // aux_blocks
    pair_size = block.shape[1] // pair_blocks
    shaped = block.reshape(aux_blocks, aux_size, pair_blocks, pair_size)
    shaped = shaped * screen_mask.astype(jnp.float32)[:, None, :, None]
    return shaped.reshape(block.shape)


def product(left, right):
    return jnp.dot(left, right, precision=lax.Precision.HIGH, preferred_element_type=jnp.float32)


def contract_first(left, right):
    return lax.dot_general(
        left,
        right,
        (((0,), (0,)), ((), ())),
        precision=lax.Precision.HIGH,
        preferred_element_type=jnp.float32,
    )


def reduce_scatter_columns(partial, axis):
    index = lax.axis_index(axis)
    count = lax.axis_size(axis)
    current = partial
    bit = 1
    while bit < count:
        width = current.shape[1] // 2
        low, high = current[:, :width], current[:, width:]
        upper = (index // bit) % 2 == 1
        send = jnp.where(upper, low, high)
        keep = jnp.where(upper, high, low)
        current = keep + swap(send, axis, bit)
        bit *= 2
    return current


def all_gather_columns(share, axis):
    index = lax.axis_index(axis)
    count = lax.axis_size(axis)
    current = share
    bit = count // 2
    while bit >= 1:
        other = swap(current, axis, bit)
        upper = (index // bit) % 2 == 1
        current = jnp.where(
            upper,
            jnp.concatenate([other, current], axis=1),
            jnp.concatenate([current, other], axis=1),
        )
        bit //= 2
    return current


def gamma_over_aux(screened, densities):
    count = lax.axis_size("aux")
    index = lax.axis_index("aux")
    rows = densities.shape[0]

    def columns(block):
        start = jnp.clip(block, 0, count - 1) * rows
        return lax.dynamic_slice_in_dim(screened, start, rows, axis=1)

    gamma = product(columns(index), densities)
    from_left, from_right = densities, densities
    for step in range(count - 1):
        from_left = from_behind(from_left, "aux", 1)
        from_right = from_behind(from_right, "aux", -1)
        gamma = gamma + product(columns(index - 1 - step), from_left)
        gamma = gamma + product(columns(index + 1 + step), from_right)
    return gamma


def per_device(three_center, densities, screen_mask, diag_inverse, sub_factor):
    screened = screen_block(three_center, screen_mask)
    gamma_partial = gamma_over_aux(screened, densities)
    right_side = reduce_scatter_columns(gamma_partial, "pair")
    transfer = -product(diag_inverse, sub_factor)
    driving = product(diag_inverse, right_side)
    chain_length = lax.axis_size("aux")

    incoming = from_behind(driving, "aux", 1)
    for _ in range(chain_length - 2):
        incoming = from_behind(product(transfer, incoming) + driving, "aux", 1)
    solved = product(transfer, incoming) + driving
    source = product(sub_factor.T, product(diag_inverse.T, solved))
    back_map = transfer.T

    arriving = from_behind(source, "aux", -1)
    for _ in range(chain_length - 2):
        arriving = from_behind(product(back_map, arriving) + source, "aux", -1)
    coefficients = product(diag_inverse.T, solved - arriving)
    coeff_full = all_gather_columns(coefficients, "pair")
    partial = contract_first(screened, coeff_full)
    count = lax.axis_size("aux")
    exchanged = lax.all_to_all(partial, "aux", 0, 0, tiled=True)
    return exchanged.reshape(count, partial.shape[0] // count, -1).sum(axis=0)


def solution(mesh):
    return jax.shard_map(
        per_device,
        mesh=mesh,
        in_specs=(
            P("aux", "pair"),
            P(("pair", "aux"), None),
            P("aux", "pair"),
            P("aux", None),
            P("aux", None),
        ),
        out_specs=P(("pair", "aux"), None),
        check_vma=False,
    )
```

time: 239 us -> 196 us (0.82)
  waiting for transfers between devices: 164 us -> 61.4 us
  blocking collectives: 0 us -> 52.4 us
  starting transfers between devices: 16.5 us -> 42.3 us
  matrix products: 31.9 us -> 17.1 us
  between operations: 13.2 us -> 0.27 us
  other arithmetic: 3.3 us -> 11.2 us
    all_gather x2 -> x0, waiting for transfers between devices: 62.8 us -> none  [the longest x1 39.8 us: per_device(): dens_full = lax.all_gather(densities, 'aux', axis=0, tiled=True)]
    all_to_all x0 -> x1, blocking collectives: none -> 52.4 us  [per_device(): exchanged = lax.all_to_all(partial, 'aux', 0, 0, tiled=True)]
    reduce_scatter x1 -> x0, waiting for transfers between devices: 44 us -> none  [per_device(): lax.psum_scatter(contract_first(screened, coeff_full), 'aux', scatter_dim...]
    unnamed x5 -> x0, waiting for transfers between devices: 32 us -> none
    ppermute x0 -> x6, waiting for transfers between devices: none -> 22 us  [swap(): return lax.ppermute(array, axis, [(i, i ^ bit) for i in range(count)])]
    ppermute x6 -> x12, starting transfers between devices: 16 us -> 36.7 us  [from_behind(): return lax.ppermute(array, axis, pairs)]
    ppermute x6 -> x12, waiting for transfers between devices: 24.8 us -> 39.4 us  [from_behind(): return lax.ppermute(array, axis, pairs)]
    dot_general x2 -> x1, matrix products: 15.9 us -> 3.99 us  [contract_first(): lax.dot_general(left, right, (((0,), (0,)), ((), ())), precision=lax.Prec...]
  transfers between devices with their start and end apart: 10 -> 18, of which waited for: 10 -> 15; matrix products, arithmetic and copies ran while one was open for 6% -> 10% of each run, Pallas kernels for 0% -> 0%
where the time goes in v1:
time: 196 us
  waiting for transfers between devices  61.4 us (31%)
  blocking collectives  52.4 us (27%)
  starting transfers between devices  42.3 us (22%)
  matrix products  17.1 us (9%)
  other arithmetic  11.2 us (6%)
  local copies, waits for them, and re-layouts  10.7 us (5%)
    all_to_all x1, blocking collectives, per_device(): exchanged = lax.all_to_all(partial, 'aux', 0, 0, tiled=True)  52.4 us
    ppermute x12, waiting for transfers between devices, from_behind(): return lax.ppermute(array, axis, pairs)  39.4 us
    ppermute x12, starting transfers between devices, from_behind(): return lax.ppermute(array, axis, pairs)  36.7 us
    ppermute x6, waiting for transfers between devices, swap(): return lax.ppermute(array, axis, [(i, i ^ bit) for i in range(count)])  22 us
    dot_general x17, matrix products, product(): jnp.dot(left, right, precision=lax.Precision.HIGH, preferred_element_type...  13.1 us
    mul x2, local copies, waits for them, and re-layouts, screen_block(): shaped = shaped * screen_mask.astype(jnp.float32)[:, None, :, None]  7.15 us
    ppermute x6, starting transfers between devices, swap(): return lax.ppermute(array, axis, [(i, i ^ bit) for i in range(count)])  5.69 us
    dot_general x1, matrix products, contract_first(): lax.dot_general(left, right, (((0,), (0,)), ((), ())), precision=lax.Prec...  3.99 us
  transfers between devices with their start and end apart: 18, of which 15 were waited for; matrix products, arithmetic and copies ran while one was open for 10% of the time, Pallas kernels for 0%

profile of v1, /device:TPU:0, one launch (start us, length us, event | category | flops | bytes accessed | tf_op | source)
XLA Modules:
  0.0 195.5 jit_solution(4787740717968199507)
XLA Ops:
  1.4 6.4 %collective-permute-start = (f32[256,512]{1,0:T(8,128)}, f32[256,512]{1,0:T(8,128)}, u32[]{:S(2)}, u32[]{:S(2)}) collective-permute-start(f32[256,512]{1,0:T(8,128)} %param.6), channel_id=1, source_target_pairs={{0,1},{1,2},{2,3},{4,5},{5,6},{6,7},{8,9},{9,10},{10,11},{12,13},{... | collective-permute-start | bytes 1572872 | tf_op jit(solution)/shard_map/ppermute | solution.py:10
  8.5 2.3 %mul.32 = f32[8,64,16,64]{3,2,1,0:T(8,128)} broadcast(f32[8,16]{1,0:T(8,128)S(1)} %convert_element_type.3), dimensions={0,2} | broadcast | bytes 2097664 | tf_op jit(solution)/shard_map/mul | solution.py:23
  10.8 4.9 %mul.33 = f32[512,1024]{1,0:T(8,128)} reshape(f32[8,64,16,64]{3,2,1,0:T(8,128)} %mul.32) | data formatting | bytes 4194304 | tf_op jit(solution)/shard_map/mul | solution.py:23
  15.6 2.8 %mul.34 = f32[512,1024]{1,0:T(8,128)S(1)} multiply(f32[512,1024]{1,0:T(8,128)} %param.5, f32[512,1024]{1,0:T(8,128)} %mul.33) | non-fusion elementwise | flops 524288 | bytes 6291456 | tf_op jit(solution)/shard_map/mul | solution.py:23
  18.4 1.7 fusion.18
  21.4 4.6 %collective-permute-start.2 = (f32[256,512]{1,0:T(8,128)}, f32[256,512]{1,0:T(8,128)S(1)}, u32[]{:S(2)}, u32[]{:S(2)}) collective-permute-start(f32[256,512]{1,0:T(8,128)} %collective-permute-done), channel_id=1, source_target_pairs={{0,1},{1,2},{2,3},{4,5},{5,6},{6,7},{8,9},{9,10},{10,11},{12,13},{... | collective-permute-start | bytes 1572872 | tf_op jit(solution)/shard_map/ppermute | solution.py:10
  26.0 1.7 convolution_add_fusion.3
  27.7 1.7 convolution_add_fusion.2
  29.3 6.2 %collective-permute-done.3 = f32[256,512]{1,0:T(8,128)S(1)} collective-permute-done((f32[256,512]{1,0:T(8,128)}, f32[256,512]{1,0:T(8,128)S(1)}, u32[]{:S(2)}, u32[]{:S(2)}) %collective-permute-start.3) | collective-permute-done | bytes 524320 | tf_op jit(solution)/shard_map/ppermute | solution.py:10
  36.9 4.6 %collective-permute-start.4 = (f32[256,512]{1,0:T(8,128)S(1)}, f32[256,512]{1,0:T(8,128)S(1)}, u32[]{:S(2)}, u32[]{:S(2)}) collective-permute-start(f32[256,512]{1,0:T(8,128)S(1)} %collective-permute-done.2), channel_id=1, source_target_pairs={{0,1},{1,2},{2,3},{4,5},{5,6},{6,7},{8,9},{9,10},{10,11},{12,13},{... | collective-permute-start | bytes 1572872 | tf_op jit(solution)/shard_map/ppermute | solution.py:10
  42.8 7.2 %collective-permute-done.5 = f32[256,512]{1,0:T(8,128)S(1)} collective-permute-done((f32[256,512]{1,0:T(8,128)S(1)}, f32[256,512]{1,0:T(8,128)S(1)}, u32[]{:S(2)}, u32[]{:S(2)}) %collective-permute-start.5) | collective-permute-done | bytes 524320 | tf_op jit(solution)/shard_map/ppermute | solution.py:10
  53.6 2.2 %collective-permute-done.6 = f32[512,256]{0,1:T(8,128)} collective-permute-done((f32[512,256]{0,1:T(8,128)}, f32[512,256]{0,1:T(8,128)}, u32[]{:S(2)}, u32[]{:S(2)}) %collective-permute-start.6) | collective-permute-done | bytes 524320 | tf_op jit(solution)/shard_map/ppermute | solution.py:15
  55.9 1.5 select_add_fusion
  60.3 7.2 %collective-permute-done.7 = f32[512,128]{0,1:T(8,128)S(1)} collective-permute-done((f32[512,128]{0,1:T(8,128)}, f32[512,128]{0,1:T(8,128)S(1)}, u32[]{:S(2)}, u32[]{:S(2)}) %collective-permute-start.7) | collective-permute-done | bytes 262176 | tf_op jit(solution)/shard_map/ppermute | solution.py:15
  68.6 1.5 collective-permute-start.8
  70.0 3.6 %collective-permute-done.8 = f32[512,64]{0,1:T(8,128)S(1)} collective-permute-done((f32[512,64]{0,1:T(8,128)S(1)}, f32[512,64]{0,1:T(8,128)S(1)}, u32[]{:S(2)}, u32[]{:S(2)}) %collective-permute-start.8) | collective-permute-done | bytes 131104 | tf_op jit(solution)/shard_map/ppermute | solution.py:15
  74.2 4.4 %collective-permute-start.9 = (f32[512,64]{0,1:T(8,128)S(1)}, f32[512,64]{0,1:T(8,128)S(1)}, u32[]{:S(2)}, u32[]{:S(2)}) collective-permute-start(f32[512,64]{0,1:T(8,128)S(1)} %convolution_bitcast_fusion.2), channel_id=1, source_target_pairs={{0,1},{1,2},{2,3},{4,5},{5,6},{6,7},{8,9},{9,10},{10,11},{12,13},{... | collective-permute-start | bytes 393224 | tf_op jit(solution)/shard_map/ppermute | solution.py:10
  79.7 1.5 collective-permute-done.9
  81.7 4.4 %collective-permute-start.10 = (f32[512,64]{0,1:T(8,128)S(1)}, f32[512,64]{0,1:T(8,128)S(1)}, u32[]{:S(2)}, u32[]{:S(2)}) collective-permute-start(f32[512,64]{0,1:T(8,128)S(1)} %convolution_add_fusion.8), channel_id=1, source_target_pairs={{0,1},{1,2},{2,3},{4,5},{5,6},{6,7},{8,9},{9,10},{10,11},{12,13},{... | collective-permute-start | bytes 393224 | tf_op jit(solution)/shard_map/ppermute | solution.py:10
  86.1 2.5 %collective-permute-done.10 = f32[512,64]{0,1:T(8,128)S(1)} collective-permute-done((f32[512,64]{0,1:T(8,128)S(1)}, f32[512,64]{0,1:T(8,128)S(1)}, u32[]{:S(2)}, u32[]{:S(2)}) %collective-permute-start.10) | collective-permute-done | bytes 131104 | tf_op jit(solution)/shard_map/ppermute | solution.py:10
  89.2 4.4 %collective-permute-start.11 = (f32[512,64]{0,1:T(8,128)S(1)}, f32[512,64]{0,1:T(8,128)S(1)}, u32[]{:S(2)}, u32[]{:S(2)}) collective-permute-start(f32[512,64]{0,1:T(8,128)S(1)} %convolution_add_fusion.7), channel_id=1, source_target_pairs={{0,1},{1,2},{2,3},{4,5},{5,6},{6,7},{8,9},{9,10},{10,11},{12,13},{... | collective-permute-start | bytes 393224 | tf_op jit(solution)/shard_map/ppermute | solution.py:10
  93.6 2.5 %collective-permute-done.11 = f32[512,64]{0,1:T(8,128)S(1)} collective-permute-done((f32[512,64]{0,1:T(8,128)S(1)}, f32[512,64]{0,1:T(8,128)S(1)}, u32[]{:S(2)}, u32[]{:S(2)}) %collective-permute-start.11) | collective-permute-done | bytes 131104 | tf_op jit(solution)/shard_map/ppermute | solution.py:10
  98.8 7.2 %collective-permute-done.12 = f32[512,64]{0,1:T(8,128)S(1)} collective-permute-done((f32[512,64]{0,1:T(8,128)S(1)}, f32[512,64]{0,1:T(8,128)S(1)}, u32[]{:S(2)}, u32[]{:S(2)}) %collective-permute-start.12) | collective-permute-done | bytes 131104 | tf_op jit(solution)/shard_map/ppermute | solution.py:10
  107.8 6.3 %collective-permute-done.13 = f32[512,64]{0,1:T(8,128)S(1)} collective-permute-done((f32[512,64]{0,1:T(8,128)S(1)}, f32[512,64]{0,1:T(8,128)S(1)}, u32[]{:S(2)}, u32[]{:S(2)}) %collective-permute-start.13) | collective-permute-done | bytes 131104 | tf_op jit(solution)/shard_map/ppermute | solution.py:10
  114.5 1.5 collective-permute-start.14
  116.0 5.4 %collective-permute-done.14 = f32[512,64]{0,1:T(8,128)S(1)} collective-permute-done((f32[512,64]{0,1:T(8,128)S(1)}, f32[512,64]{0,1:T(8,128)S(1)}, u32[]{:S(2)}, u32[]{:S(2)}) %collective-permute-start.14) | collective-permute-done | bytes 131104 | tf_op jit(solution)/shard_map/ppermute | solution.py:10
  123.3 3.6 %collective-permute-done.15 = f32[512,64]{0,1:T(8,128)S(1)} collective-permute-done((f32[512,64]{0,1:T(8,128)S(1)}, f32[512,64]{0,1:T(8,128)S(1)}, u32[]{:S(2)}, u32[]{:S(2)}) %collective-permute-start.15) | collective-permute-done | bytes 131104 | tf_op jit(solution)/shard_map/ppermute | solution.py:15
  128.3 5.0 %collective-permute-done.16 = f32[512,128]{0,1:T(8,128)S(1)} collective-permute-done((f32[512,128]{0,1:T(8,128)S(1)}, f32[512,128]{0,1:T(8,128)S(1)}, u32[]{:S(2)}, u32[]{:S(2)}) %collective-permute-start.16) | collective-permute-done | bytes 262176 | tf_op jit(solution)/shard_map/ppermute | solution.py:15
  134.2 1.8 copy.9
  136.4 4.0 %fusion.3 = f32[4,256,512]{2,1,0:T(8,128)S(1)} fusion(f32[4,256,512]{2,1,0:T(8,128)} %bitcast.40, f32[512,256]{0,1:T(8,128)} %maximum_select_fusion.1, f32[512,256]{0,1:T(8,128)} %collective-permute-done.17, pred[]{:T(512)S(6)} %eq.19), kind=kOutput, calls=%fused_computation.17 | convolution fusion | flops 1611399168 | bytes 5242881 | tf_op jit(solution)/shard_map/dot_general | solution.py:32
  140.4 52.4 %all_to_all.6 = f32[4,256,512]{2,1,0:T(8,128)} all-to-all(f32[4,256,512]{2,1,0:T(8,128)S(1)} %fusion.3), channel_id=1, replica_groups=mesh['pair'=8,'aux'=4] {'aux'}, dimensions={0} | all-to-all | bytes 4194304 | tf_op jit(solution)/shard_map/all_to_all | solution.py:115
  192.9 2.7 %reduce_sum.9 = f32[256,512]{1,0:T(8,128)} reduce(f32[4,256,512]{2,1,0:T(8,128)} %all_to_all.6, f32[]{:T(128)} %constant.88.clone.1), dimensions={0}, to_apply=%region_0.1 | reduce | flops 393216 | bytes 2621444 | tf_op jit(solution)/shard_map/reduce_sum | solution.py:116
  (44 shorter events, 25.9 us)
Async XLA Ops:
  0.0 73.6 %copy-start = (f32[512,512]{1,0:T(8,128)S(1)}, f32[512,512]{1,0:T(8,128)}, u32[]{:S(2)}) copy-start(f32[512,512]{1,0:T(8,128)} %param.8) | copy-start | bytes 3145732
  0.0 20.1 %collective-permute-start.1 = (f32[256,512]{1,0:T(8,128)}, f32[256,512]{1,0:T(8,128)}, u32[]{:S(2)}, u32[]{:S(2)}) collective-permute-start(f32[256,512]{1,0:T(8,128)} %param.6), channel_id=1, source_target_pairs={{1,0},{2,1},{3,2},{5,4},{6,5},{7,6},{9,8},{10,9},{11,10},{13,12},{... | collective-permute-start | bytes 1572872 | tf_op jit(solution)/shard_map/ppermute | solution.py:10
  1.4 20.0 %collective-permute-start = (f32[256,512]{1,0:T(8,128)}, f32[256,512]{1,0:T(8,128)}, u32[]{:S(2)}, u32[]{:S(2)}) collective-permute-start(f32[256,512]{1,0:T(8,128)} %param.6), channel_id=1, source_target_pairs={{0,1},{1,2},{2,3},{4,5},{5,6},{6,7},{8,9},{9,10},{10,11},{12,13},{... | collective-permute-start | bytes 1572872 | tf_op jit(solution)/shard_map/ppermute | solution.py:10
  20.1 15.5 %collective-permute-start.3 = (f32[256,512]{1,0:T(8,128)}, f32[256,512]{1,0:T(8,128)S(1)}, u32[]{:S(2)}, u32[]{:S(2)}) collective-permute-start(f32[256,512]{1,0:T(8,128)} %collective-permute-done.1), channel_id=1, source_target_pairs={{1,0},{2,1},{3,2},{5,4},{6,5},{7,6},{9,8},{10,9},{11,10},{13,12},{... | collective-permute-start | bytes 1572872 | tf_op jit(solution)/shard_map/ppermute | solution.py:10
  21.4 15.5 %collective-permute-start.2 = (f32[256,512]{1,0:T(8,128)}, f32[256,512]{1,0:T(8,128)S(1)}, u32[]{:S(2)}, u32[]{:S(2)}) collective-permute-start(f32[256,512]{1,0:T(8,128)} %collective-permute-done), channel_id=1, source_target_pairs={{0,1},{1,2},{2,3},{4,5},{5,6},{6,7},{8,9},{9,10},{10,11},{12,13},{... | collective-permute-start | bytes 1572872 | tf_op jit(solution)/shard_map/ppermute | solution.py:10
  35.6 14.4 %collective-permute-start.5 = (f32[256,512]{1,0:T(8,128)S(1)}, f32[256,512]{1,0:T(8,128)S(1)}, u32[]{:S(2)}, u32[]{:S(2)}) collective-permute-start(f32[256,512]{1,0:T(8,128)S(1)} %collective-permute-done.3), channel_id=1, source_target_pairs={{1,0},{2,1},{3,2},{5,4},{6,5},{7,6},{9,8},{10,9},{11,10},{13,12},{... | collective-permute-start | bytes 1572872 | tf_op jit(solution)/shard_map/ppermute | solution.py:10
  36.9 14.2 %collective-permute-start.4 = (f32[256,512]{1,0:T(8,128)S(1)}, f32[256,512]{1,0:T(8,128)S(1)}, u32[]{:S(2)}, u32[]{:S(2)}) collective-permute-start(f32[256,512]{1,0:T(8,128)S(1)} %collective-permute-done.2), channel_id=1, source_target_pairs={{0,1},{1,2},{2,3},{4,5},{5,6},{6,7},{8,9},{9,10},{10,11},{12,13},{... | collective-permute-start | bytes 1572872 | tf_op jit(solution)/shard_map/ppermute | solution.py:10
  51.8 1.0 copy-start.1
  53.6 2.3 %collective-permute-start.6 = (f32[512,256]{0,1:T(8,128)}, f32[512,256]{0,1:T(8,128)}, u32[]{:S(2)}, u32[]{:S(2)}) collective-permute-start(f32[512,256]{0,1:T(8,128)} %slice_select_fusion), channel_id=1, source_target_pairs={{0,4},{4,0},{8,12},{12,8},{16,20},{20,16},{24,28},{28,24},{1,5},{5... | collective-permute-start | bytes 1572872 | tf_op jit(solution)/shard_map/ppermute | solution.py:15
  57.4 0.8 copy-start.2
  58.9 8.6 %collective-permute-start.7 = (f32[512,128]{0,1:T(8,128)}, f32[512,128]{0,1:T(8,128)S(1)}, u32[]{:S(2)}, u32[]{:S(2)}) collective-permute-start(f32[512,128]{0,1:T(8,128)} %slice_select_fusion.1), channel_id=1, source_target_pairs={{0,8},{4,12},{8,0},{12,4},{16,24},{20,28},{24,16},{28,20},{1,9},{5... | collective-permute-start | bytes 786440 | tf_op jit(solution)/shard_map/ppermute | solution.py:15
  60.3 18.4 %copy-start.3 = (f32[512,512]{1,0:T(8,128)S(1)}, f32[512,512]{1,0:T(8,128)}, u32[]{:S(2)}) copy-start(f32[512,512]{1,0:T(8,128)} %param.9) | copy-start | bytes 3145732
  68.6 5.0 %collective-permute-start.8 = (f32[512,64]{0,1:T(8,128)S(1)}, f32[512,64]{0,1:T(8,128)S(1)}, u32[]{:S(2)}, u32[]{:S(2)}) collective-permute-start(f32[512,64]{0,1:T(8,128)S(1)} %slice_select_fusion.2), channel_id=1, source_target_pairs={{0,16},{4,20},{8,24},{12,28},{16,0},{20,4},{24,8},{28,12},{1,17},{... | collective-permute-start | bytes 393224 | tf_op jit(solution)/shard_map/ppermute | solution.py:15
  74.2 6.9 %collective-permute-start.9 = (f32[512,64]{0,1:T(8,128)S(1)}, f32[512,64]{0,1:T(8,128)S(1)}, u32[]{:S(2)}, u32[]{:S(2)}) collective-permute-start(f32[512,64]{0,1:T(8,128)S(1)} %convolution_bitcast_fusion.2), channel_id=1, source_target_pairs={{0,1},{1,2},{2,3},{4,5},{5,6},{6,7},{8,9},{9,10},{10,11},{12,13},{... | collective-permute-start | bytes 393224 | tf_op jit(solution)/shard_map/ppermute | solution.py:10
  81.7 6.9 %collective-permute-start.10 = (f32[512,64]{0,1:T(8,128)S(1)}, f32[512,64]{0,1:T(8,128)S(1)}, u32[]{:S(2)}, u32[]{:S(2)}) collective-permute-start(f32[512,64]{0,1:T(8,128)S(1)} %convolution_add_fusion.8), channel_id=1, source_target_pairs={{0,1},{1,2},{2,3},{4,5},{5,6},{6,7},{8,9},{9,10},{10,11},{12,13},{... | collective-permute-start | bytes 393224 | tf_op jit(solution)/shard_map/ppermute | solution.py:10
  89.2 6.9 %collective-permute-start.11 = (f32[512,64]{0,1:T(8,128)S(1)}, f32[512,64]{0,1:T(8,128)S(1)}, u32[]{:S(2)}, u32[]{:S(2)}) collective-permute-start(f32[512,64]{0,1:T(8,128)S(1)} %convolution_add_fusion.7), channel_id=1, source_target_pairs={{0,1},{1,2},{2,3},{4,5},{5,6},{6,7},{8,9},{9,10},{10,11},{12,13},{... | collective-permute-start | bytes 393224 | tf_op jit(solution)/shard_map/ppermute | solution.py:10
  97.5 8.5 %collective-permute-start.12 = (f32[512,64]{0,1:T(8,128)S(1)}, f32[512,64]{0,1:T(8,128)S(1)}, u32[]{:S(2)}, u32[]{:S(2)}) collective-permute-start(f32[512,64]{0,1:T(8,128)S(1)} %convolution_bitcast_fusion.1), channel_id=1, source_target_pairs={{1,0},{2,1},{3,2},{5,4},{6,5},{7,6},{9,8},{10,9},{11,10},{13,12},{... | collective-permute-start | bytes 393224 | tf_op jit(solution)/shard_map/ppermute | solution.py:10
  106.5 7.6 %collective-permute-start.13 = (f32[512,64]{0,1:T(8,128)S(1)}, f32[512,64]{0,1:T(8,128)S(1)}, u32[]{:S(2)}, u32[]{:S(2)}) collective-permute-start(f32[512,64]{0,1:T(8,128)S(1)} %convolution_add_fusion.5), channel_id=1, source_target_pairs={{1,0},{2,1},{3,2},{5,4},{6,5},{7,6},{9,8},{10,9},{11,10},{13,12},{... | collective-permute-start | bytes 393224 | tf_op jit(solution)/shard_map/ppermute | solution.py:10
  114.5 6.9 %collective-permute-start.14 = (f32[512,64]{0,1:T(8,128)S(1)}, f32[512,64]{0,1:T(8,128)S(1)}, u32[]{:S(2)}, u32[]{:S(2)}) collective-permute-start(f32[512,64]{0,1:T(8,128)S(1)} %convolution_add_fusion.4), channel_id=1, source_target_pairs={{1,0},{2,1},{3,2},{5,4},{6,5},{7,6},{9,8},{10,9},{11,10},{13,12},{... | collective-permute-start | bytes 393224 | tf_op jit(solution)/shard_map/ppermute | solution.py:10
  121.8 5.0 %collective-permute-start.15 = (f32[512,64]{0,1:T(8,128)S(1)}, f32[512,64]{0,1:T(8,128)S(1)}, u32[]{:S(2)}, u32[]{:S(2)}) collective-permute-start(f32[512,64]{0,1:T(8,128)S(1)} %convolution_bitcast_fusion), channel_id=1, source_target_pairs={{0,16},{4,20},{8,24},{12,28},{16,0},{20,4},{24,8},{28,12},{1,17},{... | collective-permute-start | bytes 393224 | tf_op jit(solution)/shard_map/ppermute | solution.py:15
  126.9 6.4 %collective-permute-start.16 = (f32[512,128]{0,1:T(8,128)S(1)}, f32[512,128]{0,1:T(8,128)S(1)}, u32[]{:S(2)}, u32[]{:S(2)}) collective-permute-start(f32[512,128]{0,1:T(8,128)S(1)} %maximum_select_fusion.2), channel_id=1, source_target_pairs={{0,8},{4,12},{8,0},{12,4},{16,24},{20,28},{24,16},{28,20},{1,9},{5... | collective-permute-start | bytes 786440 | tf_op jit(solution)/shard_map/ppermute | solution.py:15
  134.2 2.3 %collective-permute-start.17 = (f32[512,256]{0,1:T(8,128)}, f32[512,256]{0,1:T(8,128)}, u32[]{:S(2)}, u32[]{:S(2)}) collective-permute-start(f32[512,256]{0,1:T(8,128)} %maximum_select_fusion.1), channel_id=1, source_target_pairs={{0,4},{4,0},{8,12},{12,8},{16,20},{20,16},{24,28},{28,24},{1,5},{5... | collective-permute-start | bytes 1572872 | tf_op jit(solution)/shard_map/ppermute | solution.py:15

commit v2 on v1

--- a/solution.py
+++ b/solution.py
@@ -19,9 +19,8 @@
     aux_blocks, pair_blocks = screen_mask.shape
     aux_size = block.shape[0] // aux_blocks
     pair_size = block.shape[1] // pair_blocks
-    shaped = block.reshape(aux_blocks, aux_size, pair_blocks, pair_size)
-    shaped = shaped * screen_mask.astype(jnp.float32)[:, None, :, None]
-    return shaped.reshape(block.shape)
+    expanded = jnp.repeat(jnp.repeat(screen_mask.astype(jnp.float32), aux_size, 0), pair_size, 1)
+    return block * expanded
 
 
 def product(left, right):
@@ -90,30 +89,55 @@
     return gamma
 
 
-def per_device(three_center, densities, screen_mask, diag_inverse, sub_factor):
-    screened = screen_block(three_center, screen_mask)
-    gamma_partial = gamma_over_aux(screened, densities)
-    right_side = reduce_scatter_columns(gamma_partial, "pair")
-    transfer = -product(diag_inverse, sub_factor)
+def reduce_over_aux(partial):
+    count = lax.axis_size("aux")
+    index = lax.axis_index("aux")
+    rows = partial.shape[0] // count
+
+    def block(owner):
+        start = jnp.clip(owner, 0, count - 1) * rows
+        return lax.dynamic_slice_in_dim(partial, start, rows, axis=0)
+
+    to_right = jnp.zeros((rows, partial.shape[1]), partial.dtype)
+    to_left = jnp.zeros((rows, partial.shape[1]), partial.dtype)
+    for step in range(count - 1):
+        to_right = from_behind(to_right + block(index + count - 1 - step), "aux", 1)
+        to_left = from_behind(to_left + block(index - (count - 1) + step), "aux", -1)
+    return to_right + to_left + block(index)
+
+
+def solve(right_side, transfer, diag_inverse, sub_factor):
     driving = product(diag_inverse, right_side)
     chain_length = lax.axis_size("aux")
-
     incoming = from_behind(driving, "aux", 1)
     for _ in range(chain_length - 2):
         incoming = from_behind(product(transfer, incoming) + driving, "aux", 1)
     solved = product(transfer, incoming) + driving
     source = product(sub_factor.T, product(diag_inverse.T, solved))
     back_map = transfer.T
-
     arriving = from_behind(source, "aux", -1)
     for _ in range(chain_length - 2):
         arriving = from_behind(product(back_map, arriving) + source, "aux", -1)
-    coefficients = product(diag_inverse.T, solved - arriving)
-    coeff_full = all_gather_columns(coefficients, "pair")
-    partial = contract_first(screened, coeff_full)
-    count = lax.axis_size("aux")
-    exchanged = lax.all_to_all(partial, "aux", 0, 0, tiled=True)
-    return exchanged.reshape(count, partial.shape[0] // count, -1).sum(axis=0)
+    return product(diag_inverse.T, solved - arriving)
+
+
+SLICES = 2
+
+
+def per_device(three_center, densities, screen_mask, diag_inverse, sub_factor):
+    screened = screen_block(three_center, screen_mask)
+    transfer = -product(diag_inverse, sub_factor)
+    width = densities.shape[1] // SLICES
+    results = []
+    for part in range(SLICES):
+        dens_part = densities[:, part * width:(part + 1) * width]
+        gamma_partial = gamma_over_aux(screened, dens_part)
+        right_side = reduce_scatter_columns(gamma_partial, "pair")
+        coefficients = solve(right_side, transfer, diag_inverse, sub_factor)
+        coeff_full = all_gather_columns(coefficients, "pair")
+        partial = contract_first(screened, coeff_full)
+        results.append(reduce_over_aux(partial))
+    return jnp.concatenate(results, axis=1)
 
 
 def solution(mesh):

time: 196 us -> 181 us (0.923)
  starting transfers between devices: 42.3 us -> 106 us
  blocking collectives: 52.4 us -> 0 us
  waiting for transfers between devices: 61.4 us -> 40.6 us
  other arithmetic: 11.2 us -> 2.82 us
  matrix products: 17.1 us -> 22.7 us
  local copies, waits for them, and re-layouts: 10.7 us -> 6.6 us
    ppermute x12 -> x36, starting transfers between devices: 36.7 us -> 93.6 us  [from_behind(): return lax.ppermute(array, axis, pairs)]
    all_to_all x1 -> x0, blocking collectives: 52.4 us -> none  [per_device(): exchanged = lax.all_to_all(partial, 'aux', 0, 0, tiled=True)]
    ppermute x12 -> x36, waiting for transfers between devices: 39.4 us -> 28.8 us  [from_behind(): return lax.ppermute(array, axis, pairs)]
    ppermute x6 -> x12, waiting for transfers between devices: 22 us -> 11.8 us  [swap(): return lax.ppermute(array, axis, [(i, i ^ bit) for i in range(count)])]
    dot_general x17 -> x33, matrix products: 13.1 us -> 20.7 us  [product(): jnp.dot(left, right, precision=lax.Precision.HIGH, preferred_element_type...]
    mul x2 -> x0, local copies, waits for them, and re-layouts: 7.15 us -> none  [screen_block(): shaped = shaped * screen_mask.astype(jnp.float32)[:, None, :, None]]
    ppermute x6 -> x12, starting transfers between devices: 5.69 us -> 12.3 us  [swap(): return lax.ppermute(array, axis, [(i, i ^ bit) for i in range(count)])]
    reduce_sum x1 -> x0, other arithmetic: 2.66 us -> none  [per_device(): return exchanged.reshape(count, partial.shape[0] // count, -1).sum(axis=0)]
  transfers between devices with their start and end apart: 18 -> 48, of which waited for: 15 -> 21; matrix products, arithmetic and copies ran while one was open for 10% -> 16% of each run, Pallas kernels for 0% -> 0%
where the time goes in v2:
time: 181 us; the launch traced here: 180 us
  starting transfers between devices  106 us (59%)
  waiting for transfers between devices  40.6 us (22%)
  matrix products  22.7 us (13%)
  local copies, waits for them, and re-layouts  6.6 us (4%)
  other arithmetic  2.82 us (2%)
    ppermute x36, starting transfers between devices, from_behind(): return lax.ppermute(array, axis, pairs)  93.6 us
    ppermute x36, waiting for transfers between devices, from_behind(): return lax.ppermute(array, axis, pairs)  28.8 us
    dot_general x33, matrix products, product(): jnp.dot(left, right, precision=lax.Precision.HIGH, preferred_element_type...  20.7 us
    ppermute x12, starting transfers between devices, swap(): return lax.ppermute(array, axis, [(i, i ^ bit) for i in range(count)])  12.3 us
    ppermute x12, waiting for transfers between devices, swap(): return lax.ppermute(array, axis, [(i, i ^ bit) for i in range(count)])  11.8 us
  transfers between devices with their start and end apart: 48, of which 21 were waited for; matrix products, arithmetic and copies ran while one was open for 16% of the time, Pallas kernels for 0%

profile of v2, /device:TPU:0, one launch (start us, length us, event | category | flops | bytes accessed | tf_op | source)
XLA Modules:
  0.0 179.6 jit_solution(3159549592799567063)
XLA Ops:
  0.0 1.9 %fusion.68 = (f32[256,256]{1,0:T(8,128)}, f32[256,256]{1,0:T(8,128)}) fusion(f32[256,512]{1,0:T(8,128)} %param.6), kind=kLoop, calls=%fused_computation.125 | loop fusion | bytes 1048576 | tf_op jit(solution)/shard_map/slice | solution.py:133
  1.9 5.7 %collective-permute-start = (f32[256,256]{1,0:T(8,128)}, f32[256,256]{1,0:T(8,128)}, u32[]{:S(2)}, u32[]{:S(2)}) collective-permute-start(f32[256,256]{1,0:T(8,128)} %get-tuple-element.17), channel_id=1, source_target_pairs={{0,1},{1,2},{2,3},{4,5},{5,6},{6,7},{8,9},{9,10},{10,11},{12,13},{... | collective-permute-start | bytes 786440 | tf_op jit(solution)/shard_map/ppermute | solution.py:10
  8.9 4.6 %collective-permute-start.24 = (f32[256,256]{1,0:T(8,128)}, f32[256,256]{1,0:T(8,128)S(1)}, u32[]{:S(2)}, u32[]{:S(2)}) collective-permute-start(f32[256,256]{1,0:T(8,128)} %get-tuple-element.18), channel_id=1, source_target_pairs={{0,1},{1,2},{2,3},{4,5},{5,6},{6,7},{8,9},{9,10},{10,11},{12,13},{... | collective-permute-start | bytes 786440 | tf_op jit(solution)/shard_map/ppermute | solution.py:10
  14.8 2.9 %copy.8 = f32[512,1024]{0,1:T(8,128)} copy(f32[512,1024]{1,0:T(8,128)} %param.5) | data formatting | bytes 4194304 | tf_op args[0]
  17.9 1.9 %bitcast_multiply_fusion = f32[512,1024]{0,1:T(8,128)S(1)} fusion(f32[512,1024]{0,1:T(8,128)} %copy.8, f32[512,16]{0,1:T(8,128)S(1)} %reshape.6), kind=kLoop, calls=%fused_computation | loop fusion | flops 524288 | bytes 4227072 | tf_op jit(solution)/shard_map/mul | solution.py:23
  25.6 5.2 %collective-permute-start.2 = (f32[256,256]{1,0:T(8,128)}, f32[256,256]{1,0:T(8,128)S(1)}, u32[]{:S(2)}, u32[]{:S(2)}) collective-permute-start(f32[256,256]{1,0:T(8,128)} %collective-permute-done), channel_id=1, source_target_pairs={{0,1},{1,2},{2,3},{4,5},{5,6},{6,7},{8,9},{9,10},{10,11},{12,13},{... | collective-permute-start | bytes 786440 | tf_op jit(solution)/shard_map/ppermute | solution.py:10
  30.8 3.9 %collective-permute-start.26 = (f32[256,256]{1,0:T(8,128)S(1)}, f32[256,256]{1,0:T(8,128)S(1)}, u32[]{:S(2)}, u32[]{:S(2)}) collective-permute-start(f32[256,256]{1,0:T(8,128)S(1)} %collective-permute-done.24), channel_id=1, source_target_pairs={{0,1},{1,2},{2,3},{4,5},{5,6},{6,7},{8,9},{9,10},{10,11},{12,13},{... | collective-permute-start | bytes 786440 | tf_op jit(solution)/shard_map/ppermute | solution.py:10
  34.7 1.7 convolution_add_fusion.7
  42.7 5.2 %collective-permute-start.4 = (f32[256,256]{1,0:T(8,128)S(1)}, f32[256,256]{1,0:T(8,128)S(1)}, u32[]{:S(2)}, u32[]{:S(2)}) collective-permute-start(f32[256,256]{1,0:T(8,128)S(1)} %collective-permute-done.2), channel_id=1, source_target_pairs={{0,1},{1,2},{2,3},{4,5},{5,6},{6,7},{8,9},{9,10},{10,11},{12,13},{... | collective-permute-start | bytes 786440 | tf_op jit(solution)/shard_map/ppermute | solution.py:10
  49.7 4.6 %collective-permute-start.28 = (f32[256,256]{1,0:T(8,128)S(1)}, f32[256,256]{1,0:T(8,128)S(1)}, u32[]{:S(2)}, u32[]{:S(2)}) collective-permute-start(f32[256,256]{1,0:T(8,128)S(1)} %collective-permute-done.26), channel_id=1, source_target_pairs={{0,1},{1,2},{2,3},{4,5},{5,6},{6,7},{8,9},{9,10},{10,11},{12,13},{... | collective-permute-start | bytes 786440 | tf_op jit(solution)/shard_map/ppermute | solution.py:10
  61.8 3.3 %collective-permute-done.7 = f32[512,64]{0,1:T(8,128)S(1)} collective-permute-done((f32[512,64]{0,1:T(8,128)S(1)}, f32[512,64]{0,1:T(8,128)S(1)}, u32[]{:S(2)}, u32[]{:S(2)}) %collective-permute-start.7) | collective-permute-done | bytes 131104 | tf_op jit(solution)/shard_map/ppermute | solution.py:15
  70.1 4.4 %collective-permute-start.9 = (f32[512,32]{0,1:T(8,128)S(1)}, f32[512,32]{0,1:T(8,128)S(1)}, u32[]{:S(2)}, u32[]{:S(2)}) collective-permute-start(f32[512,32]{0,1:T(8,128)S(1)} %convolution_bitcast_fusion.5), channel_id=1, source_target_pairs={{0,1},{1,2},{2,3},{4,5},{5,6},{6,7},{8,9},{9,10},{10,11},{12,13},{... | collective-permute-start | bytes 196616 | tf_op jit(solution)/shard_map/ppermute | solution.py:10
  75.1 3.9 %collective-permute-start.33 = (f32[512,32]{0,1:T(8,128)S(1)}, f32[512,32]{0,1:T(8,128)S(1)}, u32[]{:S(2)}, u32[]{:S(2)}) collective-permute-start(f32[512,32]{0,1:T(8,128)S(1)} %convolution_bitcast_fusion.2), channel_id=1, source_target_pairs={{0,1},{1,2},{2,3},{4,5},{5,6},{6,7},{8,9},{9,10},{10,11},{12,13},{... | collective-permute-start | bytes 196616 | tf_op jit(solution)/shard_map/ppermute | solution.py:10
  79.6 3.1 %collective-permute-start.10 = (f32[512,32]{0,1:T(8,128)S(1)}, f32[512,32]{0,1:T(8,128)S(1)}, u32[]{:S(2)}, u32[]{:S(2)}) collective-permute-start(f32[512,32]{0,1:T(8,128)S(1)} %convolution_add_fusion.17), channel_id=1, source_target_pairs={{0,1},{1,2},{2,3},{4,5},{5,6},{6,7},{8,9},{9,10},{10,11},{12,13},{... | collective-permute-start | bytes 196616 | tf_op jit(solution)/shard_map/ppermute | solution.py:10
  83.2 2.5 %collective-permute-start.34 = (f32[512,32]{0,1:T(8,128)S(1)}, f32[512,32]{0,1:T(8,128)S(1)}, u32[]{:S(2)}, u32[]{:S(2)}) collective-permute-start(f32[512,32]{0,1:T(8,128)S(1)} %convolution_add_fusion.12), channel_id=1, source_target_pairs={{0,1},{1,2},{2,3},{4,5},{5,6},{6,7},{8,9},{9,10},{10,11},{12,13},{... | collective-permute-start | bytes 196616 | tf_op jit(solution)/shard_map/ppermute | solution.py:10
  86.3 3.9 %collective-permute-start.11 = (f32[512,32]{0,1:T(8,128)S(1)}, f32[512,32]{0,1:T(8,128)S(1)}, u32[]{:S(2)}, u32[]{:S(2)}) collective-permute-start(f32[512,32]{0,1:T(8,128)S(1)} %convolution_add_fusion.16), channel_id=1, source_target_pairs={{0,1},{1,2},{2,3},{4,5},{5,6},{6,7},{8,9},{9,10},{10,11},{12,13},{... | collective-permute-start | bytes 196616 | tf_op jit(solution)/shard_map/ppermute | solution.py:10
  90.8 2.3 %collective-permute-start.35 = (f32[512,32]{0,1:T(8,128)S(1)}, f32[512,32]{0,1:T(8,128)S(1)}, u32[]{:S(2)}, u32[]{:S(2)}) collective-permute-start(f32[512,32]{0,1:T(8,128)S(1)} %convolution_add_fusion.11), channel_id=1, source_target_pairs={{0,1},{1,2},{2,3},{4,5},{5,6},{6,7},{8,9},{9,10},{10,11},{12,13},{... | collective-permute-start | bytes 196616 | tf_op jit(solution)/shard_map/ppermute | solution.py:10
  96.7 3.9 %collective-permute-done.12 = f32[512,32]{0,1:T(8,128)S(1)} collective-permute-done((f32[512,32]{0,1:T(8,128)S(1)}, f32[512,32]{0,1:T(8,128)S(1)}, u32[]{:S(2)}, u32[]{:S(2)}) %collective-permute-start.12) | collective-permute-done | bytes 65568 | tf_op jit(solution)/shard_map/ppermute | solution.py:10
  104.0 3.8 %collective-permute-done.13 = f32[512,32]{0,1:T(8,128)S(1)} collective-permute-done((f32[512,32]{0,1:T(8,128)S(1)}, f32[512,32]{0,1:T(8,128)S(1)}, u32[]{:S(2)}, u32[]{:S(2)}) %collective-permute-start.13) | collective-permute-done | bytes 65568 | tf_op jit(solution)/shard_map/ppermute | solution.py:10
  111.8 2.6 %collective-permute-done.14 = f32[512,32]{0,1:T(8,128)S(1)} collective-permute-done((f32[512,32]{0,1:T(8,128)S(1)}, f32[512,32]{0,1:T(8,128)S(1)}, u32[]{:S(2)}, u32[]{:S(2)}) %collective-permute-start.14) | collective-permute-done | bytes 65568 | tf_op jit(solution)/shard_map/ppermute | solution.py:10
  121.0 2.2 %collective-permute-done.38 = f32[512,32]{0,1:T(8,128)S(1)} collective-permute-done((f32[512,32]{0,1:T(8,128)S(1)}, f32[512,32]{0,1:T(8,128)S(1)}, u32[]{:S(2)}, u32[]{:S(2)}) %collective-permute-start.38) | collective-permute-done | bytes 65568 | tf_op jit(solution)/shard_map/ppermute | solution.py:10
  125.1 2.9 %collective-permute-done.39 = f32[512,32]{0,1:T(8,128)S(1)} collective-permute-done((f32[512,32]{0,1:T(8,128)S(1)}, f32[512,32]{0,1:T(8,128)S(1)}, u32[]{:S(2)}, u32[]{:S(2)}) %collective-permute-start.39) | collective-permute-done | bytes 65568 | tf_op jit(solution)/shard_map/ppermute | solution.py:15
  129.6 3.5 %collective-permute-done.40 = f32[512,64]{0,1:T(8,128)S(1)} collective-permute-done((f32[512,64]{0,1:T(8,128)S(1)}, f32[512,64]{0,1:T(8,128)S(1)}, u32[]{:S(2)}, u32[]{:S(2)}) %collective-permute-start.40) | collective-permute-done | bytes 131104 | tf_op jit(solution)/shard_map/ppermute | solution.py:15
  134.2 3.9 %collective-permute-start.18 = (f32[256,256]{0,1:T(8,128)S(1)}, f32[256,256]{0,1:T(8,128)S(1)}, u32[]{:S(2)}, u32[]{:S(2)}) collective-permute-start(f32[256,256]{0,1:T(8,128)S(1)} %get-tuple-element.10), channel_id=1, source_target_pairs={{0,1},{1,2},{2,3},{4,5},{5,6},{6,7},{8,9},{9,10},{10,11},{12,13},{... | collective-permute-start | bytes 786440 | tf_op jit(solution)/shard_map/ppermute | solution.py:10
  140.6 4.6 %collective-permute-start.42 = (f32[256,256]{0,1:T(8,128)S(1)}, f32[256,256]{0,1:T(8,128)S(1)}, u32[]{:S(2)}, u32[]{:S(2)}) collective-permute-start(f32[256,256]{0,1:T(8,128)S(1)} %get-tuple-element.16), channel_id=1, source_target_pairs={{0,1},{1,2},{2,3},{4,5},{5,6},{6,7},{8,9},{9,10},{10,11},{12,13},{... | collective-permute-start | bytes 786440 | tf_op jit(solution)/shard_map/ppermute | solution.py:10
  146.5 2.0 %collective-permute-done.21 = f32[256,256]{0,1:T(8,128)S(1)} collective-permute-done((f32[256,256]{0,1:T(8,128)S(1)}, f32[256,256]{0,1:T(8,128)S(1)}, u32[]{:S(2)}, u32[]{:S(2)}) %collective-permute-start.21) | collective-permute-done | bytes 262176 | tf_op jit(solution)/shard_map/ppermute | solution.py:10
  148.6 3.1 %collective-permute-start.19 = (f32[256,256]{0,1:T(8,128)S(1)}, f32[256,256]{0,1:T(8,128)S(1)}, u32[]{:S(2)}, u32[]{:S(2)}) collective-permute-start(f32[256,256]{0,1:T(8,128)S(1)} %get-tuple-element.8), channel_id=1, source_target_pairs={{0,1},{1,2},{2,3},{4,5},{5,6},{6,7},{8,9},{9,10},{10,11},{12,13},{... | collective-permute-start | bytes 786440 | tf_op jit(solution)/shard_map/ppermute | solution.py:10
  153.0 1.9 %collective-permute-done.45 = f32[256,256]{0,1:T(8,128)S(1)} collective-permute-done((f32[256,256]{0,1:T(8,128)S(1)}, f32[256,256]{0,1:T(8,128)S(1)}, u32[]{:S(2)}, u32[]{:S(2)}) %collective-permute-start.45) | collective-permute-done | bytes 262176 | tf_op jit(solution)/shard_map/ppermute | solution.py:10
  155.0 3.2 %collective-permute-start.43 = (f32[256,256]{0,1:T(8,128)S(1)}, f32[256,256]{0,1:T(8,128)S(1)}, u32[]{:S(2)}, u32[]{:S(2)}) collective-permute-start(f32[256,256]{0,1:T(8,128)S(1)} %get-tuple-element.14), channel_id=1, source_target_pairs={{0,1},{1,2},{2,3},{4,5},{5,6},{6,7},{8,9},{9,10},{10,11},{12,13},{... | collective-permute-start | bytes 786440 | tf_op jit(solution)/shard_map/ppermute | solution.py:10
  161.0 3.2 %collective-permute-start.20 = (f32[256,256]{0,1:T(8,128)S(1)}, f32[256,256]{0,1:T(8,128)S(1)}, u32[]{:S(2)}, u32[]{:S(2)}) collective-permute-start(f32[256,256]{0,1:T(8,128)S(1)} %get-tuple-element.6), channel_id=1, source_target_pairs={{0,1},{1,2},{2,3},{4,5},{5,6},{6,7},{8,9},{9,10},{10,11},{12,13},{... | collective-permute-start | bytes 786440 | tf_op jit(solution)/shard_map/ppermute | solution.py:10
  166.9 3.3 %collective-permute-start.44 = (f32[256,256]{0,1:T(8,128)S(1)}, f32[256,256]{0,1:T(8,128)S(1)}, u32[]{:S(2)}, u32[]{:S(2)}) collective-permute-start(f32[256,256]{0,1:T(8,128)S(1)} %get-tuple-element.12), channel_id=1, source_target_pairs={{0,1},{1,2},{2,3},{4,5},{5,6},{6,7},{8,9},{9,10},{10,11},{12,13},{... | collective-permute-start | bytes 786440 | tf_op jit(solution)/shard_map/ppermute | solution.py:10
  174.0 4.4 %collective-permute-done.47 = f32[256,256]{0,1:T(8,128)S(1)} collective-permute-done((f32[256,256]{0,1:T(8,128)S(1)}, f32[256,256]{0,1:T(8,128)S(1)}, u32[]{:S(2)}, u32[]{:S(2)}) %collective-permute-start.47) | collective-permute-done | bytes 262176 | tf_op jit(solution)/shard_map/ppermute | solution.py:10
  (142 shorter events, 69.2 us)
Async XLA Ops:
  1.9 23.6 %collective-permute-start = (f32[256,256]{1,0:T(8,128)}, f32[256,256]{1,0:T(8,128)}, u32[]{:S(2)}, u32[]{:S(2)}) collective-permute-start(f32[256,256]{1,0:T(8,128)} %get-tuple-element.17), channel_id=1, source_target_pairs={{0,1},{1,2},{2,3},{4,5},{5,6},{6,7},{8,9},{9,10},{10,11},{12,13},{... | collective-permute-start | bytes 786440 | tf_op jit(solution)/shard_map/ppermute | solution.py:10
  7.6 16.6 %collective-permute-start.1 = (f32[256,256]{1,0:T(8,128)}, f32[256,256]{1,0:T(8,128)}, u32[]{:S(2)}, u32[]{:S(2)}) collective-permute-start(f32[256,256]{1,0:T(8,128)} %get-tuple-element.17), channel_id=1, source_target_pairs={{1,0},{2,1},{3,2},{5,4},{6,5},{7,6},{9,8},{10,9},{11,10},{13,12},{... | collective-permute-start | bytes 786440 | tf_op jit(solution)/shard_map/ppermute | solution.py:10
  8.9 21.9 %collective-permute-start.24 = (f32[256,256]{1,0:T(8,128)}, f32[256,256]{1,0:T(8,128)S(1)}, u32[]{:S(2)}, u32[]{:S(2)}) collective-permute-start(f32[256,256]{1,0:T(8,128)} %get-tuple-element.18), channel_id=1, source_target_pairs={{0,1},{1,2},{2,3},{4,5},{5,6},{6,7},{8,9},{9,10},{10,11},{12,13},{... | collective-permute-start | bytes 786440 | tf_op jit(solution)/shard_map/ppermute | solution.py:10
  13.5 23.4 %collective-permute-start.25 = (f32[256,256]{1,0:T(8,128)}, f32[256,256]{1,0:T(8,128)}, u32[]{:S(2)}, u32[]{:S(2)}) collective-permute-start(f32[256,256]{1,0:T(8,128)} %get-tuple-element.18), channel_id=1, source_target_pairs={{1,0},{2,1},{3,2},{5,4},{6,5},{7,6},{9,8},{10,9},{11,10},{13,12},{... | collective-permute-start | bytes 786440 | tf_op jit(solution)/shard_map/ppermute | solution.py:10
  24.3 16.7 %collective-permute-start.3 = (f32[256,256]{1,0:T(8,128)}, f32[256,256]{1,0:T(8,128)S(1)}, u32[]{:S(2)}, u32[]{:S(2)}) collective-permute-start(f32[256,256]{1,0:T(8,128)} %collective-permute-done.1), channel_id=1, source_target_pairs={{1,0},{2,1},{3,2},{5,4},{6,5},{7,6},{9,8},{10,9},{11,10},{13,12},{... | collective-permute-start | bytes 786440 | tf_op jit(solution)/shard_map/ppermute | solution.py:10
  25.6 17.1 %collective-permute-start.2 = (f32[256,256]{1,0:T(8,128)}, f32[256,256]{1,0:T(8,128)S(1)}, u32[]{:S(2)}, u32[]{:S(2)}) collective-permute-start(f32[256,256]{1,0:T(8,128)} %collective-permute-done), channel_id=1, source_target_pairs={{0,1},{1,2},{2,3},{4,5},{5,6},{6,7},{8,9},{9,10},{10,11},{12,13},{... | collective-permute-start | bytes 786440 | tf_op jit(solution)/shard_map/ppermute | solution.py:10
  30.8 18.9 %collective-permute-start.26 = (f32[256,256]{1,0:T(8,128)S(1)}, f32[256,256]{1,0:T(8,128)S(1)}, u32[]{:S(2)}, u32[]{:S(2)}) collective-permute-start(f32[256,256]{1,0:T(8,128)S(1)} %collective-permute-done.24), channel_id=1, source_target_pairs={{0,1},{1,2},{2,3},{4,5},{5,6},{6,7},{8,9},{9,10},{10,11},{12,13},{... | collective-permute-start | bytes 786440 | tf_op jit(solution)/shard_map/ppermute | solution.py:10
  36.9 11.0 %collective-permute-start.27 = (f32[256,256]{1,0:T(8,128)}, f32[256,256]{1,0:T(8,128)S(1)}, u32[]{:S(2)}, u32[]{:S(2)}) collective-permute-start(f32[256,256]{1,0:T(8,128)} %collective-permute-done.25), channel_id=1, source_target_pairs={{1,0},{2,1},{3,2},{5,4},{6,5},{7,6},{9,8},{10,9},{11,10},{13,12},{... | collective-permute-start | bytes 786440 | tf_op jit(solution)/shard_map/ppermute | solution.py:10
  41.0 14.1 %collective-permute-start.5 = (f32[256,256]{1,0:T(8,128)S(1)}, f32[256,256]{1,0:T(8,128)S(1)}, u32[]{:S(2)}, u32[]{:S(2)}) collective-permute-start(f32[256,256]{1,0:T(8,128)S(1)} %collective-permute-done.3), channel_id=1, source_target_pairs={{1,0},{2,1},{3,2},{5,4},{6,5},{7,6},{9,8},{10,9},{11,10},{13,12},{... | collective-permute-start | bytes 786440 | tf_op jit(solution)/shard_map/ppermute | solution.py:10
  42.7 12.8 %collective-permute-start.4 = (f32[256,256]{1,0:T(8,128)S(1)}, f32[256,256]{1,0:T(8,128)S(1)}, u32[]{:S(2)}, u32[]{:S(2)}) collective-permute-start(f32[256,256]{1,0:T(8,128)S(1)} %collective-permute-done.2), channel_id=1, source_target_pairs={{0,1},{1,2},{2,3},{4,5},{5,6},{6,7},{8,9},{9,10},{10,11},{12,13},{... | collective-permute-start | bytes 786440 | tf_op jit(solution)/shard_map/ppermute | solution.py:10
  47.9 8.7 %collective-permute-start.29 = (f32[256,256]{1,0:T(8,128)S(1)}, f32[256,256]{1,0:T(8,128)S(1)}, u32[]{:S(2)}, u32[]{:S(2)}) collective-permute-start(f32[256,256]{1,0:T(8,128)S(1)} %collective-permute-done.27), channel_id=1, source_target_pairs={{1,0},{2,1},{3,2},{5,4},{6,5},{7,6},{9,8},{10,9},{11,10},{13,12},{... | collective-permute-start | bytes 786440 | tf_op jit(solution)/shard_map/ppermute | solution.py:10
  49.7 8.4 %collective-permute-start.28 = (f32[256,256]{1,0:T(8,128)S(1)}, f32[256,256]{1,0:T(8,128)S(1)}, u32[]{:S(2)}, u32[]{:S(2)}) collective-permute-start(f32[256,256]{1,0:T(8,128)S(1)} %collective-permute-done.26), channel_id=1, source_target_pairs={{0,1},{1,2},{2,3},{4,5},{5,6},{6,7},{8,9},{9,10},{10,11},{12,13},{... | collective-permute-start | bytes 786440 | tf_op jit(solution)/shard_map/ppermute | solution.py:10
  60.4 7.1 %collective-permute-start.31 = (f32[512,64]{0,1:T(8,128)S(1)}, f32[512,64]{0,1:T(8,128)S(1)}, u32[]{:S(2)}, u32[]{:S(2)}) collective-permute-start(f32[512,64]{0,1:T(8,128)S(1)} %slice_select_fusion.2), channel_id=1, source_target_pairs={{0,8},{4,12},{8,0},{12,4},{16,24},{20,28},{24,16},{28,20},{1,9},{5... | collective-permute-start | bytes 393224 | tf_op jit(solution)/shard_map/ppermute | solution.py:15
  67.6 6.9 %collective-permute-start.32 = (f32[512,32]{0,1:T(8,128)S(1)}, f32[512,32]{0,1:T(8,128)S(1)}, u32[]{:S(2)}, u32[]{:S(2)}) collective-permute-start(f32[512,32]{0,1:T(8,128)S(1)} %slice_select_fusion.4), channel_id=1, source_target_pairs={{0,16},{4,20},{8,24},{12,28},{16,0},{20,4},{24,8},{28,12},{1,17},{... | collective-permute-start | bytes 196616 | tf_op jit(solution)/shard_map/ppermute | solution.py:15
  70.1 8.9 %collective-permute-start.9 = (f32[512,32]{0,1:T(8,128)S(1)}, f32[512,32]{0,1:T(8,128)S(1)}, u32[]{:S(2)}, u32[]{:S(2)}) collective-permute-start(f32[512,32]{0,1:T(8,128)S(1)} %convolution_bitcast_fusion.5), channel_id=1, source_target_pairs={{0,1},{1,2},{2,3},{4,5},{5,6},{6,7},{8,9},{9,10},{10,11},{12,13},{... | collective-permute-start | bytes 196616 | tf_op jit(solution)/shard_map/ppermute | solution.py:10
  75.1 7.6 %collective-permute-start.33 = (f32[512,32]{0,1:T(8,128)S(1)}, f32[512,32]{0,1:T(8,128)S(1)}, u32[]{:S(2)}, u32[]{:S(2)}) collective-permute-start(f32[512,32]{0,1:T(8,128)S(1)} %convolution_bitcast_fusion.2), channel_id=1, source_target_pairs={{0,1},{1,2},{2,3},{4,5},{5,6},{6,7},{8,9},{9,10},{10,11},{12,13},{... | collective-permute-start | bytes 196616 | tf_op jit(solution)/shard_map/ppermute | solution.py:10
  83.2 7.0 %collective-permute-start.34 = (f32[512,32]{0,1:T(8,128)S(1)}, f32[512,32]{0,1:T(8,128)S(1)}, u32[]{:S(2)}, u32[]{:S(2)}) collective-permute-start(f32[512,32]{0,1:T(8,128)S(1)} %convolution_add_fusion.12), channel_id=1, source_target_pairs={{0,1},{1,2},{2,3},{4,5},{5,6},{6,7},{8,9},{9,10},{10,11},{12,13},{... | collective-permute-start | bytes 196616 | tf_op jit(solution)/shard_map/ppermute | solution.py:10
  86.3 6.8 %collective-permute-start.11 = (f32[512,32]{0,1:T(8,128)S(1)}, f32[512,32]{0,1:T(8,128)S(1)}, u32[]{:S(2)}, u32[]{:S(2)}) collective-permute-start(f32[512,32]{0,1:T(8,128)S(1)} %convolution_add_fusion.16), channel_id=1, source_target_pairs={{0,1},{1,2},{2,3},{4,5},{5,6},{6,7},{8,9},{9,10},{10,11},{12,13},{... | collective-permute-start | bytes 196616 | tf_op jit(solution)/shard_map/ppermute | solution.py:10
  102.7 7.4 %collective-permute-start.36 = (f32[512,32]{0,1:T(8,128)S(1)}, f32[512,32]{0,1:T(8,128)S(1)}, u32[]{:S(2)}, u32[]{:S(2)}) collective-permute-start(f32[512,32]{0,1:T(8,128)S(1)} %convolution_bitcast_fusion.1), channel_id=1, source_target_pairs={{1,0},{2,1},{3,2},{5,4},{6,5},{7,6},{9,8},{10,9},{11,10},{13,12},{... | collective-permute-start | bytes 196616 | tf_op jit(solution)/shard_map/ppermute | solution.py:10
  125.1 8.1 %collective-permute-start.17 = (f32[512,128]{0,1:T(8,128)S(1)}, f32[512,128]{0,1:T(8,128)S(1)}, u32[]{:S(2)}, u32[]{:S(2)}) collective-permute-start(f32[512,128]{0,1:T(8,128)S(1)} %maximum_select_fusion.4), channel_id=1, source_target_pairs={{0,4},{4,0},{8,12},{12,8},{16,20},{20,16},{24,28},{28,24},{1,5},{5... | collective-permute-start | bytes 786440 | tf_op jit(solution)/shard_map/ppermute | solution.py:15
  134.2 12.2 %collective-permute-start.18 = (f32[256,256]{0,1:T(8,128)S(1)}, f32[256,256]{0,1:T(8,128)S(1)}, u32[]{:S(2)}, u32[]{:S(2)}) collective-permute-start(f32[256,256]{0,1:T(8,128)S(1)} %get-tuple-element.10), channel_id=1, source_target_pairs={{0,1},{1,2},{2,3},{4,5},{5,6},{6,7},{8,9},{9,10},{10,11},{12,13},{... | collective-permute-start | bytes 786440 | tf_op jit(solution)/shard_map/ppermute | solution.py:10
  138.2 10.3 %collective-permute-start.21 = (f32[256,256]{0,1:T(8,128)S(1)}, f32[256,256]{0,1:T(8,128)S(1)}, u32[]{:S(2)}, u32[]{:S(2)}) collective-permute-start(f32[256,256]{0,1:T(8,128)S(1)} %get-tuple-element.9), channel_id=1, source_target_pairs={{1,0},{2,1},{3,2},{5,4},{6,5},{7,6},{9,8},{10,9},{11,10},{13,12},{... | collective-permute-start | bytes 786440 | tf_op jit(solution)/shard_map/ppermute | solution.py:10
  140.6 12.4 %collective-permute-start.42 = (f32[256,256]{0,1:T(8,128)S(1)}, f32[256,256]{0,1:T(8,128)S(1)}, u32[]{:S(2)}, u32[]{:S(2)}) collective-permute-start(f32[256,256]{0,1:T(8,128)S(1)} %get-tuple-element.16), channel_id=1, source_target_pairs={{0,1},{1,2},{2,3},{4,5},{5,6},{6,7},{8,9},{9,10},{10,11},{12,13},{... | collective-permute-start | bytes 786440 | tf_op jit(solution)/shard_map/ppermute | solution.py:10
  145.2 9.8 %collective-permute-start.45 = (f32[256,256]{0,1:T(8,128)S(1)}, f32[256,256]{0,1:T(8,128)S(1)}, u32[]{:S(2)}, u32[]{:S(2)}) collective-permute-start(f32[256,256]{0,1:T(8,128)S(1)} %get-tuple-element.15), channel_id=1, source_target_pairs={{1,0},{2,1},{3,2},{5,4},{6,5},{7,6},{9,8},{10,9},{11,10},{13,12},{... | collective-permute-start | bytes 786440 | tf_op jit(solution)/shard_map/ppermute | solution.py:10
  148.6 10.9 %collective-permute-start.19 = (f32[256,256]{0,1:T(8,128)S(1)}, f32[256,256]{0,1:T(8,128)S(1)}, u32[]{:S(2)}, u32[]{:S(2)}) collective-permute-start(f32[256,256]{0,1:T(8,128)S(1)} %get-tuple-element.8), channel_id=1, source_target_pairs={{0,1},{1,2},{2,3},{4,5},{5,6},{6,7},{8,9},{9,10},{10,11},{12,13},{... | collective-permute-start | bytes 786440 | tf_op jit(solution)/shard_map/ppermute | solution.py:10
  151.7 9.2 %collective-permute-start.22 = (f32[256,256]{0,1:T(8,128)S(1)}, f32[256,256]{0,1:T(8,128)S(1)}, u32[]{:S(2)}, u32[]{:S(2)}) collective-permute-start(f32[256,256]{0,1:T(8,128)S(1)} %get-tuple-element.7), channel_id=1, source_target_pairs={{1,0},{2,1},{3,2},{5,4},{6,5},{7,6},{9,8},{10,9},{11,10},{13,12},{... | collective-permute-start | bytes 786440 | tf_op jit(solution)/shard_map/ppermute | solution.py:10
  155.0 10.5 %collective-permute-start.43 = (f32[256,256]{0,1:T(8,128)S(1)}, f32[256,256]{0,1:T(8,128)S(1)}, u32[]{:S(2)}, u32[]{:S(2)}) collective-permute-start(f32[256,256]{0,1:T(8,128)S(1)} %get-tuple-element.14), channel_id=1, source_target_pairs={{0,1},{1,2},{2,3},{4,5},{5,6},{6,7},{8,9},{9,10},{10,11},{12,13},{... | collective-permute-start | bytes 786440 | tf_op jit(solution)/shard_map/ppermute | solution.py:10
  158.2 8.6 %collective-permute-start.46 = (f32[256,256]{0,1:T(8,128)S(1)}, f32[256,256]{0,1:T(8,128)S(1)}, u32[]{:S(2)}, u32[]{:S(2)}) collective-permute-start(f32[256,256]{0,1:T(8,128)S(1)} %get-tuple-element.13), channel_id=1, source_target_pairs={{1,0},{2,1},{3,2},{5,4},{6,5},{7,6},{9,8},{10,9},{11,10},{13,12},{... | collective-permute-start | bytes 786440 | tf_op jit(solution)/shard_map/ppermute | solution.py:10
  161.0 10.5 %collective-permute-start.20 = (f32[256,256]{0,1:T(8,128)S(1)}, f32[256,256]{0,1:T(8,128)S(1)}, u32[]{:S(2)}, u32[]{:S(2)}) collective-permute-start(f32[256,256]{0,1:T(8,128)S(1)} %get-tuple-element.6), channel_id=1, source_target_pairs={{0,1},{1,2},{2,3},{4,5},{5,6},{6,7},{8,9},{9,10},{10,11},{12,13},{... | collective-permute-start | bytes 786440 | tf_op jit(solution)/shard_map/ppermute | solution.py:10
  164.2 8.7 %collective-permute-start.23 = (f32[256,256]{0,1:T(8,128)S(1)}, f32[256,256]{0,1:T(8,128)S(1)}, u32[]{:S(2)}, u32[]{:S(2)}) collective-permute-start(f32[256,256]{0,1:T(8,128)S(1)} %get-tuple-element.5), channel_id=1, source_target_pairs={{1,0},{2,1},{3,2},{5,4},{6,5},{7,6},{9,8},{10,9},{11,10},{13,12},{... | collective-permute-start | bytes 786440 | tf_op jit(solution)/shard_map/ppermute | solution.py:10
  166.9 7.2 %collective-permute-start.44 = (f32[256,256]{0,1:T(8,128)S(1)}, f32[256,256]{0,1:T(8,128)S(1)}, u32[]{:S(2)}, u32[]{:S(2)}) collective-permute-start(f32[256,256]{0,1:T(8,128)S(1)} %get-tuple-element.12), channel_id=1, source_target_pairs={{0,1},{1,2},{2,3},{4,5},{5,6},{6,7},{8,9},{9,10},{10,11},{12,13},{... | collective-permute-start | bytes 786440 | tf_op jit(solution)/shard_map/ppermute | solution.py:10
  170.2 8.3 %collective-permute-start.47 = (f32[256,256]{0,1:T(8,128)S(1)}, f32[256,256]{0,1:T(8,128)S(1)}, u32[]{:S(2)}, u32[]{:S(2)}) collective-permute-start(f32[256,256]{0,1:T(8,128)S(1)} %get-tuple-element.11), channel_id=1, source_target_pairs={{1,0},{2,1},{3,2},{5,4},{6,5},{7,6},{9,8},{10,9},{11,10},{13,12},{... | collective-permute-start | bytes 786440 | tf_op jit(solution)/shard_map/ppermute | solution.py:10
  (22 other events, 125.1 us)

commit v3 on v2

--- a/solution.py
+++ b/solution.py
@@ -131,12 +131,13 @@
     results = []
     for part in range(SLICES):
         dens_part = densities[:, part * width:(part + 1) * width]
-        gamma_partial = gamma_over_aux(screened, dens_part)
+        dens_full = lax.all_gather(dens_part, "aux", axis=0, tiled=True)
+        gamma_partial = product(screened, dens_full)
         right_side = reduce_scatter_columns(gamma_partial, "pair")
         coefficients = solve(right_side, transfer, diag_inverse, sub_factor)
         coeff_full = all_gather_columns(coefficients, "pair")
         partial = contract_first(screened, coeff_full)
-        results.append(reduce_over_aux(partial))
+        results.append(lax.psum_scatter(partial, "aux", scatter_dimension=0, tiled=True))
     return jnp.concatenate(results, axis=1)
 
 

time: 181 us -> 210 us (1.16)
  waiting for transfers between devices: 40.6 us -> 121 us
  starting transfers between devices: 106 us -> 45.8 us
  between operations: 0.95 us -> 13.7 us
  matrix products: 22.7 us -> 18 us
  other arithmetic: 2.82 us -> 5.85 us
    ppermute x36 -> x12, starting transfers between devices: 93.6 us -> 33 us  [from_behind(): return lax.ppermute(array, axis, pairs)]
    all_gather x0 -> x2, waiting for transfers between devices: none -> 46.1 us  [per_device(): dens_full = lax.all_gather(dens_part, 'aux', axis=0, tiled=True)]
    reduce_scatter x0 -> x2, waiting for transfers between devices: none -> 26.4 us  [per_device(): lax.psum_scatter(partial, 'aux', scatter_dimension=0, tiled=True)]
    dot_general x33 -> x21, matrix products: 20.7 us -> 14 us  [product(): jnp.dot(left, right, precision=lax.Precision.HIGH, preferred_element_type...]
    ppermute x36 -> x12, waiting for transfers between devices: 28.8 us -> 34.9 us  [from_behind(): return lax.ppermute(array, axis, pairs)]
  transfers between devices with their start and end apart: 48 -> 28, of which waited for: 21 -> 19; matrix products, arithmetic and copies ran while one was open for 16% -> 11% of each run, Pallas kernels for 0% -> 0%
where the time goes in v3:
time: 210 us
  waiting for transfers between devices  121 us (58%)
  starting transfers between devices  45.8 us (22%)
  matrix products  18 us (9%)
  between operations  13.7 us (7%)
  local copies, waits for them, and re-layouts  5.96 us (3%)
  other arithmetic  5.85 us (3%)
    all_gather x2, waiting for transfers between devices, per_device(): dens_full = lax.all_gather(dens_part, 'aux', axis=0, tiled=True)  46.1 us
    ppermute x12, waiting for transfers between devices, from_behind(): return lax.ppermute(array, axis, pairs)  34.9 us
    ppermute x12, starting transfers between devices, from_behind(): return lax.ppermute(array, axis, pairs)  33 us
    reduce_scatter x2, waiting for transfers between devices, per_device(): lax.psum_scatter(partial, 'aux', scatter_dimension=0, tiled=True)  26.4 us
    dot_general x21, matrix products, product(): jnp.dot(left, right, precision=lax.Precision.HIGH, preferred_element_type...  14 us
    ppermute x12, starting transfers between devices, swap(): return lax.ppermute(array, axis, [(i, i ^ bit) for i in range(count)])  12.7 us
    ppermute x12, waiting for transfers between devices, swap(): return lax.ppermute(array, axis, [(i, i ^ bit) for i in range(count)])  12.5 us
  transfers between devices with their start and end apart: 28, of which 19 were waited for; matrix products, arithmetic and copies ran while one was open for 11% of the time, Pallas kernels for 0%

profile of v3, /device:TPU:0, one launch (start us, length us, event | category | flops | bytes accessed | tf_op | source)
XLA Modules:
  0.0 209.8 jit_solution(305365723263324616)
XLA Ops:
  6.5 2.0 fusion.28
  9.4 2.9 %copy.7 = f32[512,1024]{0,1:T(8,128)} copy(f32[512,1024]{1,0:T(8,128)} %param.5) | data formatting | bytes 4194304 | tf_op args[0]
  12.5 1.8 bitcast_multiply_fusion
  14.4 25.2 %all-gather.3.cloned.1.call-done = f32[1024,256]{1,0:T(8,128)} async-done(((f32[256,256]{1,0:T(8,128)}), f32[1024,256]{1,0:T(8,128)}) %all-gather.3.cloned.1.call-update) | async-done | bytes 1048592 | tf_op jit(solution)/shard_map/all_gather | solution.py:134
  39.6 2.3 %fusion.29 = f32[512,256]{0,1:T(8,128)S(1)} fusion(f32[512,1024]{0,1:T(8,128)S(1)} %bitcast_multiply_fusion, f32[1024,256]{1,0:T(8,128)} %all-gather.3.cloned.1.call-done), kind=kOutput, calls=%fused_computation.64 | convolution fusion | flops 805306368 | bytes 3670016 | tf_op jit(solution)/shard_map/dot_general | solution.py:27
  42.8 1.6 collective-permute-done
  47.7 20.9 %all-gather.5.cloned.1.call-done = f32[1024,256]{1,0:T(8,128)} async-done(((f32[256,256]{1,0:T(8,128)}), f32[1024,256]{1,0:T(8,128)}) %all-gather.5.cloned.1.call-update) | async-done | bytes 1048592 | tf_op jit(solution)/shard_map/all_gather | solution.py:134
  68.6 2.3 %fusion.31 = f32[512,256]{0,1:T(8,128)S(1)} fusion(f32[512,1024]{0,1:T(8,128)S(1)} %bitcast_multiply_fusion, f32[1024,256]{1,0:T(8,128)} %all-gather.5.cloned.1.call-done), kind=kOutput, calls=%fused_computation.66 | convolution fusion | flops 805306368 | bytes 3670016 | tf_op jit(solution)/shard_map/dot_general | solution.py:27
  72.6 2.7 %collective-permute-done.2 = f32[512,32]{0,1:T(8,128)S(1)} collective-permute-done((f32[512,32]{0,1:T(8,128)S(1)}, f32[512,32]{0,1:T(8,128)S(1)}, u32[]{:S(2)}, u32[]{:S(2)}) %collective-permute-start.2) | collective-permute-done | bytes 65568 | tf_op jit(solution)/shard_map/ppermute | solution.py:15
  75.9 3.3 %collective-permute-start.3 = (f32[512,32]{0,1:T(8,128)S(1)}, f32[512,32]{0,1:T(8,128)S(1)}, u32[]{:S(2)}, u32[]{:S(2)}) collective-permute-start(f32[512,32]{0,1:T(8,128)S(1)} %convolution_bitcast_fusion.5), channel_id=1, source_target_pairs={{0,1},{1,2},{2,3},{4,5},{5,6},{6,7},{8,9},{9,10},{10,11},{12,13},{... | collective-permute-start | bytes 196616 | tf_op jit(solution)/shard_map/ppermute | solution.py:10
  81.7 4.3 %collective-permute-start.4 = (f32[512,32]{0,1:T(8,128)S(1)}, f32[512,32]{0,1:T(8,128)S(1)}, u32[]{:S(2)}, u32[]{:S(2)}) collective-permute-start(f32[512,32]{0,1:T(8,128)S(1)} %convolution_add_fusion.9), channel_id=1, source_target_pairs={{0,1},{1,2},{2,3},{4,5},{5,6},{6,7},{8,9},{9,10},{10,11},{12,13},{... | collective-permute-start | bytes 196616 | tf_op jit(solution)/shard_map/ppermute | solution.py:10
  86.0 1.8 collective-permute-done.4
  88.4 4.3 %collective-permute-start.5 = (f32[512,32]{0,1:T(8,128)S(1)}, f32[512,32]{0,1:T(8,128)S(1)}, u32[]{:S(2)}, u32[]{:S(2)}) collective-permute-start(f32[512,32]{0,1:T(8,128)S(1)} %convolution_add_fusion.8), channel_id=1, source_target_pairs={{0,1},{1,2},{2,3},{4,5},{5,6},{6,7},{8,9},{9,10},{10,11},{12,13},{... | collective-permute-start | bytes 196616 | tf_op jit(solution)/shard_map/ppermute | solution.py:10
  97.8 5.3 %collective-permute-done.6 = f32[512,32]{0,1:T(8,128)S(1)} collective-permute-done((f32[512,32]{0,1:T(8,128)S(1)}, f32[512,32]{0,1:T(8,128)S(1)}, u32[]{:S(2)}, u32[]{:S(2)}) %collective-permute-start.6) | collective-permute-done | bytes 65568 | tf_op jit(solution)/shard_map/ppermute | solution.py:10
  106.4 3.3 %collective-permute-done.7 = f32[512,32]{0,1:T(8,128)S(1)} collective-permute-done((f32[512,32]{0,1:T(8,128)S(1)}, f32[512,32]{0,1:T(8,128)S(1)}, u32[]{:S(2)}, u32[]{:S(2)}) %collective-permute-start.7) | collective-permute-done | bytes 65568 | tf_op jit(solution)/shard_map/ppermute | solution.py:10
  112.0 4.5 %collective-permute-start.15 = (f32[512,32]{0,1:T(8,128)S(1)}, f32[512,32]{0,1:T(8,128)S(1)}, u32[]{:S(2)}, u32[]{:S(2)}) collective-permute-start(f32[512,32]{0,1:T(8,128)S(1)} %convolution_bitcast_fusion.2), channel_id=1, source_target_pairs={{0,1},{1,2},{2,3},{4,5},{5,6},{6,7},{8,9},{9,10},{10,11},{12,13},{... | collective-permute-start | bytes 196616 | tf_op jit(solution)/shard_map/ppermute | solution.py:10
  119.0 4.2 %collective-permute-start.16 = (f32[512,32]{0,1:T(8,128)S(1)}, f32[512,32]{0,1:T(8,128)S(1)}, u32[]{:S(2)}, u32[]{:S(2)}) collective-permute-start(f32[512,32]{0,1:T(8,128)S(1)} %convolution_add_fusion.4), channel_id=1, source_target_pairs={{0,1},{1,2},{2,3},{4,5},{5,6},{6,7},{8,9},{9,10},{10,11},{12,13},{... | collective-permute-start | bytes 196616 | tf_op jit(solution)/shard_map/ppermute | solution.py:10
  123.3 1.6 collective-permute-start.10
  125.7 4.3 %collective-permute-start.17 = (f32[512,32]{0,1:T(8,128)S(1)}, f32[512,32]{0,1:T(8,128)S(1)}, u32[]{:S(2)}, u32[]{:S(2)}) collective-permute-start(f32[512,32]{0,1:T(8,128)S(1)} %convolution_add_fusion.3), channel_id=1, source_target_pairs={{0,1},{1,2},{2,3},{4,5},{5,6},{6,7},{8,9},{9,10},{10,11},{12,13},{... | collective-permute-start | bytes 196616 | tf_op jit(solution)/shard_map/ppermute | solution.py:10
  130.1 1.8 collective-permute-done.17
  132.8 2.0 fusion
  135.3 1.6 collective-permute-start.18
  136.9 5.2 %collective-permute-done.18 = f32[512,32]{0,1:T(8,128)S(1)} collective-permute-done((f32[512,32]{0,1:T(8,128)S(1)}, f32[512,32]{0,1:T(8,128)S(1)}, u32[]{:S(2)}, u32[]{:S(2)}) %collective-permute-start.18) | collective-permute-done | bytes 65568 | tf_op jit(solution)/shard_map/ppermute | solution.py:10
  143.9 8.2 %collective-permute-done.19 = f32[512,32]{0,1:T(8,128)S(1)} collective-permute-done((f32[512,32]{0,1:T(8,128)S(1)}, f32[512,32]{0,1:T(8,128)S(1)}, u32[]{:S(2)}, u32[]{:S(2)}) %collective-permute-start.19) | collective-permute-done | bytes 65568 | tf_op jit(solution)/shard_map/ppermute | solution.py:10
  153.8 7.8 %collective-permute-done.20 = f32[512,32]{0,1:T(8,128)S(1)} collective-permute-done((f32[512,32]{0,1:T(8,128)S(1)}, f32[512,32]{0,1:T(8,128)S(1)}, u32[]{:S(2)}, u32[]{:S(2)}) %collective-permute-start.20) | collective-permute-done | bytes 65568 | tf_op jit(solution)/shard_map/ppermute | solution.py:10
  162.0 1.6 collective-permute-start.21
  163.6 2.7 %collective-permute-done.21 = f32[512,32]{0,1:T(8,128)S(1)} collective-permute-done((f32[512,32]{0,1:T(8,128)S(1)}, f32[512,32]{0,1:T(8,128)S(1)}, u32[]{:S(2)}, u32[]{:S(2)}) %collective-permute-start.21) | collective-permute-done | bytes 65568 | tf_op jit(solution)/shard_map/ppermute | solution.py:15
  166.3 1.6 collective-permute-start.22
  168.0 3.4 %collective-permute-done.22 = f32[512,64]{0,1:T(8,128)S(1)} collective-permute-done((f32[512,64]{0,1:T(8,128)S(1)}, f32[512,64]{0,1:T(8,128)S(1)}, u32[]{:S(2)}, u32[]{:S(2)}) %collective-permute-start.22) | collective-permute-done | bytes 131104 | tf_op jit(solution)/shard_map/ppermute | solution.py:15
  173.0 2.0 fusion.6
  175.1 26.4 %reduce-scatter.5.cloned.1.call-done = f32[256,256]{1,0:T(8,128)} async-done(((f32[1024,256]{1,0:T(8,128)}), f32[256,256]{1,0:T(8,128)}) %reduce-scatter.5.cloned.1.call-update) | async-done | bytes 262160 | tf_op jit(solution)/shard_map/reduce_scatter | solution.py:140
  201.4 1.9 pad_maximum_fusion
  (87 shorter events, 31.5 us)
Async XLA Ops:
  6.5 68.8 %copy-start = (f32[512,512]{1,0:T(8,128)S(1)}, f32[512,512]{1,0:T(8,128)}, u32[]{:S(2)}) copy-start(f32[512,512]{1,0:T(8,128)} %param.8) | copy-start | bytes 3145732
  6.5 33.1 %all-gather.3.cloned.1.call-start = ((), (), s32[]{:S(2)}) async-start(), calls=%async_computation.2 | async-start | bytes 1310720 | tf_op jit(solution)/shard_map/all_gather | solution.py:134
  8.5 60.1 %all-gather.5.cloned.1.call-start = ((), (), s32[]{:S(2)}) async-start(), calls=%async_computation.4 | async-start | bytes 1310720 | tf_op jit(solution)/shard_map/all_gather | solution.py:134
  9.3 165.8 %reduce-scatter.3.cloned.1.call-start = ((), (), s32[]{:S(2)}) async-start(), calls=%async_computation.3 | async-start | bytes 1310720 | tf_op jit(solution)/shard_map/reduce_scatter | solution.py:140
  14.4 54.2 %copy-start.1 = (f32[512,1024]{0,1:T(8,128)}, f32[512,1024]{0,1:T(8,128)S(1)}, u32[]{:S(2)}) copy-start(f32[512,1024]{0,1:T(8,128)S(1)} %bitcast_multiply_fusion) | copy-start | bytes 6291460
  42.7 1.7 collective-permute-start
  46.3 24.6 %collective-permute-start.1 = (f32[512,64]{0,1:T(8,128)}, f32[512,64]{0,1:T(8,128)S(1)}, u32[]{:S(2)}, u32[]{:S(2)}) collective-permute-start(f32[512,64]{0,1:T(8,128)} %slice_select_fusion.3), channel_id=1, source_target_pairs={{0,8},{4,12},{8,0},{12,4},{16,24},{20,28},{24,16},{28,20},{1,9},{5... | collective-permute-start | bytes 393224 | tf_op jit(solution)/shard_map/ppermute | solution.py:15
  71.0 4.3 %collective-permute-start.2 = (f32[512,32]{0,1:T(8,128)S(1)}, f32[512,32]{0,1:T(8,128)S(1)}, u32[]{:S(2)}, u32[]{:S(2)}) collective-permute-start(f32[512,32]{0,1:T(8,128)S(1)} %slice_select_fusion.5), channel_id=1, source_target_pairs={{0,16},{4,20},{8,24},{12,28},{16,0},{20,4},{24,8},{28,12},{1,17},{... | collective-permute-start | bytes 196616 | tf_op jit(solution)/shard_map/ppermute | solution.py:15
  72.5 13.4 %collective-permute-start.12 = (f32[512,128]{0,1:T(8,128)S(1)}, f32[512,128]{0,1:T(8,128)S(1)}, u32[]{:S(2)}, u32[]{:S(2)}) collective-permute-start(f32[512,128]{0,1:T(8,128)S(1)} %slice_select_fusion), channel_id=1, source_target_pairs={{0,4},{4,0},{8,12},{12,8},{16,20},{20,16},{24,28},{28,24},{1,5},{5... | collective-permute-start | bytes 786440 | tf_op jit(solution)/shard_map/ppermute | solution.py:15
  75.9 5.2 %collective-permute-start.3 = (f32[512,32]{0,1:T(8,128)S(1)}, f32[512,32]{0,1:T(8,128)S(1)}, u32[]{:S(2)}, u32[]{:S(2)}) collective-permute-start(f32[512,32]{0,1:T(8,128)S(1)} %convolution_bitcast_fusion.5), channel_id=1, source_target_pairs={{0,1},{1,2},{2,3},{4,5},{5,6},{6,7},{8,9},{9,10},{10,11},{12,13},{... | collective-permute-start | bytes 196616 | tf_op jit(solution)/shard_map/ppermute | solution.py:10
  81.7 6.2 %collective-permute-start.4 = (f32[512,32]{0,1:T(8,128)S(1)}, f32[512,32]{0,1:T(8,128)S(1)}, u32[]{:S(2)}, u32[]{:S(2)}) collective-permute-start(f32[512,32]{0,1:T(8,128)S(1)} %convolution_add_fusion.9), channel_id=1, source_target_pairs={{0,1},{1,2},{2,3},{4,5},{5,6},{6,7},{8,9},{9,10},{10,11},{12,13},{... | collective-permute-start | bytes 196616 | tf_op jit(solution)/shard_map/ppermute | solution.py:10
  88.4 6.2 %collective-permute-start.5 = (f32[512,32]{0,1:T(8,128)S(1)}, f32[512,32]{0,1:T(8,128)S(1)}, u32[]{:S(2)}, u32[]{:S(2)}) collective-permute-start(f32[512,32]{0,1:T(8,128)S(1)} %convolution_add_fusion.8), channel_id=1, source_target_pairs={{0,1},{1,2},{2,3},{4,5},{5,6},{6,7},{8,9},{9,10},{10,11},{12,13},{... | collective-permute-start | bytes 196616 | tf_op jit(solution)/shard_map/ppermute | solution.py:10
  92.7 5.0 %collective-permute-start.13 = (f32[512,64]{0,1:T(8,128)S(1)}, f32[512,64]{0,1:T(8,128)S(1)}, u32[]{:S(2)}, u32[]{:S(2)}) collective-permute-start(f32[512,64]{0,1:T(8,128)S(1)} %slice_select_fusion.2), channel_id=1, source_target_pairs={{0,8},{4,12},{8,0},{12,4},{16,24},{20,28},{24,16},{28,20},{1,9},{5... | collective-permute-start | bytes 393224 | tf_op jit(solution)/shard_map/ppermute | solution.py:15
  95.9 7.2 %collective-permute-start.6 = (f32[512,32]{0,1:T(8,128)S(1)}, f32[512,32]{0,1:T(8,128)S(1)}, u32[]{:S(2)}, u32[]{:S(2)}) collective-permute-start(f32[512,32]{0,1:T(8,128)S(1)} %convolution_bitcast_fusion.4), channel_id=1, source_target_pairs={{1,0},{2,1},{3,2},{5,4},{6,5},{7,6},{9,8},{10,9},{11,10},{13,12},{... | collective-permute-start | bytes 196616 | tf_op jit(solution)/shard_map/ppermute | solution.py:10
  103.5 6.2 %collective-permute-start.7 = (f32[512,32]{0,1:T(8,128)S(1)}, f32[512,32]{0,1:T(8,128)S(1)}, u32[]{:S(2)}, u32[]{:S(2)}) collective-permute-start(f32[512,32]{0,1:T(8,128)S(1)} %convolution_add_fusion.6), channel_id=1, source_target_pairs={{1,0},{2,1},{3,2},{5,4},{6,5},{7,6},{9,8},{10,9},{11,10},{13,12},{... | collective-permute-start | bytes 196616 | tf_op jit(solution)/shard_map/ppermute | solution.py:10
  104.8 6.6 %collective-permute-start.14 = (f32[512,32]{0,1:T(8,128)S(1)}, f32[512,32]{0,1:T(8,128)S(1)}, u32[]{:S(2)}, u32[]{:S(2)}) collective-permute-start(f32[512,32]{0,1:T(8,128)S(1)} %slice_select_fusion.4), channel_id=1, source_target_pairs={{0,16},{4,20},{8,24},{12,28},{16,0},{20,4},{24,8},{28,12},{1,17},{... | collective-permute-start | bytes 196616 | tf_op jit(solution)/shard_map/ppermute | solution.py:15
  110.1 6.5 %collective-permute-start.8 = (f32[512,32]{0,1:T(8,128)S(1)}, f32[512,32]{0,1:T(8,128)S(1)}, u32[]{:S(2)}, u32[]{:S(2)}) collective-permute-start(f32[512,32]{0,1:T(8,128)S(1)} %convolution_add_fusion.5), channel_id=1, source_target_pairs={{1,0},{2,1},{3,2},{5,4},{6,5},{7,6},{9,8},{10,9},{11,10},{13,12},{... | collective-permute-start | bytes 196616 | tf_op jit(solution)/shard_map/ppermute | solution.py:10
  112.0 6.5 %collective-permute-start.15 = (f32[512,32]{0,1:T(8,128)S(1)}, f32[512,32]{0,1:T(8,128)S(1)}, u32[]{:S(2)}, u32[]{:S(2)}) collective-permute-start(f32[512,32]{0,1:T(8,128)S(1)} %convolution_bitcast_fusion.2), channel_id=1, source_target_pairs={{0,1},{1,2},{2,3},{4,5},{5,6},{6,7},{8,9},{9,10},{10,11},{12,13},{... | collective-permute-start | bytes 196616 | tf_op jit(solution)/shard_map/ppermute | solution.py:10
  116.9 6.3 %collective-permute-start.9 = (f32[512,32]{0,1:T(8,128)S(1)}, f32[512,32]{0,1:T(8,128)S(1)}, u32[]{:S(2)}, u32[]{:S(2)}) collective-permute-start(f32[512,32]{0,1:T(8,128)S(1)} %convolution_bitcast_fusion.3), channel_id=1, source_target_pairs={{0,16},{4,20},{8,24},{12,28},{16,0},{20,4},{24,8},{28,12},{1,17},{... | collective-permute-start | bytes 196616 | tf_op jit(solution)/shard_map/ppermute | solution.py:15
  119.0 6.1 %collective-permute-start.16 = (f32[512,32]{0,1:T(8,128)S(1)}, f32[512,32]{0,1:T(8,128)S(1)}, u32[]{:S(2)}, u32[]{:S(2)}) collective-permute-start(f32[512,32]{0,1:T(8,128)S(1)} %convolution_add_fusion.4), channel_id=1, source_target_pairs={{0,1},{1,2},{2,3},{4,5},{5,6},{6,7},{8,9},{9,10},{10,11},{12,13},{... | collective-permute-start | bytes 196616 | tf_op jit(solution)/shard_map/ppermute | solution.py:10
  123.3 9.6 %copy-start.2 = (f32[512,1024]{0,1:T(8,128)S(1)}, f32[512,1024]{0,1:T(8,128)}, u32[]{:S(2)}) copy-start(f32[512,1024]{0,1:T(8,128)} %copy-done.1) | copy-start | bytes 6291460
  123.3 6.7 %collective-permute-start.10 = (f32[512,64]{0,1:T(8,128)S(1)}, f32[512,64]{0,1:T(8,128)S(1)}, u32[]{:S(2)}, u32[]{:S(2)}) collective-permute-start(f32[512,64]{0,1:T(8,128)S(1)} %maximum_select_fusion.6), channel_id=1, source_target_pairs={{0,8},{4,12},{8,0},{12,4},{16,24},{20,28},{24,16},{28,20},{1,9},{5... | collective-permute-start | bytes 393224 | tf_op jit(solution)/shard_map/ppermute | solution.py:15
  125.7 6.2 %collective-permute-start.17 = (f32[512,32]{0,1:T(8,128)S(1)}, f32[512,32]{0,1:T(8,128)S(1)}, u32[]{:S(2)}, u32[]{:S(2)}) collective-permute-start(f32[512,32]{0,1:T(8,128)S(1)} %convolution_add_fusion.3), channel_id=1, source_target_pairs={{0,1},{1,2},{2,3},{4,5},{5,6},{6,7},{8,9},{9,10},{10,11},{12,13},{... | collective-permute-start | bytes 196616 | tf_op jit(solution)/shard_map/ppermute | solution.py:10
  130.0 2.8 %collective-permute-start.11 = (f32[512,128]{0,1:T(8,128)S(1)}, f32[512,128]{0,1:T(8,128)S(1)}, u32[]{:S(2)}, u32[]{:S(2)}) collective-permute-start(f32[512,128]{0,1:T(8,128)S(1)} %maximum_select_fusion.4), channel_id=1, source_target_pairs={{0,4},{4,0},{8,12},{12,8},{16,20},{20,16},{24,28},{28,24},{1,5},{5... | collective-permute-start | bytes 786440 | tf_op jit(solution)/shard_map/ppermute | solution.py:15
  134.9 66.5 %reduce-scatter.5.cloned.1.call-start = ((), (), s32[]{:S(2)}) async-start(), calls=%async_computation.5 | async-start | bytes 1310720 | tf_op jit(solution)/shard_map/reduce_scatter | solution.py:140
  135.3 37.7 %copy-start.3 = (f32[512,1024]{0,1:T(8,128)S(1)}, f32[512,1024]{0,1:T(8,128)}, u32[]{:S(2)}) copy-start(f32[512,1024]{0,1:T(8,128)} %copy-done.1) | copy-start | bytes 6291460
  135.3 6.8 %collective-permute-start.18 = (f32[512,32]{0,1:T(8,128)S(1)}, f32[512,32]{0,1:T(8,128)S(1)}, u32[]{:S(2)}, u32[]{:S(2)}) collective-permute-start(f32[512,32]{0,1:T(8,128)S(1)} %convolution_bitcast_fusion.1), channel_id=1, source_target_pairs={{1,0},{2,1},{3,2},{5,4},{6,5},{7,6},{9,8},{10,9},{11,10},{13,12},{... | collective-permute-start | bytes 196616 | tf_op jit(solution)/shard_map/ppermute | solution.py:10
  142.6 9.5 %collective-permute-start.19 = (f32[512,32]{0,1:T(8,128)S(1)}, f32[512,32]{0,1:T(8,128)S(1)}, u32[]{:S(2)}, u32[]{:S(2)}) collective-permute-start(f32[512,32]{0,1:T(8,128)S(1)} %convolution_add_fusion.1), channel_id=1, source_target_pairs={{1,0},{2,1},{3,2},{5,4},{6,5},{7,6},{9,8},{10,9},{11,10},{13,12},{... | collective-permute-start | bytes 196616 | tf_op jit(solution)/shard_map/ppermute | solution.py:10
  152.5 9.1 %collective-permute-start.20 = (f32[512,32]{0,1:T(8,128)S(1)}, f32[512,32]{0,1:T(8,128)S(1)}, u32[]{:S(2)}, u32[]{:S(2)}) collective-permute-start(f32[512,32]{0,1:T(8,128)S(1)} %convolution_add_fusion), channel_id=1, source_target_pairs={{1,0},{2,1},{3,2},{5,4},{6,5},{7,6},{9,8},{10,9},{11,10},{13,12},{... | collective-permute-start | bytes 196616 | tf_op jit(solution)/shard_map/ppermute | solution.py:10
  162.0 4.3 %collective-permute-start.21 = (f32[512,32]{0,1:T(8,128)S(1)}, f32[512,32]{0,1:T(8,128)S(1)}, u32[]{:S(2)}, u32[]{:S(2)}) collective-permute-start(f32[512,32]{0,1:T(8,128)S(1)} %convolution_bitcast_fusion), channel_id=1, source_target_pairs={{0,16},{4,20},{8,24},{12,28},{16,0},{20,4},{24,8},{28,12},{1,17},{... | collective-permute-start | bytes 196616 | tf_op jit(solution)/shard_map/ppermute | solution.py:15
  166.3 5.0 %collective-permute-start.22 = (f32[512,64]{0,1:T(8,128)S(1)}, f32[512,64]{0,1:T(8,128)S(1)}, u32[]{:S(2)}, u32[]{:S(2)}) collective-permute-start(f32[512,64]{0,1:T(8,128)S(1)} %maximum_select_fusion.7), channel_id=1, source_target_pairs={{0,8},{4,12},{8,0},{12,4},{16,24},{20,28},{24,16},{28,20},{1,9},{5... | collective-permute-start | bytes 393224 | tf_op jit(solution)/shard_map/ppermute | solution.py:15
  171.4 1.6 collective-permute-start.23
  (3 other events, 12.1 us)
Sparse Core Ops, SparseCore 0:
  8.9 30.6 all-gather.2
  41.2 27.4 all-gather.4
  135.0 31.1 reduce-scatter.2
  175.2 26.2 reduce-scatter.4

commit v4 on v2

--- a/solution.py
+++ b/solution.py
@@ -136,7 +136,7 @@
         coefficients = solve(right_side, transfer, diag_inverse, sub_factor)
         coeff_full = all_gather_columns(coefficients, "pair")
         partial = contract_first(screened, coeff_full)
-        results.append(reduce_over_aux(partial))
+        results.append(lax.psum_scatter(partial, "aux", scatter_dimension=0, tiled=True))
     return jnp.concatenate(results, axis=1)
 
 

time: 181 us -> 208 us (1.15)
  waiting for transfers between devices: 40.6 us -> 76.1 us
  starting transfers between devices: 106 us -> 83.2 us
  between operations: 0.95 us -> 14.2 us
    reduce_scatter x0 -> x2, waiting for transfers between devices: none -> 26.7 us  [per_device(): lax.psum_scatter(partial, 'aux', scatter_dimension=0, tiled=True)]
    ppermute x36 -> x24, starting transfers between devices: 93.6 us -> 70.3 us  [from_behind(): return lax.ppermute(array, axis, pairs)]
    ppermute x36 -> x24, waiting for transfers between devices: 28.8 us -> 34.9 us  [from_behind(): return lax.ppermute(array, axis, pairs)]
    ppermute x12, waiting for transfers between devices: 11.8 us -> 14.5 us  [swap(): return lax.ppermute(array, axis, [(i, i ^ bit) for i in range(count)])]
  transfers between devices with their start and end apart: 48 -> 38, of which waited for: 21 -> 19; matrix products, arithmetic and copies ran while one was open for 16% -> 13% of each run, Pallas kernels for 0% -> 0%
where the time goes in v4:
time: 208 us; the launch traced here: 207 us
  starting transfers between devices  83.2 us (40%)
  waiting for transfers between devices  76.1 us (37%)
  matrix products  24.5 us (12%)
  between operations  14.2 us (7%)
  local copies, waits for them, and re-layouts  5.14 us (2%)
  other arithmetic  4.14 us (2%)
    ppermute x24, starting transfers between devices, from_behind(): return lax.ppermute(array, axis, pairs)  70.3 us
    ppermute x24, waiting for transfers between devices, from_behind(): return lax.ppermute(array, axis, pairs)  34.9 us
    reduce_scatter x2, waiting for transfers between devices, per_device(): lax.psum_scatter(partial, 'aux', scatter_dimension=0, tiled=True)  26.7 us
    dot_general x33, matrix products, product(): jnp.dot(left, right, precision=lax.Precision.HIGH, preferred_element_type...  20.4 us
    ppermute x12, waiting for transfers between devices, swap(): return lax.ppermute(array, axis, [(i, i ^ bit) for i in range(count)])  14.5 us
    ppermute x12, starting transfers between devices, swap(): return lax.ppermute(array, axis, [(i, i ^ bit) for i in range(count)])  12.8 us
  transfers between devices with their start and end apart: 38, of which 19 were waited for; matrix products, arithmetic and copies ran while one was open for 13% of the time, Pallas kernels for 0%

profile of v4, /device:TPU:0, one launch (start us, length us, event | category | flops | bytes accessed | tf_op | source)
XLA Modules:
  0.0 207.2 jit_solution(8983026691151412904)
XLA Ops:
  6.5 1.9 fusion.68
  8.5 5.6 %collective-permute-start = (f32[256,256]{1,0:T(8,128)}, f32[256,256]{1,0:T(8,128)}, u32[]{:S(2)}, u32[]{:S(2)}) collective-permute-start(f32[256,256]{1,0:T(8,128)} %get-tuple-element.5), channel_id=1, source_target_pairs={{0,1},{1,2},{2,3},{4,5},{5,6},{6,7},{8,9},{9,10},{10,11},{12,13},{... | collective-permute-start | bytes 786440 | tf_op jit(solution)/shard_map/ppermute | solution.py:10
  15.4 4.6 %collective-permute-start.18 = (f32[256,256]{1,0:T(8,128)}, f32[256,256]{1,0:T(8,128)S(1)}, u32[]{:S(2)}, u32[]{:S(2)}) collective-permute-start(f32[256,256]{1,0:T(8,128)} %get-tuple-element.6), channel_id=1, source_target_pairs={{0,1},{1,2},{2,3},{4,5},{5,6},{6,7},{8,9},{9,10},{10,11},{12,13},{... | collective-permute-start | bytes 786440 | tf_op jit(solution)/shard_map/ppermute | solution.py:10
  21.3 2.9 %copy.7 = f32[512,1024]{0,1:T(8,128)} copy(f32[512,1024]{1,0:T(8,128)} %param.5) | data formatting | bytes 4194304 | tf_op args[0]
  24.5 1.9 bitcast_multiply_fusion
  30.6 5.2 %collective-permute-start.2 = (f32[256,256]{1,0:T(8,128)}, f32[256,256]{1,0:T(8,128)S(1)}, u32[]{:S(2)}, u32[]{:S(2)}) collective-permute-start(f32[256,256]{1,0:T(8,128)} %collective-permute-done), channel_id=1, source_target_pairs={{0,1},{1,2},{2,3},{4,5},{5,6},{6,7},{8,9},{9,10},{10,11},{12,13},{... | collective-permute-start | bytes 786440 | tf_op jit(solution)/shard_map/ppermute | solution.py:10
  35.8 3.9 %collective-permute-start.20 = (f32[256,256]{1,0:T(8,128)S(1)}, f32[256,256]{1,0:T(8,128)S(1)}, u32[]{:S(2)}, u32[]{:S(2)}) collective-permute-start(f32[256,256]{1,0:T(8,128)S(1)} %collective-permute-done.18), channel_id=1, source_target_pairs={{0,1},{1,2},{2,3},{4,5},{5,6},{6,7},{8,9},{9,10},{10,11},{12,13},{... | collective-permute-start | bytes 786440 | tf_op jit(solution)/shard_map/ppermute | solution.py:10
  47.5 5.2 %collective-permute-start.4 = (f32[256,256]{1,0:T(8,128)S(1)}, f32[256,256]{1,0:T(8,128)S(1)}, u32[]{:S(2)}, u32[]{:S(2)}) collective-permute-start(f32[256,256]{1,0:T(8,128)S(1)} %collective-permute-done.2), channel_id=1, source_target_pairs={{0,1},{1,2},{2,3},{4,5},{5,6},{6,7},{8,9},{9,10},{10,11},{12,13},{... | collective-permute-start | bytes 786440 | tf_op jit(solution)/shard_map/ppermute | solution.py:10
  54.5 4.6 %collective-permute-start.22 = (f32[256,256]{1,0:T(8,128)S(1)}, f32[256,256]{1,0:T(8,128)S(1)}, u32[]{:S(2)}, u32[]{:S(2)}) collective-permute-start(f32[256,256]{1,0:T(8,128)S(1)} %collective-permute-done.20), channel_id=1, source_target_pairs={{0,1},{1,2},{2,3},{4,5},{5,6},{6,7},{8,9},{9,10},{10,11},{12,13},{... | collective-permute-start | bytes 786440 | tf_op jit(solution)/shard_map/ppermute | solution.py:10
  64.1 3.6 %collective-permute-done.7 = f32[512,64]{0,1:T(8,128)S(1)} collective-permute-done((f32[512,64]{0,1:T(8,128)S(1)}, f32[512,64]{0,1:T(8,128)S(1)}, u32[]{:S(2)}, u32[]{:S(2)}) %collective-permute-start.7) | collective-permute-done | bytes 131104 | tf_op jit(solution)/shard_map/ppermute | solution.py:15
  67.8 1.6 collective-permute-start.8
  69.5 2.6 %collective-permute-done.8 = f32[512,32]{0,1:T(8,128)S(1)} collective-permute-done((f32[512,32]{0,1:T(8,128)S(1)}, f32[512,32]{0,1:T(8,128)S(1)}, u32[]{:S(2)}, u32[]{:S(2)}) %collective-permute-start.8) | collective-permute-done | bytes 65568 | tf_op jit(solution)/shard_map/ppermute | solution.py:15
  72.7 3.9 %collective-permute-start.9 = (f32[512,32]{0,1:T(8,128)S(1)}, f32[512,32]{0,1:T(8,128)S(1)}, u32[]{:S(2)}, u32[]{:S(2)}) collective-permute-start(f32[512,32]{0,1:T(8,128)S(1)} %convolution_bitcast_fusion.5), channel_id=1, source_target_pairs={{0,1},{1,2},{2,3},{4,5},{5,6},{6,7},{8,9},{9,10},{10,11},{12,13},{... | collective-permute-start | bytes 196616 | tf_op jit(solution)/shard_map/ppermute | solution.py:10
  79.0 4.3 %collective-permute-start.10 = (f32[512,32]{0,1:T(8,128)S(1)}, f32[512,32]{0,1:T(8,128)S(1)}, u32[]{:S(2)}, u32[]{:S(2)}) collective-permute-start(f32[512,32]{0,1:T(8,128)S(1)} %convolution_add_fusion.17), channel_id=1, source_target_pairs={{0,1},{1,2},{2,3},{4,5},{5,6},{6,7},{8,9},{9,10},{10,11},{12,13},{... | collective-permute-start | bytes 196616 | tf_op jit(solution)/shard_map/ppermute | solution.py:10
  83.4 1.8 collective-permute-done.10
  85.8 4.3 %collective-permute-start.11 = (f32[512,32]{0,1:T(8,128)S(1)}, f32[512,32]{0,1:T(8,128)S(1)}, u32[]{:S(2)}, u32[]{:S(2)}) collective-permute-start(f32[512,32]{0,1:T(8,128)S(1)} %convolution_add_fusion.16), channel_id=1, source_target_pairs={{0,1},{1,2},{2,3},{4,5},{5,6},{6,7},{8,9},{9,10},{10,11},{12,13},{... | collective-permute-start | bytes 196616 | tf_op jit(solution)/shard_map/ppermute | solution.py:10
  95.1 5.1 %collective-permute-done.12 = f32[512,32]{0,1:T(8,128)S(1)} collective-permute-done((f32[512,32]{0,1:T(8,128)S(1)}, f32[512,32]{0,1:T(8,128)S(1)}, u32[]{:S(2)}, u32[]{:S(2)}) %collective-permute-start.12) | collective-permute-done | bytes 65568 | tf_op jit(solution)/shard_map/ppermute | solution.py:10
  101.9 1.6 collective-permute-start.26
  103.5 3.3 %collective-permute-done.13 = f32[512,32]{0,1:T(8,128)S(1)} collective-permute-done((f32[512,32]{0,1:T(8,128)S(1)}, f32[512,32]{0,1:T(8,128)S(1)}, u32[]{:S(2)}, u32[]{:S(2)}) %collective-permute-start.13) | collective-permute-done | bytes 65568 | tf_op jit(solution)/shard_map/ppermute | solution.py:10
  109.1 4.5 %collective-permute-start.27 = (f32[512,32]{0,1:T(8,128)S(1)}, f32[512,32]{0,1:T(8,128)S(1)}, u32[]{:S(2)}, u32[]{:S(2)}) collective-permute-start(f32[512,32]{0,1:T(8,128)S(1)} %convolution_bitcast_fusion.2), channel_id=1, source_target_pairs={{0,1},{1,2},{2,3},{4,5},{5,6},{6,7},{8,9},{9,10},{10,11},{12,13},{... | collective-permute-start | bytes 196616 | tf_op jit(solution)/shard_map/ppermute | solution.py:10
  116.2 4.2 %collective-permute-start.28 = (f32[512,32]{0,1:T(8,128)S(1)}, f32[512,32]{0,1:T(8,128)S(1)}, u32[]{:S(2)}, u32[]{:S(2)}) collective-permute-start(f32[512,32]{0,1:T(8,128)S(1)} %convolution_add_fusion.12), channel_id=1, source_target_pairs={{0,1},{1,2},{2,3},{4,5},{5,6},{6,7},{8,9},{9,10},{10,11},{12,13},{... | collective-permute-start | bytes 196616 | tf_op jit(solution)/shard_map/ppermute | solution.py:10
  122.8 4.3 %collective-permute-start.29 = (f32[512,32]{0,1:T(8,128)S(1)}, f32[512,32]{0,1:T(8,128)S(1)}, u32[]{:S(2)}, u32[]{:S(2)}) collective-permute-start(f32[512,32]{0,1:T(8,128)S(1)} %convolution_add_fusion.11), channel_id=1, source_target_pairs={{0,1},{1,2},{2,3},{4,5},{5,6},{6,7},{8,9},{9,10},{10,11},{12,13},{... | collective-permute-start | bytes 196616 | tf_op jit(solution)/shard_map/ppermute | solution.py:10
  127.2 1.8 collective-permute-done.29
  130.0 2.0 fusion.4
  133.9 5.2 %collective-permute-done.30 = f32[512,32]{0,1:T(8,128)S(1)} collective-permute-done((f32[512,32]{0,1:T(8,128)S(1)}, f32[512,32]{0,1:T(8,128)S(1)}, u32[]{:S(2)}, u32[]{:S(2)}) %collective-permute-start.30) | collective-permute-done | bytes 65568 | tf_op jit(solution)/shard_map/ppermute | solution.py:10
  140.8 8.1 %collective-permute-done.31 = f32[512,32]{0,1:T(8,128)S(1)} collective-permute-done((f32[512,32]{0,1:T(8,128)S(1)}, f32[512,32]{0,1:T(8,128)S(1)}, u32[]{:S(2)}, u32[]{:S(2)}) %collective-permute-start.31) | collective-permute-done | bytes 65568 | tf_op jit(solution)/shard_map/ppermute | solution.py:10
  150.7 7.7 %collective-permute-done.32 = f32[512,32]{0,1:T(8,128)S(1)} collective-permute-done((f32[512,32]{0,1:T(8,128)S(1)}, f32[512,32]{0,1:T(8,128)S(1)}, u32[]{:S(2)}, u32[]{:S(2)}) %collective-permute-start.32) | collective-permute-done | bytes 65568 | tf_op jit(solution)/shard_map/ppermute | solution.py:10
  160.3 2.8 %collective-permute-done.33 = f32[512,32]{0,1:T(8,128)S(1)} collective-permute-done((f32[512,32]{0,1:T(8,128)S(1)}, f32[512,32]{0,1:T(8,128)S(1)}, u32[]{:S(2)}, u32[]{:S(2)}) %collective-permute-start.33) | collective-permute-done | bytes 65568 | tf_op jit(solution)/shard_map/ppermute | solution.py:15
  164.6 3.5 %collective-permute-done.34 = f32[512,64]{0,1:T(8,128)S(1)} collective-permute-done((f32[512,64]{0,1:T(8,128)S(1)}, f32[512,64]{0,1:T(8,128)S(1)}, u32[]{:S(2)}, u32[]{:S(2)}) %collective-permute-start.34) | collective-permute-done | bytes 131104 | tf_op jit(solution)/shard_map/ppermute | solution.py:15
  169.7 2.0 fusion.10
  171.8 26.6 %reduce-scatter.5.cloned.1.call-done = f32[256,256]{1,0:T(8,128)} async-done(((f32[1024,256]{1,0:T(8,128)}), f32[256,256]{1,0:T(8,128)}) %reduce-scatter.5.cloned.1.call-update) | async-done | bytes 262160 | tf_op jit(solution)/shard_map/reduce_scatter | solution.py:139
  198.5 1.9 pad_maximum_fusion
  (119 shorter events, 50.6 us)
Async XLA Ops:
  6.5 165.3 %reduce-scatter.3.cloned.1.call-start = ((), (), s32[]{:S(2)}) async-start(), calls=%async_computation.2 | async-start | bytes 1310720 | tf_op jit(solution)/shard_map/reduce_scatter | solution.py:139
  8.5 22.1 %collective-permute-start = (f32[256,256]{1,0:T(8,128)}, f32[256,256]{1,0:T(8,128)}, u32[]{:S(2)}, u32[]{:S(2)}) collective-permute-start(f32[256,256]{1,0:T(8,128)} %get-tuple-element.5), channel_id=1, source_target_pairs={{0,1},{1,2},{2,3},{4,5},{5,6},{6,7},{8,9},{9,10},{10,11},{12,13},{... | collective-permute-start | bytes 786440 | tf_op jit(solution)/shard_map/ppermute | solution.py:10
  14.1 15.1 %collective-permute-start.1 = (f32[256,256]{1,0:T(8,128)}, f32[256,256]{1,0:T(8,128)}, u32[]{:S(2)}, u32[]{:S(2)}) collective-permute-start(f32[256,256]{1,0:T(8,128)} %get-tuple-element.5), channel_id=1, source_target_pairs={{1,0},{2,1},{3,2},{5,4},{6,5},{7,6},{9,8},{10,9},{11,10},{13,12},{... | collective-permute-start | bytes 786440 | tf_op jit(solution)/shard_map/ppermute | solution.py:10
  15.4 20.4 %collective-permute-start.18 = (f32[256,256]{1,0:T(8,128)}, f32[256,256]{1,0:T(8,128)S(1)}, u32[]{:S(2)}, u32[]{:S(2)}) collective-permute-start(f32[256,256]{1,0:T(8,128)} %get-tuple-element.6), channel_id=1, source_target_pairs={{0,1},{1,2},{2,3},{4,5},{5,6},{6,7},{8,9},{9,10},{10,11},{12,13},{... | collective-permute-start | bytes 786440 | tf_op jit(solution)/shard_map/ppermute | solution.py:10
  20.0 21.7 %collective-permute-start.19 = (f32[256,256]{1,0:T(8,128)}, f32[256,256]{1,0:T(8,128)}, u32[]{:S(2)}, u32[]{:S(2)}) collective-permute-start(f32[256,256]{1,0:T(8,128)} %get-tuple-element.6), channel_id=1, source_target_pairs={{1,0},{2,1},{3,2},{5,4},{6,5},{7,6},{9,8},{10,9},{11,10},{13,12},{... | collective-permute-start | bytes 786440 | tf_op jit(solution)/shard_map/ppermute | solution.py:10
  29.2 16.5 %collective-permute-start.3 = (f32[256,256]{1,0:T(8,128)}, f32[256,256]{1,0:T(8,128)S(1)}, u32[]{:S(2)}, u32[]{:S(2)}) collective-permute-start(f32[256,256]{1,0:T(8,128)} %collective-permute-done.1), channel_id=1, source_target_pairs={{1,0},{2,1},{3,2},{5,4},{6,5},{7,6},{9,8},{10,9},{11,10},{13,12},{... | collective-permute-start | bytes 786440 | tf_op jit(solution)/shard_map/ppermute | solution.py:10
  30.6 17.0 %collective-permute-start.2 = (f32[256,256]{1,0:T(8,128)}, f32[256,256]{1,0:T(8,128)S(1)}, u32[]{:S(2)}, u32[]{:S(2)}) collective-permute-start(f32[256,256]{1,0:T(8,128)} %collective-permute-done), channel_id=1, source_target_pairs={{0,1},{1,2},{2,3},{4,5},{5,6},{6,7},{8,9},{9,10},{10,11},{12,13},{... | collective-permute-start | bytes 786440 | tf_op jit(solution)/shard_map/ppermute | solution.py:10
  35.8 18.7 %collective-permute-start.20 = (f32[256,256]{1,0:T(8,128)S(1)}, f32[256,256]{1,0:T(8,128)S(1)}, u32[]{:S(2)}, u32[]{:S(2)}) collective-permute-start(f32[256,256]{1,0:T(8,128)S(1)} %collective-permute-done.18), channel_id=1, source_target_pairs={{0,1},{1,2},{2,3},{4,5},{5,6},{6,7},{8,9},{9,10},{10,11},{12,13},{... | collective-permute-start | bytes 786440 | tf_op jit(solution)/shard_map/ppermute | solution.py:10
  41.7 11.0 %collective-permute-start.21 = (f32[256,256]{1,0:T(8,128)}, f32[256,256]{1,0:T(8,128)S(1)}, u32[]{:S(2)}, u32[]{:S(2)}) collective-permute-start(f32[256,256]{1,0:T(8,128)} %collective-permute-done.19), channel_id=1, source_target_pairs={{1,0},{2,1},{3,2},{5,4},{6,5},{7,6},{9,8},{10,9},{11,10},{13,12},{... | collective-permute-start | bytes 786440 | tf_op jit(solution)/shard_map/ppermute | solution.py:10
  45.8 13.7 %collective-permute-start.5 = (f32[256,256]{1,0:T(8,128)S(1)}, f32[256,256]{1,0:T(8,128)S(1)}, u32[]{:S(2)}, u32[]{:S(2)}) collective-permute-start(f32[256,256]{1,0:T(8,128)S(1)} %collective-permute-done.3), channel_id=1, source_target_pairs={{1,0},{2,1},{3,2},{5,4},{6,5},{7,6},{9,8},{10,9},{11,10},{13,12},{... | collective-permute-start | bytes 786440 | tf_op jit(solution)/shard_map/ppermute | solution.py:10
  47.5 12.4 %collective-permute-start.4 = (f32[256,256]{1,0:T(8,128)S(1)}, f32[256,256]{1,0:T(8,128)S(1)}, u32[]{:S(2)}, u32[]{:S(2)}) collective-permute-start(f32[256,256]{1,0:T(8,128)S(1)} %collective-permute-done.2), channel_id=1, source_target_pairs={{0,1},{1,2},{2,3},{4,5},{5,6},{6,7},{8,9},{9,10},{10,11},{12,13},{... | collective-permute-start | bytes 786440 | tf_op jit(solution)/shard_map/ppermute | solution.py:10
  52.7 8.7 %collective-permute-start.23 = (f32[256,256]{1,0:T(8,128)S(1)}, f32[256,256]{1,0:T(8,128)S(1)}, u32[]{:S(2)}, u32[]{:S(2)}) collective-permute-start(f32[256,256]{1,0:T(8,128)S(1)} %collective-permute-done.21), channel_id=1, source_target_pairs={{1,0},{2,1},{3,2},{5,4},{6,5},{7,6},{9,8},{10,9},{11,10},{13,12},{... | collective-permute-start | bytes 786440 | tf_op jit(solution)/shard_map/ppermute | solution.py:10
  54.5 9.2 %collective-permute-start.22 = (f32[256,256]{1,0:T(8,128)S(1)}, f32[256,256]{1,0:T(8,128)S(1)}, u32[]{:S(2)}, u32[]{:S(2)}) collective-permute-start(f32[256,256]{1,0:T(8,128)S(1)} %collective-permute-done.20), channel_id=1, source_target_pairs={{0,1},{1,2},{2,3},{4,5},{5,6},{6,7},{8,9},{9,10},{10,11},{12,13},{... | collective-permute-start | bytes 786440 | tf_op jit(solution)/shard_map/ppermute | solution.py:10
  62.1 5.6 %collective-permute-start.7 = (f32[512,64]{0,1:T(8,128)S(1)}, f32[512,64]{0,1:T(8,128)S(1)}, u32[]{:S(2)}, u32[]{:S(2)}) collective-permute-start(f32[512,64]{0,1:T(8,128)S(1)} %slice_select_fusion.3), channel_id=1, source_target_pairs={{0,8},{4,12},{8,0},{12,4},{16,24},{20,28},{24,16},{28,20},{1,9},{5... | collective-permute-start | bytes 393224 | tf_op jit(solution)/shard_map/ppermute | solution.py:15
  69.4 13.9 %collective-permute-start.24 = (f32[512,128]{0,1:T(8,128)S(1)}, f32[512,128]{0,1:T(8,128)S(1)}, u32[]{:S(2)}, u32[]{:S(2)}) collective-permute-start(f32[512,128]{0,1:T(8,128)S(1)} %slice_select_fusion), channel_id=1, source_target_pairs={{0,4},{4,0},{8,12},{12,8},{16,20},{20,16},{24,28},{28,24},{1,5},{5... | collective-permute-start | bytes 786440 | tf_op jit(solution)/shard_map/ppermute | solution.py:15
  72.7 5.8 %collective-permute-start.9 = (f32[512,32]{0,1:T(8,128)S(1)}, f32[512,32]{0,1:T(8,128)S(1)}, u32[]{:S(2)}, u32[]{:S(2)}) collective-permute-start(f32[512,32]{0,1:T(8,128)S(1)} %convolution_bitcast_fusion.5), channel_id=1, source_target_pairs={{0,1},{1,2},{2,3},{4,5},{5,6},{6,7},{8,9},{9,10},{10,11},{12,13},{... | collective-permute-start | bytes 196616 | tf_op jit(solution)/shard_map/ppermute | solution.py:10
  79.0 6.2 %collective-permute-start.10 = (f32[512,32]{0,1:T(8,128)S(1)}, f32[512,32]{0,1:T(8,128)S(1)}, u32[]{:S(2)}, u32[]{:S(2)}) collective-permute-start(f32[512,32]{0,1:T(8,128)S(1)} %convolution_add_fusion.17), channel_id=1, source_target_pairs={{0,1},{1,2},{2,3},{4,5},{5,6},{6,7},{8,9},{9,10},{10,11},{12,13},{... | collective-permute-start | bytes 196616 | tf_op jit(solution)/shard_map/ppermute | solution.py:10
  85.8 6.2 %collective-permute-start.11 = (f32[512,32]{0,1:T(8,128)S(1)}, f32[512,32]{0,1:T(8,128)S(1)}, u32[]{:S(2)}, u32[]{:S(2)}) collective-permute-start(f32[512,32]{0,1:T(8,128)S(1)} %convolution_add_fusion.16), channel_id=1, source_target_pairs={{0,1},{1,2},{2,3},{4,5},{5,6},{6,7},{8,9},{9,10},{10,11},{12,13},{... | collective-permute-start | bytes 196616 | tf_op jit(solution)/shard_map/ppermute | solution.py:10
  90.1 5.0 %collective-permute-start.25 = (f32[512,64]{0,1:T(8,128)S(1)}, f32[512,64]{0,1:T(8,128)S(1)}, u32[]{:S(2)}, u32[]{:S(2)}) collective-permute-start(f32[512,64]{0,1:T(8,128)S(1)} %slice_select_fusion.2), channel_id=1, source_target_pairs={{0,8},{4,12},{8,0},{12,4},{16,24},{20,28},{24,16},{28,20},{1,9},{5... | collective-permute-start | bytes 393224 | tf_op jit(solution)/shard_map/ppermute | solution.py:15
  93.3 6.9 %collective-permute-start.12 = (f32[512,32]{0,1:T(8,128)S(1)}, f32[512,32]{0,1:T(8,128)S(1)}, u32[]{:S(2)}, u32[]{:S(2)}) collective-permute-start(f32[512,32]{0,1:T(8,128)S(1)} %convolution_bitcast_fusion.4), channel_id=1, source_target_pairs={{1,0},{2,1},{3,2},{5,4},{6,5},{7,6},{9,8},{10,9},{11,10},{13,12},{... | collective-permute-start | bytes 196616 | tf_op jit(solution)/shard_map/ppermute | solution.py:10
  100.6 6.2 %collective-permute-start.13 = (f32[512,32]{0,1:T(8,128)S(1)}, f32[512,32]{0,1:T(8,128)S(1)}, u32[]{:S(2)}, u32[]{:S(2)}) collective-permute-start(f32[512,32]{0,1:T(8,128)S(1)} %convolution_add_fusion.14), channel_id=1, source_target_pairs={{1,0},{2,1},{3,2},{5,4},{6,5},{7,6},{9,8},{10,9},{11,10},{13,12},{... | collective-permute-start | bytes 196616 | tf_op jit(solution)/shard_map/ppermute | solution.py:10
  101.9 6.6 %collective-permute-start.26 = (f32[512,32]{0,1:T(8,128)S(1)}, f32[512,32]{0,1:T(8,128)S(1)}, u32[]{:S(2)}, u32[]{:S(2)}) collective-permute-start(f32[512,32]{0,1:T(8,128)S(1)} %slice_select_fusion.4), channel_id=1, source_target_pairs={{0,16},{4,20},{8,24},{12,28},{16,0},{20,4},{24,8},{28,12},{1,17},{... | collective-permute-start | bytes 196616 | tf_op jit(solution)/shard_map/ppermute | solution.py:15
  107.2 6.5 %collective-permute-start.14 = (f32[512,32]{0,1:T(8,128)S(1)}, f32[512,32]{0,1:T(8,128)S(1)}, u32[]{:S(2)}, u32[]{:S(2)}) collective-permute-start(f32[512,32]{0,1:T(8,128)S(1)} %convolution_add_fusion.13), channel_id=1, source_target_pairs={{1,0},{2,1},{3,2},{5,4},{6,5},{7,6},{9,8},{10,9},{11,10},{13,12},{... | collective-permute-start | bytes 196616 | tf_op jit(solution)/shard_map/ppermute | solution.py:10
  109.1 6.5 %collective-permute-start.27 = (f32[512,32]{0,1:T(8,128)S(1)}, f32[512,32]{0,1:T(8,128)S(1)}, u32[]{:S(2)}, u32[]{:S(2)}) collective-permute-start(f32[512,32]{0,1:T(8,128)S(1)} %convolution_bitcast_fusion.2), channel_id=1, source_target_pairs={{0,1},{1,2},{2,3},{4,5},{5,6},{6,7},{8,9},{9,10},{10,11},{12,13},{... | collective-permute-start | bytes 196616 | tf_op jit(solution)/shard_map/ppermute | solution.py:10
  114.1 6.3 %collective-permute-start.15 = (f32[512,32]{0,1:T(8,128)S(1)}, f32[512,32]{0,1:T(8,128)S(1)}, u32[]{:S(2)}, u32[]{:S(2)}) collective-permute-start(f32[512,32]{0,1:T(8,128)S(1)} %convolution_bitcast_fusion.3), channel_id=1, source_target_pairs={{0,16},{4,20},{8,24},{12,28},{16,0},{20,4},{24,8},{28,12},{1,17},{... | collective-permute-start | bytes 196616 | tf_op jit(solution)/shard_map/ppermute | solution.py:15
  116.2 6.1 %collective-permute-start.28 = (f32[512,32]{0,1:T(8,128)S(1)}, f32[512,32]{0,1:T(8,128)S(1)}, u32[]{:S(2)}, u32[]{:S(2)}) collective-permute-start(f32[512,32]{0,1:T(8,128)S(1)} %convolution_add_fusion.12), channel_id=1, source_target_pairs={{0,1},{1,2},{2,3},{4,5},{5,6},{6,7},{8,9},{9,10},{10,11},{12,13},{... | collective-permute-start | bytes 196616 | tf_op jit(solution)/shard_map/ppermute | solution.py:10
  120.4 6.7 %collective-permute-start.16 = (f32[512,64]{0,1:T(8,128)S(1)}, f32[512,64]{0,1:T(8,128)S(1)}, u32[]{:S(2)}, u32[]{:S(2)}) collective-permute-start(f32[512,64]{0,1:T(8,128)S(1)} %maximum_select_fusion.6), channel_id=1, source_target_pairs={{0,8},{4,12},{8,0},{12,4},{16,24},{20,28},{24,16},{28,20},{1,9},{5... | collective-permute-start | bytes 393224 | tf_op jit(solution)/shard_map/ppermute | solution.py:15
  122.8 6.2 %collective-permute-start.29 = (f32[512,32]{0,1:T(8,128)S(1)}, f32[512,32]{0,1:T(8,128)S(1)}, u32[]{:S(2)}, u32[]{:S(2)}) collective-permute-start(f32[512,32]{0,1:T(8,128)S(1)} %convolution_add_fusion.11), channel_id=1, source_target_pairs={{0,1},{1,2},{2,3},{4,5},{5,6},{6,7},{8,9},{9,10},{10,11},{12,13},{... | collective-permute-start | bytes 196616 | tf_op jit(solution)/shard_map/ppermute | solution.py:10
  132.0 66.5 %reduce-scatter.5.cloned.1.call-start = ((), (), s32[]{:S(2)}) async-start(), calls=%async_computation.3 | async-start | bytes 1310720 | tf_op jit(solution)/shard_map/reduce_scatter | solution.py:139
  132.5 6.6 %collective-permute-start.30 = (f32[512,32]{0,1:T(8,128)S(1)}, f32[512,32]{0,1:T(8,128)S(1)}, u32[]{:S(2)}, u32[]{:S(2)}) collective-permute-start(f32[512,32]{0,1:T(8,128)S(1)} %convolution_bitcast_fusion.1), channel_id=1, source_target_pairs={{1,0},{2,1},{3,2},{5,4},{6,5},{7,6},{9,8},{10,9},{11,10},{13,12},{... | collective-permute-start | bytes 196616 | tf_op jit(solution)/shard_map/ppermute | solution.py:10
  139.5 9.4 %collective-permute-start.31 = (f32[512,32]{0,1:T(8,128)S(1)}, f32[512,32]{0,1:T(8,128)S(1)}, u32[]{:S(2)}, u32[]{:S(2)}) collective-permute-start(f32[512,32]{0,1:T(8,128)S(1)} %convolution_add_fusion.9), channel_id=1, source_target_pairs={{1,0},{2,1},{3,2},{5,4},{6,5},{7,6},{9,8},{10,9},{11,10},{13,12},{... | collective-permute-start | bytes 196616 | tf_op jit(solution)/shard_map/ppermute | solution.py:10
  149.4 9.0 %collective-permute-start.32 = (f32[512,32]{0,1:T(8,128)S(1)}, f32[512,32]{0,1:T(8,128)S(1)}, u32[]{:S(2)}, u32[]{:S(2)}) collective-permute-start(f32[512,32]{0,1:T(8,128)S(1)} %convolution_add_fusion.8), channel_id=1, source_target_pairs={{1,0},{2,1},{3,2},{5,4},{6,5},{7,6},{9,8},{10,9},{11,10},{13,12},{... | collective-permute-start | bytes 196616 | tf_op jit(solution)/shard_map/ppermute | solution.py:10
  (14 other events, 190.9 us)
Sparse Core Ops, SparseCore 0:
  132.2 30.9 reduce-scatter.2
  171.9 26.5 reduce-scatter.4

commit v5 on v2

--- a/solution.py
+++ b/solution.py
@@ -106,18 +106,43 @@
     return to_right + to_left + block(index)
 
 
-def solve(right_side, transfer, diag_inverse, sub_factor):
+def gathered_position(axis):
+    index = lax.axis_index(axis)
+    count = lax.axis_size(axis)
+    position = 0
+    bit, mirror = 1, count // 2
+    while bit < count:
+        position = position + ((index // bit) % 2) * mirror
+        bit, mirror = bit * 2, mirror // 2
+    return position
+
+
+def neighbour_maps(transfer):
+    count = lax.axis_size("pair")
+    width = transfer.shape[1] // count
+    start = gathered_position("pair") * width
+    mine = lax.dynamic_slice_in_dim(transfer, start, width, axis=1)
+    pieces = jnp.concatenate(
+        [from_behind(mine, "aux", 1), from_behind(mine, "aux", -1)], axis=1
+    )
+    full = all_gather_columns(pieces, "pair").reshape(transfer.shape[0], count, 2, width)
+    rows = transfer.shape[0]
+    return full[:, :, 0, :].reshape(rows, -1), full[:, :, 1, :].reshape(rows, -1)
+
+
+def solve(right_side, transfer, two_step, next_map, diag_inverse):
+    chain_length = lax.axis_size("aux")
     driving = product(diag_inverse, right_side)
-    chain_length = lax.axis_size("aux")
-    incoming = from_behind(driving, "aux", 1)
+    paired = driving + product(transfer, from_behind(driving, "aux", 1))
+    solved = paired
+    for _ in range(chain_length // 2 - 1):
+        solved = paired + product(two_step, from_behind(solved, "aux", 2))
+    solved_next = from_behind(driving, "aux", -1) + product(next_map, solved)
+    back_map = next_map.T
+    source = -product(back_map, solved_next)
+    arriving = source
     for _ in range(chain_length - 2):
-        incoming = from_behind(product(transfer, incoming) + driving, "aux", 1)
-    solved = product(transfer, incoming) + driving
-    source = product(sub_factor.T, product(diag_inverse.T, solved))
-    back_map = transfer.T
-    arriving = from_behind(source, "aux", -1)
-    for _ in range(chain_length - 2):
-        arriving = from_behind(product(back_map, arriving) + source, "aux", -1)
+        arriving = source + product(back_map, from_behind(arriving, "aux", -1))
     return product(diag_inverse.T, solved - arriving)
 
 
@@ -127,13 +152,15 @@
 def per_device(three_center, densities, screen_mask, diag_inverse, sub_factor):
     screened = screen_block(three_center, screen_mask)
     transfer = -product(diag_inverse, sub_factor)
+    previous_map, next_map = neighbour_maps(transfer)
+    two_step = product(transfer, previous_map)
     width = densities.shape[1] // SLICES
     results = []
     for part in range(SLICES):
         dens_part = densities[:, part * width:(part + 1) * width]
         gamma_partial = gamma_over_aux(screened, dens_part)
         right_side = reduce_scatter_columns(gamma_partial, "pair")
-        coefficients = solve(right_side, transfer, diag_inverse, sub_factor)
+        coefficients = solve(right_side, transfer, two_step, next_map, diag_inverse)
         coeff_full = all_gather_columns(coefficients, "pair")
         partial = contract_first(screened, coeff_full)
         results.append(reduce_over_aux(partial))

time: 181 us -> 184 us (1.017)
  matrix products: 22.7 us -> 24.9 us
    ppermute x36, waiting for transfers between devices: 28.8 us -> 22.5 us  [from_behind(): return lax.ppermute(array, axis, pairs)]
    ppermute x12 -> x15, waiting for transfers between devices: 11.8 us -> 17.1 us  [swap(): return lax.ppermute(array, axis, [(i, i ^ bit) for i in range(count)])]
    ppermute x36, starting transfers between devices: 93.6 us -> 97.3 us  [from_behind(): return lax.ppermute(array, axis, pairs)]
    ppermute x12 -> x15, starting transfers between devices: 12.3 us -> 9.79 us  [swap(): return lax.ppermute(array, axis, [(i, i ^ bit) for i in range(count)])]
    dot_general x33 -> x32, matrix products: 20.7 us -> 22.8 us  [product(): jnp.dot(left, right, precision=lax.Precision.HIGH, preferred_element_type...]
  transfers between devices with their start and end apart: 48 -> 51, of which waited for: 21 -> 20; matrix products, arithmetic and copies ran while one was open for 16% -> 18% of each run, Pallas kernels for 0% -> 0%
where the time goes in v5:
time: 184 us; the launch traced here: 183 us
  starting transfers between devices  107 us (58%)
  waiting for transfers between devices  39.6 us (22%)
  matrix products  24.9 us (14%)
  local copies, waits for them, and re-layouts  7.17 us (4%)
  other arithmetic  3.41 us (2%)
    ppermute x36, starting transfers between devices, from_behind(): return lax.ppermute(array, axis, pairs)  97.3 us
    dot_general x32, matrix products, product(): jnp.dot(left, right, precision=lax.Precision.HIGH, preferred_element_type...  22.8 us
    ppermute x36, waiting for transfers between devices, from_behind(): return lax.ppermute(array, axis, pairs)  22.5 us
    ppermute x15, waiting for transfers between devices, swap(): return lax.ppermute(array, axis, [(i, i ^ bit) for i in range(count)])  17.1 us
    ppermute x15, starting transfers between devices, swap(): return lax.ppermute(array, axis, [(i, i ^ bit) for i in range(count)])  9.79 us
  transfers between devices with their start and end apart: 51, of which 20 were waited for; matrix products, arithmetic and copies ran while one was open for 18% of the time, Pallas kernels for 0%

profile of v5, /device:TPU:0, one launch (start us, length us, event | category | flops | bytes accessed | tf_op | source)
XLA Modules:
  0.0 183.2 jit_solution(11699472354924827304)
XLA Ops:
  0.0 2.0 %fusion.71 = (f32[256,256]{1,0:T(8,128)}, f32[256,256]{1,0:T(8,128)}) fusion(f32[256,512]{1,0:T(8,128)} %param.6), kind=kLoop, calls=%fused_computation.132 | loop fusion | bytes 1048576 | tf_op jit(solution)/shard_map/slice | solution.py:160
  2.0 5.6 %collective-permute-start = (f32[256,256]{1,0:T(8,128)}, f32[256,256]{1,0:T(8,128)}, u32[]{:S(2)}, u32[]{:S(2)}) collective-permute-start(f32[256,256]{1,0:T(8,128)} %get-tuple-element.19), channel_id=1, source_target_pairs={{0,1},{1,2},{2,3},{4,5},{5,6},{6,7},{8,9},{9,10},{10,11},{12,13},{... | collective-permute-start | bytes 786440 | tf_op jit(solution)/shard_map/ppermute | solution.py:10
  8.9 2.2 %convolution_negate_fusion = f32[512,512]{0,1:T(8,128)S(1)} fusion(f32[512,512]{1,0:T(8,128)S(1)} %copy-done, f32[512,512]{1,0:T(8,128)} %param.9), kind=kOutput, calls=%fused_computation.2 | convolution fusion | flops 805568512 | bytes 3145728 | tf_op jit(solution)/shard_map/dot_general | solution.py:27
  12.0 4.5 %collective-permute-start.10 = (f32[512,64]{0,1:T(8,128)}, f32[512,64]{0,1:T(8,128)S(1)}, u32[]{:S(2)}, u32[]{:S(2)}) collective-permute-start(f32[512,64]{0,1:T(8,128)} %constant_dynamic-slice_fusion.4), channel_id=1, source_target_pairs={{0,1},{1,2},{2,3},{4,5},{5,6},{6,7},{8,9},{9,10},{10,11},{12,13},{... | collective-permute-start | bytes 393224 | tf_op jit(solution)/shard_map/ppermute | solution.py:10
  17.8 5.3 %collective-permute-start.28 = (f32[256,256]{1,0:T(8,128)}, f32[256,256]{1,0:T(8,128)}, u32[]{:S(2)}, u32[]{:S(2)}) collective-permute-start(f32[256,256]{1,0:T(8,128)} %get-tuple-element.20), channel_id=1, source_target_pairs={{0,1},{1,2},{2,3},{4,5},{5,6},{6,7},{8,9},{9,10},{10,11},{12,13},{... | collective-permute-start | bytes 786440 | tf_op jit(solution)/shard_map/ppermute | solution.py:10
  23.1 2.9 %copy.8 = f32[512,1024]{0,1:T(8,128)} copy(f32[512,1024]{1,0:T(8,128)} %param.5) | data formatting | bytes 4194304 | tf_op args[0]
  26.3 1.9 %bitcast_multiply_fusion = f32[512,1024]{0,1:T(8,128)S(1)} fusion(f32[512,1024]{0,1:T(8,128)} %copy.8, f32[512,16]{0,1:T(8,128)S(1)} %reshape.19), kind=kLoop, calls=%fused_computation.1 | loop fusion | flops 524288 | bytes 4227072 | tf_op jit(solution)/shard_map/mul | solution.py:23
  32.2 1.6 collective-permute-start.12
  35.1 5.2 %collective-permute-start.2 = (f32[256,256]{1,0:T(8,128)}, f32[256,256]{1,0:T(8,128)S(1)}, u32[]{:S(2)}, u32[]{:S(2)}) collective-permute-start(f32[256,256]{1,0:T(8,128)} %collective-permute-done), channel_id=1, source_target_pairs={{0,1},{1,2},{2,3},{4,5},{5,6},{6,7},{8,9},{9,10},{10,11},{12,13},{... | collective-permute-start | bytes 786440 | tf_op jit(solution)/shard_map/ppermute | solution.py:10
  40.3 3.9 %collective-permute-start.30 = (f32[256,256]{1,0:T(8,128)}, f32[256,256]{1,0:T(8,128)S(1)}, u32[]{:S(2)}, u32[]{:S(2)}) collective-permute-start(f32[256,256]{1,0:T(8,128)} %collective-permute-done.28), channel_id=1, source_target_pairs={{0,1},{1,2},{2,3},{4,5},{5,6},{6,7},{8,9},{9,10},{10,11},{12,13},{... | collective-permute-start | bytes 786440 | tf_op jit(solution)/shard_map/ppermute | solution.py:10
  50.2 1.6 collective-permute-start.13
  53.5 5.2 %collective-permute-start.4 = (f32[256,256]{1,0:T(8,128)S(1)}, f32[256,256]{1,0:T(8,128)S(1)}, u32[]{:S(2)}, u32[]{:S(2)}) collective-permute-start(f32[256,256]{1,0:T(8,128)S(1)} %collective-permute-done.2), channel_id=1, source_target_pairs={{0,1},{1,2},{2,3},{4,5},{5,6},{6,7},{8,9},{9,10},{10,11},{12,13},{... | collective-permute-start | bytes 786440 | tf_op jit(solution)/shard_map/ppermute | solution.py:10
  60.4 4.6 %collective-permute-start.32 = (f32[256,256]{1,0:T(8,128)S(1)}, f32[256,256]{1,0:T(8,128)S(1)}, u32[]{:S(2)}, u32[]{:S(2)}) collective-permute-start(f32[256,256]{1,0:T(8,128)S(1)} %collective-permute-done.30), channel_id=1, source_target_pairs={{0,1},{1,2},{2,3},{4,5},{5,6},{6,7},{8,9},{9,10},{10,11},{12,13},{... | collective-permute-start | bytes 786440 | tf_op jit(solution)/shard_map/ppermute | solution.py:10
  72.6 4.2 %collective-permute-done.7 = f32[512,64]{0,1:T(8,128)S(1)} collective-permute-done((f32[512,64]{0,1:T(8,128)S(1)}, f32[512,64]{0,1:T(8,128)S(1)}, u32[]{:S(2)}, u32[]{:S(2)}) %collective-permute-start.7) | collective-permute-done | bytes 131104 | tf_op jit(solution)/shard_map/ppermute | solution.py:15
  79.2 2.5 %collective-permute-done.8 = f32[512,32]{0,1:T(8,128)S(1)} collective-permute-done((f32[512,32]{0,1:T(8,128)S(1)}, f32[512,32]{0,1:T(8,128)S(1)}, u32[]{:S(2)}, u32[]{:S(2)}) %collective-permute-start.8) | collective-permute-done | bytes 65568 | tf_op jit(solution)/shard_map/ppermute | solution.py:15
  82.3 4.4 %collective-permute-start.9 = (f32[512,32]{0,1:T(8,128)S(1)}, f32[512,32]{0,1:T(8,128)S(1)}, u32[]{:S(2)}, u32[]{:S(2)}) collective-permute-start(f32[512,32]{0,1:T(8,128)S(1)} %convolution_bitcast_fusion.3), channel_id=1, source_target_pairs={{0,1},{1,2},{2,3},{4,5},{5,6},{6,7},{8,9},{9,10},{10,11},{12,13},{... | collective-permute-start | bytes 196616 | tf_op jit(solution)/shard_map/ppermute | solution.py:10
  88.6 4.5 %collective-permute-start.37 = (f32[512,32]{0,1:T(8,128)S(1)}, f32[512,32]{0,1:T(8,128)S(1)}, u32[]{:S(2)}, u32[]{:S(2)}) collective-permute-start(f32[512,32]{0,1:T(8,128)S(1)} %convolution_bitcast_fusion.1), channel_id=1, source_target_pairs={{0,1},{1,2},{2,3},{4,5},{5,6},{6,7},{8,9},{9,10},{10,11},{12,13},{... | collective-permute-start | bytes 196616 | tf_op jit(solution)/shard_map/ppermute | solution.py:10
  94.9 6.2 %collective-permute-start.15 = (f32[512,32]{0,1:T(8,128)S(1)}, f32[512,32]{0,1:T(8,128)S(1)}, u32[]{:S(2)}, u32[]{:S(2)}) collective-permute-start(f32[512,32]{0,1:T(8,128)S(1)} %convolution_add_fusion.15), channel_id=1, source_target_pairs={{0,2},{1,3},{4,6},{5,7},{8,10},{9,11},{12,14},{13,15},{16,18},{17,... | collective-permute-start | bytes 196616 | tf_op jit(solution)/shard_map/ppermute | solution.py:10
  103.3 1.9 %fusion.72 = f32[512,512]{1,0:T(8,128)S(1)} fusion(f32[512,512]{0,1:T(8,128)S(1)} %copy-done.2, f32[512,512]{0,1:T(8,128)S(1)} %bitcast.72), kind=kOutput, calls=%fused_computation.133 | convolution fusion | flops 805306368 | bytes 3145728 | tf_op jit(solution)/shard_map/dot_general | solution.py:27
  110.9 2.4 %collective-permute-done.17 = f32[512,32]{0,1:T(8,128)S(1)} collective-permute-done((f32[512,32]{0,1:T(8,128)S(1)}, f32[512,32]{0,1:T(8,128)S(1)}, u32[]{:S(2)}, u32[]{:S(2)}) %collective-permute-start.17) | collective-permute-done | bytes 65568 | tf_op jit(solution)/shard_map/ppermute | solution.py:10
  115.2 1.9 %collective-permute-done.40 = f32[512,32]{0,1:T(8,128)S(1)} collective-permute-done((f32[512,32]{0,1:T(8,128)S(1)}, f32[512,32]{0,1:T(8,128)S(1)}, u32[]{:S(2)}, u32[]{:S(2)}) %collective-permute-start.40) | collective-permute-done | bytes 65568 | tf_op jit(solution)/shard_map/ppermute | solution.py:10
  121.2 2.7 %collective-permute-done.41 = f32[512,32]{0,1:T(8,128)S(1)} collective-permute-done((f32[512,32]{0,1:T(8,128)S(1)}, f32[512,32]{0,1:T(8,128)S(1)}, u32[]{:S(2)}, u32[]{:S(2)}) %collective-permute-start.41) | collective-permute-done | bytes 65568 | tf_op jit(solution)/shard_map/ppermute | solution.py:10
  126.5 3.9 %collective-permute-done.20 = f32[512,64]{0,1:T(8,128)S(1)} collective-permute-done((f32[512,64]{0,1:T(8,128)S(1)}, f32[512,64]{0,1:T(8,128)S(1)}, u32[]{:S(2)}, u32[]{:S(2)}) %collective-permute-start.20) | collective-permute-done | bytes 131104 | tf_op jit(solution)/shard_map/ppermute | solution.py:15
  132.2 4.2 %collective-permute-done.43 = f32[512,64]{0,1:T(8,128)S(1)} collective-permute-done((f32[512,64]{0,1:T(8,128)S(1)}, f32[512,64]{0,1:T(8,128)S(1)}, u32[]{:S(2)}, u32[]{:S(2)}) %collective-permute-start.43) | collective-permute-done | bytes 131104 | tf_op jit(solution)/shard_map/ppermute | solution.py:15
  137.7 3.5 %collective-permute-start.22 = (f32[256,256]{0,1:T(8,128)S(1)}, f32[256,256]{0,1:T(8,128)S(1)}, u32[]{:S(2)}, u32[]{:S(2)}) collective-permute-start(f32[256,256]{0,1:T(8,128)S(1)} %get-tuple-element.12), channel_id=1, source_target_pairs={{0,1},{1,2},{2,3},{4,5},{5,6},{6,7},{8,9},{9,10},{10,11},{12,13},{... | collective-permute-start | bytes 786440 | tf_op jit(solution)/shard_map/ppermute | solution.py:10
  143.6 4.6 %collective-permute-start.45 = (f32[256,256]{0,1:T(8,128)S(1)}, f32[256,256]{0,1:T(8,128)S(1)}, u32[]{:S(2)}, u32[]{:S(2)}) collective-permute-start(f32[256,256]{0,1:T(8,128)S(1)} %get-tuple-element.18), channel_id=1, source_target_pairs={{0,1},{1,2},{2,3},{4,5},{5,6},{6,7},{8,9},{9,10},{10,11},{12,13},{... | collective-permute-start | bytes 786440 | tf_op jit(solution)/shard_map/ppermute | solution.py:10
  149.5 2.0 %collective-permute-done.25 = f32[256,256]{0,1:T(8,128)S(1)} collective-permute-done((f32[256,256]{0,1:T(8,128)S(1)}, f32[256,256]{0,1:T(8,128)S(1)}, u32[]{:S(2)}, u32[]{:S(2)}) %collective-permute-start.25) | collective-permute-done | bytes 262176 | tf_op jit(solution)/shard_map/ppermute | solution.py:10
  151.6 3.7 %collective-permute-start.23 = (f32[256,256]{0,1:T(8,128)S(1)}, f32[256,256]{0,1:T(8,128)S(1)}, u32[]{:S(2)}, u32[]{:S(2)}) collective-permute-start(f32[256,256]{0,1:T(8,128)S(1)} %get-tuple-element.10), channel_id=1, source_target_pairs={{0,1},{1,2},{2,3},{4,5},{5,6},{6,7},{8,9},{9,10},{10,11},{12,13},{... | collective-permute-start | bytes 786440 | tf_op jit(solution)/shard_map/ppermute | solution.py:10
  158.0 3.7 %collective-permute-start.46 = (f32[256,256]{0,1:T(8,128)S(1)}, f32[256,256]{0,1:T(8,128)S(1)}, u32[]{:S(2)}, u32[]{:S(2)}) collective-permute-start(f32[256,256]{0,1:T(8,128)S(1)} %get-tuple-element.16), channel_id=1, source_target_pairs={{0,1},{1,2},{2,3},{4,5},{5,6},{6,7},{8,9},{9,10},{10,11},{12,13},{... | collective-permute-start | bytes 786440 | tf_op jit(solution)/shard_map/ppermute | solution.py:10
  164.6 3.2 %collective-permute-start.24 = (f32[256,256]{0,1:T(8,128)S(1)}, f32[256,256]{0,1:T(8,128)S(1)}, u32[]{:S(2)}, u32[]{:S(2)}) collective-permute-start(f32[256,256]{0,1:T(8,128)S(1)} %get-tuple-element.8), channel_id=1, source_target_pairs={{0,1},{1,2},{2,3},{4,5},{5,6},{6,7},{8,9},{9,10},{10,11},{12,13},{... | collective-permute-start | bytes 786440 | tf_op jit(solution)/shard_map/ppermute | solution.py:10
  170.4 3.4 %collective-permute-start.47 = (f32[256,256]{0,1:T(8,128)S(1)}, f32[256,256]{0,1:T(8,128)S(1)}, u32[]{:S(2)}, u32[]{:S(2)}) collective-permute-start(f32[256,256]{0,1:T(8,128)S(1)} %get-tuple-element.14), channel_id=1, source_target_pairs={{0,1},{1,2},{2,3},{4,5},{5,6},{6,7},{8,9},{9,10},{10,11},{12,13},{... | collective-permute-start | bytes 786440 | tf_op jit(solution)/shard_map/ppermute | solution.py:10
  177.7 4.4 %collective-permute-done.50 = f32[256,256]{0,1:T(8,128)S(1)} collective-permute-done((f32[256,256]{0,1:T(8,128)S(1)}, f32[256,256]{0,1:T(8,128)S(1)}, u32[]{:S(2)}, u32[]{:S(2)}) %collective-permute-start.50) | collective-permute-done | bytes 262176 | tf_op jit(solution)/shard_map/ppermute | solution.py:10
  (154 shorter events, 68.4 us)
Async XLA Ops:
  2.0 33.1 %collective-permute-start = (f32[256,256]{1,0:T(8,128)}, f32[256,256]{1,0:T(8,128)}, u32[]{:S(2)}, u32[]{:S(2)}) collective-permute-start(f32[256,256]{1,0:T(8,128)} %get-tuple-element.19), channel_id=1, source_target_pairs={{0,1},{1,2},{2,3},{4,5},{5,6},{6,7},{8,9},{9,10},{10,11},{12,13},{... | collective-permute-start | bytes 786440 | tf_op jit(solution)/shard_map/ppermute | solution.py:10
  7.6 26.2 %collective-permute-start.1 = (f32[256,256]{1,0:T(8,128)}, f32[256,256]{1,0:T(8,128)}, u32[]{:S(2)}, u32[]{:S(2)}) collective-permute-start(f32[256,256]{1,0:T(8,128)} %get-tuple-element.19), channel_id=1, source_target_pairs={{1,0},{2,1},{3,2},{5,4},{6,5},{7,6},{9,8},{10,9},{11,10},{13,12},{... | collective-permute-start | bytes 786440 | tf_op jit(solution)/shard_map/ppermute | solution.py:10
  12.0 18.9 %collective-permute-start.10 = (f32[512,64]{0,1:T(8,128)}, f32[512,64]{0,1:T(8,128)S(1)}, u32[]{:S(2)}, u32[]{:S(2)}) collective-permute-start(f32[512,64]{0,1:T(8,128)} %constant_dynamic-slice_fusion.4), channel_id=1, source_target_pairs={{0,1},{1,2},{2,3},{4,5},{5,6},{6,7},{8,9},{9,10},{10,11},{12,13},{... | collective-permute-start | bytes 393224 | tf_op jit(solution)/shard_map/ppermute | solution.py:10
  16.5 15.7 %collective-permute-start.11 = (f32[512,64]{0,1:T(8,128)}, f32[512,64]{0,1:T(8,128)S(1)}, u32[]{:S(2)}, u32[]{:S(2)}) collective-permute-start(f32[512,64]{0,1:T(8,128)} %constant_dynamic-slice_fusion.4), channel_id=1, source_target_pairs={{1,0},{2,1},{3,2},{5,4},{6,5},{7,6},{9,8},{10,9},{11,10},{13,12},{... | collective-permute-start | bytes 393224 | tf_op jit(solution)/shard_map/ppermute | solution.py:10
  17.8 22.5 %collective-permute-start.28 = (f32[256,256]{1,0:T(8,128)}, f32[256,256]{1,0:T(8,128)}, u32[]{:S(2)}, u32[]{:S(2)}) collective-permute-start(f32[256,256]{1,0:T(8,128)} %get-tuple-element.20), channel_id=1, source_target_pairs={{0,1},{1,2},{2,3},{4,5},{5,6},{6,7},{8,9},{9,10},{10,11},{12,13},{... | collective-permute-start | bytes 786440 | tf_op jit(solution)/shard_map/ppermute | solution.py:10
  30.9 16.1 %collective-permute-start.29 = (f32[256,256]{1,0:T(8,128)}, f32[256,256]{1,0:T(8,128)S(1)}, u32[]{:S(2)}, u32[]{:S(2)}) collective-permute-start(f32[256,256]{1,0:T(8,128)} %get-tuple-element.20), channel_id=1, source_target_pairs={{1,0},{2,1},{3,2},{5,4},{6,5},{7,6},{9,8},{10,9},{11,10},{13,12},{... | collective-permute-start | bytes 786440 | tf_op jit(solution)/shard_map/ppermute | solution.py:10
  32.2 18.0 %collective-permute-start.12 = (f32[512,128]{0,1:T(8,128)S(1)}, f32[512,128]{0,1:T(8,128)S(1)}, u32[]{:S(2)}, u32[]{:S(2)}) collective-permute-start(f32[512,128]{0,1:T(8,128)S(1)} %pad_maximum_fusion.1), channel_id=1, source_target_pairs={{0,16},{4,20},{8,24},{12,28},{16,0},{20,4},{24,8},{28,12},{1,17},{... | collective-permute-start | bytes 786440 | tf_op jit(solution)/shard_map/ppermute | solution.py:15
  33.8 18.0 %collective-permute-start.3 = (f32[256,256]{1,0:T(8,128)}, f32[256,256]{1,0:T(8,128)S(1)}, u32[]{:S(2)}, u32[]{:S(2)}) collective-permute-start(f32[256,256]{1,0:T(8,128)} %collective-permute-done.1), channel_id=1, source_target_pairs={{1,0},{2,1},{3,2},{5,4},{6,5},{7,6},{9,8},{10,9},{11,10},{13,12},{... | collective-permute-start | bytes 786440 | tf_op jit(solution)/shard_map/ppermute | solution.py:10
  35.1 18.4 %collective-permute-start.2 = (f32[256,256]{1,0:T(8,128)}, f32[256,256]{1,0:T(8,128)S(1)}, u32[]{:S(2)}, u32[]{:S(2)}) collective-permute-start(f32[256,256]{1,0:T(8,128)} %collective-permute-done), channel_id=1, source_target_pairs={{0,1},{1,2},{2,3},{4,5},{5,6},{6,7},{8,9},{9,10},{10,11},{12,13},{... | collective-permute-start | bytes 786440 | tf_op jit(solution)/shard_map/ppermute | solution.py:10
  40.3 20.1 %collective-permute-start.30 = (f32[256,256]{1,0:T(8,128)}, f32[256,256]{1,0:T(8,128)S(1)}, u32[]{:S(2)}, u32[]{:S(2)}) collective-permute-start(f32[256,256]{1,0:T(8,128)} %collective-permute-done.28), channel_id=1, source_target_pairs={{0,1},{1,2},{2,3},{4,5},{5,6},{6,7},{8,9},{9,10},{10,11},{12,13},{... | collective-permute-start | bytes 786440 | tf_op jit(solution)/shard_map/ppermute | solution.py:10
  47.0 11.7 %collective-permute-start.31 = (f32[256,256]{1,0:T(8,128)S(1)}, f32[256,256]{1,0:T(8,128)S(1)}, u32[]{:S(2)}, u32[]{:S(2)}) collective-permute-start(f32[256,256]{1,0:T(8,128)S(1)} %collective-permute-done.29), channel_id=1, source_target_pairs={{1,0},{2,1},{3,2},{5,4},{6,5},{7,6},{9,8},{10,9},{11,10},{13,12},{... | collective-permute-start | bytes 786440 | tf_op jit(solution)/shard_map/ppermute | solution.py:10
  50.2 19.2 %collective-permute-start.13 = (f32[512,256]{0,1:T(8,128)S(1)}, f32[512,256]{0,1:T(8,128)S(1)}, u32[]{:S(2)}, u32[]{:S(2)}) collective-permute-start(f32[512,256]{0,1:T(8,128)S(1)} %maximum_select_fusion.3), channel_id=1, source_target_pairs={{0,8},{4,12},{8,0},{12,4},{16,24},{20,28},{24,16},{28,20},{1,9},{5... | collective-permute-start | bytes 1572872 | tf_op jit(solution)/shard_map/ppermute | solution.py:15
  51.8 14.1 %collective-permute-start.5 = (f32[256,256]{1,0:T(8,128)S(1)}, f32[256,256]{1,0:T(8,128)S(1)}, u32[]{:S(2)}, u32[]{:S(2)}) collective-permute-start(f32[256,256]{1,0:T(8,128)S(1)} %collective-permute-done.3), channel_id=1, source_target_pairs={{1,0},{2,1},{3,2},{5,4},{6,5},{7,6},{9,8},{10,9},{11,10},{13,12},{... | collective-permute-start | bytes 786440 | tf_op jit(solution)/shard_map/ppermute | solution.py:10
  53.5 12.8 %collective-permute-start.4 = (f32[256,256]{1,0:T(8,128)S(1)}, f32[256,256]{1,0:T(8,128)S(1)}, u32[]{:S(2)}, u32[]{:S(2)}) collective-permute-start(f32[256,256]{1,0:T(8,128)S(1)} %collective-permute-done.2), channel_id=1, source_target_pairs={{0,1},{1,2},{2,3},{4,5},{5,6},{6,7},{8,9},{9,10},{10,11},{12,13},{... | collective-permute-start | bytes 786440 | tf_op jit(solution)/shard_map/ppermute | solution.py:10
  60.4 8.4 %collective-permute-start.32 = (f32[256,256]{1,0:T(8,128)S(1)}, f32[256,256]{1,0:T(8,128)S(1)}, u32[]{:S(2)}, u32[]{:S(2)}) collective-permute-start(f32[256,256]{1,0:T(8,128)S(1)} %collective-permute-done.30), channel_id=1, source_target_pairs={{0,1},{1,2},{2,3},{4,5},{5,6},{6,7},{8,9},{9,10},{10,11},{12,13},{... | collective-permute-start | bytes 786440 | tf_op jit(solution)/shard_map/ppermute | solution.py:10
  69.5 33.2 %collective-permute-start.14 = (f32[512,512]{0,1:T(8,128)S(1)}, f32[512,512]{0,1:T(8,128)S(1)}, u32[]{:S(2)}, u32[]{:S(2)}) collective-permute-start(f32[512,512]{0,1:T(8,128)S(1)} %maximum_select_fusion.1), channel_id=1, source_target_pairs={{0,4},{4,0},{8,12},{12,8},{16,20},{20,16},{24,28},{28,24},{1,5},{5... | collective-permute-start | bytes 3145736 | tf_op jit(solution)/shard_map/ppermute | solution.py:15
  78.6 9.4 %collective-permute-start.36 = (f32[512,32]{0,1:T(8,128)S(1)}, f32[512,32]{0,1:T(8,128)S(1)}, u32[]{:S(2)}, u32[]{:S(2)}) collective-permute-start(f32[512,32]{0,1:T(8,128)S(1)} %slice_select_fusion.4), channel_id=1, source_target_pairs={{0,16},{4,20},{8,24},{12,28},{16,0},{20,4},{24,8},{28,12},{1,17},{... | collective-permute-start | bytes 196616 | tf_op jit(solution)/shard_map/ppermute | solution.py:15
  82.3 12.2 %collective-permute-start.9 = (f32[512,32]{0,1:T(8,128)S(1)}, f32[512,32]{0,1:T(8,128)S(1)}, u32[]{:S(2)}, u32[]{:S(2)}) collective-permute-start(f32[512,32]{0,1:T(8,128)S(1)} %convolution_bitcast_fusion.3), channel_id=1, source_target_pairs={{0,1},{1,2},{2,3},{4,5},{5,6},{6,7},{8,9},{9,10},{10,11},{12,13},{... | collective-permute-start | bytes 196616 | tf_op jit(solution)/shard_map/ppermute | solution.py:10
  86.7 19.5 %collective-permute-start.16 = (f32[512,32]{0,1:T(8,128)S(1)}, f32[512,32]{0,1:T(8,128)S(1)}, u32[]{:S(2)}, u32[]{:S(2)}) collective-permute-start(f32[512,32]{0,1:T(8,128)S(1)} %convolution_bitcast_fusion.3), channel_id=1, source_target_pairs={{1,0},{2,1},{3,2},{5,4},{6,5},{7,6},{9,8},{10,9},{11,10},{13,12},{... | collective-permute-start | bytes 196616 | tf_op jit(solution)/shard_map/ppermute | solution.py:10
  88.6 12.5 %collective-permute-start.37 = (f32[512,32]{0,1:T(8,128)S(1)}, f32[512,32]{0,1:T(8,128)S(1)}, u32[]{:S(2)}, u32[]{:S(2)}) collective-permute-start(f32[512,32]{0,1:T(8,128)S(1)} %convolution_bitcast_fusion.1), channel_id=1, source_target_pairs={{0,1},{1,2},{2,3},{4,5},{5,6},{6,7},{8,9},{9,10},{10,11},{12,13},{... | collective-permute-start | bytes 196616 | tf_op jit(solution)/shard_map/ppermute | solution.py:10
  93.1 15.9 %collective-permute-start.39 = (f32[512,32]{0,1:T(8,128)S(1)}, f32[512,32]{0,1:T(8,128)S(1)}, u32[]{:S(2)}, u32[]{:S(2)}) collective-permute-start(f32[512,32]{0,1:T(8,128)S(1)} %convolution_bitcast_fusion.1), channel_id=1, source_target_pairs={{1,0},{2,1},{3,2},{5,4},{6,5},{7,6},{9,8},{10,9},{11,10},{13,12},{... | collective-permute-start | bytes 196616 | tf_op jit(solution)/shard_map/ppermute | solution.py:10
  94.9 10.3 %collective-permute-start.15 = (f32[512,32]{0,1:T(8,128)S(1)}, f32[512,32]{0,1:T(8,128)S(1)}, u32[]{:S(2)}, u32[]{:S(2)}) collective-permute-start(f32[512,32]{0,1:T(8,128)S(1)} %convolution_add_fusion.15), channel_id=1, source_target_pairs={{0,2},{1,3},{4,6},{5,7},{8,10},{9,11},{12,14},{13,15},{16,18},{17,... | collective-permute-start | bytes 196616 | tf_op jit(solution)/shard_map/ppermute | solution.py:10
  137.7 11.8 %collective-permute-start.22 = (f32[256,256]{0,1:T(8,128)S(1)}, f32[256,256]{0,1:T(8,128)S(1)}, u32[]{:S(2)}, u32[]{:S(2)}) collective-permute-start(f32[256,256]{0,1:T(8,128)S(1)} %get-tuple-element.12), channel_id=1, source_target_pairs={{0,1},{1,2},{2,3},{4,5},{5,6},{6,7},{8,9},{9,10},{10,11},{12,13},{... | collective-permute-start | bytes 786440 | tf_op jit(solution)/shard_map/ppermute | solution.py:10
  141.2 10.3 %collective-permute-start.25 = (f32[256,256]{0,1:T(8,128)S(1)}, f32[256,256]{0,1:T(8,128)S(1)}, u32[]{:S(2)}, u32[]{:S(2)}) collective-permute-start(f32[256,256]{0,1:T(8,128)S(1)} %get-tuple-element.11), channel_id=1, source_target_pairs={{1,0},{2,1},{3,2},{5,4},{6,5},{7,6},{9,8},{10,9},{11,10},{13,12},{... | collective-permute-start | bytes 786440 | tf_op jit(solution)/shard_map/ppermute | solution.py:10
  143.6 13.0 %collective-permute-start.45 = (f32[256,256]{0,1:T(8,128)S(1)}, f32[256,256]{0,1:T(8,128)S(1)}, u32[]{:S(2)}, u32[]{:S(2)}) collective-permute-start(f32[256,256]{0,1:T(8,128)S(1)} %get-tuple-element.18), channel_id=1, source_target_pairs={{0,1},{1,2},{2,3},{4,5},{5,6},{6,7},{8,9},{9,10},{10,11},{12,13},{... | collective-permute-start | bytes 786440 | tf_op jit(solution)/shard_map/ppermute | solution.py:10
  148.2 9.8 %collective-permute-start.48 = (f32[256,256]{0,1:T(8,128)S(1)}, f32[256,256]{0,1:T(8,128)S(1)}, u32[]{:S(2)}, u32[]{:S(2)}) collective-permute-start(f32[256,256]{0,1:T(8,128)S(1)} %get-tuple-element.17), channel_id=1, source_target_pairs={{1,0},{2,1},{3,2},{5,4},{6,5},{7,6},{9,8},{10,9},{11,10},{13,12},{... | collective-permute-start | bytes 786440 | tf_op jit(solution)/shard_map/ppermute | solution.py:10
  151.6 11.5 %collective-permute-start.23 = (f32[256,256]{0,1:T(8,128)S(1)}, f32[256,256]{0,1:T(8,128)S(1)}, u32[]{:S(2)}, u32[]{:S(2)}) collective-permute-start(f32[256,256]{0,1:T(8,128)S(1)} %get-tuple-element.10), channel_id=1, source_target_pairs={{0,1},{1,2},{2,3},{4,5},{5,6},{6,7},{8,9},{9,10},{10,11},{12,13},{... | collective-permute-start | bytes 786440 | tf_op jit(solution)/shard_map/ppermute | solution.py:10
  155.2 9.2 %collective-permute-start.26 = (f32[256,256]{0,1:T(8,128)S(1)}, f32[256,256]{0,1:T(8,128)S(1)}, u32[]{:S(2)}, u32[]{:S(2)}) collective-permute-start(f32[256,256]{0,1:T(8,128)S(1)} %get-tuple-element.9), channel_id=1, source_target_pairs={{1,0},{2,1},{3,2},{5,4},{6,5},{7,6},{9,8},{10,9},{11,10},{13,12},{... | collective-permute-start | bytes 786440 | tf_op jit(solution)/shard_map/ppermute | solution.py:10
  158.0 11.1 %collective-permute-start.46 = (f32[256,256]{0,1:T(8,128)S(1)}, f32[256,256]{0,1:T(8,128)S(1)}, u32[]{:S(2)}, u32[]{:S(2)}) collective-permute-start(f32[256,256]{0,1:T(8,128)S(1)} %get-tuple-element.16), channel_id=1, source_target_pairs={{0,1},{1,2},{2,3},{4,5},{5,6},{6,7},{8,9},{9,10},{10,11},{12,13},{... | collective-permute-start | bytes 786440 | tf_op jit(solution)/shard_map/ppermute | solution.py:10
  161.8 8.5 %collective-permute-start.49 = (f32[256,256]{0,1:T(8,128)S(1)}, f32[256,256]{0,1:T(8,128)S(1)}, u32[]{:S(2)}, u32[]{:S(2)}) collective-permute-start(f32[256,256]{0,1:T(8,128)S(1)} %get-tuple-element.15), channel_id=1, source_target_pairs={{1,0},{2,1},{3,2},{5,4},{6,5},{7,6},{9,8},{10,9},{11,10},{13,12},{... | collective-permute-start | bytes 786440 | tf_op jit(solution)/shard_map/ppermute | solution.py:10
  164.6 10.5 %collective-permute-start.24 = (f32[256,256]{0,1:T(8,128)S(1)}, f32[256,256]{0,1:T(8,128)S(1)}, u32[]{:S(2)}, u32[]{:S(2)}) collective-permute-start(f32[256,256]{0,1:T(8,128)S(1)} %get-tuple-element.8), channel_id=1, source_target_pairs={{0,1},{1,2},{2,3},{4,5},{5,6},{6,7},{8,9},{9,10},{10,11},{12,13},{... | collective-permute-start | bytes 786440 | tf_op jit(solution)/shard_map/ppermute | solution.py:10
  167.8 8.7 %collective-permute-start.27 = (f32[256,256]{0,1:T(8,128)S(1)}, f32[256,256]{0,1:T(8,128)S(1)}, u32[]{:S(2)}, u32[]{:S(2)}) collective-permute-start(f32[256,256]{0,1:T(8,128)S(1)} %get-tuple-element.7), channel_id=1, source_target_pairs={{1,0},{2,1},{3,2},{5,4},{6,5},{7,6},{9,8},{10,9},{11,10},{13,12},{... | collective-permute-start | bytes 786440 | tf_op jit(solution)/shard_map/ppermute | solution.py:10
  (25 other events, 179.0 us)

commit v6 on v2

--- a/solution.py
+++ b/solution.py
@@ -1,7 +1,86 @@
+import functools
+
 import jax
 import jax.numpy as jnp
 from jax import lax
+from jax.experimental import pallas as pl
+from jax.experimental.pallas import tpu as pltpu
 from jax.sharding import PartitionSpec as P
+
+
+def split3(x):
+    high = x.astype(jnp.bfloat16)
+    low = (x - high.astype(jnp.float32)).astype(jnp.bfloat16)
+    return high, low
+
+
+def dot3(a, b, dims):
+    ah, al = split3(a)
+    bh, bl = split3(b)
+    f = functools.partial(lax.dot_general, dimension_numbers=(dims, ((), ())), preferred_element_type=jnp.float32)
+    return f(ah, bh) + (f(ah, bl) + f(al, bh))
+
+
+def expanded_mask(mask, rows, start_col, cols, row_size, col_size):
+    mask_rows, mask_cols = mask.shape
+    pick_rows = (lax.broadcasted_iota(jnp.int32, (rows, mask_rows), 0) // row_size
+                 == lax.broadcasted_iota(jnp.int32, (rows, mask_rows), 1))
+    pick_cols = (lax.broadcasted_iota(jnp.int32, (mask_cols, cols), 0)
+                 == (lax.broadcasted_iota(jnp.int32, (mask_cols, cols), 1) + start_col) // col_size)
+    by_rows = jnp.dot(pick_rows.astype(jnp.bfloat16), mask.astype(jnp.bfloat16), preferred_element_type=jnp.float32)
+    return jnp.dot(by_rows.astype(jnp.bfloat16), pick_cols.astype(jnp.bfloat16), preferred_element_type=jnp.float32)
+
+
+def gamma_kernel(block_ref, three_ref, mask_ref, dens_ref, acc_ref, out_ref, *, row_size, col_size, cut):
+    rows, width = dens_ref.shape
+    start = block_ref[0] * rows
+    if cut:
+        tile = three_ref[:, pl.ds(pl.multiple_of(start, 128), rows)]
+    else:
+        tile = three_ref[...]
+    screened = tile * expanded_mask(mask_ref[...], tile.shape[0], start, rows, row_size, col_size)
+    out_ref[...] = acc_ref[...] + dot3(screened, dens_ref[...], ((1,), (0,)))
+
+
+def gamma_block(block, three_center, mask_f, dens, acc):
+    rows_total, cols_total = three_center.shape
+    row_size = rows_total // mask_f.shape[0]
+    col_size = cols_total // mask_f.shape[1]
+    rows = dens.shape[0]
+    cut = rows % 128 == 0
+    if not cut:
+        three_center = lax.dynamic_slice_in_dim(three_center, block * rows, rows, axis=1)
+    kernel = functools.partial(gamma_kernel, row_size=row_size, col_size=col_size, cut=cut)
+    vmem = pl.BlockSpec(memory_space=pltpu.VMEM)
+    return pl.pallas_call(
+        kernel,
+        out_shape=jax.ShapeDtypeStruct(acc.shape, jnp.float32),
+        in_specs=[pl.BlockSpec(memory_space=pltpu.SMEM), vmem, vmem, vmem, vmem],
+        out_specs=vmem,
+        input_output_aliases={4: 0},
+        cost_estimate=pl.CostEstimate(flops=6 * rows_total * rows * dens.shape[1], transcendentals=0,
+                                      bytes_accessed=4 * (rows_total * rows + dens.size + 2 * acc.size)),
+    )(jnp.reshape(block, (1,)).astype(jnp.int32), three_center, mask_f, dens, acc)
+
+
+def response_kernel(three_ref, mask_ref, coef_ref, out_ref, *, row_size, col_size):
+    rows, cols = three_ref.shape
+    screened = three_ref[...] * expanded_mask(mask_ref[...], rows, 0, cols, row_size, col_size)
+    out_ref[...] = dot3(screened, coef_ref[...], ((0,), (0,)))
+
+
+def response(three_center, mask_f, coef):
+    rows_total, cols_total = three_center.shape
+    kernel = functools.partial(response_kernel, row_size=rows_total // mask_f.shape[0], col_size=cols_total // mask_f.shape[1])
+    vmem = pl.BlockSpec(memory_space=pltpu.VMEM)
+    return pl.pallas_call(
+        kernel,
+        out_shape=jax.ShapeDtypeStruct((cols_total, coef.shape[1]), jnp.float32),
+        in_specs=[vmem, vmem, vmem],
+        out_specs=vmem,
+        cost_estimate=pl.CostEstimate(flops=6 * rows_total * cols_total * coef.shape[1], transcendentals=0,
+                                      bytes_accessed=4 * (three_center.size + coef.size + cols_total * coef.shape[1])),
+    )(three_center, mask_f, coef)
 
 
 def from_behind(array, axis, by):
@@ -70,22 +149,21 @@
     return current
 
 
-def gamma_over_aux(screened, densities):
+def gamma_over_aux(three_center, mask_f, densities):
     count = lax.axis_size("aux")
     index = lax.axis_index("aux")
-    rows = densities.shape[0]
-
-    def columns(block):
-        start = jnp.clip(block, 0, count - 1) * rows
-        return lax.dynamic_slice_in_dim(screened, start, rows, axis=1)
-
-    gamma = product(columns(index), densities)
+
+    def clip(block):
+        return jnp.clip(block, 0, count - 1)
+
+    gamma = jnp.zeros((three_center.shape[0], densities.shape[1]), jnp.float32)
+    gamma = gamma_block(index, three_center, mask_f, densities, gamma)
     from_left, from_right = densities, densities
     for step in range(count - 1):
         from_left = from_behind(from_left, "aux", 1)
         from_right = from_behind(from_right, "aux", -1)
-        gamma = gamma + product(columns(index - 1 - step), from_left)
-        gamma = gamma + product(columns(index + 1 + step), from_right)
+        gamma = gamma_block(clip(index - 1 - step), three_center, mask_f, from_left, gamma)
+        gamma = gamma_block(clip(index + 1 + step), three_center, mask_f, from_right, gamma)
     return gamma
 
 
@@ -125,17 +203,17 @@
 
 
 def per_device(three_center, densities, screen_mask, diag_inverse, sub_factor):
-    screened = screen_block(three_center, screen_mask)
+    mask_f = screen_mask.astype(jnp.float32)
     transfer = -product(diag_inverse, sub_factor)
     width = densities.shape[1] // SLICES
     results = []
     for part in range(SLICES):
         dens_part = densities[:, part * width:(part + 1) * width]
-        gamma_partial = gamma_over_aux(screened, dens_part)
+        gamma_partial = gamma_over_aux(three_center, mask_f, dens_part)
         right_side = reduce_scatter_columns(gamma_partial, "pair")
         coefficients = solve(right_side, transfer, diag_inverse, sub_factor)
         coeff_full = all_gather_columns(coefficients, "pair")
-        partial = contract_first(screened, coeff_full)
+        partial = response(three_center, mask_f, coeff_full)
         results.append(reduce_over_aux(partial))
     return jnp.concatenate(results, axis=1)
 

time: 181 us -> 251 us (1.39)
  Pallas kernels: 0 us -> 53.2 us
  other arithmetic: 2.82 us -> 17.2 us
  starting transfers between devices: 106 us -> 119 us
  matrix products: 22.7 us -> 12.3 us
    pallas_call x0 -> x16, Pallas kernels: none -> 53.2 us  [the longest x14 44.7 us: gamma_block(): pl.pallas_call(kernel, out_shape=jax.ShapeDtypeStruct(acc.shape, jnp.floa...]
    ppermute x36, waiting for transfers between devices: 28.8 us -> 13.6 us  [from_behind(): return lax.ppermute(array, axis, pairs)]
    ppermute x36, starting transfers between devices: 93.6 us -> 108 us  [from_behind(): return lax.ppermute(array, axis, pairs)]
    ppermute x12, waiting for transfers between devices: 11.8 us -> 25.4 us  [swap(): return lax.ppermute(array, axis, [(i, i ^ bit) for i in range(count)])]
    dot_general x33 -> x19, matrix products: 20.7 us -> 12.3 us  [product(): jnp.dot(left, right, precision=lax.Precision.HIGH, preferred_element_type...]
    add x4, other arithmetic: 0.36 us -> 7.48 us  [reduce_over_aux(): to_left + block(index - (count - 1) + step)]
    dynamic_slice x2, local copies, waits for them, and re-layouts: 0.09 us -> 3.72 us  [block(): return lax.dynamic_slice_in_dim(partial, start, rows, axis=0)]
    select_n x6, other arithmetic: 0.14 us -> 3.4 us  [reduce_scatter_columns(): send = jnp.where(upper, low, high)]
  transfers between devices with their start and end apart: 48 -> 48, of which waited for: 21 -> 14; matrix products, arithmetic and copies ran while one was open for 16% -> 13% of each run, Pallas kernels for 0% -> 21%
where the time goes in v6:
time: 251 us; the launch traced here: 249 us
  starting transfers between devices  119 us (47%)
  Pallas kernels  53.2 us (21%)
  waiting for transfers between devices  39.1 us (16%)
  other arithmetic  17.2 us (7%)
  matrix products  12.3 us (5%)
  local copies, waits for them, and re-layouts  7.28 us (3%)
    ppermute x36, starting transfers between devices, from_behind(): return lax.ppermute(array, axis, pairs)  108 us
    pallas_call x14, Pallas kernels, gamma_block(): pl.pallas_call(kernel, out_shape=jax.ShapeDtypeStruct(acc.shape, jnp.floa...  44.7 us
    ppermute x12, waiting for transfers between devices, swap(): return lax.ppermute(array, axis, [(i, i ^ bit) for i in range(count)])  25.4 us
    ppermute x36, waiting for transfers between devices, from_behind(): return lax.ppermute(array, axis, pairs)  13.6 us
    dot_general x19, matrix products, product(): jnp.dot(left, right, precision=lax.Precision.HIGH, preferred_element_type...  12.3 us
    ppermute x12, starting transfers between devices, swap(): return lax.ppermute(array, axis, [(i, i ^ bit) for i in range(count)])  11.8 us
    pallas_call x2, Pallas kernels, response(): pl.pallas_call(kernel, out_shape=jax.ShapeDtypeStruct((cols_total, coef.s...  8.46 us
    add x4, other arithmetic, reduce_over_aux(): to_left + block(index - (count - 1) + step)  7.48 us
  transfers between devices with their start and end apart: 48, of which 14 were waited for; matrix products, arithmetic and copies ran while one was open for 13% of the time, Pallas kernels for 21%

profile of v6, /device:TPU:0, one launch (start us, length us, event | category | flops | bytes accessed | tf_op | source)
XLA Modules:
  0.0 249.2 jit_solution(638514001505379785)
XLA Ops:
  1.2 4.9 %collective-permute-start.3 = (f32[256,256]{1,0:T(8,128)S(1)}, f32[256,256]{1,0:T(8,128)S(1)}, u32[]{:S(2)}, u32[]{:S(2)}) collective-permute-start(f32[256,256]{1,0:T(8,128)S(1)} %get-tuple-element.17.dens_ref), channel_id=1, source_target_pairs={{0,1},{1,2},{2,3},{4,5},{5,6},{6,7},{8,9},{9,10},{10,11},{12,13},{... | collective-permute-start | bytes 786440 | tf_op jit(solution)/shard_map/ppermute | solution.py:89
  7.4 5.3 %collective-permute-start.27 = (f32[256,256]{1,0:T(8,128)S(1)}, f32[256,256]{1,0:T(8,128)}, u32[]{:S(2)}, u32[]{:S(2)}) collective-permute-start(f32[256,256]{1,0:T(8,128)S(1)} %get-tuple-element.18.dens_ref), channel_id=1, source_target_pairs={{0,1},{1,2},{2,3},{4,5},{5,6},{6,7},{8,9},{9,10},{10,11},{12,13},{... | collective-permute-start | bytes 786440 | tf_op jit(solution)/shard_map/ppermute | solution.py:89
  14.0 4.6 %collective-permute-start.4 = (f32[256,256]{1,0:T(8,128)S(1)}, f32[256,256]{1,0:T(8,128)S(1)}, u32[]{:S(2)}, u32[]{:S(2)}) collective-permute-start(f32[256,256]{1,0:T(8,128)S(1)} %collective-permute-done.3.dens_ref), channel_id=1, source_target_pairs={{0,1},{1,2},{2,3},{4,5},{5,6},{6,7},{8,9},{9,10},{10,11},{12,13},{... | collective-permute-start | bytes 786440 | tf_op jit(solution)/shard_map/ppermute | solution.py:89
  19.9 4.6 %collective-permute-start.28 = (f32[256,256]{1,0:T(8,128)}, f32[256,256]{1,0:T(8,128)S(1)}, u32[]{:S(2)}, u32[]{:S(2)}) collective-permute-start(f32[256,256]{1,0:T(8,128)} %collective-permute-done.27.dens_ref), channel_id=1, source_target_pairs={{0,1},{1,2},{2,3},{4,5},{5,6},{6,7},{8,9},{9,10},{10,11},{12,13},{... | collective-permute-start | bytes 786440 | tf_op jit(solution)/shard_map/ppermute | solution.py:89
  25.8 5.3 %collective-permute-start.5 = (f32[256,256]{1,0:T(8,128)S(1)}, f32[256,256]{1,0:T(8,128)}, u32[]{:S(2)}, u32[]{:S(2)}) collective-permute-start(f32[256,256]{1,0:T(8,128)S(1)} %collective-permute-done.4.dens_ref), channel_id=1, source_target_pairs={{0,1},{1,2},{2,3},{4,5},{5,6},{6,7},{8,9},{9,10},{10,11},{12,13},{... | collective-permute-start | bytes 786440 | tf_op jit(solution)/shard_map/ppermute | solution.py:89
  36.1 3.2 %shard_map.55.acc_ref = f32[512,256]{1,0:T(8,128)} custom-call(s32[1]{0:T(128)} %bitcast.6.block_ref, f32[512,1024]{1,0:T(8,128)} %three_ref.31, f32[8,16]{1,0:T(8,128)} %convert_element_type.3.mask_ref, f32[256,256]{1,0:T(8,128)} %copy-done.7, f32[512,256]{1,0:T(8,128)} %broadcast_1_acc_ref.2.clone.1.acc_ref), custom_call_target="tpu_custom_call", output_to_operand_aliasing={{}: (4, {})} | custom-call | flops 201326592 | bytes 1835008 | tf_op jit(solution)/shard_map/pallas_call | solution.py:55
  43.4 3.2 %shard_map.56.acc_ref = f32[512,256]{1,0:T(8,128)} custom-call(s32[1]{0:T(128)} %bitcast.5.block_ref, f32[512,1024]{1,0:T(8,128)} %three_ref.31, f32[8,16]{1,0:T(8,128)} %convert_element_type.3.mask_ref, f32[256,256]{1,0:T(8,128)} %copy-done.12, f32[512,256]{1,0:T(8,128)} %shard_map.55.acc_ref), custom_call_target="tpu_custom_call", output_to_operand_aliasing={{}: (4, {})} | custom-call | flops 201326592 | bytes 1835008 | tf_op jit(solution)/shard_map/pallas_call | solution.py:55
  49.7 3.2 %shard_map.57.acc_ref = f32[512,256]{1,0:T(8,128)} custom-call(s32[1]{0:T(128)} %bitcast.4.block_ref, f32[512,1024]{1,0:T(8,128)} %three_ref.31, f32[8,16]{1,0:T(8,128)} %convert_element_type.3.mask_ref, f32[256,256]{1,0:T(8,128)} %copy-done.11, f32[512,256]{1,0:T(8,128)} %shard_map.56.acc_ref), custom_call_target="tpu_custom_call", output_to_operand_aliasing={{}: (4, {})} | custom-call | flops 201326592 | bytes 1835008 | tf_op jit(solution)/shard_map/pallas_call | solution.py:55
  56.1 4.6 %collective-permute-start.29 = (f32[256,256]{1,0:T(8,128)S(1)}, f32[256,256]{1,0:T(8,128)S(1)}, u32[]{:S(2)}, u32[]{:S(2)}) collective-permute-start(f32[256,256]{1,0:T(8,128)S(1)} %collective-permute-done.28.dens_ref), channel_id=1, source_target_pairs={{0,1},{1,2},{2,3},{4,5},{5,6},{6,7},{8,9},{9,10},{10,11},{12,13},{... | collective-permute-start | bytes 786440 | tf_op jit(solution)/shard_map/ppermute | solution.py:89
  62.0 3.2 %shard_map.58.acc_ref = f32[512,256]{1,0:T(8,128)} custom-call(s32[1]{0:T(128)} %bitcast.3.block_ref, f32[512,1024]{1,0:T(8,128)} %three_ref.31, f32[8,16]{1,0:T(8,128)} %convert_element_type.3.mask_ref, f32[256,256]{1,0:T(8,128)} %copy-done.10, f32[512,256]{1,0:T(8,128)} %shard_map.57.acc_ref), custom_call_target="tpu_custom_call", output_to_operand_aliasing={{}: (4, {})} | custom-call | flops 201326592 | bytes 1835008 | tf_op jit(solution)/shard_map/pallas_call | solution.py:55
  65.2 3.2 %shard_map.66.acc_ref = f32[512,256]{1,0:T(8,128)} custom-call(s32[1]{0:T(128)} %bitcast.3.block_ref, f32[512,1024]{1,0:T(8,128)} %three_ref.31, f32[8,16]{1,0:T(8,128)} %convert_element_type.3.mask_ref, f32[256,256]{1,0:T(8,128)} %copy-done.8, f32[512,256]{1,0:T(8,128)} %shard_map.65.acc_ref), custom_call_target="tpu_custom_call", output_to_operand_aliasing={{}: (4, {})} | custom-call | flops 201326592 | bytes 1835008 | tf_op jit(solution)/shard_map/pallas_call | solution.py:55
  68.4 3.2 %shard_map.59.acc_ref = f32[512,256]{1,0:T(8,128)} custom-call(s32[1]{0:T(128)} %bitcast.2.block_ref, f32[512,1024]{1,0:T(8,128)} %three_ref.31, f32[8,16]{1,0:T(8,128)} %convert_element_type.3.mask_ref, f32[256,256]{1,0:T(8,128)} %collective-permute-done.1.dens_ref, f32[512,256]{1,0:T(8,128)} %shard_map.58.acc_ref), custom_call_target="tpu_custom_call", output_to_operand_aliasing={{}: (4, {})} | custom-call | flops 201326592 | bytes 1835008 | tf_op jit(solution)/shard_map/pallas_call | solution.py:55
  74.8 3.2 %shard_map.60.acc_ref = f32[512,256]{1,0:T(8,128)} custom-call(s32[1]{0:T(128)} %bitcast.1.block_ref, f32[512,1024]{1,0:T(8,128)} %three_ref.31, f32[8,16]{1,0:T(8,128)} %convert_element_type.3.mask_ref, f32[256,256]{1,0:T(8,128)} %collective-permute-done.5.dens_ref, f32[512,256]{1,0:T(8,128)} %shard_map.59.acc_ref), custom_call_target="tpu_custom_call", output_to_operand_aliasing={{}: (4, {})} | custom-call | flops 201326592 | bytes 1835008 | tf_op jit(solution)/shard_map/pallas_call | solution.py:55
  78.0 3.2 %shard_map.61 = f32[512,256]{1,0:T(8,128)} custom-call(s32[1]{0:T(128)} %bitcast.block_ref, f32[512,1024]{1,0:T(8,128)} %three_ref.31, f32[8,16]{1,0:T(8,128)} %convert_element_type.3.mask_ref, f32[256,256]{1,0:T(8,128)} %collective-permute-done.2.dens_ref, f32[512,256]{1,0:T(8,128)} %shard_map.60.acc_ref), custom_call_target="tpu_custom_call", output_to_operand_aliasing={{}: (4, {})} | custom-call | flops 201326592 | bytes 1835008 | tf_op jit(solution)/shard_map/pallas_call | solution.py:55
  86.8 3.2 %shard_map.69 = f32[512,256]{1,0:T(8,128)} custom-call(s32[1]{0:T(128)} %bitcast.block_ref, f32[512,1024]{1,0:T(8,128)} %three_ref.31, f32[8,16]{1,0:T(8,128)} %convert_element_type.3.mask_ref, f32[256,256]{1,0:T(8,128)} %collective-permute-done.26.dens_ref, f32[512,256]{1,0:T(8,128)} %shard_map.68.acc_ref), custom_call_target="tpu_custom_call", output_to_operand_aliasing={{}: (4, {})} | custom-call | flops 201326592 | bytes 1835008 | tf_op jit(solution)/shard_map/pallas_call | solution.py:55
  94.7 6.5 %collective-permute-done.7 = f32[512,64]{1,0:T(8,128)S(1)} collective-permute-done((f32[512,64]{1,0:T(8,128)S(1)}, f32[512,64]{1,0:T(8,128)S(1)}, u32[]{:S(2)}, u32[]{:S(2)}) %collective-permute-start.7) | collective-permute-done | bytes 131104 | tf_op jit(solution)/shard_map/ppermute | solution.py:94
  108.8 4.5 %collective-permute-start.9 = (f32[512,32]{0,1:T(8,128)S(1)}, f32[512,32]{0,1:T(8,128)S(1)}, u32[]{:S(2)}, u32[]{:S(2)}) collective-permute-start(f32[512,32]{0,1:T(8,128)S(1)} %convolution_bitcast_fusion.5), channel_id=1, source_target_pairs={{0,1},{1,2},{2,3},{4,5},{5,6},{6,7},{8,9},{9,10},{10,11},{12,13},{... | collective-permute-start | bytes 196616 | tf_op jit(solution)/shard_map/ppermute | solution.py:89
  114.4 4.7 %collective-permute-start.33 = (f32[512,32]{0,1:T(8,128)S(1)}, f32[512,32]{0,1:T(8,128)S(1)}, u32[]{:S(2)}, u32[]{:S(2)}) collective-permute-start(f32[512,32]{0,1:T(8,128)S(1)} %convolution_bitcast_fusion.3), channel_id=1, source_target_pairs={{0,1},{1,2},{2,3},{4,5},{5,6},{6,7},{8,9},{9,10},{10,11},{12,13},{... | collective-permute-start | bytes 196616 | tf_op jit(solution)/shard_map/ppermute | solution.py:89
  119.7 3.7 %collective-permute-start.10 = (f32[512,32]{0,1:T(8,128)S(1)}, f32[512,32]{0,1:T(8,128)S(1)}, u32[]{:S(2)}, u32[]{:S(2)}) collective-permute-start(f32[512,32]{0,1:T(8,128)S(1)} %convolution_add_fusion.9), channel_id=1, source_target_pairs={{0,1},{1,2},{2,3},{4,5},{5,6},{6,7},{8,9},{9,10},{10,11},{12,13},{... | collective-permute-start | bytes 196616 | tf_op jit(solution)/shard_map/ppermute | solution.py:89
  124.0 4.6 %collective-permute-start.34 = (f32[512,32]{0,1:T(8,128)S(1)}, f32[512,32]{0,1:T(8,128)S(1)}, u32[]{:S(2)}, u32[]{:S(2)}) collective-permute-start(f32[512,32]{0,1:T(8,128)S(1)} %convolution_add_fusion.4), channel_id=1, source_target_pairs={{0,1},{1,2},{2,3},{4,5},{5,6},{6,7},{8,9},{9,10},{10,11},{12,13},{... | collective-permute-start | bytes 196616 | tf_op jit(solution)/shard_map/ppermute | solution.py:89
  131.8 4.1 %collective-permute-start.35 = (f32[512,32]{0,1:T(8,128)S(1)}, f32[512,32]{0,1:T(8,128)S(1)}, u32[]{:S(2)}, u32[]{:S(2)}) collective-permute-start(f32[512,32]{0,1:T(8,128)S(1)} %convolution_add_fusion.3), channel_id=1, source_target_pairs={{0,1},{1,2},{2,3},{4,5},{5,6},{6,7},{8,9},{9,10},{10,11},{12,13},{... | collective-permute-start | bytes 196616 | tf_op jit(solution)/shard_map/ppermute | solution.py:89
  139.6 4.4 %collective-permute-done.12 = f32[512,32]{0,1:T(8,128)S(1)} collective-permute-done((f32[512,32]{0,1:T(8,128)S(1)}, f32[512,32]{0,1:T(8,128)S(1)}, u32[]{:S(2)}, u32[]{:S(2)}) %collective-permute-start.12) | collective-permute-done | bytes 65568 | tf_op jit(solution)/shard_map/ppermute | solution.py:89
  161.9 5.1 %collective-permute-done.15 = f32[512,32]{1,0:T(8,128)S(1)} collective-permute-done((f32[512,32]{1,0:T(8,128)S(1)}, f32[512,32]{1,0:T(8,128)S(1)}, u32[]{:S(2)}, u32[]{:S(2)}) %collective-permute-start.15) | collective-permute-done | bytes 65568 | tf_op jit(solution)/shard_map/ppermute | solution.py:94
  177.0 5.9 %collective-permute-done.40 = f32[512,64]{1,0:T(8,128)S(1)} collective-permute-done((f32[512,64]{1,0:T(8,128)S(1)}, f32[512,64]{1,0:T(8,128)S(1)}, u32[]{:S(2)}, u32[]{:S(2)}) %collective-permute-start.40) | collective-permute-done | bytes 131104 | tf_op jit(solution)/shard_map/ppermute | solution.py:94
  184.0 4.2 %shard_map.62 = f32[1024,256]{1,0:T(8,128)} custom-call(f32[512,1024]{1,0:T(8,128)} %three_ref.31, f32[8,16]{1,0:T(8,128)} %convert_element_type.3.mask_ref, f32[512,256]{1,0:T(8,128)} %maximum_select_fusion.coef_ref), custom_call_target="tpu_custom_call" | custom-call | flops 805306368 | bytes 3670016 | tf_op jit(solution)/shard_map/pallas_call | solution.py:76
  191.3 5.3 %collective-permute-start.18 = (f32[256,256]{1,0:T(8,128)S(1)}, f32[256,256]{1,0:T(8,128)}, u32[]{:S(2)}, u32[]{:S(2)}) collective-permute-start(f32[256,256]{1,0:T(8,128)S(1)} %get-tuple-element.10), channel_id=1, source_target_pairs={{0,1},{1,2},{2,3},{4,5},{5,6},{6,7},{8,9},{9,10},{10,11},{12,13},{... | collective-permute-start | bytes 786440 | tf_op jit(solution)/shard_map/ppermute | solution.py:89
  197.4 4.3 %shard_map.70 = f32[1024,256]{1,0:T(8,128)} custom-call(f32[512,1024]{1,0:T(8,128)} %three_ref.31, f32[8,16]{1,0:T(8,128)} %convert_element_type.3.mask_ref, f32[512,256]{1,0:T(8,128)} %maximum_select_fusion.1.coef_ref), custom_call_target="tpu_custom_call" | custom-call | flops 805306368 | bytes 3670016 | tf_op jit(solution)/shard_map/pallas_call | solution.py:76
  204.9 5.2 %collective-permute-start.42 = (f32[256,256]{1,0:T(8,128)}, f32[256,256]{1,0:T(8,128)}, u32[]{:S(2)}, u32[]{:S(2)}) collective-permute-start(f32[256,256]{1,0:T(8,128)} %get-tuple-element.16), channel_id=1, source_target_pairs={{0,1},{1,2},{2,3},{4,5},{5,6},{6,7},{8,9},{9,10},{10,11},{12,13},{... | collective-permute-start | bytes 786440 | tf_op jit(solution)/shard_map/ppermute | solution.py:89
  213.3 5.3 %collective-permute-start.19 = (f32[256,256]{1,0:T(8,128)}, f32[256,256]{1,0:T(8,128)}, u32[]{:S(2)}, u32[]{:S(2)}) collective-permute-start(f32[256,256]{1,0:T(8,128)} %get-tuple-element.8), channel_id=1, source_target_pairs={{0,1},{1,2},{2,3},{4,5},{5,6},{6,7},{8,9},{9,10},{10,11},{12,13},{... | collective-permute-start | bytes 786440 | tf_op jit(solution)/shard_map/ppermute | solution.py:89
  221.8 5.3 %collective-permute-start.43 = (f32[256,256]{1,0:T(8,128)}, f32[256,256]{1,0:T(8,128)}, u32[]{:S(2)}, u32[]{:S(2)}) collective-permute-start(f32[256,256]{1,0:T(8,128)} %get-tuple-element.14), channel_id=1, source_target_pairs={{0,1},{1,2},{2,3},{4,5},{5,6},{6,7},{8,9},{9,10},{10,11},{12,13},{... | collective-permute-start | bytes 786440 | tf_op jit(solution)/shard_map/ppermute | solution.py:89
  230.1 5.3 %collective-permute-start.20 = (f32[256,256]{1,0:T(8,128)}, f32[256,256]{1,0:T(8,128)}, u32[]{:S(2)}, u32[]{:S(2)}) collective-permute-start(f32[256,256]{1,0:T(8,128)} %get-tuple-element.6), channel_id=1, source_target_pairs={{0,1},{1,2},{2,3},{4,5},{5,6},{6,7},{8,9},{9,10},{10,11},{12,13},{... | collective-permute-start | bytes 786440 | tf_op jit(solution)/shard_map/ppermute | solution.py:89
  238.6 5.2 %collective-permute-start.44 = (f32[256,256]{1,0:T(8,128)}, f32[256,256]{1,0:T(8,128)}, u32[]{:S(2)}, u32[]{:S(2)}) collective-permute-start(f32[256,256]{1,0:T(8,128)} %get-tuple-element.12), channel_id=1, source_target_pairs={{0,1},{1,2},{2,3},{4,5},{5,6},{6,7},{8,9},{9,10},{10,11},{12,13},{... | collective-permute-start | bytes 786440 | tf_op jit(solution)/shard_map/ppermute | solution.py:89
  (158 shorter events, 107.0 us)
Async XLA Ops:
  1.2 12.8 %collective-permute-start.3 = (f32[256,256]{1,0:T(8,128)S(1)}, f32[256,256]{1,0:T(8,128)S(1)}, u32[]{:S(2)}, u32[]{:S(2)}) collective-permute-start(f32[256,256]{1,0:T(8,128)S(1)} %get-tuple-element.17.dens_ref), channel_id=1, source_target_pairs={{0,1},{1,2},{2,3},{4,5},{5,6},{6,7},{8,9},{9,10},{10,11},{12,13},{... | collective-permute-start | bytes 786440 | tf_op jit(solution)/shard_map/ppermute | solution.py:89
  6.1 12.4 %collective-permute-start = (f32[256,256]{1,0:T(8,128)S(1)}, f32[256,256]{1,0:T(8,128)S(1)}, u32[]{:S(2)}, u32[]{:S(2)}) collective-permute-start(f32[256,256]{1,0:T(8,128)S(1)} %get-tuple-element.17.dens_ref), channel_id=1, source_target_pairs={{1,0},{2,1},{3,2},{5,4},{6,5},{7,6},{9,8},{10,9},{11,10},{13,12},{... | collective-permute-start | bytes 786440 | tf_op jit(solution)/shard_map/ppermute | solution.py:89
  7.4 12.5 %collective-permute-start.27 = (f32[256,256]{1,0:T(8,128)S(1)}, f32[256,256]{1,0:T(8,128)}, u32[]{:S(2)}, u32[]{:S(2)}) collective-permute-start(f32[256,256]{1,0:T(8,128)S(1)} %get-tuple-element.18.dens_ref), channel_id=1, source_target_pairs={{0,1},{1,2},{2,3},{4,5},{5,6},{6,7},{8,9},{9,10},{10,11},{12,13},{... | collective-permute-start | bytes 786440 | tf_op jit(solution)/shard_map/ppermute | solution.py:89
  12.7 11.8 %collective-permute-start.24 = (f32[256,256]{1,0:T(8,128)S(1)}, f32[256,256]{1,0:T(8,128)}, u32[]{:S(2)}, u32[]{:S(2)}) collective-permute-start(f32[256,256]{1,0:T(8,128)S(1)} %get-tuple-element.18.dens_ref), channel_id=1, source_target_pairs={{1,0},{2,1},{3,2},{5,4},{6,5},{7,6},{9,8},{10,9},{11,10},{13,12},{... | collective-permute-start | bytes 786440 | tf_op jit(solution)/shard_map/ppermute | solution.py:89
  14.0 11.8 %collective-permute-start.4 = (f32[256,256]{1,0:T(8,128)S(1)}, f32[256,256]{1,0:T(8,128)S(1)}, u32[]{:S(2)}, u32[]{:S(2)}) collective-permute-start(f32[256,256]{1,0:T(8,128)S(1)} %collective-permute-done.3.dens_ref), channel_id=1, source_target_pairs={{0,1},{1,2},{2,3},{4,5},{5,6},{6,7},{8,9},{9,10},{10,11},{12,13},{... | collective-permute-start | bytes 786440 | tf_op jit(solution)/shard_map/ppermute | solution.py:89
  18.6 12.5 %collective-permute-start.1 = (f32[256,256]{1,0:T(8,128)S(1)}, f32[256,256]{1,0:T(8,128)}, u32[]{:S(2)}, u32[]{:S(2)}) collective-permute-start(f32[256,256]{1,0:T(8,128)S(1)} %collective-permute-done.dens_ref), channel_id=1, source_target_pairs={{1,0},{2,1},{3,2},{5,4},{6,5},{7,6},{9,8},{10,9},{11,10},{13,12},{... | collective-permute-start | bytes 786440 | tf_op jit(solution)/shard_map/ppermute | solution.py:89
  19.9 36.2 %collective-permute-start.28 = (f32[256,256]{1,0:T(8,128)}, f32[256,256]{1,0:T(8,128)S(1)}, u32[]{:S(2)}, u32[]{:S(2)}) collective-permute-start(f32[256,256]{1,0:T(8,128)} %collective-permute-done.27.dens_ref), channel_id=1, source_target_pairs={{0,1},{1,2},{2,3},{4,5},{5,6},{6,7},{8,9},{9,10},{10,11},{12,13},{... | collective-permute-start | bytes 786440 | tf_op jit(solution)/shard_map/ppermute | solution.py:89
  24.5 36.2 %collective-permute-start.25 = (f32[256,256]{1,0:T(8,128)}, f32[256,256]{1,0:T(8,128)S(1)}, u32[]{:S(2)}, u32[]{:S(2)}) collective-permute-start(f32[256,256]{1,0:T(8,128)} %collective-permute-done.24.dens_ref), channel_id=1, source_target_pairs={{1,0},{2,1},{3,2},{5,4},{6,5},{7,6},{9,8},{10,9},{11,10},{13,12},{... | collective-permute-start | bytes 786440 | tf_op jit(solution)/shard_map/ppermute | solution.py:89
  25.8 49.0 %collective-permute-start.5 = (f32[256,256]{1,0:T(8,128)S(1)}, f32[256,256]{1,0:T(8,128)}, u32[]{:S(2)}, u32[]{:S(2)}) collective-permute-start(f32[256,256]{1,0:T(8,128)S(1)} %collective-permute-done.4.dens_ref), channel_id=1, source_target_pairs={{0,1},{1,2},{2,3},{4,5},{5,6},{6,7},{8,9},{9,10},{10,11},{12,13},{... | collective-permute-start | bytes 786440 | tf_op jit(solution)/shard_map/ppermute | solution.py:89
  31.1 46.9 %collective-permute-start.2 = (f32[256,256]{1,0:T(8,128)}, f32[256,256]{1,0:T(8,128)}, u32[]{:S(2)}, u32[]{:S(2)}) collective-permute-start(f32[256,256]{1,0:T(8,128)} %collective-permute-done.1.dens_ref), channel_id=1, source_target_pairs={{1,0},{2,1},{3,2},{5,4},{6,5},{7,6},{9,8},{10,9},{11,10},{13,12},{... | collective-permute-start | bytes 786440 | tf_op jit(solution)/shard_map/ppermute | solution.py:89
  56.1 26.8 %collective-permute-start.29 = (f32[256,256]{1,0:T(8,128)S(1)}, f32[256,256]{1,0:T(8,128)S(1)}, u32[]{:S(2)}, u32[]{:S(2)}) collective-permute-start(f32[256,256]{1,0:T(8,128)S(1)} %collective-permute-done.28.dens_ref), channel_id=1, source_target_pairs={{0,1},{1,2},{2,3},{4,5},{5,6},{6,7},{8,9},{9,10},{10,11},{12,13},{... | collective-permute-start | bytes 786440 | tf_op jit(solution)/shard_map/ppermute | solution.py:89
  60.7 26.1 %collective-permute-start.26 = (f32[256,256]{1,0:T(8,128)S(1)}, f32[256,256]{1,0:T(8,128)}, u32[]{:S(2)}, u32[]{:S(2)}) collective-permute-start(f32[256,256]{1,0:T(8,128)S(1)} %collective-permute-done.25.dens_ref), channel_id=1, source_target_pairs={{1,0},{2,1},{3,2},{5,4},{6,5},{7,6},{9,8},{10,9},{11,10},{13,12},{... | collective-permute-start | bytes 786440 | tf_op jit(solution)/shard_map/ppermute | solution.py:89
  82.9 8.8 %collective-permute-start.6 = (f32[512,128]{1,0:T(8,128)}, f32[512,128]{1,0:T(8,128)S(1)}, u32[]{:S(2)}, u32[]{:S(2)}) collective-permute-start(f32[512,128]{1,0:T(8,128)} %slice_select_fusion.5), channel_id=1, source_target_pairs={{0,4},{4,0},{8,12},{12,8},{16,20},{20,16},{24,28},{28,24},{1,5},{5... | collective-permute-start | bytes 786440 | tf_op jit(solution)/shard_map/ppermute | solution.py:94
  92.0 9.2 %collective-permute-start.7 = (f32[512,64]{1,0:T(8,128)S(1)}, f32[512,64]{1,0:T(8,128)S(1)}, u32[]{:S(2)}, u32[]{:S(2)}) collective-permute-start(f32[512,64]{1,0:T(8,128)S(1)} %slice_select_fusion.4), channel_id=1, source_target_pairs={{0,8},{4,12},{8,0},{12,4},{16,24},{20,28},{24,16},{28,20},{1,9},{5... | collective-permute-start | bytes 393224 | tf_op jit(solution)/shard_map/ppermute | solution.py:94
  93.7 12.2 %collective-permute-start.31 = (f32[512,64]{1,0:T(8,128)S(1)}, f32[512,64]{1,0:T(8,128)S(1)}, u32[]{:S(2)}, u32[]{:S(2)}) collective-permute-start(f32[512,64]{1,0:T(8,128)S(1)} %slice_select_fusion.1), channel_id=1, source_target_pairs={{0,8},{4,12},{8,0},{12,4},{16,24},{20,28},{24,16},{28,20},{1,9},{5... | collective-permute-start | bytes 393224 | tf_op jit(solution)/shard_map/ppermute | solution.py:94
  108.8 10.4 %collective-permute-start.9 = (f32[512,32]{0,1:T(8,128)S(1)}, f32[512,32]{0,1:T(8,128)S(1)}, u32[]{:S(2)}, u32[]{:S(2)}) collective-permute-start(f32[512,32]{0,1:T(8,128)S(1)} %convolution_bitcast_fusion.5), channel_id=1, source_target_pairs={{0,1},{1,2},{2,3},{4,5},{5,6},{6,7},{8,9},{9,10},{10,11},{12,13},{... | collective-permute-start | bytes 196616 | tf_op jit(solution)/shard_map/ppermute | solution.py:89
  114.4 9.0 %collective-permute-start.33 = (f32[512,32]{0,1:T(8,128)S(1)}, f32[512,32]{0,1:T(8,128)S(1)}, u32[]{:S(2)}, u32[]{:S(2)}) collective-permute-start(f32[512,32]{0,1:T(8,128)S(1)} %convolution_bitcast_fusion.3), channel_id=1, source_target_pairs={{0,1},{1,2},{2,3},{4,5},{5,6},{6,7},{8,9},{9,10},{10,11},{12,13},{... | collective-permute-start | bytes 196616 | tf_op jit(solution)/shard_map/ppermute | solution.py:89
  119.7 8.9 %collective-permute-start.10 = (f32[512,32]{0,1:T(8,128)S(1)}, f32[512,32]{0,1:T(8,128)S(1)}, u32[]{:S(2)}, u32[]{:S(2)}) collective-permute-start(f32[512,32]{0,1:T(8,128)S(1)} %convolution_add_fusion.9), channel_id=1, source_target_pairs={{0,1},{1,2},{2,3},{4,5},{5,6},{6,7},{8,9},{9,10},{10,11},{12,13},{... | collective-permute-start | bytes 196616 | tf_op jit(solution)/shard_map/ppermute | solution.py:89
  173.8 9.4 %collective-permute-start.17 = (f32[512,128]{1,0:T(8,128)S(1)}, f32[512,128]{1,0:T(8,128)S(1)}, u32[]{:S(2)}, u32[]{:S(2)}) collective-permute-start(f32[512,128]{1,0:T(8,128)S(1)} %maximum_select_fusion.3), channel_id=1, source_target_pairs={{0,4},{4,0},{8,12},{12,8},{16,20},{20,16},{24,28},{28,24},{1,5},{5... | collective-permute-start | bytes 786440 | tf_op jit(solution)/shard_map/ppermute | solution.py:94
  183.1 13.4 %collective-permute-start.41 = (f32[512,128]{1,0:T(8,128)S(1)}, f32[512,128]{1,0:T(8,128)S(1)}, u32[]{:S(2)}, u32[]{:S(2)}) collective-permute-start(f32[512,128]{1,0:T(8,128)S(1)} %maximum_select_fusion.5), channel_id=1, source_target_pairs={{0,4},{4,0},{8,12},{12,8},{16,20},{20,16},{24,28},{28,24},{1,5},{5... | collective-permute-start | bytes 786440 | tf_op jit(solution)/shard_map/ppermute | solution.py:94
  190.0 20.1 %collective-permute-start.21 = (f32[256,256]{1,0:T(8,128)}, f32[256,256]{1,0:T(8,128)}, u32[]{:S(2)}, u32[]{:S(2)}) collective-permute-start(f32[256,256]{1,0:T(8,128)} %get-tuple-element.9), channel_id=1, source_target_pairs={{1,0},{2,1},{3,2},{5,4},{6,5},{7,6},{9,8},{10,9},{11,10},{13,12},{... | collective-permute-start | bytes 786440 | tf_op jit(solution)/shard_map/ppermute | solution.py:89
  191.3 18.9 %collective-permute-start.18 = (f32[256,256]{1,0:T(8,128)S(1)}, f32[256,256]{1,0:T(8,128)}, u32[]{:S(2)}, u32[]{:S(2)}) collective-permute-start(f32[256,256]{1,0:T(8,128)S(1)} %get-tuple-element.10), channel_id=1, source_target_pairs={{0,1},{1,2},{2,3},{4,5},{5,6},{6,7},{8,9},{9,10},{10,11},{12,13},{... | collective-permute-start | bytes 786440 | tf_op jit(solution)/shard_map/ppermute | solution.py:89
  203.6 15.0 %collective-permute-start.45 = (f32[256,256]{1,0:T(8,128)}, f32[256,256]{1,0:T(8,128)}, u32[]{:S(2)}, u32[]{:S(2)}) collective-permute-start(f32[256,256]{1,0:T(8,128)} %get-tuple-element.15), channel_id=1, source_target_pairs={{1,0},{2,1},{3,2},{5,4},{6,5},{7,6},{9,8},{10,9},{11,10},{13,12},{... | collective-permute-start | bytes 786440 | tf_op jit(solution)/shard_map/ppermute | solution.py:89
  204.9 13.7 %collective-permute-start.42 = (f32[256,256]{1,0:T(8,128)}, f32[256,256]{1,0:T(8,128)}, u32[]{:S(2)}, u32[]{:S(2)}) collective-permute-start(f32[256,256]{1,0:T(8,128)} %get-tuple-element.16), channel_id=1, source_target_pairs={{0,1},{1,2},{2,3},{4,5},{5,6},{6,7},{8,9},{9,10},{10,11},{12,13},{... | collective-permute-start | bytes 786440 | tf_op jit(solution)/shard_map/ppermute | solution.py:89
  212.0 15.0 %collective-permute-start.22 = (f32[256,256]{1,0:T(8,128)}, f32[256,256]{1,0:T(8,128)S(1)}, u32[]{:S(2)}, u32[]{:S(2)}) collective-permute-start(f32[256,256]{1,0:T(8,128)} %get-tuple-element.7), channel_id=1, source_target_pairs={{1,0},{2,1},{3,2},{5,4},{6,5},{7,6},{9,8},{10,9},{11,10},{13,12},{... | collective-permute-start | bytes 786440 | tf_op jit(solution)/shard_map/ppermute | solution.py:89
  213.3 13.7 %collective-permute-start.19 = (f32[256,256]{1,0:T(8,128)}, f32[256,256]{1,0:T(8,128)}, u32[]{:S(2)}, u32[]{:S(2)}) collective-permute-start(f32[256,256]{1,0:T(8,128)} %get-tuple-element.8), channel_id=1, source_target_pairs={{0,1},{1,2},{2,3},{4,5},{5,6},{6,7},{8,9},{9,10},{10,11},{12,13},{... | collective-permute-start | bytes 786440 | tf_op jit(solution)/shard_map/ppermute | solution.py:89
  220.5 14.9 %collective-permute-start.46 = (f32[256,256]{1,0:T(8,128)}, f32[256,256]{1,0:T(8,128)}, u32[]{:S(2)}, u32[]{:S(2)}) collective-permute-start(f32[256,256]{1,0:T(8,128)} %get-tuple-element.13), channel_id=1, source_target_pairs={{1,0},{2,1},{3,2},{5,4},{6,5},{7,6},{9,8},{10,9},{11,10},{13,12},{... | collective-permute-start | bytes 786440 | tf_op jit(solution)/shard_map/ppermute | solution.py:89
  221.8 13.6 %collective-permute-start.43 = (f32[256,256]{1,0:T(8,128)}, f32[256,256]{1,0:T(8,128)}, u32[]{:S(2)}, u32[]{:S(2)}) collective-permute-start(f32[256,256]{1,0:T(8,128)} %get-tuple-element.14), channel_id=1, source_target_pairs={{0,1},{1,2},{2,3},{4,5},{5,6},{6,7},{8,9},{9,10},{10,11},{12,13},{... | collective-permute-start | bytes 786440 | tf_op jit(solution)/shard_map/ppermute | solution.py:89
  228.8 15.0 %collective-permute-start.23 = (f32[256,256]{1,0:T(8,128)}, f32[256,256]{1,0:T(8,128)S(1)}, u32[]{:S(2)}, u32[]{:S(2)}) collective-permute-start(f32[256,256]{1,0:T(8,128)} %get-tuple-element.5), channel_id=1, source_target_pairs={{1,0},{2,1},{3,2},{5,4},{6,5},{7,6},{9,8},{10,9},{11,10},{13,12},{... | collective-permute-start | bytes 786440 | tf_op jit(solution)/shard_map/ppermute | solution.py:89
  230.1 13.7 %collective-permute-start.20 = (f32[256,256]{1,0:T(8,128)}, f32[256,256]{1,0:T(8,128)}, u32[]{:S(2)}, u32[]{:S(2)}) collective-permute-start(f32[256,256]{1,0:T(8,128)} %get-tuple-element.6), channel_id=1, source_target_pairs={{0,1},{1,2},{2,3},{4,5},{5,6},{6,7},{8,9},{9,10},{10,11},{12,13},{... | collective-permute-start | bytes 786440 | tf_op jit(solution)/shard_map/ppermute | solution.py:89
  237.3 8.6 %collective-permute-start.47 = (f32[256,256]{1,0:T(8,128)}, f32[256,256]{1,0:T(8,128)}, u32[]{:S(2)}, u32[]{:S(2)}) collective-permute-start(f32[256,256]{1,0:T(8,128)} %get-tuple-element.11), channel_id=1, source_target_pairs={{1,0},{2,1},{3,2},{5,4},{6,5},{7,6},{9,8},{10,9},{11,10},{13,12},{... | collective-permute-start | bytes 786440 | tf_op jit(solution)/shard_map/ppermute | solution.py:89
  238.6 8.7 %collective-permute-start.44 = (f32[256,256]{1,0:T(8,128)}, f32[256,256]{1,0:T(8,128)}, u32[]{:S(2)}, u32[]{:S(2)}) collective-permute-start(f32[256,256]{1,0:T(8,128)} %get-tuple-element.12), channel_id=1, source_target_pairs={{0,1},{1,2},{2,3},{4,5},{5,6},{6,7},{8,9},{9,10},{10,11},{12,13},{... | collective-permute-start | bytes 786440 | tf_op jit(solution)/shard_map/ppermute | solution.py:89
  (31 other events, 352.9 us)

commit v7 on v6

--- a/solution.py
+++ b/solution.py
@@ -31,13 +31,10 @@
     return jnp.dot(by_rows.astype(jnp.bfloat16), pick_cols.astype(jnp.bfloat16), preferred_element_type=jnp.float32)
 
 
-def gamma_kernel(block_ref, three_ref, mask_ref, dens_ref, acc_ref, out_ref, *, row_size, col_size, cut):
+def gamma_kernel(block_ref, three_ref, mask_ref, dens_ref, acc_ref, out_ref, *, row_size, col_size):
     rows, width = dens_ref.shape
     start = block_ref[0] * rows
-    if cut:
-        tile = three_ref[:, pl.ds(pl.multiple_of(start, 128), rows)]
-    else:
-        tile = three_ref[...]
+    tile = three_ref[...]
     screened = tile * expanded_mask(mask_ref[...], tile.shape[0], start, rows, row_size, col_size)
     out_ref[...] = acc_ref[...] + dot3(screened, dens_ref[...], ((1,), (0,)))
 
@@ -47,37 +44,55 @@
     row_size = rows_total // mask_f.shape[0]
     col_size = cols_total // mask_f.shape[1]
     rows = dens.shape[0]
-    cut = rows % 128 == 0
-    if not cut:
-        three_center = lax.dynamic_slice_in_dim(three_center, block * rows, rows, axis=1)
-    kernel = functools.partial(gamma_kernel, row_size=row_size, col_size=col_size, cut=cut)
-    vmem = pl.BlockSpec(memory_space=pltpu.VMEM)
+    block = jnp.reshape(block, (1,)).astype(jnp.int32)
+    if rows % 128 == 0:
+        tile_spec = pl.BlockSpec((rows_total, rows), lambda i, b: (0, b[0]))
+    else:
+        three_center = lax.dynamic_slice_in_dim(three_center, block[0] * rows, rows, axis=1)
+        tile_spec = pl.BlockSpec((rows_total, rows), lambda i, b: (0, 0))
+    kernel = functools.partial(gamma_kernel, row_size=row_size, col_size=col_size)
+    whole = lambda i, b: (0, 0)
     return pl.pallas_call(
         kernel,
         out_shape=jax.ShapeDtypeStruct(acc.shape, jnp.float32),
-        in_specs=[pl.BlockSpec(memory_space=pltpu.SMEM), vmem, vmem, vmem, vmem],
-        out_specs=vmem,
+        grid_spec=pltpu.PrefetchScalarGridSpec(
+            num_scalar_prefetch=1,
+            grid=(1,),
+            in_specs=[
+                tile_spec,
+                pl.BlockSpec(mask_f.shape, whole),
+                pl.BlockSpec(dens.shape, whole),
+                pl.BlockSpec(acc.shape, whole),
+            ],
+            out_specs=pl.BlockSpec(acc.shape, whole),
+        ),
         input_output_aliases={4: 0},
         cost_estimate=pl.CostEstimate(flops=6 * rows_total * rows * dens.shape[1], transcendentals=0,
                                       bytes_accessed=4 * (rows_total * rows + dens.size + 2 * acc.size)),
-    )(jnp.reshape(block, (1,)).astype(jnp.int32), three_center, mask_f, dens, acc)
+    )(block, three_center, mask_f, dens, acc)
 
 
 def response_kernel(three_ref, mask_ref, coef_ref, out_ref, *, row_size, col_size):
     rows, cols = three_ref.shape
-    screened = three_ref[...] * expanded_mask(mask_ref[...], rows, 0, cols, row_size, col_size)
+    start = pl.program_id(0) * cols
+    screened = three_ref[...] * expanded_mask(mask_ref[...], rows, start, cols, row_size, col_size)
     out_ref[...] = dot3(screened, coef_ref[...], ((0,), (0,)))
 
 
 def response(three_center, mask_f, coef):
     rows_total, cols_total = three_center.shape
+    tile = 256 if cols_total % 256 == 0 else cols_total
     kernel = functools.partial(response_kernel, row_size=rows_total // mask_f.shape[0], col_size=cols_total // mask_f.shape[1])
-    vmem = pl.BlockSpec(memory_space=pltpu.VMEM)
     return pl.pallas_call(
         kernel,
         out_shape=jax.ShapeDtypeStruct((cols_total, coef.shape[1]), jnp.float32),
-        in_specs=[vmem, vmem, vmem],
-        out_specs=vmem,
+        grid=(cols_total // tile,),
+        in_specs=[
+            pl.BlockSpec((rows_total, tile), lambda j: (0, j)),
+            pl.BlockSpec(mask_f.shape, lambda j: (0, 0)),
+            pl.BlockSpec(coef.shape, lambda j: (0, 0)),
+        ],
+        out_specs=pl.BlockSpec((tile, coef.shape[1]), lambda j: (j, 0)),
         cost_estimate=pl.CostEstimate(flops=6 * rows_total * cols_total * coef.shape[1], transcendentals=0,
                                       bytes_accessed=4 * (three_center.size + coef.size + cols_total * coef.shape[1])),
     )(three_center, mask_f, coef)

time: 251 us -> 247 us (0.984)
  Pallas kernels: 53.2 us -> 49 us
    pallas_call x14, Pallas kernels: 44.7 us -> 38.2 us  [gamma_block(): pl.pallas_call(kernel, out_shape=jax.ShapeDtypeStruct(acc.shape, jnp.floa...]
  transfers between devices with their start and end apart: 48 -> 48, of which waited for: 14 -> 14; matrix products, arithmetic and copies ran while one was open for 13% -> 13% of each run, Pallas kernels for 21% -> 20%
where the time goes in v7:
time: 247 us; the launch traced here: 245 us
  starting transfers between devices  119 us (48%)
  Pallas kernels  49 us (20%)
  waiting for transfers between devices  39.1 us (16%)
  other arithmetic  17.2 us (7%)
  matrix products  12.3 us (5%)
  local copies, waits for them, and re-layouts  7.28 us (3%)
    ppermute x36, starting transfers between devices, from_behind(): return lax.ppermute(array, axis, pairs)  108 us
    pallas_call x14, Pallas kernels, gamma_block(): pl.pallas_call(kernel, out_shape=jax.ShapeDtypeStruct(acc.shape, jnp.floa...  38.2 us
    ppermute x12, waiting for transfers between devices, swap(): return lax.ppermute(array, axis, [(i, i ^ bit) for i in range(count)])  25.4 us
    ppermute x36, waiting for transfers between devices, from_behind(): return lax.ppermute(array, axis, pairs)  13.7 us
    dot_general x19, matrix products, product(): jnp.dot(left, right, precision=lax.Precision.HIGH, preferred_element_type...  12.3 us
    ppermute x12, starting transfers between devices, swap(): return lax.ppermute(array, axis, [(i, i ^ bit) for i in range(count)])  11.8 us
    pallas_call x2, Pallas kernels, response(): pl.pallas_call(kernel, out_shape=jax.ShapeDtypeStruct((cols_total, coef.s...  10.8 us
    add x4, other arithmetic, reduce_over_aux(): to_left + block(index - (count - 1) + step)  7.48 us
  transfers between devices with their start and end apart: 48, of which 14 were waited for; matrix products, arithmetic and copies ran while one was open for 13% of the time, Pallas kernels for 20%

profile of v7, /device:TPU:0, one launch (start us, length us, event | category | flops | bytes accessed | tf_op | source)
XLA Modules:
  0.0 245.0 jit_solution(12406181657826664465)
XLA Ops:
  1.2 4.9 %collective-permute-start.3 = (f32[256,256]{1,0:T(8,128)S(1)}, f32[256,256]{1,0:T(8,128)S(1)}, u32[]{:S(2)}, u32[]{:S(2)}) collective-permute-start(f32[256,256]{1,0:T(8,128)S(1)} %get-tuple-element.17.dens_ref), channel_id=1, source_target_pairs={{0,1},{1,2},{2,3},{4,5},{5,6},{6,7},{8,9},{9,10},{10,11},{12,13},{... | collective-permute-start | bytes 786440 | tf_op jit(solution)/shard_map/ppermute | solution.py:104
  7.4 5.3 %collective-permute-start.27 = (f32[256,256]{1,0:T(8,128)S(1)}, f32[256,256]{1,0:T(8,128)}, u32[]{:S(2)}, u32[]{:S(2)}) collective-permute-start(f32[256,256]{1,0:T(8,128)S(1)} %get-tuple-element.18.dens_ref), channel_id=1, source_target_pairs={{0,1},{1,2},{2,3},{4,5},{5,6},{6,7},{8,9},{9,10},{10,11},{12,13},{... | collective-permute-start | bytes 786440 | tf_op jit(solution)/shard_map/ppermute | solution.py:104
  14.0 4.6 %collective-permute-start.4 = (f32[256,256]{1,0:T(8,128)S(1)}, f32[256,256]{1,0:T(8,128)S(1)}, u32[]{:S(2)}, u32[]{:S(2)}) collective-permute-start(f32[256,256]{1,0:T(8,128)S(1)} %collective-permute-done.3.dens_ref), channel_id=1, source_target_pairs={{0,1},{1,2},{2,3},{4,5},{5,6},{6,7},{8,9},{9,10},{10,11},{12,13},{... | collective-permute-start | bytes 786440 | tf_op jit(solution)/shard_map/ppermute | solution.py:104
  19.9 4.6 %collective-permute-start.28 = (f32[256,256]{1,0:T(8,128)}, f32[256,256]{1,0:T(8,128)S(1)}, u32[]{:S(2)}, u32[]{:S(2)}) collective-permute-start(f32[256,256]{1,0:T(8,128)} %collective-permute-done.27.dens_ref), channel_id=1, source_target_pairs={{0,1},{1,2},{2,3},{4,5},{5,6},{6,7},{8,9},{9,10},{10,11},{12,13},{... | collective-permute-start | bytes 786440 | tf_op jit(solution)/shard_map/ppermute | solution.py:104
  25.8 5.3 %collective-permute-start.5 = (f32[256,256]{1,0:T(8,128)S(1)}, f32[256,256]{1,0:T(8,128)}, u32[]{:S(2)}, u32[]{:S(2)}) collective-permute-start(f32[256,256]{1,0:T(8,128)S(1)} %collective-permute-done.4.dens_ref), channel_id=1, source_target_pairs={{0,1},{1,2},{2,3},{4,5},{5,6},{6,7},{8,9},{9,10},{10,11},{12,13},{... | collective-permute-start | bytes 786440 | tf_op jit(solution)/shard_map/ppermute | solution.py:104
  36.1 2.7 %shard_map.55.acc_ref = f32[512,256]{1,0:T(8,128)} custom-call(s32[1]{0:T(128)} %bitcast.6.block_ref, f32[512,1024]{1,0:T(8,128)} %three_ref.31, f32[8,16]{1,0:T(8,128)} %convert_element_type.3.mask_ref, f32[256,256]{1,0:T(8,128)} %copy-done.7, f32[512,256]{1,0:T(8,128)} %broadcast_1_acc_ref.2.clone.1.acc_ref), custom_call_target="tpu_custom_call", output_to_operand_aliasing={{}: (4, {})} | custom-call | flops 201326592 | bytes 1835008 | tf_op jit(solution)/shard_map/pallas_call | solution.py:55
  53.3 4.6 %collective-permute-start.29 = (f32[256,256]{1,0:T(8,128)S(1)}, f32[256,256]{1,0:T(8,128)S(1)}, u32[]{:S(2)}, u32[]{:S(2)}) collective-permute-start(f32[256,256]{1,0:T(8,128)S(1)} %collective-permute-done.28.dens_ref), channel_id=1, source_target_pairs={{0,1},{1,2},{2,3},{4,5},{5,6},{6,7},{8,9},{9,10},{10,11},{12,13},{... | collective-permute-start | bytes 786440 | tf_op jit(solution)/shard_map/ppermute | solution.py:104
  59.2 2.7 %shard_map.58.acc_ref = f32[512,256]{1,0:T(8,128)} custom-call(s32[1]{0:T(128)} %bitcast.3.block_ref, f32[512,1024]{1,0:T(8,128)} %three_ref.31, f32[8,16]{1,0:T(8,128)} %convert_element_type.3.mask_ref, f32[256,256]{1,0:T(8,128)} %copy-done.10, f32[512,256]{1,0:T(8,128)} %shard_map.57.acc_ref), custom_call_target="tpu_custom_call", output_to_operand_aliasing={{}: (4, {})} | custom-call | flops 201326592 | bytes 1835008 | tf_op jit(solution)/shard_map/pallas_call | solution.py:55
  64.7 2.7 %shard_map.59.acc_ref = f32[512,256]{1,0:T(8,128)} custom-call(s32[1]{0:T(128)} %bitcast.2.block_ref, f32[512,1024]{1,0:T(8,128)} %three_ref.31, f32[8,16]{1,0:T(8,128)} %convert_element_type.3.mask_ref, f32[256,256]{1,0:T(8,128)} %collective-permute-done.1.dens_ref, f32[512,256]{1,0:T(8,128)} %shard_map.58.acc_ref), custom_call_target="tpu_custom_call", output_to_operand_aliasing={{}: (4, {})} | custom-call | flops 201326592 | bytes 1835008 | tf_op jit(solution)/shard_map/pallas_call | solution.py:55
  70.1 2.7 %shard_map.60.acc_ref = f32[512,256]{1,0:T(8,128)} custom-call(s32[1]{0:T(128)} %bitcast.1.block_ref, f32[512,1024]{1,0:T(8,128)} %three_ref.31, f32[8,16]{1,0:T(8,128)} %convert_element_type.3.mask_ref, f32[256,256]{1,0:T(8,128)} %collective-permute-done.5.dens_ref, f32[512,256]{1,0:T(8,128)} %shard_map.59.acc_ref), custom_call_target="tpu_custom_call", output_to_operand_aliasing={{}: (4, {})} | custom-call | flops 201326592 | bytes 1835008 | tf_op jit(solution)/shard_map/pallas_call | solution.py:55
  72.8 2.7 %shard_map.61 = f32[512,256]{1,0:T(8,128)} custom-call(s32[1]{0:T(128)} %bitcast.block_ref, f32[512,1024]{1,0:T(8,128)} %three_ref.31, f32[8,16]{1,0:T(8,128)} %convert_element_type.3.mask_ref, f32[256,256]{1,0:T(8,128)} %collective-permute-done.2.dens_ref, f32[512,256]{1,0:T(8,128)} %shard_map.60.acc_ref), custom_call_target="tpu_custom_call", output_to_operand_aliasing={{}: (4, {})} | custom-call | flops 201326592 | bytes 1835008 | tf_op jit(solution)/shard_map/pallas_call | solution.py:55
  80.7 2.8 %shard_map.69 = f32[512,256]{1,0:T(8,128)} custom-call(s32[1]{0:T(128)} %bitcast.block_ref, f32[512,1024]{1,0:T(8,128)} %three_ref.31, f32[8,16]{1,0:T(8,128)} %convert_element_type.3.mask_ref, f32[256,256]{1,0:T(8,128)} %collective-permute-done.26.dens_ref, f32[512,256]{1,0:T(8,128)} %shard_map.68.acc_ref), custom_call_target="tpu_custom_call", output_to_operand_aliasing={{}: (4, {})} | custom-call | flops 201326592 | bytes 1835008 | tf_op jit(solution)/shard_map/pallas_call | solution.py:55
  88.2 6.5 %collective-permute-done.7 = f32[512,64]{1,0:T(8,128)S(1)} collective-permute-done((f32[512,64]{1,0:T(8,128)S(1)}, f32[512,64]{1,0:T(8,128)S(1)}, u32[]{:S(2)}, u32[]{:S(2)}) %collective-permute-start.7) | collective-permute-done | bytes 131104 | tf_op jit(solution)/shard_map/ppermute | solution.py:109
  96.5 2.8 %collective-permute-done.31 = f32[512,64]{1,0:T(8,128)S(1)} collective-permute-done((f32[512,64]{1,0:T(8,128)S(1)}, f32[512,64]{1,0:T(8,128)S(1)}, u32[]{:S(2)}, u32[]{:S(2)}) %collective-permute-start.31) | collective-permute-done | bytes 131104 | tf_op jit(solution)/shard_map/ppermute | solution.py:109
  102.2 4.6 %collective-permute-start.9 = (f32[512,32]{0,1:T(8,128)S(1)}, f32[512,32]{0,1:T(8,128)S(1)}, u32[]{:S(2)}, u32[]{:S(2)}) collective-permute-start(f32[512,32]{0,1:T(8,128)S(1)} %convolution_bitcast_fusion.5), channel_id=1, source_target_pairs={{0,1},{1,2},{2,3},{4,5},{5,6},{6,7},{8,9},{9,10},{10,11},{12,13},{... | collective-permute-start | bytes 196616 | tf_op jit(solution)/shard_map/ppermute | solution.py:104
  107.8 4.7 %collective-permute-start.33 = (f32[512,32]{0,1:T(8,128)S(1)}, f32[512,32]{0,1:T(8,128)S(1)}, u32[]{:S(2)}, u32[]{:S(2)}) collective-permute-start(f32[512,32]{0,1:T(8,128)S(1)} %convolution_bitcast_fusion.3), channel_id=1, source_target_pairs={{0,1},{1,2},{2,3},{4,5},{5,6},{6,7},{8,9},{9,10},{10,11},{12,13},{... | collective-permute-start | bytes 196616 | tf_op jit(solution)/shard_map/ppermute | solution.py:104
  113.1 3.7 %collective-permute-start.10 = (f32[512,32]{0,1:T(8,128)S(1)}, f32[512,32]{0,1:T(8,128)S(1)}, u32[]{:S(2)}, u32[]{:S(2)}) collective-permute-start(f32[512,32]{0,1:T(8,128)S(1)} %convolution_add_fusion.9), channel_id=1, source_target_pairs={{0,1},{1,2},{2,3},{4,5},{5,6},{6,7},{8,9},{9,10},{10,11},{12,13},{... | collective-permute-start | bytes 196616 | tf_op jit(solution)/shard_map/ppermute | solution.py:104
  117.4 4.6 %collective-permute-start.34 = (f32[512,32]{0,1:T(8,128)S(1)}, f32[512,32]{0,1:T(8,128)S(1)}, u32[]{:S(2)}, u32[]{:S(2)}) collective-permute-start(f32[512,32]{0,1:T(8,128)S(1)} %convolution_add_fusion.4), channel_id=1, source_target_pairs={{0,1},{1,2},{2,3},{4,5},{5,6},{6,7},{8,9},{9,10},{10,11},{12,13},{... | collective-permute-start | bytes 196616 | tf_op jit(solution)/shard_map/ppermute | solution.py:104
  125.3 4.1 %collective-permute-start.35 = (f32[512,32]{0,1:T(8,128)S(1)}, f32[512,32]{0,1:T(8,128)S(1)}, u32[]{:S(2)}, u32[]{:S(2)}) collective-permute-start(f32[512,32]{0,1:T(8,128)S(1)} %convolution_add_fusion.3), channel_id=1, source_target_pairs={{0,1},{1,2},{2,3},{4,5},{5,6},{6,7},{8,9},{9,10},{10,11},{12,13},{... | collective-permute-start | bytes 196616 | tf_op jit(solution)/shard_map/ppermute | solution.py:104
  133.1 4.4 %collective-permute-done.12 = f32[512,32]{0,1:T(8,128)S(1)} collective-permute-done((f32[512,32]{0,1:T(8,128)S(1)}, f32[512,32]{0,1:T(8,128)S(1)}, u32[]{:S(2)}, u32[]{:S(2)}) %collective-permute-start.12) | collective-permute-done | bytes 65568 | tf_op jit(solution)/shard_map/ppermute | solution.py:104
  140.9 3.1 %collective-permute-done.13 = f32[512,32]{0,1:T(8,128)S(1)} collective-permute-done((f32[512,32]{0,1:T(8,128)S(1)}, f32[512,32]{0,1:T(8,128)S(1)}, u32[]{:S(2)}, u32[]{:S(2)}) %collective-permute-start.13) | collective-permute-done | bytes 65568 | tf_op jit(solution)/shard_map/ppermute | solution.py:104
  148.1 2.9 %collective-permute-done.14 = f32[512,32]{0,1:T(8,128)S(1)} collective-permute-done((f32[512,32]{0,1:T(8,128)S(1)}, f32[512,32]{0,1:T(8,128)S(1)}, u32[]{:S(2)}, u32[]{:S(2)}) %collective-permute-start.14) | collective-permute-done | bytes 65568 | tf_op jit(solution)/shard_map/ppermute | solution.py:104
  155.3 5.1 %collective-permute-done.15 = f32[512,32]{1,0:T(8,128)S(1)} collective-permute-done((f32[512,32]{1,0:T(8,128)S(1)}, f32[512,32]{1,0:T(8,128)S(1)}, u32[]{:S(2)}, u32[]{:S(2)}) %collective-permute-start.15) | collective-permute-done | bytes 65568 | tf_op jit(solution)/shard_map/ppermute | solution.py:109
  170.4 5.9 %collective-permute-done.40 = f32[512,64]{1,0:T(8,128)S(1)} collective-permute-done((f32[512,64]{1,0:T(8,128)S(1)}, f32[512,64]{1,0:T(8,128)S(1)}, u32[]{:S(2)}, u32[]{:S(2)}) %collective-permute-start.40) | collective-permute-done | bytes 131104 | tf_op jit(solution)/shard_map/ppermute | solution.py:109
  177.5 5.4 %shard_map.62 = f32[1024,256]{1,0:T(8,128)} custom-call(f32[512,1024]{1,0:T(8,128)} %three_ref.31, f32[8,16]{1,0:T(8,128)} %convert_element_type.3.mask_ref, f32[512,256]{1,0:T(8,128)} %maximum_select_fusion.coef_ref), custom_call_target="tpu_custom_call" | custom-call | flops 805306368 | bytes 3670016 | tf_op jit(solution)/shard_map/pallas_call | solution.py:86
  185.9 5.3 %collective-permute-start.18 = (f32[256,256]{1,0:T(8,128)S(1)}, f32[256,256]{1,0:T(8,128)}, u32[]{:S(2)}, u32[]{:S(2)}) collective-permute-start(f32[256,256]{1,0:T(8,128)S(1)} %get-tuple-element.10), channel_id=1, source_target_pairs={{0,1},{1,2},{2,3},{4,5},{5,6},{6,7},{8,9},{9,10},{10,11},{12,13},{... | collective-permute-start | bytes 786440 | tf_op jit(solution)/shard_map/ppermute | solution.py:104
  192.0 5.4 %shard_map.70 = f32[1024,256]{1,0:T(8,128)} custom-call(f32[512,1024]{1,0:T(8,128)} %three_ref.31, f32[8,16]{1,0:T(8,128)} %convert_element_type.3.mask_ref, f32[512,256]{1,0:T(8,128)} %maximum_select_fusion.1.coef_ref), custom_call_target="tpu_custom_call" | custom-call | flops 805306368 | bytes 3670016 | tf_op jit(solution)/shard_map/pallas_call | solution.py:86
  200.6 5.2 %collective-permute-start.42 = (f32[256,256]{1,0:T(8,128)}, f32[256,256]{1,0:T(8,128)}, u32[]{:S(2)}, u32[]{:S(2)}) collective-permute-start(f32[256,256]{1,0:T(8,128)} %get-tuple-element.16), channel_id=1, source_target_pairs={{0,1},{1,2},{2,3},{4,5},{5,6},{6,7},{8,9},{9,10},{10,11},{12,13},{... | collective-permute-start | bytes 786440 | tf_op jit(solution)/shard_map/ppermute | solution.py:104
  209.1 5.3 %collective-permute-start.19 = (f32[256,256]{1,0:T(8,128)}, f32[256,256]{1,0:T(8,128)}, u32[]{:S(2)}, u32[]{:S(2)}) collective-permute-start(f32[256,256]{1,0:T(8,128)} %get-tuple-element.8), channel_id=1, source_target_pairs={{0,1},{1,2},{2,3},{4,5},{5,6},{6,7},{8,9},{9,10},{10,11},{12,13},{... | collective-permute-start | bytes 786440 | tf_op jit(solution)/shard_map/ppermute | solution.py:104
  217.5 5.3 %collective-permute-start.43 = (f32[256,256]{1,0:T(8,128)}, f32[256,256]{1,0:T(8,128)}, u32[]{:S(2)}, u32[]{:S(2)}) collective-permute-start(f32[256,256]{1,0:T(8,128)} %get-tuple-element.14), channel_id=1, source_target_pairs={{0,1},{1,2},{2,3},{4,5},{5,6},{6,7},{8,9},{9,10},{10,11},{12,13},{... | collective-permute-start | bytes 786440 | tf_op jit(solution)/shard_map/ppermute | solution.py:104
  225.9 5.3 %collective-permute-start.20 = (f32[256,256]{1,0:T(8,128)}, f32[256,256]{1,0:T(8,128)}, u32[]{:S(2)}, u32[]{:S(2)}) collective-permute-start(f32[256,256]{1,0:T(8,128)} %get-tuple-element.6), channel_id=1, source_target_pairs={{0,1},{1,2},{2,3},{4,5},{5,6},{6,7},{8,9},{9,10},{10,11},{12,13},{... | collective-permute-start | bytes 786440 | tf_op jit(solution)/shard_map/ppermute | solution.py:104
  234.3 5.2 %collective-permute-start.44 = (f32[256,256]{1,0:T(8,128)}, f32[256,256]{1,0:T(8,128)}, u32[]{:S(2)}, u32[]{:S(2)}) collective-permute-start(f32[256,256]{1,0:T(8,128)} %get-tuple-element.12), channel_id=1, source_target_pairs={{0,1},{1,2},{2,3},{4,5},{5,6},{6,7},{8,9},{9,10},{10,11},{12,13},{... | collective-permute-start | bytes 786440 | tf_op jit(solution)/shard_map/ppermute | solution.py:104
  (158 shorter events, 103.9 us)
Async XLA Ops:
  1.2 12.8 %collective-permute-start.3 = (f32[256,256]{1,0:T(8,128)S(1)}, f32[256,256]{1,0:T(8,128)S(1)}, u32[]{:S(2)}, u32[]{:S(2)}) collective-permute-start(f32[256,256]{1,0:T(8,128)S(1)} %get-tuple-element.17.dens_ref), channel_id=1, source_target_pairs={{0,1},{1,2},{2,3},{4,5},{5,6},{6,7},{8,9},{9,10},{10,11},{12,13},{... | collective-permute-start | bytes 786440 | tf_op jit(solution)/shard_map/ppermute | solution.py:104
  6.1 12.4 %collective-permute-start = (f32[256,256]{1,0:T(8,128)S(1)}, f32[256,256]{1,0:T(8,128)S(1)}, u32[]{:S(2)}, u32[]{:S(2)}) collective-permute-start(f32[256,256]{1,0:T(8,128)S(1)} %get-tuple-element.17.dens_ref), channel_id=1, source_target_pairs={{1,0},{2,1},{3,2},{5,4},{6,5},{7,6},{9,8},{10,9},{11,10},{13,12},{... | collective-permute-start | bytes 786440 | tf_op jit(solution)/shard_map/ppermute | solution.py:104
  7.4 12.5 %collective-permute-start.27 = (f32[256,256]{1,0:T(8,128)S(1)}, f32[256,256]{1,0:T(8,128)}, u32[]{:S(2)}, u32[]{:S(2)}) collective-permute-start(f32[256,256]{1,0:T(8,128)S(1)} %get-tuple-element.18.dens_ref), channel_id=1, source_target_pairs={{0,1},{1,2},{2,3},{4,5},{5,6},{6,7},{8,9},{9,10},{10,11},{12,13},{... | collective-permute-start | bytes 786440 | tf_op jit(solution)/shard_map/ppermute | solution.py:104
  12.7 11.8 %collective-permute-start.24 = (f32[256,256]{1,0:T(8,128)S(1)}, f32[256,256]{1,0:T(8,128)}, u32[]{:S(2)}, u32[]{:S(2)}) collective-permute-start(f32[256,256]{1,0:T(8,128)S(1)} %get-tuple-element.18.dens_ref), channel_id=1, source_target_pairs={{1,0},{2,1},{3,2},{5,4},{6,5},{7,6},{9,8},{10,9},{11,10},{13,12},{... | collective-permute-start | bytes 786440 | tf_op jit(solution)/shard_map/ppermute | solution.py:104
  14.0 11.8 %collective-permute-start.4 = (f32[256,256]{1,0:T(8,128)S(1)}, f32[256,256]{1,0:T(8,128)S(1)}, u32[]{:S(2)}, u32[]{:S(2)}) collective-permute-start(f32[256,256]{1,0:T(8,128)S(1)} %collective-permute-done.3.dens_ref), channel_id=1, source_target_pairs={{0,1},{1,2},{2,3},{4,5},{5,6},{6,7},{8,9},{9,10},{10,11},{12,13},{... | collective-permute-start | bytes 786440 | tf_op jit(solution)/shard_map/ppermute | solution.py:104
  18.6 12.5 %collective-permute-start.1 = (f32[256,256]{1,0:T(8,128)S(1)}, f32[256,256]{1,0:T(8,128)}, u32[]{:S(2)}, u32[]{:S(2)}) collective-permute-start(f32[256,256]{1,0:T(8,128)S(1)} %collective-permute-done.dens_ref), channel_id=1, source_target_pairs={{1,0},{2,1},{3,2},{5,4},{6,5},{7,6},{9,8},{10,9},{11,10},{13,12},{... | collective-permute-start | bytes 786440 | tf_op jit(solution)/shard_map/ppermute | solution.py:104
  19.9 33.4 %collective-permute-start.28 = (f32[256,256]{1,0:T(8,128)}, f32[256,256]{1,0:T(8,128)S(1)}, u32[]{:S(2)}, u32[]{:S(2)}) collective-permute-start(f32[256,256]{1,0:T(8,128)} %collective-permute-done.27.dens_ref), channel_id=1, source_target_pairs={{0,1},{1,2},{2,3},{4,5},{5,6},{6,7},{8,9},{9,10},{10,11},{12,13},{... | collective-permute-start | bytes 786440 | tf_op jit(solution)/shard_map/ppermute | solution.py:104
  24.5 33.4 %collective-permute-start.25 = (f32[256,256]{1,0:T(8,128)}, f32[256,256]{1,0:T(8,128)S(1)}, u32[]{:S(2)}, u32[]{:S(2)}) collective-permute-start(f32[256,256]{1,0:T(8,128)} %collective-permute-done.24.dens_ref), channel_id=1, source_target_pairs={{1,0},{2,1},{3,2},{5,4},{6,5},{7,6},{9,8},{10,9},{11,10},{13,12},{... | collective-permute-start | bytes 786440 | tf_op jit(solution)/shard_map/ppermute | solution.py:104
  25.8 44.3 %collective-permute-start.5 = (f32[256,256]{1,0:T(8,128)S(1)}, f32[256,256]{1,0:T(8,128)}, u32[]{:S(2)}, u32[]{:S(2)}) collective-permute-start(f32[256,256]{1,0:T(8,128)S(1)} %collective-permute-done.4.dens_ref), channel_id=1, source_target_pairs={{0,1},{1,2},{2,3},{4,5},{5,6},{6,7},{8,9},{9,10},{10,11},{12,13},{... | collective-permute-start | bytes 786440 | tf_op jit(solution)/shard_map/ppermute | solution.py:104
  31.1 41.8 %collective-permute-start.2 = (f32[256,256]{1,0:T(8,128)}, f32[256,256]{1,0:T(8,128)}, u32[]{:S(2)}, u32[]{:S(2)}) collective-permute-start(f32[256,256]{1,0:T(8,128)} %collective-permute-done.1.dens_ref), channel_id=1, source_target_pairs={{1,0},{2,1},{3,2},{5,4},{6,5},{7,6},{9,8},{10,9},{11,10},{13,12},{... | collective-permute-start | bytes 786440 | tf_op jit(solution)/shard_map/ppermute | solution.py:104
  53.3 24.0 %collective-permute-start.29 = (f32[256,256]{1,0:T(8,128)S(1)}, f32[256,256]{1,0:T(8,128)S(1)}, u32[]{:S(2)}, u32[]{:S(2)}) collective-permute-start(f32[256,256]{1,0:T(8,128)S(1)} %collective-permute-done.28.dens_ref), channel_id=1, source_target_pairs={{0,1},{1,2},{2,3},{4,5},{5,6},{6,7},{8,9},{9,10},{10,11},{12,13},{... | collective-permute-start | bytes 786440 | tf_op jit(solution)/shard_map/ppermute | solution.py:104
  57.9 22.8 %collective-permute-start.26 = (f32[256,256]{1,0:T(8,128)S(1)}, f32[256,256]{1,0:T(8,128)}, u32[]{:S(2)}, u32[]{:S(2)}) collective-permute-start(f32[256,256]{1,0:T(8,128)S(1)} %collective-permute-done.25.dens_ref), channel_id=1, source_target_pairs={{1,0},{2,1},{3,2},{5,4},{6,5},{7,6},{9,8},{10,9},{11,10},{13,12},{... | collective-permute-start | bytes 786440 | tf_op jit(solution)/shard_map/ppermute | solution.py:104
  85.4 9.2 %collective-permute-start.7 = (f32[512,64]{1,0:T(8,128)S(1)}, f32[512,64]{1,0:T(8,128)S(1)}, u32[]{:S(2)}, u32[]{:S(2)}) collective-permute-start(f32[512,64]{1,0:T(8,128)S(1)} %slice_select_fusion.4), channel_id=1, source_target_pairs={{0,8},{4,12},{8,0},{12,4},{16,24},{20,28},{24,16},{28,20},{1,9},{5... | collective-permute-start | bytes 393224 | tf_op jit(solution)/shard_map/ppermute | solution.py:109
  87.2 12.2 %collective-permute-start.31 = (f32[512,64]{1,0:T(8,128)S(1)}, f32[512,64]{1,0:T(8,128)S(1)}, u32[]{:S(2)}, u32[]{:S(2)}) collective-permute-start(f32[512,64]{1,0:T(8,128)S(1)} %slice_select_fusion.1), channel_id=1, source_target_pairs={{0,8},{4,12},{8,0},{12,4},{16,24},{20,28},{24,16},{28,20},{1,9},{5... | collective-permute-start | bytes 393224 | tf_op jit(solution)/shard_map/ppermute | solution.py:109
  102.2 10.4 %collective-permute-start.9 = (f32[512,32]{0,1:T(8,128)S(1)}, f32[512,32]{0,1:T(8,128)S(1)}, u32[]{:S(2)}, u32[]{:S(2)}) collective-permute-start(f32[512,32]{0,1:T(8,128)S(1)} %convolution_bitcast_fusion.5), channel_id=1, source_target_pairs={{0,1},{1,2},{2,3},{4,5},{5,6},{6,7},{8,9},{9,10},{10,11},{12,13},{... | collective-permute-start | bytes 196616 | tf_op jit(solution)/shard_map/ppermute | solution.py:104
  107.8 9.0 %collective-permute-start.33 = (f32[512,32]{0,1:T(8,128)S(1)}, f32[512,32]{0,1:T(8,128)S(1)}, u32[]{:S(2)}, u32[]{:S(2)}) collective-permute-start(f32[512,32]{0,1:T(8,128)S(1)} %convolution_bitcast_fusion.3), channel_id=1, source_target_pairs={{0,1},{1,2},{2,3},{4,5},{5,6},{6,7},{8,9},{9,10},{10,11},{12,13},{... | collective-permute-start | bytes 196616 | tf_op jit(solution)/shard_map/ppermute | solution.py:104
  113.1 8.9 %collective-permute-start.10 = (f32[512,32]{0,1:T(8,128)S(1)}, f32[512,32]{0,1:T(8,128)S(1)}, u32[]{:S(2)}, u32[]{:S(2)}) collective-permute-start(f32[512,32]{0,1:T(8,128)S(1)} %convolution_add_fusion.9), channel_id=1, source_target_pairs={{0,1},{1,2},{2,3},{4,5},{5,6},{6,7},{8,9},{9,10},{10,11},{12,13},{... | collective-permute-start | bytes 196616 | tf_op jit(solution)/shard_map/ppermute | solution.py:104
  152.0 8.4 %collective-permute-start.15 = (f32[512,32]{1,0:T(8,128)S(1)}, f32[512,32]{1,0:T(8,128)S(1)}, u32[]{:S(2)}, u32[]{:S(2)}) collective-permute-start(f32[512,32]{1,0:T(8,128)S(1)} %convolution_bitcast_fusion.1), channel_id=1, source_target_pairs={{0,16},{4,20},{8,24},{12,28},{16,0},{20,4},{24,8},{28,12},{1,17},{... | collective-permute-start | bytes 196616 | tf_op jit(solution)/shard_map/ppermute | solution.py:109
  167.3 9.4 %collective-permute-start.17 = (f32[512,128]{1,0:T(8,128)S(1)}, f32[512,128]{1,0:T(8,128)S(1)}, u32[]{:S(2)}, u32[]{:S(2)}) collective-permute-start(f32[512,128]{1,0:T(8,128)S(1)} %maximum_select_fusion.3), channel_id=1, source_target_pairs={{0,4},{4,0},{8,12},{12,8},{16,20},{20,16},{24,28},{28,24},{1,5},{5... | collective-permute-start | bytes 786440 | tf_op jit(solution)/shard_map/ppermute | solution.py:109
  176.6 14.6 %collective-permute-start.41 = (f32[512,128]{1,0:T(8,128)S(1)}, f32[512,128]{1,0:T(8,128)S(1)}, u32[]{:S(2)}, u32[]{:S(2)}) collective-permute-start(f32[512,128]{1,0:T(8,128)S(1)} %maximum_select_fusion.5), channel_id=1, source_target_pairs={{0,4},{4,0},{8,12},{12,8},{16,20},{20,16},{24,28},{28,24},{1,5},{5... | collective-permute-start | bytes 786440 | tf_op jit(solution)/shard_map/ppermute | solution.py:109
  184.6 21.3 %collective-permute-start.21 = (f32[256,256]{1,0:T(8,128)}, f32[256,256]{1,0:T(8,128)}, u32[]{:S(2)}, u32[]{:S(2)}) collective-permute-start(f32[256,256]{1,0:T(8,128)} %get-tuple-element.9), channel_id=1, source_target_pairs={{1,0},{2,1},{3,2},{5,4},{6,5},{7,6},{9,8},{10,9},{11,10},{13,12},{... | collective-permute-start | bytes 786440 | tf_op jit(solution)/shard_map/ppermute | solution.py:104
  185.9 20.0 %collective-permute-start.18 = (f32[256,256]{1,0:T(8,128)S(1)}, f32[256,256]{1,0:T(8,128)}, u32[]{:S(2)}, u32[]{:S(2)}) collective-permute-start(f32[256,256]{1,0:T(8,128)S(1)} %get-tuple-element.10), channel_id=1, source_target_pairs={{0,1},{1,2},{2,3},{4,5},{5,6},{6,7},{8,9},{9,10},{10,11},{12,13},{... | collective-permute-start | bytes 786440 | tf_op jit(solution)/shard_map/ppermute | solution.py:104
  199.3 15.0 %collective-permute-start.45 = (f32[256,256]{1,0:T(8,128)}, f32[256,256]{1,0:T(8,128)}, u32[]{:S(2)}, u32[]{:S(2)}) collective-permute-start(f32[256,256]{1,0:T(8,128)} %get-tuple-element.15), channel_id=1, source_target_pairs={{1,0},{2,1},{3,2},{5,4},{6,5},{7,6},{9,8},{10,9},{11,10},{13,12},{... | collective-permute-start | bytes 786440 | tf_op jit(solution)/shard_map/ppermute | solution.py:104
  200.6 13.7 %collective-permute-start.42 = (f32[256,256]{1,0:T(8,128)}, f32[256,256]{1,0:T(8,128)}, u32[]{:S(2)}, u32[]{:S(2)}) collective-permute-start(f32[256,256]{1,0:T(8,128)} %get-tuple-element.16), channel_id=1, source_target_pairs={{0,1},{1,2},{2,3},{4,5},{5,6},{6,7},{8,9},{9,10},{10,11},{12,13},{... | collective-permute-start | bytes 786440 | tf_op jit(solution)/shard_map/ppermute | solution.py:104
  207.8 15.0 %collective-permute-start.22 = (f32[256,256]{1,0:T(8,128)}, f32[256,256]{1,0:T(8,128)S(1)}, u32[]{:S(2)}, u32[]{:S(2)}) collective-permute-start(f32[256,256]{1,0:T(8,128)} %get-tuple-element.7), channel_id=1, source_target_pairs={{1,0},{2,1},{3,2},{5,4},{6,5},{7,6},{9,8},{10,9},{11,10},{13,12},{... | collective-permute-start | bytes 786440 | tf_op jit(solution)/shard_map/ppermute | solution.py:104
  209.1 13.7 %collective-permute-start.19 = (f32[256,256]{1,0:T(8,128)}, f32[256,256]{1,0:T(8,128)}, u32[]{:S(2)}, u32[]{:S(2)}) collective-permute-start(f32[256,256]{1,0:T(8,128)} %get-tuple-element.8), channel_id=1, source_target_pairs={{0,1},{1,2},{2,3},{4,5},{5,6},{6,7},{8,9},{9,10},{10,11},{12,13},{... | collective-permute-start | bytes 786440 | tf_op jit(solution)/shard_map/ppermute | solution.py:104
  216.2 14.9 %collective-permute-start.46 = (f32[256,256]{1,0:T(8,128)}, f32[256,256]{1,0:T(8,128)}, u32[]{:S(2)}, u32[]{:S(2)}) collective-permute-start(f32[256,256]{1,0:T(8,128)} %get-tuple-element.13), channel_id=1, source_target_pairs={{1,0},{2,1},{3,2},{5,4},{6,5},{7,6},{9,8},{10,9},{11,10},{13,12},{... | collective-permute-start | bytes 786440 | tf_op jit(solution)/shard_map/ppermute | solution.py:104
  217.5 13.6 %collective-permute-start.43 = (f32[256,256]{1,0:T(8,128)}, f32[256,256]{1,0:T(8,128)}, u32[]{:S(2)}, u32[]{:S(2)}) collective-permute-start(f32[256,256]{1,0:T(8,128)} %get-tuple-element.14), channel_id=1, source_target_pairs={{0,1},{1,2},{2,3},{4,5},{5,6},{6,7},{8,9},{9,10},{10,11},{12,13},{... | collective-permute-start | bytes 786440 | tf_op jit(solution)/shard_map/ppermute | solution.py:104
  224.6 15.0 %collective-permute-start.23 = (f32[256,256]{1,0:T(8,128)}, f32[256,256]{1,0:T(8,128)S(1)}, u32[]{:S(2)}, u32[]{:S(2)}) collective-permute-start(f32[256,256]{1,0:T(8,128)} %get-tuple-element.5), channel_id=1, source_target_pairs={{1,0},{2,1},{3,2},{5,4},{6,5},{7,6},{9,8},{10,9},{11,10},{13,12},{... | collective-permute-start | bytes 786440 | tf_op jit(solution)/shard_map/ppermute | solution.py:104
  225.9 13.7 %collective-permute-start.20 = (f32[256,256]{1,0:T(8,128)}, f32[256,256]{1,0:T(8,128)}, u32[]{:S(2)}, u32[]{:S(2)}) collective-permute-start(f32[256,256]{1,0:T(8,128)} %get-tuple-element.6), channel_id=1, source_target_pairs={{0,1},{1,2},{2,3},{4,5},{5,6},{6,7},{8,9},{9,10},{10,11},{12,13},{... | collective-permute-start | bytes 786440 | tf_op jit(solution)/shard_map/ppermute | solution.py:104
  233.0 8.6 %collective-permute-start.47 = (f32[256,256]{1,0:T(8,128)}, f32[256,256]{1,0:T(8,128)}, u32[]{:S(2)}, u32[]{:S(2)}) collective-permute-start(f32[256,256]{1,0:T(8,128)} %get-tuple-element.11), channel_id=1, source_target_pairs={{1,0},{2,1},{3,2},{5,4},{6,5},{7,6},{9,8},{10,9},{11,10},{13,12},{... | collective-permute-start | bytes 786440 | tf_op jit(solution)/shard_map/ppermute | solution.py:104
  234.3 8.7 %collective-permute-start.44 = (f32[256,256]{1,0:T(8,128)}, f32[256,256]{1,0:T(8,128)}, u32[]{:S(2)}, u32[]{:S(2)}) collective-permute-start(f32[256,256]{1,0:T(8,128)} %get-tuple-element.12), channel_id=1, source_target_pairs={{0,1},{1,2},{2,3},{4,5},{5,6},{6,7},{8,9},{9,10},{10,11},{12,13},{... | collective-permute-start | bytes 786440 | tf_op jit(solution)/shard_map/ppermute | solution.py:104
  (31 other events, 350.7 us)

commit v8 on v2

--- a/solution.py
+++ b/solution.py
@@ -121,7 +121,7 @@
     return product(diag_inverse.T, solved - arriving)
 
 
-SLICES = 2
+SLICES = 1
 
 
 def per_device(three_center, densities, screen_mask, diag_inverse, sub_factor):

time: 181 us -> 189 us (1.044)
  waiting for transfers between devices: 40.6 us -> 106 us
  starting transfers between devices: 106 us -> 54.1 us
  matrix products: 22.7 us -> 15 us
  other arithmetic: 2.82 us -> 7.47 us
    ppermute x36 -> x18, waiting for transfers between devices: 28.8 us -> 81.3 us  [from_behind(): return lax.ppermute(array, axis, pairs)]
    ppermute x36 -> x18, starting transfers between devices: 93.6 us -> 49.7 us  [from_behind(): return lax.ppermute(array, axis, pairs)]
    ppermute x12 -> x6, waiting for transfers between devices: 11.8 us -> 24.9 us  [swap(): return lax.ppermute(array, axis, [(i, i ^ bit) for i in range(count)])]
    ppermute x12 -> x6, starting transfers between devices: 12.3 us -> 4.37 us  [swap(): return lax.ppermute(array, axis, [(i, i ^ bit) for i in range(count)])]
    dot_general x33 -> x17, matrix products: 20.7 us -> 13.1 us  [product(): jnp.dot(left, right, precision=lax.Precision.HIGH, preferred_element_type...]
    add x4 -> x2, other arithmetic: 0.16 us -> 2.59 us  [reduce_scatter_columns(): current = keep + swap(send, axis, bit)]
    slice x1 -> x0, local copies, waits for them, and re-layouts: 1.94 us -> none  [per_device(): dens_part = densities[:, part * width:(part + 1) * width]]
    unnamed x13 -> x11, local copies, waits for them, and re-layouts: 3.34 us -> 4.7 us
  transfers between devices with their start and end apart: 48 -> 24, of which waited for: 21 -> 22; matrix products, arithmetic and copies ran while one was open for 16% -> 7% of each run, Pallas kernels for 0% -> 0%
where the time goes in v8:
time: 189 us; the launch traced here: 188 us
  waiting for transfers between devices  106 us (56%)
  starting transfers between devices  54.1 us (29%)
  matrix products  15 us (8%)
  other arithmetic  7.47 us (4%)
  local copies, waits for them, and re-layouts  5.01 us (3%)
    ppermute x18, waiting for transfers between devices, from_behind(): return lax.ppermute(array, axis, pairs)  81.3 us
    ppermute x18, starting transfers between devices, from_behind(): return lax.ppermute(array, axis, pairs)  49.7 us
    ppermute x6, waiting for transfers between devices, swap(): return lax.ppermute(array, axis, [(i, i ^ bit) for i in range(count)])  24.9 us
    dot_general x17, matrix products, product(): jnp.dot(left, right, precision=lax.Precision.HIGH, preferred_element_type...  13.1 us
    unnamed x11, local copies, waits for them, and re-layouts  4.7 us
    ppermute x6, starting transfers between devices, swap(): return lax.ppermute(array, axis, [(i, i ^ bit) for i in range(count)])  4.37 us
  transfers between devices with their start and end apart: 24, of which 22 were waited for; matrix products, arithmetic and copies ran while one was open for 7% of the time, Pallas kernels for 0%

profile of v8, /device:TPU:0, one launch (start us, length us, event | category | flops | bytes accessed | tf_op | source)
XLA Modules:
  0.0 188.1 jit_solution(4996437362662376615)
XLA Ops:
  1.4 6.4 %collective-permute-start = (f32[256,512]{1,0:T(8,128)}, f32[256,512]{1,0:T(8,128)}, u32[]{:S(2)}, u32[]{:S(2)}) collective-permute-start(f32[256,512]{1,0:T(8,128)} %param.6), channel_id=1, source_target_pairs={{0,1},{1,2},{2,3},{4,5},{5,6},{6,7},{8,9},{9,10},{10,11},{12,13},{... | collective-permute-start | bytes 1572872 | tf_op jit(solution)/shard_map/ppermute | solution.py:10
  7.8 2.9 %copy.7 = f32[512,1024]{0,1:T(8,128)} copy(f32[512,1024]{1,0:T(8,128)} %param.5) | data formatting | bytes 4194304 | tf_op args[0]
  10.9 1.8 bitcast_multiply_fusion
  14.5 2.8 %collective-permute-done.1 = f32[256,512]{1,0:T(8,128)} collective-permute-done((f32[256,512]{1,0:T(8,128)}, f32[256,512]{1,0:T(8,128)}, u32[]{:S(2)}, u32[]{:S(2)}) %collective-permute-start.1) | collective-permute-done | bytes 524320 | tf_op jit(solution)/shard_map/ppermute | solution.py:10
  18.6 4.6 %collective-permute-start.2 = (f32[256,512]{1,0:T(8,128)}, f32[256,512]{1,0:T(8,128)S(1)}, u32[]{:S(2)}, u32[]{:S(2)}) collective-permute-start(f32[256,512]{1,0:T(8,128)} %collective-permute-done), channel_id=1, source_target_pairs={{0,1},{1,2},{2,3},{4,5},{5,6},{6,7},{8,9},{9,10},{10,11},{12,13},{... | collective-permute-start | bytes 1572872 | tf_op jit(solution)/shard_map/ppermute | solution.py:10
  26.5 5.9 %collective-permute-done.3 = f32[256,512]{1,0:T(8,128)S(1)} collective-permute-done((f32[256,512]{1,0:T(8,128)}, f32[256,512]{1,0:T(8,128)S(1)}, u32[]{:S(2)}, u32[]{:S(2)}) %collective-permute-start.3) | collective-permute-done | bytes 524320 | tf_op jit(solution)/shard_map/ppermute | solution.py:10
  33.8 4.6 %collective-permute-start.4 = (f32[256,512]{1,0:T(8,128)S(1)}, f32[256,512]{1,0:T(8,128)S(1)}, u32[]{:S(2)}, u32[]{:S(2)}) collective-permute-start(f32[256,512]{1,0:T(8,128)S(1)} %collective-permute-done.2), channel_id=1, source_target_pairs={{0,1},{1,2},{2,3},{4,5},{5,6},{6,7},{8,9},{9,10},{10,11},{12,13},{... | collective-permute-start | bytes 1572872 | tf_op jit(solution)/shard_map/ppermute | solution.py:10
  39.7 6.9 %collective-permute-done.5 = f32[256,512]{1,0:T(8,128)S(1)} collective-permute-done((f32[256,512]{1,0:T(8,128)S(1)}, f32[256,512]{1,0:T(8,128)S(1)}, u32[]{:S(2)}, u32[]{:S(2)}) %collective-permute-start.5) | collective-permute-done | bytes 524320 | tf_op jit(solution)/shard_map/ppermute | solution.py:10
  50.3 2.2 %collective-permute-done.6 = f32[512,256]{0,1:T(8,128)} collective-permute-done((f32[512,256]{0,1:T(8,128)}, f32[512,256]{0,1:T(8,128)}, u32[]{:S(2)}, u32[]{:S(2)}) %collective-permute-start.6) | collective-permute-done | bytes 524320 | tf_op jit(solution)/shard_map/ppermute | solution.py:15
  56.6 7.5 %collective-permute-done.7 = f32[512,128]{0,1:T(8,128)S(1)} collective-permute-done((f32[512,128]{0,1:T(8,128)}, f32[512,128]{0,1:T(8,128)S(1)}, u32[]{:S(2)}, u32[]{:S(2)}) %collective-permute-start.7) | collective-permute-done | bytes 262176 | tf_op jit(solution)/shard_map/ppermute | solution.py:15
  66.3 3.9 %collective-permute-done.8 = f32[512,64]{0,1:T(8,128)S(1)} collective-permute-done((f32[512,64]{0,1:T(8,128)S(1)}, f32[512,64]{0,1:T(8,128)S(1)}, u32[]{:S(2)}, u32[]{:S(2)}) %collective-permute-start.8) | collective-permute-done | bytes 131104 | tf_op jit(solution)/shard_map/ppermute | solution.py:15
  70.9 4.4 %collective-permute-start.9 = (f32[512,64]{0,1:T(8,128)S(1)}, f32[512,64]{0,1:T(8,128)S(1)}, u32[]{:S(2)}, u32[]{:S(2)}) collective-permute-start(f32[512,64]{0,1:T(8,128)S(1)} %convolution_bitcast_fusion.2), channel_id=1, source_target_pairs={{0,1},{1,2},{2,3},{4,5},{5,6},{6,7},{8,9},{9,10},{10,11},{12,13},{... | collective-permute-start | bytes 393224 | tf_op jit(solution)/shard_map/ppermute | solution.py:10
  78.4 4.4 %collective-permute-start.10 = (f32[512,64]{0,1:T(8,128)S(1)}, f32[512,64]{0,1:T(8,128)S(1)}, u32[]{:S(2)}, u32[]{:S(2)}) collective-permute-start(f32[512,64]{0,1:T(8,128)S(1)} %convolution_add_fusion.8), channel_id=1, source_target_pairs={{0,1},{1,2},{2,3},{4,5},{5,6},{6,7},{8,9},{9,10},{10,11},{12,13},{... | collective-permute-start | bytes 393224 | tf_op jit(solution)/shard_map/ppermute | solution.py:10
  82.7 2.5 %collective-permute-done.10 = f32[512,64]{0,1:T(8,128)S(1)} collective-permute-done((f32[512,64]{0,1:T(8,128)S(1)}, f32[512,64]{0,1:T(8,128)S(1)}, u32[]{:S(2)}, u32[]{:S(2)}) %collective-permute-start.10) | collective-permute-done | bytes 131104 | tf_op jit(solution)/shard_map/ppermute | solution.py:10
  85.8 4.4 %collective-permute-start.11 = (f32[512,64]{0,1:T(8,128)S(1)}, f32[512,64]{0,1:T(8,128)S(1)}, u32[]{:S(2)}, u32[]{:S(2)}) collective-permute-start(f32[512,64]{0,1:T(8,128)S(1)} %convolution_add_fusion.7), channel_id=1, source_target_pairs={{0,1},{1,2},{2,3},{4,5},{5,6},{6,7},{8,9},{9,10},{10,11},{12,13},{... | collective-permute-start | bytes 393224 | tf_op jit(solution)/shard_map/ppermute | solution.py:10
  90.2 2.5 %collective-permute-done.11 = f32[512,64]{0,1:T(8,128)S(1)} collective-permute-done((f32[512,64]{0,1:T(8,128)S(1)}, f32[512,64]{0,1:T(8,128)S(1)}, u32[]{:S(2)}, u32[]{:S(2)}) %collective-permute-start.11) | collective-permute-done | bytes 131104 | tf_op jit(solution)/shard_map/ppermute | solution.py:10
  95.5 7.2 %collective-permute-done.12 = f32[512,64]{0,1:T(8,128)S(1)} collective-permute-done((f32[512,64]{0,1:T(8,128)S(1)}, f32[512,64]{0,1:T(8,128)S(1)}, u32[]{:S(2)}, u32[]{:S(2)}) %collective-permute-start.12) | collective-permute-done | bytes 131104 | tf_op jit(solution)/shard_map/ppermute | solution.py:10
  104.4 6.3 %collective-permute-done.13 = f32[512,64]{0,1:T(8,128)S(1)} collective-permute-done((f32[512,64]{0,1:T(8,128)S(1)}, f32[512,64]{0,1:T(8,128)S(1)}, u32[]{:S(2)}, u32[]{:S(2)}) %collective-permute-start.13) | collective-permute-done | bytes 131104 | tf_op jit(solution)/shard_map/ppermute | solution.py:10
  112.7 5.4 %collective-permute-done.14 = f32[512,64]{0,1:T(8,128)S(1)} collective-permute-done((f32[512,64]{0,1:T(8,128)S(1)}, f32[512,64]{0,1:T(8,128)S(1)}, u32[]{:S(2)}, u32[]{:S(2)}) %collective-permute-start.14) | collective-permute-done | bytes 131104 | tf_op jit(solution)/shard_map/ppermute | solution.py:10
  119.6 3.9 %collective-permute-done.15 = f32[512,64]{0,1:T(8,128)S(1)} collective-permute-done((f32[512,64]{0,1:T(8,128)S(1)}, f32[512,64]{0,1:T(8,128)S(1)}, u32[]{:S(2)}, u32[]{:S(2)}) %collective-permute-start.15) | collective-permute-done | bytes 131104 | tf_op jit(solution)/shard_map/ppermute | solution.py:15
  124.6 5.4 %collective-permute-done.16 = f32[512,128]{0,1:T(8,128)S(1)} collective-permute-done((f32[512,128]{0,1:T(8,128)S(1)}, f32[512,128]{0,1:T(8,128)S(1)}, u32[]{:S(2)}, u32[]{:S(2)}) %collective-permute-start.16) | collective-permute-done | bytes 262176 | tf_op jit(solution)/shard_map/ppermute | solution.py:15
  130.1 1.9 %collective-permute-done.17 = f32[512,256]{0,1:T(8,128)S(1)} collective-permute-done((f32[512,256]{0,1:T(8,128)S(1)}, f32[512,256]{0,1:T(8,128)S(1)}, u32[]{:S(2)}, u32[]{:S(2)}) %collective-permute-start.17) | collective-permute-done | bytes 524320 | tf_op jit(solution)/shard_map/ppermute | solution.py:15
  132.0 1.9 fusion.2
  134.0 3.7 %collective-permute-start.18 = (f32[256,512]{1,0:T(8,128)S(1)}, f32[256,512]{1,0:T(8,128)S(1)}, u32[]{:S(2)}, u32[]{:S(2)}) collective-permute-start(f32[256,512]{1,0:T(8,128)S(1)} %get-tuple-element.10), channel_id=1, source_target_pairs={{0,1},{1,2},{2,3},{4,5},{5,6},{6,7},{8,9},{9,10},{10,11},{12,13},{... | collective-permute-start | bytes 1572872 | tf_op jit(solution)/shard_map/ppermute | solution.py:10
  138.9 10.1 %collective-permute-done.18 = f32[256,512]{1,0:T(8,128)S(1)} collective-permute-done((f32[256,512]{1,0:T(8,128)S(1)}, f32[256,512]{1,0:T(8,128)S(1)}, u32[]{:S(2)}, u32[]{:S(2)}) %collective-permute-start.18) | collective-permute-done | bytes 524320 | tf_op jit(solution)/shard_map/ppermute | solution.py:10
  149.1 4.1 %collective-permute-done.21 = f32[256,512]{1,0:T(8,128)S(1)} collective-permute-done((f32[256,512]{1,0:T(8,128)S(1)}, f32[256,512]{1,0:T(8,128)S(1)}, u32[]{:S(2)}, u32[]{:S(2)}) %collective-permute-start.21) | collective-permute-done | bytes 524320 | tf_op jit(solution)/shard_map/ppermute | solution.py:10
  153.4 3.0 %collective-permute-start.19 = (f32[256,512]{1,0:T(8,128)S(1)}, f32[256,512]{1,0:T(8,128)S(1)}, u32[]{:S(2)}, u32[]{:S(2)}) collective-permute-start(f32[256,512]{1,0:T(8,128)S(1)} %get-tuple-element.8), channel_id=1, source_target_pairs={{0,1},{1,2},{2,3},{4,5},{5,6},{6,7},{8,9},{9,10},{10,11},{12,13},{... | collective-permute-start | bytes 1572872 | tf_op jit(solution)/shard_map/ppermute | solution.py:10
  157.7 9.0 %collective-permute-done.19 = f32[256,512]{1,0:T(8,128)S(1)} collective-permute-done((f32[256,512]{1,0:T(8,128)S(1)}, f32[256,512]{1,0:T(8,128)S(1)}, u32[]{:S(2)}, u32[]{:S(2)}) %collective-permute-start.19) | collective-permute-done | bytes 524320 | tf_op jit(solution)/shard_map/ppermute | solution.py:10
  166.7 4.1 %collective-permute-done.22 = f32[256,512]{1,0:T(8,128)S(1)} collective-permute-done((f32[256,512]{1,0:T(8,128)S(1)}, f32[256,512]{1,0:T(8,128)S(1)}, u32[]{:S(2)}, u32[]{:S(2)}) %collective-permute-start.22) | collective-permute-done | bytes 524320 | tf_op jit(solution)/shard_map/ppermute | solution.py:10
  171.1 2.5 %collective-permute-start.20 = (f32[256,512]{1,0:T(8,128)S(1)}, f32[256,512]{1,0:T(8,128)S(1)}, u32[]{:S(2)}, u32[]{:S(2)}) collective-permute-start(f32[256,512]{1,0:T(8,128)S(1)} %get-tuple-element.6), channel_id=1, source_target_pairs={{0,1},{1,2},{2,3},{4,5},{5,6},{6,7},{8,9},{9,10},{10,11},{12,13},{... | collective-permute-start | bytes 1572872 | tf_op jit(solution)/shard_map/ppermute | solution.py:10
  174.9 8.1 %collective-permute-done.20 = f32[256,512]{1,0:T(8,128)S(1)} collective-permute-done((f32[256,512]{1,0:T(8,128)S(1)}, f32[256,512]{1,0:T(8,128)S(1)}, u32[]{:S(2)}, u32[]{:S(2)}) %collective-permute-start.20) | collective-permute-done | bytes 524320 | tf_op jit(solution)/shard_map/ppermute | solution.py:10
  183.0 4.1 %collective-permute-done.23 = f32[256,512]{1,0:T(8,128)S(1)} collective-permute-done((f32[256,512]{1,0:T(8,128)S(1)}, f32[256,512]{1,0:T(8,128)S(1)}, u32[]{:S(2)}, u32[]{:S(2)}) %collective-permute-start.23) | collective-permute-done | bytes 524320 | tf_op jit(solution)/shard_map/ppermute | solution.py:10
  (61 shorter events, 39.2 us)
Async XLA Ops:
  0.0 70.3 %copy-start = (f32[512,512]{1,0:T(8,128)S(1)}, f32[512,512]{1,0:T(8,128)}, u32[]{:S(2)}) copy-start(f32[512,512]{1,0:T(8,128)} %param.8) | copy-start | bytes 3145732
  0.0 17.3 %collective-permute-start.1 = (f32[256,512]{1,0:T(8,128)}, f32[256,512]{1,0:T(8,128)}, u32[]{:S(2)}, u32[]{:S(2)}) collective-permute-start(f32[256,512]{1,0:T(8,128)} %param.6), channel_id=1, source_target_pairs={{1,0},{2,1},{3,2},{5,4},{6,5},{7,6},{9,8},{10,9},{11,10},{13,12},{... | collective-permute-start | bytes 1572872 | tf_op jit(solution)/shard_map/ppermute | solution.py:10
  1.4 17.2 %collective-permute-start = (f32[256,512]{1,0:T(8,128)}, f32[256,512]{1,0:T(8,128)}, u32[]{:S(2)}, u32[]{:S(2)}) collective-permute-start(f32[256,512]{1,0:T(8,128)} %param.6), channel_id=1, source_target_pairs={{0,1},{1,2},{2,3},{4,5},{5,6},{6,7},{8,9},{9,10},{10,11},{12,13},{... | collective-permute-start | bytes 1572872 | tf_op jit(solution)/shard_map/ppermute | solution.py:10
  7.8 2.9 %copy-start.4 = (s32[8,16]{1,0:T(8,128)S(1)}, s32[8,16]{1,0:T(8,128)}, u32[]{:S(2)}) copy-start(s32[8,16]{1,0:T(8,128)} %param.7) | copy-start | bytes 1540
  17.3 15.2 %collective-permute-start.3 = (f32[256,512]{1,0:T(8,128)}, f32[256,512]{1,0:T(8,128)S(1)}, u32[]{:S(2)}, u32[]{:S(2)}) collective-permute-start(f32[256,512]{1,0:T(8,128)} %collective-permute-done.1), channel_id=1, source_target_pairs={{1,0},{2,1},{3,2},{5,4},{6,5},{7,6},{9,8},{10,9},{11,10},{13,12},{... | collective-permute-start | bytes 1572872 | tf_op jit(solution)/shard_map/ppermute | solution.py:10
  18.6 15.2 %collective-permute-start.2 = (f32[256,512]{1,0:T(8,128)}, f32[256,512]{1,0:T(8,128)S(1)}, u32[]{:S(2)}, u32[]{:S(2)}) collective-permute-start(f32[256,512]{1,0:T(8,128)} %collective-permute-done), channel_id=1, source_target_pairs={{0,1},{1,2},{2,3},{4,5},{5,6},{6,7},{8,9},{9,10},{10,11},{12,13},{... | collective-permute-start | bytes 1572872 | tf_op jit(solution)/shard_map/ppermute | solution.py:10
  32.5 14.1 %collective-permute-start.5 = (f32[256,512]{1,0:T(8,128)S(1)}, f32[256,512]{1,0:T(8,128)S(1)}, u32[]{:S(2)}, u32[]{:S(2)}) collective-permute-start(f32[256,512]{1,0:T(8,128)S(1)} %collective-permute-done.3), channel_id=1, source_target_pairs={{1,0},{2,1},{3,2},{5,4},{6,5},{7,6},{9,8},{10,9},{11,10},{13,12},{... | collective-permute-start | bytes 1572872 | tf_op jit(solution)/shard_map/ppermute | solution.py:10
  33.8 14.0 %collective-permute-start.4 = (f32[256,512]{1,0:T(8,128)S(1)}, f32[256,512]{1,0:T(8,128)S(1)}, u32[]{:S(2)}, u32[]{:S(2)}) collective-permute-start(f32[256,512]{1,0:T(8,128)S(1)} %collective-permute-done.2), channel_id=1, source_target_pairs={{0,1},{1,2},{2,3},{4,5},{5,6},{6,7},{8,9},{9,10},{10,11},{12,13},{... | collective-permute-start | bytes 1572872 | tf_op jit(solution)/shard_map/ppermute | solution.py:10
  48.4 1.0 copy-start.1
  50.3 2.3 %collective-permute-start.6 = (f32[512,256]{0,1:T(8,128)}, f32[512,256]{0,1:T(8,128)}, u32[]{:S(2)}, u32[]{:S(2)}) collective-permute-start(f32[512,256]{0,1:T(8,128)} %slice_select_fusion), channel_id=1, source_target_pairs={{0,4},{4,0},{8,12},{12,8},{16,20},{20,16},{24,28},{28,24},{1,5},{5... | collective-permute-start | bytes 1572872 | tf_op jit(solution)/shard_map/ppermute | solution.py:15
  54.0 0.8 copy-start.2
  55.5 8.6 %collective-permute-start.7 = (f32[512,128]{0,1:T(8,128)}, f32[512,128]{0,1:T(8,128)S(1)}, u32[]{:S(2)}, u32[]{:S(2)}) collective-permute-start(f32[512,128]{0,1:T(8,128)} %slice_select_fusion.1), channel_id=1, source_target_pairs={{0,8},{4,12},{8,0},{12,4},{16,24},{20,28},{24,16},{28,20},{1,9},{5... | collective-permute-start | bytes 786440 | tf_op jit(solution)/shard_map/ppermute | solution.py:15
  56.6 18.7 %copy-start.3 = (f32[512,512]{1,0:T(8,128)S(1)}, f32[512,512]{1,0:T(8,128)}, u32[]{:S(2)}) copy-start(f32[512,512]{1,0:T(8,128)} %param.9) | copy-start | bytes 3145732
  65.2 5.0 %collective-permute-start.8 = (f32[512,64]{0,1:T(8,128)S(1)}, f32[512,64]{0,1:T(8,128)S(1)}, u32[]{:S(2)}, u32[]{:S(2)}) collective-permute-start(f32[512,64]{0,1:T(8,128)S(1)} %slice_select_fusion.2), channel_id=1, source_target_pairs={{0,16},{4,20},{8,24},{12,28},{16,0},{20,4},{24,8},{28,12},{1,17},{... | collective-permute-start | bytes 393224 | tf_op jit(solution)/shard_map/ppermute | solution.py:15
  70.9 6.9 %collective-permute-start.9 = (f32[512,64]{0,1:T(8,128)S(1)}, f32[512,64]{0,1:T(8,128)S(1)}, u32[]{:S(2)}, u32[]{:S(2)}) collective-permute-start(f32[512,64]{0,1:T(8,128)S(1)} %convolution_bitcast_fusion.2), channel_id=1, source_target_pairs={{0,1},{1,2},{2,3},{4,5},{5,6},{6,7},{8,9},{9,10},{10,11},{12,13},{... | collective-permute-start | bytes 393224 | tf_op jit(solution)/shard_map/ppermute | solution.py:10
  78.4 6.9 %collective-permute-start.10 = (f32[512,64]{0,1:T(8,128)S(1)}, f32[512,64]{0,1:T(8,128)S(1)}, u32[]{:S(2)}, u32[]{:S(2)}) collective-permute-start(f32[512,64]{0,1:T(8,128)S(1)} %convolution_add_fusion.8), channel_id=1, source_target_pairs={{0,1},{1,2},{2,3},{4,5},{5,6},{6,7},{8,9},{9,10},{10,11},{12,13},{... | collective-permute-start | bytes 393224 | tf_op jit(solution)/shard_map/ppermute | solution.py:10
  85.8 6.9 %collective-permute-start.11 = (f32[512,64]{0,1:T(8,128)S(1)}, f32[512,64]{0,1:T(8,128)S(1)}, u32[]{:S(2)}, u32[]{:S(2)}) collective-permute-start(f32[512,64]{0,1:T(8,128)S(1)} %convolution_add_fusion.7), channel_id=1, source_target_pairs={{0,1},{1,2},{2,3},{4,5},{5,6},{6,7},{8,9},{9,10},{10,11},{12,13},{... | collective-permute-start | bytes 393224 | tf_op jit(solution)/shard_map/ppermute | solution.py:10
  94.2 8.5 %collective-permute-start.12 = (f32[512,64]{0,1:T(8,128)S(1)}, f32[512,64]{0,1:T(8,128)S(1)}, u32[]{:S(2)}, u32[]{:S(2)}) collective-permute-start(f32[512,64]{0,1:T(8,128)S(1)} %convolution_bitcast_fusion.1), channel_id=1, source_target_pairs={{1,0},{2,1},{3,2},{5,4},{6,5},{7,6},{9,8},{10,9},{11,10},{13,12},{... | collective-permute-start | bytes 393224 | tf_op jit(solution)/shard_map/ppermute | solution.py:10
  103.1 7.6 %collective-permute-start.13 = (f32[512,64]{0,1:T(8,128)S(1)}, f32[512,64]{0,1:T(8,128)S(1)}, u32[]{:S(2)}, u32[]{:S(2)}) collective-permute-start(f32[512,64]{0,1:T(8,128)S(1)} %convolution_add_fusion.5), channel_id=1, source_target_pairs={{1,0},{2,1},{3,2},{5,4},{6,5},{7,6},{9,8},{10,9},{11,10},{13,12},{... | collective-permute-start | bytes 393224 | tf_op jit(solution)/shard_map/ppermute | solution.py:10
  111.2 6.9 %collective-permute-start.14 = (f32[512,64]{0,1:T(8,128)S(1)}, f32[512,64]{0,1:T(8,128)S(1)}, u32[]{:S(2)}, u32[]{:S(2)}) collective-permute-start(f32[512,64]{0,1:T(8,128)S(1)} %convolution_add_fusion.4), channel_id=1, source_target_pairs={{1,0},{2,1},{3,2},{5,4},{6,5},{7,6},{9,8},{10,9},{11,10},{13,12},{... | collective-permute-start | bytes 393224 | tf_op jit(solution)/shard_map/ppermute | solution.py:10
  118.5 5.0 %collective-permute-start.15 = (f32[512,64]{0,1:T(8,128)S(1)}, f32[512,64]{0,1:T(8,128)S(1)}, u32[]{:S(2)}, u32[]{:S(2)}) collective-permute-start(f32[512,64]{0,1:T(8,128)S(1)} %convolution_bitcast_fusion), channel_id=1, source_target_pairs={{0,16},{4,20},{8,24},{12,28},{16,0},{20,4},{24,8},{28,12},{1,17},{... | collective-permute-start | bytes 393224 | tf_op jit(solution)/shard_map/ppermute | solution.py:15
  123.5 6.4 %collective-permute-start.16 = (f32[512,128]{0,1:T(8,128)S(1)}, f32[512,128]{0,1:T(8,128)S(1)}, u32[]{:S(2)}, u32[]{:S(2)}) collective-permute-start(f32[512,128]{0,1:T(8,128)S(1)} %maximum_select_fusion.3), channel_id=1, source_target_pairs={{0,8},{4,12},{8,0},{12,4},{16,24},{20,28},{24,16},{28,20},{1,9},{5... | collective-permute-start | bytes 786440 | tf_op jit(solution)/shard_map/ppermute | solution.py:15
  130.0 2.0 %collective-permute-start.17 = (f32[512,256]{0,1:T(8,128)S(1)}, f32[512,256]{0,1:T(8,128)S(1)}, u32[]{:S(2)}, u32[]{:S(2)}) collective-permute-start(f32[512,256]{0,1:T(8,128)S(1)} %maximum_select_fusion.2), channel_id=1, source_target_pairs={{0,4},{4,0},{8,12},{12,8},{16,20},{20,16},{24,28},{28,24},{1,5},{5... | collective-permute-start | bytes 1572872 | tf_op jit(solution)/shard_map/ppermute | solution.py:15
  134.0 15.1 %collective-permute-start.18 = (f32[256,512]{1,0:T(8,128)S(1)}, f32[256,512]{1,0:T(8,128)S(1)}, u32[]{:S(2)}, u32[]{:S(2)}) collective-permute-start(f32[256,512]{1,0:T(8,128)S(1)} %get-tuple-element.10), channel_id=1, source_target_pairs={{0,1},{1,2},{2,3},{4,5},{5,6},{6,7},{8,9},{9,10},{10,11},{12,13},{... | collective-permute-start | bytes 1572872 | tf_op jit(solution)/shard_map/ppermute | solution.py:10
  137.6 15.6 %collective-permute-start.21 = (f32[256,512]{1,0:T(8,128)S(1)}, f32[256,512]{1,0:T(8,128)S(1)}, u32[]{:S(2)}, u32[]{:S(2)}) collective-permute-start(f32[256,512]{1,0:T(8,128)S(1)} %get-tuple-element.9), channel_id=1, source_target_pairs={{1,0},{2,1},{3,2},{5,4},{6,5},{7,6},{9,8},{10,9},{11,10},{13,12},{... | collective-permute-start | bytes 1572872 | tf_op jit(solution)/shard_map/ppermute | solution.py:10
  153.4 13.3 %collective-permute-start.19 = (f32[256,512]{1,0:T(8,128)S(1)}, f32[256,512]{1,0:T(8,128)S(1)}, u32[]{:S(2)}, u32[]{:S(2)}) collective-permute-start(f32[256,512]{1,0:T(8,128)S(1)} %get-tuple-element.8), channel_id=1, source_target_pairs={{0,1},{1,2},{2,3},{4,5},{5,6},{6,7},{8,9},{9,10},{10,11},{12,13},{... | collective-permute-start | bytes 1572872 | tf_op jit(solution)/shard_map/ppermute | solution.py:10
  156.4 14.4 %collective-permute-start.22 = (f32[256,512]{1,0:T(8,128)S(1)}, f32[256,512]{1,0:T(8,128)S(1)}, u32[]{:S(2)}, u32[]{:S(2)}) collective-permute-start(f32[256,512]{1,0:T(8,128)S(1)} %get-tuple-element.7), channel_id=1, source_target_pairs={{1,0},{2,1},{3,2},{5,4},{6,5},{7,6},{9,8},{10,9},{11,10},{13,12},{... | collective-permute-start | bytes 1572872 | tf_op jit(solution)/shard_map/ppermute | solution.py:10
  171.1 11.9 %collective-permute-start.20 = (f32[256,512]{1,0:T(8,128)S(1)}, f32[256,512]{1,0:T(8,128)S(1)}, u32[]{:S(2)}, u32[]{:S(2)}) collective-permute-start(f32[256,512]{1,0:T(8,128)S(1)} %get-tuple-element.6), channel_id=1, source_target_pairs={{0,1},{1,2},{2,3},{4,5},{5,6},{6,7},{8,9},{9,10},{10,11},{12,13},{... | collective-permute-start | bytes 1572872 | tf_op jit(solution)/shard_map/ppermute | solution.py:10
  173.6 13.5 %collective-permute-start.23 = (f32[256,512]{1,0:T(8,128)S(1)}, f32[256,512]{1,0:T(8,128)S(1)}, u32[]{:S(2)}, u32[]{:S(2)}) collective-permute-start(f32[256,512]{1,0:T(8,128)S(1)} %get-tuple-element.5), channel_id=1, source_target_pairs={{1,0},{2,1},{3,2},{5,4},{6,5},{7,6},{9,8},{10,9},{11,10},{13,12},{... | collective-permute-start | bytes 1572872 | tf_op jit(solution)/shard_map/ppermute | solution.py:10

commit v9 on v2

--- a/solution.py
+++ b/solution.py
@@ -129,10 +129,14 @@
     transfer = -product(diag_inverse, sub_factor)
     width = densities.shape[1] // SLICES
     results = []
+    gate = None
     for part in range(SLICES):
         dens_part = densities[:, part * width:(part + 1) * width]
+        if gate is not None:
+            dens_part, _ = lax.optimization_barrier((dens_part, gate))
         gamma_partial = gamma_over_aux(screened, dens_part)
         right_side = reduce_scatter_columns(gamma_partial, "pair")
+        gate = right_side
         coefficients = solve(right_side, transfer, diag_inverse, sub_factor)
         coeff_full = all_gather_columns(coefficients, "pair")
         partial = contract_first(screened, coeff_full)

time: 181 us -> 198 us (1.094)
  starting transfers between devices: 106 us -> 117 us
  waiting for transfers between devices: 40.6 us -> 47.9 us
  matrix products: 22.7 us -> 19.4 us
    ppermute x36, starting transfers between devices: 93.6 us -> 104 us  [from_behind(): return lax.ppermute(array, axis, pairs)]
    ppermute x12, waiting for transfers between devices: 11.8 us -> 16.7 us  [swap(): return lax.ppermute(array, axis, [(i, i ^ bit) for i in range(count)])]
    dot_general x33, matrix products: 20.7 us -> 17.3 us  [product(): jnp.dot(left, right, precision=lax.Precision.HIGH, preferred_element_type...]
    ppermute x36, waiting for transfers between devices: 28.8 us -> 31.2 us  [from_behind(): return lax.ppermute(array, axis, pairs)]
  transfers between devices with their start and end apart: 48 -> 48, of which waited for: 21 -> 26; matrix products, arithmetic and copies ran while one was open for 16% -> 12% of each run, Pallas kernels for 0% -> 0%
where the time goes in v9:
time: 198 us; the launch traced here: 197 us
  starting transfers between devices  117 us (59%)
  waiting for transfers between devices  47.9 us (24%)
  matrix products  19.4 us (10%)
  local copies, waits for them, and re-layouts  7.01 us (4%)
  other arithmetic  4.53 us (2%)
    ppermute x36, starting transfers between devices, from_behind(): return lax.ppermute(array, axis, pairs)  104 us
    ppermute x36, waiting for transfers between devices, from_behind(): return lax.ppermute(array, axis, pairs)  31.2 us
    dot_general x33, matrix products, product(): jnp.dot(left, right, precision=lax.Precision.HIGH, preferred_element_type...  17.3 us
    ppermute x12, waiting for transfers between devices, swap(): return lax.ppermute(array, axis, [(i, i ^ bit) for i in range(count)])  16.7 us
    ppermute x12, starting transfers between devices, swap(): return lax.ppermute(array, axis, [(i, i ^ bit) for i in range(count)])  12.8 us
  transfers between devices with their start and end apart: 48, of which 26 were waited for; matrix products, arithmetic and copies ran while one was open for 12% of the time, Pallas kernels for 0%

profile of v9, /device:TPU:0, one launch (start us, length us, event | category | flops | bytes accessed | tf_op | source)
XLA Modules:
  0.0 196.7 jit_solution(6613768292507185961)
XLA Ops:
  0.0 2.0 fusion.62
  3.2 5.6 %collective-permute-start = (f32[256,256]{1,0:T(8,128)}, f32[256,256]{1,0:T(8,128)S(1)}, u32[]{:S(2)}, u32[]{:S(2)}) collective-permute-start(f32[256,256]{1,0:T(8,128)} %get-tuple-element.19), channel_id=1, source_target_pairs={{0,1},{1,2},{2,3},{4,5},{5,6},{6,7},{8,9},{9,10},{10,11},{12,13},{... | collective-permute-start | bytes 786440 | tf_op jit(solution)/shard_map/ppermute | solution.py:10
  8.9 2.9 %copy.8 = f32[512,1024]{0,1:T(8,128)} copy(f32[512,1024]{1,0:T(8,128)} %param.5) | data formatting | bytes 4194304 | tf_op args[0]
  16.6 4.6 %collective-permute-start.2 = (f32[256,256]{1,0:T(8,128)S(1)}, f32[256,256]{1,0:T(8,128)S(1)}, u32[]{:S(2)}, u32[]{:S(2)}) collective-permute-start(f32[256,256]{1,0:T(8,128)S(1)} %collective-permute-done), channel_id=1, source_target_pairs={{0,1},{1,2},{2,3},{4,5},{5,6},{6,7},{8,9},{9,10},{10,11},{12,13},{... | collective-permute-start | bytes 786440 | tf_op jit(solution)/shard_map/ppermute | solution.py:10
  23.0 2.2 %collective-permute-done.3 = f32[256,256]{1,0:T(8,128)S(1)} collective-permute-done((f32[256,256]{1,0:T(8,128)}, f32[256,256]{1,0:T(8,128)S(1)}, u32[]{:S(2)}, u32[]{:S(2)}) %collective-permute-start.3) | collective-permute-done | bytes 262176 | tf_op jit(solution)/shard_map/ppermute | solution.py:10
  26.9 4.8 %collective-permute-start.4 = (f32[256,256]{1,0:T(8,128)S(1)}, f32[256,256]{1,0:T(8,128)S(1)}, u32[]{:S(2)}, u32[]{:S(2)}) collective-permute-start(f32[256,256]{1,0:T(8,128)S(1)} %collective-permute-done.2), channel_id=1, source_target_pairs={{0,1},{1,2},{2,3},{4,5},{5,6},{6,7},{8,9},{9,10},{10,11},{12,13},{... | collective-permute-start | bytes 786440 | tf_op jit(solution)/shard_map/ppermute | solution.py:10
  32.1 2.3 %collective-permute-done.5 = f32[256,256]{1,0:T(8,128)S(1)} collective-permute-done((f32[256,256]{1,0:T(8,128)S(1)}, f32[256,256]{1,0:T(8,128)S(1)}, u32[]{:S(2)}, u32[]{:S(2)}) %collective-permute-start.5) | collective-permute-done | bytes 262176 | tf_op jit(solution)/shard_map/ppermute | solution.py:10
  42.4 4.3 %collective-permute-done.7 = f32[512,64]{0,1:T(8,128)S(1)} collective-permute-done((f32[512,64]{0,1:T(8,128)}, f32[512,64]{0,1:T(8,128)S(1)}, u32[]{:S(2)}, u32[]{:S(2)}) %collective-permute-start.7) | collective-permute-done | bytes 131104 | tf_op jit(solution)/shard_map/ppermute | solution.py:15
  48.3 2.8 %collective-permute-done.8 = f32[512,32]{0,1:T(8,128)S(1)} collective-permute-done((f32[512,32]{0,1:T(8,128)S(1)}, f32[512,32]{0,1:T(8,128)S(1)}, u32[]{:S(2)}, u32[]{:S(2)}) %collective-permute-start.8) | collective-permute-done | bytes 65568 | tf_op jit(solution)/shard_map/ppermute | solution.py:15
  52.3 5.0 %collective-permute-start.24 = (f32[256,256]{1,0:T(8,128)}, f32[256,256]{1,0:T(8,128)S(1)}, u32[]{:S(2)}, u32[]{:S(2)}) collective-permute-start(f32[256,256]{1,0:T(8,128)} %get-tuple-element.6), channel_id=1, source_target_pairs={{0,1},{1,2},{2,3},{4,5},{5,6},{6,7},{8,9},{9,10},{10,11},{12,13},{... | collective-permute-start | bytes 786440 | tf_op jit(solution)/shard_map/ppermute | solution.py:10
  58.0 3.9 %collective-permute-start.9 = (f32[512,32]{0,1:T(8,128)S(1)}, f32[512,32]{0,1:T(8,128)S(1)}, u32[]{:S(2)}, u32[]{:S(2)}) collective-permute-start(f32[512,32]{0,1:T(8,128)S(1)} %convolution_bitcast_fusion.5), channel_id=1, source_target_pairs={{0,1},{1,2},{2,3},{4,5},{5,6},{6,7},{8,9},{9,10},{10,11},{12,13},{... | collective-permute-start | bytes 196616 | tf_op jit(solution)/shard_map/ppermute | solution.py:10
  64.1 4.6 %collective-permute-start.26 = (f32[256,256]{1,0:T(8,128)S(1)}, f32[256,256]{1,0:T(8,128)S(1)}, u32[]{:S(2)}, u32[]{:S(2)}) collective-permute-start(f32[256,256]{1,0:T(8,128)S(1)} %collective-permute-done.24), channel_id=1, source_target_pairs={{0,1},{1,2},{2,3},{4,5},{5,6},{6,7},{8,9},{9,10},{10,11},{12,13},{... | collective-permute-start | bytes 786440 | tf_op jit(solution)/shard_map/ppermute | solution.py:10
  72.5 4.4 %collective-permute-start.28 = (f32[256,256]{1,0:T(8,128)S(1)}, f32[256,256]{1,0:T(8,128)S(1)}, u32[]{:S(2)}, u32[]{:S(2)}) collective-permute-start(f32[256,256]{1,0:T(8,128)S(1)} %collective-permute-done.26), channel_id=1, source_target_pairs={{0,1},{1,2},{2,3},{4,5},{5,6},{6,7},{8,9},{9,10},{10,11},{12,13},{... | collective-permute-start | bytes 786440 | tf_op jit(solution)/shard_map/ppermute | solution.py:10
  78.8 1.9 collective-permute-done.28
  82.9 4.4 %collective-permute-start.10 = (f32[512,32]{0,1:T(8,128)S(1)}, f32[512,32]{0,1:T(8,128)S(1)}, u32[]{:S(2)}, u32[]{:S(2)}) collective-permute-start(f32[512,32]{0,1:T(8,128)S(1)} %convolution_add_fusion.17), channel_id=1, source_target_pairs={{0,1},{1,2},{2,3},{4,5},{5,6},{6,7},{8,9},{9,10},{10,11},{12,13},{... | collective-permute-start | bytes 196616 | tf_op jit(solution)/shard_map/ppermute | solution.py:10
  89.9 4.4 %collective-permute-start.11 = (f32[512,32]{0,1:T(8,128)S(1)}, f32[512,32]{0,1:T(8,128)S(1)}, u32[]{:S(2)}, u32[]{:S(2)}) collective-permute-start(f32[512,32]{0,1:T(8,128)S(1)} %convolution_add_fusion.16), channel_id=1, source_target_pairs={{0,1},{1,2},{2,3},{4,5},{5,6},{6,7},{8,9},{9,10},{10,11},{12,13},{... | collective-permute-start | bytes 196616 | tf_op jit(solution)/shard_map/ppermute | solution.py:10
  96.7 1.9 collective-permute-done.32
  99.2 3.8 %collective-permute-start.33 = (f32[512,32]{0,1:T(8,128)S(1)}, f32[512,32]{0,1:T(8,128)S(1)}, u32[]{:S(2)}, u32[]{:S(2)}) collective-permute-start(f32[512,32]{0,1:T(8,128)S(1)} %convolution_bitcast_fusion.2), channel_id=1, source_target_pairs={{0,1},{1,2},{2,3},{4,5},{5,6},{6,7},{8,9},{9,10},{10,11},{12,13},{... | collective-permute-start | bytes 196616 | tf_op jit(solution)/shard_map/ppermute | solution.py:10
  105.4 4.3 %collective-permute-start.34 = (f32[512,32]{0,1:T(8,128)S(1)}, f32[512,32]{0,1:T(8,128)S(1)}, u32[]{:S(2)}, u32[]{:S(2)}) collective-permute-start(f32[512,32]{0,1:T(8,128)S(1)} %convolution_add_fusion.12), channel_id=1, source_target_pairs={{0,1},{1,2},{2,3},{4,5},{5,6},{6,7},{8,9},{9,10},{10,11},{12,13},{... | collective-permute-start | bytes 196616 | tf_op jit(solution)/shard_map/ppermute | solution.py:10
  112.1 4.4 %collective-permute-start.35 = (f32[512,32]{0,1:T(8,128)S(1)}, f32[512,32]{0,1:T(8,128)S(1)}, u32[]{:S(2)}, u32[]{:S(2)}) collective-permute-start(f32[512,32]{0,1:T(8,128)S(1)} %convolution_add_fusion.11), channel_id=1, source_target_pairs={{0,1},{1,2},{2,3},{4,5},{5,6},{6,7},{8,9},{9,10},{10,11},{12,13},{... | collective-permute-start | bytes 196616 | tf_op jit(solution)/shard_map/ppermute | solution.py:10
  121.0 2.0 %collective-permute-done.13 = f32[512,32]{0,1:T(8,128)S(1)} collective-permute-done((f32[512,32]{0,1:T(8,128)S(1)}, f32[512,32]{0,1:T(8,128)S(1)}, u32[]{:S(2)}, u32[]{:S(2)}) %collective-permute-start.13) | collective-permute-done | bytes 65568 | tf_op jit(solution)/shard_map/ppermute | solution.py:10
  136.6 3.5 %collective-permute-done.38 = f32[512,32]{0,1:T(8,128)S(1)} collective-permute-done((f32[512,32]{0,1:T(8,128)S(1)}, f32[512,32]{0,1:T(8,128)S(1)}, u32[]{:S(2)}, u32[]{:S(2)}) %collective-permute-start.38) | collective-permute-done | bytes 65568 | tf_op jit(solution)/shard_map/ppermute | solution.py:10
  142.1 2.6 %collective-permute-done.39 = f32[512,32]{0,1:T(8,128)S(1)} collective-permute-done((f32[512,32]{0,1:T(8,128)S(1)}, f32[512,32]{0,1:T(8,128)S(1)}, u32[]{:S(2)}, u32[]{:S(2)}) %collective-permute-start.39) | collective-permute-done | bytes 65568 | tf_op jit(solution)/shard_map/ppermute | solution.py:15
  146.3 3.5 %collective-permute-done.40 = f32[512,64]{0,1:T(8,128)S(1)} collective-permute-done((f32[512,64]{0,1:T(8,128)S(1)}, f32[512,64]{0,1:T(8,128)S(1)}, u32[]{:S(2)}, u32[]{:S(2)}) %collective-permute-start.40) | collective-permute-done | bytes 131104 | tf_op jit(solution)/shard_map/ppermute | solution.py:15
  152.3 4.6 %collective-permute-start.18 = (f32[256,256]{0,1:T(8,128)S(1)}, f32[256,256]{0,1:T(8,128)S(1)}, u32[]{:S(2)}, u32[]{:S(2)}) collective-permute-start(f32[256,256]{0,1:T(8,128)S(1)} %get-tuple-element.12), channel_id=1, source_target_pairs={{0,1},{1,2},{2,3},{4,5},{5,6},{6,7},{8,9},{9,10},{10,11},{12,13},{... | collective-permute-start | bytes 786440 | tf_op jit(solution)/shard_map/ppermute | solution.py:10
  159.3 4.6 %collective-permute-start.42 = (f32[256,256]{0,1:T(8,128)S(1)}, f32[256,256]{0,1:T(8,128)S(1)}, u32[]{:S(2)}, u32[]{:S(2)}) collective-permute-start(f32[256,256]{0,1:T(8,128)S(1)} %get-tuple-element.18), channel_id=1, source_target_pairs={{0,1},{1,2},{2,3},{4,5},{5,6},{6,7},{8,9},{9,10},{10,11},{12,13},{... | collective-permute-start | bytes 786440 | tf_op jit(solution)/shard_map/ppermute | solution.py:10
  165.3 4.6 %collective-permute-start.19 = (f32[256,256]{0,1:T(8,128)S(1)}, f32[256,256]{0,1:T(8,128)S(1)}, u32[]{:S(2)}, u32[]{:S(2)}) collective-permute-start(f32[256,256]{0,1:T(8,128)S(1)} %get-tuple-element.10), channel_id=1, source_target_pairs={{0,1},{1,2},{2,3},{4,5},{5,6},{6,7},{8,9},{9,10},{10,11},{12,13},{... | collective-permute-start | bytes 786440 | tf_op jit(solution)/shard_map/ppermute | solution.py:10
  171.3 4.8 %collective-permute-start.43 = (f32[256,256]{0,1:T(8,128)S(1)}, f32[256,256]{0,1:T(8,128)S(1)}, u32[]{:S(2)}, u32[]{:S(2)}) collective-permute-start(f32[256,256]{0,1:T(8,128)S(1)} %get-tuple-element.16), channel_id=1, source_target_pairs={{0,1},{1,2},{2,3},{4,5},{5,6},{6,7},{8,9},{9,10},{10,11},{12,13},{... | collective-permute-start | bytes 786440 | tf_op jit(solution)/shard_map/ppermute | solution.py:10
  176.2 3.9 %collective-permute-start.20 = (f32[256,256]{0,1:T(8,128)S(1)}, f32[256,256]{0,1:T(8,128)S(1)}, u32[]{:S(2)}, u32[]{:S(2)}) collective-permute-start(f32[256,256]{0,1:T(8,128)S(1)} %get-tuple-element.8), channel_id=1, source_target_pairs={{0,1},{1,2},{2,3},{4,5},{5,6},{6,7},{8,9},{9,10},{10,11},{12,13},{... | collective-permute-start | bytes 786440 | tf_op jit(solution)/shard_map/ppermute | solution.py:10
  182.9 4.4 %collective-permute-start.44 = (f32[256,256]{0,1:T(8,128)S(1)}, f32[256,256]{0,1:T(8,128)S(1)}, u32[]{:S(2)}, u32[]{:S(2)}) collective-permute-start(f32[256,256]{0,1:T(8,128)S(1)} %get-tuple-element.14), channel_id=1, source_target_pairs={{0,1},{1,2},{2,3},{4,5},{5,6},{6,7},{8,9},{9,10},{10,11},{12,13},{... | collective-permute-start | bytes 786440 | tf_op jit(solution)/shard_map/ppermute | solution.py:10
  188.7 3.3 %collective-permute-done.44 = f32[256,256]{0,1:T(8,128)S(1)} collective-permute-done((f32[256,256]{0,1:T(8,128)S(1)}, f32[256,256]{0,1:T(8,128)S(1)}, u32[]{:S(2)}, u32[]{:S(2)}) %collective-permute-start.44) | collective-permute-done | bytes 262176 | tf_op jit(solution)/shard_map/ppermute | solution.py:10
  192.0 3.6 %collective-permute-done.47 = f32[256,256]{0,1:T(8,128)S(1)} collective-permute-done((f32[256,256]{0,1:T(8,128)S(1)}, f32[256,256]{0,1:T(8,128)S(1)}, u32[]{:S(2)}, u32[]{:S(2)}) %collective-permute-start.47) | collective-permute-done | bytes 262176 | tf_op jit(solution)/shard_map/ppermute | solution.py:10
  (141 shorter events, 76.1 us)
Async XLA Ops:
  2.0 13.3 %collective-permute-start.1 = (f32[256,256]{1,0:T(8,128)}, f32[256,256]{1,0:T(8,128)}, u32[]{:S(2)}, u32[]{:S(2)}) collective-permute-start(f32[256,256]{1,0:T(8,128)} %get-tuple-element.19), channel_id=1, source_target_pairs={{1,0},{2,1},{3,2},{5,4},{6,5},{7,6},{9,8},{10,9},{11,10},{13,12},{... | collective-permute-start | bytes 786440 | tf_op jit(solution)/shard_map/ppermute | solution.py:10
  3.2 13.3 %collective-permute-start = (f32[256,256]{1,0:T(8,128)}, f32[256,256]{1,0:T(8,128)S(1)}, u32[]{:S(2)}, u32[]{:S(2)}) collective-permute-start(f32[256,256]{1,0:T(8,128)} %get-tuple-element.19), channel_id=1, source_target_pairs={{0,1},{1,2},{2,3},{4,5},{5,6},{6,7},{8,9},{9,10},{10,11},{12,13},{... | collective-permute-start | bytes 786440 | tf_op jit(solution)/shard_map/ppermute | solution.py:10
  15.3 9.9 %collective-permute-start.3 = (f32[256,256]{1,0:T(8,128)}, f32[256,256]{1,0:T(8,128)S(1)}, u32[]{:S(2)}, u32[]{:S(2)}) collective-permute-start(f32[256,256]{1,0:T(8,128)} %collective-permute-done.1), channel_id=1, source_target_pairs={{1,0},{2,1},{3,2},{5,4},{6,5},{7,6},{9,8},{10,9},{11,10},{13,12},{... | collective-permute-start | bytes 786440 | tf_op jit(solution)/shard_map/ppermute | solution.py:10
  16.6 10.3 %collective-permute-start.2 = (f32[256,256]{1,0:T(8,128)S(1)}, f32[256,256]{1,0:T(8,128)S(1)}, u32[]{:S(2)}, u32[]{:S(2)}) collective-permute-start(f32[256,256]{1,0:T(8,128)S(1)} %collective-permute-done), channel_id=1, source_target_pairs={{0,1},{1,2},{2,3},{4,5},{5,6},{6,7},{8,9},{9,10},{10,11},{12,13},{... | collective-permute-start | bytes 786440 | tf_op jit(solution)/shard_map/ppermute | solution.py:10
  25.2 9.3 %collective-permute-start.5 = (f32[256,256]{1,0:T(8,128)S(1)}, f32[256,256]{1,0:T(8,128)S(1)}, u32[]{:S(2)}, u32[]{:S(2)}) collective-permute-start(f32[256,256]{1,0:T(8,128)S(1)} %collective-permute-done.3), channel_id=1, source_target_pairs={{1,0},{2,1},{3,2},{5,4},{6,5},{7,6},{9,8},{10,9},{11,10},{13,12},{... | collective-permute-start | bytes 786440 | tf_op jit(solution)/shard_map/ppermute | solution.py:10
  26.9 9.2 %collective-permute-start.4 = (f32[256,256]{1,0:T(8,128)S(1)}, f32[256,256]{1,0:T(8,128)S(1)}, u32[]{:S(2)}, u32[]{:S(2)}) collective-permute-start(f32[256,256]{1,0:T(8,128)S(1)} %collective-permute-done.2), channel_id=1, source_target_pairs={{0,1},{1,2},{2,3},{4,5},{5,6},{6,7},{8,9},{9,10},{10,11},{12,13},{... | collective-permute-start | bytes 786440 | tf_op jit(solution)/shard_map/ppermute | solution.py:10
  51.0 10.8 %collective-permute-start.25 = (f32[256,256]{1,0:T(8,128)}, f32[256,256]{1,0:T(8,128)S(1)}, u32[]{:S(2)}, u32[]{:S(2)}) collective-permute-start(f32[256,256]{1,0:T(8,128)} %get-tuple-element.6), channel_id=1, source_target_pairs={{1,0},{2,1},{3,2},{5,4},{6,5},{7,6},{9,8},{10,9},{11,10},{13,12},{... | collective-permute-start | bytes 786440 | tf_op jit(solution)/shard_map/ppermute | solution.py:10
  52.3 10.9 %collective-permute-start.24 = (f32[256,256]{1,0:T(8,128)}, f32[256,256]{1,0:T(8,128)S(1)}, u32[]{:S(2)}, u32[]{:S(2)}) collective-permute-start(f32[256,256]{1,0:T(8,128)} %get-tuple-element.6), channel_id=1, source_target_pairs={{0,1},{1,2},{2,3},{4,5},{5,6},{6,7},{8,9},{9,10},{10,11},{12,13},{... | collective-permute-start | bytes 786440 | tf_op jit(solution)/shard_map/ppermute | solution.py:10
  58.0 24.4 %collective-permute-start.9 = (f32[512,32]{0,1:T(8,128)S(1)}, f32[512,32]{0,1:T(8,128)S(1)}, u32[]{:S(2)}, u32[]{:S(2)}) collective-permute-start(f32[512,32]{0,1:T(8,128)S(1)} %convolution_bitcast_fusion.5), channel_id=1, source_target_pairs={{0,1},{1,2},{2,3},{4,5},{5,6},{6,7},{8,9},{9,10},{10,11},{12,13},{... | collective-permute-start | bytes 196616 | tf_op jit(solution)/shard_map/ppermute | solution.py:10
  61.9 8.3 %collective-permute-start.27 = (f32[256,256]{1,0:T(8,128)S(1)}, f32[256,256]{1,0:T(8,128)S(1)}, u32[]{:S(2)}, u32[]{:S(2)}) collective-permute-start(f32[256,256]{1,0:T(8,128)S(1)} %collective-permute-done.25), channel_id=1, source_target_pairs={{1,0},{2,1},{3,2},{5,4},{6,5},{7,6},{9,8},{10,9},{11,10},{13,12},{... | collective-permute-start | bytes 786440 | tf_op jit(solution)/shard_map/ppermute | solution.py:10
  64.1 8.4 %collective-permute-start.26 = (f32[256,256]{1,0:T(8,128)S(1)}, f32[256,256]{1,0:T(8,128)S(1)}, u32[]{:S(2)}, u32[]{:S(2)}) collective-permute-start(f32[256,256]{1,0:T(8,128)S(1)} %collective-permute-done.24), channel_id=1, source_target_pairs={{0,1},{1,2},{2,3},{4,5},{5,6},{6,7},{8,9},{9,10},{10,11},{12,13},{... | collective-permute-start | bytes 786440 | tf_op jit(solution)/shard_map/ppermute | solution.py:10
  70.1 8.3 %collective-permute-start.29 = (f32[256,256]{1,0:T(8,128)S(1)}, f32[256,256]{1,0:T(8,128)S(1)}, u32[]{:S(2)}, u32[]{:S(2)}) collective-permute-start(f32[256,256]{1,0:T(8,128)S(1)} %collective-permute-done.27), channel_id=1, source_target_pairs={{1,0},{2,1},{3,2},{5,4},{6,5},{7,6},{9,8},{10,9},{11,10},{13,12},{... | collective-permute-start | bytes 786440 | tf_op jit(solution)/shard_map/ppermute | solution.py:10
  72.5 8.3 %collective-permute-start.28 = (f32[256,256]{1,0:T(8,128)S(1)}, f32[256,256]{1,0:T(8,128)S(1)}, u32[]{:S(2)}, u32[]{:S(2)}) collective-permute-start(f32[256,256]{1,0:T(8,128)S(1)} %collective-permute-done.26), channel_id=1, source_target_pairs={{0,1},{1,2},{2,3},{4,5},{5,6},{6,7},{8,9},{9,10},{10,11},{12,13},{... | collective-permute-start | bytes 786440 | tf_op jit(solution)/shard_map/ppermute | solution.py:10
  87.4 6.8 %collective-permute-start.31 = (f32[512,64]{0,1:T(8,128)S(1)}, f32[512,64]{0,1:T(8,128)S(1)}, u32[]{:S(2)}, u32[]{:S(2)}) collective-permute-start(f32[512,64]{0,1:T(8,128)S(1)} %slice_select_fusion.2), channel_id=1, source_target_pairs={{0,8},{4,12},{8,0},{12,4},{16,24},{20,28},{24,16},{28,20},{1,9},{5... | collective-permute-start | bytes 393224 | tf_op jit(solution)/shard_map/ppermute | solution.py:15
  110.0 6.4 %collective-permute-start.12 = (f32[512,32]{0,1:T(8,128)S(1)}, f32[512,32]{0,1:T(8,128)S(1)}, u32[]{:S(2)}, u32[]{:S(2)}) collective-permute-start(f32[512,32]{0,1:T(8,128)S(1)} %convolution_bitcast_fusion.4), channel_id=1, source_target_pairs={{1,0},{2,1},{3,2},{5,4},{6,5},{7,6},{9,8},{10,9},{11,10},{13,12},{... | collective-permute-start | bytes 196616 | tf_op jit(solution)/shard_map/ppermute | solution.py:10
  119.7 6.6 %collective-permute-start.36 = (f32[512,32]{0,1:T(8,128)S(1)}, f32[512,32]{0,1:T(8,128)S(1)}, u32[]{:S(2)}, u32[]{:S(2)}) collective-permute-start(f32[512,32]{0,1:T(8,128)S(1)} %convolution_bitcast_fusion.1), channel_id=1, source_target_pairs={{1,0},{2,1},{3,2},{5,4},{6,5},{7,6},{9,8},{10,9},{11,10},{13,12},{... | collective-permute-start | bytes 196616 | tf_op jit(solution)/shard_map/ppermute | solution.py:10
  126.7 6.5 %collective-permute-start.37 = (f32[512,32]{0,1:T(8,128)S(1)}, f32[512,32]{0,1:T(8,128)S(1)}, u32[]{:S(2)}, u32[]{:S(2)}) collective-permute-start(f32[512,32]{0,1:T(8,128)S(1)} %convolution_add_fusion.9), channel_id=1, source_target_pairs={{1,0},{2,1},{3,2},{5,4},{6,5},{7,6},{9,8},{10,9},{11,10},{13,12},{... | collective-permute-start | bytes 196616 | tf_op jit(solution)/shard_map/ppermute | solution.py:10
  135.0 7.0 %collective-permute-start.16 = (f32[512,64]{0,1:T(8,128)S(1)}, f32[512,64]{0,1:T(8,128)S(1)}, u32[]{:S(2)}, u32[]{:S(2)}) collective-permute-start(f32[512,64]{0,1:T(8,128)S(1)} %maximum_select_fusion.6), channel_id=1, source_target_pairs={{0,8},{4,12},{8,0},{12,4},{16,24},{20,28},{24,16},{28,20},{1,9},{5... | collective-permute-start | bytes 393224 | tf_op jit(solution)/shard_map/ppermute | solution.py:15
  142.1 7.9 %collective-permute-start.17 = (f32[512,128]{0,1:T(8,128)S(1)}, f32[512,128]{0,1:T(8,128)S(1)}, u32[]{:S(2)}, u32[]{:S(2)}) collective-permute-start(f32[512,128]{0,1:T(8,128)S(1)} %maximum_select_fusion.4), channel_id=1, source_target_pairs={{0,4},{4,0},{8,12},{12,8},{16,20},{20,16},{24,28},{28,24},{1,5},{5... | collective-permute-start | bytes 786440 | tf_op jit(solution)/shard_map/ppermute | solution.py:15
  149.8 7.1 %collective-permute-start.41 = (f32[512,128]{0,1:T(8,128)S(1)}, f32[512,128]{0,1:T(8,128)S(1)}, u32[]{:S(2)}, u32[]{:S(2)}) collective-permute-start(f32[512,128]{0,1:T(8,128)S(1)} %maximum_select_fusion.5), channel_id=1, source_target_pairs={{0,4},{4,0},{8,12},{12,8},{16,20},{20,16},{24,28},{28,24},{1,5},{5... | collective-permute-start | bytes 786440 | tf_op jit(solution)/shard_map/ppermute | solution.py:15
  151.0 12.9 %collective-permute-start.21 = (f32[256,256]{0,1:T(8,128)S(1)}, f32[256,256]{0,1:T(8,128)S(1)}, u32[]{:S(2)}, u32[]{:S(2)}) collective-permute-start(f32[256,256]{0,1:T(8,128)S(1)} %get-tuple-element.11), channel_id=1, source_target_pairs={{1,0},{2,1},{3,2},{5,4},{6,5},{7,6},{9,8},{10,9},{11,10},{13,12},{... | collective-permute-start | bytes 786440 | tf_op jit(solution)/shard_map/ppermute | solution.py:10
  152.3 11.6 %collective-permute-start.18 = (f32[256,256]{0,1:T(8,128)S(1)}, f32[256,256]{0,1:T(8,128)S(1)}, u32[]{:S(2)}, u32[]{:S(2)}) collective-permute-start(f32[256,256]{0,1:T(8,128)S(1)} %get-tuple-element.12), channel_id=1, source_target_pairs={{0,1},{1,2},{2,3},{4,5},{5,6},{6,7},{8,9},{9,10},{10,11},{12,13},{... | collective-permute-start | bytes 786440 | tf_op jit(solution)/shard_map/ppermute | solution.py:10
  158.0 11.9 %collective-permute-start.45 = (f32[256,256]{0,1:T(8,128)S(1)}, f32[256,256]{0,1:T(8,128)S(1)}, u32[]{:S(2)}, u32[]{:S(2)}) collective-permute-start(f32[256,256]{0,1:T(8,128)S(1)} %get-tuple-element.17), channel_id=1, source_target_pairs={{1,0},{2,1},{3,2},{5,4},{6,5},{7,6},{9,8},{10,9},{11,10},{13,12},{... | collective-permute-start | bytes 786440 | tf_op jit(solution)/shard_map/ppermute | solution.py:10
  159.3 10.6 %collective-permute-start.42 = (f32[256,256]{0,1:T(8,128)S(1)}, f32[256,256]{0,1:T(8,128)S(1)}, u32[]{:S(2)}, u32[]{:S(2)}) collective-permute-start(f32[256,256]{0,1:T(8,128)S(1)} %get-tuple-element.18), channel_id=1, source_target_pairs={{0,1},{1,2},{2,3},{4,5},{5,6},{6,7},{8,9},{9,10},{10,11},{12,13},{... | collective-permute-start | bytes 786440 | tf_op jit(solution)/shard_map/ppermute | solution.py:10
  164.0 12.1 %collective-permute-start.22 = (f32[256,256]{0,1:T(8,128)S(1)}, f32[256,256]{0,1:T(8,128)S(1)}, u32[]{:S(2)}, u32[]{:S(2)}) collective-permute-start(f32[256,256]{0,1:T(8,128)S(1)} %get-tuple-element.9), channel_id=1, source_target_pairs={{1,0},{2,1},{3,2},{5,4},{6,5},{7,6},{9,8},{10,9},{11,10},{13,12},{... | collective-permute-start | bytes 786440 | tf_op jit(solution)/shard_map/ppermute | solution.py:10
  165.3 10.8 %collective-permute-start.19 = (f32[256,256]{0,1:T(8,128)S(1)}, f32[256,256]{0,1:T(8,128)S(1)}, u32[]{:S(2)}, u32[]{:S(2)}) collective-permute-start(f32[256,256]{0,1:T(8,128)S(1)} %get-tuple-element.10), channel_id=1, source_target_pairs={{0,1},{1,2},{2,3},{4,5},{5,6},{6,7},{8,9},{9,10},{10,11},{12,13},{... | collective-permute-start | bytes 786440 | tf_op jit(solution)/shard_map/ppermute | solution.py:10
  170.0 11.4 %collective-permute-start.46 = (f32[256,256]{0,1:T(8,128)S(1)}, f32[256,256]{0,1:T(8,128)S(1)}, u32[]{:S(2)}, u32[]{:S(2)}) collective-permute-start(f32[256,256]{0,1:T(8,128)S(1)} %get-tuple-element.15), channel_id=1, source_target_pairs={{1,0},{2,1},{3,2},{5,4},{6,5},{7,6},{9,8},{10,9},{11,10},{13,12},{... | collective-permute-start | bytes 786440 | tf_op jit(solution)/shard_map/ppermute | solution.py:10
  171.3 11.5 %collective-permute-start.43 = (f32[256,256]{0,1:T(8,128)S(1)}, f32[256,256]{0,1:T(8,128)S(1)}, u32[]{:S(2)}, u32[]{:S(2)}) collective-permute-start(f32[256,256]{0,1:T(8,128)S(1)} %get-tuple-element.16), channel_id=1, source_target_pairs={{0,1},{1,2},{2,3},{4,5},{5,6},{6,7},{8,9},{9,10},{10,11},{12,13},{... | collective-permute-start | bytes 786440 | tf_op jit(solution)/shard_map/ppermute | solution.py:10
  176.2 12.4 %collective-permute-start.20 = (f32[256,256]{0,1:T(8,128)S(1)}, f32[256,256]{0,1:T(8,128)S(1)}, u32[]{:S(2)}, u32[]{:S(2)}) collective-permute-start(f32[256,256]{0,1:T(8,128)S(1)} %get-tuple-element.8), channel_id=1, source_target_pairs={{0,1},{1,2},{2,3},{4,5},{5,6},{6,7},{8,9},{9,10},{10,11},{12,13},{... | collective-permute-start | bytes 786440 | tf_op jit(solution)/shard_map/ppermute | solution.py:10
  180.1 8.5 %collective-permute-start.23 = (f32[256,256]{0,1:T(8,128)S(1)}, f32[256,256]{0,1:T(8,128)S(1)}, u32[]{:S(2)}, u32[]{:S(2)}) collective-permute-start(f32[256,256]{0,1:T(8,128)S(1)} %get-tuple-element.7), channel_id=1, source_target_pairs={{1,0},{2,1},{3,2},{5,4},{6,5},{7,6},{9,8},{10,9},{11,10},{13,12},{... | collective-permute-start | bytes 786440 | tf_op jit(solution)/shard_map/ppermute | solution.py:10
  182.9 9.1 %collective-permute-start.44 = (f32[256,256]{0,1:T(8,128)S(1)}, f32[256,256]{0,1:T(8,128)S(1)}, u32[]{:S(2)}, u32[]{:S(2)}) collective-permute-start(f32[256,256]{0,1:T(8,128)S(1)} %get-tuple-element.14), channel_id=1, source_target_pairs={{0,1},{1,2},{2,3},{4,5},{5,6},{6,7},{8,9},{9,10},{10,11},{12,13},{... | collective-permute-start | bytes 786440 | tf_op jit(solution)/shard_map/ppermute | solution.py:10
  187.3 8.3 %collective-permute-start.47 = (f32[256,256]{0,1:T(8,128)S(1)}, f32[256,256]{0,1:T(8,128)S(1)}, u32[]{:S(2)}, u32[]{:S(2)}) collective-permute-start(f32[256,256]{0,1:T(8,128)S(1)} %get-tuple-element.13), channel_id=1, source_target_pairs={{1,0},{2,1},{3,2},{5,4},{6,5},{7,6},{9,8},{10,9},{11,10},{13,12},{... | collective-permute-start | bytes 786440 | tf_op jit(solution)/shard_map/ppermute | solution.py:10
  (21 other events, 172.2 us)

commit v10 on v2

--- a/solution.py
+++ b/solution.py
@@ -127,12 +127,11 @@
 def per_device(three_center, densities, screen_mask, diag_inverse, sub_factor):
     screened = screen_block(three_center, screen_mask)
     transfer = -product(diag_inverse, sub_factor)
-    width = densities.shape[1] // SLICES
+    gamma_partial = gamma_over_aux(screened, densities)
+    width = gamma_partial.shape[1] // SLICES
     results = []
     for part in range(SLICES):
-        dens_part = densities[:, part * width:(part + 1) * width]
-        gamma_partial = gamma_over_aux(screened, dens_part)
-        right_side = reduce_scatter_columns(gamma_partial, "pair")
+        right_side = reduce_scatter_columns(gamma_partial[:, part * width:(part + 1) * width], "pair")
         coefficients = solve(right_side, transfer, diag_inverse, sub_factor)
         coeff_full = all_gather_columns(coefficients, "pair")
         partial = contract_first(screened, coeff_full)

time: 181 us -> 172 us (0.950)
  starting transfers between devices: 106 us -> 86.3 us
  waiting for transfers between devices: 40.6 us -> 57.6 us
  matrix products: 22.7 us -> 19.1 us
  local copies, waits for them, and re-layouts: 6.6 us -> 4.24 us
    ppermute x36 -> x30, starting transfers between devices: 93.6 us -> 74.9 us  [from_behind(): return lax.ppermute(array, axis, pairs)]
    ppermute x36 -> x30, waiting for transfers between devices: 28.8 us -> 43.3 us  [from_behind(): return lax.ppermute(array, axis, pairs)]
    dot_general x33 -> x26, matrix products: 20.7 us -> 17 us  [product(): jnp.dot(left, right, precision=lax.Precision.HIGH, preferred_element_type...]
    ppermute x12, waiting for transfers between devices: 11.8 us -> 14.3 us  [swap(): return lax.ppermute(array, axis, [(i, i ^ bit) for i in range(count)])]
    slice x1 -> x0, local copies, waits for them, and re-layouts: 1.94 us -> none  [per_device(): dens_part = densities[:, part * width:(part + 1) * width]]
  transfers between devices with their start and end apart: 48 -> 42, of which waited for: 21 -> 23; matrix products, arithmetic and copies ran while one was open for 16% -> 14% of each run, Pallas kernels for 0% -> 0%
where the time goes in v10:
time: 172 us; the launch traced here: 171 us
  starting transfers between devices  86.3 us (50%)
  waiting for transfers between devices  57.6 us (33%)
  matrix products  19.1 us (11%)
  local copies, waits for them, and re-layouts  4.24 us (2%)
  other arithmetic  2.82 us (2%)
    ppermute x30, starting transfers between devices, from_behind(): return lax.ppermute(array, axis, pairs)  74.9 us
    ppermute x30, waiting for transfers between devices, from_behind(): return lax.ppermute(array, axis, pairs)  43.3 us
    dot_general x26, matrix products, product(): jnp.dot(left, right, precision=lax.Precision.HIGH, preferred_element_type...  17 us
    ppermute x12, waiting for transfers between devices, swap(): return lax.ppermute(array, axis, [(i, i ^ bit) for i in range(count)])  14.3 us
    ppermute x12, starting transfers between devices, swap(): return lax.ppermute(array, axis, [(i, i ^ bit) for i in range(count)])  11.3 us
  transfers between devices with their start and end apart: 42, of which 23 were waited for; matrix products, arithmetic and copies ran while one was open for 14% of the time, Pallas kernels for 0%

profile of v10, /device:TPU:0, one launch (start us, length us, event | category | flops | bytes accessed | tf_op | source)
XLA Modules:
  0.0 170.7 jit_solution(8107517282460722177)
XLA Ops:
  1.4 6.4 %collective-permute-start = (f32[256,512]{1,0:T(8,128)}, f32[256,512]{1,0:T(8,128)}, u32[]{:S(2)}, u32[]{:S(2)}) collective-permute-start(f32[256,512]{1,0:T(8,128)} %param.6), channel_id=1, source_target_pairs={{0,1},{1,2},{2,3},{4,5},{5,6},{6,7},{8,9},{9,10},{10,11},{12,13},{... | collective-permute-start | bytes 1572872 | tf_op jit(solution)/shard_map/ppermute | solution.py:10
  7.8 2.9 %copy.8 = f32[512,1024]{0,1:T(8,128)} copy(f32[512,1024]{1,0:T(8,128)} %param.5) | data formatting | bytes 4194304 | tf_op args[0]
  10.9 1.8 %bitcast_multiply_fusion = f32[512,1024]{0,1:T(8,128)S(1)} fusion(f32[512,1024]{0,1:T(8,128)} %copy.8, f32[512,16]{0,1:T(8,128)S(1)} %reshape.6), kind=kLoop, calls=%fused_computation | loop fusion | flops 524288 | bytes 4227072 | tf_op jit(solution)/shard_map/mul | solution.py:23
  14.5 2.8 %collective-permute-done.1 = f32[256,512]{1,0:T(8,128)} collective-permute-done((f32[256,512]{1,0:T(8,128)}, f32[256,512]{1,0:T(8,128)}, u32[]{:S(2)}, u32[]{:S(2)}) %collective-permute-start.1) | collective-permute-done | bytes 524320 | tf_op jit(solution)/shard_map/ppermute | solution.py:10
  18.6 4.6 %collective-permute-start.2 = (f32[256,512]{1,0:T(8,128)}, f32[256,512]{1,0:T(8,128)S(1)}, u32[]{:S(2)}, u32[]{:S(2)}) collective-permute-start(f32[256,512]{1,0:T(8,128)} %collective-permute-done), channel_id=1, source_target_pairs={{0,1},{1,2},{2,3},{4,5},{5,6},{6,7},{8,9},{9,10},{10,11},{12,13},{... | collective-permute-start | bytes 1572872 | tf_op jit(solution)/shard_map/ppermute | solution.py:10
  23.2 1.7 convolution_add_fusion.3
  24.9 1.7 convolution_add_fusion.2
  26.5 5.9 %collective-permute-done.3 = f32[256,512]{1,0:T(8,128)S(1)} collective-permute-done((f32[256,512]{1,0:T(8,128)}, f32[256,512]{1,0:T(8,128)S(1)}, u32[]{:S(2)}, u32[]{:S(2)}) %collective-permute-start.3) | collective-permute-done | bytes 524320 | tf_op jit(solution)/shard_map/ppermute | solution.py:10
  33.8 4.6 %collective-permute-start.4 = (f32[256,512]{1,0:T(8,128)S(1)}, f32[256,512]{1,0:T(8,128)S(1)}, u32[]{:S(2)}, u32[]{:S(2)}) collective-permute-start(f32[256,512]{1,0:T(8,128)S(1)} %collective-permute-done.2), channel_id=1, source_target_pairs={{0,1},{1,2},{2,3},{4,5},{5,6},{6,7},{8,9},{9,10},{10,11},{12,13},{... | collective-permute-start | bytes 1572872 | tf_op jit(solution)/shard_map/ppermute | solution.py:10
  39.6 6.9 %collective-permute-done.5 = f32[256,512]{1,0:T(8,128)S(1)} collective-permute-done((f32[256,512]{1,0:T(8,128)S(1)}, f32[256,512]{1,0:T(8,128)S(1)}, u32[]{:S(2)}, u32[]{:S(2)}) %collective-permute-start.5) | collective-permute-done | bytes 524320 | tf_op jit(solution)/shard_map/ppermute | solution.py:10
  52.8 4.2 %collective-permute-done.7 = f32[512,64]{0,1:T(8,128)S(1)} collective-permute-done((f32[512,64]{0,1:T(8,128)S(1)}, f32[512,64]{0,1:T(8,128)S(1)}, u32[]{:S(2)}, u32[]{:S(2)}) %collective-permute-start.7) | collective-permute-done | bytes 131104 | tf_op jit(solution)/shard_map/ppermute | solution.py:15
  62.5 4.4 %collective-permute-start.9 = (f32[512,32]{0,1:T(8,128)S(1)}, f32[512,32]{0,1:T(8,128)S(1)}, u32[]{:S(2)}, u32[]{:S(2)}) collective-permute-start(f32[512,32]{0,1:T(8,128)S(1)} %convolution_bitcast_fusion.5), channel_id=1, source_target_pairs={{0,1},{1,2},{2,3},{4,5},{5,6},{6,7},{8,9},{9,10},{10,11},{12,13},{... | collective-permute-start | bytes 196616 | tf_op jit(solution)/shard_map/ppermute | solution.py:10
  67.4 3.0 %collective-permute-start.27 = (f32[512,32]{0,1:T(8,128)S(1)}, f32[512,32]{0,1:T(8,128)S(1)}, u32[]{:S(2)}, u32[]{:S(2)}) collective-permute-start(f32[512,32]{0,1:T(8,128)S(1)} %convolution_bitcast_fusion.2), channel_id=1, source_target_pairs={{0,1},{1,2},{2,3},{4,5},{5,6},{6,7},{8,9},{9,10},{10,11},{12,13},{... | collective-permute-start | bytes 196616 | tf_op jit(solution)/shard_map/ppermute | solution.py:10
  71.0 3.6 %collective-permute-start.10 = (f32[512,32]{0,1:T(8,128)S(1)}, f32[512,32]{0,1:T(8,128)S(1)}, u32[]{:S(2)}, u32[]{:S(2)}) collective-permute-start(f32[512,32]{0,1:T(8,128)S(1)} %convolution_add_fusion.13), channel_id=1, source_target_pairs={{0,1},{1,2},{2,3},{4,5},{5,6},{6,7},{8,9},{9,10},{10,11},{12,13},{... | collective-permute-start | bytes 196616 | tf_op jit(solution)/shard_map/ppermute | solution.py:10
  75.2 2.2 %collective-permute-start.28 = (f32[512,32]{0,1:T(8,128)S(1)}, f32[512,32]{0,1:T(8,128)S(1)}, u32[]{:S(2)}, u32[]{:S(2)}) collective-permute-start(f32[512,32]{0,1:T(8,128)S(1)} %convolution_add_fusion.8), channel_id=1, source_target_pairs={{0,1},{1,2},{2,3},{4,5},{5,6},{6,7},{8,9},{9,10},{10,11},{12,13},{... | collective-permute-start | bytes 196616 | tf_op jit(solution)/shard_map/ppermute | solution.py:10
  78.0 3.5 %collective-permute-start.11 = (f32[512,32]{0,1:T(8,128)S(1)}, f32[512,32]{0,1:T(8,128)S(1)}, u32[]{:S(2)}, u32[]{:S(2)}) collective-permute-start(f32[512,32]{0,1:T(8,128)S(1)} %convolution_add_fusion.12), channel_id=1, source_target_pairs={{0,1},{1,2},{2,3},{4,5},{5,6},{6,7},{8,9},{9,10},{10,11},{12,13},{... | collective-permute-start | bytes 196616 | tf_op jit(solution)/shard_map/ppermute | solution.py:10
  82.1 2.5 %collective-permute-start.29 = (f32[512,32]{0,1:T(8,128)S(1)}, f32[512,32]{0,1:T(8,128)S(1)}, u32[]{:S(2)}, u32[]{:S(2)}) collective-permute-start(f32[512,32]{0,1:T(8,128)S(1)} %convolution_add_fusion.7), channel_id=1, source_target_pairs={{0,1},{1,2},{2,3},{4,5},{5,6},{6,7},{8,9},{9,10},{10,11},{12,13},{... | collective-permute-start | bytes 196616 | tf_op jit(solution)/shard_map/ppermute | solution.py:10
  88.3 4.3 %collective-permute-done.12 = f32[512,32]{0,1:T(8,128)S(1)} collective-permute-done((f32[512,32]{0,1:T(8,128)S(1)}, f32[512,32]{0,1:T(8,128)S(1)}, u32[]{:S(2)}, u32[]{:S(2)}) %collective-permute-start.12) | collective-permute-done | bytes 65568 | tf_op jit(solution)/shard_map/ppermute | solution.py:10
  96.0 3.2 %collective-permute-done.13 = f32[512,32]{0,1:T(8,128)S(1)} collective-permute-done((f32[512,32]{0,1:T(8,128)S(1)}, f32[512,32]{0,1:T(8,128)S(1)}, u32[]{:S(2)}, u32[]{:S(2)}) %collective-permute-start.13) | collective-permute-done | bytes 65568 | tf_op jit(solution)/shard_map/ppermute | solution.py:10
  103.2 3.0 %collective-permute-done.14 = f32[512,32]{0,1:T(8,128)S(1)} collective-permute-done((f32[512,32]{0,1:T(8,128)S(1)}, f32[512,32]{0,1:T(8,128)S(1)}, u32[]{:S(2)}, u32[]{:S(2)}) %collective-permute-start.14) | collective-permute-done | bytes 65568 | tf_op jit(solution)/shard_map/ppermute | solution.py:10
  112.5 2.3 %collective-permute-done.32 = f32[512,32]{0,1:T(8,128)S(1)} collective-permute-done((f32[512,32]{0,1:T(8,128)S(1)}, f32[512,32]{0,1:T(8,128)S(1)}, u32[]{:S(2)}, u32[]{:S(2)}) %collective-permute-start.32) | collective-permute-done | bytes 65568 | tf_op jit(solution)/shard_map/ppermute | solution.py:10
  116.8 2.7 %collective-permute-done.33 = f32[512,32]{0,1:T(8,128)S(1)} collective-permute-done((f32[512,32]{0,1:T(8,128)S(1)}, f32[512,32]{0,1:T(8,128)S(1)}, u32[]{:S(2)}, u32[]{:S(2)}) %collective-permute-start.33) | collective-permute-done | bytes 65568 | tf_op jit(solution)/shard_map/ppermute | solution.py:15
  121.1 3.5 %collective-permute-done.34 = f32[512,64]{0,1:T(8,128)S(1)} collective-permute-done((f32[512,64]{0,1:T(8,128)S(1)}, f32[512,64]{0,1:T(8,128)S(1)}, u32[]{:S(2)}, u32[]{:S(2)}) %collective-permute-start.34) | collective-permute-done | bytes 131104 | tf_op jit(solution)/shard_map/ppermute | solution.py:15
  125.8 3.9 %collective-permute-start.18 = (f32[256,256]{0,1:T(8,128)S(1)}, f32[256,256]{0,1:T(8,128)S(1)}, u32[]{:S(2)}, u32[]{:S(2)}) collective-permute-start(f32[256,256]{0,1:T(8,128)S(1)} %get-tuple-element.10), channel_id=1, source_target_pairs={{0,1},{1,2},{2,3},{4,5},{5,6},{6,7},{8,9},{9,10},{10,11},{12,13},{... | collective-permute-start | bytes 786440 | tf_op jit(solution)/shard_map/ppermute | solution.py:10
  132.0 4.6 %collective-permute-start.36 = (f32[256,256]{0,1:T(8,128)S(1)}, f32[256,256]{0,1:T(8,128)S(1)}, u32[]{:S(2)}, u32[]{:S(2)}) collective-permute-start(f32[256,256]{0,1:T(8,128)S(1)} %get-tuple-element.20), channel_id=1, source_target_pairs={{0,1},{1,2},{2,3},{4,5},{5,6},{6,7},{8,9},{9,10},{10,11},{12,13},{... | collective-permute-start | bytes 786440 | tf_op jit(solution)/shard_map/ppermute | solution.py:10
  137.9 2.0 %collective-permute-done.21 = f32[256,256]{0,1:T(8,128)S(1)} collective-permute-done((f32[256,256]{0,1:T(8,128)S(1)}, f32[256,256]{0,1:T(8,128)S(1)}, u32[]{:S(2)}, u32[]{:S(2)}) %collective-permute-start.21) | collective-permute-done | bytes 262176 | tf_op jit(solution)/shard_map/ppermute | solution.py:10
  140.0 2.8 %collective-permute-start.19 = (f32[256,256]{0,1:T(8,128)S(1)}, f32[256,256]{0,1:T(8,128)S(1)}, u32[]{:S(2)}, u32[]{:S(2)}) collective-permute-start(f32[256,256]{0,1:T(8,128)S(1)} %get-tuple-element.8), channel_id=1, source_target_pairs={{0,1},{1,2},{2,3},{4,5},{5,6},{6,7},{8,9},{9,10},{10,11},{12,13},{... | collective-permute-start | bytes 786440 | tf_op jit(solution)/shard_map/ppermute | solution.py:10
  144.1 2.2 %collective-permute-done.39 = f32[256,256]{0,1:T(8,128)S(1)} collective-permute-done((f32[256,256]{0,1:T(8,128)S(1)}, f32[256,256]{0,1:T(8,128)S(1)}, u32[]{:S(2)}, u32[]{:S(2)}) %collective-permute-start.39) | collective-permute-done | bytes 262176 | tf_op jit(solution)/shard_map/ppermute | solution.py:10
  146.5 2.9 %collective-permute-start.37 = (f32[256,256]{0,1:T(8,128)S(1)}, f32[256,256]{0,1:T(8,128)S(1)}, u32[]{:S(2)}, u32[]{:S(2)}) collective-permute-start(f32[256,256]{0,1:T(8,128)S(1)} %get-tuple-element.18), channel_id=1, source_target_pairs={{0,1},{1,2},{2,3},{4,5},{5,6},{6,7},{8,9},{9,10},{10,11},{12,13},{... | collective-permute-start | bytes 786440 | tf_op jit(solution)/shard_map/ppermute | solution.py:10
  152.1 3.2 %collective-permute-start.20 = (f32[256,256]{0,1:T(8,128)S(1)}, f32[256,256]{0,1:T(8,128)S(1)}, u32[]{:S(2)}, u32[]{:S(2)}) collective-permute-start(f32[256,256]{0,1:T(8,128)S(1)} %get-tuple-element.6), channel_id=1, source_target_pairs={{0,1},{1,2},{2,3},{4,5},{5,6},{6,7},{8,9},{9,10},{10,11},{12,13},{... | collective-permute-start | bytes 786440 | tf_op jit(solution)/shard_map/ppermute | solution.py:10
  158.0 3.3 %collective-permute-start.38 = (f32[256,256]{0,1:T(8,128)S(1)}, f32[256,256]{0,1:T(8,128)S(1)}, u32[]{:S(2)}, u32[]{:S(2)}) collective-permute-start(f32[256,256]{0,1:T(8,128)S(1)} %get-tuple-element.16), channel_id=1, source_target_pairs={{0,1},{1,2},{2,3},{4,5},{5,6},{6,7},{8,9},{9,10},{10,11},{12,13},{... | collective-permute-start | bytes 786440 | tf_op jit(solution)/shard_map/ppermute | solution.py:10
  165.2 4.4 %collective-permute-done.41 = f32[256,256]{0,1:T(8,128)S(1)} collective-permute-done((f32[256,256]{0,1:T(8,128)S(1)}, f32[256,256]{0,1:T(8,128)S(1)}, u32[]{:S(2)}, u32[]{:S(2)}) %collective-permute-start.41) | collective-permute-done | bytes 262176 | tf_op jit(solution)/shard_map/ppermute | solution.py:10
  (114 shorter events, 59.2 us)
Async XLA Ops:
  0.0 17.3 %collective-permute-start.1 = (f32[256,512]{1,0:T(8,128)}, f32[256,512]{1,0:T(8,128)}, u32[]{:S(2)}, u32[]{:S(2)}) collective-permute-start(f32[256,512]{1,0:T(8,128)} %param.6), channel_id=1, source_target_pairs={{1,0},{2,1},{3,2},{5,4},{6,5},{7,6},{9,8},{10,9},{11,10},{13,12},{... | collective-permute-start | bytes 1572872 | tf_op jit(solution)/shard_map/ppermute | solution.py:10
  1.4 17.2 %collective-permute-start = (f32[256,512]{1,0:T(8,128)}, f32[256,512]{1,0:T(8,128)}, u32[]{:S(2)}, u32[]{:S(2)}) collective-permute-start(f32[256,512]{1,0:T(8,128)} %param.6), channel_id=1, source_target_pairs={{0,1},{1,2},{2,3},{4,5},{5,6},{6,7},{8,9},{9,10},{10,11},{12,13},{... | collective-permute-start | bytes 1572872 | tf_op jit(solution)/shard_map/ppermute | solution.py:10
  17.3 15.2 %collective-permute-start.3 = (f32[256,512]{1,0:T(8,128)}, f32[256,512]{1,0:T(8,128)S(1)}, u32[]{:S(2)}, u32[]{:S(2)}) collective-permute-start(f32[256,512]{1,0:T(8,128)} %collective-permute-done.1), channel_id=1, source_target_pairs={{1,0},{2,1},{3,2},{5,4},{6,5},{7,6},{9,8},{10,9},{11,10},{13,12},{... | collective-permute-start | bytes 1572872 | tf_op jit(solution)/shard_map/ppermute | solution.py:10
  18.6 15.2 %collective-permute-start.2 = (f32[256,512]{1,0:T(8,128)}, f32[256,512]{1,0:T(8,128)S(1)}, u32[]{:S(2)}, u32[]{:S(2)}) collective-permute-start(f32[256,512]{1,0:T(8,128)} %collective-permute-done), channel_id=1, source_target_pairs={{0,1},{1,2},{2,3},{4,5},{5,6},{6,7},{8,9},{9,10},{10,11},{12,13},{... | collective-permute-start | bytes 1572872 | tf_op jit(solution)/shard_map/ppermute | solution.py:10
  32.5 14.1 %collective-permute-start.5 = (f32[256,512]{1,0:T(8,128)S(1)}, f32[256,512]{1,0:T(8,128)S(1)}, u32[]{:S(2)}, u32[]{:S(2)}) collective-permute-start(f32[256,512]{1,0:T(8,128)S(1)} %collective-permute-done.3), channel_id=1, source_target_pairs={{1,0},{2,1},{3,2},{5,4},{6,5},{7,6},{9,8},{10,9},{11,10},{13,12},{... | collective-permute-start | bytes 1572872 | tf_op jit(solution)/shard_map/ppermute | solution.py:10
  33.8 14.0 %collective-permute-start.4 = (f32[256,512]{1,0:T(8,128)S(1)}, f32[256,512]{1,0:T(8,128)S(1)}, u32[]{:S(2)}, u32[]{:S(2)}) collective-permute-start(f32[256,512]{1,0:T(8,128)S(1)} %collective-permute-done.2), channel_id=1, source_target_pairs={{0,1},{1,2},{2,3},{4,5},{5,6},{6,7},{8,9},{9,10},{10,11},{12,13},{... | collective-permute-start | bytes 1572872 | tf_op jit(solution)/shard_map/ppermute | solution.py:10
  50.6 6.4 %collective-permute-start.7 = (f32[512,64]{0,1:T(8,128)S(1)}, f32[512,64]{0,1:T(8,128)S(1)}, u32[]{:S(2)}, u32[]{:S(2)}) collective-permute-start(f32[512,64]{0,1:T(8,128)S(1)} %slice_select_fusion.3), channel_id=1, source_target_pairs={{0,8},{4,12},{8,0},{12,4},{16,24},{20,28},{24,16},{28,20},{1,9},{5... | collective-permute-start | bytes 393224 | tf_op jit(solution)/shard_map/ppermute | solution.py:15
  51.7 7.3 %collective-permute-start.25 = (f32[512,64]{0,1:T(8,128)S(1)}, f32[512,64]{0,1:T(8,128)S(1)}, u32[]{:S(2)}, u32[]{:S(2)}) collective-permute-start(f32[512,64]{0,1:T(8,128)S(1)} %slice_select_fusion.2), channel_id=1, source_target_pairs={{0,8},{4,12},{8,0},{12,4},{16,24},{20,28},{24,16},{28,20},{1,9},{5... | collective-permute-start | bytes 393224 | tf_op jit(solution)/shard_map/ppermute | solution.py:15
  59.1 7.7 %collective-permute-start.26 = (f32[512,32]{0,1:T(8,128)S(1)}, f32[512,32]{0,1:T(8,128)S(1)}, u32[]{:S(2)}, u32[]{:S(2)}) collective-permute-start(f32[512,32]{0,1:T(8,128)S(1)} %slice_select_fusion.4), channel_id=1, source_target_pairs={{0,16},{4,20},{8,24},{12,28},{16,0},{20,4},{24,8},{28,12},{1,17},{... | collective-permute-start | bytes 196616 | tf_op jit(solution)/shard_map/ppermute | solution.py:15
  62.5 8.0 %collective-permute-start.9 = (f32[512,32]{0,1:T(8,128)S(1)}, f32[512,32]{0,1:T(8,128)S(1)}, u32[]{:S(2)}, u32[]{:S(2)}) collective-permute-start(f32[512,32]{0,1:T(8,128)S(1)} %convolution_bitcast_fusion.5), channel_id=1, source_target_pairs={{0,1},{1,2},{2,3},{4,5},{5,6},{6,7},{8,9},{9,10},{10,11},{12,13},{... | collective-permute-start | bytes 196616 | tf_op jit(solution)/shard_map/ppermute | solution.py:10
  67.4 7.2 %collective-permute-start.27 = (f32[512,32]{0,1:T(8,128)S(1)}, f32[512,32]{0,1:T(8,128)S(1)}, u32[]{:S(2)}, u32[]{:S(2)}) collective-permute-start(f32[512,32]{0,1:T(8,128)S(1)} %convolution_bitcast_fusion.2), channel_id=1, source_target_pairs={{0,1},{1,2},{2,3},{4,5},{5,6},{6,7},{8,9},{9,10},{10,11},{12,13},{... | collective-permute-start | bytes 196616 | tf_op jit(solution)/shard_map/ppermute | solution.py:10
  71.0 6.4 %collective-permute-start.10 = (f32[512,32]{0,1:T(8,128)S(1)}, f32[512,32]{0,1:T(8,128)S(1)}, u32[]{:S(2)}, u32[]{:S(2)}) collective-permute-start(f32[512,32]{0,1:T(8,128)S(1)} %convolution_add_fusion.13), channel_id=1, source_target_pairs={{0,1},{1,2},{2,3},{4,5},{5,6},{6,7},{8,9},{9,10},{10,11},{12,13},{... | collective-permute-start | bytes 196616 | tf_op jit(solution)/shard_map/ppermute | solution.py:10
  75.2 6.2 %collective-permute-start.28 = (f32[512,32]{0,1:T(8,128)S(1)}, f32[512,32]{0,1:T(8,128)S(1)}, u32[]{:S(2)}, u32[]{:S(2)}) collective-permute-start(f32[512,32]{0,1:T(8,128)S(1)} %convolution_add_fusion.8), channel_id=1, source_target_pairs={{0,1},{1,2},{2,3},{4,5},{5,6},{6,7},{8,9},{9,10},{10,11},{12,13},{... | collective-permute-start | bytes 196616 | tf_op jit(solution)/shard_map/ppermute | solution.py:10
  78.0 6.5 %collective-permute-start.11 = (f32[512,32]{0,1:T(8,128)S(1)}, f32[512,32]{0,1:T(8,128)S(1)}, u32[]{:S(2)}, u32[]{:S(2)}) collective-permute-start(f32[512,32]{0,1:T(8,128)S(1)} %convolution_add_fusion.12), channel_id=1, source_target_pairs={{0,1},{1,2},{2,3},{4,5},{5,6},{6,7},{8,9},{9,10},{10,11},{12,13},{... | collective-permute-start | bytes 196616 | tf_op jit(solution)/shard_map/ppermute | solution.py:10
  85.9 6.7 %collective-permute-start.12 = (f32[512,32]{0,1:T(8,128)S(1)}, f32[512,32]{0,1:T(8,128)S(1)}, u32[]{:S(2)}, u32[]{:S(2)}) collective-permute-start(f32[512,32]{0,1:T(8,128)S(1)} %convolution_bitcast_fusion.4), channel_id=1, source_target_pairs={{1,0},{2,1},{3,2},{5,4},{6,5},{7,6},{9,8},{10,9},{11,10},{13,12},{... | collective-permute-start | bytes 196616 | tf_op jit(solution)/shard_map/ppermute | solution.py:10
  94.7 6.8 %collective-permute-start.30 = (f32[512,32]{0,1:T(8,128)S(1)}, f32[512,32]{0,1:T(8,128)S(1)}, u32[]{:S(2)}, u32[]{:S(2)}) collective-permute-start(f32[512,32]{0,1:T(8,128)S(1)} %convolution_bitcast_fusion.1), channel_id=1, source_target_pairs={{1,0},{2,1},{3,2},{5,4},{6,5},{7,6},{9,8},{10,9},{11,10},{13,12},{... | collective-permute-start | bytes 196616 | tf_op jit(solution)/shard_map/ppermute | solution.py:10
  99.6 6.6 %collective-permute-start.14 = (f32[512,32]{0,1:T(8,128)S(1)}, f32[512,32]{0,1:T(8,128)S(1)}, u32[]{:S(2)}, u32[]{:S(2)}) collective-permute-start(f32[512,32]{0,1:T(8,128)S(1)} %convolution_add_fusion.9), channel_id=1, source_target_pairs={{1,0},{2,1},{3,2},{5,4},{6,5},{7,6},{9,8},{10,9},{11,10},{13,12},{... | collective-permute-start | bytes 196616 | tf_op jit(solution)/shard_map/ppermute | solution.py:10
  101.9 6.3 %collective-permute-start.31 = (f32[512,32]{0,1:T(8,128)S(1)}, f32[512,32]{0,1:T(8,128)S(1)}, u32[]{:S(2)}, u32[]{:S(2)}) collective-permute-start(f32[512,32]{0,1:T(8,128)S(1)} %convolution_add_fusion.5), channel_id=1, source_target_pairs={{1,0},{2,1},{3,2},{5,4},{6,5},{7,6},{9,8},{10,9},{11,10},{13,12},{... | collective-permute-start | bytes 196616 | tf_op jit(solution)/shard_map/ppermute | solution.py:10
  116.7 7.9 %collective-permute-start.17 = (f32[512,128]{0,1:T(8,128)S(1)}, f32[512,128]{0,1:T(8,128)S(1)}, u32[]{:S(2)}, u32[]{:S(2)}) collective-permute-start(f32[512,128]{0,1:T(8,128)S(1)} %maximum_select_fusion.4), channel_id=1, source_target_pairs={{0,4},{4,0},{8,12},{12,8},{16,20},{20,16},{24,28},{28,24},{1,5},{5... | collective-permute-start | bytes 786440 | tf_op jit(solution)/shard_map/ppermute | solution.py:15
  124.6 6.4 %collective-permute-start.35 = (f32[512,128]{0,1:T(8,128)S(1)}, f32[512,128]{0,1:T(8,128)S(1)}, u32[]{:S(2)}, u32[]{:S(2)}) collective-permute-start(f32[512,128]{0,1:T(8,128)S(1)} %maximum_select_fusion.5), channel_id=1, source_target_pairs={{0,4},{4,0},{8,12},{12,8},{16,20},{20,16},{24,28},{28,24},{1,5},{5... | collective-permute-start | bytes 786440 | tf_op jit(solution)/shard_map/ppermute | solution.py:15
  125.8 12.1 %collective-permute-start.18 = (f32[256,256]{0,1:T(8,128)S(1)}, f32[256,256]{0,1:T(8,128)S(1)}, u32[]{:S(2)}, u32[]{:S(2)}) collective-permute-start(f32[256,256]{0,1:T(8,128)S(1)} %get-tuple-element.10), channel_id=1, source_target_pairs={{0,1},{1,2},{2,3},{4,5},{5,6},{6,7},{8,9},{9,10},{10,11},{12,13},{... | collective-permute-start | bytes 786440 | tf_op jit(solution)/shard_map/ppermute | solution.py:10
  129.6 10.3 %collective-permute-start.21 = (f32[256,256]{0,1:T(8,128)S(1)}, f32[256,256]{0,1:T(8,128)S(1)}, u32[]{:S(2)}, u32[]{:S(2)}) collective-permute-start(f32[256,256]{0,1:T(8,128)S(1)} %get-tuple-element.9), channel_id=1, source_target_pairs={{1,0},{2,1},{3,2},{5,4},{6,5},{7,6},{9,8},{10,9},{11,10},{13,12},{... | collective-permute-start | bytes 786440 | tf_op jit(solution)/shard_map/ppermute | solution.py:10
  132.0 12.1 %collective-permute-start.36 = (f32[256,256]{0,1:T(8,128)S(1)}, f32[256,256]{0,1:T(8,128)S(1)}, u32[]{:S(2)}, u32[]{:S(2)}) collective-permute-start(f32[256,256]{0,1:T(8,128)S(1)} %get-tuple-element.20), channel_id=1, source_target_pairs={{0,1},{1,2},{2,3},{4,5},{5,6},{6,7},{8,9},{9,10},{10,11},{12,13},{... | collective-permute-start | bytes 786440 | tf_op jit(solution)/shard_map/ppermute | solution.py:10
  136.6 9.8 %collective-permute-start.39 = (f32[256,256]{0,1:T(8,128)S(1)}, f32[256,256]{0,1:T(8,128)S(1)}, u32[]{:S(2)}, u32[]{:S(2)}) collective-permute-start(f32[256,256]{0,1:T(8,128)S(1)} %get-tuple-element.19), channel_id=1, source_target_pairs={{1,0},{2,1},{3,2},{5,4},{6,5},{7,6},{9,8},{10,9},{11,10},{13,12},{... | collective-permute-start | bytes 786440 | tf_op jit(solution)/shard_map/ppermute | solution.py:10
  140.0 10.6 %collective-permute-start.19 = (f32[256,256]{0,1:T(8,128)S(1)}, f32[256,256]{0,1:T(8,128)S(1)}, u32[]{:S(2)}, u32[]{:S(2)}) collective-permute-start(f32[256,256]{0,1:T(8,128)S(1)} %get-tuple-element.8), channel_id=1, source_target_pairs={{0,1},{1,2},{2,3},{4,5},{5,6},{6,7},{8,9},{9,10},{10,11},{12,13},{... | collective-permute-start | bytes 786440 | tf_op jit(solution)/shard_map/ppermute | solution.py:10
  142.8 9.2 %collective-permute-start.22 = (f32[256,256]{0,1:T(8,128)S(1)}, f32[256,256]{0,1:T(8,128)S(1)}, u32[]{:S(2)}, u32[]{:S(2)}) collective-permute-start(f32[256,256]{0,1:T(8,128)S(1)} %get-tuple-element.7), channel_id=1, source_target_pairs={{1,0},{2,1},{3,2},{5,4},{6,5},{7,6},{9,8},{10,9},{11,10},{13,12},{... | collective-permute-start | bytes 786440 | tf_op jit(solution)/shard_map/ppermute | solution.py:10
  146.5 10.2 %collective-permute-start.37 = (f32[256,256]{0,1:T(8,128)S(1)}, f32[256,256]{0,1:T(8,128)S(1)}, u32[]{:S(2)}, u32[]{:S(2)}) collective-permute-start(f32[256,256]{0,1:T(8,128)S(1)} %get-tuple-element.18), channel_id=1, source_target_pairs={{0,1},{1,2},{2,3},{4,5},{5,6},{6,7},{8,9},{9,10},{10,11},{12,13},{... | collective-permute-start | bytes 786440 | tf_op jit(solution)/shard_map/ppermute | solution.py:10
  149.3 8.6 %collective-permute-start.40 = (f32[256,256]{0,1:T(8,128)S(1)}, f32[256,256]{0,1:T(8,128)S(1)}, u32[]{:S(2)}, u32[]{:S(2)}) collective-permute-start(f32[256,256]{0,1:T(8,128)S(1)} %get-tuple-element.17), channel_id=1, source_target_pairs={{1,0},{2,1},{3,2},{5,4},{6,5},{7,6},{9,8},{10,9},{11,10},{13,12},{... | collective-permute-start | bytes 786440 | tf_op jit(solution)/shard_map/ppermute | solution.py:10
  152.1 10.5 %collective-permute-start.20 = (f32[256,256]{0,1:T(8,128)S(1)}, f32[256,256]{0,1:T(8,128)S(1)}, u32[]{:S(2)}, u32[]{:S(2)}) collective-permute-start(f32[256,256]{0,1:T(8,128)S(1)} %get-tuple-element.6), channel_id=1, source_target_pairs={{0,1},{1,2},{2,3},{4,5},{5,6},{6,7},{8,9},{9,10},{10,11},{12,13},{... | collective-permute-start | bytes 786440 | tf_op jit(solution)/shard_map/ppermute | solution.py:10
  155.4 8.7 %collective-permute-start.23 = (f32[256,256]{0,1:T(8,128)S(1)}, f32[256,256]{0,1:T(8,128)S(1)}, u32[]{:S(2)}, u32[]{:S(2)}) collective-permute-start(f32[256,256]{0,1:T(8,128)S(1)} %get-tuple-element.5), channel_id=1, source_target_pairs={{1,0},{2,1},{3,2},{5,4},{6,5},{7,6},{9,8},{10,9},{11,10},{13,12},{... | collective-permute-start | bytes 786440 | tf_op jit(solution)/shard_map/ppermute | solution.py:10
  158.0 7.2 %collective-permute-start.38 = (f32[256,256]{0,1:T(8,128)S(1)}, f32[256,256]{0,1:T(8,128)S(1)}, u32[]{:S(2)}, u32[]{:S(2)}) collective-permute-start(f32[256,256]{0,1:T(8,128)S(1)} %get-tuple-element.16), channel_id=1, source_target_pairs={{0,1},{1,2},{2,3},{4,5},{5,6},{6,7},{8,9},{9,10},{10,11},{12,13},{... | collective-permute-start | bytes 786440 | tf_op jit(solution)/shard_map/ppermute | solution.py:10
  161.4 8.3 %collective-permute-start.41 = (f32[256,256]{0,1:T(8,128)S(1)}, f32[256,256]{0,1:T(8,128)S(1)}, u32[]{:S(2)}, u32[]{:S(2)}) collective-permute-start(f32[256,256]{0,1:T(8,128)S(1)} %get-tuple-element.15), channel_id=1, source_target_pairs={{1,0},{2,1},{3,2},{5,4},{6,5},{7,6},{9,8},{10,9},{11,10},{13,12},{... | collective-permute-start | bytes 786440 | tf_op jit(solution)/shard_map/ppermute | solution.py:10
  (13 other events, 99.2 us)

commit v11 on v10

--- a/solution.py
+++ b/solution.py
@@ -121,7 +121,7 @@
     return product(diag_inverse.T, solved - arriving)
 
 
-SLICES = 2
+SLICES = 4
 
 
 def per_device(three_center, densities, screen_mask, diag_inverse, sub_factor):

time: 172 us -> 227 us (1.32)
  starting transfers between devices: 86.3 us -> 153 us
  waiting for transfers between devices: 57.6 us -> 33.3 us
  matrix products: 19.1 us -> 29.3 us
    ppermute x30 -> x54, starting transfers between devices: 74.9 us -> 134 us  [from_behind(): return lax.ppermute(array, axis, pairs)]
    ppermute x30 -> x54, waiting for transfers between devices: 43.3 us -> 28.3 us  [from_behind(): return lax.ppermute(array, axis, pairs)]
    ppermute x12 -> x24, waiting for transfers between devices: 14.3 us -> 4.98 us  [swap(): return lax.ppermute(array, axis, [(i, i ^ bit) for i in range(count)])]
    dot_general x26 -> x44, matrix products: 17 us -> 24.7 us  [product(): jnp.dot(left, right, precision=lax.Precision.HIGH, preferred_element_type...]
    ppermute x12 -> x24, starting transfers between devices: 11.3 us -> 18.7 us  [swap(): return lax.ppermute(array, axis, [(i, i ^ bit) for i in range(count)])]
    dot_general x2 -> x4, matrix products: 2.08 us -> 4.65 us  [contract_first(): lax.dot_general(left, right, (((0,), (0,)), ((), ())), precision=lax.Prec...]
  transfers between devices with their start and end apart: 42 -> 78, of which waited for: 23 -> 24; matrix products, arithmetic and copies ran while one was open for 14% -> 15% of each run, Pallas kernels for 0% -> 0%
where the time goes in v11:
time: 227 us; the launch traced here: 225 us
  starting transfers between devices  153 us (67%)
  waiting for transfers between devices  33.3 us (15%)
  matrix products  29.3 us (13%)
  other arithmetic  4.52 us (2%)
  local copies, waits for them, and re-layouts  4.28 us (2%)
    ppermute x54, starting transfers between devices, from_behind(): return lax.ppermute(array, axis, pairs)  134 us
    ppermute x54, waiting for transfers between devices, from_behind(): return lax.ppermute(array, axis, pairs)  28.3 us
    dot_general x44, matrix products, product(): jnp.dot(left, right, precision=lax.Precision.HIGH, preferred_element_type...  24.7 us
    ppermute x24, starting transfers between devices, swap(): return lax.ppermute(array, axis, [(i, i ^ bit) for i in range(count)])  18.7 us
    ppermute x24, waiting for transfers between devices, swap(): return lax.ppermute(array, axis, [(i, i ^ bit) for i in range(count)])  4.98 us
    dot_general x4, matrix products, contract_first(): lax.dot_general(left, right, (((0,), (0,)), ((), ())), precision=lax.Prec...  4.65 us
  transfers between devices with their start and end apart: 78, of which 24 were waited for; matrix products, arithmetic and copies ran while one was open for 15% of the time, Pallas kernels for 0%

profile of v11, /device:TPU:0, one launch (start us, length us, event | category | flops | bytes accessed | tf_op | source)
XLA Modules:
  0.0 225.2 jit_solution(18279748278688189367)
XLA Ops:
  1.4 6.4 %collective-permute-start = (f32[256,512]{1,0:T(8,128)}, f32[256,512]{1,0:T(8,128)}, u32[]{:S(2)}, u32[]{:S(2)}) collective-permute-start(f32[256,512]{1,0:T(8,128)} %param.6), channel_id=1, source_target_pairs={{0,1},{1,2},{2,3},{4,5},{5,6},{6,7},{8,9},{9,10},{10,11},{12,13},{... | collective-permute-start | bytes 1572872 | tf_op jit(solution)/shard_map/ppermute | solution.py:10
  7.8 2.9 %copy.8 = f32[512,1024]{0,1:T(8,128)} copy(f32[512,1024]{1,0:T(8,128)} %param.5) | data formatting | bytes 4194304 | tf_op args[0]
  12.8 2.1 fusion.10
  14.9 2.4 %collective-permute-done.1 = f32[256,512]{1,0:T(8,128)} collective-permute-done((f32[256,512]{1,0:T(8,128)}, f32[256,512]{1,0:T(8,128)}, u32[]{:S(2)}, u32[]{:S(2)}) %collective-permute-start.1) | collective-permute-done | bytes 524320 | tf_op jit(solution)/shard_map/ppermute | solution.py:10
  18.6 4.6 %collective-permute-start.2 = (f32[256,512]{1,0:T(8,128)}, f32[256,512]{1,0:T(8,128)S(1)}, u32[]{:S(2)}, u32[]{:S(2)}) collective-permute-start(f32[256,512]{1,0:T(8,128)} %collective-permute-done), channel_id=1, source_target_pairs={{0,1},{1,2},{2,3},{4,5},{5,6},{6,7},{8,9},{9,10},{10,11},{12,13},{... | collective-permute-start | bytes 1572872 | tf_op jit(solution)/shard_map/ppermute | solution.py:10
  26.5 5.9 %collective-permute-done.3 = f32[256,512]{1,0:T(8,128)S(1)} collective-permute-done((f32[256,512]{1,0:T(8,128)}, f32[256,512]{1,0:T(8,128)S(1)}, u32[]{:S(2)}, u32[]{:S(2)}) %collective-permute-start.3) | collective-permute-done | bytes 524320 | tf_op jit(solution)/shard_map/ppermute | solution.py:10
  33.8 4.6 %collective-permute-start.4 = (f32[256,512]{1,0:T(8,128)S(1)}, f32[256,512]{1,0:T(8,128)S(1)}, u32[]{:S(2)}, u32[]{:S(2)}) collective-permute-start(f32[256,512]{1,0:T(8,128)S(1)} %collective-permute-done.2), channel_id=1, source_target_pairs={{0,1},{1,2},{2,3},{4,5},{5,6},{6,7},{8,9},{9,10},{10,11},{12,13},{... | collective-permute-start | bytes 1572872 | tf_op jit(solution)/shard_map/ppermute | solution.py:10
  39.6 6.9 %collective-permute-done.5 = f32[256,512]{1,0:T(8,128)S(1)} collective-permute-done((f32[256,512]{1,0:T(8,128)S(1)}, f32[256,512]{1,0:T(8,128)S(1)}, u32[]{:S(2)}, u32[]{:S(2)}) %collective-permute-start.5) | collective-permute-done | bytes 524320 | tf_op jit(solution)/shard_map/ppermute | solution.py:10
  63.3 4.4 %collective-permute-start.9 = (f32[512,16]{0,1:T(8,128)S(1)}, f32[512,16]{0,1:T(8,128)S(1)}, u32[]{:S(2)}, u32[]{:S(2)}) collective-permute-start(f32[512,16]{0,1:T(8,128)S(1)} %convolution_bitcast_fusion.11), channel_id=1, source_target_pairs={{0,1},{1,2},{2,3},{4,5},{5,6},{6,7},{8,9},{9,10},{10,11},{12,13},{... | collective-permute-start | bytes 98312 | tf_op jit(solution)/shard_map/ppermute | solution.py:10
  68.2 3.4 %collective-permute-start.27 = (f32[512,16]{0,1:T(8,128)S(1)}, f32[512,16]{0,1:T(8,128)S(1)}, u32[]{:S(2)}, u32[]{:S(2)}) collective-permute-start(f32[512,16]{0,1:T(8,128)S(1)} %convolution_bitcast_fusion.8), channel_id=1, source_target_pairs={{0,1},{1,2},{2,3},{4,5},{5,6},{6,7},{8,9},{9,10},{10,11},{12,13},{... | collective-permute-start | bytes 98312 | tf_op jit(solution)/shard_map/ppermute | solution.py:10
  72.2 3.6 %collective-permute-start.45 = (f32[512,16]{0,1:T(8,128)S(1)}, f32[512,16]{0,1:T(8,128)S(1)}, u32[]{:S(2)}, u32[]{:S(2)}) collective-permute-start(f32[512,16]{0,1:T(8,128)S(1)} %convolution_bitcast_fusion.5), channel_id=1, source_target_pairs={{0,1},{1,2},{2,3},{4,5},{5,6},{6,7},{8,9},{9,10},{10,11},{12,13},{... | collective-permute-start | bytes 98312 | tf_op jit(solution)/shard_map/ppermute | solution.py:10
  76.4 1.9 collective-permute-start.63
  78.8 1.9 collective-permute-start.10
  81.3 1.9 collective-permute-start.28
  83.7 1.9 collective-permute-start.46
  86.2 2.1 collective-permute-start.64
  88.8 1.9 collective-permute-start.11
  91.3 2.1 collective-permute-start.29
  96.3 1.9 collective-permute-start.65
  144.3 4.0 %collective-permute-start.18 = (f32[256,128]{0,1:T(8,128)S(1)}, f32[256,128]{0,1:T(8,128)S(1)}, u32[]{:S(2)}, u32[]{:S(2)}) collective-permute-start(f32[256,128]{0,1:T(8,128)S(1)} %get-tuple-element.18), channel_id=1, source_target_pairs={{0,1},{1,2},{2,3},{4,5},{5,6},{6,7},{8,9},{9,10},{10,11},{12,13},{... | collective-permute-start | bytes 393224 | tf_op jit(solution)/shard_map/ppermute | solution.py:10
  151.0 4.6 %collective-permute-start.36 = (f32[256,128]{0,1:T(8,128)S(1)}, f32[256,128]{0,1:T(8,128)S(1)}, u32[]{:S(2)}, u32[]{:S(2)}) collective-permute-start(f32[256,128]{0,1:T(8,128)S(1)} %get-tuple-element.24), channel_id=1, source_target_pairs={{0,1},{1,2},{2,3},{4,5},{5,6},{6,7},{8,9},{9,10},{10,11},{12,13},{... | collective-permute-start | bytes 393224 | tf_op jit(solution)/shard_map/ppermute | solution.py:10
  158.1 4.6 %collective-permute-start.54 = (f32[256,128]{0,1:T(8,128)S(1)}, f32[256,128]{0,1:T(8,128)S(1)}, u32[]{:S(2)}, u32[]{:S(2)}) collective-permute-start(f32[256,128]{0,1:T(8,128)S(1)} %get-tuple-element.30), channel_id=1, source_target_pairs={{0,1},{1,2},{2,3},{4,5},{5,6},{6,7},{8,9},{9,10},{10,11},{12,13},{... | collective-permute-start | bytes 393224 | tf_op jit(solution)/shard_map/ppermute | solution.py:10
  165.2 4.6 %collective-permute-start.72 = (f32[256,128]{0,1:T(8,128)S(1)}, f32[256,128]{0,1:T(8,128)S(1)}, u32[]{:S(2)}, u32[]{:S(2)}) collective-permute-start(f32[256,128]{0,1:T(8,128)S(1)} %get-tuple-element.36), channel_id=1, source_target_pairs={{0,1},{1,2},{2,3},{4,5},{5,6},{6,7},{8,9},{9,10},{10,11},{12,13},{... | collective-permute-start | bytes 393224 | tf_op jit(solution)/shard_map/ppermute | solution.py:10
  171.1 4.6 %collective-permute-start.19 = (f32[256,128]{0,1:T(8,128)S(1)}, f32[256,128]{0,1:T(8,128)S(1)}, u32[]{:S(2)}, u32[]{:S(2)}) collective-permute-start(f32[256,128]{0,1:T(8,128)S(1)} %get-tuple-element.16), channel_id=1, source_target_pairs={{0,1},{1,2},{2,3},{4,5},{5,6},{6,7},{8,9},{9,10},{10,11},{12,13},{... | collective-permute-start | bytes 393224 | tf_op jit(solution)/shard_map/ppermute | solution.py:10
  177.1 4.6 %collective-permute-start.37 = (f32[256,128]{0,1:T(8,128)S(1)}, f32[256,128]{0,1:T(8,128)S(1)}, u32[]{:S(2)}, u32[]{:S(2)}) collective-permute-start(f32[256,128]{0,1:T(8,128)S(1)} %get-tuple-element.22), channel_id=1, source_target_pairs={{0,1},{1,2},{2,3},{4,5},{5,6},{6,7},{8,9},{9,10},{10,11},{12,13},{... | collective-permute-start | bytes 393224 | tf_op jit(solution)/shard_map/ppermute | solution.py:10
  183.0 4.6 %collective-permute-start.55 = (f32[256,128]{0,1:T(8,128)S(1)}, f32[256,128]{0,1:T(8,128)S(1)}, u32[]{:S(2)}, u32[]{:S(2)}) collective-permute-start(f32[256,128]{0,1:T(8,128)S(1)} %get-tuple-element.28), channel_id=1, source_target_pairs={{0,1},{1,2},{2,3},{4,5},{5,6},{6,7},{8,9},{9,10},{10,11},{12,13},{... | collective-permute-start | bytes 393224 | tf_op jit(solution)/shard_map/ppermute | solution.py:10
  188.9 4.6 %collective-permute-start.73 = (f32[256,128]{0,1:T(8,128)S(1)}, f32[256,128]{0,1:T(8,128)S(1)}, u32[]{:S(2)}, u32[]{:S(2)}) collective-permute-start(f32[256,128]{0,1:T(8,128)S(1)} %get-tuple-element.34), channel_id=1, source_target_pairs={{0,1},{1,2},{2,3},{4,5},{5,6},{6,7},{8,9},{9,10},{10,11},{12,13},{... | collective-permute-start | bytes 393224 | tf_op jit(solution)/shard_map/ppermute | solution.py:10
  194.9 4.6 %collective-permute-start.20 = (f32[256,128]{0,1:T(8,128)S(1)}, f32[256,128]{0,1:T(8,128)S(1)}, u32[]{:S(2)}, u32[]{:S(2)}) collective-permute-start(f32[256,128]{0,1:T(8,128)S(1)} %get-tuple-element.14), channel_id=1, source_target_pairs={{0,1},{1,2},{2,3},{4,5},{5,6},{6,7},{8,9},{9,10},{10,11},{12,13},{... | collective-permute-start | bytes 393224 | tf_op jit(solution)/shard_map/ppermute | solution.py:10
  200.8 4.6 %collective-permute-start.38 = (f32[256,128]{0,1:T(8,128)S(1)}, f32[256,128]{0,1:T(8,128)S(1)}, u32[]{:S(2)}, u32[]{:S(2)}) collective-permute-start(f32[256,128]{0,1:T(8,128)S(1)} %get-tuple-element.20), channel_id=1, source_target_pairs={{0,1},{1,2},{2,3},{4,5},{5,6},{6,7},{8,9},{9,10},{10,11},{12,13},{... | collective-permute-start | bytes 393224 | tf_op jit(solution)/shard_map/ppermute | solution.py:10
  206.7 4.6 %collective-permute-start.56 = (f32[256,128]{0,1:T(8,128)S(1)}, f32[256,128]{0,1:T(8,128)S(1)}, u32[]{:S(2)}, u32[]{:S(2)}) collective-permute-start(f32[256,128]{0,1:T(8,128)S(1)} %get-tuple-element.26), channel_id=1, source_target_pairs={{0,1},{1,2},{2,3},{4,5},{5,6},{6,7},{8,9},{9,10},{10,11},{12,13},{... | collective-permute-start | bytes 393224 | tf_op jit(solution)/shard_map/ppermute | solution.py:10
  212.7 4.6 %collective-permute-start.74 = (f32[256,128]{0,1:T(8,128)S(1)}, f32[256,128]{0,1:T(8,128)S(1)}, u32[]{:S(2)}, u32[]{:S(2)}) collective-permute-start(f32[256,128]{0,1:T(8,128)S(1)} %get-tuple-element.32), channel_id=1, source_target_pairs={{0,1},{1,2},{2,3},{4,5},{5,6},{6,7},{8,9},{9,10},{10,11},{12,13},{... | collective-permute-start | bytes 393224 | tf_op jit(solution)/shard_map/ppermute | solution.py:10
  219.7 4.4 %collective-permute-done.77 = f32[256,128]{0,1:T(8,128)S(1)} collective-permute-done((f32[256,128]{0,1:T(8,128)S(1)}, f32[256,128]{0,1:T(8,128)S(1)}, u32[]{:S(2)}, u32[]{:S(2)}) %collective-permute-start.77) | collective-permute-done | bytes 131104 | tf_op jit(solution)/shard_map/ppermute | solution.py:10
  (234 shorter events, 102.5 us)
Async XLA Ops:
  0.0 17.3 %collective-permute-start.1 = (f32[256,512]{1,0:T(8,128)}, f32[256,512]{1,0:T(8,128)}, u32[]{:S(2)}, u32[]{:S(2)}) collective-permute-start(f32[256,512]{1,0:T(8,128)} %param.6), channel_id=1, source_target_pairs={{1,0},{2,1},{3,2},{5,4},{6,5},{7,6},{9,8},{10,9},{11,10},{13,12},{... | collective-permute-start | bytes 1572872 | tf_op jit(solution)/shard_map/ppermute | solution.py:10
  1.4 17.2 %collective-permute-start = (f32[256,512]{1,0:T(8,128)}, f32[256,512]{1,0:T(8,128)}, u32[]{:S(2)}, u32[]{:S(2)}) collective-permute-start(f32[256,512]{1,0:T(8,128)} %param.6), channel_id=1, source_target_pairs={{0,1},{1,2},{2,3},{4,5},{5,6},{6,7},{8,9},{9,10},{10,11},{12,13},{... | collective-permute-start | bytes 1572872 | tf_op jit(solution)/shard_map/ppermute | solution.py:10
  17.3 15.2 %collective-permute-start.3 = (f32[256,512]{1,0:T(8,128)}, f32[256,512]{1,0:T(8,128)S(1)}, u32[]{:S(2)}, u32[]{:S(2)}) collective-permute-start(f32[256,512]{1,0:T(8,128)} %collective-permute-done.1), channel_id=1, source_target_pairs={{1,0},{2,1},{3,2},{5,4},{6,5},{7,6},{9,8},{10,9},{11,10},{13,12},{... | collective-permute-start | bytes 1572872 | tf_op jit(solution)/shard_map/ppermute | solution.py:10
  18.6 15.2 %collective-permute-start.2 = (f32[256,512]{1,0:T(8,128)}, f32[256,512]{1,0:T(8,128)S(1)}, u32[]{:S(2)}, u32[]{:S(2)}) collective-permute-start(f32[256,512]{1,0:T(8,128)} %collective-permute-done), channel_id=1, source_target_pairs={{0,1},{1,2},{2,3},{4,5},{5,6},{6,7},{8,9},{9,10},{10,11},{12,13},{... | collective-permute-start | bytes 1572872 | tf_op jit(solution)/shard_map/ppermute | solution.py:10
  32.5 14.1 %collective-permute-start.5 = (f32[256,512]{1,0:T(8,128)S(1)}, f32[256,512]{1,0:T(8,128)S(1)}, u32[]{:S(2)}, u32[]{:S(2)}) collective-permute-start(f32[256,512]{1,0:T(8,128)S(1)} %collective-permute-done.3), channel_id=1, source_target_pairs={{1,0},{2,1},{3,2},{5,4},{6,5},{7,6},{9,8},{10,9},{11,10},{13,12},{... | collective-permute-start | bytes 1572872 | tf_op jit(solution)/shard_map/ppermute | solution.py:10
  33.8 14.0 %collective-permute-start.4 = (f32[256,512]{1,0:T(8,128)S(1)}, f32[256,512]{1,0:T(8,128)S(1)}, u32[]{:S(2)}, u32[]{:S(2)}) collective-permute-start(f32[256,512]{1,0:T(8,128)S(1)} %collective-permute-done.2), channel_id=1, source_target_pairs={{0,1},{1,2},{2,3},{4,5},{5,6},{6,7},{8,9},{9,10},{10,11},{12,13},{... | collective-permute-start | bytes 1572872 | tf_op jit(solution)/shard_map/ppermute | solution.py:10
  61.8 14.1 %collective-permute-start.62 = (f32[512,16]{0,1:T(8,128)S(1)}, f32[512,16]{0,1:T(8,128)S(1)}, u32[]{:S(2)}, u32[]{:S(2)}) collective-permute-start(f32[512,16]{0,1:T(8,128)S(1)} %slice_select_fusion.8), channel_id=1, source_target_pairs={{0,16},{4,20},{8,24},{12,28},{16,0},{20,4},{24,8},{28,12},{1,17},{... | collective-permute-start | bytes 98312 | tf_op jit(solution)/shard_map/ppermute | solution.py:15
  63.3 15.0 %collective-permute-start.9 = (f32[512,16]{0,1:T(8,128)S(1)}, f32[512,16]{0,1:T(8,128)S(1)}, u32[]{:S(2)}, u32[]{:S(2)}) collective-permute-start(f32[512,16]{0,1:T(8,128)S(1)} %convolution_bitcast_fusion.11), channel_id=1, source_target_pairs={{0,1},{1,2},{2,3},{4,5},{5,6},{6,7},{8,9},{9,10},{10,11},{12,13},{... | collective-permute-start | bytes 98312 | tf_op jit(solution)/shard_map/ppermute | solution.py:10
  68.2 12.5 %collective-permute-start.27 = (f32[512,16]{0,1:T(8,128)S(1)}, f32[512,16]{0,1:T(8,128)S(1)}, u32[]{:S(2)}, u32[]{:S(2)}) collective-permute-start(f32[512,16]{0,1:T(8,128)S(1)} %convolution_bitcast_fusion.8), channel_id=1, source_target_pairs={{0,1},{1,2},{2,3},{4,5},{5,6},{6,7},{8,9},{9,10},{10,11},{12,13},{... | collective-permute-start | bytes 98312 | tf_op jit(solution)/shard_map/ppermute | solution.py:10
  141.5 14.1 %collective-permute-start.53 = (f32[512,64]{0,1:T(8,128)S(1)}, f32[512,64]{0,1:T(8,128)S(1)}, u32[]{:S(2)}, u32[]{:S(2)}) collective-permute-start(f32[512,64]{0,1:T(8,128)S(1)} %maximum_select_fusion.10), channel_id=1, source_target_pairs={{0,4},{4,0},{8,12},{12,8},{16,20},{20,16},{24,28},{28,24},{1,5},{5... | collective-permute-start | bytes 393224 | tf_op jit(solution)/shard_map/ppermute | solution.py:15
  143.0 15.1 %collective-permute-start.71 = (f32[512,64]{0,1:T(8,128)S(1)}, f32[512,64]{0,1:T(8,128)S(1)}, u32[]{:S(2)}, u32[]{:S(2)}) collective-permute-start(f32[512,64]{0,1:T(8,128)S(1)} %maximum_select_fusion.11), channel_id=1, source_target_pairs={{0,4},{4,0},{8,12},{12,8},{16,20},{20,16},{24,28},{28,24},{1,5},{5... | collective-permute-start | bytes 393224 | tf_op jit(solution)/shard_map/ppermute | solution.py:15
  144.3 19.6 %collective-permute-start.18 = (f32[256,128]{0,1:T(8,128)S(1)}, f32[256,128]{0,1:T(8,128)S(1)}, u32[]{:S(2)}, u32[]{:S(2)}) collective-permute-start(f32[256,128]{0,1:T(8,128)S(1)} %get-tuple-element.18), channel_id=1, source_target_pairs={{0,1},{1,2},{2,3},{4,5},{5,6},{6,7},{8,9},{9,10},{10,11},{12,13},{... | collective-permute-start | bytes 393224 | tf_op jit(solution)/shard_map/ppermute | solution.py:10
  148.3 16.9 %collective-permute-start.21 = (f32[256,128]{0,1:T(8,128)S(1)}, f32[256,128]{0,1:T(8,128)S(1)}, u32[]{:S(2)}, u32[]{:S(2)}) collective-permute-start(f32[256,128]{0,1:T(8,128)S(1)} %get-tuple-element.17), channel_id=1, source_target_pairs={{1,0},{2,1},{3,2},{5,4},{6,5},{7,6},{9,8},{10,9},{11,10},{13,12},{... | collective-permute-start | bytes 393224 | tf_op jit(solution)/shard_map/ppermute | solution.py:10
  151.0 18.8 %collective-permute-start.36 = (f32[256,128]{0,1:T(8,128)S(1)}, f32[256,128]{0,1:T(8,128)S(1)}, u32[]{:S(2)}, u32[]{:S(2)}) collective-permute-start(f32[256,128]{0,1:T(8,128)S(1)} %get-tuple-element.24), channel_id=1, source_target_pairs={{0,1},{1,2},{2,3},{4,5},{5,6},{6,7},{8,9},{9,10},{10,11},{12,13},{... | collective-permute-start | bytes 393224 | tf_op jit(solution)/shard_map/ppermute | solution.py:10
  155.6 15.5 %collective-permute-start.39 = (f32[256,128]{0,1:T(8,128)S(1)}, f32[256,128]{0,1:T(8,128)S(1)}, u32[]{:S(2)}, u32[]{:S(2)}) collective-permute-start(f32[256,128]{0,1:T(8,128)S(1)} %get-tuple-element.23), channel_id=1, source_target_pairs={{1,0},{2,1},{3,2},{5,4},{6,5},{7,6},{9,8},{10,9},{11,10},{13,12},{... | collective-permute-start | bytes 393224 | tf_op jit(solution)/shard_map/ppermute | solution.py:10
  158.1 17.6 %collective-permute-start.54 = (f32[256,128]{0,1:T(8,128)S(1)}, f32[256,128]{0,1:T(8,128)S(1)}, u32[]{:S(2)}, u32[]{:S(2)}) collective-permute-start(f32[256,128]{0,1:T(8,128)S(1)} %get-tuple-element.30), channel_id=1, source_target_pairs={{0,1},{1,2},{2,3},{4,5},{5,6},{6,7},{8,9},{9,10},{10,11},{12,13},{... | collective-permute-start | bytes 393224 | tf_op jit(solution)/shard_map/ppermute | solution.py:10
  163.9 13.2 %collective-permute-start.57 = (f32[256,128]{0,1:T(8,128)S(1)}, f32[256,128]{0,1:T(8,128)S(1)}, u32[]{:S(2)}, u32[]{:S(2)}) collective-permute-start(f32[256,128]{0,1:T(8,128)S(1)} %get-tuple-element.29), channel_id=1, source_target_pairs={{1,0},{2,1},{3,2},{5,4},{6,5},{7,6},{9,8},{10,9},{11,10},{13,12},{... | collective-permute-start | bytes 393224 | tf_op jit(solution)/shard_map/ppermute | solution.py:10
  165.2 16.5 %collective-permute-start.72 = (f32[256,128]{0,1:T(8,128)S(1)}, f32[256,128]{0,1:T(8,128)S(1)}, u32[]{:S(2)}, u32[]{:S(2)}) collective-permute-start(f32[256,128]{0,1:T(8,128)S(1)} %get-tuple-element.36), channel_id=1, source_target_pairs={{0,1},{1,2},{2,3},{4,5},{5,6},{6,7},{8,9},{9,10},{10,11},{12,13},{... | collective-permute-start | bytes 393224 | tf_op jit(solution)/shard_map/ppermute | solution.py:10
  169.8 13.2 %collective-permute-start.75 = (f32[256,128]{0,1:T(8,128)S(1)}, f32[256,128]{0,1:T(8,128)S(1)}, u32[]{:S(2)}, u32[]{:S(2)}) collective-permute-start(f32[256,128]{0,1:T(8,128)S(1)} %get-tuple-element.35), channel_id=1, source_target_pairs={{1,0},{2,1},{3,2},{5,4},{6,5},{7,6},{9,8},{10,9},{11,10},{13,12},{... | collective-permute-start | bytes 393224 | tf_op jit(solution)/shard_map/ppermute | solution.py:10
  171.1 16.5 %collective-permute-start.19 = (f32[256,128]{0,1:T(8,128)S(1)}, f32[256,128]{0,1:T(8,128)S(1)}, u32[]{:S(2)}, u32[]{:S(2)}) collective-permute-start(f32[256,128]{0,1:T(8,128)S(1)} %get-tuple-element.16), channel_id=1, source_target_pairs={{0,1},{1,2},{2,3},{4,5},{5,6},{6,7},{8,9},{9,10},{10,11},{12,13},{... | collective-permute-start | bytes 393224 | tf_op jit(solution)/shard_map/ppermute | solution.py:10
  175.8 13.2 %collective-permute-start.22 = (f32[256,128]{0,1:T(8,128)S(1)}, f32[256,128]{0,1:T(8,128)S(1)}, u32[]{:S(2)}, u32[]{:S(2)}) collective-permute-start(f32[256,128]{0,1:T(8,128)S(1)} %get-tuple-element.15), channel_id=1, source_target_pairs={{1,0},{2,1},{3,2},{5,4},{6,5},{7,6},{9,8},{10,9},{11,10},{13,12},{... | collective-permute-start | bytes 393224 | tf_op jit(solution)/shard_map/ppermute | solution.py:10
  177.1 16.5 %collective-permute-start.37 = (f32[256,128]{0,1:T(8,128)S(1)}, f32[256,128]{0,1:T(8,128)S(1)}, u32[]{:S(2)}, u32[]{:S(2)}) collective-permute-start(f32[256,128]{0,1:T(8,128)S(1)} %get-tuple-element.22), channel_id=1, source_target_pairs={{0,1},{1,2},{2,3},{4,5},{5,6},{6,7},{8,9},{9,10},{10,11},{12,13},{... | collective-permute-start | bytes 393224 | tf_op jit(solution)/shard_map/ppermute | solution.py:10
  181.7 13.2 %collective-permute-start.40 = (f32[256,128]{0,1:T(8,128)S(1)}, f32[256,128]{0,1:T(8,128)S(1)}, u32[]{:S(2)}, u32[]{:S(2)}) collective-permute-start(f32[256,128]{0,1:T(8,128)S(1)} %get-tuple-element.21), channel_id=1, source_target_pairs={{1,0},{2,1},{3,2},{5,4},{6,5},{7,6},{9,8},{10,9},{11,10},{13,12},{... | collective-permute-start | bytes 393224 | tf_op jit(solution)/shard_map/ppermute | solution.py:10
  183.0 16.5 %collective-permute-start.55 = (f32[256,128]{0,1:T(8,128)S(1)}, f32[256,128]{0,1:T(8,128)S(1)}, u32[]{:S(2)}, u32[]{:S(2)}) collective-permute-start(f32[256,128]{0,1:T(8,128)S(1)} %get-tuple-element.28), channel_id=1, source_target_pairs={{0,1},{1,2},{2,3},{4,5},{5,6},{6,7},{8,9},{9,10},{10,11},{12,13},{... | collective-permute-start | bytes 393224 | tf_op jit(solution)/shard_map/ppermute | solution.py:10
  187.6 13.2 %collective-permute-start.58 = (f32[256,128]{0,1:T(8,128)S(1)}, f32[256,128]{0,1:T(8,128)S(1)}, u32[]{:S(2)}, u32[]{:S(2)}) collective-permute-start(f32[256,128]{0,1:T(8,128)S(1)} %get-tuple-element.27), channel_id=1, source_target_pairs={{1,0},{2,1},{3,2},{5,4},{6,5},{7,6},{9,8},{10,9},{11,10},{13,12},{... | collective-permute-start | bytes 393224 | tf_op jit(solution)/shard_map/ppermute | solution.py:10
  188.9 16.5 %collective-permute-start.73 = (f32[256,128]{0,1:T(8,128)S(1)}, f32[256,128]{0,1:T(8,128)S(1)}, u32[]{:S(2)}, u32[]{:S(2)}) collective-permute-start(f32[256,128]{0,1:T(8,128)S(1)} %get-tuple-element.34), channel_id=1, source_target_pairs={{0,1},{1,2},{2,3},{4,5},{5,6},{6,7},{8,9},{9,10},{10,11},{12,13},{... | collective-permute-start | bytes 393224 | tf_op jit(solution)/shard_map/ppermute | solution.py:10
  193.6 13.2 %collective-permute-start.76 = (f32[256,128]{0,1:T(8,128)S(1)}, f32[256,128]{0,1:T(8,128)S(1)}, u32[]{:S(2)}, u32[]{:S(2)}) collective-permute-start(f32[256,128]{0,1:T(8,128)S(1)} %get-tuple-element.33), channel_id=1, source_target_pairs={{1,0},{2,1},{3,2},{5,4},{6,5},{7,6},{9,8},{10,9},{11,10},{13,12},{... | collective-permute-start | bytes 393224 | tf_op jit(solution)/shard_map/ppermute | solution.py:10
  194.9 16.5 %collective-permute-start.20 = (f32[256,128]{0,1:T(8,128)S(1)}, f32[256,128]{0,1:T(8,128)S(1)}, u32[]{:S(2)}, u32[]{:S(2)}) collective-permute-start(f32[256,128]{0,1:T(8,128)S(1)} %get-tuple-element.14), channel_id=1, source_target_pairs={{0,1},{1,2},{2,3},{4,5},{5,6},{6,7},{8,9},{9,10},{10,11},{12,13},{... | collective-permute-start | bytes 393224 | tf_op jit(solution)/shard_map/ppermute | solution.py:10
  199.5 13.2 %collective-permute-start.23 = (f32[256,128]{0,1:T(8,128)S(1)}, f32[256,128]{0,1:T(8,128)S(1)}, u32[]{:S(2)}, u32[]{:S(2)}) collective-permute-start(f32[256,128]{0,1:T(8,128)S(1)} %get-tuple-element.13), channel_id=1, source_target_pairs={{1,0},{2,1},{3,2},{5,4},{6,5},{7,6},{9,8},{10,9},{11,10},{13,12},{... | collective-permute-start | bytes 393224 | tf_op jit(solution)/shard_map/ppermute | solution.py:10
  200.8 16.5 %collective-permute-start.38 = (f32[256,128]{0,1:T(8,128)S(1)}, f32[256,128]{0,1:T(8,128)S(1)}, u32[]{:S(2)}, u32[]{:S(2)}) collective-permute-start(f32[256,128]{0,1:T(8,128)S(1)} %get-tuple-element.20), channel_id=1, source_target_pairs={{0,1},{1,2},{2,3},{4,5},{5,6},{6,7},{8,9},{9,10},{10,11},{12,13},{... | collective-permute-start | bytes 393224 | tf_op jit(solution)/shard_map/ppermute | solution.py:10
  205.4 13.2 %collective-permute-start.41 = (f32[256,128]{0,1:T(8,128)S(1)}, f32[256,128]{0,1:T(8,128)S(1)}, u32[]{:S(2)}, u32[]{:S(2)}) collective-permute-start(f32[256,128]{0,1:T(8,128)S(1)} %get-tuple-element.19), channel_id=1, source_target_pairs={{1,0},{2,1},{3,2},{5,4},{6,5},{7,6},{9,8},{10,9},{11,10},{13,12},{... | collective-permute-start | bytes 393224 | tf_op jit(solution)/shard_map/ppermute | solution.py:10
  206.7 11.9 %collective-permute-start.56 = (f32[256,128]{0,1:T(8,128)S(1)}, f32[256,128]{0,1:T(8,128)S(1)}, u32[]{:S(2)}, u32[]{:S(2)}) collective-permute-start(f32[256,128]{0,1:T(8,128)S(1)} %get-tuple-element.26), channel_id=1, source_target_pairs={{0,1},{1,2},{2,3},{4,5},{5,6},{6,7},{8,9},{9,10},{10,11},{12,13},{... | collective-permute-start | bytes 393224 | tf_op jit(solution)/shard_map/ppermute | solution.py:10
  (54 other events, 447.4 us)

commit v12 on v10

--- a/solution.py
+++ b/solution.py
@@ -128,15 +128,16 @@
     screened = screen_block(three_center, screen_mask)
     transfer = -product(diag_inverse, sub_factor)
     gamma_partial = gamma_over_aux(screened, densities)
-    width = gamma_partial.shape[1] // SLICES
+    right_side = reduce_scatter_columns(gamma_partial, "pair")
+    width = right_side.shape[1] // SLICES
     results = []
     for part in range(SLICES):
-        right_side = reduce_scatter_columns(gamma_partial[:, part * width:(part + 1) * width], "pair")
-        coefficients = solve(right_side, transfer, diag_inverse, sub_factor)
+        coefficients = solve(right_side[:, part * width:(part + 1) * width], transfer, diag_inverse, sub_factor)
         coeff_full = all_gather_columns(coefficients, "pair")
         partial = contract_first(screened, coeff_full)
-        results.append(reduce_over_aux(partial))
-    return jnp.concatenate(results, axis=1)
+        results.append(reduce_over_aux(partial).reshape(partial.shape[0] // lax.axis_size("aux"), -1, width))
+    joined = jnp.concatenate(results, axis=2)
+    return joined.reshape(joined.shape[0], -1)
 
 
 def solution(mesh):

time: 172 us -> 181 us (1.052)
  waiting for transfers between devices: 57.6 us -> 62.3 us
  other arithmetic: 2.82 us -> 6.68 us
    ppermute x12 -> x9, waiting for transfers between devices: 14.3 us -> 20.1 us  [swap(): return lax.ppermute(array, axis, [(i, i ^ bit) for i in range(count)])]
    ppermute x12 -> x9, starting transfers between devices: 11.3 us -> 8.52 us  [swap(): return lax.ppermute(array, axis, [(i, i ^ bit) for i in range(count)])]
    add x3, other arithmetic: 0.2 us -> 2.61 us  [reduce_scatter_columns(): current = keep + swap(send, axis, bit)]
    unnamed x7 -> x11, local copies, waits for them, and re-layouts: 2.92 us -> 4.71 us
  transfers between devices with their start and end apart: 42 -> 39, of which waited for: 23 -> 23; matrix products, arithmetic and copies ran while one was open for 14% -> 13% of each run, Pallas kernels for 0% -> 0%
where the time goes in v12:
time: 181 us; the launch traced here: 179 us
  starting transfers between devices  84.6 us (47%)
  waiting for transfers between devices  62.3 us (34%)
  matrix products  19.1 us (11%)
  other arithmetic  6.68 us (4%)
  local copies, waits for them, and re-layouts  6.03 us (3%)
    ppermute x30, starting transfers between devices, from_behind(): return lax.ppermute(array, axis, pairs)  76.1 us
    ppermute x30, waiting for transfers between devices, from_behind(): return lax.ppermute(array, axis, pairs)  42.2 us
    ppermute x9, waiting for transfers between devices, swap(): return lax.ppermute(array, axis, [(i, i ^ bit) for i in range(count)])  20.1 us
    dot_general x26, matrix products, product(): jnp.dot(left, right, precision=lax.Precision.HIGH, preferred_element_type...  17 us
    ppermute x9, starting transfers between devices, swap(): return lax.ppermute(array, axis, [(i, i ^ bit) for i in range(count)])  8.52 us
    unnamed x11, local copies, waits for them, and re-layouts  4.71 us
  transfers between devices with their start and end apart: 39, of which 23 were waited for; matrix products, arithmetic and copies ran while one was open for 13% of the time, Pallas kernels for 0%

profile of v12, /device:TPU:0, one launch (start us, length us, event | category | flops | bytes accessed | tf_op | source)
XLA Modules:
  0.0 179.4 jit_solution(2131584823303839738)
XLA Ops:
  1.4 6.4 %collective-permute-start = (f32[256,512]{1,0:T(8,128)}, f32[256,512]{1,0:T(8,128)}, u32[]{:S(2)}, u32[]{:S(2)}) collective-permute-start(f32[256,512]{1,0:T(8,128)} %param.6), channel_id=1, source_target_pairs={{0,1},{1,2},{2,3},{4,5},{5,6},{6,7},{8,9},{9,10},{10,11},{12,13},{... | collective-permute-start | bytes 1572872 | tf_op jit(solution)/shard_map/ppermute | solution.py:10
  7.8 2.9 %copy.8 = f32[512,1024]{0,1:T(8,128)} copy(f32[512,1024]{1,0:T(8,128)} %param.5) | data formatting | bytes 4194304 | tf_op args[0]
  10.9 1.8 %bitcast_multiply_fusion = f32[512,1024]{0,1:T(8,128)S(1)} fusion(f32[512,1024]{0,1:T(8,128)} %copy.8, f32[512,16]{0,1:T(8,128)S(1)} %reshape.15), kind=kLoop, calls=%fused_computation | loop fusion | flops 524288 | bytes 4227072 | tf_op jit(solution)/shard_map/mul | solution.py:23
  14.5 2.8 %collective-permute-done.1 = f32[256,512]{1,0:T(8,128)} collective-permute-done((f32[256,512]{1,0:T(8,128)}, f32[256,512]{1,0:T(8,128)}, u32[]{:S(2)}, u32[]{:S(2)}) %collective-permute-start.1) | collective-permute-done | bytes 524320 | tf_op jit(solution)/shard_map/ppermute | solution.py:10
  18.6 4.6 %collective-permute-start.2 = (f32[256,512]{1,0:T(8,128)}, f32[256,512]{1,0:T(8,128)S(1)}, u32[]{:S(2)}, u32[]{:S(2)}) collective-permute-start(f32[256,512]{1,0:T(8,128)} %collective-permute-done), channel_id=1, source_target_pairs={{0,1},{1,2},{2,3},{4,5},{5,6},{6,7},{8,9},{9,10},{10,11},{12,13},{... | collective-permute-start | bytes 1572872 | tf_op jit(solution)/shard_map/ppermute | solution.py:10
  23.2 1.7 convolution_add_fusion.3
  26.5 5.9 %collective-permute-done.3 = f32[256,512]{1,0:T(8,128)S(1)} collective-permute-done((f32[256,512]{1,0:T(8,128)}, f32[256,512]{1,0:T(8,128)S(1)}, u32[]{:S(2)}, u32[]{:S(2)}) %collective-permute-start.3) | collective-permute-done | bytes 524320 | tf_op jit(solution)/shard_map/ppermute | solution.py:10
  33.8 4.6 %collective-permute-start.4 = (f32[256,512]{1,0:T(8,128)S(1)}, f32[256,512]{1,0:T(8,128)S(1)}, u32[]{:S(2)}, u32[]{:S(2)}) collective-permute-start(f32[256,512]{1,0:T(8,128)S(1)} %collective-permute-done.2), channel_id=1, source_target_pairs={{0,1},{1,2},{2,3},{4,5},{5,6},{6,7},{8,9},{9,10},{10,11},{12,13},{... | collective-permute-start | bytes 1572872 | tf_op jit(solution)/shard_map/ppermute | solution.py:10
  39.6 6.9 %collective-permute-done.5 = f32[256,512]{1,0:T(8,128)S(1)} collective-permute-done((f32[256,512]{1,0:T(8,128)S(1)}, f32[256,512]{1,0:T(8,128)S(1)}, u32[]{:S(2)}, u32[]{:S(2)}) %collective-permute-start.5) | collective-permute-done | bytes 524320 | tf_op jit(solution)/shard_map/ppermute | solution.py:10
  50.3 2.2 %collective-permute-done.6 = f32[512,256]{0,1:T(8,128)} collective-permute-done((f32[512,256]{0,1:T(8,128)}, f32[512,256]{0,1:T(8,128)}, u32[]{:S(2)}, u32[]{:S(2)}) %collective-permute-start.6) | collective-permute-done | bytes 524320 | tf_op jit(solution)/shard_map/ppermute | solution.py:15
  56.6 7.5 %collective-permute-done.7 = f32[512,128]{0,1:T(8,128)S(1)} collective-permute-done((f32[512,128]{0,1:T(8,128)}, f32[512,128]{0,1:T(8,128)S(1)}, u32[]{:S(2)}, u32[]{:S(2)}) %collective-permute-start.7) | collective-permute-done | bytes 262176 | tf_op jit(solution)/shard_map/ppermute | solution.py:15
  67.4 2.9 %collective-permute-done.8 = f32[512,64]{0,1:T(8,128)S(1)} collective-permute-done((f32[512,64]{0,1:T(8,128)S(1)}, f32[512,64]{0,1:T(8,128)S(1)}, u32[]{:S(2)}, u32[]{:S(2)}) %collective-permute-start.8) | collective-permute-done | bytes 131104 | tf_op jit(solution)/shard_map/ppermute | solution.py:15
  70.9 4.4 %collective-permute-start.9 = (f32[512,32]{0,1:T(8,128)S(1)}, f32[512,32]{0,1:T(8,128)S(1)}, u32[]{:S(2)}, u32[]{:S(2)}) collective-permute-start(f32[512,32]{0,1:T(8,128)S(1)} %convolution_bitcast_fusion.5), channel_id=1, source_target_pairs={{0,1},{1,2},{2,3},{4,5},{5,6},{6,7},{8,9},{9,10},{10,11},{12,13},{... | collective-permute-start | bytes 196616 | tf_op jit(solution)/shard_map/ppermute | solution.py:10
  75.9 3.0 %collective-permute-start.24 = (f32[512,32]{0,1:T(8,128)S(1)}, f32[512,32]{0,1:T(8,128)S(1)}, u32[]{:S(2)}, u32[]{:S(2)}) collective-permute-start(f32[512,32]{0,1:T(8,128)S(1)} %convolution_bitcast_fusion.2), channel_id=1, source_target_pairs={{0,1},{1,2},{2,3},{4,5},{5,6},{6,7},{8,9},{9,10},{10,11},{12,13},{... | collective-permute-start | bytes 196616 | tf_op jit(solution)/shard_map/ppermute | solution.py:10
  79.4 3.7 %collective-permute-start.10 = (f32[512,32]{0,1:T(8,128)S(1)}, f32[512,32]{0,1:T(8,128)S(1)}, u32[]{:S(2)}, u32[]{:S(2)}) collective-permute-start(f32[512,32]{0,1:T(8,128)S(1)} %convolution_add_fusion.13), channel_id=1, source_target_pairs={{0,1},{1,2},{2,3},{4,5},{5,6},{6,7},{8,9},{9,10},{10,11},{12,13},{... | collective-permute-start | bytes 196616 | tf_op jit(solution)/shard_map/ppermute | solution.py:10
  83.7 1.9 %collective-permute-start.25 = (f32[512,32]{0,1:T(8,128)S(1)}, f32[512,32]{0,1:T(8,128)S(1)}, u32[]{:S(2)}, u32[]{:S(2)}) collective-permute-start(f32[512,32]{0,1:T(8,128)S(1)} %convolution_add_fusion.8), channel_id=1, source_target_pairs={{0,1},{1,2},{2,3},{4,5},{5,6},{6,7},{8,9},{9,10},{10,11},{12,13},{... | collective-permute-start | bytes 196616 | tf_op jit(solution)/shard_map/ppermute | solution.py:10
  86.2 4.0 %collective-permute-start.11 = (f32[512,32]{0,1:T(8,128)S(1)}, f32[512,32]{0,1:T(8,128)S(1)}, u32[]{:S(2)}, u32[]{:S(2)}) collective-permute-start(f32[512,32]{0,1:T(8,128)S(1)} %convolution_add_fusion.12), channel_id=1, source_target_pairs={{0,1},{1,2},{2,3},{4,5},{5,6},{6,7},{8,9},{9,10},{10,11},{12,13},{... | collective-permute-start | bytes 196616 | tf_op jit(solution)/shard_map/ppermute | solution.py:10
  90.8 2.2 %collective-permute-start.26 = (f32[512,32]{0,1:T(8,128)S(1)}, f32[512,32]{0,1:T(8,128)S(1)}, u32[]{:S(2)}, u32[]{:S(2)}) collective-permute-start(f32[512,32]{0,1:T(8,128)S(1)} %convolution_add_fusion.7), channel_id=1, source_target_pairs={{0,1},{1,2},{2,3},{4,5},{5,6},{6,7},{8,9},{9,10},{10,11},{12,13},{... | collective-permute-start | bytes 196616 | tf_op jit(solution)/shard_map/ppermute | solution.py:10
  96.8 3.8 %collective-permute-done.12 = f32[512,32]{0,1:T(8,128)S(1)} collective-permute-done((f32[512,32]{0,1:T(8,128)S(1)}, f32[512,32]{0,1:T(8,128)S(1)}, u32[]{:S(2)}, u32[]{:S(2)}) %collective-permute-start.12) | collective-permute-done | bytes 65568 | tf_op jit(solution)/shard_map/ppermute | solution.py:10
  104.1 3.3 %collective-permute-done.13 = f32[512,32]{0,1:T(8,128)S(1)} collective-permute-done((f32[512,32]{0,1:T(8,128)S(1)}, f32[512,32]{0,1:T(8,128)S(1)}, u32[]{:S(2)}, u32[]{:S(2)}) %collective-permute-start.13) | collective-permute-done | bytes 65568 | tf_op jit(solution)/shard_map/ppermute | solution.py:10
  111.4 2.5 %collective-permute-done.14 = f32[512,32]{0,1:T(8,128)S(1)} collective-permute-done((f32[512,32]{0,1:T(8,128)S(1)}, f32[512,32]{0,1:T(8,128)S(1)}, u32[]{:S(2)}, u32[]{:S(2)}) %collective-permute-start.14) | collective-permute-done | bytes 65568 | tf_op jit(solution)/shard_map/ppermute | solution.py:10
  120.9 2.0 %collective-permute-done.29 = f32[512,32]{0,1:T(8,128)S(1)} collective-permute-done((f32[512,32]{0,1:T(8,128)S(1)}, f32[512,32]{0,1:T(8,128)S(1)}, u32[]{:S(2)}, u32[]{:S(2)}) %collective-permute-start.29) | collective-permute-done | bytes 65568 | tf_op jit(solution)/shard_map/ppermute | solution.py:10
  125.0 2.6 %collective-permute-done.30 = f32[512,32]{0,1:T(8,128)S(1)} collective-permute-done((f32[512,32]{0,1:T(8,128)S(1)}, f32[512,32]{0,1:T(8,128)S(1)}, u32[]{:S(2)}, u32[]{:S(2)}) %collective-permute-start.30) | collective-permute-done | bytes 65568 | tf_op jit(solution)/shard_map/ppermute | solution.py:15
  129.2 3.5 %collective-permute-done.31 = f32[512,64]{0,1:T(8,128)S(1)} collective-permute-done((f32[512,64]{0,1:T(8,128)S(1)}, f32[512,64]{0,1:T(8,128)S(1)}, u32[]{:S(2)}, u32[]{:S(2)}) %collective-permute-start.31) | collective-permute-done | bytes 131104 | tf_op jit(solution)/shard_map/ppermute | solution.py:15
  133.9 3.9 %collective-permute-start.18 = (f32[256,256]{0,1:T(8,128)S(1)}, f32[256,256]{0,1:T(8,128)S(1)}, u32[]{:S(2)}, u32[]{:S(2)}) collective-permute-start(f32[256,256]{0,1:T(8,128)S(1)} %get-tuple-element.10), channel_id=1, source_target_pairs={{0,1},{1,2},{2,3},{4,5},{5,6},{6,7},{8,9},{9,10},{10,11},{12,13},{... | collective-permute-start | bytes 786440 | tf_op jit(solution)/shard_map/ppermute | solution.py:10
  140.2 4.6 %collective-permute-start.33 = (f32[256,256]{0,1:T(8,128)S(1)}, f32[256,256]{0,1:T(8,128)S(1)}, u32[]{:S(2)}, u32[]{:S(2)}) collective-permute-start(f32[256,256]{0,1:T(8,128)S(1)} %get-tuple-element.16), channel_id=1, source_target_pairs={{0,1},{1,2},{2,3},{4,5},{5,6},{6,7},{8,9},{9,10},{10,11},{12,13},{... | collective-permute-start | bytes 786440 | tf_op jit(solution)/shard_map/ppermute | solution.py:10
  146.1 2.0 %collective-permute-done.21 = f32[256,256]{0,1:T(8,128)S(1)} collective-permute-done((f32[256,256]{0,1:T(8,128)S(1)}, f32[256,256]{0,1:T(8,128)S(1)}, u32[]{:S(2)}, u32[]{:S(2)}) %collective-permute-start.21) | collective-permute-done | bytes 262176 | tf_op jit(solution)/shard_map/ppermute | solution.py:10
  148.2 3.3 %collective-permute-start.19 = (f32[256,256]{0,1:T(8,128)S(1)}, f32[256,256]{0,1:T(8,128)S(1)}, u32[]{:S(2)}, u32[]{:S(2)}) collective-permute-start(f32[256,256]{0,1:T(8,128)S(1)} %get-tuple-element.8), channel_id=1, source_target_pairs={{0,1},{1,2},{2,3},{4,5},{5,6},{6,7},{8,9},{9,10},{10,11},{12,13},{... | collective-permute-start | bytes 786440 | tf_op jit(solution)/shard_map/ppermute | solution.py:10
  154.6 3.4 %collective-permute-start.34 = (f32[256,256]{0,1:T(8,128)S(1)}, f32[256,256]{0,1:T(8,128)S(1)}, u32[]{:S(2)}, u32[]{:S(2)}) collective-permute-start(f32[256,256]{0,1:T(8,128)S(1)} %get-tuple-element.14), channel_id=1, source_target_pairs={{0,1},{1,2},{2,3},{4,5},{5,6},{6,7},{8,9},{9,10},{10,11},{12,13},{... | collective-permute-start | bytes 786440 | tf_op jit(solution)/shard_map/ppermute | solution.py:10
  160.8 3.2 %collective-permute-start.20 = (f32[256,256]{0,1:T(8,128)S(1)}, f32[256,256]{0,1:T(8,128)S(1)}, u32[]{:S(2)}, u32[]{:S(2)}) collective-permute-start(f32[256,256]{0,1:T(8,128)S(1)} %get-tuple-element.6), channel_id=1, source_target_pairs={{0,1},{1,2},{2,3},{4,5},{5,6},{6,7},{8,9},{9,10},{10,11},{12,13},{... | collective-permute-start | bytes 786440 | tf_op jit(solution)/shard_map/ppermute | solution.py:10
  166.7 3.3 %collective-permute-start.35 = (f32[256,256]{0,1:T(8,128)S(1)}, f32[256,256]{0,1:T(8,128)S(1)}, u32[]{:S(2)}, u32[]{:S(2)}) collective-permute-start(f32[256,256]{0,1:T(8,128)S(1)} %get-tuple-element.12), channel_id=1, source_target_pairs={{0,1},{1,2},{2,3},{4,5},{5,6},{6,7},{8,9},{9,10},{10,11},{12,13},{... | collective-permute-start | bytes 786440 | tf_op jit(solution)/shard_map/ppermute | solution.py:10
  173.9 4.4 %collective-permute-done.38 = f32[256,256]{0,1:T(8,128)S(1)} collective-permute-done((f32[256,256]{0,1:T(8,128)S(1)}, f32[256,256]{0,1:T(8,128)S(1)}, u32[]{:S(2)}, u32[]{:S(2)}) %collective-permute-start.38) | collective-permute-done | bytes 262176 | tf_op jit(solution)/shard_map/ppermute | solution.py:10
  (110 shorter events, 63.2 us)
Async XLA Ops:
  0.0 17.3 %collective-permute-start.1 = (f32[256,512]{1,0:T(8,128)}, f32[256,512]{1,0:T(8,128)}, u32[]{:S(2)}, u32[]{:S(2)}) collective-permute-start(f32[256,512]{1,0:T(8,128)} %param.6), channel_id=1, source_target_pairs={{1,0},{2,1},{3,2},{5,4},{6,5},{7,6},{9,8},{10,9},{11,10},{13,12},{... | collective-permute-start | bytes 1572872 | tf_op jit(solution)/shard_map/ppermute | solution.py:10
  1.4 17.2 %collective-permute-start = (f32[256,512]{1,0:T(8,128)}, f32[256,512]{1,0:T(8,128)}, u32[]{:S(2)}, u32[]{:S(2)}) collective-permute-start(f32[256,512]{1,0:T(8,128)} %param.6), channel_id=1, source_target_pairs={{0,1},{1,2},{2,3},{4,5},{5,6},{6,7},{8,9},{9,10},{10,11},{12,13},{... | collective-permute-start | bytes 1572872 | tf_op jit(solution)/shard_map/ppermute | solution.py:10
  17.3 15.2 %collective-permute-start.3 = (f32[256,512]{1,0:T(8,128)}, f32[256,512]{1,0:T(8,128)S(1)}, u32[]{:S(2)}, u32[]{:S(2)}) collective-permute-start(f32[256,512]{1,0:T(8,128)} %collective-permute-done.1), channel_id=1, source_target_pairs={{1,0},{2,1},{3,2},{5,4},{6,5},{7,6},{9,8},{10,9},{11,10},{13,12},{... | collective-permute-start | bytes 1572872 | tf_op jit(solution)/shard_map/ppermute | solution.py:10
  18.6 15.2 %collective-permute-start.2 = (f32[256,512]{1,0:T(8,128)}, f32[256,512]{1,0:T(8,128)S(1)}, u32[]{:S(2)}, u32[]{:S(2)}) collective-permute-start(f32[256,512]{1,0:T(8,128)} %collective-permute-done), channel_id=1, source_target_pairs={{0,1},{1,2},{2,3},{4,5},{5,6},{6,7},{8,9},{9,10},{10,11},{12,13},{... | collective-permute-start | bytes 1572872 | tf_op jit(solution)/shard_map/ppermute | solution.py:10
  32.5 14.1 %collective-permute-start.5 = (f32[256,512]{1,0:T(8,128)S(1)}, f32[256,512]{1,0:T(8,128)S(1)}, u32[]{:S(2)}, u32[]{:S(2)}) collective-permute-start(f32[256,512]{1,0:T(8,128)S(1)} %collective-permute-done.3), channel_id=1, source_target_pairs={{1,0},{2,1},{3,2},{5,4},{6,5},{7,6},{9,8},{10,9},{11,10},{13,12},{... | collective-permute-start | bytes 1572872 | tf_op jit(solution)/shard_map/ppermute | solution.py:10
  33.8 14.0 %collective-permute-start.4 = (f32[256,512]{1,0:T(8,128)S(1)}, f32[256,512]{1,0:T(8,128)S(1)}, u32[]{:S(2)}, u32[]{:S(2)}) collective-permute-start(f32[256,512]{1,0:T(8,128)S(1)} %collective-permute-done.2), channel_id=1, source_target_pairs={{0,1},{1,2},{2,3},{4,5},{5,6},{6,7},{8,9},{9,10},{10,11},{12,13},{... | collective-permute-start | bytes 1572872 | tf_op jit(solution)/shard_map/ppermute | solution.py:10
  55.6 8.6 %collective-permute-start.7 = (f32[512,128]{0,1:T(8,128)}, f32[512,128]{0,1:T(8,128)S(1)}, u32[]{:S(2)}, u32[]{:S(2)}) collective-permute-start(f32[512,128]{0,1:T(8,128)} %slice_select_fusion.1), channel_id=1, source_target_pairs={{0,8},{4,12},{8,0},{12,4},{16,24},{20,28},{24,16},{28,20},{1,9},{5... | collective-permute-start | bytes 786440 | tf_op jit(solution)/shard_map/ppermute | solution.py:15
  70.9 8.0 %collective-permute-start.9 = (f32[512,32]{0,1:T(8,128)S(1)}, f32[512,32]{0,1:T(8,128)S(1)}, u32[]{:S(2)}, u32[]{:S(2)}) collective-permute-start(f32[512,32]{0,1:T(8,128)S(1)} %convolution_bitcast_fusion.5), channel_id=1, source_target_pairs={{0,1},{1,2},{2,3},{4,5},{5,6},{6,7},{8,9},{9,10},{10,11},{12,13},{... | collective-permute-start | bytes 196616 | tf_op jit(solution)/shard_map/ppermute | solution.py:10
  75.9 7.3 %collective-permute-start.24 = (f32[512,32]{0,1:T(8,128)S(1)}, f32[512,32]{0,1:T(8,128)S(1)}, u32[]{:S(2)}, u32[]{:S(2)}) collective-permute-start(f32[512,32]{0,1:T(8,128)S(1)} %convolution_bitcast_fusion.2), channel_id=1, source_target_pairs={{0,1},{1,2},{2,3},{4,5},{5,6},{6,7},{8,9},{9,10},{10,11},{12,13},{... | collective-permute-start | bytes 196616 | tf_op jit(solution)/shard_map/ppermute | solution.py:10
  79.4 6.2 %collective-permute-start.10 = (f32[512,32]{0,1:T(8,128)S(1)}, f32[512,32]{0,1:T(8,128)S(1)}, u32[]{:S(2)}, u32[]{:S(2)}) collective-permute-start(f32[512,32]{0,1:T(8,128)S(1)} %convolution_add_fusion.13), channel_id=1, source_target_pairs={{0,1},{1,2},{2,3},{4,5},{5,6},{6,7},{8,9},{9,10},{10,11},{12,13},{... | collective-permute-start | bytes 196616 | tf_op jit(solution)/shard_map/ppermute | solution.py:10
  83.7 6.5 %collective-permute-start.25 = (f32[512,32]{0,1:T(8,128)S(1)}, f32[512,32]{0,1:T(8,128)S(1)}, u32[]{:S(2)}, u32[]{:S(2)}) collective-permute-start(f32[512,32]{0,1:T(8,128)S(1)} %convolution_add_fusion.8), channel_id=1, source_target_pairs={{0,1},{1,2},{2,3},{4,5},{5,6},{6,7},{8,9},{9,10},{10,11},{12,13},{... | collective-permute-start | bytes 196616 | tf_op jit(solution)/shard_map/ppermute | solution.py:10
  86.2 6.8 %collective-permute-start.11 = (f32[512,32]{0,1:T(8,128)S(1)}, f32[512,32]{0,1:T(8,128)S(1)}, u32[]{:S(2)}, u32[]{:S(2)}) collective-permute-start(f32[512,32]{0,1:T(8,128)S(1)} %convolution_add_fusion.12), channel_id=1, source_target_pairs={{0,1},{1,2},{2,3},{4,5},{5,6},{6,7},{8,9},{9,10},{10,11},{12,13},{... | collective-permute-start | bytes 196616 | tf_op jit(solution)/shard_map/ppermute | solution.py:10
  94.4 6.3 %collective-permute-start.12 = (f32[512,32]{0,1:T(8,128)S(1)}, f32[512,32]{0,1:T(8,128)S(1)}, u32[]{:S(2)}, u32[]{:S(2)}) collective-permute-start(f32[512,32]{0,1:T(8,128)S(1)} %convolution_bitcast_fusion.4), channel_id=1, source_target_pairs={{1,0},{2,1},{3,2},{5,4},{6,5},{7,6},{9,8},{10,9},{11,10},{13,12},{... | collective-permute-start | bytes 196616 | tf_op jit(solution)/shard_map/ppermute | solution.py:10
  101.1 6.3 %collective-permute-start.13 = (f32[512,32]{0,1:T(8,128)S(1)}, f32[512,32]{0,1:T(8,128)S(1)}, u32[]{:S(2)}, u32[]{:S(2)}) collective-permute-start(f32[512,32]{0,1:T(8,128)S(1)} %convolution_add_fusion.10), channel_id=1, source_target_pairs={{1,0},{2,1},{3,2},{5,4},{6,5},{7,6},{9,8},{10,9},{11,10},{13,12},{... | collective-permute-start | bytes 196616 | tf_op jit(solution)/shard_map/ppermute | solution.py:10
  102.8 7.0 %collective-permute-start.27 = (f32[512,32]{0,1:T(8,128)S(1)}, f32[512,32]{0,1:T(8,128)S(1)}, u32[]{:S(2)}, u32[]{:S(2)}) collective-permute-start(f32[512,32]{0,1:T(8,128)S(1)} %convolution_bitcast_fusion.1), channel_id=1, source_target_pairs={{1,0},{2,1},{3,2},{5,4},{6,5},{7,6},{9,8},{10,9},{11,10},{13,12},{... | collective-permute-start | bytes 196616 | tf_op jit(solution)/shard_map/ppermute | solution.py:10
  107.8 6.2 %collective-permute-start.14 = (f32[512,32]{0,1:T(8,128)S(1)}, f32[512,32]{0,1:T(8,128)S(1)}, u32[]{:S(2)}, u32[]{:S(2)}) collective-permute-start(f32[512,32]{0,1:T(8,128)S(1)} %convolution_add_fusion.9), channel_id=1, source_target_pairs={{1,0},{2,1},{3,2},{5,4},{6,5},{7,6},{9,8},{10,9},{11,10},{13,12},{... | collective-permute-start | bytes 196616 | tf_op jit(solution)/shard_map/ppermute | solution.py:10
  110.1 6.2 %collective-permute-start.28 = (f32[512,32]{0,1:T(8,128)S(1)}, f32[512,32]{0,1:T(8,128)S(1)}, u32[]{:S(2)}, u32[]{:S(2)}) collective-permute-start(f32[512,32]{0,1:T(8,128)S(1)} %convolution_add_fusion.5), channel_id=1, source_target_pairs={{1,0},{2,1},{3,2},{5,4},{6,5},{7,6},{9,8},{10,9},{11,10},{13,12},{... | collective-permute-start | bytes 196616 | tf_op jit(solution)/shard_map/ppermute | solution.py:10
  116.7 6.2 %collective-permute-start.29 = (f32[512,32]{0,1:T(8,128)S(1)}, f32[512,32]{0,1:T(8,128)S(1)}, u32[]{:S(2)}, u32[]{:S(2)}) collective-permute-start(f32[512,32]{0,1:T(8,128)S(1)} %convolution_add_fusion.4), channel_id=1, source_target_pairs={{1,0},{2,1},{3,2},{5,4},{6,5},{7,6},{9,8},{10,9},{11,10},{13,12},{... | collective-permute-start | bytes 196616 | tf_op jit(solution)/shard_map/ppermute | solution.py:10
  124.9 7.9 %collective-permute-start.17 = (f32[512,128]{0,1:T(8,128)S(1)}, f32[512,128]{0,1:T(8,128)S(1)}, u32[]{:S(2)}, u32[]{:S(2)}) collective-permute-start(f32[512,128]{0,1:T(8,128)S(1)} %maximum_select_fusion.4), channel_id=1, source_target_pairs={{0,4},{4,0},{8,12},{12,8},{16,20},{20,16},{24,28},{28,24},{1,5},{5... | collective-permute-start | bytes 786440 | tf_op jit(solution)/shard_map/ppermute | solution.py:15
  132.7 6.4 %collective-permute-start.32 = (f32[512,128]{0,1:T(8,128)S(1)}, f32[512,128]{0,1:T(8,128)S(1)}, u32[]{:S(2)}, u32[]{:S(2)}) collective-permute-start(f32[512,128]{0,1:T(8,128)S(1)} %maximum_select_fusion.5), channel_id=1, source_target_pairs={{0,4},{4,0},{8,12},{12,8},{16,20},{20,16},{24,28},{28,24},{1,5},{5... | collective-permute-start | bytes 786440 | tf_op jit(solution)/shard_map/ppermute | solution.py:15
  133.9 12.2 %collective-permute-start.18 = (f32[256,256]{0,1:T(8,128)S(1)}, f32[256,256]{0,1:T(8,128)S(1)}, u32[]{:S(2)}, u32[]{:S(2)}) collective-permute-start(f32[256,256]{0,1:T(8,128)S(1)} %get-tuple-element.10), channel_id=1, source_target_pairs={{0,1},{1,2},{2,3},{4,5},{5,6},{6,7},{8,9},{9,10},{10,11},{12,13},{... | collective-permute-start | bytes 786440 | tf_op jit(solution)/shard_map/ppermute | solution.py:10
  137.8 10.3 %collective-permute-start.21 = (f32[256,256]{0,1:T(8,128)S(1)}, f32[256,256]{0,1:T(8,128)S(1)}, u32[]{:S(2)}, u32[]{:S(2)}) collective-permute-start(f32[256,256]{0,1:T(8,128)S(1)} %get-tuple-element.9), channel_id=1, source_target_pairs={{1,0},{2,1},{3,2},{5,4},{6,5},{7,6},{9,8},{10,9},{11,10},{13,12},{... | collective-permute-start | bytes 786440 | tf_op jit(solution)/shard_map/ppermute | solution.py:10
  140.2 12.6 %collective-permute-start.33 = (f32[256,256]{0,1:T(8,128)S(1)}, f32[256,256]{0,1:T(8,128)S(1)}, u32[]{:S(2)}, u32[]{:S(2)}) collective-permute-start(f32[256,256]{0,1:T(8,128)S(1)} %get-tuple-element.16), channel_id=1, source_target_pairs={{0,1},{1,2},{2,3},{4,5},{5,6},{6,7},{8,9},{9,10},{10,11},{12,13},{... | collective-permute-start | bytes 786440 | tf_op jit(solution)/shard_map/ppermute | solution.py:10
  144.8 9.8 %collective-permute-start.36 = (f32[256,256]{0,1:T(8,128)S(1)}, f32[256,256]{0,1:T(8,128)S(1)}, u32[]{:S(2)}, u32[]{:S(2)}) collective-permute-start(f32[256,256]{0,1:T(8,128)S(1)} %get-tuple-element.15), channel_id=1, source_target_pairs={{1,0},{2,1},{3,2},{5,4},{6,5},{7,6},{9,8},{10,9},{11,10},{13,12},{... | collective-permute-start | bytes 786440 | tf_op jit(solution)/shard_map/ppermute | solution.py:10
  148.2 11.2 %collective-permute-start.19 = (f32[256,256]{0,1:T(8,128)S(1)}, f32[256,256]{0,1:T(8,128)S(1)}, u32[]{:S(2)}, u32[]{:S(2)}) collective-permute-start(f32[256,256]{0,1:T(8,128)S(1)} %get-tuple-element.8), channel_id=1, source_target_pairs={{0,1},{1,2},{2,3},{4,5},{5,6},{6,7},{8,9},{9,10},{10,11},{12,13},{... | collective-permute-start | bytes 786440 | tf_op jit(solution)/shard_map/ppermute | solution.py:10
  151.5 9.2 %collective-permute-start.22 = (f32[256,256]{0,1:T(8,128)S(1)}, f32[256,256]{0,1:T(8,128)S(1)}, u32[]{:S(2)}, u32[]{:S(2)}) collective-permute-start(f32[256,256]{0,1:T(8,128)S(1)} %get-tuple-element.7), channel_id=1, source_target_pairs={{1,0},{2,1},{3,2},{5,4},{6,5},{7,6},{9,8},{10,9},{11,10},{13,12},{... | collective-permute-start | bytes 786440 | tf_op jit(solution)/shard_map/ppermute | solution.py:10
  154.6 10.7 %collective-permute-start.34 = (f32[256,256]{0,1:T(8,128)S(1)}, f32[256,256]{0,1:T(8,128)S(1)}, u32[]{:S(2)}, u32[]{:S(2)}) collective-permute-start(f32[256,256]{0,1:T(8,128)S(1)} %get-tuple-element.14), channel_id=1, source_target_pairs={{0,1},{1,2},{2,3},{4,5},{5,6},{6,7},{8,9},{9,10},{10,11},{12,13},{... | collective-permute-start | bytes 786440 | tf_op jit(solution)/shard_map/ppermute | solution.py:10
  158.1 8.6 %collective-permute-start.37 = (f32[256,256]{0,1:T(8,128)S(1)}, f32[256,256]{0,1:T(8,128)S(1)}, u32[]{:S(2)}, u32[]{:S(2)}) collective-permute-start(f32[256,256]{0,1:T(8,128)S(1)} %get-tuple-element.13), channel_id=1, source_target_pairs={{1,0},{2,1},{3,2},{5,4},{6,5},{7,6},{9,8},{10,9},{11,10},{13,12},{... | collective-permute-start | bytes 786440 | tf_op jit(solution)/shard_map/ppermute | solution.py:10
  160.8 10.5 %collective-permute-start.20 = (f32[256,256]{0,1:T(8,128)S(1)}, f32[256,256]{0,1:T(8,128)S(1)}, u32[]{:S(2)}, u32[]{:S(2)}) collective-permute-start(f32[256,256]{0,1:T(8,128)S(1)} %get-tuple-element.6), channel_id=1, source_target_pairs={{0,1},{1,2},{2,3},{4,5},{5,6},{6,7},{8,9},{9,10},{10,11},{12,13},{... | collective-permute-start | bytes 786440 | tf_op jit(solution)/shard_map/ppermute | solution.py:10
  164.1 8.7 %collective-permute-start.23 = (f32[256,256]{0,1:T(8,128)S(1)}, f32[256,256]{0,1:T(8,128)S(1)}, u32[]{:S(2)}, u32[]{:S(2)}) collective-permute-start(f32[256,256]{0,1:T(8,128)S(1)} %get-tuple-element.5), channel_id=1, source_target_pairs={{1,0},{2,1},{3,2},{5,4},{6,5},{7,6},{9,8},{10,9},{11,10},{13,12},{... | collective-permute-start | bytes 786440 | tf_op jit(solution)/shard_map/ppermute | solution.py:10
  166.7 7.2 %collective-permute-start.35 = (f32[256,256]{0,1:T(8,128)S(1)}, f32[256,256]{0,1:T(8,128)S(1)}, u32[]{:S(2)}, u32[]{:S(2)}) collective-permute-start(f32[256,256]{0,1:T(8,128)S(1)} %get-tuple-element.12), channel_id=1, source_target_pairs={{0,1},{1,2},{2,3},{4,5},{5,6},{6,7},{8,9},{9,10},{10,11},{12,13},{... | collective-permute-start | bytes 786440 | tf_op jit(solution)/shard_map/ppermute | solution.py:10
  170.1 8.3 %collective-permute-start.38 = (f32[256,256]{0,1:T(8,128)S(1)}, f32[256,256]{0,1:T(8,128)S(1)}, u32[]{:S(2)}, u32[]{:S(2)}) collective-permute-start(f32[256,256]{0,1:T(8,128)S(1)} %get-tuple-element.11), channel_id=1, source_target_pairs={{1,0},{2,1},{3,2},{5,4},{6,5},{7,6},{9,8},{10,9},{11,10},{13,12},{... | collective-permute-start | bytes 786440 | tf_op jit(solution)/shard_map/ppermute | solution.py:10
  (12 other events, 113.0 us)

commit v13 on v10

--- a/solution.py
+++ b/solution.py
@@ -43,8 +43,8 @@
     current = partial
     bit = 1
     while bit < count:
-        width = current.shape[1] // 2
-        low, high = current[:, :width], current[:, width:]
+        width = current.shape[-1] // 2
+        low, high = current[..., :width], current[..., width:]
         upper = (index // bit) % 2 == 1
         send = jnp.where(upper, low, high)
         keep = jnp.where(upper, high, low)
@@ -80,13 +80,29 @@
         return lax.dynamic_slice_in_dim(screened, start, rows, axis=1)
 
     gamma = product(columns(index), densities)
+    helped = count >= 4
+    steps = count - 2 if helped else count - 1
     from_left, from_right = densities, densities
-    for step in range(count - 1):
-        from_left = from_behind(from_left, "aux", 1)
-        from_right = from_behind(from_right, "aux", -1)
+    for step in range(steps):
+        rightward = [(i, i + 1) for i in range(step, count - 1)]
+        leftward = [(i + 1, i) for i in range(count - 1 - step)]
+        from_left = lax.ppermute(from_left, "aux", rightward)
+        from_right = lax.ppermute(from_right, "aux", leftward)
         gamma = gamma + product(columns(index - 1 - step), from_left)
         gamma = gamma + product(columns(index + 1 + step), from_right)
-    return gamma
+    if not helped:
+        return gamma, jnp.zeros_like(gamma)
+    end_pairs = [(0, 1), (count - 1, count - 2)]
+    end_columns = lax.ppermute(columns(jnp.where(index == 0, count - 1, 0)), "aux", end_pairs)
+    far = product(end_columns, jnp.where(index == 1, from_right, from_left))
+    return gamma, far
+
+
+def return_far(far_share):
+    count = lax.axis_size("aux")
+    if count < 4:
+        return far_share
+    return lax.ppermute(far_share, "aux", [(1, 0), (count - 2, count - 1)])
 
 
 def reduce_over_aux(partial):
@@ -127,11 +143,13 @@
 def per_device(three_center, densities, screen_mask, diag_inverse, sub_factor):
     screened = screen_block(three_center, screen_mask)
     transfer = -product(diag_inverse, sub_factor)
-    gamma_partial = gamma_over_aux(screened, densities)
+    gamma_partial, far = gamma_over_aux(screened, densities)
     width = gamma_partial.shape[1] // SLICES
     results = []
     for part in range(SLICES):
-        right_side = reduce_scatter_columns(gamma_partial[:, part * width:(part + 1) * width], "pair")
+        columns = slice(part * width, (part + 1) * width)
+        both = reduce_scatter_columns(jnp.stack([gamma_partial[:, columns], far[:, columns]]), "pair")
+        right_side = both[0] + return_far(both[1])
         coefficients = solve(right_side, transfer, diag_inverse, sub_factor)
         coeff_full = all_gather_columns(coefficients, "pair")
         partial = contract_first(screened, coeff_full)

time: 172 us -> 176 us (1.023)
  other arithmetic: 2.82 us -> 7.26 us
  matrix products: 19.1 us -> 21.5 us
  starting transfers between devices: 86.3 us -> 84 us
    ppermute x30 -> x24, starting transfers between devices: 74.9 us -> 55.6 us  [from_behind(): return lax.ppermute(array, axis, pairs)]
    ppermute x30 -> x24, waiting for transfers between devices: 43.3 us -> 26.4 us  [from_behind(): return lax.ppermute(array, axis, pairs)]
    ppermute x0 -> x7, starting transfers between devices: none -> 16.3 us  [the longest x2 7.07 us: gamma_over_aux(): from_left = lax.ppermute(from_left, 'aux', rightward)]
    ppermute x0 -> x7, waiting for transfers between devices: none -> 11.3 us  [the longest x2 9.56 us: gamma_over_aux(): from_right = lax.ppermute(from_right, 'aux', leftward)]
    ppermute x12, waiting for transfers between devices: 14.3 us -> 18.3 us  [swap(): return lax.ppermute(array, axis, [(i, i ^ bit) for i in range(count)])]
    add x3 -> x6, other arithmetic: 0.2 us -> 2.93 us  [reduce_scatter_columns(): current = keep + swap(send, axis, bit)]
    dot_general x26 -> x25, matrix products: 17 us -> 17.8 us  [product(): jnp.dot(left, right, precision=lax.Precision.HIGH, preferred_element_type...]
  transfers between devices with their start and end apart: 42 -> 43, of which waited for: 23 -> 20; matrix products, arithmetic and copies ran while one was open for 14% -> 17% of each run, Pallas kernels for 0% -> 0%
where the time goes in v13:
time: 176 us; the launch traced here: 175 us
  starting transfers between devices  84 us (48%)
  waiting for transfers between devices  56 us (32%)
  matrix products  21.5 us (12%)
  other arithmetic  7.26 us (4%)
  local copies, waits for them, and re-layouts  5.34 us (3%)
    ppermute x24, starting transfers between devices, from_behind(): return lax.ppermute(array, axis, pairs)  55.6 us
    ppermute x24, waiting for transfers between devices, from_behind(): return lax.ppermute(array, axis, pairs)  26.4 us
    ppermute x12, waiting for transfers between devices, swap(): return lax.ppermute(array, axis, [(i, i ^ bit) for i in range(count)])  18.3 us
    dot_general x25, matrix products, product(): jnp.dot(left, right, precision=lax.Precision.HIGH, preferred_element_type...  17.8 us
    ppermute x12, starting transfers between devices, swap(): return lax.ppermute(array, axis, [(i, i ^ bit) for i in range(count)])  12.1 us
    ppermute x2, waiting for transfers between devices, gamma_over_aux(): from_right = lax.ppermute(from_right, 'aux', leftward)  9.56 us
    ppermute x2, starting transfers between devices, gamma_over_aux(): from_left = lax.ppermute(from_left, 'aux', rightward)  7.07 us
    ppermute x1, starting transfers between devices, gamma_over_aux(): lax.ppermute(columns(jnp.where(index == 0, count - 1, 0)), 'aux', end_pairs)  3.93 us
  transfers between devices with their start and end apart: 43, of which 20 were waited for; matrix products, arithmetic and copies ran while one was open for 17% of the time, Pallas kernels for 0%

profile of v13, /device:TPU:0, one launch (start us, length us, event | category | flops | bytes accessed | tf_op | source)
XLA Modules:
  0.0 175.0 jit_solution(4436835999269465262)
XLA Ops:
  1.4 6.4 %collective-permute-start = (f32[256,512]{1,0:T(8,128)}, f32[256,512]{1,0:T(8,128)}, u32[]{:S(2)}, u32[]{:S(2)}) collective-permute-start(f32[256,512]{1,0:T(8,128)} %param.6), channel_id=1, source_target_pairs={{0,1},{1,2},{2,3},{4,5},{5,6},{6,7},{8,9},{9,10},{10,11},{12,13},{... | collective-permute-start | bytes 1572872 | tf_op jit(solution)/shard_map/ppermute | solution.py:89
  7.8 2.9 %copy.8 = f32[512,1024]{0,1:T(8,128)} copy(f32[512,1024]{1,0:T(8,128)} %param.5) | data formatting | bytes 4194304 | tf_op args[0]
  11.0 1.8 %bitcast_multiply_fusion = f32[512,1024]{0,1:T(8,128)S(1)} fusion(f32[512,1024]{0,1:T(8,128)} %copy.8, f32[512,16]{0,1:T(8,128)S(1)} %reshape.6), kind=kLoop, calls=%fused_computation | loop fusion | flops 524288 | bytes 4227072 | tf_op jit(solution)/shard_map/mul | solution.py:23
  13.7 3.9 %collective-permute-start.4 = (f32[512,256]{0,1:T(8,128)}, f32[512,256]{0,1:T(8,128)}, u32[]{:S(2)}, u32[]{:S(2)}) collective-permute-start(f32[512,256]{0,1:T(8,128)} %constant_dynamic-slice_fusion.4), channel_id=1, source_target_pairs={{0,1},{3,2},{4,5},{7,6},{8,9},{11,10},{12,13},{15,14},{16,17},{19,... | collective-permute-start | bytes 1572872 | tf_op jit(solution)/shard_map/ppermute | solution.py:96
  24.7 9.6 %collective-permute-done.3 = f32[256,512]{1,0:T(8,128)S(1)} collective-permute-done((f32[256,512]{1,0:T(8,128)}, f32[256,512]{1,0:T(8,128)S(1)}, u32[]{:S(2)}, u32[]{:S(2)}) %collective-permute-start.3) | collective-permute-done | bytes 524320 | tf_op jit(solution)/shard_map/ppermute | solution.py:90
  35.7 2.0 %fusion.15 = f32[512,512]{0,1:T(8,128)S(1)} fusion(f32[512,256]{0,1:T(8,128)} %collective-permute-done.4, f32[256,512]{1,0:T(8,128)S(1)} %collective-permute-done.3, f32[256,512]{1,0:T(8,128)S(1)} %collective-permute-done.2, pred[]{:T(512)S(6)} %eq.41), kind=kOutput, calls=%fused_computation.51 | convolution fusion | flops 402784256 | bytes 2621441 | tf_op jit(solution)/shard_map/dot_general | solution.py:27
  46.2 5.8 %collective-permute-done.6 = f32[2,512,64]{1,2,0:T(8,128)S(1)} collective-permute-done((f32[2,512,64]{1,2,0:T(8,128)S(1)}, f32[2,512,64]{1,2,0:T(8,128)S(1)}, u32[]{:S(2)}, u32[]{:S(2)}) %collective-permute-start.6) | collective-permute-done | bytes 262176 | tf_op jit(solution)/shard_map/ppermute | solution.py:15
  53.7 3.0 %collective-permute-done.25 = f32[2,512,64]{1,2,0:T(8,128)S(1)} collective-permute-done((f32[2,512,64]{1,2,0:T(8,128)S(1)}, f32[2,512,64]{1,2,0:T(8,128)S(1)}, u32[]{:S(2)}, u32[]{:S(2)}) %collective-permute-start.25) | collective-permute-done | bytes 262176 | tf_op jit(solution)/shard_map/ppermute | solution.py:15
  59.8 2.1 %collective-permute-done.26 = f32[2,512,32]{1,2,0:T(8,128)S(1)} collective-permute-done((f32[2,512,32]{1,2,0:T(8,128)S(1)}, f32[2,512,32]{1,2,0:T(8,128)S(1)}, u32[]{:S(2)}, u32[]{:S(2)}) %collective-permute-start.26) | collective-permute-done | bytes 131104 | tf_op jit(solution)/shard_map/ppermute | solution.py:15
  63.2 1.7 collective-permute-done.8
  65.5 2.9 %collective-permute-start.9 = (f32[512,32]{0,1:T(8,128)S(1)}, f32[512,32]{0,1:T(8,128)S(1)}, u32[]{:S(2)}, u32[]{:S(2)}) collective-permute-start(f32[512,32]{0,1:T(8,128)S(1)} %convolution_bitcast_fusion.5), channel_id=1, source_target_pairs={{0,1},{1,2},{2,3},{4,5},{5,6},{6,7},{8,9},{9,10},{10,11},{12,13},{... | collective-permute-start | bytes 196616 | tf_op jit(solution)/shard_map/ppermute | solution.py:10
  69.0 4.6 %collective-permute-start.28 = (f32[512,32]{0,1:T(8,128)S(1)}, f32[512,32]{0,1:T(8,128)S(1)}, u32[]{:S(2)}, u32[]{:S(2)}) collective-permute-start(f32[512,32]{0,1:T(8,128)S(1)} %convolution_bitcast_fusion.2), channel_id=1, source_target_pairs={{0,1},{1,2},{2,3},{4,5},{5,6},{6,7},{8,9},{9,10},{10,11},{12,13},{... | collective-permute-start | bytes 196616 | tf_op jit(solution)/shard_map/ppermute | solution.py:10
  74.1 3.0 %collective-permute-start.10 = (f32[512,32]{0,1:T(8,128)S(1)}, f32[512,32]{0,1:T(8,128)S(1)}, u32[]{:S(2)}, u32[]{:S(2)}) collective-permute-start(f32[512,32]{0,1:T(8,128)S(1)} %convolution_add_fusion.12), channel_id=1, source_target_pairs={{0,1},{1,2},{2,3},{4,5},{5,6},{6,7},{8,9},{9,10},{10,11},{12,13},{... | collective-permute-start | bytes 196616 | tf_op jit(solution)/shard_map/ppermute | solution.py:10
  77.7 3.2 %collective-permute-start.29 = (f32[512,32]{0,1:T(8,128)S(1)}, f32[512,32]{0,1:T(8,128)S(1)}, u32[]{:S(2)}, u32[]{:S(2)}) collective-permute-start(f32[512,32]{0,1:T(8,128)S(1)} %convolution_add_fusion.7), channel_id=1, source_target_pairs={{0,1},{1,2},{2,3},{4,5},{5,6},{6,7},{8,9},{9,10},{10,11},{12,13},{... | collective-permute-start | bytes 196616 | tf_op jit(solution)/shard_map/ppermute | solution.py:10
  81.5 2.4 %collective-permute-start.11 = (f32[512,32]{0,1:T(8,128)S(1)}, f32[512,32]{0,1:T(8,128)S(1)}, u32[]{:S(2)}, u32[]{:S(2)}) collective-permute-start(f32[512,32]{0,1:T(8,128)S(1)} %convolution_add_fusion.11), channel_id=1, source_target_pairs={{0,1},{1,2},{2,3},{4,5},{5,6},{6,7},{8,9},{9,10},{10,11},{12,13},{... | collective-permute-start | bytes 196616 | tf_op jit(solution)/shard_map/ppermute | solution.py:10
  84.4 3.2 %collective-permute-start.30 = (f32[512,32]{0,1:T(8,128)S(1)}, f32[512,32]{0,1:T(8,128)S(1)}, u32[]{:S(2)}, u32[]{:S(2)}) collective-permute-start(f32[512,32]{0,1:T(8,128)S(1)} %convolution_add_fusion.6), channel_id=1, source_target_pairs={{0,1},{1,2},{2,3},{4,5},{5,6},{6,7},{8,9},{9,10},{10,11},{12,13},{... | collective-permute-start | bytes 196616 | tf_op jit(solution)/shard_map/ppermute | solution.py:10
  91.4 3.9 %collective-permute-done.12 = f32[512,32]{0,1:T(8,128)S(1)} collective-permute-done((f32[512,32]{0,1:T(8,128)S(1)}, f32[512,32]{0,1:T(8,128)S(1)}, u32[]{:S(2)}, u32[]{:S(2)}) %collective-permute-start.12) | collective-permute-done | bytes 65568 | tf_op jit(solution)/shard_map/ppermute | solution.py:10
  98.7 3.2 %collective-permute-done.13 = f32[512,32]{0,1:T(8,128)S(1)} collective-permute-done((f32[512,32]{0,1:T(8,128)S(1)}, f32[512,32]{0,1:T(8,128)S(1)}, u32[]{:S(2)}, u32[]{:S(2)}) %collective-permute-start.13) | collective-permute-done | bytes 65568 | tf_op jit(solution)/shard_map/ppermute | solution.py:10
  105.9 3.2 %collective-permute-done.14 = f32[512,32]{0,1:T(8,128)S(1)} collective-permute-done((f32[512,32]{0,1:T(8,128)S(1)}, f32[512,32]{0,1:T(8,128)S(1)}, u32[]{:S(2)}, u32[]{:S(2)}) %collective-permute-start.14) | collective-permute-done | bytes 65568 | tf_op jit(solution)/shard_map/ppermute | solution.py:10
  115.4 2.1 %collective-permute-done.33 = f32[512,32]{0,1:T(8,128)S(1)} collective-permute-done((f32[512,32]{0,1:T(8,128)S(1)}, f32[512,32]{0,1:T(8,128)S(1)}, u32[]{:S(2)}, u32[]{:S(2)}) %collective-permute-start.33) | collective-permute-done | bytes 65568 | tf_op jit(solution)/shard_map/ppermute | solution.py:10
  119.5 2.7 %collective-permute-done.34 = f32[512,32]{0,1:T(8,128)S(1)} collective-permute-done((f32[512,32]{0,1:T(8,128)S(1)}, f32[512,32]{0,1:T(8,128)S(1)}, u32[]{:S(2)}, u32[]{:S(2)}) %collective-permute-start.34) | collective-permute-done | bytes 65568 | tf_op jit(solution)/shard_map/ppermute | solution.py:15
  123.8 3.5 %collective-permute-done.35 = f32[512,64]{0,1:T(8,128)S(1)} collective-permute-done((f32[512,64]{0,1:T(8,128)S(1)}, f32[512,64]{0,1:T(8,128)S(1)}, u32[]{:S(2)}, u32[]{:S(2)}) %collective-permute-start.35) | collective-permute-done | bytes 131104 | tf_op jit(solution)/shard_map/ppermute | solution.py:15
  127.4 2.8 %fusion.3 = f32[1024,256]{0,1:T(8,128)S(1)} fusion(f32[512,1024]{0,1:T(8,128)} %copy-done.1, f32[512,128]{0,1:T(8,128)S(1)} %maximum_select_fusion.4, f32[512,128]{0,1:T(8,128)S(1)} %collective-permute-done.17, pred[]{:T(512)S(6)} %eq.37), kind=kOutput, calls=%fused_computation.35 | convolution fusion | flops 805699584 | bytes 3670017 | tf_op jit(solution)/shard_map/dot_general | solution.py:31
  130.3 3.8 %collective-permute-start.18 = (f32[256,256]{0,1:T(8,128)S(1)}, f32[256,256]{0,1:T(8,128)S(1)}, u32[]{:S(2)}, u32[]{:S(2)}) collective-permute-start(f32[256,256]{0,1:T(8,128)S(1)} %get-tuple-element.10), channel_id=1, source_target_pairs={{0,1},{1,2},{2,3},{4,5},{5,6},{6,7},{8,9},{9,10},{10,11},{12,13},{... | collective-permute-start | bytes 786440 | tf_op jit(solution)/shard_map/ppermute | solution.py:10
  136.5 4.6 %collective-permute-start.37 = (f32[256,256]{0,1:T(8,128)S(1)}, f32[256,256]{0,1:T(8,128)S(1)}, u32[]{:S(2)}, u32[]{:S(2)}) collective-permute-start(f32[256,256]{0,1:T(8,128)S(1)} %get-tuple-element.20), channel_id=1, source_target_pairs={{0,1},{1,2},{2,3},{4,5},{5,6},{6,7},{8,9},{9,10},{10,11},{12,13},{... | collective-permute-start | bytes 786440 | tf_op jit(solution)/shard_map/ppermute | solution.py:10
  142.4 1.9 %collective-permute-done.21 = f32[256,256]{0,1:T(8,128)S(1)} collective-permute-done((f32[256,256]{0,1:T(8,128)S(1)}, f32[256,256]{0,1:T(8,128)S(1)}, u32[]{:S(2)}, u32[]{:S(2)}) %collective-permute-start.21) | collective-permute-done | bytes 262176 | tf_op jit(solution)/shard_map/ppermute | solution.py:10
  144.3 2.8 %collective-permute-start.19 = (f32[256,256]{0,1:T(8,128)S(1)}, f32[256,256]{0,1:T(8,128)S(1)}, u32[]{:S(2)}, u32[]{:S(2)}) collective-permute-start(f32[256,256]{0,1:T(8,128)S(1)} %get-tuple-element.8), channel_id=1, source_target_pairs={{0,1},{1,2},{2,3},{4,5},{5,6},{6,7},{8,9},{9,10},{10,11},{12,13},{... | collective-permute-start | bytes 786440 | tf_op jit(solution)/shard_map/ppermute | solution.py:10
  148.4 2.3 %collective-permute-done.40 = f32[256,256]{0,1:T(8,128)S(1)} collective-permute-done((f32[256,256]{0,1:T(8,128)S(1)}, f32[256,256]{0,1:T(8,128)S(1)}, u32[]{:S(2)}, u32[]{:S(2)}) %collective-permute-start.40) | collective-permute-done | bytes 262176 | tf_op jit(solution)/shard_map/ppermute | solution.py:10
  150.8 2.8 %collective-permute-start.38 = (f32[256,256]{0,1:T(8,128)S(1)}, f32[256,256]{0,1:T(8,128)S(1)}, u32[]{:S(2)}, u32[]{:S(2)}) collective-permute-start(f32[256,256]{0,1:T(8,128)S(1)} %get-tuple-element.18), channel_id=1, source_target_pairs={{0,1},{1,2},{2,3},{4,5},{5,6},{6,7},{8,9},{9,10},{10,11},{12,13},{... | collective-permute-start | bytes 786440 | tf_op jit(solution)/shard_map/ppermute | solution.py:10
  156.4 3.3 %collective-permute-start.20 = (f32[256,256]{0,1:T(8,128)S(1)}, f32[256,256]{0,1:T(8,128)S(1)}, u32[]{:S(2)}, u32[]{:S(2)}) collective-permute-start(f32[256,256]{0,1:T(8,128)S(1)} %get-tuple-element.6), channel_id=1, source_target_pairs={{0,1},{1,2},{2,3},{4,5},{5,6},{6,7},{8,9},{9,10},{10,11},{12,13},{... | collective-permute-start | bytes 786440 | tf_op jit(solution)/shard_map/ppermute | solution.py:10
  162.1 3.5 %collective-permute-start.39 = (f32[256,256]{0,1:T(8,128)S(1)}, f32[256,256]{0,1:T(8,128)S(1)}, u32[]{:S(2)}, u32[]{:S(2)}) collective-permute-start(f32[256,256]{0,1:T(8,128)S(1)} %get-tuple-element.16), channel_id=1, source_target_pairs={{0,1},{1,2},{2,3},{4,5},{5,6},{6,7},{8,9},{9,10},{10,11},{12,13},{... | collective-permute-start | bytes 786440 | tf_op jit(solution)/shard_map/ppermute | solution.py:10
  169.5 4.4 %collective-permute-done.42 = f32[256,256]{0,1:T(8,128)S(1)} collective-permute-done((f32[256,256]{0,1:T(8,128)S(1)}, f32[256,256]{0,1:T(8,128)S(1)}, u32[]{:S(2)}, u32[]{:S(2)}) %collective-permute-start.42) | collective-permute-done | bytes 262176 | tf_op jit(solution)/shard_map/ppermute | solution.py:10
  (140 shorter events, 65.0 us)
Async XLA Ops:
  0.0 19.3 %collective-permute-start.1 = (f32[256,512]{1,0:T(8,128)}, f32[256,512]{1,0:T(8,128)}, u32[]{:S(2)}, u32[]{:S(2)}) collective-permute-start(f32[256,512]{1,0:T(8,128)} %param.6), channel_id=1, source_target_pairs={{1,0},{2,1},{3,2},{5,4},{6,5},{7,6},{9,8},{10,9},{11,10},{13,12},{... | collective-permute-start | bytes 1572872 | tf_op jit(solution)/shard_map/ppermute | solution.py:90
  1.4 19.2 %collective-permute-start = (f32[256,512]{1,0:T(8,128)}, f32[256,512]{1,0:T(8,128)}, u32[]{:S(2)}, u32[]{:S(2)}) collective-permute-start(f32[256,512]{1,0:T(8,128)} %param.6), channel_id=1, source_target_pairs={{0,1},{1,2},{2,3},{4,5},{5,6},{6,7},{8,9},{9,10},{10,11},{12,13},{... | collective-permute-start | bytes 1572872 | tf_op jit(solution)/shard_map/ppermute | solution.py:89
  13.7 21.9 %collective-permute-start.4 = (f32[512,256]{0,1:T(8,128)}, f32[512,256]{0,1:T(8,128)}, u32[]{:S(2)}, u32[]{:S(2)}) collective-permute-start(f32[512,256]{0,1:T(8,128)} %constant_dynamic-slice_fusion.4), channel_id=1, source_target_pairs={{0,1},{3,2},{4,5},{7,6},{8,9},{11,10},{12,13},{15,14},{16,17},{19,... | collective-permute-start | bytes 1572872 | tf_op jit(solution)/shard_map/ppermute | solution.py:96
  19.3 14.9 %collective-permute-start.3 = (f32[256,512]{1,0:T(8,128)}, f32[256,512]{1,0:T(8,128)S(1)}, u32[]{:S(2)}, u32[]{:S(2)}) collective-permute-start(f32[256,512]{1,0:T(8,128)} %collective-permute-done.1), channel_id=1, source_target_pairs={{1,0},{2,1},{5,4},{6,5},{9,8},{10,9},{13,12},{14,13},{17,16},{18,1... | collective-permute-start | bytes 1572872 | tf_op jit(solution)/shard_map/ppermute | solution.py:90
  20.6 14.2 %collective-permute-start.2 = (f32[256,512]{1,0:T(8,128)}, f32[256,512]{1,0:T(8,128)S(1)}, u32[]{:S(2)}, u32[]{:S(2)}) collective-permute-start(f32[256,512]{1,0:T(8,128)} %collective-permute-done), channel_id=1, source_target_pairs={{1,2},{2,3},{5,6},{6,7},{9,10},{10,11},{13,14},{14,15},{17,18},{18... | collective-permute-start | bytes 1572872 | tf_op jit(solution)/shard_map/ppermute | solution.py:89
  42.8 9.2 %collective-permute-start.6 = (f32[2,512,64]{1,2,0:T(8,128)S(1)}, f32[2,512,64]{1,2,0:T(8,128)S(1)}, u32[]{:S(2)}, u32[]{:S(2)}) collective-permute-start(f32[2,512,64]{1,2,0:T(8,128)S(1)} %slice_select_fusion.1), channel_id=1, source_target_pairs={{0,8},{4,12},{8,0},{12,4},{16,24},{20,28},{24,16},{28,20},{1,9},{5... | collective-permute-start | bytes 786440 | tf_op jit(solution)/shard_map/ppermute | solution.py:15
  45.6 11.1 %collective-permute-start.25 = (f32[2,512,64]{1,2,0:T(8,128)S(1)}, f32[2,512,64]{1,2,0:T(8,128)S(1)}, u32[]{:S(2)}, u32[]{:S(2)}) collective-permute-start(f32[2,512,64]{1,2,0:T(8,128)S(1)} %slice_select_fusion), channel_id=1, source_target_pairs={{0,8},{4,12},{8,0},{12,4},{16,24},{20,28},{24,16},{28,20},{1,9},{5... | collective-permute-start | bytes 786440 | tf_op jit(solution)/shard_map/ppermute | solution.py:15
  52.2 6.3 %collective-permute-start.7 = (f32[2,512,32]{1,2,0:T(8,128)S(1)}, f32[2,512,32]{1,2,0:T(8,128)S(1)}, u32[]{:S(2)}, u32[]{:S(2)}) collective-permute-start(f32[2,512,32]{1,2,0:T(8,128)S(1)} %slice_select_fusion.3), channel_id=1, source_target_pairs={{0,16},{4,20},{8,24},{12,28},{16,0},{20,4},{24,8},{28,12},{1,17},{... | collective-permute-start | bytes 393224 | tf_op jit(solution)/shard_map/ppermute | solution.py:15
  58.5 6.4 %collective-permute-start.8 = (f32[512,32]{0,1:T(8,128)S(1)}, f32[512,32]{0,1:T(8,128)S(1)}, u32[]{:S(2)}, u32[]{:S(2)}) collective-permute-start(f32[512,32]{0,1:T(8,128)S(1)} %slice_bitcast_fusion.6), channel_id=1, source_target_pairs={{1,0},{2,3},{5,4},{6,7},{9,8},{10,11},{13,12},{14,15},{17,16},{18,... | collective-permute-start | bytes 196616 | tf_op jit(solution)/shard_map/ppermute | solution.py:105
  61.9 6.4 %collective-permute-start.27 = (f32[512,32]{0,1:T(8,128)S(1)}, f32[512,32]{0,1:T(8,128)S(1)}, u32[]{:S(2)}, u32[]{:S(2)}) collective-permute-start(f32[512,32]{0,1:T(8,128)S(1)} %slice_bitcast_fusion.4), channel_id=1, source_target_pairs={{1,0},{2,3},{5,4},{6,7},{9,8},{10,11},{13,12},{14,15},{17,16},{18,... | collective-permute-start | bytes 196616 | tf_op jit(solution)/shard_map/ppermute | solution.py:105
  65.5 8.1 %collective-permute-start.9 = (f32[512,32]{0,1:T(8,128)S(1)}, f32[512,32]{0,1:T(8,128)S(1)}, u32[]{:S(2)}, u32[]{:S(2)}) collective-permute-start(f32[512,32]{0,1:T(8,128)S(1)} %convolution_bitcast_fusion.5), channel_id=1, source_target_pairs={{0,1},{1,2},{2,3},{4,5},{5,6},{6,7},{8,9},{9,10},{10,11},{12,13},{... | collective-permute-start | bytes 196616 | tf_op jit(solution)/shard_map/ppermute | solution.py:10
  69.0 8.2 %collective-permute-start.28 = (f32[512,32]{0,1:T(8,128)S(1)}, f32[512,32]{0,1:T(8,128)S(1)}, u32[]{:S(2)}, u32[]{:S(2)}) collective-permute-start(f32[512,32]{0,1:T(8,128)S(1)} %convolution_bitcast_fusion.2), channel_id=1, source_target_pairs={{0,1},{1,2},{2,3},{4,5},{5,6},{6,7},{8,9},{9,10},{10,11},{12,13},{... | collective-permute-start | bytes 196616 | tf_op jit(solution)/shard_map/ppermute | solution.py:10
  74.1 6.8 %collective-permute-start.10 = (f32[512,32]{0,1:T(8,128)S(1)}, f32[512,32]{0,1:T(8,128)S(1)}, u32[]{:S(2)}, u32[]{:S(2)}) collective-permute-start(f32[512,32]{0,1:T(8,128)S(1)} %convolution_add_fusion.12), channel_id=1, source_target_pairs={{0,1},{1,2},{2,3},{4,5},{5,6},{6,7},{8,9},{9,10},{10,11},{12,13},{... | collective-permute-start | bytes 196616 | tf_op jit(solution)/shard_map/ppermute | solution.py:10
  89.0 6.4 %collective-permute-start.12 = (f32[512,32]{0,1:T(8,128)S(1)}, f32[512,32]{0,1:T(8,128)S(1)}, u32[]{:S(2)}, u32[]{:S(2)}) collective-permute-start(f32[512,32]{0,1:T(8,128)S(1)} %convolution_bitcast_fusion.4), channel_id=1, source_target_pairs={{1,0},{2,1},{3,2},{5,4},{6,5},{7,6},{9,8},{10,9},{11,10},{13,12},{... | collective-permute-start | bytes 196616 | tf_op jit(solution)/shard_map/ppermute | solution.py:10
  95.7 6.2 %collective-permute-start.13 = (f32[512,32]{0,1:T(8,128)S(1)}, f32[512,32]{0,1:T(8,128)S(1)}, u32[]{:S(2)}, u32[]{:S(2)}) collective-permute-start(f32[512,32]{0,1:T(8,128)S(1)} %convolution_add_fusion.9), channel_id=1, source_target_pairs={{1,0},{2,1},{3,2},{5,4},{6,5},{7,6},{9,8},{10,9},{11,10},{13,12},{... | collective-permute-start | bytes 196616 | tf_op jit(solution)/shard_map/ppermute | solution.py:10
  97.4 6.8 %collective-permute-start.31 = (f32[512,32]{0,1:T(8,128)S(1)}, f32[512,32]{0,1:T(8,128)S(1)}, u32[]{:S(2)}, u32[]{:S(2)}) collective-permute-start(f32[512,32]{0,1:T(8,128)S(1)} %convolution_bitcast_fusion.1), channel_id=1, source_target_pairs={{1,0},{2,1},{3,2},{5,4},{6,5},{7,6},{9,8},{10,9},{11,10},{13,12},{... | collective-permute-start | bytes 196616 | tf_op jit(solution)/shard_map/ppermute | solution.py:10
  102.3 6.8 %collective-permute-start.14 = (f32[512,32]{0,1:T(8,128)S(1)}, f32[512,32]{0,1:T(8,128)S(1)}, u32[]{:S(2)}, u32[]{:S(2)}) collective-permute-start(f32[512,32]{0,1:T(8,128)S(1)} %convolution_add_fusion.8), channel_id=1, source_target_pairs={{1,0},{2,1},{3,2},{5,4},{6,5},{7,6},{9,8},{10,9},{11,10},{13,12},{... | collective-permute-start | bytes 196616 | tf_op jit(solution)/shard_map/ppermute | solution.py:10
  104.6 6.3 %collective-permute-start.32 = (f32[512,32]{0,1:T(8,128)S(1)}, f32[512,32]{0,1:T(8,128)S(1)}, u32[]{:S(2)}, u32[]{:S(2)}) collective-permute-start(f32[512,32]{0,1:T(8,128)S(1)} %convolution_add_fusion.4), channel_id=1, source_target_pairs={{1,0},{2,1},{3,2},{5,4},{6,5},{7,6},{9,8},{10,9},{11,10},{13,12},{... | collective-permute-start | bytes 196616 | tf_op jit(solution)/shard_map/ppermute | solution.py:10
  119.5 8.0 %collective-permute-start.17 = (f32[512,128]{0,1:T(8,128)S(1)}, f32[512,128]{0,1:T(8,128)S(1)}, u32[]{:S(2)}, u32[]{:S(2)}) collective-permute-start(f32[512,128]{0,1:T(8,128)S(1)} %maximum_select_fusion.4), channel_id=1, source_target_pairs={{0,4},{4,0},{8,12},{12,8},{16,20},{20,16},{24,28},{28,24},{1,5},{5... | collective-permute-start | bytes 786440 | tf_op jit(solution)/shard_map/ppermute | solution.py:15
  127.4 8.0 %collective-permute-start.36 = (f32[512,128]{0,1:T(8,128)S(1)}, f32[512,128]{0,1:T(8,128)S(1)}, u32[]{:S(2)}, u32[]{:S(2)}) collective-permute-start(f32[512,128]{0,1:T(8,128)S(1)} %maximum_select_fusion.5), channel_id=1, source_target_pairs={{0,4},{4,0},{8,12},{12,8},{16,20},{20,16},{24,28},{28,24},{1,5},{5... | collective-permute-start | bytes 786440 | tf_op jit(solution)/shard_map/ppermute | solution.py:15
  130.3 12.1 %collective-permute-start.18 = (f32[256,256]{0,1:T(8,128)S(1)}, f32[256,256]{0,1:T(8,128)S(1)}, u32[]{:S(2)}, u32[]{:S(2)}) collective-permute-start(f32[256,256]{0,1:T(8,128)S(1)} %get-tuple-element.10), channel_id=1, source_target_pairs={{0,1},{1,2},{2,3},{4,5},{5,6},{6,7},{8,9},{9,10},{10,11},{12,13},{... | collective-permute-start | bytes 786440 | tf_op jit(solution)/shard_map/ppermute | solution.py:10
  134.1 10.2 %collective-permute-start.21 = (f32[256,256]{0,1:T(8,128)S(1)}, f32[256,256]{0,1:T(8,128)S(1)}, u32[]{:S(2)}, u32[]{:S(2)}) collective-permute-start(f32[256,256]{0,1:T(8,128)S(1)} %get-tuple-element.9), channel_id=1, source_target_pairs={{1,0},{2,1},{3,2},{5,4},{6,5},{7,6},{9,8},{10,9},{11,10},{13,12},{... | collective-permute-start | bytes 786440 | tf_op jit(solution)/shard_map/ppermute | solution.py:10
  136.5 11.9 %collective-permute-start.37 = (f32[256,256]{0,1:T(8,128)S(1)}, f32[256,256]{0,1:T(8,128)S(1)}, u32[]{:S(2)}, u32[]{:S(2)}) collective-permute-start(f32[256,256]{0,1:T(8,128)S(1)} %get-tuple-element.20), channel_id=1, source_target_pairs={{0,1},{1,2},{2,3},{4,5},{5,6},{6,7},{8,9},{9,10},{10,11},{12,13},{... | collective-permute-start | bytes 786440 | tf_op jit(solution)/shard_map/ppermute | solution.py:10
  141.0 9.7 %collective-permute-start.40 = (f32[256,256]{0,1:T(8,128)S(1)}, f32[256,256]{0,1:T(8,128)S(1)}, u32[]{:S(2)}, u32[]{:S(2)}) collective-permute-start(f32[256,256]{0,1:T(8,128)S(1)} %get-tuple-element.19), channel_id=1, source_target_pairs={{1,0},{2,1},{3,2},{5,4},{6,5},{7,6},{9,8},{10,9},{11,10},{13,12},{... | collective-permute-start | bytes 786440 | tf_op jit(solution)/shard_map/ppermute | solution.py:10
  144.3 10.6 %collective-permute-start.19 = (f32[256,256]{0,1:T(8,128)S(1)}, f32[256,256]{0,1:T(8,128)S(1)}, u32[]{:S(2)}, u32[]{:S(2)}) collective-permute-start(f32[256,256]{0,1:T(8,128)S(1)} %get-tuple-element.8), channel_id=1, source_target_pairs={{0,1},{1,2},{2,3},{4,5},{5,6},{6,7},{8,9},{9,10},{10,11},{12,13},{... | collective-permute-start | bytes 786440 | tf_op jit(solution)/shard_map/ppermute | solution.py:10
  147.1 9.2 %collective-permute-start.22 = (f32[256,256]{0,1:T(8,128)S(1)}, f32[256,256]{0,1:T(8,128)S(1)}, u32[]{:S(2)}, u32[]{:S(2)}) collective-permute-start(f32[256,256]{0,1:T(8,128)S(1)} %get-tuple-element.7), channel_id=1, source_target_pairs={{1,0},{2,1},{3,2},{5,4},{6,5},{7,6},{9,8},{10,9},{11,10},{13,12},{... | collective-permute-start | bytes 786440 | tf_op jit(solution)/shard_map/ppermute | solution.py:10
  150.8 10.2 %collective-permute-start.38 = (f32[256,256]{0,1:T(8,128)S(1)}, f32[256,256]{0,1:T(8,128)S(1)}, u32[]{:S(2)}, u32[]{:S(2)}) collective-permute-start(f32[256,256]{0,1:T(8,128)S(1)} %get-tuple-element.18), channel_id=1, source_target_pairs={{0,1},{1,2},{2,3},{4,5},{5,6},{6,7},{8,9},{9,10},{10,11},{12,13},{... | collective-permute-start | bytes 786440 | tf_op jit(solution)/shard_map/ppermute | solution.py:10
  153.6 8.4 %collective-permute-start.41 = (f32[256,256]{0,1:T(8,128)S(1)}, f32[256,256]{0,1:T(8,128)S(1)}, u32[]{:S(2)}, u32[]{:S(2)}) collective-permute-start(f32[256,256]{0,1:T(8,128)S(1)} %get-tuple-element.17), channel_id=1, source_target_pairs={{1,0},{2,1},{3,2},{5,4},{6,5},{7,6},{9,8},{10,9},{11,10},{13,12},{... | collective-permute-start | bytes 786440 | tf_op jit(solution)/shard_map/ppermute | solution.py:10
  156.4 10.6 %collective-permute-start.20 = (f32[256,256]{0,1:T(8,128)S(1)}, f32[256,256]{0,1:T(8,128)S(1)}, u32[]{:S(2)}, u32[]{:S(2)}) collective-permute-start(f32[256,256]{0,1:T(8,128)S(1)} %get-tuple-element.6), channel_id=1, source_target_pairs={{0,1},{1,2},{2,3},{4,5},{5,6},{6,7},{8,9},{9,10},{10,11},{12,13},{... | collective-permute-start | bytes 786440 | tf_op jit(solution)/shard_map/ppermute | solution.py:10
  159.7 8.9 %collective-permute-start.23 = (f32[256,256]{0,1:T(8,128)S(1)}, f32[256,256]{0,1:T(8,128)S(1)}, u32[]{:S(2)}, u32[]{:S(2)}) collective-permute-start(f32[256,256]{0,1:T(8,128)S(1)} %get-tuple-element.5), channel_id=1, source_target_pairs={{1,0},{2,1},{3,2},{5,4},{6,5},{7,6},{9,8},{10,9},{11,10},{13,12},{... | collective-permute-start | bytes 786440 | tf_op jit(solution)/shard_map/ppermute | solution.py:10
  162.1 7.4 %collective-permute-start.39 = (f32[256,256]{0,1:T(8,128)S(1)}, f32[256,256]{0,1:T(8,128)S(1)}, u32[]{:S(2)}, u32[]{:S(2)}) collective-permute-start(f32[256,256]{0,1:T(8,128)S(1)} %get-tuple-element.16), channel_id=1, source_target_pairs={{0,1},{1,2},{2,3},{4,5},{5,6},{6,7},{8,9},{9,10},{10,11},{12,13},{... | collective-permute-start | bytes 786440 | tf_op jit(solution)/shard_map/ppermute | solution.py:10
  165.7 8.3 %collective-permute-start.42 = (f32[256,256]{0,1:T(8,128)S(1)}, f32[256,256]{0,1:T(8,128)S(1)}, u32[]{:S(2)}, u32[]{:S(2)}) collective-permute-start(f32[256,256]{0,1:T(8,128)S(1)} %get-tuple-element.15), channel_id=1, source_target_pairs={{1,0},{2,1},{3,2},{5,4},{6,5},{7,6},{9,8},{10,9},{11,10},{13,12},{... | collective-permute-start | bytes 786440 | tf_op jit(solution)/shard_map/ppermute | solution.py:10
  (22 other events, 146.9 us)

commit v14 on v5

--- a/solution.py
+++ b/solution.py
@@ -154,12 +154,11 @@
     transfer = -product(diag_inverse, sub_factor)
     previous_map, next_map = neighbour_maps(transfer)
     two_step = product(transfer, previous_map)
-    width = densities.shape[1] // SLICES
+    gamma_partial = gamma_over_aux(screened, densities)
+    width = gamma_partial.shape[1] // SLICES
     results = []
     for part in range(SLICES):
-        dens_part = densities[:, part * width:(part + 1) * width]
-        gamma_partial = gamma_over_aux(screened, dens_part)
-        right_side = reduce_scatter_columns(gamma_partial, "pair")
+        right_side = reduce_scatter_columns(gamma_partial[:, part * width:(part + 1) * width], "pair")
         coefficients = solve(right_side, transfer, two_step, next_map, diag_inverse)
         coeff_full = all_gather_columns(coefficients, "pair")
         partial = contract_first(screened, coeff_full)

time: 184 us -> 176 us (0.957)
  starting transfers between devices: 107 us -> 96.6 us
  waiting for transfers between devices: 39.6 us -> 44.6 us
  matrix products: 24.9 us -> 21.8 us
    ppermute x36 -> x30, starting transfers between devices: 97.3 us -> 83.4 us  [from_behind(): return lax.ppermute(array, axis, pairs)]
    ppermute x15, starting transfers between devices: 9.79 us -> 13.2 us  [swap(): return lax.ppermute(array, axis, [(i, i ^ bit) for i in range(count)])]
    ppermute x36 -> x30, waiting for transfers between devices: 22.5 us -> 25.6 us  [from_behind(): return lax.ppermute(array, axis, pairs)]
    dot_general x32 -> x25, matrix products: 22.8 us -> 19.7 us  [product(): jnp.dot(left, right, precision=lax.Precision.HIGH, preferred_element_type...]
    unnamed x13 -> x9, local copies, waits for them, and re-layouts: 2.95 us -> 5.16 us
    slice x1 -> x0, local copies, waits for them, and re-layouts: 1.96 us -> none  [per_device(): dens_part = densities[:, part * width:(part + 1) * width]]
  transfers between devices with their start and end apart: 51 -> 45, of which waited for: 20 -> 21; matrix products, arithmetic and copies ran while one was open for 18% -> 15% of each run, Pallas kernels for 0% -> 0%
where the time goes in v14:
time: 176 us; the launch traced here: 175 us
  starting transfers between devices  96.6 us (55%)
  waiting for transfers between devices  44.6 us (25%)
  matrix products  21.8 us (12%)
  local copies, waits for them, and re-layouts  7.41 us (4%)
  other arithmetic  3.4 us (2%)
    ppermute x30, starting transfers between devices, from_behind(): return lax.ppermute(array, axis, pairs)  83.4 us
    ppermute x30, waiting for transfers between devices, from_behind(): return lax.ppermute(array, axis, pairs)  25.6 us
    dot_general x25, matrix products, product(): jnp.dot(left, right, precision=lax.Precision.HIGH, preferred_element_type...  19.7 us
    ppermute x15, waiting for transfers between devices, swap(): return lax.ppermute(array, axis, [(i, i ^ bit) for i in range(count)])  18.9 us
    ppermute x15, starting transfers between devices, swap(): return lax.ppermute(array, axis, [(i, i ^ bit) for i in range(count)])  13.2 us
    unnamed x9, local copies, waits for them, and re-layouts  5.16 us
  transfers between devices with their start and end apart: 45, of which 21 were waited for; matrix products, arithmetic and copies ran while one was open for 15% of the time, Pallas kernels for 0%

profile of v14, /device:TPU:0, one launch (start us, length us, event | category | flops | bytes accessed | tf_op | source)
XLA Modules:
  0.0 174.6 jit_solution(16973837190370089988)
XLA Ops:
  1.2 2.2 %convolution_negate_fusion = f32[512,512]{0,1:T(8,128)S(1)} fusion(f32[512,512]{1,0:T(8,128)S(1)} %copy-done, f32[512,512]{1,0:T(8,128)} %param.9), kind=kOutput, calls=%fused_computation.2 | convolution fusion | flops 805568512 | bytes 3145728 | tf_op jit(solution)/shard_map/dot_general | solution.py:27
  5.5 5.6 %collective-permute-start.10 = (f32[512,64]{0,1:T(8,128)}, f32[512,64]{0,1:T(8,128)S(1)}, u32[]{:S(2)}, u32[]{:S(2)}) collective-permute-start(f32[512,64]{0,1:T(8,128)} %constant_dynamic-slice_fusion.4), channel_id=1, source_target_pairs={{0,1},{1,2},{2,3},{4,5},{5,6},{6,7},{8,9},{9,10},{10,11},{12,13},{... | collective-permute-start | bytes 393224 | tf_op jit(solution)/shard_map/ppermute | solution.py:10
  12.4 5.4 %collective-permute-start = (f32[256,512]{1,0:T(8,128)}, f32[256,512]{1,0:T(8,128)}, u32[]{:S(2)}, u32[]{:S(2)}) collective-permute-start(f32[256,512]{1,0:T(8,128)} %param.6), channel_id=1, source_target_pairs={{0,1},{1,2},{2,3},{4,5},{5,6},{6,7},{8,9},{9,10},{10,11},{12,13},{... | collective-permute-start | bytes 1572872 | tf_op jit(solution)/shard_map/ppermute | solution.py:10
  17.8 2.9 %copy.8 = f32[512,1024]{0,1:T(8,128)} copy(f32[512,1024]{1,0:T(8,128)} %param.5) | data formatting | bytes 4194304 | tf_op args[0]
  20.9 1.8 %bitcast_multiply_fusion = f32[512,1024]{0,1:T(8,128)S(1)} fusion(f32[512,1024]{0,1:T(8,128)} %copy.8, f32[512,16]{0,1:T(8,128)S(1)} %reshape.19), kind=kLoop, calls=%fused_computation.1 | loop fusion | flops 524288 | bytes 4227072 | tf_op jit(solution)/shard_map/mul | solution.py:23
  22.8 2.0 %collective-permute-start.12 = (f32[512,128]{0,1:T(8,128)S(1)}, f32[512,128]{0,1:T(8,128)S(1)}, u32[]{:S(2)}, u32[]{:S(2)}) collective-permute-start(f32[512,128]{0,1:T(8,128)S(1)} %pad_maximum_fusion.1), channel_id=1, source_target_pairs={{0,16},{4,20},{8,24},{12,28},{16,0},{20,4},{24,8},{28,12},{1,17},{... | collective-permute-start | bytes 786440 | tf_op jit(solution)/shard_map/ppermute | solution.py:15
  26.5 3.6 %collective-permute-done.12 = f32[512,128]{0,1:T(8,128)S(1)} collective-permute-done((f32[512,128]{0,1:T(8,128)S(1)}, f32[512,128]{0,1:T(8,128)S(1)}, u32[]{:S(2)}, u32[]{:S(2)}) %collective-permute-start.12) | collective-permute-done | bytes 262176 | tf_op jit(solution)/shard_map/ppermute | solution.py:15
  30.1 1.7 collective-permute-start.13
  33.2 4.6 %collective-permute-start.2 = (f32[256,512]{1,0:T(8,128)}, f32[256,512]{1,0:T(8,128)S(1)}, u32[]{:S(2)}, u32[]{:S(2)}) collective-permute-start(f32[256,512]{1,0:T(8,128)} %collective-permute-done), channel_id=1, source_target_pairs={{0,1},{1,2},{2,3},{4,5},{5,6},{6,7},{8,9},{9,10},{10,11},{12,13},{... | collective-permute-start | bytes 1572872 | tf_op jit(solution)/shard_map/ppermute | solution.py:10
  37.7 1.7 convolution_add_fusion.3
  39.4 1.7 convolution_add_fusion.2
  41.1 4.2 %collective-permute-done.3 = f32[256,512]{1,0:T(8,128)S(1)} collective-permute-done((f32[256,512]{1,0:T(8,128)}, f32[256,512]{1,0:T(8,128)S(1)}, u32[]{:S(2)}, u32[]{:S(2)}) %collective-permute-start.3) | collective-permute-done | bytes 524320 | tf_op jit(solution)/shard_map/ppermute | solution.py:10
  46.6 4.6 %collective-permute-start.4 = (f32[256,512]{1,0:T(8,128)S(1)}, f32[256,512]{1,0:T(8,128)S(1)}, u32[]{:S(2)}, u32[]{:S(2)}) collective-permute-start(f32[256,512]{1,0:T(8,128)S(1)} %collective-permute-done.2), channel_id=1, source_target_pairs={{0,1},{1,2},{2,3},{4,5},{5,6},{6,7},{8,9},{9,10},{10,11},{12,13},{... | collective-permute-start | bytes 1572872 | tf_op jit(solution)/shard_map/ppermute | solution.py:10
  52.5 5.3 %collective-permute-done.5 = f32[256,512]{1,0:T(8,128)S(1)} collective-permute-done((f32[256,512]{1,0:T(8,128)S(1)}, f32[256,512]{1,0:T(8,128)S(1)}, u32[]{:S(2)}, u32[]{:S(2)}) %collective-permute-start.5) | collective-permute-done | bytes 524320 | tf_op jit(solution)/shard_map/ppermute | solution.py:10
  64.1 4.2 %collective-permute-done.29 = f32[512,64]{0,1:T(8,128)S(1)} collective-permute-done((f32[512,64]{0,1:T(8,128)S(1)}, f32[512,64]{0,1:T(8,128)S(1)}, u32[]{:S(2)}, u32[]{:S(2)}) %collective-permute-start.29) | collective-permute-done | bytes 131104 | tf_op jit(solution)/shard_map/ppermute | solution.py:15
  73.5 1.9 %fusion.50 = f32[512,512]{1,0:T(8,128)S(1)} fusion(f32[512,512]{0,1:T(8,128)S(1)} %copy-done.2, f32[512,512]{0,1:T(8,128)S(1)} %bitcast.67), kind=kOutput, calls=%fused_computation.107 | convolution fusion | flops 805306368 | bytes 3145728 | tf_op jit(solution)/shard_map/dot_general | solution.py:27
  76.0 4.4 %collective-permute-start.31 = (f32[512,32]{0,1:T(8,128)S(1)}, f32[512,32]{0,1:T(8,128)S(1)}, u32[]{:S(2)}, u32[]{:S(2)}) collective-permute-start(f32[512,32]{0,1:T(8,128)S(1)} %convolution_bitcast_fusion.1), channel_id=1, source_target_pairs={{0,1},{1,2},{2,3},{4,5},{5,6},{6,7},{8,9},{9,10},{10,11},{12,13},{... | collective-permute-start | bytes 196616 | tf_op jit(solution)/shard_map/ppermute | solution.py:10
  82.3 4.5 %collective-permute-start.9 = (f32[512,32]{0,1:T(8,128)S(1)}, f32[512,32]{0,1:T(8,128)S(1)}, u32[]{:S(2)}, u32[]{:S(2)}) collective-permute-start(f32[512,32]{0,1:T(8,128)S(1)} %convolution_bitcast_fusion.3), channel_id=1, source_target_pairs={{0,1},{1,2},{2,3},{4,5},{5,6},{6,7},{8,9},{9,10},{10,11},{12,13},{... | collective-permute-start | bytes 196616 | tf_op jit(solution)/shard_map/ppermute | solution.py:10
  88.7 5.7 %collective-permute-start.32 = (f32[512,32]{0,1:T(8,128)S(1)}, f32[512,32]{0,1:T(8,128)S(1)}, u32[]{:S(2)}, u32[]{:S(2)}) collective-permute-start(f32[512,32]{0,1:T(8,128)S(1)} %convolution_add_fusion.7), channel_id=1, source_target_pairs={{0,2},{1,3},{4,6},{5,7},{8,10},{9,11},{12,14},{13,15},{16,18},{17,... | collective-permute-start | bytes 196616 | tf_op jit(solution)/shard_map/ppermute | solution.py:10
  102.1 2.7 %collective-permute-done.34 = f32[512,32]{0,1:T(8,128)S(1)} collective-permute-done((f32[512,32]{0,1:T(8,128)S(1)}, f32[512,32]{0,1:T(8,128)S(1)}, u32[]{:S(2)}, u32[]{:S(2)}) %collective-permute-start.34) | collective-permute-done | bytes 65568 | tf_op jit(solution)/shard_map/ppermute | solution.py:10
  109.5 2.0 %collective-permute-done.35 = f32[512,32]{0,1:T(8,128)S(1)} collective-permute-done((f32[512,32]{0,1:T(8,128)S(1)}, f32[512,32]{0,1:T(8,128)S(1)}, u32[]{:S(2)}, u32[]{:S(2)}) %collective-permute-start.35) | collective-permute-done | bytes 65568 | tf_op jit(solution)/shard_map/ppermute | solution.py:10
  114.9 1.8 %collective-permute-done.36 = f32[512,32]{0,1:T(8,128)S(1)} collective-permute-done((f32[512,32]{0,1:T(8,128)S(1)}, f32[512,32]{0,1:T(8,128)S(1)}, u32[]{:S(2)}, u32[]{:S(2)}) %collective-permute-start.36) | collective-permute-done | bytes 65568 | tf_op jit(solution)/shard_map/ppermute | solution.py:15
  118.4 3.4 %collective-permute-done.37 = f32[512,64]{0,1:T(8,128)S(1)} collective-permute-done((f32[512,64]{0,1:T(8,128)S(1)}, f32[512,64]{0,1:T(8,128)S(1)}, u32[]{:S(2)}, u32[]{:S(2)}) %collective-permute-start.37) | collective-permute-done | bytes 131104 | tf_op jit(solution)/shard_map/ppermute | solution.py:15
  123.7 4.2 %collective-permute-done.20 = f32[512,64]{0,1:T(8,128)S(1)} collective-permute-done((f32[512,64]{0,1:T(8,128)S(1)}, f32[512,64]{0,1:T(8,128)S(1)}, u32[]{:S(2)}, u32[]{:S(2)}) %collective-permute-start.20) | collective-permute-done | bytes 131104 | tf_op jit(solution)/shard_map/ppermute | solution.py:15
  130.4 4.6 %collective-permute-start.39 = (f32[256,256]{0,1:T(8,128)S(1)}, f32[256,256]{0,1:T(8,128)S(1)}, u32[]{:S(2)}, u32[]{:S(2)}) collective-permute-start(f32[256,256]{0,1:T(8,128)S(1)} %get-tuple-element.22), channel_id=1, source_target_pairs={{0,1},{1,2},{2,3},{4,5},{5,6},{6,7},{8,9},{9,10},{10,11},{12,13},{... | collective-permute-start | bytes 786440 | tf_op jit(solution)/shard_map/ppermute | solution.py:10
  137.4 4.6 %collective-permute-start.22 = (f32[256,256]{0,1:T(8,128)S(1)}, f32[256,256]{0,1:T(8,128)S(1)}, u32[]{:S(2)}, u32[]{:S(2)}) collective-permute-start(f32[256,256]{0,1:T(8,128)S(1)} %get-tuple-element.12), channel_id=1, source_target_pairs={{0,1},{1,2},{2,3},{4,5},{5,6},{6,7},{8,9},{9,10},{10,11},{12,13},{... | collective-permute-start | bytes 786440 | tf_op jit(solution)/shard_map/ppermute | solution.py:10
  143.4 4.6 %collective-permute-start.40 = (f32[256,256]{0,1:T(8,128)S(1)}, f32[256,256]{0,1:T(8,128)S(1)}, u32[]{:S(2)}, u32[]{:S(2)}) collective-permute-start(f32[256,256]{0,1:T(8,128)S(1)} %get-tuple-element.20), channel_id=1, source_target_pairs={{0,1},{1,2},{2,3},{4,5},{5,6},{6,7},{8,9},{9,10},{10,11},{12,13},{... | collective-permute-start | bytes 786440 | tf_op jit(solution)/shard_map/ppermute | solution.py:10
  149.4 4.6 %collective-permute-start.23 = (f32[256,256]{0,1:T(8,128)S(1)}, f32[256,256]{0,1:T(8,128)S(1)}, u32[]{:S(2)}, u32[]{:S(2)}) collective-permute-start(f32[256,256]{0,1:T(8,128)S(1)} %get-tuple-element.10), channel_id=1, source_target_pairs={{0,1},{1,2},{2,3},{4,5},{5,6},{6,7},{8,9},{9,10},{10,11},{12,13},{... | collective-permute-start | bytes 786440 | tf_op jit(solution)/shard_map/ppermute | solution.py:10
  154.1 3.8 %collective-permute-start.41 = (f32[256,256]{0,1:T(8,128)S(1)}, f32[256,256]{0,1:T(8,128)S(1)}, u32[]{:S(2)}, u32[]{:S(2)}) collective-permute-start(f32[256,256]{0,1:T(8,128)S(1)} %get-tuple-element.18), channel_id=1, source_target_pairs={{0,1},{1,2},{2,3},{4,5},{5,6},{6,7},{8,9},{9,10},{10,11},{12,13},{... | collective-permute-start | bytes 786440 | tf_op jit(solution)/shard_map/ppermute | solution.py:10
  160.8 4.4 %collective-permute-start.24 = (f32[256,256]{0,1:T(8,128)S(1)}, f32[256,256]{0,1:T(8,128)S(1)}, u32[]{:S(2)}, u32[]{:S(2)}) collective-permute-start(f32[256,256]{0,1:T(8,128)S(1)} %get-tuple-element.8), channel_id=1, source_target_pairs={{0,1},{1,2},{2,3},{4,5},{5,6},{6,7},{8,9},{9,10},{10,11},{12,13},{... | collective-permute-start | bytes 786440 | tf_op jit(solution)/shard_map/ppermute | solution.py:10
  166.8 3.0 %collective-permute-done.24 = f32[256,256]{0,1:T(8,128)S(1)} collective-permute-done((f32[256,256]{0,1:T(8,128)S(1)}, f32[256,256]{0,1:T(8,128)S(1)}, u32[]{:S(2)}, u32[]{:S(2)}) %collective-permute-start.24) | collective-permute-done | bytes 262176 | tf_op jit(solution)/shard_map/ppermute | solution.py:10
  169.8 3.7 %collective-permute-done.27 = f32[256,256]{0,1:T(8,128)S(1)} collective-permute-done((f32[256,256]{0,1:T(8,128)S(1)}, f32[256,256]{0,1:T(8,128)S(1)}, u32[]{:S(2)}, u32[]{:S(2)}) %collective-permute-start.27) | collective-permute-done | bytes 262176 | tf_op jit(solution)/shard_map/ppermute | solution.py:10
  (128 shorter events, 58.4 us)
Async XLA Ops:
  4.2 18.5 %collective-permute-start.11 = (f32[512,64]{0,1:T(8,128)}, f32[512,64]{0,1:T(8,128)S(1)}, u32[]{:S(2)}, u32[]{:S(2)}) collective-permute-start(f32[512,64]{0,1:T(8,128)} %constant_dynamic-slice_fusion.4), channel_id=1, source_target_pairs={{1,0},{2,1},{3,2},{5,4},{6,5},{7,6},{9,8},{10,9},{11,10},{13,12},{... | collective-permute-start | bytes 393224 | tf_op jit(solution)/shard_map/ppermute | solution.py:10
  5.5 17.3 %collective-permute-start.10 = (f32[512,64]{0,1:T(8,128)}, f32[512,64]{0,1:T(8,128)S(1)}, u32[]{:S(2)}, u32[]{:S(2)}) collective-permute-start(f32[512,64]{0,1:T(8,128)} %constant_dynamic-slice_fusion.4), channel_id=1, source_target_pairs={{0,1},{1,2},{2,3},{4,5},{5,6},{6,7},{8,9},{9,10},{10,11},{12,13},{... | collective-permute-start | bytes 393224 | tf_op jit(solution)/shard_map/ppermute | solution.py:10
  11.1 20.8 %collective-permute-start.1 = (f32[256,512]{1,0:T(8,128)}, f32[256,512]{1,0:T(8,128)}, u32[]{:S(2)}, u32[]{:S(2)}) collective-permute-start(f32[256,512]{1,0:T(8,128)} %param.6), channel_id=1, source_target_pairs={{1,0},{2,1},{3,2},{5,4},{6,5},{7,6},{9,8},{10,9},{11,10},{13,12},{... | collective-permute-start | bytes 1572872 | tf_op jit(solution)/shard_map/ppermute | solution.py:10
  12.4 20.8 %collective-permute-start = (f32[256,512]{1,0:T(8,128)}, f32[256,512]{1,0:T(8,128)}, u32[]{:S(2)}, u32[]{:S(2)}) collective-permute-start(f32[256,512]{1,0:T(8,128)} %param.6), channel_id=1, source_target_pairs={{0,1},{1,2},{2,3},{4,5},{5,6},{6,7},{8,9},{9,10},{10,11},{12,13},{... | collective-permute-start | bytes 1572872 | tf_op jit(solution)/shard_map/ppermute | solution.py:10
  22.8 7.3 %collective-permute-start.12 = (f32[512,128]{0,1:T(8,128)S(1)}, f32[512,128]{0,1:T(8,128)S(1)}, u32[]{:S(2)}, u32[]{:S(2)}) collective-permute-start(f32[512,128]{0,1:T(8,128)S(1)} %pad_maximum_fusion.1), channel_id=1, source_target_pairs={{0,16},{4,20},{8,24},{12,28},{16,0},{20,4},{24,8},{28,12},{1,17},{... | collective-permute-start | bytes 786440 | tf_op jit(solution)/shard_map/ppermute | solution.py:15
  30.1 30.2 %collective-permute-start.13 = (f32[512,256]{0,1:T(8,128)S(1)}, f32[512,256]{0,1:T(8,128)S(1)}, u32[]{:S(2)}, u32[]{:S(2)}) collective-permute-start(f32[512,256]{0,1:T(8,128)S(1)} %maximum_select_fusion.3), channel_id=1, source_target_pairs={{0,8},{4,12},{8,0},{12,4},{16,24},{20,28},{24,16},{28,20},{1,9},{5... | collective-permute-start | bytes 1572872 | tf_op jit(solution)/shard_map/ppermute | solution.py:15
  31.9 13.4 %collective-permute-start.3 = (f32[256,512]{1,0:T(8,128)}, f32[256,512]{1,0:T(8,128)S(1)}, u32[]{:S(2)}, u32[]{:S(2)}) collective-permute-start(f32[256,512]{1,0:T(8,128)} %collective-permute-done.1), channel_id=1, source_target_pairs={{1,0},{2,1},{3,2},{5,4},{6,5},{7,6},{9,8},{10,9},{11,10},{13,12},{... | collective-permute-start | bytes 1572872 | tf_op jit(solution)/shard_map/ppermute | solution.py:10
  33.2 13.4 %collective-permute-start.2 = (f32[256,512]{1,0:T(8,128)}, f32[256,512]{1,0:T(8,128)S(1)}, u32[]{:S(2)}, u32[]{:S(2)}) collective-permute-start(f32[256,512]{1,0:T(8,128)} %collective-permute-done), channel_id=1, source_target_pairs={{0,1},{1,2},{2,3},{4,5},{5,6},{6,7},{8,9},{9,10},{10,11},{12,13},{... | collective-permute-start | bytes 1572872 | tf_op jit(solution)/shard_map/ppermute | solution.py:10
  45.3 12.5 %collective-permute-start.5 = (f32[256,512]{1,0:T(8,128)S(1)}, f32[256,512]{1,0:T(8,128)S(1)}, u32[]{:S(2)}, u32[]{:S(2)}) collective-permute-start(f32[256,512]{1,0:T(8,128)S(1)} %collective-permute-done.3), channel_id=1, source_target_pairs={{1,0},{2,1},{3,2},{5,4},{6,5},{7,6},{9,8},{10,9},{11,10},{13,12},{... | collective-permute-start | bytes 1572872 | tf_op jit(solution)/shard_map/ppermute | solution.py:10
  46.6 12.4 %collective-permute-start.4 = (f32[256,512]{1,0:T(8,128)S(1)}, f32[256,512]{1,0:T(8,128)S(1)}, u32[]{:S(2)}, u32[]{:S(2)}) collective-permute-start(f32[256,512]{1,0:T(8,128)S(1)} %collective-permute-done.2), channel_id=1, source_target_pairs={{0,1},{1,2},{2,3},{4,5},{5,6},{6,7},{8,9},{9,10},{10,11},{12,13},{... | collective-permute-start | bytes 1572872 | tf_op jit(solution)/shard_map/ppermute | solution.py:10
  60.4 11.6 %collective-permute-start.14 = (f32[512,512]{0,1:T(8,128)S(1)}, f32[512,512]{0,1:T(8,128)S(1)}, u32[]{:S(2)}, u32[]{:S(2)}) collective-permute-start(f32[512,512]{0,1:T(8,128)S(1)} %maximum_select_fusion.1), channel_id=1, source_target_pairs={{0,4},{4,0},{8,12},{12,8},{16,20},{20,16},{24,28},{28,24},{1,5},{5... | collective-permute-start | bytes 3145736 | tf_op jit(solution)/shard_map/ppermute | solution.py:15
  62.7 7.6 %collective-permute-start.7 = (f32[512,64]{0,1:T(8,128)S(1)}, f32[512,64]{0,1:T(8,128)S(1)}, u32[]{:S(2)}, u32[]{:S(2)}) collective-permute-start(f32[512,64]{0,1:T(8,128)S(1)} %slice_select_fusion.3), channel_id=1, source_target_pairs={{0,8},{4,12},{8,0},{12,4},{16,24},{20,28},{24,16},{28,20},{1,9},{5... | collective-permute-start | bytes 393224 | tf_op jit(solution)/shard_map/ppermute | solution.py:15
  68.3 7.0 %collective-permute-start.30 = (f32[512,32]{0,1:T(8,128)S(1)}, f32[512,32]{0,1:T(8,128)S(1)}, u32[]{:S(2)}, u32[]{:S(2)}) collective-permute-start(f32[512,32]{0,1:T(8,128)S(1)} %slice_select_fusion.4), channel_id=1, source_target_pairs={{0,16},{4,20},{8,24},{12,28},{16,0},{20,4},{24,8},{28,12},{1,17},{... | collective-permute-start | bytes 196616 | tf_op jit(solution)/shard_map/ppermute | solution.py:15
  70.4 11.3 %collective-permute-start.8 = (f32[512,32]{0,1:T(8,128)S(1)}, f32[512,32]{0,1:T(8,128)S(1)}, u32[]{:S(2)}, u32[]{:S(2)}) collective-permute-start(f32[512,32]{0,1:T(8,128)S(1)} %slice_select_fusion.5), channel_id=1, source_target_pairs={{0,16},{4,20},{8,24},{12,28},{16,0},{20,4},{24,8},{28,12},{1,17},{... | collective-permute-start | bytes 196616 | tf_op jit(solution)/shard_map/ppermute | solution.py:15
  76.0 12.3 %collective-permute-start.31 = (f32[512,32]{0,1:T(8,128)S(1)}, f32[512,32]{0,1:T(8,128)S(1)}, u32[]{:S(2)}, u32[]{:S(2)}) collective-permute-start(f32[512,32]{0,1:T(8,128)S(1)} %convolution_bitcast_fusion.1), channel_id=1, source_target_pairs={{0,1},{1,2},{2,3},{4,5},{5,6},{6,7},{8,9},{9,10},{10,11},{12,13},{... | collective-permute-start | bytes 196616 | tf_op jit(solution)/shard_map/ppermute | solution.py:10
  80.4 16.9 %collective-permute-start.33 = (f32[512,32]{0,1:T(8,128)S(1)}, f32[512,32]{0,1:T(8,128)S(1)}, u32[]{:S(2)}, u32[]{:S(2)}) collective-permute-start(f32[512,32]{0,1:T(8,128)S(1)} %convolution_bitcast_fusion.1), channel_id=1, source_target_pairs={{1,0},{2,1},{3,2},{5,4},{6,5},{7,6},{9,8},{10,9},{11,10},{13,12},{... | collective-permute-start | bytes 196616 | tf_op jit(solution)/shard_map/ppermute | solution.py:10
  82.3 12.2 %collective-permute-start.9 = (f32[512,32]{0,1:T(8,128)S(1)}, f32[512,32]{0,1:T(8,128)S(1)}, u32[]{:S(2)}, u32[]{:S(2)}) collective-permute-start(f32[512,32]{0,1:T(8,128)S(1)} %convolution_bitcast_fusion.3), channel_id=1, source_target_pairs={{0,1},{1,2},{2,3},{4,5},{5,6},{6,7},{8,9},{9,10},{10,11},{12,13},{... | collective-permute-start | bytes 196616 | tf_op jit(solution)/shard_map/ppermute | solution.py:10
  86.8 13.4 %collective-permute-start.16 = (f32[512,32]{0,1:T(8,128)S(1)}, f32[512,32]{0,1:T(8,128)S(1)}, u32[]{:S(2)}, u32[]{:S(2)}) collective-permute-start(f32[512,32]{0,1:T(8,128)S(1)} %convolution_bitcast_fusion.3), channel_id=1, source_target_pairs={{1,0},{2,1},{3,2},{5,4},{6,5},{7,6},{9,8},{10,9},{11,10},{13,12},{... | collective-permute-start | bytes 196616 | tf_op jit(solution)/shard_map/ppermute | solution.py:10
  88.7 7.6 %collective-permute-start.32 = (f32[512,32]{0,1:T(8,128)S(1)}, f32[512,32]{0,1:T(8,128)S(1)}, u32[]{:S(2)}, u32[]{:S(2)}) collective-permute-start(f32[512,32]{0,1:T(8,128)S(1)} %convolution_add_fusion.7), channel_id=1, source_target_pairs={{0,2},{1,3},{4,6},{5,7},{8,10},{9,11},{12,14},{13,15},{16,18},{17,... | collective-permute-start | bytes 196616 | tf_op jit(solution)/shard_map/ppermute | solution.py:10
  127.9 7.1 %collective-permute-start.21 = (f32[512,128]{0,1:T(8,128)S(1)}, f32[512,128]{0,1:T(8,128)S(1)}, u32[]{:S(2)}, u32[]{:S(2)}) collective-permute-start(f32[512,128]{0,1:T(8,128)S(1)} %maximum_select_fusion.8), channel_id=1, source_target_pairs={{0,4},{4,0},{8,12},{12,8},{16,20},{20,16},{24,28},{28,24},{1,5},{5... | collective-permute-start | bytes 786440 | tf_op jit(solution)/shard_map/ppermute | solution.py:15
  129.1 12.9 %collective-permute-start.42 = (f32[256,256]{0,1:T(8,128)S(1)}, f32[256,256]{0,1:T(8,128)S(1)}, u32[]{:S(2)}, u32[]{:S(2)}) collective-permute-start(f32[256,256]{0,1:T(8,128)S(1)} %get-tuple-element.21), channel_id=1, source_target_pairs={{1,0},{2,1},{3,2},{5,4},{6,5},{7,6},{9,8},{10,9},{11,10},{13,12},{... | collective-permute-start | bytes 786440 | tf_op jit(solution)/shard_map/ppermute | solution.py:10
  130.4 11.6 %collective-permute-start.39 = (f32[256,256]{0,1:T(8,128)S(1)}, f32[256,256]{0,1:T(8,128)S(1)}, u32[]{:S(2)}, u32[]{:S(2)}) collective-permute-start(f32[256,256]{0,1:T(8,128)S(1)} %get-tuple-element.22), channel_id=1, source_target_pairs={{0,1},{1,2},{2,3},{4,5},{5,6},{6,7},{8,9},{9,10},{10,11},{12,13},{... | collective-permute-start | bytes 786440 | tf_op jit(solution)/shard_map/ppermute | solution.py:10
  136.1 11.9 %collective-permute-start.25 = (f32[256,256]{0,1:T(8,128)S(1)}, f32[256,256]{0,1:T(8,128)S(1)}, u32[]{:S(2)}, u32[]{:S(2)}) collective-permute-start(f32[256,256]{0,1:T(8,128)S(1)} %get-tuple-element.11), channel_id=1, source_target_pairs={{1,0},{2,1},{3,2},{5,4},{6,5},{7,6},{9,8},{10,9},{11,10},{13,12},{... | collective-permute-start | bytes 786440 | tf_op jit(solution)/shard_map/ppermute | solution.py:10
  137.4 10.6 %collective-permute-start.22 = (f32[256,256]{0,1:T(8,128)S(1)}, f32[256,256]{0,1:T(8,128)S(1)}, u32[]{:S(2)}, u32[]{:S(2)}) collective-permute-start(f32[256,256]{0,1:T(8,128)S(1)} %get-tuple-element.12), channel_id=1, source_target_pairs={{0,1},{1,2},{2,3},{4,5},{5,6},{6,7},{8,9},{9,10},{10,11},{12,13},{... | collective-permute-start | bytes 786440 | tf_op jit(solution)/shard_map/ppermute | solution.py:10
  142.1 11.9 %collective-permute-start.43 = (f32[256,256]{0,1:T(8,128)S(1)}, f32[256,256]{0,1:T(8,128)S(1)}, u32[]{:S(2)}, u32[]{:S(2)}) collective-permute-start(f32[256,256]{0,1:T(8,128)S(1)} %get-tuple-element.19), channel_id=1, source_target_pairs={{1,0},{2,1},{3,2},{5,4},{6,5},{7,6},{9,8},{10,9},{11,10},{13,12},{... | collective-permute-start | bytes 786440 | tf_op jit(solution)/shard_map/ppermute | solution.py:10
  143.4 10.6 %collective-permute-start.40 = (f32[256,256]{0,1:T(8,128)S(1)}, f32[256,256]{0,1:T(8,128)S(1)}, u32[]{:S(2)}, u32[]{:S(2)}) collective-permute-start(f32[256,256]{0,1:T(8,128)S(1)} %get-tuple-element.20), channel_id=1, source_target_pairs={{0,1},{1,2},{2,3},{4,5},{5,6},{6,7},{8,9},{9,10},{10,11},{12,13},{... | collective-permute-start | bytes 786440 | tf_op jit(solution)/shard_map/ppermute | solution.py:10
  148.1 11.2 %collective-permute-start.26 = (f32[256,256]{0,1:T(8,128)S(1)}, f32[256,256]{0,1:T(8,128)S(1)}, u32[]{:S(2)}, u32[]{:S(2)}) collective-permute-start(f32[256,256]{0,1:T(8,128)S(1)} %get-tuple-element.9), channel_id=1, source_target_pairs={{1,0},{2,1},{3,2},{5,4},{6,5},{7,6},{9,8},{10,9},{11,10},{13,12},{... | collective-permute-start | bytes 786440 | tf_op jit(solution)/shard_map/ppermute | solution.py:10
  149.4 11.3 %collective-permute-start.23 = (f32[256,256]{0,1:T(8,128)S(1)}, f32[256,256]{0,1:T(8,128)S(1)}, u32[]{:S(2)}, u32[]{:S(2)}) collective-permute-start(f32[256,256]{0,1:T(8,128)S(1)} %get-tuple-element.10), channel_id=1, source_target_pairs={{0,1},{1,2},{2,3},{4,5},{5,6},{6,7},{8,9},{9,10},{10,11},{12,13},{... | collective-permute-start | bytes 786440 | tf_op jit(solution)/shard_map/ppermute | solution.py:10
  154.1 12.4 %collective-permute-start.41 = (f32[256,256]{0,1:T(8,128)S(1)}, f32[256,256]{0,1:T(8,128)S(1)}, u32[]{:S(2)}, u32[]{:S(2)}) collective-permute-start(f32[256,256]{0,1:T(8,128)S(1)} %get-tuple-element.18), channel_id=1, source_target_pairs={{0,1},{1,2},{2,3},{4,5},{5,6},{6,7},{8,9},{9,10},{10,11},{12,13},{... | collective-permute-start | bytes 786440 | tf_op jit(solution)/shard_map/ppermute | solution.py:10
  157.9 8.7 %collective-permute-start.44 = (f32[256,256]{0,1:T(8,128)S(1)}, f32[256,256]{0,1:T(8,128)S(1)}, u32[]{:S(2)}, u32[]{:S(2)}) collective-permute-start(f32[256,256]{0,1:T(8,128)S(1)} %get-tuple-element.17), channel_id=1, source_target_pairs={{1,0},{2,1},{3,2},{5,4},{6,5},{7,6},{9,8},{10,9},{11,10},{13,12},{... | collective-permute-start | bytes 786440 | tf_op jit(solution)/shard_map/ppermute | solution.py:10
  160.8 9.0 %collective-permute-start.24 = (f32[256,256]{0,1:T(8,128)S(1)}, f32[256,256]{0,1:T(8,128)S(1)}, u32[]{:S(2)}, u32[]{:S(2)}) collective-permute-start(f32[256,256]{0,1:T(8,128)S(1)} %get-tuple-element.8), channel_id=1, source_target_pairs={{0,1},{1,2},{2,3},{4,5},{5,6},{6,7},{8,9},{9,10},{10,11},{12,13},{... | collective-permute-start | bytes 786440 | tf_op jit(solution)/shard_map/ppermute | solution.py:10
  165.2 8.3 %collective-permute-start.27 = (f32[256,256]{0,1:T(8,128)S(1)}, f32[256,256]{0,1:T(8,128)S(1)}, u32[]{:S(2)}, u32[]{:S(2)}) collective-permute-start(f32[256,256]{0,1:T(8,128)S(1)} %get-tuple-element.7), channel_id=1, source_target_pairs={{1,0},{2,1},{3,2},{5,4},{6,5},{7,6},{9,8},{10,9},{11,10},{13,12},{... | collective-permute-start | bytes 786440 | tf_op jit(solution)/shard_map/ppermute | solution.py:10
  (17 other events, 88.5 us)

commit v15 on v10

--- a/solution.py
+++ b/solution.py
@@ -82,8 +82,10 @@
     gamma = product(columns(index), densities)
     from_left, from_right = densities, densities
     for step in range(count - 1):
-        from_left = from_behind(from_left, "aux", 1)
-        from_right = from_behind(from_right, "aux", -1)
+        rightward = [(i, i + 1) for i in range(step, count - 1)]
+        leftward = [(i + 1, i) for i in range(count - 1 - step)]
+        from_left = lax.ppermute(from_left, "aux", rightward)
+        from_right = lax.ppermute(from_right, "aux", leftward)
         gamma = gamma + product(columns(index - 1 - step), from_left)
         gamma = gamma + product(columns(index + 1 + step), from_right)
     return gamma
@@ -101,8 +103,10 @@
     to_right = jnp.zeros((rows, partial.shape[1]), partial.dtype)
     to_left = jnp.zeros((rows, partial.shape[1]), partial.dtype)
     for step in range(count - 1):
-        to_right = from_behind(to_right + block(index + count - 1 - step), "aux", 1)
-        to_left = from_behind(to_left + block(index - (count - 1) + step), "aux", -1)
+        rightward = [(i, i + 1) for i in range(min(step + 1, count - 1))]
+        leftward = [(i + 1, i) for i in range(count - 2 - step, count - 1)]
+        to_right = lax.ppermute(to_right + block(index + count - 1 - step), "aux", rightward)
+        to_left = lax.ppermute(to_left + block(index - (count - 1) + step), "aux", leftward)
     return to_right + to_left + block(index)
 
 

time: 172 us -> 170 us (0.988)
  starting transfers between devices: 86.3 us -> 79.5 us
  waiting for transfers between devices: 57.6 us -> 62.5 us
    ppermute x30 -> x12, starting transfers between devices: 74.9 us -> 27.6 us  [from_behind(): return lax.ppermute(array, axis, pairs)]
    ppermute x0 -> x18, starting transfers between devices: none -> 41.5 us  [the longest x6 24.5 us: reduce_over_aux(): lax.ppermute(to_right + block(index + count - 1 - step), 'aux', rightward)]
    ppermute x0 -> x18, waiting for transfers between devices: none -> 34 us  [the longest x3 23.5 us: gamma_over_aux(): from_right = lax.ppermute(from_right, 'aux', leftward)]
    ppermute x30 -> x12, waiting for transfers between devices: 43.3 us -> 13.7 us  [from_behind(): return lax.ppermute(array, axis, pairs)]
  transfers between devices with their start and end apart: 42 -> 42, of which waited for: 23 -> 22; matrix products, arithmetic and copies ran while one was open for 14% -> 14% of each run, Pallas kernels for 0% -> 0%
where the time goes in v15:
time: 170 us; the launch traced here: 169 us
  starting transfers between devices  79.5 us (47%)
  waiting for transfers between devices  62.5 us (37%)
  matrix products  19.1 us (11%)
  local copies, waits for them, and re-layouts  4.24 us (2%)
  other arithmetic  2.83 us (2%)
    ppermute x12, starting transfers between devices, from_behind(): return lax.ppermute(array, axis, pairs)  27.6 us
    ppermute x6, starting transfers between devices, reduce_over_aux(): lax.ppermute(to_right + block(index + count - 1 - step), 'aux', rightward)  24.5 us
    ppermute x3, waiting for transfers between devices, gamma_over_aux(): from_right = lax.ppermute(from_right, 'aux', leftward)  23.5 us
    dot_general x26, matrix products, product(): jnp.dot(left, right, precision=lax.Precision.HIGH, preferred_element_type...  17 us
    ppermute x12, waiting for transfers between devices, swap(): return lax.ppermute(array, axis, [(i, i ^ bit) for i in range(count)])  14.8 us
    ppermute x12, waiting for transfers between devices, from_behind(): return lax.ppermute(array, axis, pairs)  13.7 us
    ppermute x12, starting transfers between devices, swap(): return lax.ppermute(array, axis, [(i, i ^ bit) for i in range(count)])  10.4 us
    ppermute x3, starting transfers between devices, gamma_over_aux(): from_left = lax.ppermute(from_left, 'aux', rightward)  7.75 us
  transfers between devices with their start and end apart: 42, of which 22 were waited for; matrix products, arithmetic and copies ran while one was open for 14% of the time, Pallas kernels for 0%

profile of v15, /device:TPU:0, one launch (start us, length us, event | category | flops | bytes accessed | tf_op | source)
XLA Modules:
  0.0 168.8 jit_solution(6007953058753923601)
XLA Ops:
  1.4 6.4 %collective-permute-start = (f32[256,512]{1,0:T(8,128)}, f32[256,512]{1,0:T(8,128)}, u32[]{:S(2)}, u32[]{:S(2)}) collective-permute-start(f32[256,512]{1,0:T(8,128)} %param.6), channel_id=1, source_target_pairs={{0,1},{1,2},{2,3},{4,5},{5,6},{6,7},{8,9},{9,10},{10,11},{12,13},{... | collective-permute-start | bytes 1572872 | tf_op jit(solution)/shard_map/ppermute | solution.py:87
  7.8 2.9 %copy.8 = f32[512,1024]{0,1:T(8,128)} copy(f32[512,1024]{1,0:T(8,128)} %param.5) | data formatting | bytes 4194304 | tf_op args[0]
  10.9 1.8 %bitcast_multiply_fusion = f32[512,1024]{0,1:T(8,128)S(1)} fusion(f32[512,1024]{0,1:T(8,128)} %copy.8, f32[512,16]{0,1:T(8,128)S(1)} %reshape.6), kind=kLoop, calls=%fused_computation | loop fusion | flops 524288 | bytes 4227072 | tf_op jit(solution)/shard_map/mul | solution.py:23
  12.8 1.7 fusion.22
  14.5 2.8 %collective-permute-done.1 = f32[256,512]{1,0:T(8,128)} collective-permute-done((f32[256,512]{1,0:T(8,128)}, f32[256,512]{1,0:T(8,128)}, u32[]{:S(2)}, u32[]{:S(2)}) %collective-permute-start.1) | collective-permute-done | bytes 524320 | tf_op jit(solution)/shard_map/ppermute | solution.py:88
  19.3 1.7 convolution_add_fusion.3
  21.0 1.7 convolution_add_fusion.2
  22.6 9.8 %collective-permute-done.3 = f32[256,512]{1,0:T(8,128)S(1)} collective-permute-done((f32[256,512]{1,0:T(8,128)}, f32[256,512]{1,0:T(8,128)S(1)}, u32[]{:S(2)}, u32[]{:S(2)}) %collective-permute-start.3) | collective-permute-done | bytes 524320 | tf_op jit(solution)/shard_map/ppermute | solution.py:88
  35.8 10.8 %collective-permute-done.5 = f32[256,512]{1,0:T(8,128)S(1)} collective-permute-done((f32[256,512]{1,0:T(8,128)S(1)}, f32[256,512]{1,0:T(8,128)S(1)}, u32[]{:S(2)}, u32[]{:S(2)}) %collective-permute-start.5) | collective-permute-done | bytes 524320 | tf_op jit(solution)/shard_map/ppermute | solution.py:88
  52.3 4.2 %collective-permute-done.7 = f32[512,64]{0,1:T(8,128)S(1)} collective-permute-done((f32[512,64]{0,1:T(8,128)S(1)}, f32[512,64]{0,1:T(8,128)S(1)}, u32[]{:S(2)}, u32[]{:S(2)}) %collective-permute-start.7) | collective-permute-done | bytes 131104 | tf_op jit(solution)/shard_map/ppermute | solution.py:15
  59.7 1.7 collective-permute-done.8
  64.0 5.7 %collective-permute-start.27 = (f32[512,32]{0,1:T(8,128)S(1)}, f32[512,32]{0,1:T(8,128)S(1)}, u32[]{:S(2)}, u32[]{:S(2)}) collective-permute-start(f32[512,32]{0,1:T(8,128)S(1)} %convolution_bitcast_fusion.2), channel_id=1, source_target_pairs={{0,1},{1,2},{2,3},{4,5},{5,6},{6,7},{8,9},{9,10},{10,11},{12,13},{... | collective-permute-start | bytes 196616 | tf_op jit(solution)/shard_map/ppermute | solution.py:10
  70.3 4.4 %collective-permute-start.10 = (f32[512,32]{0,1:T(8,128)S(1)}, f32[512,32]{0,1:T(8,128)S(1)}, u32[]{:S(2)}, u32[]{:S(2)}) collective-permute-start(f32[512,32]{0,1:T(8,128)S(1)} %convolution_add_fusion.13), channel_id=1, source_target_pairs={{0,1},{1,2},{2,3},{4,5},{5,6},{6,7},{8,9},{9,10},{10,11},{12,13},{... | collective-permute-start | bytes 196616 | tf_op jit(solution)/shard_map/ppermute | solution.py:10
  75.2 1.9 %collective-permute-start.28 = (f32[512,32]{0,1:T(8,128)S(1)}, f32[512,32]{0,1:T(8,128)S(1)}, u32[]{:S(2)}, u32[]{:S(2)}) collective-permute-start(f32[512,32]{0,1:T(8,128)S(1)} %convolution_add_fusion.8), channel_id=1, source_target_pairs={{0,1},{1,2},{2,3},{4,5},{5,6},{6,7},{8,9},{9,10},{10,11},{12,13},{... | collective-permute-start | bytes 196616 | tf_op jit(solution)/shard_map/ppermute | solution.py:10
  77.8 3.7 %collective-permute-start.11 = (f32[512,32]{0,1:T(8,128)S(1)}, f32[512,32]{0,1:T(8,128)S(1)}, u32[]{:S(2)}, u32[]{:S(2)}) collective-permute-start(f32[512,32]{0,1:T(8,128)S(1)} %convolution_add_fusion.12), channel_id=1, source_target_pairs={{0,1},{1,2},{2,3},{4,5},{5,6},{6,7},{8,9},{9,10},{10,11},{12,13},{... | collective-permute-start | bytes 196616 | tf_op jit(solution)/shard_map/ppermute | solution.py:10
  82.1 2.5 %collective-permute-start.29 = (f32[512,32]{0,1:T(8,128)S(1)}, f32[512,32]{0,1:T(8,128)S(1)}, u32[]{:S(2)}, u32[]{:S(2)}) collective-permute-start(f32[512,32]{0,1:T(8,128)S(1)} %convolution_add_fusion.7), channel_id=1, source_target_pairs={{0,1},{1,2},{2,3},{4,5},{5,6},{6,7},{8,9},{9,10},{10,11},{12,13},{... | collective-permute-start | bytes 196616 | tf_op jit(solution)/shard_map/ppermute | solution.py:10
  88.3 4.3 %collective-permute-done.12 = f32[512,32]{0,1:T(8,128)S(1)} collective-permute-done((f32[512,32]{0,1:T(8,128)S(1)}, f32[512,32]{0,1:T(8,128)S(1)}, u32[]{:S(2)}, u32[]{:S(2)}) %collective-permute-start.12) | collective-permute-done | bytes 65568 | tf_op jit(solution)/shard_map/ppermute | solution.py:10
  96.0 3.2 %collective-permute-done.13 = f32[512,32]{0,1:T(8,128)S(1)} collective-permute-done((f32[512,32]{0,1:T(8,128)S(1)}, f32[512,32]{0,1:T(8,128)S(1)}, u32[]{:S(2)}, u32[]{:S(2)}) %collective-permute-start.13) | collective-permute-done | bytes 65568 | tf_op jit(solution)/shard_map/ppermute | solution.py:10
  103.2 3.0 %collective-permute-done.14 = f32[512,32]{0,1:T(8,128)S(1)} collective-permute-done((f32[512,32]{0,1:T(8,128)S(1)}, f32[512,32]{0,1:T(8,128)S(1)}, u32[]{:S(2)}, u32[]{:S(2)}) %collective-permute-start.14) | collective-permute-done | bytes 65568 | tf_op jit(solution)/shard_map/ppermute | solution.py:10
  111.0 1.5 collective-permute-start.16
  112.5 2.2 %collective-permute-done.32 = f32[512,32]{0,1:T(8,128)S(1)} collective-permute-done((f32[512,32]{0,1:T(8,128)S(1)}, f32[512,32]{0,1:T(8,128)S(1)}, u32[]{:S(2)}, u32[]{:S(2)}) %collective-permute-start.32) | collective-permute-done | bytes 65568 | tf_op jit(solution)/shard_map/ppermute | solution.py:10
  116.3 3.1 %collective-permute-done.33 = f32[512,32]{0,1:T(8,128)S(1)} collective-permute-done((f32[512,32]{0,1:T(8,128)S(1)}, f32[512,32]{0,1:T(8,128)S(1)}, u32[]{:S(2)}, u32[]{:S(2)}) %collective-permute-start.33) | collective-permute-done | bytes 65568 | tf_op jit(solution)/shard_map/ppermute | solution.py:15
  119.4 1.6 collective-permute-start.34
  121.0 3.5 %collective-permute-done.34 = f32[512,64]{0,1:T(8,128)S(1)} collective-permute-done((f32[512,64]{0,1:T(8,128)S(1)}, f32[512,64]{0,1:T(8,128)S(1)}, u32[]{:S(2)}, u32[]{:S(2)}) %collective-permute-start.34) | collective-permute-done | bytes 131104 | tf_op jit(solution)/shard_map/ppermute | solution.py:15
  125.7 3.9 %collective-permute-start.18 = (f32[256,256]{0,1:T(8,128)S(1)}, f32[256,256]{0,1:T(8,128)S(1)}, u32[]{:S(2)}, u32[]{:S(2)}) collective-permute-start(f32[256,256]{0,1:T(8,128)S(1)} %get-tuple-element.10), channel_id=1, source_target_pairs={{0,1},{4,5},{8,9},{12,13},{16,17},{20,21},{24,25},{28,29}} | collective-permute-start | bytes 786440 | tf_op jit(solution)/shard_map/ppermute | solution.py:108
  133.4 2.8 %collective-permute-done.18 = f32[256,256]{0,1:T(8,128)S(1)} collective-permute-done((f32[256,256]{0,1:T(8,128)S(1)}, f32[256,256]{0,1:T(8,128)S(1)}, u32[]{:S(2)}, u32[]{:S(2)}) %collective-permute-start.18) | collective-permute-done | bytes 262176 | tf_op jit(solution)/shard_map/ppermute | solution.py:108
  136.3 4.4 %collective-permute-start.19 = (f32[256,256]{0,1:T(8,128)S(1)}, f32[256,256]{0,1:T(8,128)S(1)}, u32[]{:S(2)}, u32[]{:S(2)}) collective-permute-start(f32[256,256]{0,1:T(8,128)S(1)} %get-tuple-element.8), channel_id=1, source_target_pairs={{0,1},{1,2},{4,5},{5,6},{8,9},{9,10},{12,13},{13,14},{16,17},{17,1... | collective-permute-start | bytes 786440 | tf_op jit(solution)/shard_map/ppermute | solution.py:108
  141.9 4.4 %collective-permute-start.37 = (f32[256,256]{0,1:T(8,128)S(1)}, f32[256,256]{0,1:T(8,128)S(1)}, u32[]{:S(2)}, u32[]{:S(2)}) collective-permute-start(f32[256,256]{0,1:T(8,128)S(1)} %get-tuple-element.18), channel_id=1, source_target_pairs={{0,1},{1,2},{4,5},{5,6},{8,9},{9,10},{12,13},{13,14},{16,17},{17,1... | collective-permute-start | bytes 786440 | tf_op jit(solution)/shard_map/ppermute | solution.py:108
  147.6 5.9 %collective-permute-start.20 = (f32[256,256]{0,1:T(8,128)S(1)}, f32[256,256]{0,1:T(8,128)S(1)}, u32[]{:S(2)}, u32[]{:S(2)}) collective-permute-start(f32[256,256]{0,1:T(8,128)S(1)} %get-tuple-element.6), channel_id=1, source_target_pairs={{0,1},{1,2},{2,3},{4,5},{5,6},{6,7},{8,9},{9,10},{10,11},{12,13},{... | collective-permute-start | bytes 786440 | tf_op jit(solution)/shard_map/ppermute | solution.py:108
  154.9 4.6 %collective-permute-start.38 = (f32[256,256]{0,1:T(8,128)S(1)}, f32[256,256]{0,1:T(8,128)S(1)}, u32[]{:S(2)}, u32[]{:S(2)}) collective-permute-start(f32[256,256]{0,1:T(8,128)S(1)} %get-tuple-element.16), channel_id=1, source_target_pairs={{0,1},{1,2},{2,3},{4,5},{5,6},{6,7},{8,9},{9,10},{10,11},{12,13},{... | collective-permute-start | bytes 786440 | tf_op jit(solution)/shard_map/ppermute | solution.py:108
  162.2 1.7 %collective-permute-done.38 = f32[256,256]{0,1:T(8,128)S(1)} collective-permute-done((f32[256,256]{0,1:T(8,128)S(1)}, f32[256,256]{0,1:T(8,128)S(1)}, u32[]{:S(2)}, u32[]{:S(2)}) %collective-permute-start.38) | collective-permute-done | bytes 262176 | tf_op jit(solution)/shard_map/ppermute | solution.py:108
  163.9 3.8 %collective-permute-done.41 = f32[256,256]{0,1:T(8,128)S(1)} collective-permute-done((f32[256,256]{0,1:T(8,128)S(1)}, f32[256,256]{0,1:T(8,128)S(1)}, u32[]{:S(2)}, u32[]{:S(2)}) %collective-permute-start.41) | collective-permute-done | bytes 262176 | tf_op jit(solution)/shard_map/ppermute | solution.py:109
  (114 shorter events, 50.6 us)
Async XLA Ops:
  0.0 17.3 %collective-permute-start.1 = (f32[256,512]{1,0:T(8,128)}, f32[256,512]{1,0:T(8,128)}, u32[]{:S(2)}, u32[]{:S(2)}) collective-permute-start(f32[256,512]{1,0:T(8,128)} %param.6), channel_id=1, source_target_pairs={{1,0},{2,1},{3,2},{5,4},{6,5},{7,6},{9,8},{10,9},{11,10},{13,12},{... | collective-permute-start | bytes 1572872 | tf_op jit(solution)/shard_map/ppermute | solution.py:88
  1.4 17.2 %collective-permute-start = (f32[256,512]{1,0:T(8,128)}, f32[256,512]{1,0:T(8,128)}, u32[]{:S(2)}, u32[]{:S(2)}) collective-permute-start(f32[256,512]{1,0:T(8,128)} %param.6), channel_id=1, source_target_pairs={{0,1},{1,2},{2,3},{4,5},{5,6},{6,7},{8,9},{9,10},{10,11},{12,13},{... | collective-permute-start | bytes 1572872 | tf_op jit(solution)/shard_map/ppermute | solution.py:87
  17.3 15.2 %collective-permute-start.3 = (f32[256,512]{1,0:T(8,128)}, f32[256,512]{1,0:T(8,128)S(1)}, u32[]{:S(2)}, u32[]{:S(2)}) collective-permute-start(f32[256,512]{1,0:T(8,128)} %collective-permute-done.1), channel_id=1, source_target_pairs={{1,0},{2,1},{5,4},{6,5},{9,8},{10,9},{13,12},{14,13},{17,16},{18,1... | collective-permute-start | bytes 1572872 | tf_op jit(solution)/shard_map/ppermute | solution.py:88
  18.6 15.2 %collective-permute-start.2 = (f32[256,512]{1,0:T(8,128)}, f32[256,512]{1,0:T(8,128)S(1)}, u32[]{:S(2)}, u32[]{:S(2)}) collective-permute-start(f32[256,512]{1,0:T(8,128)} %collective-permute-done), channel_id=1, source_target_pairs={{1,2},{2,3},{5,6},{6,7},{9,10},{10,11},{13,14},{14,15},{17,18},{18... | collective-permute-start | bytes 1572872 | tf_op jit(solution)/shard_map/ppermute | solution.py:87
  32.5 14.1 %collective-permute-start.5 = (f32[256,512]{1,0:T(8,128)S(1)}, f32[256,512]{1,0:T(8,128)S(1)}, u32[]{:S(2)}, u32[]{:S(2)}) collective-permute-start(f32[256,512]{1,0:T(8,128)S(1)} %collective-permute-done.3), channel_id=1, source_target_pairs={{1,0},{5,4},{9,8},{13,12},{17,16},{21,20},{25,24},{29,28}} | collective-permute-start | bytes 1572872 | tf_op jit(solution)/shard_map/ppermute | solution.py:88
  33.8 13.4 %collective-permute-start.4 = (f32[256,512]{1,0:T(8,128)S(1)}, f32[256,512]{1,0:T(8,128)S(1)}, u32[]{:S(2)}, u32[]{:S(2)}) collective-permute-start(f32[256,512]{1,0:T(8,128)S(1)} %collective-permute-done.2), channel_id=1, source_target_pairs={{2,3},{6,7},{10,11},{14,15},{18,19},{22,23},{26,27},{30,31}} | collective-permute-start | bytes 1572872 | tf_op jit(solution)/shard_map/ppermute | solution.py:87
  50.1 6.4 %collective-permute-start.7 = (f32[512,64]{0,1:T(8,128)S(1)}, f32[512,64]{0,1:T(8,128)S(1)}, u32[]{:S(2)}, u32[]{:S(2)}) collective-permute-start(f32[512,64]{0,1:T(8,128)S(1)} %slice_select_fusion.3), channel_id=1, source_target_pairs={{0,8},{4,12},{8,0},{12,4},{16,24},{20,28},{24,16},{28,20},{1,9},{5... | collective-permute-start | bytes 393224 | tf_op jit(solution)/shard_map/ppermute | solution.py:15
  51.2 7.3 %collective-permute-start.25 = (f32[512,64]{0,1:T(8,128)S(1)}, f32[512,64]{0,1:T(8,128)S(1)}, u32[]{:S(2)}, u32[]{:S(2)}) collective-permute-start(f32[512,64]{0,1:T(8,128)S(1)} %slice_select_fusion.2), channel_id=1, source_target_pairs={{0,8},{4,12},{8,0},{12,4},{16,24},{20,28},{24,16},{28,20},{1,9},{5... | collective-permute-start | bytes 393224 | tf_op jit(solution)/shard_map/ppermute | solution.py:15
  61.9 7.8 %collective-permute-start.9 = (f32[512,32]{0,1:T(8,128)S(1)}, f32[512,32]{0,1:T(8,128)S(1)}, u32[]{:S(2)}, u32[]{:S(2)}) collective-permute-start(f32[512,32]{0,1:T(8,128)S(1)} %convolution_bitcast_fusion.5), channel_id=1, source_target_pairs={{0,1},{1,2},{2,3},{4,5},{5,6},{6,7},{8,9},{9,10},{10,11},{12,13},{... | collective-permute-start | bytes 196616 | tf_op jit(solution)/shard_map/ppermute | solution.py:10
  64.0 10.7 %collective-permute-start.27 = (f32[512,32]{0,1:T(8,128)S(1)}, f32[512,32]{0,1:T(8,128)S(1)}, u32[]{:S(2)}, u32[]{:S(2)}) collective-permute-start(f32[512,32]{0,1:T(8,128)S(1)} %convolution_bitcast_fusion.2), channel_id=1, source_target_pairs={{0,1},{1,2},{2,3},{4,5},{5,6},{6,7},{8,9},{9,10},{10,11},{12,13},{... | collective-permute-start | bytes 196616 | tf_op jit(solution)/shard_map/ppermute | solution.py:10
  70.3 6.9 %collective-permute-start.10 = (f32[512,32]{0,1:T(8,128)S(1)}, f32[512,32]{0,1:T(8,128)S(1)}, u32[]{:S(2)}, u32[]{:S(2)}) collective-permute-start(f32[512,32]{0,1:T(8,128)S(1)} %convolution_add_fusion.13), channel_id=1, source_target_pairs={{0,1},{1,2},{2,3},{4,5},{5,6},{6,7},{8,9},{9,10},{10,11},{12,13},{... | collective-permute-start | bytes 196616 | tf_op jit(solution)/shard_map/ppermute | solution.py:10
  75.2 6.2 %collective-permute-start.28 = (f32[512,32]{0,1:T(8,128)S(1)}, f32[512,32]{0,1:T(8,128)S(1)}, u32[]{:S(2)}, u32[]{:S(2)}) collective-permute-start(f32[512,32]{0,1:T(8,128)S(1)} %convolution_add_fusion.8), channel_id=1, source_target_pairs={{0,1},{1,2},{2,3},{4,5},{5,6},{6,7},{8,9},{9,10},{10,11},{12,13},{... | collective-permute-start | bytes 196616 | tf_op jit(solution)/shard_map/ppermute | solution.py:10
  77.8 6.8 %collective-permute-start.11 = (f32[512,32]{0,1:T(8,128)S(1)}, f32[512,32]{0,1:T(8,128)S(1)}, u32[]{:S(2)}, u32[]{:S(2)}) collective-permute-start(f32[512,32]{0,1:T(8,128)S(1)} %convolution_add_fusion.12), channel_id=1, source_target_pairs={{0,1},{1,2},{2,3},{4,5},{5,6},{6,7},{8,9},{9,10},{10,11},{12,13},{... | collective-permute-start | bytes 196616 | tf_op jit(solution)/shard_map/ppermute | solution.py:10
  85.9 6.7 %collective-permute-start.12 = (f32[512,32]{0,1:T(8,128)S(1)}, f32[512,32]{0,1:T(8,128)S(1)}, u32[]{:S(2)}, u32[]{:S(2)}) collective-permute-start(f32[512,32]{0,1:T(8,128)S(1)} %convolution_bitcast_fusion.4), channel_id=1, source_target_pairs={{1,0},{2,1},{3,2},{5,4},{6,5},{7,6},{9,8},{10,9},{11,10},{13,12},{... | collective-permute-start | bytes 196616 | tf_op jit(solution)/shard_map/ppermute | solution.py:10
  93.0 6.2 %collective-permute-start.13 = (f32[512,32]{0,1:T(8,128)S(1)}, f32[512,32]{0,1:T(8,128)S(1)}, u32[]{:S(2)}, u32[]{:S(2)}) collective-permute-start(f32[512,32]{0,1:T(8,128)S(1)} %convolution_add_fusion.10), channel_id=1, source_target_pairs={{1,0},{2,1},{3,2},{5,4},{6,5},{7,6},{9,8},{10,9},{11,10},{13,12},{... | collective-permute-start | bytes 196616 | tf_op jit(solution)/shard_map/ppermute | solution.py:10
  94.7 6.8 %collective-permute-start.30 = (f32[512,32]{0,1:T(8,128)S(1)}, f32[512,32]{0,1:T(8,128)S(1)}, u32[]{:S(2)}, u32[]{:S(2)}) collective-permute-start(f32[512,32]{0,1:T(8,128)S(1)} %convolution_bitcast_fusion.1), channel_id=1, source_target_pairs={{1,0},{2,1},{3,2},{5,4},{6,5},{7,6},{9,8},{10,9},{11,10},{13,12},{... | collective-permute-start | bytes 196616 | tf_op jit(solution)/shard_map/ppermute | solution.py:10
  99.6 6.6 %collective-permute-start.14 = (f32[512,32]{0,1:T(8,128)S(1)}, f32[512,32]{0,1:T(8,128)S(1)}, u32[]{:S(2)}, u32[]{:S(2)}) collective-permute-start(f32[512,32]{0,1:T(8,128)S(1)} %convolution_add_fusion.9), channel_id=1, source_target_pairs={{1,0},{2,1},{3,2},{5,4},{6,5},{7,6},{9,8},{10,9},{11,10},{13,12},{... | collective-permute-start | bytes 196616 | tf_op jit(solution)/shard_map/ppermute | solution.py:10
  101.9 6.2 %collective-permute-start.31 = (f32[512,32]{0,1:T(8,128)S(1)}, f32[512,32]{0,1:T(8,128)S(1)}, u32[]{:S(2)}, u32[]{:S(2)}) collective-permute-start(f32[512,32]{0,1:T(8,128)S(1)} %convolution_add_fusion.5), channel_id=1, source_target_pairs={{1,0},{2,1},{3,2},{5,4},{6,5},{7,6},{9,8},{10,9},{11,10},{13,12},{... | collective-permute-start | bytes 196616 | tf_op jit(solution)/shard_map/ppermute | solution.py:10
  108.5 6.2 %collective-permute-start.32 = (f32[512,32]{0,1:T(8,128)S(1)}, f32[512,32]{0,1:T(8,128)S(1)}, u32[]{:S(2)}, u32[]{:S(2)}) collective-permute-start(f32[512,32]{0,1:T(8,128)S(1)} %convolution_add_fusion.4), channel_id=1, source_target_pairs={{1,0},{2,1},{3,2},{5,4},{6,5},{7,6},{9,8},{10,9},{11,10},{13,12},{... | collective-permute-start | bytes 196616 | tf_op jit(solution)/shard_map/ppermute | solution.py:10
  116.3 8.3 %collective-permute-start.17 = (f32[512,128]{0,1:T(8,128)S(1)}, f32[512,128]{0,1:T(8,128)S(1)}, u32[]{:S(2)}, u32[]{:S(2)}) collective-permute-start(f32[512,128]{0,1:T(8,128)S(1)} %maximum_select_fusion.4), channel_id=1, source_target_pairs={{0,4},{4,0},{8,12},{12,8},{16,20},{20,16},{24,28},{28,24},{1,5},{5... | collective-permute-start | bytes 786440 | tf_op jit(solution)/shard_map/ppermute | solution.py:15
  125.7 10.5 %collective-permute-start.18 = (f32[256,256]{0,1:T(8,128)S(1)}, f32[256,256]{0,1:T(8,128)S(1)}, u32[]{:S(2)}, u32[]{:S(2)}) collective-permute-start(f32[256,256]{0,1:T(8,128)S(1)} %get-tuple-element.10), channel_id=1, source_target_pairs={{0,1},{4,5},{8,9},{12,13},{16,17},{20,21},{24,25},{28,29}} | collective-permute-start | bytes 786440 | tf_op jit(solution)/shard_map/ppermute | solution.py:108
  129.6 6.6 %collective-permute-start.21 = (f32[256,256]{0,1:T(8,128)S(1)}, f32[256,256]{0,1:T(8,128)S(1)}, u32[]{:S(2)}, u32[]{:S(2)}) collective-permute-start(f32[256,256]{0,1:T(8,128)S(1)} %get-tuple-element.9), channel_id=1, source_target_pairs={{3,2},{7,6},{11,10},{15,14},{19,18},{23,22},{27,26},{31,30}} | collective-permute-start | bytes 786440 | tf_op jit(solution)/shard_map/ppermute | solution.py:109
  131.4 10.4 %collective-permute-start.36 = (f32[256,256]{0,1:T(8,128)S(1)}, f32[256,256]{0,1:T(8,128)S(1)}, u32[]{:S(2)}, u32[]{:S(2)}) collective-permute-start(f32[256,256]{0,1:T(8,128)S(1)} %get-tuple-element.20), channel_id=1, source_target_pairs={{0,1},{4,5},{8,9},{12,13},{16,17},{20,21},{24,25},{28,29}} | collective-permute-start | bytes 786440 | tf_op jit(solution)/shard_map/ppermute | solution.py:108
  132.7 9.1 %collective-permute-start.39 = (f32[256,256]{0,1:T(8,128)S(1)}, f32[256,256]{0,1:T(8,128)S(1)}, u32[]{:S(2)}, u32[]{:S(2)}) collective-permute-start(f32[256,256]{0,1:T(8,128)S(1)} %get-tuple-element.19), channel_id=1, source_target_pairs={{3,2},{7,6},{11,10},{15,14},{19,18},{23,22},{27,26},{31,30}} | collective-permute-start | bytes 786440 | tf_op jit(solution)/shard_map/ppermute | solution.py:109
  136.3 11.1 %collective-permute-start.19 = (f32[256,256]{0,1:T(8,128)S(1)}, f32[256,256]{0,1:T(8,128)S(1)}, u32[]{:S(2)}, u32[]{:S(2)}) collective-permute-start(f32[256,256]{0,1:T(8,128)S(1)} %get-tuple-element.8), channel_id=1, source_target_pairs={{0,1},{1,2},{4,5},{5,6},{8,9},{9,10},{12,13},{13,14},{16,17},{17,1... | collective-permute-start | bytes 786440 | tf_op jit(solution)/shard_map/ppermute | solution.py:108
  140.7 6.7 %collective-permute-start.22 = (f32[256,256]{0,1:T(8,128)S(1)}, f32[256,256]{0,1:T(8,128)S(1)}, u32[]{:S(2)}, u32[]{:S(2)}) collective-permute-start(f32[256,256]{0,1:T(8,128)S(1)} %get-tuple-element.7), channel_id=1, source_target_pairs={{2,1},{3,2},{6,5},{7,6},{10,9},{11,10},{14,13},{15,14},{18,17},{19... | collective-permute-start | bytes 786440 | tf_op jit(solution)/shard_map/ppermute | solution.py:109
  141.9 12.8 %collective-permute-start.37 = (f32[256,256]{0,1:T(8,128)S(1)}, f32[256,256]{0,1:T(8,128)S(1)}, u32[]{:S(2)}, u32[]{:S(2)}) collective-permute-start(f32[256,256]{0,1:T(8,128)S(1)} %get-tuple-element.18), channel_id=1, source_target_pairs={{0,1},{1,2},{4,5},{5,6},{8,9},{9,10},{12,13},{13,14},{16,17},{17,1... | collective-permute-start | bytes 786440 | tf_op jit(solution)/shard_map/ppermute | solution.py:108
  146.3 8.4 %collective-permute-start.40 = (f32[256,256]{0,1:T(8,128)S(1)}, f32[256,256]{0,1:T(8,128)S(1)}, u32[]{:S(2)}, u32[]{:S(2)}) collective-permute-start(f32[256,256]{0,1:T(8,128)S(1)} %get-tuple-element.17), channel_id=1, source_target_pairs={{2,1},{3,2},{6,5},{7,6},{10,9},{11,10},{14,13},{15,14},{18,17},{19... | collective-permute-start | bytes 786440 | tf_op jit(solution)/shard_map/ppermute | solution.py:109
  147.6 13.2 %collective-permute-start.20 = (f32[256,256]{0,1:T(8,128)S(1)}, f32[256,256]{0,1:T(8,128)S(1)}, u32[]{:S(2)}, u32[]{:S(2)}) collective-permute-start(f32[256,256]{0,1:T(8,128)S(1)} %get-tuple-element.6), channel_id=1, source_target_pairs={{0,1},{1,2},{2,3},{4,5},{5,6},{6,7},{8,9},{9,10},{10,11},{12,13},{... | collective-permute-start | bytes 786440 | tf_op jit(solution)/shard_map/ppermute | solution.py:108
  153.4 8.7 %collective-permute-start.23 = (f32[256,256]{0,1:T(8,128)S(1)}, f32[256,256]{0,1:T(8,128)S(1)}, u32[]{:S(2)}, u32[]{:S(2)}) collective-permute-start(f32[256,256]{0,1:T(8,128)S(1)} %get-tuple-element.5), channel_id=1, source_target_pairs={{1,0},{2,1},{3,2},{5,4},{6,5},{7,6},{9,8},{10,9},{11,10},{13,12},{... | collective-permute-start | bytes 786440 | tf_op jit(solution)/shard_map/ppermute | solution.py:109
  154.9 9.0 %collective-permute-start.38 = (f32[256,256]{0,1:T(8,128)S(1)}, f32[256,256]{0,1:T(8,128)S(1)}, u32[]{:S(2)}, u32[]{:S(2)}) collective-permute-start(f32[256,256]{0,1:T(8,128)S(1)} %get-tuple-element.16), channel_id=1, source_target_pairs={{0,1},{1,2},{2,3},{4,5},{5,6},{6,7},{8,9},{9,10},{10,11},{12,13},{... | collective-permute-start | bytes 786440 | tf_op jit(solution)/shard_map/ppermute | solution.py:108
  159.4 8.3 %collective-permute-start.41 = (f32[256,256]{0,1:T(8,128)S(1)}, f32[256,256]{0,1:T(8,128)S(1)}, u32[]{:S(2)}, u32[]{:S(2)}) collective-permute-start(f32[256,256]{0,1:T(8,128)S(1)} %get-tuple-element.15), channel_id=1, source_target_pairs={{1,0},{2,1},{3,2},{5,4},{6,5},{7,6},{9,8},{10,9},{11,10},{13,12},{... | collective-permute-start | bytes 786440 | tf_op jit(solution)/shard_map/ppermute | solution.py:109
  (13 other events, 96.0 us)

commit v16 on v15

--- a/solution.py
+++ b/solution.py
@@ -133,14 +133,12 @@
     transfer = -product(diag_inverse, sub_factor)
     gamma_partial = gamma_over_aux(screened, densities)
     width = gamma_partial.shape[1] // SLICES
-    results = []
-    for part in range(SLICES):
-        right_side = reduce_scatter_columns(gamma_partial[:, part * width:(part + 1) * width], "pair")
-        coefficients = solve(right_side, transfer, diag_inverse, sub_factor)
-        coeff_full = all_gather_columns(coefficients, "pair")
-        partial = contract_first(screened, coeff_full)
-        results.append(reduce_over_aux(partial))
-    return jnp.concatenate(results, axis=1)
+    parts = range(SLICES)
+    right_sides = [reduce_scatter_columns(gamma_partial[:, p * width:(p + 1) * width], "pair") for p in parts]
+    coefficients = [solve(r, transfer, diag_inverse, sub_factor) for r in right_sides]
+    coeff_full = [all_gather_columns(c, "pair") for c in coefficients]
+    partials = [contract_first(screened, c) for c in coeff_full]
+    return jnp.concatenate([reduce_over_aux(p) for p in partials], axis=1)
 
 
 def solution(mesh):

time: 170 us -> 170 us (level)
  no operation moved by 1% of the time
where the time goes in v16:
time: 170 us; the launch traced here: 169 us
  starting transfers between devices  79.5 us (47%)
  waiting for transfers between devices  62.5 us (37%)
  matrix products  19.1 us (11%)
  local copies, waits for them, and re-layouts  4.24 us (2%)
  other arithmetic  2.83 us (2%)
    ppermute x12, starting transfers between devices, from_behind(): return lax.ppermute(array, axis, pairs)  27.6 us
    ppermute x6, starting transfers between devices, reduce_over_aux(): lax.ppermute(to_right + block(index + count - 1 - step), 'aux', rightward)  24.5 us
    ppermute x3, waiting for transfers between devices, gamma_over_aux(): from_right = lax.ppermute(from_right, 'aux', leftward)  23.5 us
    dot_general x26, matrix products, product(): jnp.dot(left, right, precision=lax.Precision.HIGH, preferred_element_type...  17 us
    ppermute x12, waiting for transfers between devices, swap(): return lax.ppermute(array, axis, [(i, i ^ bit) for i in range(count)])  14.8 us
    ppermute x12, waiting for transfers between devices, from_behind(): return lax.ppermute(array, axis, pairs)  13.7 us
    ppermute x12, starting transfers between devices, swap(): return lax.ppermute(array, axis, [(i, i ^ bit) for i in range(count)])  10.4 us
    ppermute x3, starting transfers between devices, gamma_over_aux(): from_left = lax.ppermute(from_left, 'aux', rightward)  7.75 us
  transfers between devices with their start and end apart: 42, of which 22 were waited for; matrix products, arithmetic and copies ran while one was open for 14% of the time, Pallas kernels for 0%

profile of v16, /device:TPU:0, one launch (start us, length us, event | category | flops | bytes accessed | tf_op | source)
XLA Modules:
  0.0 168.8 jit_solution(6007953058753923601)
XLA Ops:
  1.4 6.4 %collective-permute-start = (f32[256,512]{1,0:T(8,128)}, f32[256,512]{1,0:T(8,128)}, u32[]{:S(2)}, u32[]{:S(2)}) collective-permute-start(f32[256,512]{1,0:T(8,128)} %param.6), channel_id=1, source_target_pairs={{0,1},{1,2},{2,3},{4,5},{5,6},{6,7},{8,9},{9,10},{10,11},{12,13},{... | collective-permute-start | bytes 1572872 | tf_op jit(solution)/shard_map/ppermute | solution.py:87
  7.8 2.9 %copy.8 = f32[512,1024]{0,1:T(8,128)} copy(f32[512,1024]{1,0:T(8,128)} %param.5) | data formatting | bytes 4194304 | tf_op args[0]
  10.9 1.8 %bitcast_multiply_fusion = f32[512,1024]{0,1:T(8,128)S(1)} fusion(f32[512,1024]{0,1:T(8,128)} %copy.8, f32[512,16]{0,1:T(8,128)S(1)} %reshape.6), kind=kLoop, calls=%fused_computation | loop fusion | flops 524288 | bytes 4227072 | tf_op jit(solution)/shard_map/mul | solution.py:23
  12.8 1.7 fusion.22
  14.5 2.8 %collective-permute-done.1 = f32[256,512]{1,0:T(8,128)} collective-permute-done((f32[256,512]{1,0:T(8,128)}, f32[256,512]{1,0:T(8,128)}, u32[]{:S(2)}, u32[]{:S(2)}) %collective-permute-start.1) | collective-permute-done | bytes 524320 | tf_op jit(solution)/shard_map/ppermute | solution.py:88
  19.3 1.7 convolution_add_fusion.3
  21.0 1.7 convolution_add_fusion.2
  22.6 9.8 %collective-permute-done.3 = f32[256,512]{1,0:T(8,128)S(1)} collective-permute-done((f32[256,512]{1,0:T(8,128)}, f32[256,512]{1,0:T(8,128)S(1)}, u32[]{:S(2)}, u32[]{:S(2)}) %collective-permute-start.3) | collective-permute-done | bytes 524320 | tf_op jit(solution)/shard_map/ppermute | solution.py:88
  35.8 10.8 %collective-permute-done.5 = f32[256,512]{1,0:T(8,128)S(1)} collective-permute-done((f32[256,512]{1,0:T(8,128)S(1)}, f32[256,512]{1,0:T(8,128)S(1)}, u32[]{:S(2)}, u32[]{:S(2)}) %collective-permute-start.5) | collective-permute-done | bytes 524320 | tf_op jit(solution)/shard_map/ppermute | solution.py:88
  52.3 4.2 %collective-permute-done.7 = f32[512,64]{0,1:T(8,128)S(1)} collective-permute-done((f32[512,64]{0,1:T(8,128)S(1)}, f32[512,64]{0,1:T(8,128)S(1)}, u32[]{:S(2)}, u32[]{:S(2)}) %collective-permute-start.7) | collective-permute-done | bytes 131104 | tf_op jit(solution)/shard_map/ppermute | solution.py:15
  59.7 1.7 collective-permute-done.8
  64.0 5.7 %collective-permute-start.27 = (f32[512,32]{0,1:T(8,128)S(1)}, f32[512,32]{0,1:T(8,128)S(1)}, u32[]{:S(2)}, u32[]{:S(2)}) collective-permute-start(f32[512,32]{0,1:T(8,128)S(1)} %convolution_bitcast_fusion.2), channel_id=1, source_target_pairs={{0,1},{1,2},{2,3},{4,5},{5,6},{6,7},{8,9},{9,10},{10,11},{12,13},{... | collective-permute-start | bytes 196616 | tf_op jit(solution)/shard_map/ppermute | solution.py:10
  70.3 4.4 %collective-permute-start.10 = (f32[512,32]{0,1:T(8,128)S(1)}, f32[512,32]{0,1:T(8,128)S(1)}, u32[]{:S(2)}, u32[]{:S(2)}) collective-permute-start(f32[512,32]{0,1:T(8,128)S(1)} %convolution_add_fusion.13), channel_id=1, source_target_pairs={{0,1},{1,2},{2,3},{4,5},{5,6},{6,7},{8,9},{9,10},{10,11},{12,13},{... | collective-permute-start | bytes 196616 | tf_op jit(solution)/shard_map/ppermute | solution.py:10
  75.2 1.9 %collective-permute-start.28 = (f32[512,32]{0,1:T(8,128)S(1)}, f32[512,32]{0,1:T(8,128)S(1)}, u32[]{:S(2)}, u32[]{:S(2)}) collective-permute-start(f32[512,32]{0,1:T(8,128)S(1)} %convolution_add_fusion.8), channel_id=1, source_target_pairs={{0,1},{1,2},{2,3},{4,5},{5,6},{6,7},{8,9},{9,10},{10,11},{12,13},{... | collective-permute-start | bytes 196616 | tf_op jit(solution)/shard_map/ppermute | solution.py:10
  77.8 3.7 %collective-permute-start.11 = (f32[512,32]{0,1:T(8,128)S(1)}, f32[512,32]{0,1:T(8,128)S(1)}, u32[]{:S(2)}, u32[]{:S(2)}) collective-permute-start(f32[512,32]{0,1:T(8,128)S(1)} %convolution_add_fusion.12), channel_id=1, source_target_pairs={{0,1},{1,2},{2,3},{4,5},{5,6},{6,7},{8,9},{9,10},{10,11},{12,13},{... | collective-permute-start | bytes 196616 | tf_op jit(solution)/shard_map/ppermute | solution.py:10
  82.1 2.5 %collective-permute-start.29 = (f32[512,32]{0,1:T(8,128)S(1)}, f32[512,32]{0,1:T(8,128)S(1)}, u32[]{:S(2)}, u32[]{:S(2)}) collective-permute-start(f32[512,32]{0,1:T(8,128)S(1)} %convolution_add_fusion.7), channel_id=1, source_target_pairs={{0,1},{1,2},{2,3},{4,5},{5,6},{6,7},{8,9},{9,10},{10,11},{12,13},{... | collective-permute-start | bytes 196616 | tf_op jit(solution)/shard_map/ppermute | solution.py:10
  88.3 4.3 %collective-permute-done.12 = f32[512,32]{0,1:T(8,128)S(1)} collective-permute-done((f32[512,32]{0,1:T(8,128)S(1)}, f32[512,32]{0,1:T(8,128)S(1)}, u32[]{:S(2)}, u32[]{:S(2)}) %collective-permute-start.12) | collective-permute-done | bytes 65568 | tf_op jit(solution)/shard_map/ppermute | solution.py:10
  96.0 3.2 %collective-permute-done.13 = f32[512,32]{0,1:T(8,128)S(1)} collective-permute-done((f32[512,32]{0,1:T(8,128)S(1)}, f32[512,32]{0,1:T(8,128)S(1)}, u32[]{:S(2)}, u32[]{:S(2)}) %collective-permute-start.13) | collective-permute-done | bytes 65568 | tf_op jit(solution)/shard_map/ppermute | solution.py:10
  103.2 3.0 %collective-permute-done.14 = f32[512,32]{0,1:T(8,128)S(1)} collective-permute-done((f32[512,32]{0,1:T(8,128)S(1)}, f32[512,32]{0,1:T(8,128)S(1)}, u32[]{:S(2)}, u32[]{:S(2)}) %collective-permute-start.14) | collective-permute-done | bytes 65568 | tf_op jit(solution)/shard_map/ppermute | solution.py:10
  111.0 1.5 collective-permute-start.16
  112.5 2.2 %collective-permute-done.32 = f32[512,32]{0,1:T(8,128)S(1)} collective-permute-done((f32[512,32]{0,1:T(8,128)S(1)}, f32[512,32]{0,1:T(8,128)S(1)}, u32[]{:S(2)}, u32[]{:S(2)}) %collective-permute-start.32) | collective-permute-done | bytes 65568 | tf_op jit(solution)/shard_map/ppermute | solution.py:10
  116.3 3.1 %collective-permute-done.33 = f32[512,32]{0,1:T(8,128)S(1)} collective-permute-done((f32[512,32]{0,1:T(8,128)S(1)}, f32[512,32]{0,1:T(8,128)S(1)}, u32[]{:S(2)}, u32[]{:S(2)}) %collective-permute-start.33) | collective-permute-done | bytes 65568 | tf_op jit(solution)/shard_map/ppermute | solution.py:15
  119.4 1.6 collective-permute-start.34
  121.0 3.5 %collective-permute-done.34 = f32[512,64]{0,1:T(8,128)S(1)} collective-permute-done((f32[512,64]{0,1:T(8,128)S(1)}, f32[512,64]{0,1:T(8,128)S(1)}, u32[]{:S(2)}, u32[]{:S(2)}) %collective-permute-start.34) | collective-permute-done | bytes 131104 | tf_op jit(solution)/shard_map/ppermute | solution.py:15
  125.7 3.9 %collective-permute-start.18 = (f32[256,256]{0,1:T(8,128)S(1)}, f32[256,256]{0,1:T(8,128)S(1)}, u32[]{:S(2)}, u32[]{:S(2)}) collective-permute-start(f32[256,256]{0,1:T(8,128)S(1)} %get-tuple-element.10), channel_id=1, source_target_pairs={{0,1},{4,5},{8,9},{12,13},{16,17},{20,21},{24,25},{28,29}} | collective-permute-start | bytes 786440 | tf_op jit(solution)/shard_map/ppermute | solution.py:108
  133.4 2.8 %collective-permute-done.18 = f32[256,256]{0,1:T(8,128)S(1)} collective-permute-done((f32[256,256]{0,1:T(8,128)S(1)}, f32[256,256]{0,1:T(8,128)S(1)}, u32[]{:S(2)}, u32[]{:S(2)}) %collective-permute-start.18) | collective-permute-done | bytes 262176 | tf_op jit(solution)/shard_map/ppermute | solution.py:108
  136.3 4.4 %collective-permute-start.19 = (f32[256,256]{0,1:T(8,128)S(1)}, f32[256,256]{0,1:T(8,128)S(1)}, u32[]{:S(2)}, u32[]{:S(2)}) collective-permute-start(f32[256,256]{0,1:T(8,128)S(1)} %get-tuple-element.8), channel_id=1, source_target_pairs={{0,1},{1,2},{4,5},{5,6},{8,9},{9,10},{12,13},{13,14},{16,17},{17,1... | collective-permute-start | bytes 786440 | tf_op jit(solution)/shard_map/ppermute | solution.py:108
  141.9 4.4 %collective-permute-start.37 = (f32[256,256]{0,1:T(8,128)S(1)}, f32[256,256]{0,1:T(8,128)S(1)}, u32[]{:S(2)}, u32[]{:S(2)}) collective-permute-start(f32[256,256]{0,1:T(8,128)S(1)} %get-tuple-element.18), channel_id=1, source_target_pairs={{0,1},{1,2},{4,5},{5,6},{8,9},{9,10},{12,13},{13,14},{16,17},{17,1... | collective-permute-start | bytes 786440 | tf_op jit(solution)/shard_map/ppermute | solution.py:108
  147.6 5.9 %collective-permute-start.20 = (f32[256,256]{0,1:T(8,128)S(1)}, f32[256,256]{0,1:T(8,128)S(1)}, u32[]{:S(2)}, u32[]{:S(2)}) collective-permute-start(f32[256,256]{0,1:T(8,128)S(1)} %get-tuple-element.6), channel_id=1, source_target_pairs={{0,1},{1,2},{2,3},{4,5},{5,6},{6,7},{8,9},{9,10},{10,11},{12,13},{... | collective-permute-start | bytes 786440 | tf_op jit(solution)/shard_map/ppermute | solution.py:108
  154.9 4.6 %collective-permute-start.38 = (f32[256,256]{0,1:T(8,128)S(1)}, f32[256,256]{0,1:T(8,128)S(1)}, u32[]{:S(2)}, u32[]{:S(2)}) collective-permute-start(f32[256,256]{0,1:T(8,128)S(1)} %get-tuple-element.16), channel_id=1, source_target_pairs={{0,1},{1,2},{2,3},{4,5},{5,6},{6,7},{8,9},{9,10},{10,11},{12,13},{... | collective-permute-start | bytes 786440 | tf_op jit(solution)/shard_map/ppermute | solution.py:108
  162.2 1.7 %collective-permute-done.38 = f32[256,256]{0,1:T(8,128)S(1)} collective-permute-done((f32[256,256]{0,1:T(8,128)S(1)}, f32[256,256]{0,1:T(8,128)S(1)}, u32[]{:S(2)}, u32[]{:S(2)}) %collective-permute-start.38) | collective-permute-done | bytes 262176 | tf_op jit(solution)/shard_map/ppermute | solution.py:108
  163.9 3.8 %collective-permute-done.41 = f32[256,256]{0,1:T(8,128)S(1)} collective-permute-done((f32[256,256]{0,1:T(8,128)S(1)}, f32[256,256]{0,1:T(8,128)S(1)}, u32[]{:S(2)}, u32[]{:S(2)}) %collective-permute-start.41) | collective-permute-done | bytes 262176 | tf_op jit(solution)/shard_map/ppermute | solution.py:109
  (114 shorter events, 50.6 us)
Async XLA Ops:
  0.0 17.3 %collective-permute-start.1 = (f32[256,512]{1,0:T(8,128)}, f32[256,512]{1,0:T(8,128)}, u32[]{:S(2)}, u32[]{:S(2)}) collective-permute-start(f32[256,512]{1,0:T(8,128)} %param.6), channel_id=1, source_target_pairs={{1,0},{2,1},{3,2},{5,4},{6,5},{7,6},{9,8},{10,9},{11,10},{13,12},{... | collective-permute-start | bytes 1572872 | tf_op jit(solution)/shard_map/ppermute | solution.py:88
  1.4 17.2 %collective-permute-start = (f32[256,512]{1,0:T(8,128)}, f32[256,512]{1,0:T(8,128)}, u32[]{:S(2)}, u32[]{:S(2)}) collective-permute-start(f32[256,512]{1,0:T(8,128)} %param.6), channel_id=1, source_target_pairs={{0,1},{1,2},{2,3},{4,5},{5,6},{6,7},{8,9},{9,10},{10,11},{12,13},{... | collective-permute-start | bytes 1572872 | tf_op jit(solution)/shard_map/ppermute | solution.py:87
  17.3 15.2 %collective-permute-start.3 = (f32[256,512]{1,0:T(8,128)}, f32[256,512]{1,0:T(8,128)S(1)}, u32[]{:S(2)}, u32[]{:S(2)}) collective-permute-start(f32[256,512]{1,0:T(8,128)} %collective-permute-done.1), channel_id=1, source_target_pairs={{1,0},{2,1},{5,4},{6,5},{9,8},{10,9},{13,12},{14,13},{17,16},{18,1... | collective-permute-start | bytes 1572872 | tf_op jit(solution)/shard_map/ppermute | solution.py:88
  18.6 15.2 %collective-permute-start.2 = (f32[256,512]{1,0:T(8,128)}, f32[256,512]{1,0:T(8,128)S(1)}, u32[]{:S(2)}, u32[]{:S(2)}) collective-permute-start(f32[256,512]{1,0:T(8,128)} %collective-permute-done), channel_id=1, source_target_pairs={{1,2},{2,3},{5,6},{6,7},{9,10},{10,11},{13,14},{14,15},{17,18},{18... | collective-permute-start | bytes 1572872 | tf_op jit(solution)/shard_map/ppermute | solution.py:87
  32.5 14.1 %collective-permute-start.5 = (f32[256,512]{1,0:T(8,128)S(1)}, f32[256,512]{1,0:T(8,128)S(1)}, u32[]{:S(2)}, u32[]{:S(2)}) collective-permute-start(f32[256,512]{1,0:T(8,128)S(1)} %collective-permute-done.3), channel_id=1, source_target_pairs={{1,0},{5,4},{9,8},{13,12},{17,16},{21,20},{25,24},{29,28}} | collective-permute-start | bytes 1572872 | tf_op jit(solution)/shard_map/ppermute | solution.py:88
  33.8 13.4 %collective-permute-start.4 = (f32[256,512]{1,0:T(8,128)S(1)}, f32[256,512]{1,0:T(8,128)S(1)}, u32[]{:S(2)}, u32[]{:S(2)}) collective-permute-start(f32[256,512]{1,0:T(8,128)S(1)} %collective-permute-done.2), channel_id=1, source_target_pairs={{2,3},{6,7},{10,11},{14,15},{18,19},{22,23},{26,27},{30,31}} | collective-permute-start | bytes 1572872 | tf_op jit(solution)/shard_map/ppermute | solution.py:87
  50.1 6.4 %collective-permute-start.7 = (f32[512,64]{0,1:T(8,128)S(1)}, f32[512,64]{0,1:T(8,128)S(1)}, u32[]{:S(2)}, u32[]{:S(2)}) collective-permute-start(f32[512,64]{0,1:T(8,128)S(1)} %slice_select_fusion.3), channel_id=1, source_target_pairs={{0,8},{4,12},{8,0},{12,4},{16,24},{20,28},{24,16},{28,20},{1,9},{5... | collective-permute-start | bytes 393224 | tf_op jit(solution)/shard_map/ppermute | solution.py:15
  51.2 7.3 %collective-permute-start.25 = (f32[512,64]{0,1:T(8,128)S(1)}, f32[512,64]{0,1:T(8,128)S(1)}, u32[]{:S(2)}, u32[]{:S(2)}) collective-permute-start(f32[512,64]{0,1:T(8,128)S(1)} %slice_select_fusion.2), channel_id=1, source_target_pairs={{0,8},{4,12},{8,0},{12,4},{16,24},{20,28},{24,16},{28,20},{1,9},{5... | collective-permute-start | bytes 393224 | tf_op jit(solution)/shard_map/ppermute | solution.py:15
  61.9 7.8 %collective-permute-start.9 = (f32[512,32]{0,1:T(8,128)S(1)}, f32[512,32]{0,1:T(8,128)S(1)}, u32[]{:S(2)}, u32[]{:S(2)}) collective-permute-start(f32[512,32]{0,1:T(8,128)S(1)} %convolution_bitcast_fusion.5), channel_id=1, source_target_pairs={{0,1},{1,2},{2,3},{4,5},{5,6},{6,7},{8,9},{9,10},{10,11},{12,13},{... | collective-permute-start | bytes 196616 | tf_op jit(solution)/shard_map/ppermute | solution.py:10
  64.0 10.7 %collective-permute-start.27 = (f32[512,32]{0,1:T(8,128)S(1)}, f32[512,32]{0,1:T(8,128)S(1)}, u32[]{:S(2)}, u32[]{:S(2)}) collective-permute-start(f32[512,32]{0,1:T(8,128)S(1)} %convolution_bitcast_fusion.2), channel_id=1, source_target_pairs={{0,1},{1,2},{2,3},{4,5},{5,6},{6,7},{8,9},{9,10},{10,11},{12,13},{... | collective-permute-start | bytes 196616 | tf_op jit(solution)/shard_map/ppermute | solution.py:10
  70.3 6.9 %collective-permute-start.10 = (f32[512,32]{0,1:T(8,128)S(1)}, f32[512,32]{0,1:T(8,128)S(1)}, u32[]{:S(2)}, u32[]{:S(2)}) collective-permute-start(f32[512,32]{0,1:T(8,128)S(1)} %convolution_add_fusion.13), channel_id=1, source_target_pairs={{0,1},{1,2},{2,3},{4,5},{5,6},{6,7},{8,9},{9,10},{10,11},{12,13},{... | collective-permute-start | bytes 196616 | tf_op jit(solution)/shard_map/ppermute | solution.py:10
  75.2 6.2 %collective-permute-start.28 = (f32[512,32]{0,1:T(8,128)S(1)}, f32[512,32]{0,1:T(8,128)S(1)}, u32[]{:S(2)}, u32[]{:S(2)}) collective-permute-start(f32[512,32]{0,1:T(8,128)S(1)} %convolution_add_fusion.8), channel_id=1, source_target_pairs={{0,1},{1,2},{2,3},{4,5},{5,6},{6,7},{8,9},{9,10},{10,11},{12,13},{... | collective-permute-start | bytes 196616 | tf_op jit(solution)/shard_map/ppermute | solution.py:10
  77.8 6.8 %collective-permute-start.11 = (f32[512,32]{0,1:T(8,128)S(1)}, f32[512,32]{0,1:T(8,128)S(1)}, u32[]{:S(2)}, u32[]{:S(2)}) collective-permute-start(f32[512,32]{0,1:T(8,128)S(1)} %convolution_add_fusion.12), channel_id=1, source_target_pairs={{0,1},{1,2},{2,3},{4,5},{5,6},{6,7},{8,9},{9,10},{10,11},{12,13},{... | collective-permute-start | bytes 196616 | tf_op jit(solution)/shard_map/ppermute | solution.py:10
  85.9 6.7 %collective-permute-start.12 = (f32[512,32]{0,1:T(8,128)S(1)}, f32[512,32]{0,1:T(8,128)S(1)}, u32[]{:S(2)}, u32[]{:S(2)}) collective-permute-start(f32[512,32]{0,1:T(8,128)S(1)} %convolution_bitcast_fusion.4), channel_id=1, source_target_pairs={{1,0},{2,1},{3,2},{5,4},{6,5},{7,6},{9,8},{10,9},{11,10},{13,12},{... | collective-permute-start | bytes 196616 | tf_op jit(solution)/shard_map/ppermute | solution.py:10
  93.0 6.2 %collective-permute-start.13 = (f32[512,32]{0,1:T(8,128)S(1)}, f32[512,32]{0,1:T(8,128)S(1)}, u32[]{:S(2)}, u32[]{:S(2)}) collective-permute-start(f32[512,32]{0,1:T(8,128)S(1)} %convolution_add_fusion.10), channel_id=1, source_target_pairs={{1,0},{2,1},{3,2},{5,4},{6,5},{7,6},{9,8},{10,9},{11,10},{13,12},{... | collective-permute-start | bytes 196616 | tf_op jit(solution)/shard_map/ppermute | solution.py:10
  94.7 6.8 %collective-permute-start.30 = (f32[512,32]{0,1:T(8,128)S(1)}, f32[512,32]{0,1:T(8,128)S(1)}, u32[]{:S(2)}, u32[]{:S(2)}) collective-permute-start(f32[512,32]{0,1:T(8,128)S(1)} %convolution_bitcast_fusion.1), channel_id=1, source_target_pairs={{1,0},{2,1},{3,2},{5,4},{6,5},{7,6},{9,8},{10,9},{11,10},{13,12},{... | collective-permute-start | bytes 196616 | tf_op jit(solution)/shard_map/ppermute | solution.py:10
  99.6 6.6 %collective-permute-start.14 = (f32[512,32]{0,1:T(8,128)S(1)}, f32[512,32]{0,1:T(8,128)S(1)}, u32[]{:S(2)}, u32[]{:S(2)}) collective-permute-start(f32[512,32]{0,1:T(8,128)S(1)} %convolution_add_fusion.9), channel_id=1, source_target_pairs={{1,0},{2,1},{3,2},{5,4},{6,5},{7,6},{9,8},{10,9},{11,10},{13,12},{... | collective-permute-start | bytes 196616 | tf_op jit(solution)/shard_map/ppermute | solution.py:10
  101.9 6.2 %collective-permute-start.31 = (f32[512,32]{0,1:T(8,128)S(1)}, f32[512,32]{0,1:T(8,128)S(1)}, u32[]{:S(2)}, u32[]{:S(2)}) collective-permute-start(f32[512,32]{0,1:T(8,128)S(1)} %convolution_add_fusion.5), channel_id=1, source_target_pairs={{1,0},{2,1},{3,2},{5,4},{6,5},{7,6},{9,8},{10,9},{11,10},{13,12},{... | collective-permute-start | bytes 196616 | tf_op jit(solution)/shard_map/ppermute | solution.py:10
  108.5 6.2 %collective-permute-start.32 = (f32[512,32]{0,1:T(8,128)S(1)}, f32[512,32]{0,1:T(8,128)S(1)}, u32[]{:S(2)}, u32[]{:S(2)}) collective-permute-start(f32[512,32]{0,1:T(8,128)S(1)} %convolution_add_fusion.4), channel_id=1, source_target_pairs={{1,0},{2,1},{3,2},{5,4},{6,5},{7,6},{9,8},{10,9},{11,10},{13,12},{... | collective-permute-start | bytes 196616 | tf_op jit(solution)/shard_map/ppermute | solution.py:10
  116.3 8.3 %collective-permute-start.17 = (f32[512,128]{0,1:T(8,128)S(1)}, f32[512,128]{0,1:T(8,128)S(1)}, u32[]{:S(2)}, u32[]{:S(2)}) collective-permute-start(f32[512,128]{0,1:T(8,128)S(1)} %maximum_select_fusion.4), channel_id=1, source_target_pairs={{0,4},{4,0},{8,12},{12,8},{16,20},{20,16},{24,28},{28,24},{1,5},{5... | collective-permute-start | bytes 786440 | tf_op jit(solution)/shard_map/ppermute | solution.py:15
  125.7 10.5 %collective-permute-start.18 = (f32[256,256]{0,1:T(8,128)S(1)}, f32[256,256]{0,1:T(8,128)S(1)}, u32[]{:S(2)}, u32[]{:S(2)}) collective-permute-start(f32[256,256]{0,1:T(8,128)S(1)} %get-tuple-element.10), channel_id=1, source_target_pairs={{0,1},{4,5},{8,9},{12,13},{16,17},{20,21},{24,25},{28,29}} | collective-permute-start | bytes 786440 | tf_op jit(solution)/shard_map/ppermute | solution.py:108
  129.6 6.6 %collective-permute-start.21 = (f32[256,256]{0,1:T(8,128)S(1)}, f32[256,256]{0,1:T(8,128)S(1)}, u32[]{:S(2)}, u32[]{:S(2)}) collective-permute-start(f32[256,256]{0,1:T(8,128)S(1)} %get-tuple-element.9), channel_id=1, source_target_pairs={{3,2},{7,6},{11,10},{15,14},{19,18},{23,22},{27,26},{31,30}} | collective-permute-start | bytes 786440 | tf_op jit(solution)/shard_map/ppermute | solution.py:109
  131.4 10.4 %collective-permute-start.36 = (f32[256,256]{0,1:T(8,128)S(1)}, f32[256,256]{0,1:T(8,128)S(1)}, u32[]{:S(2)}, u32[]{:S(2)}) collective-permute-start(f32[256,256]{0,1:T(8,128)S(1)} %get-tuple-element.20), channel_id=1, source_target_pairs={{0,1},{4,5},{8,9},{12,13},{16,17},{20,21},{24,25},{28,29}} | collective-permute-start | bytes 786440 | tf_op jit(solution)/shard_map/ppermute | solution.py:108
  132.7 9.1 %collective-permute-start.39 = (f32[256,256]{0,1:T(8,128)S(1)}, f32[256,256]{0,1:T(8,128)S(1)}, u32[]{:S(2)}, u32[]{:S(2)}) collective-permute-start(f32[256,256]{0,1:T(8,128)S(1)} %get-tuple-element.19), channel_id=1, source_target_pairs={{3,2},{7,6},{11,10},{15,14},{19,18},{23,22},{27,26},{31,30}} | collective-permute-start | bytes 786440 | tf_op jit(solution)/shard_map/ppermute | solution.py:109
  136.3 11.1 %collective-permute-start.19 = (f32[256,256]{0,1:T(8,128)S(1)}, f32[256,256]{0,1:T(8,128)S(1)}, u32[]{:S(2)}, u32[]{:S(2)}) collective-permute-start(f32[256,256]{0,1:T(8,128)S(1)} %get-tuple-element.8), channel_id=1, source_target_pairs={{0,1},{1,2},{4,5},{5,6},{8,9},{9,10},{12,13},{13,14},{16,17},{17,1... | collective-permute-start | bytes 786440 | tf_op jit(solution)/shard_map/ppermute | solution.py:108
  140.7 6.7 %collective-permute-start.22 = (f32[256,256]{0,1:T(8,128)S(1)}, f32[256,256]{0,1:T(8,128)S(1)}, u32[]{:S(2)}, u32[]{:S(2)}) collective-permute-start(f32[256,256]{0,1:T(8,128)S(1)} %get-tuple-element.7), channel_id=1, source_target_pairs={{2,1},{3,2},{6,5},{7,6},{10,9},{11,10},{14,13},{15,14},{18,17},{19... | collective-permute-start | bytes 786440 | tf_op jit(solution)/shard_map/ppermute | solution.py:109
  141.9 12.8 %collective-permute-start.37 = (f32[256,256]{0,1:T(8,128)S(1)}, f32[256,256]{0,1:T(8,128)S(1)}, u32[]{:S(2)}, u32[]{:S(2)}) collective-permute-start(f32[256,256]{0,1:T(8,128)S(1)} %get-tuple-element.18), channel_id=1, source_target_pairs={{0,1},{1,2},{4,5},{5,6},{8,9},{9,10},{12,13},{13,14},{16,17},{17,1... | collective-permute-start | bytes 786440 | tf_op jit(solution)/shard_map/ppermute | solution.py:108
  146.3 8.4 %collective-permute-start.40 = (f32[256,256]{0,1:T(8,128)S(1)}, f32[256,256]{0,1:T(8,128)S(1)}, u32[]{:S(2)}, u32[]{:S(2)}) collective-permute-start(f32[256,256]{0,1:T(8,128)S(1)} %get-tuple-element.17), channel_id=1, source_target_pairs={{2,1},{3,2},{6,5},{7,6},{10,9},{11,10},{14,13},{15,14},{18,17},{19... | collective-permute-start | bytes 786440 | tf_op jit(solution)/shard_map/ppermute | solution.py:109
  147.6 13.2 %collective-permute-start.20 = (f32[256,256]{0,1:T(8,128)S(1)}, f32[256,256]{0,1:T(8,128)S(1)}, u32[]{:S(2)}, u32[]{:S(2)}) collective-permute-start(f32[256,256]{0,1:T(8,128)S(1)} %get-tuple-element.6), channel_id=1, source_target_pairs={{0,1},{1,2},{2,3},{4,5},{5,6},{6,7},{8,9},{9,10},{10,11},{12,13},{... | collective-permute-start | bytes 786440 | tf_op jit(solution)/shard_map/ppermute | solution.py:108
  153.4 8.7 %collective-permute-start.23 = (f32[256,256]{0,1:T(8,128)S(1)}, f32[256,256]{0,1:T(8,128)S(1)}, u32[]{:S(2)}, u32[]{:S(2)}) collective-permute-start(f32[256,256]{0,1:T(8,128)S(1)} %get-tuple-element.5), channel_id=1, source_target_pairs={{1,0},{2,1},{3,2},{5,4},{6,5},{7,6},{9,8},{10,9},{11,10},{13,12},{... | collective-permute-start | bytes 786440 | tf_op jit(solution)/shard_map/ppermute | solution.py:109
  154.9 9.0 %collective-permute-start.38 = (f32[256,256]{0,1:T(8,128)S(1)}, f32[256,256]{0,1:T(8,128)S(1)}, u32[]{:S(2)}, u32[]{:S(2)}) collective-permute-start(f32[256,256]{0,1:T(8,128)S(1)} %get-tuple-element.16), channel_id=1, source_target_pairs={{0,1},{1,2},{2,3},{4,5},{5,6},{6,7},{8,9},{9,10},{10,11},{12,13},{... | collective-permute-start | bytes 786440 | tf_op jit(solution)/shard_map/ppermute | solution.py:108
  159.4 8.3 %collective-permute-start.41 = (f32[256,256]{0,1:T(8,128)S(1)}, f32[256,256]{0,1:T(8,128)S(1)}, u32[]{:S(2)}, u32[]{:S(2)}) collective-permute-start(f32[256,256]{0,1:T(8,128)S(1)} %get-tuple-element.15), channel_id=1, source_target_pairs={{1,0},{2,1},{3,2},{5,4},{6,5},{7,6},{9,8},{10,9},{11,10},{13,12},{... | collective-permute-start | bytes 786440 | tf_op jit(solution)/shard_map/ppermute | solution.py:109
  (13 other events, 96.0 us)

commit v17 on v15

--- a/solution.py
+++ b/solution.py
@@ -113,15 +113,18 @@
 def solve(right_side, transfer, diag_inverse, sub_factor):
     driving = product(diag_inverse, right_side)
     chain_length = lax.axis_size("aux")
-    incoming = from_behind(driving, "aux", 1)
-    for _ in range(chain_length - 2):
-        incoming = from_behind(product(transfer, incoming) + driving, "aux", 1)
+    incoming = jnp.zeros_like(driving)
+    for turn in range(chain_length - 1):
+        value = driving if turn == 0 else product(transfer, incoming) + driving
+        incoming = incoming + lax.ppermute(value, "aux", [(turn, turn + 1)])
     solved = product(transfer, incoming) + driving
     source = product(sub_factor.T, product(diag_inverse.T, solved))
     back_map = transfer.T
-    arriving = from_behind(source, "aux", -1)
-    for _ in range(chain_length - 2):
-        arriving = from_behind(product(back_map, arriving) + source, "aux", -1)
+    arriving = jnp.zeros_like(driving)
+    for turn in range(chain_length - 1):
+        sender = chain_length - 1 - turn
+        value = source if turn == 0 else product(back_map, arriving) + source
+        arriving = arriving + lax.ppermute(value, "aux", [(sender, sender - 1)])
     return product(diag_inverse.T, solved - arriving)
 
 

time: 170 us -> 154 us (0.906)
  starting transfers between devices: 79.5 us -> 59.1 us
  waiting for transfers between devices: 62.5 us -> 67.2 us
    ppermute x12, starting transfers between devices: 27.6 us -> 10.8 us  [the longest x6 5.42 us: solve(): arriving = arriving + lax.ppermute(value, 'aux', [(sender, sender - 1)])]
    ppermute x12, waiting for transfers between devices: 13.7 us -> 17.6 us  [the longest x6 17 us: solve(): arriving = arriving + lax.ppermute(value, 'aux', [(sender, sender - 1)])]
    ppermute x6, starting transfers between devices: 24.5 us -> 20.9 us  [reduce_over_aux(): lax.ppermute(to_right + block(index + count - 1 - step), 'aux', rightward)]
  transfers between devices with their start and end apart: 42 -> 42, of which waited for: 22 -> 20; matrix products, arithmetic and copies ran while one was open for 14% -> 16% of each run, Pallas kernels for 0% -> 0%
where the time goes in v17:
time: 154 us; the launch traced here: 153 us
  waiting for transfers between devices  67.2 us (44%)
  starting transfers between devices  59.1 us (38%)
  matrix products  19.1 us (12%)
  local copies, waits for them, and re-layouts  4.24 us (3%)
  other arithmetic  2.88 us (2%)
    ppermute x3, waiting for transfers between devices, gamma_over_aux(): from_right = lax.ppermute(from_right, 'aux', leftward)  23.5 us
    ppermute x6, starting transfers between devices, reduce_over_aux(): lax.ppermute(to_right + block(index + count - 1 - step), 'aux', rightward)  20.9 us
    dot_general x26, matrix products, product(): jnp.dot(left, right, precision=lax.Precision.HIGH, preferred_element_type...  17 us
    ppermute x6, waiting for transfers between devices, solve(): arriving = arriving + lax.ppermute(value, 'aux', [(sender, sender - 1)])  17 us
    ppermute x12, waiting for transfers between devices, swap(): return lax.ppermute(array, axis, [(i, i ^ bit) for i in range(count)])  15.3 us
    ppermute x12, starting transfers between devices, swap(): return lax.ppermute(array, axis, [(i, i ^ bit) for i in range(count)])  10.4 us
    ppermute x3, starting transfers between devices, gamma_over_aux(): from_left = lax.ppermute(from_left, 'aux', rightward)  7.75 us
    ppermute x6, waiting for transfers between devices, reduce_over_aux(): lax.ppermute(to_right + block(index + count - 1 - step), 'aux', rightward)  6.35 us
  transfers between devices with their start and end apart: 42, of which 20 were waited for; matrix products, arithmetic and copies ran while one was open for 16% of the time, Pallas kernels for 0%

profile of v17, /device:TPU:0, one launch (start us, length us, event | category | flops | bytes accessed | tf_op | source)
XLA Modules:
  0.0 153.3 jit_solution(4751588112518187247)
XLA Ops:
  0.0 1.4 collective-permute-start.1
  1.4 6.4 %collective-permute-start = (f32[256,512]{1,0:T(8,128)}, f32[256,512]{1,0:T(8,128)}, u32[]{:S(2)}, u32[]{:S(2)}) collective-permute-start(f32[256,512]{1,0:T(8,128)} %param.6), channel_id=1, source_target_pairs={{0,1},{1,2},{2,3},{4,5},{5,6},{6,7},{8,9},{9,10},{10,11},{12,13},{... | collective-permute-start | bytes 1572872 | tf_op jit(solution)/shard_map/ppermute | solution.py:87
  7.8 2.9 %copy.8 = f32[512,1024]{0,1:T(8,128)} copy(f32[512,1024]{1,0:T(8,128)} %param.5) | data formatting | bytes 4194304 | tf_op args[0]
  10.9 1.8 %bitcast_multiply_fusion = f32[512,1024]{0,1:T(8,128)S(1)} fusion(f32[512,1024]{0,1:T(8,128)} %copy.8, f32[512,16]{0,1:T(8,128)S(1)} %reshape.6), kind=kLoop, calls=%fused_computation | loop fusion | flops 524288 | bytes 4227072 | tf_op jit(solution)/shard_map/mul | solution.py:23
  12.8 1.7 %fusion.22 = f32[512,512]{0,1:T(8,128)S(1)} fusion(f32[256,512]{1,0:T(8,128)} %param.6, f32[512,1024]{0,1:T(8,128)S(1)} %bitcast_multiply_fusion, s32[]{:T(128)S(6)} %select_n.188), kind=kOutput, calls=%fused_computation.47 | convolution fusion | flops 402653184 | bytes 2097156 | tf_op jit(solution)/shard_map/dot_general | solution.py:27
  14.5 2.8 %collective-permute-done.1 = f32[256,512]{1,0:T(8,128)} collective-permute-done((f32[256,512]{1,0:T(8,128)}, f32[256,512]{1,0:T(8,128)}, u32[]{:S(2)}, u32[]{:S(2)}) %collective-permute-start.1) | collective-permute-done | bytes 524320 | tf_op jit(solution)/shard_map/ppermute | solution.py:88
  19.3 1.7 %convolution_add_fusion.3 = f32[512,512]{0,1:T(8,128)S(1)} fusion(f32[512,512]{0,1:T(8,128)S(1)} %fusion.22, f32[256,512]{1,0:T(8,128)} %collective-permute-done, f32[512,1024]{0,1:T(8,128)S(1)} %bitcast_multiply_fusion, s32[]{:T(128)S(6)} %select_n.189), kind=kOutput, calls=%fused_computation.6 | convolution fusion | flops 402915328 | bytes 3145732 | tf_op jit(solution)/shard_map/dot_general | solution.py:27
  21.0 1.7 %convolution_add_fusion.2 = f32[512,512]{0,1:T(8,128)S(1)} fusion(f32[512,512]{0,1:T(8,128)S(1)} %convolution_add_fusion.3, f32[256,512]{1,0:T(8,128)} %collective-permute-done.1, f32[512,1024]{0,1:T(8,128)S(1)} %bitcast_multiply_fusion, s32[]{:T(128)S(6)} %select_n.190), kind=kOutput, calls=%fused_computation.5 | convolution fusion | flops 402915328 | bytes 3145732 | tf_op jit(solution)/shard_map/dot_general | solution.py:27
  22.6 9.8 %collective-permute-done.3 = f32[256,512]{1,0:T(8,128)S(1)} collective-permute-done((f32[256,512]{1,0:T(8,128)}, f32[256,512]{1,0:T(8,128)S(1)}, u32[]{:S(2)}, u32[]{:S(2)}) %collective-permute-start.3) | collective-permute-done | bytes 524320 | tf_op jit(solution)/shard_map/ppermute | solution.py:88
  35.8 10.8 %collective-permute-done.5 = f32[256,512]{1,0:T(8,128)S(1)} collective-permute-done((f32[256,512]{1,0:T(8,128)S(1)}, f32[256,512]{1,0:T(8,128)S(1)}, u32[]{:S(2)}, u32[]{:S(2)}) %collective-permute-start.5) | collective-permute-done | bytes 524320 | tf_op jit(solution)/shard_map/ppermute | solution.py:88
  52.3 4.2 %collective-permute-done.7 = f32[512,64]{0,1:T(8,128)S(1)} collective-permute-done((f32[512,64]{0,1:T(8,128)S(1)}, f32[512,64]{0,1:T(8,128)S(1)}, u32[]{:S(2)}, u32[]{:S(2)}) %collective-permute-start.7) | collective-permute-done | bytes 131104 | tf_op jit(solution)/shard_map/ppermute | solution.py:15
  59.7 1.7 %collective-permute-done.8 = f32[512,32]{0,1:T(8,128)S(1)} collective-permute-done((f32[512,32]{0,1:T(8,128)S(1)}, f32[512,32]{0,1:T(8,128)S(1)}, u32[]{:S(2)}, u32[]{:S(2)}) %collective-permute-start.8) | collective-permute-done | bytes 65568 | tf_op jit(solution)/shard_map/ppermute | solution.py:15
  61.9 1.4 collective-permute-start.9
  64.0 1.3 collective-permute-start.27
  79.1 14.8 %collective-permute-done.14 = f32[512,32]{0,1:T(8,128)S(1)} collective-permute-done((f32[512,32]{0,1:T(8,128)S(1)}, f32[512,32]{0,1:T(8,128)S(1)}, u32[]{:S(2)}, u32[]{:S(2)}) %collective-permute-start.14) | collective-permute-done | bytes 65568 | tf_op jit(solution)/shard_map/ppermute | solution.py:127
  94.3 1.6 %collective-permute-start.15 = (f32[512,32]{0,1:T(8,128)S(1)}, f32[512,32]{0,1:T(8,128)S(1)}, u32[]{:S(2)}, u32[]{:S(2)}) collective-permute-start(f32[512,32]{0,1:T(8,128)S(1)} %convolution_bitcast_fusion.3), channel_id=1, source_target_pairs={{0,16},{4,20},{8,24},{12,28},{16,0},{20,4},{24,8},{28,12},{1,17},{... | collective-permute-start | bytes 196616 | tf_op jit(solution)/shard_map/ppermute | solution.py:15
  96.3 1.3 collective-permute-start.32
  98.7 1.6 %collective-permute-start.16 = (f32[512,64]{0,1:T(8,128)S(1)}, f32[512,64]{0,1:T(8,128)S(1)}, u32[]{:S(2)}, u32[]{:S(2)}) collective-permute-start(f32[512,64]{0,1:T(8,128)S(1)} %maximum_select_fusion.6), channel_id=1, source_target_pairs={{0,8},{4,12},{8,0},{12,4},{16,24},{20,28},{24,16},{28,20},{1,9},{5... | collective-permute-start | bytes 393224 | tf_op jit(solution)/shard_map/ppermute | solution.py:15
  100.3 2.2 %collective-permute-done.32 = f32[512,32]{0,1:T(8,128)S(1)} collective-permute-done((f32[512,32]{0,1:T(8,128)S(1)}, f32[512,32]{0,1:T(8,128)S(1)}, u32[]{:S(2)}, u32[]{:S(2)}) %collective-permute-start.32) | collective-permute-done | bytes 65568 | tf_op jit(solution)/shard_map/ppermute | solution.py:127
  103.8 3.4 %collective-permute-done.33 = f32[512,32]{0,1:T(8,128)S(1)} collective-permute-done((f32[512,32]{0,1:T(8,128)S(1)}, f32[512,32]{0,1:T(8,128)S(1)}, u32[]{:S(2)}, u32[]{:S(2)}) %collective-permute-start.33) | collective-permute-done | bytes 65568 | tf_op jit(solution)/shard_map/ppermute | solution.py:15
  107.2 1.6 %collective-permute-start.34 = (f32[512,64]{0,1:T(8,128)S(1)}, f32[512,64]{0,1:T(8,128)S(1)}, u32[]{:S(2)}, u32[]{:S(2)}) collective-permute-start(f32[512,64]{0,1:T(8,128)S(1)} %maximum_select_fusion.7), channel_id=1, source_target_pairs={{0,8},{4,12},{8,0},{12,4},{16,24},{20,28},{24,16},{28,20},{1,9},{5... | collective-permute-start | bytes 393224 | tf_op jit(solution)/shard_map/ppermute | solution.py:15
  108.8 3.5 %collective-permute-done.34 = f32[512,64]{0,1:T(8,128)S(1)} collective-permute-done((f32[512,64]{0,1:T(8,128)S(1)}, f32[512,64]{0,1:T(8,128)S(1)}, u32[]{:S(2)}, u32[]{:S(2)}) %collective-permute-start.34) | collective-permute-done | bytes 131104 | tf_op jit(solution)/shard_map/ppermute | solution.py:15
  113.5 1.6 %collective-permute-start.18 = (f32[256,256]{0,1:T(8,128)S(1)}, f32[256,256]{0,1:T(8,128)S(1)}, u32[]{:S(2)}, u32[]{:S(2)}) collective-permute-start(f32[256,256]{0,1:T(8,128)S(1)} %get-tuple-element.10), channel_id=1, source_target_pairs={{0,1},{4,5},{8,9},{12,13},{16,17},{20,21},{24,25},{28,29}} | collective-permute-start | bytes 786440 | tf_op jit(solution)/shard_map/ppermute | solution.py:108
  116.9 1.3 collective-permute-start.36
  118.9 2.8 %collective-permute-done.18 = f32[256,256]{0,1:T(8,128)S(1)} collective-permute-done((f32[256,256]{0,1:T(8,128)S(1)}, f32[256,256]{0,1:T(8,128)S(1)}, u32[]{:S(2)}, u32[]{:S(2)}) %collective-permute-start.18) | collective-permute-done | bytes 262176 | tf_op jit(solution)/shard_map/ppermute | solution.py:108
  121.8 4.4 %collective-permute-start.19 = (f32[256,256]{0,1:T(8,128)S(1)}, f32[256,256]{0,1:T(8,128)S(1)}, u32[]{:S(2)}, u32[]{:S(2)}) collective-permute-start(f32[256,256]{0,1:T(8,128)S(1)} %get-tuple-element.8), channel_id=1, source_target_pairs={{0,1},{1,2},{4,5},{5,6},{8,9},{9,10},{12,13},{13,14},{16,17},{17,1... | collective-permute-start | bytes 786440 | tf_op jit(solution)/shard_map/ppermute | solution.py:108
  127.4 4.4 %collective-permute-start.37 = (f32[256,256]{0,1:T(8,128)S(1)}, f32[256,256]{0,1:T(8,128)S(1)}, u32[]{:S(2)}, u32[]{:S(2)}) collective-permute-start(f32[256,256]{0,1:T(8,128)S(1)} %get-tuple-element.18), channel_id=1, source_target_pairs={{0,1},{1,2},{4,5},{5,6},{8,9},{9,10},{12,13},{13,14},{16,17},{17,1... | collective-permute-start | bytes 786440 | tf_op jit(solution)/shard_map/ppermute | solution.py:108
  133.0 4.6 %collective-permute-start.20 = (f32[256,256]{0,1:T(8,128)S(1)}, f32[256,256]{0,1:T(8,128)S(1)}, u32[]{:S(2)}, u32[]{:S(2)}) collective-permute-start(f32[256,256]{0,1:T(8,128)S(1)} %get-tuple-element.6), channel_id=1, source_target_pairs={{0,1},{1,2},{2,3},{4,5},{5,6},{6,7},{8,9},{9,10},{10,11},{12,13},{... | collective-permute-start | bytes 786440 | tf_op jit(solution)/shard_map/ppermute | solution.py:108
  139.1 4.6 %collective-permute-start.38 = (f32[256,256]{0,1:T(8,128)S(1)}, f32[256,256]{0,1:T(8,128)S(1)}, u32[]{:S(2)}, u32[]{:S(2)}) collective-permute-start(f32[256,256]{0,1:T(8,128)S(1)} %get-tuple-element.16), channel_id=1, source_target_pairs={{0,1},{1,2},{2,3},{4,5},{5,6},{6,7},{8,9},{9,10},{10,11},{12,13},{... | collective-permute-start | bytes 786440 | tf_op jit(solution)/shard_map/ppermute | solution.py:108
  144.9 1.6 %collective-permute-done.23 = f32[256,256]{0,1:T(8,128)S(1)} collective-permute-done((f32[256,256]{0,1:T(8,128)S(1)}, f32[256,256]{0,1:T(8,128)S(1)}, u32[]{:S(2)}, u32[]{:S(2)}) %collective-permute-start.23) | collective-permute-done | bytes 262176 | tf_op jit(solution)/shard_map/ppermute | solution.py:109
  146.6 2.7 %collective-permute-done.38 = f32[256,256]{0,1:T(8,128)S(1)} collective-permute-done((f32[256,256]{0,1:T(8,128)S(1)}, f32[256,256]{0,1:T(8,128)S(1)}, u32[]{:S(2)}, u32[]{:S(2)}) %collective-permute-start.38) | collective-permute-done | bytes 262176 | tf_op jit(solution)/shard_map/ppermute | solution.py:108
  149.3 2.8 %collective-permute-done.41 = f32[256,256]{0,1:T(8,128)S(1)} collective-permute-done((f32[256,256]{0,1:T(8,128)S(1)}, f32[256,256]{0,1:T(8,128)S(1)}, u32[]{:S(2)}, u32[]{:S(2)}) %collective-permute-start.41) | collective-permute-done | bytes 262176 | tf_op jit(solution)/shard_map/ppermute | solution.py:109
  (118 shorter events, 42.1 us)
Async XLA Ops:
  0.0 17.3 %collective-permute-start.1 = (f32[256,512]{1,0:T(8,128)}, f32[256,512]{1,0:T(8,128)}, u32[]{:S(2)}, u32[]{:S(2)}) collective-permute-start(f32[256,512]{1,0:T(8,128)} %param.6), channel_id=1, source_target_pairs={{1,0},{2,1},{3,2},{5,4},{6,5},{7,6},{9,8},{10,9},{11,10},{13,12},{... | collective-permute-start | bytes 1572872 | tf_op jit(solution)/shard_map/ppermute | solution.py:88
  1.4 17.2 %collective-permute-start = (f32[256,512]{1,0:T(8,128)}, f32[256,512]{1,0:T(8,128)}, u32[]{:S(2)}, u32[]{:S(2)}) collective-permute-start(f32[256,512]{1,0:T(8,128)} %param.6), channel_id=1, source_target_pairs={{0,1},{1,2},{2,3},{4,5},{5,6},{6,7},{8,9},{9,10},{10,11},{12,13},{... | collective-permute-start | bytes 1572872 | tf_op jit(solution)/shard_map/ppermute | solution.py:87
  17.3 15.2 %collective-permute-start.3 = (f32[256,512]{1,0:T(8,128)}, f32[256,512]{1,0:T(8,128)S(1)}, u32[]{:S(2)}, u32[]{:S(2)}) collective-permute-start(f32[256,512]{1,0:T(8,128)} %collective-permute-done.1), channel_id=1, source_target_pairs={{1,0},{2,1},{5,4},{6,5},{9,8},{10,9},{13,12},{14,13},{17,16},{18,1... | collective-permute-start | bytes 1572872 | tf_op jit(solution)/shard_map/ppermute | solution.py:88
  18.6 15.2 %collective-permute-start.2 = (f32[256,512]{1,0:T(8,128)}, f32[256,512]{1,0:T(8,128)S(1)}, u32[]{:S(2)}, u32[]{:S(2)}) collective-permute-start(f32[256,512]{1,0:T(8,128)} %collective-permute-done), channel_id=1, source_target_pairs={{1,2},{2,3},{5,6},{6,7},{9,10},{10,11},{13,14},{14,15},{17,18},{18... | collective-permute-start | bytes 1572872 | tf_op jit(solution)/shard_map/ppermute | solution.py:87
  32.5 14.1 %collective-permute-start.5 = (f32[256,512]{1,0:T(8,128)S(1)}, f32[256,512]{1,0:T(8,128)S(1)}, u32[]{:S(2)}, u32[]{:S(2)}) collective-permute-start(f32[256,512]{1,0:T(8,128)S(1)} %collective-permute-done.3), channel_id=1, source_target_pairs={{1,0},{5,4},{9,8},{13,12},{17,16},{21,20},{25,24},{29,28}} | collective-permute-start | bytes 1572872 | tf_op jit(solution)/shard_map/ppermute | solution.py:88
  33.8 13.4 %collective-permute-start.4 = (f32[256,512]{1,0:T(8,128)S(1)}, f32[256,512]{1,0:T(8,128)S(1)}, u32[]{:S(2)}, u32[]{:S(2)}) collective-permute-start(f32[256,512]{1,0:T(8,128)S(1)} %collective-permute-done.2), channel_id=1, source_target_pairs={{2,3},{6,7},{10,11},{14,15},{18,19},{22,23},{26,27},{30,31}} | collective-permute-start | bytes 1572872 | tf_op jit(solution)/shard_map/ppermute | solution.py:87
  50.1 6.4 %collective-permute-start.7 = (f32[512,64]{0,1:T(8,128)S(1)}, f32[512,64]{0,1:T(8,128)S(1)}, u32[]{:S(2)}, u32[]{:S(2)}) collective-permute-start(f32[512,64]{0,1:T(8,128)S(1)} %slice_select_fusion.3), channel_id=1, source_target_pairs={{0,8},{4,12},{8,0},{12,4},{16,24},{20,28},{24,16},{28,20},{1,9},{5... | collective-permute-start | bytes 393224 | tf_op jit(solution)/shard_map/ppermute | solution.py:15
  51.2 7.3 %collective-permute-start.25 = (f32[512,64]{0,1:T(8,128)S(1)}, f32[512,64]{0,1:T(8,128)S(1)}, u32[]{:S(2)}, u32[]{:S(2)}) collective-permute-start(f32[512,64]{0,1:T(8,128)S(1)} %slice_select_fusion.2), channel_id=1, source_target_pairs={{0,8},{4,12},{8,0},{12,4},{16,24},{20,28},{24,16},{28,20},{1,9},{5... | collective-permute-start | bytes 393224 | tf_op jit(solution)/shard_map/ppermute | solution.py:15
  56.6 4.8 %collective-permute-start.8 = (f32[512,32]{0,1:T(8,128)S(1)}, f32[512,32]{0,1:T(8,128)S(1)}, u32[]{:S(2)}, u32[]{:S(2)}) collective-permute-start(f32[512,32]{0,1:T(8,128)S(1)} %slice_select_fusion.5), channel_id=1, source_target_pairs={{0,16},{4,20},{8,24},{12,28},{16,0},{20,4},{24,8},{28,12},{1,17},{... | collective-permute-start | bytes 196616 | tf_op jit(solution)/shard_map/ppermute | solution.py:15
  58.6 4.8 %collective-permute-start.26 = (f32[512,32]{0,1:T(8,128)S(1)}, f32[512,32]{0,1:T(8,128)S(1)}, u32[]{:S(2)}, u32[]{:S(2)}) collective-permute-start(f32[512,32]{0,1:T(8,128)S(1)} %slice_select_fusion.4), channel_id=1, source_target_pairs={{0,16},{4,20},{8,24},{12,28},{16,0},{20,4},{24,8},{28,12},{1,17},{... | collective-permute-start | bytes 196616 | tf_op jit(solution)/shard_map/ppermute | solution.py:15
  61.9 3.4 %collective-permute-start.9 = (f32[512,32]{0,1:T(8,128)S(1)}, f32[512,32]{0,1:T(8,128)S(1)}, u32[]{:S(2)}, u32[]{:S(2)}) collective-permute-start(f32[512,32]{0,1:T(8,128)S(1)} %convolution_bitcast_fusion.5), channel_id=1, source_target_pairs={{0,1},{4,5},{8,9},{12,13},{16,17},{20,21},{24,25},{28,29}} | collective-permute-start | bytes 196616 | tf_op jit(solution)/shard_map/ppermute | solution.py:119
  64.0 3.2 %collective-permute-start.27 = (f32[512,32]{0,1:T(8,128)S(1)}, f32[512,32]{0,1:T(8,128)S(1)}, u32[]{:S(2)}, u32[]{:S(2)}) collective-permute-start(f32[512,32]{0,1:T(8,128)S(1)} %convolution_bitcast_fusion.2), channel_id=1, source_target_pairs={{0,1},{4,5},{8,9},{12,13},{16,17},{20,21},{24,25},{28,29}} | collective-permute-start | bytes 196616 | tf_op jit(solution)/shard_map/ppermute | solution.py:119
  77.8 16.1 %collective-permute-start.14 = (f32[512,32]{0,1:T(8,128)S(1)}, f32[512,32]{0,1:T(8,128)S(1)}, u32[]{:S(2)}, u32[]{:S(2)}) collective-permute-start(f32[512,32]{0,1:T(8,128)S(1)} %convolution_add_fusion.9), channel_id=1, source_target_pairs={{1,0},{5,4},{9,8},{13,12},{17,16},{21,20},{25,24},{29,28}} | collective-permute-start | bytes 196616 | tf_op jit(solution)/shard_map/ppermute | solution.py:127
  94.3 4.3 %collective-permute-start.15 = (f32[512,32]{0,1:T(8,128)S(1)}, f32[512,32]{0,1:T(8,128)S(1)}, u32[]{:S(2)}, u32[]{:S(2)}) collective-permute-start(f32[512,32]{0,1:T(8,128)S(1)} %convolution_bitcast_fusion.3), channel_id=1, source_target_pairs={{0,16},{4,20},{8,24},{12,28},{16,0},{20,4},{24,8},{28,12},{1,17},{... | collective-permute-start | bytes 196616 | tf_op jit(solution)/shard_map/ppermute | solution.py:15
  96.3 6.2 %collective-permute-start.32 = (f32[512,32]{0,1:T(8,128)S(1)}, f32[512,32]{0,1:T(8,128)S(1)}, u32[]{:S(2)}, u32[]{:S(2)}) collective-permute-start(f32[512,32]{0,1:T(8,128)S(1)} %convolution_add_fusion.4), channel_id=1, source_target_pairs={{1,0},{5,4},{9,8},{13,12},{17,16},{21,20},{25,24},{29,28}} | collective-permute-start | bytes 196616 | tf_op jit(solution)/shard_map/ppermute | solution.py:127
  98.7 5.0 %collective-permute-start.16 = (f32[512,64]{0,1:T(8,128)S(1)}, f32[512,64]{0,1:T(8,128)S(1)}, u32[]{:S(2)}, u32[]{:S(2)}) collective-permute-start(f32[512,64]{0,1:T(8,128)S(1)} %maximum_select_fusion.6), channel_id=1, source_target_pairs={{0,8},{4,12},{8,0},{12,4},{16,24},{20,28},{24,16},{28,20},{1,9},{5... | collective-permute-start | bytes 393224 | tf_op jit(solution)/shard_map/ppermute | solution.py:15
  102.9 4.3 %collective-permute-start.33 = (f32[512,32]{0,1:T(8,128)S(1)}, f32[512,32]{0,1:T(8,128)S(1)}, u32[]{:S(2)}, u32[]{:S(2)}) collective-permute-start(f32[512,32]{0,1:T(8,128)S(1)} %convolution_bitcast_fusion), channel_id=1, source_target_pairs={{0,16},{4,20},{8,24},{12,28},{16,0},{20,4},{24,8},{28,12},{1,17},{... | collective-permute-start | bytes 196616 | tf_op jit(solution)/shard_map/ppermute | solution.py:15
  103.7 8.6 %collective-permute-start.17 = (f32[512,128]{0,1:T(8,128)S(1)}, f32[512,128]{0,1:T(8,128)S(1)}, u32[]{:S(2)}, u32[]{:S(2)}) collective-permute-start(f32[512,128]{0,1:T(8,128)S(1)} %maximum_select_fusion.4), channel_id=1, source_target_pairs={{0,4},{4,0},{8,12},{12,8},{16,20},{20,16},{24,28},{28,24},{1,5},{5... | collective-permute-start | bytes 786440 | tf_op jit(solution)/shard_map/ppermute | solution.py:15
  107.2 5.0 %collective-permute-start.34 = (f32[512,64]{0,1:T(8,128)S(1)}, f32[512,64]{0,1:T(8,128)S(1)}, u32[]{:S(2)}, u32[]{:S(2)}) collective-permute-start(f32[512,64]{0,1:T(8,128)S(1)} %maximum_select_fusion.7), channel_id=1, source_target_pairs={{0,8},{4,12},{8,0},{12,4},{16,24},{20,28},{24,16},{28,20},{1,9},{5... | collective-permute-start | bytes 393224 | tf_op jit(solution)/shard_map/ppermute | solution.py:15
  112.3 3.5 %collective-permute-start.35 = (f32[512,128]{0,1:T(8,128)S(1)}, f32[512,128]{0,1:T(8,128)S(1)}, u32[]{:S(2)}, u32[]{:S(2)}) collective-permute-start(f32[512,128]{0,1:T(8,128)S(1)} %maximum_select_fusion.5), channel_id=1, source_target_pairs={{0,4},{4,0},{8,12},{12,8},{16,20},{20,16},{24,28},{28,24},{1,5},{5... | collective-permute-start | bytes 786440 | tf_op jit(solution)/shard_map/ppermute | solution.py:15
  113.5 8.2 %collective-permute-start.18 = (f32[256,256]{0,1:T(8,128)S(1)}, f32[256,256]{0,1:T(8,128)S(1)}, u32[]{:S(2)}, u32[]{:S(2)}) collective-permute-start(f32[256,256]{0,1:T(8,128)S(1)} %get-tuple-element.10), channel_id=1, source_target_pairs={{0,1},{4,5},{8,9},{12,13},{16,17},{20,21},{24,25},{28,29}} | collective-permute-start | bytes 786440 | tf_op jit(solution)/shard_map/ppermute | solution.py:108
  115.1 6.6 %collective-permute-start.21 = (f32[256,256]{0,1:T(8,128)S(1)}, f32[256,256]{0,1:T(8,128)S(1)}, u32[]{:S(2)}, u32[]{:S(2)}) collective-permute-start(f32[256,256]{0,1:T(8,128)S(1)} %get-tuple-element.9), channel_id=1, source_target_pairs={{3,2},{7,6},{11,10},{15,14},{19,18},{23,22},{27,26},{31,30}} | collective-permute-start | bytes 786440 | tf_op jit(solution)/shard_map/ppermute | solution.py:109
  116.9 10.4 %collective-permute-start.36 = (f32[256,256]{0,1:T(8,128)S(1)}, f32[256,256]{0,1:T(8,128)S(1)}, u32[]{:S(2)}, u32[]{:S(2)}) collective-permute-start(f32[256,256]{0,1:T(8,128)S(1)} %get-tuple-element.20), channel_id=1, source_target_pairs={{0,1},{4,5},{8,9},{12,13},{16,17},{20,21},{24,25},{28,29}} | collective-permute-start | bytes 786440 | tf_op jit(solution)/shard_map/ppermute | solution.py:108
  118.2 9.1 %collective-permute-start.39 = (f32[256,256]{0,1:T(8,128)S(1)}, f32[256,256]{0,1:T(8,128)S(1)}, u32[]{:S(2)}, u32[]{:S(2)}) collective-permute-start(f32[256,256]{0,1:T(8,128)S(1)} %get-tuple-element.19), channel_id=1, source_target_pairs={{3,2},{7,6},{11,10},{15,14},{19,18},{23,22},{27,26},{31,30}} | collective-permute-start | bytes 786440 | tf_op jit(solution)/shard_map/ppermute | solution.py:109
  121.8 11.1 %collective-permute-start.19 = (f32[256,256]{0,1:T(8,128)S(1)}, f32[256,256]{0,1:T(8,128)S(1)}, u32[]{:S(2)}, u32[]{:S(2)}) collective-permute-start(f32[256,256]{0,1:T(8,128)S(1)} %get-tuple-element.8), channel_id=1, source_target_pairs={{0,1},{1,2},{4,5},{5,6},{8,9},{9,10},{12,13},{13,14},{16,17},{17,1... | collective-permute-start | bytes 786440 | tf_op jit(solution)/shard_map/ppermute | solution.py:108
  126.2 6.7 %collective-permute-start.22 = (f32[256,256]{0,1:T(8,128)S(1)}, f32[256,256]{0,1:T(8,128)S(1)}, u32[]{:S(2)}, u32[]{:S(2)}) collective-permute-start(f32[256,256]{0,1:T(8,128)S(1)} %get-tuple-element.7), channel_id=1, source_target_pairs={{2,1},{3,2},{6,5},{7,6},{10,9},{11,10},{14,13},{15,14},{18,17},{19... | collective-permute-start | bytes 786440 | tf_op jit(solution)/shard_map/ppermute | solution.py:109
  127.4 11.5 %collective-permute-start.37 = (f32[256,256]{0,1:T(8,128)S(1)}, f32[256,256]{0,1:T(8,128)S(1)}, u32[]{:S(2)}, u32[]{:S(2)}) collective-permute-start(f32[256,256]{0,1:T(8,128)S(1)} %get-tuple-element.18), channel_id=1, source_target_pairs={{0,1},{1,2},{4,5},{5,6},{8,9},{9,10},{12,13},{13,14},{16,17},{17,1... | collective-permute-start | bytes 786440 | tf_op jit(solution)/shard_map/ppermute | solution.py:108
  131.8 7.1 %collective-permute-start.40 = (f32[256,256]{0,1:T(8,128)S(1)}, f32[256,256]{0,1:T(8,128)S(1)}, u32[]{:S(2)}, u32[]{:S(2)}) collective-permute-start(f32[256,256]{0,1:T(8,128)S(1)} %get-tuple-element.17), channel_id=1, source_target_pairs={{2,1},{3,2},{6,5},{7,6},{10,9},{11,10},{14,13},{15,14},{18,17},{19... | collective-permute-start | bytes 786440 | tf_op jit(solution)/shard_map/ppermute | solution.py:109
  133.0 11.9 %collective-permute-start.20 = (f32[256,256]{0,1:T(8,128)S(1)}, f32[256,256]{0,1:T(8,128)S(1)}, u32[]{:S(2)}, u32[]{:S(2)}) collective-permute-start(f32[256,256]{0,1:T(8,128)S(1)} %get-tuple-element.6), channel_id=1, source_target_pairs={{0,1},{1,2},{2,3},{4,5},{5,6},{6,7},{8,9},{9,10},{10,11},{12,13},{... | collective-permute-start | bytes 786440 | tf_op jit(solution)/shard_map/ppermute | solution.py:108
  137.6 8.9 %collective-permute-start.23 = (f32[256,256]{0,1:T(8,128)S(1)}, f32[256,256]{0,1:T(8,128)S(1)}, u32[]{:S(2)}, u32[]{:S(2)}) collective-permute-start(f32[256,256]{0,1:T(8,128)S(1)} %get-tuple-element.5), channel_id=1, source_target_pairs={{1,0},{2,1},{3,2},{5,4},{6,5},{7,6},{9,8},{10,9},{11,10},{13,12},{... | collective-permute-start | bytes 786440 | tf_op jit(solution)/shard_map/ppermute | solution.py:109
  139.1 10.3 %collective-permute-start.38 = (f32[256,256]{0,1:T(8,128)S(1)}, f32[256,256]{0,1:T(8,128)S(1)}, u32[]{:S(2)}, u32[]{:S(2)}) collective-permute-start(f32[256,256]{0,1:T(8,128)S(1)} %get-tuple-element.16), channel_id=1, source_target_pairs={{0,1},{1,2},{2,3},{4,5},{5,6},{6,7},{8,9},{9,10},{10,11},{12,13},{... | collective-permute-start | bytes 786440 | tf_op jit(solution)/shard_map/ppermute | solution.py:108
  143.6 8.5 %collective-permute-start.41 = (f32[256,256]{0,1:T(8,128)S(1)}, f32[256,256]{0,1:T(8,128)S(1)}, u32[]{:S(2)}, u32[]{:S(2)}) collective-permute-start(f32[256,256]{0,1:T(8,128)S(1)} %get-tuple-element.15), channel_id=1, source_target_pairs={{1,0},{2,1},{3,2},{5,4},{6,5},{7,6},{9,8},{10,9},{11,10},{13,12},{... | collective-permute-start | bytes 786440 | tf_op jit(solution)/shard_map/ppermute | solution.py:109
  (13 other events, 74.5 us)

commit v18 on v17

--- a/solution.py
+++ b/solution.py
@@ -128,7 +128,7 @@
     return product(diag_inverse.T, solved - arriving)
 
 
-SLICES = 2
+SLICES = 1
 
 
 def per_device(three_center, densities, screen_mask, diag_inverse, sub_factor):

time: 154 us -> 172 us (1.12)
  waiting for transfers between devices: 67.2 us -> 107 us
  starting transfers between devices: 59.1 us -> 36.6 us
  other arithmetic: 2.88 us -> 7.52 us
  matrix products: 19.1 us -> 15 us
    ppermute x6 -> x3, waiting for transfers between devices: 6.35 us -> 29.3 us  [reduce_over_aux(): lax.ppermute(to_right + block(index + count - 1 - step), 'aux', rightward)]
    ppermute x12 -> x6, waiting for transfers between devices: 15.3 us -> 24.9 us  [swap(): return lax.ppermute(array, axis, [(i, i ^ bit) for i in range(count)])]
    ppermute x6 -> x3, starting transfers between devices: 20.9 us -> 12.3 us  [reduce_over_aux(): lax.ppermute(to_right + block(index + count - 1 - step), 'aux', rightward)]
    ppermute x6 -> x3, waiting for transfers between devices: 17 us -> 23.6 us  [solve(): arriving = arriving + lax.ppermute(value, 'aux', [(sender, sender - 1)])]
    ppermute x12 -> x6, starting transfers between devices: 10.4 us -> 4.37 us  [swap(): return lax.ppermute(array, axis, [(i, i ^ bit) for i in range(count)])]
    dot_general x26 -> x17, matrix products: 17 us -> 13.1 us  [product(): jnp.dot(left, right, precision=lax.Precision.HIGH, preferred_element_type...]
    ppermute x6 -> x3, starting transfers between devices: 5.4 us -> 2.78 us  [solve(): incoming = incoming + lax.ppermute(value, 'aux', [(turn, turn + 1)])]
    ppermute x6 -> x3, starting transfers between devices: 5.42 us -> 2.81 us  [solve(): arriving = arriving + lax.ppermute(value, 'aux', [(sender, sender - 1)])]
  transfers between devices with their start and end apart: 42 -> 24, of which waited for: 20 -> 15; matrix products, arithmetic and copies ran while one was open for 16% -> 8% of each run, Pallas kernels for 0% -> 0%
where the time goes in v18:
time: 172 us; the launch traced here: 171 us
  waiting for transfers between devices  107 us (62%)
  starting transfers between devices  36.6 us (21%)
  matrix products  15 us (9%)
  other arithmetic  7.52 us (4%)
  local copies, waits for them, and re-layouts  5.01 us (3%)
    ppermute x3, waiting for transfers between devices, reduce_over_aux(): lax.ppermute(to_right + block(index + count - 1 - step), 'aux', rightward)  29.3 us
    ppermute x6, waiting for transfers between devices, swap(): return lax.ppermute(array, axis, [(i, i ^ bit) for i in range(count)])  24.9 us
    ppermute x3, waiting for transfers between devices, solve(): arriving = arriving + lax.ppermute(value, 'aux', [(sender, sender - 1)])  23.6 us
    ppermute x3, waiting for transfers between devices, gamma_over_aux(): from_right = lax.ppermute(from_right, 'aux', leftward)  23.4 us
    dot_general x17, matrix products, product(): jnp.dot(left, right, precision=lax.Precision.HIGH, preferred_element_type...  13.1 us
    ppermute x3, starting transfers between devices, reduce_over_aux(): lax.ppermute(to_right + block(index + count - 1 - step), 'aux', rightward)  12.3 us
    ppermute x3, starting transfers between devices, gamma_over_aux(): from_left = lax.ppermute(from_left, 'aux', rightward)  7.75 us
    unnamed x11, local copies, waits for them, and re-layouts  4.7 us
  transfers between devices with their start and end apart: 24, of which 15 were waited for; matrix products, arithmetic and copies ran while one was open for 8% of the time, Pallas kernels for 0%

profile of v18, /device:TPU:0, one launch (start us, length us, event | category | flops | bytes accessed | tf_op | source)
XLA Modules:
  0.0 171.4 jit_solution(2577111585130676749)
XLA Ops:
  0.0 1.4 collective-permute-start.1
  1.4 6.4 %collective-permute-start = (f32[256,512]{1,0:T(8,128)}, f32[256,512]{1,0:T(8,128)}, u32[]{:S(2)}, u32[]{:S(2)}) collective-permute-start(f32[256,512]{1,0:T(8,128)} %param.6), channel_id=1, source_target_pairs={{0,1},{1,2},{2,3},{4,5},{5,6},{6,7},{8,9},{9,10},{10,11},{12,13},{... | collective-permute-start | bytes 1572872 | tf_op jit(solution)/shard_map/ppermute | solution.py:87
  7.8 2.9 %copy.7 = f32[512,1024]{0,1:T(8,128)} copy(f32[512,1024]{1,0:T(8,128)} %param.5) | data formatting | bytes 4194304 | tf_op args[0]
  10.9 1.8 %bitcast_multiply_fusion = f32[512,1024]{0,1:T(8,128)S(1)} fusion(f32[512,1024]{0,1:T(8,128)} %copy.7, f32[512,16]{0,1:T(8,128)S(1)} %reshape.6), kind=kLoop, calls=%fused_computation | loop fusion | flops 524288 | bytes 4227072 | tf_op jit(solution)/shard_map/mul | solution.py:23
  12.8 1.7 fusion.16
  14.5 2.8 %collective-permute-done.1 = f32[256,512]{1,0:T(8,128)} collective-permute-done((f32[256,512]{1,0:T(8,128)}, f32[256,512]{1,0:T(8,128)}, u32[]{:S(2)}, u32[]{:S(2)}) %collective-permute-start.1) | collective-permute-done | bytes 524320 | tf_op jit(solution)/shard_map/ppermute | solution.py:88
  17.3 1.3 collective-permute-start.3
  19.3 1.7 convolution_add_fusion.3
  21.0 1.7 convolution_add_fusion.2
  22.7 9.8 %collective-permute-done.3 = f32[256,512]{1,0:T(8,128)S(1)} collective-permute-done((f32[256,512]{1,0:T(8,128)}, f32[256,512]{1,0:T(8,128)S(1)}, u32[]{:S(2)}, u32[]{:S(2)}) %collective-permute-start.3) | collective-permute-done | bytes 524320 | tf_op jit(solution)/shard_map/ppermute | solution.py:88
  32.5 1.3 collective-permute-start.5
  35.8 10.8 %collective-permute-done.5 = f32[256,512]{1,0:T(8,128)S(1)} collective-permute-done((f32[256,512]{1,0:T(8,128)S(1)}, f32[256,512]{1,0:T(8,128)S(1)}, u32[]{:S(2)}, u32[]{:S(2)}) %collective-permute-start.5) | collective-permute-done | bytes 524320 | tf_op jit(solution)/shard_map/ppermute | solution.py:88
  49.7 2.2 %collective-permute-done.6 = f32[512,256]{0,1:T(8,128)} collective-permute-done((f32[512,256]{0,1:T(8,128)}, f32[512,256]{0,1:T(8,128)}, u32[]{:S(2)}, u32[]{:S(2)}) %collective-permute-start.6) | collective-permute-done | bytes 524320 | tf_op jit(solution)/shard_map/ppermute | solution.py:15
  52.0 1.5 select_add_fusion
  56.0 7.5 %collective-permute-done.7 = f32[512,128]{0,1:T(8,128)S(1)} collective-permute-done((f32[512,128]{0,1:T(8,128)}, f32[512,128]{0,1:T(8,128)S(1)}, u32[]{:S(2)}, u32[]{:S(2)}) %collective-permute-start.7) | collective-permute-done | bytes 262176 | tf_op jit(solution)/shard_map/ppermute | solution.py:15
  65.8 3.9 %collective-permute-done.8 = f32[512,64]{0,1:T(8,128)S(1)} collective-permute-done((f32[512,64]{0,1:T(8,128)S(1)}, f32[512,64]{0,1:T(8,128)S(1)}, u32[]{:S(2)}, u32[]{:S(2)}) %collective-permute-start.8) | collective-permute-done | bytes 131104 | tf_op jit(solution)/shard_map/ppermute | solution.py:15
  70.3 1.4 collective-permute-start.9
  72.8 1.5 collective-permute-done.9
  80.6 1.5 collective-permute-start.14
  82.1 23.6 %collective-permute-done.14 = f32[512,64]{0,1:T(8,128)S(1)} collective-permute-done((f32[512,64]{0,1:T(8,128)S(1)}, f32[512,64]{0,1:T(8,128)S(1)}, u32[]{:S(2)}, u32[]{:S(2)}) %collective-permute-start.14) | collective-permute-done | bytes 131104 | tf_op jit(solution)/shard_map/ppermute | solution.py:127
  107.2 3.9 %collective-permute-done.15 = f32[512,64]{0,1:T(8,128)S(1)} collective-permute-done((f32[512,64]{0,1:T(8,128)S(1)}, f32[512,64]{0,1:T(8,128)S(1)}, u32[]{:S(2)}, u32[]{:S(2)}) %collective-permute-start.15) | collective-permute-done | bytes 131104 | tf_op jit(solution)/shard_map/ppermute | solution.py:15
  112.2 5.4 %collective-permute-done.16 = f32[512,128]{0,1:T(8,128)S(1)} collective-permute-done((f32[512,128]{0,1:T(8,128)S(1)}, f32[512,128]{0,1:T(8,128)S(1)}, u32[]{:S(2)}, u32[]{:S(2)}) %collective-permute-start.16) | collective-permute-done | bytes 262176 | tf_op jit(solution)/shard_map/ppermute | solution.py:15
  117.7 1.9 %collective-permute-done.17 = f32[512,256]{0,1:T(8,128)S(1)} collective-permute-done((f32[512,256]{0,1:T(8,128)S(1)}, f32[512,256]{0,1:T(8,128)S(1)}, u32[]{:S(2)}, u32[]{:S(2)}) %collective-permute-start.17) | collective-permute-done | bytes 524320 | tf_op jit(solution)/shard_map/ppermute | solution.py:15
  119.6 1.9 %fusion.2 = f32[1024,512]{1,0:T(8,128)S(1)} fusion(f32[512,1024]{0,1:T(8,128)S(1)} %bitcast_multiply_fusion, f32[512,256]{0,1:T(8,128)S(1)} %maximum_select_fusion.2, f32[512,256]{0,1:T(8,128)S(1)} %collective-permute-done.17, pred[]{:T(512)S(6)} %eq.19), kind=kOutput, calls=%fused_computation.17 | convolution fusion | flops 1611399168 | bytes 5242881 | tf_op jit(solution)/shard_map/dot_general | solution.py:31
  121.6 1.5 collective-permute-start.18
  123.8 10.8 %collective-permute-done.18 = f32[256,512]{1,0:T(8,128)S(1)} collective-permute-done((f32[256,512]{1,0:T(8,128)S(1)}, f32[256,512]{1,0:T(8,128)S(1)}, u32[]{:S(2)}, u32[]{:S(2)}) %collective-permute-start.18) | collective-permute-done | bytes 524320 | tf_op jit(solution)/shard_map/ppermute | solution.py:108
  134.8 4.4 %collective-permute-start.19 = (f32[256,512]{1,0:T(8,128)S(1)}, f32[256,512]{1,0:T(8,128)S(1)}, u32[]{:S(2)}, u32[]{:S(2)}) collective-permute-start(f32[256,512]{1,0:T(8,128)S(1)} %get-tuple-element.8), channel_id=1, source_target_pairs={{0,1},{1,2},{4,5},{5,6},{8,9},{9,10},{12,13},{13,14},{16,17},{17,1... | collective-permute-start | bytes 1572872 | tf_op jit(solution)/shard_map/ppermute | solution.py:108
  140.0 10.0 %collective-permute-done.19 = f32[256,512]{1,0:T(8,128)S(1)} collective-permute-done((f32[256,512]{1,0:T(8,128)S(1)}, f32[256,512]{1,0:T(8,128)S(1)}, u32[]{:S(2)}, u32[]{:S(2)}) %collective-permute-start.19) | collective-permute-done | bytes 524320 | tf_op jit(solution)/shard_map/ppermute | solution.py:108
  150.2 6.3 %collective-permute-start.20 = (f32[256,512]{1,0:T(8,128)S(1)}, f32[256,512]{1,0:T(8,128)S(1)}, u32[]{:S(2)}, u32[]{:S(2)}) collective-permute-start(f32[256,512]{1,0:T(8,128)S(1)} %get-tuple-element.6), channel_id=1, source_target_pairs={{0,1},{1,2},{2,3},{4,5},{5,6},{6,7},{8,9},{9,10},{10,11},{12,13},{... | collective-permute-start | bytes 1572872 | tf_op jit(solution)/shard_map/ppermute | solution.py:108
  156.5 1.3 collective-permute-start.23
  157.8 8.5 %collective-permute-done.20 = f32[256,512]{1,0:T(8,128)S(1)} collective-permute-done((f32[256,512]{1,0:T(8,128)S(1)}, f32[256,512]{1,0:T(8,128)S(1)}, u32[]{:S(2)}, u32[]{:S(2)}) %collective-permute-start.20) | collective-permute-done | bytes 524320 | tf_op jit(solution)/shard_map/ppermute | solution.py:108
  166.3 4.1 %collective-permute-done.23 = f32[256,512]{1,0:T(8,128)S(1)} collective-permute-done((f32[256,512]{1,0:T(8,128)S(1)}, f32[256,512]{1,0:T(8,128)S(1)}, u32[]{:S(2)}, u32[]{:S(2)}) %collective-permute-start.23) | collective-permute-done | bytes 524320 | tf_op jit(solution)/shard_map/ppermute | solution.py:109
  (63 shorter events, 24.2 us)
Async XLA Ops:
  0.0 69.7 %copy-start = (f32[512,512]{1,0:T(8,128)S(1)}, f32[512,512]{1,0:T(8,128)}, u32[]{:S(2)}) copy-start(f32[512,512]{1,0:T(8,128)} %param.8) | copy-start | bytes 3145732
  0.0 17.3 %collective-permute-start.1 = (f32[256,512]{1,0:T(8,128)}, f32[256,512]{1,0:T(8,128)}, u32[]{:S(2)}, u32[]{:S(2)}) collective-permute-start(f32[256,512]{1,0:T(8,128)} %param.6), channel_id=1, source_target_pairs={{1,0},{2,1},{3,2},{5,4},{6,5},{7,6},{9,8},{10,9},{11,10},{13,12},{... | collective-permute-start | bytes 1572872 | tf_op jit(solution)/shard_map/ppermute | solution.py:88
  1.4 17.2 %collective-permute-start = (f32[256,512]{1,0:T(8,128)}, f32[256,512]{1,0:T(8,128)}, u32[]{:S(2)}, u32[]{:S(2)}) collective-permute-start(f32[256,512]{1,0:T(8,128)} %param.6), channel_id=1, source_target_pairs={{0,1},{1,2},{2,3},{4,5},{5,6},{6,7},{8,9},{9,10},{10,11},{12,13},{... | collective-permute-start | bytes 1572872 | tf_op jit(solution)/shard_map/ppermute | solution.py:87
  7.8 2.9 %copy-start.4 = (s32[8,16]{1,0:T(8,128)S(1)}, s32[8,16]{1,0:T(8,128)}, u32[]{:S(2)}) copy-start(s32[8,16]{1,0:T(8,128)} %param.7) | copy-start | bytes 1540
  17.3 15.2 %collective-permute-start.3 = (f32[256,512]{1,0:T(8,128)}, f32[256,512]{1,0:T(8,128)S(1)}, u32[]{:S(2)}, u32[]{:S(2)}) collective-permute-start(f32[256,512]{1,0:T(8,128)} %collective-permute-done.1), channel_id=1, source_target_pairs={{1,0},{2,1},{5,4},{6,5},{9,8},{10,9},{13,12},{14,13},{17,16},{18,1... | collective-permute-start | bytes 1572872 | tf_op jit(solution)/shard_map/ppermute | solution.py:88
  18.6 15.2 %collective-permute-start.2 = (f32[256,512]{1,0:T(8,128)}, f32[256,512]{1,0:T(8,128)S(1)}, u32[]{:S(2)}, u32[]{:S(2)}) collective-permute-start(f32[256,512]{1,0:T(8,128)} %collective-permute-done), channel_id=1, source_target_pairs={{1,2},{2,3},{5,6},{6,7},{9,10},{10,11},{13,14},{14,15},{17,18},{18... | collective-permute-start | bytes 1572872 | tf_op jit(solution)/shard_map/ppermute | solution.py:87
  32.5 14.1 %collective-permute-start.5 = (f32[256,512]{1,0:T(8,128)S(1)}, f32[256,512]{1,0:T(8,128)S(1)}, u32[]{:S(2)}, u32[]{:S(2)}) collective-permute-start(f32[256,512]{1,0:T(8,128)S(1)} %collective-permute-done.3), channel_id=1, source_target_pairs={{1,0},{5,4},{9,8},{13,12},{17,16},{21,20},{25,24},{29,28}} | collective-permute-start | bytes 1572872 | tf_op jit(solution)/shard_map/ppermute | solution.py:88
  33.8 13.4 %collective-permute-start.4 = (f32[256,512]{1,0:T(8,128)S(1)}, f32[256,512]{1,0:T(8,128)S(1)}, u32[]{:S(2)}, u32[]{:S(2)}) collective-permute-start(f32[256,512]{1,0:T(8,128)S(1)} %collective-permute-done.2), channel_id=1, source_target_pairs={{2,3},{6,7},{10,11},{14,15},{18,19},{22,23},{26,27},{30,31}} | collective-permute-start | bytes 1572872 | tf_op jit(solution)/shard_map/ppermute | solution.py:87
  47.8 1.0 copy-start.1
  49.7 2.3 %collective-permute-start.6 = (f32[512,256]{0,1:T(8,128)}, f32[512,256]{0,1:T(8,128)}, u32[]{:S(2)}, u32[]{:S(2)}) collective-permute-start(f32[512,256]{0,1:T(8,128)} %slice_select_fusion), channel_id=1, source_target_pairs={{0,4},{4,0},{8,12},{12,8},{16,20},{20,16},{24,28},{28,24},{1,5},{5... | collective-permute-start | bytes 1572872 | tf_op jit(solution)/shard_map/ppermute | solution.py:15
  53.5 0.8 copy-start.2
  55.0 8.6 %collective-permute-start.7 = (f32[512,128]{0,1:T(8,128)}, f32[512,128]{0,1:T(8,128)S(1)}, u32[]{:S(2)}, u32[]{:S(2)}) collective-permute-start(f32[512,128]{0,1:T(8,128)} %slice_select_fusion.1), channel_id=1, source_target_pairs={{0,8},{4,12},{8,0},{12,4},{16,24},{20,28},{24,16},{28,20},{1,9},{5... | collective-permute-start | bytes 786440 | tf_op jit(solution)/shard_map/ppermute | solution.py:15
  56.0 15.8 %copy-start.3 = (f32[512,512]{1,0:T(8,128)S(1)}, f32[512,512]{1,0:T(8,128)}, u32[]{:S(2)}) copy-start(f32[512,512]{1,0:T(8,128)} %param.9) | copy-start | bytes 3145732
  64.7 5.0 %collective-permute-start.8 = (f32[512,64]{0,1:T(8,128)S(1)}, f32[512,64]{0,1:T(8,128)S(1)}, u32[]{:S(2)}, u32[]{:S(2)}) collective-permute-start(f32[512,64]{0,1:T(8,128)S(1)} %slice_select_fusion.2), channel_id=1, source_target_pairs={{0,16},{4,20},{8,24},{12,28},{16,0},{20,4},{24,8},{28,12},{1,17},{... | collective-permute-start | bytes 393224 | tf_op jit(solution)/shard_map/ppermute | solution.py:15
  70.3 4.0 %collective-permute-start.9 = (f32[512,64]{0,1:T(8,128)S(1)}, f32[512,64]{0,1:T(8,128)S(1)}, u32[]{:S(2)}, u32[]{:S(2)}) collective-permute-start(f32[512,64]{0,1:T(8,128)S(1)} %convolution_bitcast_fusion.2), channel_id=1, source_target_pairs={{0,1},{4,5},{8,9},{12,13},{16,17},{20,21},{24,25},{28,29}} | collective-permute-start | bytes 393224 | tf_op jit(solution)/shard_map/ppermute | solution.py:119
  74.9 0.7 collective-permute-start.10
  76.2 0.7 collective-permute-start.11
  78.4 0.7 collective-permute-start.12
  79.5 0.7 collective-permute-start.13
  80.6 25.0 %collective-permute-start.14 = (f32[512,64]{0,1:T(8,128)S(1)}, f32[512,64]{0,1:T(8,128)S(1)}, u32[]{:S(2)}, u32[]{:S(2)}) collective-permute-start(f32[512,64]{0,1:T(8,128)S(1)} %convolution_add_fusion.4), channel_id=1, source_target_pairs={{1,0},{5,4},{9,8},{13,12},{17,16},{21,20},{25,24},{29,28}} | collective-permute-start | bytes 393224 | tf_op jit(solution)/shard_map/ppermute | solution.py:127
  106.1 5.0 %collective-permute-start.15 = (f32[512,64]{0,1:T(8,128)S(1)}, f32[512,64]{0,1:T(8,128)S(1)}, u32[]{:S(2)}, u32[]{:S(2)}) collective-permute-start(f32[512,64]{0,1:T(8,128)S(1)} %convolution_bitcast_fusion), channel_id=1, source_target_pairs={{0,16},{4,20},{8,24},{12,28},{16,0},{20,4},{24,8},{28,12},{1,17},{... | collective-permute-start | bytes 393224 | tf_op jit(solution)/shard_map/ppermute | solution.py:15
  111.2 6.4 %collective-permute-start.16 = (f32[512,128]{0,1:T(8,128)S(1)}, f32[512,128]{0,1:T(8,128)S(1)}, u32[]{:S(2)}, u32[]{:S(2)}) collective-permute-start(f32[512,128]{0,1:T(8,128)S(1)} %maximum_select_fusion.3), channel_id=1, source_target_pairs={{0,8},{4,12},{8,0},{12,4},{16,24},{20,28},{24,16},{28,20},{1,9},{5... | collective-permute-start | bytes 786440 | tf_op jit(solution)/shard_map/ppermute | solution.py:15
  117.7 2.0 %collective-permute-start.17 = (f32[512,256]{0,1:T(8,128)S(1)}, f32[512,256]{0,1:T(8,128)S(1)}, u32[]{:S(2)}, u32[]{:S(2)}) collective-permute-start(f32[512,256]{0,1:T(8,128)S(1)} %maximum_select_fusion.2), channel_id=1, source_target_pairs={{0,4},{4,0},{8,12},{12,8},{16,20},{20,16},{24,28},{28,24},{1,5},{5... | collective-permute-start | bytes 1572872 | tf_op jit(solution)/shard_map/ppermute | solution.py:15
  121.6 13.0 %collective-permute-start.18 = (f32[256,512]{1,0:T(8,128)S(1)}, f32[256,512]{1,0:T(8,128)S(1)}, u32[]{:S(2)}, u32[]{:S(2)}) collective-permute-start(f32[256,512]{1,0:T(8,128)S(1)} %get-tuple-element.10), channel_id=1, source_target_pairs={{0,1},{4,5},{8,9},{12,13},{16,17},{20,21},{24,25},{28,29}} | collective-permute-start | bytes 1572872 | tf_op jit(solution)/shard_map/ppermute | solution.py:108
  123.1 11.5 %collective-permute-start.21 = (f32[256,512]{1,0:T(8,128)S(1)}, f32[256,512]{1,0:T(8,128)S(1)}, u32[]{:S(2)}, u32[]{:S(2)}) collective-permute-start(f32[256,512]{1,0:T(8,128)S(1)} %get-tuple-element.9), channel_id=1, source_target_pairs={{3,2},{7,6},{11,10},{15,14},{19,18},{23,22},{27,26},{31,30}} | collective-permute-start | bytes 1572872 | tf_op jit(solution)/shard_map/ppermute | solution.py:109
  134.8 15.1 %collective-permute-start.19 = (f32[256,512]{1,0:T(8,128)S(1)}, f32[256,512]{1,0:T(8,128)S(1)}, u32[]{:S(2)}, u32[]{:S(2)}) collective-permute-start(f32[256,512]{1,0:T(8,128)S(1)} %get-tuple-element.8), channel_id=1, source_target_pairs={{0,1},{1,2},{4,5},{5,6},{8,9},{9,10},{12,13},{13,14},{16,17},{17,1... | collective-permute-start | bytes 1572872 | tf_op jit(solution)/shard_map/ppermute | solution.py:108
  139.3 10.7 %collective-permute-start.22 = (f32[256,512]{1,0:T(8,128)S(1)}, f32[256,512]{1,0:T(8,128)S(1)}, u32[]{:S(2)}, u32[]{:S(2)}) collective-permute-start(f32[256,512]{1,0:T(8,128)S(1)} %get-tuple-element.7), channel_id=1, source_target_pairs={{2,1},{3,2},{6,5},{7,6},{10,9},{11,10},{14,13},{15,14},{18,17},{19... | collective-permute-start | bytes 1572872 | tf_op jit(solution)/shard_map/ppermute | solution.py:109
  150.2 16.1 %collective-permute-start.20 = (f32[256,512]{1,0:T(8,128)S(1)}, f32[256,512]{1,0:T(8,128)S(1)}, u32[]{:S(2)}, u32[]{:S(2)}) collective-permute-start(f32[256,512]{1,0:T(8,128)S(1)} %get-tuple-element.6), channel_id=1, source_target_pairs={{0,1},{1,2},{2,3},{4,5},{5,6},{6,7},{8,9},{9,10},{10,11},{12,13},{... | collective-permute-start | bytes 1572872 | tf_op jit(solution)/shard_map/ppermute | solution.py:108
  156.5 13.9 %collective-permute-start.23 = (f32[256,512]{1,0:T(8,128)S(1)}, f32[256,512]{1,0:T(8,128)S(1)}, u32[]{:S(2)}, u32[]{:S(2)}) collective-permute-start(f32[256,512]{1,0:T(8,128)S(1)} %get-tuple-element.5), channel_id=1, source_target_pairs={{1,0},{2,1},{3,2},{5,4},{6,5},{7,6},{9,8},{10,9},{11,10},{13,12},{... | collective-permute-start | bytes 1572872 | tf_op jit(solution)/shard_map/ppermute | solution.py:109

commit v19 on v17

--- a/solution.py
+++ b/solution.py
@@ -8,6 +8,14 @@
     count = lax.axis_size(axis)
     pairs = [(i, i + by) for i in range(count) if 0 <= i + by < count]
     return lax.ppermute(array, axis, pairs)
+
+
+def pairwise(array, axis, pairs):
+    received = [lax.ppermute(array, axis, [pair]) for pair in pairs]
+    total = received[0]
+    for more in received[1:]:
+        total = total + more
+    return total
 
 
 def swap(array, axis, bit):
@@ -84,8 +92,8 @@
     for step in range(count - 1):
         rightward = [(i, i + 1) for i in range(step, count - 1)]
         leftward = [(i + 1, i) for i in range(count - 1 - step)]
-        from_left = lax.ppermute(from_left, "aux", rightward)
-        from_right = lax.ppermute(from_right, "aux", leftward)
+        from_left = pairwise(from_left, "aux", rightward)
+        from_right = pairwise(from_right, "aux", leftward)
         gamma = gamma + product(columns(index - 1 - step), from_left)
         gamma = gamma + product(columns(index + 1 + step), from_right)
     return gamma
@@ -105,8 +113,8 @@
     for step in range(count - 1):
         rightward = [(i, i + 1) for i in range(min(step + 1, count - 1))]
         leftward = [(i + 1, i) for i in range(count - 2 - step, count - 1)]
-        to_right = lax.ppermute(to_right + block(index + count - 1 - step), "aux", rightward)
-        to_left = lax.ppermute(to_left + block(index - (count - 1) + step), "aux", leftward)
+        to_right = pairwise(to_right + block(index + count - 1 - step), "aux", rightward)
+        to_left = pairwise(to_left + block(index - (count - 1) + step), "aux", leftward)
     return to_right + to_left + block(index)
 
 

time: 154 us -> 179 us (1.16)
  the two profiles are of different devices: /device:TPU:0 before, /device:TPU:16 now
where the time goes in v19:
time: 179 us; the launch traced here: 178 us
  starting transfers between devices  95.4 us (53%)
  waiting for transfers between devices  53.8 us (30%)
  matrix products  16.1 us (9%)
  other arithmetic  6.33 us (4%)
  local copies, waits for them, and re-layouts  4.79 us (3%)
    ppermute x36, starting transfers between devices, pairwise(): received = [lax.ppermute(array, axis, [pair]) for pair in pairs]  70.9 us
    ppermute x36, waiting for transfers between devices, pairwise(): received = [lax.ppermute(array, axis, [pair]) for pair in pairs]  27.7 us
    ppermute x12, waiting for transfers between devices, swap(): return lax.ppermute(array, axis, [(i, i ^ bit) for i in range(count)])  14.7 us
    dot_general x26, matrix products, product(): jnp.dot(left, right, precision=lax.Precision.HIGH, preferred_element_type...  14 us
    ppermute x12, starting transfers between devices, swap(): return lax.ppermute(array, axis, [(i, i ^ bit) for i in range(count)])  11.4 us
    ppermute x6, waiting for transfers between devices, solve(): incoming = incoming + lax.ppermute(value, 'aux', [(turn, turn + 1)])  7.49 us
    ppermute x6, starting transfers between devices, solve(): incoming = incoming + lax.ppermute(value, 'aux', [(turn, turn + 1)])  6.68 us
    ppermute x6, starting transfers between devices, solve(): arriving = arriving + lax.ppermute(value, 'aux', [(sender, sender - 1)])  6.5 us
  transfers between devices with their start and end apart: 60, of which 22 were waited for; matrix products, arithmetic and copies ran while one was open for 13% of the time, Pallas kernels for 0%

profile of v19, /device:TPU:16, one launch (start us, length us, event | category | flops | bytes accessed | tf_op | source)
XLA Modules:
  0.0 177.6 jit_solution(14129291898784223907)
XLA Ops:
  0.0 1.6 collective-permute-start
  2.9 4.4 %collective-permute-start.2 = (f32[256,512]{1,0:T(8,128)}, f32[256,512]{1,0:T(8,128)}, u32[]{:S(2)}, u32[]{:S(2)}) collective-permute-start(f32[256,512]{1,0:T(8,128)} %param.6), channel_id=1, source_target_pairs={{2,3},{6,7},{10,11},{14,15},{18,19},{22,23},{26,27},{30,31}} | collective-permute-start | bytes 1572872 | tf_op jit(solution)/shard_map/ppermute | solution.py:14
  8.8 4.8 %collective-permute-start.4 = (f32[256,512]{1,0:T(8,128)}, f32[256,512]{1,0:T(8,128)}, u32[]{:S(2)}, u32[]{:S(2)}) collective-permute-start(f32[256,512]{1,0:T(8,128)} %param.6), channel_id=1, source_target_pairs={{2,1},{6,5},{10,9},{14,13},{18,17},{22,21},{26,25},{30,29}} | collective-permute-start | bytes 1572872 | tf_op jit(solution)/shard_map/ppermute | solution.py:14
  15.0 2.9 %copy.8 = f32[512,1024]{0,1:T(8,128)} copy(f32[512,1024]{1,0:T(8,128)} %param.5) | data formatting | bytes 4194304 | tf_op args[0]
  18.1 1.8 %bitcast_multiply_fusion = f32[512,1024]{0,1:T(8,128)S(1)} fusion(f32[512,1024]{0,1:T(8,128)} %copy.8, f32[512,16]{0,1:T(8,128)S(1)} %reshape.6), kind=kLoop, calls=%fused_computation | loop fusion | flops 524288 | bytes 4227072 | tf_op jit(solution)/shard_map/mul | solution.py:31
  20.0 1.6 add_add_fusion.1
  22.9 4.7 %collective-permute-start.7 = (f32[256,512]{1,0:T(8,128)S(1)}, f32[256,512]{1,0:T(8,128)S(1)}, u32[]{:S(2)}, u32[]{:S(2)}) collective-permute-start(f32[256,512]{1,0:T(8,128)S(1)} %add_add_fusion.1), channel_id=1, source_target_pairs={{2,3},{6,7},{10,11},{14,15},{18,19},{22,23},{26,27},{30,31}} | collective-permute-start | bytes 1572872 | tf_op jit(solution)/shard_map/ppermute | solution.py:14
  28.6 1.5 add_add_fusion
  33.5 3.4 %collective-permute-done.6 = f32[256,512]{1,0:T(8,128)S(1)} collective-permute-done((f32[256,512]{1,0:T(8,128)S(1)}, f32[256,512]{1,0:T(8,128)S(1)}, u32[]{:S(2)}, u32[]{:S(2)}) %collective-permute-start.6) | collective-permute-done | bytes 524320 | tf_op jit(solution)/shard_map/ppermute | solution.py:14
  37.7 4.4 %collective-permute-start.10 = (f32[256,512]{1,0:T(8,128)S(1)}, f32[256,512]{1,0:T(8,128)S(1)}, u32[]{:S(2)}, u32[]{:S(2)}) collective-permute-start(f32[256,512]{1,0:T(8,128)S(1)} %add.297), channel_id=1, source_target_pairs={{2,3},{6,7},{10,11},{14,15},{18,19},{22,23},{26,27},{30,31}} | collective-permute-start | bytes 1572872 | tf_op jit(solution)/shard_map/ppermute | solution.py:14
  44.2 7.0 %collective-permute-done.10 = f32[256,512]{1,0:T(8,128)S(1)} collective-permute-done((f32[256,512]{1,0:T(8,128)S(1)}, f32[256,512]{1,0:T(8,128)S(1)}, u32[]{:S(2)}, u32[]{:S(2)}) %collective-permute-start.10) | collective-permute-done | bytes 524320 | tf_op jit(solution)/shard_map/ppermute | solution.py:14
  55.7 1.6 collective-permute-start.13
  57.9 4.3 %collective-permute-done.13 = f32[512,64]{0,1:T(8,128)S(1)} collective-permute-done((f32[512,64]{0,1:T(8,128)S(1)}, f32[512,64]{0,1:T(8,128)S(1)}, u32[]{:S(2)}, u32[]{:S(2)}) %collective-permute-start.13) | collective-permute-done | bytes 131104 | tf_op jit(solution)/shard_map/ppermute | solution.py:23
  62.2 1.6 collective-permute-start.14
  64.0 1.6 collective-permute-start.38
  65.6 1.6 collective-permute-done.14
  73.4 7.5 %collective-permute-done.16 = f32[512,32]{0,1:T(8,128)S(1)} collective-permute-done((f32[512,32]{0,1:T(8,128)S(1)}, f32[512,32]{0,1:T(8,128)S(1)}, u32[]{:S(2)}, u32[]{:S(2)}) %collective-permute-start.16) | collective-permute-done | bytes 65568 | tf_op jit(solution)/shard_map/ppermute | solution.py:127
  90.2 2.2 %collective-permute-done.18 = f32[512,32]{0,1:T(8,128)S(1)} collective-permute-done((f32[512,32]{0,1:T(8,128)S(1)}, f32[512,32]{0,1:T(8,128)S(1)}, u32[]{:S(2)}, u32[]{:S(2)}) %collective-permute-start.18) | collective-permute-done | bytes 65568 | tf_op jit(solution)/shard_map/ppermute | solution.py:135
  99.1 1.6 collective-permute-start.21
  101.8 1.7 collective-permute-done.21
  103.4 1.6 collective-permute-start.22
  105.4 1.6 collective-permute-start.45
  110.3 4.4 %collective-permute-done.46 = f32[512,64]{0,1:T(8,128)S(1)} collective-permute-done((f32[512,64]{0,1:T(8,128)S(1)}, f32[512,64]{0,1:T(8,128)S(1)}, u32[]{:S(2)}, u32[]{:S(2)}) %collective-permute-start.46) | collective-permute-done | bytes 131104 | tf_op jit(solution)/shard_map/ppermute | solution.py:23
  121.1 6.6 %collective-permute-done.30 = f32[256,256]{0,1:T(8,128)S(1)} collective-permute-done((f32[256,256]{0,1:T(8,128)S(1)}, f32[256,256]{0,1:T(8,128)S(1)}, u32[]{:S(2)}, u32[]{:S(2)}) %collective-permute-start.30) | collective-permute-done | bytes 262176 | tf_op jit(solution)/shard_map/ppermute | solution.py:14
  129.7 7.7 %collective-permute-start.31 = (f32[256,256]{0,1:T(8,128)S(1)}, f32[256,256]{0,1:T(8,128)S(1)}, u32[]{:S(2)}, u32[]{:S(2)}) collective-permute-start(f32[256,256]{0,1:T(8,128)S(1)} %get-tuple-element.8), channel_id=1, source_target_pairs={{2,1},{6,5},{10,9},{14,13},{18,17},{22,21},{26,25},{30,29}} | collective-permute-start | bytes 786440 | tf_op jit(solution)/shard_map/ppermute | solution.py:14
  141.3 6.0 %collective-permute-start.55 = (f32[256,256]{0,1:T(8,128)S(1)}, f32[256,256]{0,1:T(8,128)S(1)}, u32[]{:S(2)}, u32[]{:S(2)}) collective-permute-start(f32[256,256]{0,1:T(8,128)S(1)} %get-tuple-element.18), channel_id=1, source_target_pairs={{2,1},{6,5},{10,9},{14,13},{18,17},{22,21},{26,25},{30,29}} | collective-permute-start | bytes 786440 | tf_op jit(solution)/shard_map/ppermute | solution.py:14
  151.1 3.6 %collective-permute-start.29 = (f32[256,256]{0,1:T(8,128)S(1)}, f32[256,256]{0,1:T(8,128)S(1)}, u32[]{:S(2)}, u32[]{:S(2)}) collective-permute-start(f32[256,256]{0,1:T(8,128)S(1)} %get-tuple-element.5), channel_id=1, source_target_pairs={{2,3},{6,7},{10,11},{14,15},{18,19},{22,23},{26,27},{30,31}} | collective-permute-start | bytes 786440 | tf_op jit(solution)/shard_map/ppermute | solution.py:14
  156.5 1.6 collective-permute-start.34
  161.5 4.0 %collective-permute-start.53 = (f32[256,256]{0,1:T(8,128)S(1)}, f32[256,256]{0,1:T(8,128)S(1)}, u32[]{:S(2)}, u32[]{:S(2)}) collective-permute-start(f32[256,256]{0,1:T(8,128)S(1)} %get-tuple-element.15), channel_id=1, source_target_pairs={{2,3},{6,7},{10,11},{14,15},{18,19},{22,23},{26,27},{30,31}} | collective-permute-start | bytes 786440 | tf_op jit(solution)/shard_map/ppermute | solution.py:14
  166.5 1.6 collective-permute-start.58
  169.6 2.4 %collective-permute-done.58 = f32[256,256]{0,1:T(8,128)S(1)} collective-permute-done((f32[256,256]{0,1:T(8,128)S(1)}, f32[256,256]{0,1:T(8,128)S(1)}, u32[]{:S(2)}, u32[]{:S(2)}) %collective-permute-start.58) | collective-permute-done | bytes 262176 | tf_op jit(solution)/shard_map/ppermute | solution.py:14
  172.0 4.4 %collective-permute-done.59 = f32[256,256]{0,1:T(8,128)S(1)} collective-permute-done((f32[256,256]{0,1:T(8,128)S(1)}, f32[256,256]{0,1:T(8,128)S(1)}, u32[]{:S(2)}, u32[]{:S(2)}) %collective-permute-start.59) | collective-permute-done | bytes 262176 | tf_op jit(solution)/shard_map/ppermute | solution.py:14
  (160 shorter events, 69.4 us)
Async XLA Ops:
  0.0 13.6 %collective-permute-start = (f32[256,512]{1,0:T(8,128)}, f32[256,512]{1,0:T(8,128)}, u32[]{:S(2)}, u32[]{:S(2)}) collective-permute-start(f32[256,512]{1,0:T(8,128)} %param.6), channel_id=1, source_target_pairs={{0,1},{4,5},{8,9},{12,13},{16,17},{20,21},{24,25},{28,29}} | collective-permute-start | bytes 1572872 | tf_op jit(solution)/shard_map/ppermute | solution.py:14
  1.6 18.4 %collective-permute-start.1 = (f32[256,512]{1,0:T(8,128)}, f32[256,512]{1,0:T(8,128)}, u32[]{:S(2)}, u32[]{:S(2)}) collective-permute-start(f32[256,512]{1,0:T(8,128)} %param.6), channel_id=1, source_target_pairs={{1,2},{5,6},{9,10},{13,14},{17,18},{21,22},{25,26},{29,30}} | collective-permute-start | bytes 1572872 | tf_op jit(solution)/shard_map/ppermute | solution.py:14
  2.9 17.1 %collective-permute-start.2 = (f32[256,512]{1,0:T(8,128)}, f32[256,512]{1,0:T(8,128)}, u32[]{:S(2)}, u32[]{:S(2)}) collective-permute-start(f32[256,512]{1,0:T(8,128)} %param.6), channel_id=1, source_target_pairs={{2,3},{6,7},{10,11},{14,15},{18,19},{22,23},{26,27},{30,31}} | collective-permute-start | bytes 1572872 | tf_op jit(solution)/shard_map/ppermute | solution.py:14
  7.3 20.2 %collective-permute-start.3 = (f32[256,512]{1,0:T(8,128)}, f32[256,512]{1,0:T(8,128)}, u32[]{:S(2)}, u32[]{:S(2)}) collective-permute-start(f32[256,512]{1,0:T(8,128)} %param.6), channel_id=1, source_target_pairs={{1,0},{5,4},{9,8},{13,12},{17,16},{21,20},{25,24},{29,28}} | collective-permute-start | bytes 1572872 | tf_op jit(solution)/shard_map/ppermute | solution.py:14
  8.8 18.8 %collective-permute-start.4 = (f32[256,512]{1,0:T(8,128)}, f32[256,512]{1,0:T(8,128)}, u32[]{:S(2)}, u32[]{:S(2)}) collective-permute-start(f32[256,512]{1,0:T(8,128)} %param.6), channel_id=1, source_target_pairs={{2,1},{6,5},{10,9},{14,13},{18,17},{22,21},{26,25},{30,29}} | collective-permute-start | bytes 1572872 | tf_op jit(solution)/shard_map/ppermute | solution.py:14
  13.6 15.0 %collective-permute-start.5 = (f32[256,512]{1,0:T(8,128)}, f32[256,512]{1,0:T(8,128)}, u32[]{:S(2)}, u32[]{:S(2)}) collective-permute-start(f32[256,512]{1,0:T(8,128)} %param.6), channel_id=1, source_target_pairs={{3,2},{7,6},{11,10},{15,14},{19,18},{23,22},{27,26},{31,30}} | collective-permute-start | bytes 1572872 | tf_op jit(solution)/shard_map/ppermute | solution.py:14
  21.6 15.2 %collective-permute-start.6 = (f32[256,512]{1,0:T(8,128)S(1)}, f32[256,512]{1,0:T(8,128)S(1)}, u32[]{:S(2)}, u32[]{:S(2)}) collective-permute-start(f32[256,512]{1,0:T(8,128)S(1)} %add_add_fusion.1), channel_id=1, source_target_pairs={{1,2},{5,6},{9,10},{13,14},{17,18},{21,22},{25,26},{29,30}} | collective-permute-start | bytes 1572872 | tf_op jit(solution)/shard_map/ppermute | solution.py:14
  22.9 14.7 %collective-permute-start.7 = (f32[256,512]{1,0:T(8,128)S(1)}, f32[256,512]{1,0:T(8,128)S(1)}, u32[]{:S(2)}, u32[]{:S(2)}) collective-permute-start(f32[256,512]{1,0:T(8,128)S(1)} %add_add_fusion.1), channel_id=1, source_target_pairs={{2,3},{6,7},{10,11},{14,15},{18,19},{22,23},{26,27},{30,31}} | collective-permute-start | bytes 1572872 | tf_op jit(solution)/shard_map/ppermute | solution.py:14
  30.2 11.9 %collective-permute-start.8 = (f32[256,512]{1,0:T(8,128)S(1)}, f32[256,512]{1,0:T(8,128)S(1)}, u32[]{:S(2)}, u32[]{:S(2)}) collective-permute-start(f32[256,512]{1,0:T(8,128)S(1)} %add_add_fusion), channel_id=1, source_target_pairs={{1,0},{5,4},{9,8},{13,12},{17,16},{21,20},{25,24},{29,28}} | collective-permute-start | bytes 1572872 | tf_op jit(solution)/shard_map/ppermute | solution.py:14
  30.9 11.3 %collective-permute-start.9 = (f32[256,512]{1,0:T(8,128)S(1)}, f32[256,512]{1,0:T(8,128)S(1)}, u32[]{:S(2)}, u32[]{:S(2)}) collective-permute-start(f32[256,512]{1,0:T(8,128)S(1)} %add_add_fusion), channel_id=1, source_target_pairs={{2,1},{6,5},{10,9},{14,13},{18,17},{22,21},{26,25},{30,29}} | collective-permute-start | bytes 1572872 | tf_op jit(solution)/shard_map/ppermute | solution.py:14
  37.7 13.5 %collective-permute-start.10 = (f32[256,512]{1,0:T(8,128)S(1)}, f32[256,512]{1,0:T(8,128)S(1)}, u32[]{:S(2)}, u32[]{:S(2)}) collective-permute-start(f32[256,512]{1,0:T(8,128)S(1)} %add.297), channel_id=1, source_target_pairs={{2,3},{6,7},{10,11},{14,15},{18,19},{22,23},{26,27},{30,31}} | collective-permute-start | bytes 1572872 | tf_op jit(solution)/shard_map/ppermute | solution.py:14
  42.2 9.6 %collective-permute-start.11 = (f32[256,512]{1,0:T(8,128)S(1)}, f32[256,512]{1,0:T(8,128)S(1)}, u32[]{:S(2)}, u32[]{:S(2)}) collective-permute-start(f32[256,512]{1,0:T(8,128)S(1)} %add.301), channel_id=1, source_target_pairs={{1,0},{5,4},{9,8},{13,12},{17,16},{21,20},{25,24},{29,28}} | collective-permute-start | bytes 1572872 | tf_op jit(solution)/shard_map/ppermute | solution.py:14
  70.3 10.6 %collective-permute-start.16 = (f32[512,32]{0,1:T(8,128)S(1)}, f32[512,32]{0,1:T(8,128)S(1)}, u32[]{:S(2)}, u32[]{:S(2)}) collective-permute-start(f32[512,32]{0,1:T(8,128)S(1)} %convolution_add_fusion.11), channel_id=1, source_target_pairs={{1,2},{5,6},{9,10},{13,14},{17,18},{21,22},{25,26},{29,30}} | collective-permute-start | bytes 196616 | tf_op jit(solution)/shard_map/ppermute | solution.py:127
  72.1 10.7 %collective-permute-start.40 = (f32[512,32]{0,1:T(8,128)S(1)}, f32[512,32]{0,1:T(8,128)S(1)}, u32[]{:S(2)}, u32[]{:S(2)}) collective-permute-start(f32[512,32]{0,1:T(8,128)S(1)} %convolution_add_fusion.6), channel_id=1, source_target_pairs={{1,2},{5,6},{9,10},{13,14},{17,18},{21,22},{25,26},{29,30}} | collective-permute-start | bytes 196616 | tf_op jit(solution)/shard_map/ppermute | solution.py:127
  116.7 11.0 %collective-permute-start.30 = (f32[256,256]{0,1:T(8,128)S(1)}, f32[256,256]{0,1:T(8,128)S(1)}, u32[]{:S(2)}, u32[]{:S(2)}) collective-permute-start(f32[256,256]{0,1:T(8,128)S(1)} %get-tuple-element.10), channel_id=1, source_target_pairs={{3,2},{7,6},{11,10},{15,14},{19,18},{23,22},{27,26},{31,30}} | collective-permute-start | bytes 786440 | tf_op jit(solution)/shard_map/ppermute | solution.py:14
  119.1 18.4 %collective-permute-start.48 = (f32[256,256]{0,1:T(8,128)S(1)}, f32[256,256]{0,1:T(8,128)S(1)}, u32[]{:S(2)}, u32[]{:S(2)}) collective-permute-start(f32[256,256]{0,1:T(8,128)S(1)} %get-tuple-element.19), channel_id=1, source_target_pairs={{0,1},{4,5},{8,9},{12,13},{16,17},{20,21},{24,25},{28,29}} | collective-permute-start | bytes 786440 | tf_op jit(solution)/shard_map/ppermute | solution.py:14
  119.8 19.0 %collective-permute-start.54 = (f32[256,256]{0,1:T(8,128)S(1)}, f32[256,256]{0,1:T(8,128)S(1)}, u32[]{:S(2)}, u32[]{:S(2)}) collective-permute-start(f32[256,256]{0,1:T(8,128)S(1)} %get-tuple-element.20), channel_id=1, source_target_pairs={{3,2},{7,6},{11,10},{15,14},{19,18},{23,22},{27,26},{31,30}} | collective-permute-start | bytes 786440 | tf_op jit(solution)/shard_map/ppermute | solution.py:14
  127.8 11.8 %collective-permute-start.25 = (f32[256,256]{0,1:T(8,128)S(1)}, f32[256,256]{0,1:T(8,128)S(1)}, u32[]{:S(2)}, u32[]{:S(2)}) collective-permute-start(f32[256,256]{0,1:T(8,128)S(1)} %get-tuple-element.7), channel_id=1, source_target_pairs={{0,1},{4,5},{8,9},{12,13},{16,17},{20,21},{24,25},{28,29}} | collective-permute-start | bytes 786440 | tf_op jit(solution)/shard_map/ppermute | solution.py:14
  128.4 12.8 %collective-permute-start.26 = (f32[256,256]{0,1:T(8,128)S(1)}, f32[256,256]{0,1:T(8,128)S(1)}, u32[]{:S(2)}, u32[]{:S(2)}) collective-permute-start(f32[256,256]{0,1:T(8,128)S(1)} %get-tuple-element.7), channel_id=1, source_target_pairs={{1,2},{5,6},{9,10},{13,14},{17,18},{21,22},{25,26},{29,30}} | collective-permute-start | bytes 786440 | tf_op jit(solution)/shard_map/ppermute | solution.py:14
  129.7 17.6 %collective-permute-start.31 = (f32[256,256]{0,1:T(8,128)S(1)}, f32[256,256]{0,1:T(8,128)S(1)}, u32[]{:S(2)}, u32[]{:S(2)}) collective-permute-start(f32[256,256]{0,1:T(8,128)S(1)} %get-tuple-element.8), channel_id=1, source_target_pairs={{2,1},{6,5},{10,9},{14,13},{18,17},{22,21},{26,25},{30,29}} | collective-permute-start | bytes 786440 | tf_op jit(solution)/shard_map/ppermute | solution.py:14
  137.5 11.1 %collective-permute-start.32 = (f32[256,256]{0,1:T(8,128)S(1)}, f32[256,256]{0,1:T(8,128)S(1)}, u32[]{:S(2)}, u32[]{:S(2)}) collective-permute-start(f32[256,256]{0,1:T(8,128)S(1)} %get-tuple-element.8), channel_id=1, source_target_pairs={{3,2},{7,6},{11,10},{15,14},{19,18},{23,22},{27,26},{31,30}} | collective-permute-start | bytes 786440 | tf_op jit(solution)/shard_map/ppermute | solution.py:14
  138.9 10.5 %collective-permute-start.49 = (f32[256,256]{0,1:T(8,128)S(1)}, f32[256,256]{0,1:T(8,128)S(1)}, u32[]{:S(2)}, u32[]{:S(2)}) collective-permute-start(f32[256,256]{0,1:T(8,128)S(1)} %get-tuple-element.17), channel_id=1, source_target_pairs={{0,1},{4,5},{8,9},{12,13},{16,17},{20,21},{24,25},{28,29}} | collective-permute-start | bytes 786440 | tf_op jit(solution)/shard_map/ppermute | solution.py:14
  139.6 11.5 %collective-permute-start.50 = (f32[256,256]{0,1:T(8,128)S(1)}, f32[256,256]{0,1:T(8,128)S(1)}, u32[]{:S(2)}, u32[]{:S(2)}) collective-permute-start(f32[256,256]{0,1:T(8,128)S(1)} %get-tuple-element.17), channel_id=1, source_target_pairs={{1,2},{5,6},{9,10},{13,14},{17,18},{21,22},{25,26},{29,30}} | collective-permute-start | bytes 786440 | tf_op jit(solution)/shard_map/ppermute | solution.py:14
  141.3 13.5 %collective-permute-start.55 = (f32[256,256]{0,1:T(8,128)S(1)}, f32[256,256]{0,1:T(8,128)S(1)}, u32[]{:S(2)}, u32[]{:S(2)}) collective-permute-start(f32[256,256]{0,1:T(8,128)S(1)} %get-tuple-element.18), channel_id=1, source_target_pairs={{2,1},{6,5},{10,9},{14,13},{18,17},{22,21},{26,25},{30,29}} | collective-permute-start | bytes 786440 | tf_op jit(solution)/shard_map/ppermute | solution.py:14
  147.3 9.1 %collective-permute-start.56 = (f32[256,256]{0,1:T(8,128)S(1)}, f32[256,256]{0,1:T(8,128)S(1)}, u32[]{:S(2)}, u32[]{:S(2)}) collective-permute-start(f32[256,256]{0,1:T(8,128)S(1)} %get-tuple-element.18), channel_id=1, source_target_pairs={{3,2},{7,6},{11,10},{15,14},{19,18},{23,22},{27,26},{31,30}} | collective-permute-start | bytes 786440 | tf_op jit(solution)/shard_map/ppermute | solution.py:14
  148.8 9.4 %collective-permute-start.27 = (f32[256,256]{0,1:T(8,128)S(1)}, f32[256,256]{0,1:T(8,128)S(1)}, u32[]{:S(2)}, u32[]{:S(2)}) collective-permute-start(f32[256,256]{0,1:T(8,128)S(1)} %get-tuple-element.5), channel_id=1, source_target_pairs={{0,1},{4,5},{8,9},{12,13},{16,17},{20,21},{24,25},{28,29}} | collective-permute-start | bytes 786440 | tf_op jit(solution)/shard_map/ppermute | solution.py:14
  149.5 10.0 %collective-permute-start.28 = (f32[256,256]{0,1:T(8,128)S(1)}, f32[256,256]{0,1:T(8,128)S(1)}, u32[]{:S(2)}, u32[]{:S(2)}) collective-permute-start(f32[256,256]{0,1:T(8,128)S(1)} %get-tuple-element.5), channel_id=1, source_target_pairs={{1,2},{5,6},{9,10},{13,14},{17,18},{21,22},{25,26},{29,30}} | collective-permute-start | bytes 786440 | tf_op jit(solution)/shard_map/ppermute | solution.py:14
  151.1 9.1 %collective-permute-start.29 = (f32[256,256]{0,1:T(8,128)S(1)}, f32[256,256]{0,1:T(8,128)S(1)}, u32[]{:S(2)}, u32[]{:S(2)}) collective-permute-start(f32[256,256]{0,1:T(8,128)S(1)} %get-tuple-element.5), channel_id=1, source_target_pairs={{2,3},{6,7},{10,11},{14,15},{18,19},{22,23},{26,27},{30,31}} | collective-permute-start | bytes 786440 | tf_op jit(solution)/shard_map/ppermute | solution.py:14
  156.5 9.0 %collective-permute-start.34 = (f32[256,256]{0,1:T(8,128)S(1)}, f32[256,256]{0,1:T(8,128)S(1)}, u32[]{:S(2)}, u32[]{:S(2)}) collective-permute-start(f32[256,256]{0,1:T(8,128)S(1)} %get-tuple-element.6), channel_id=1, source_target_pairs={{2,1},{6,5},{10,9},{14,13},{18,17},{22,21},{26,25},{30,29}} | collective-permute-start | bytes 786440 | tf_op jit(solution)/shard_map/ppermute | solution.py:14
  159.5 8.6 %collective-permute-start.51 = (f32[256,256]{0,1:T(8,128)S(1)}, f32[256,256]{0,1:T(8,128)S(1)}, u32[]{:S(2)}, u32[]{:S(2)}) collective-permute-start(f32[256,256]{0,1:T(8,128)S(1)} %get-tuple-element.15), channel_id=1, source_target_pairs={{0,1},{4,5},{8,9},{12,13},{16,17},{20,21},{24,25},{28,29}} | collective-permute-start | bytes 786440 | tf_op jit(solution)/shard_map/ppermute | solution.py:14
  160.2 9.4 %collective-permute-start.52 = (f32[256,256]{0,1:T(8,128)S(1)}, f32[256,256]{0,1:T(8,128)S(1)}, u32[]{:S(2)}, u32[]{:S(2)}) collective-permute-start(f32[256,256]{0,1:T(8,128)S(1)} %get-tuple-element.15), channel_id=1, source_target_pairs={{1,2},{5,6},{9,10},{13,14},{17,18},{21,22},{25,26},{29,30}} | collective-permute-start | bytes 786440 | tf_op jit(solution)/shard_map/ppermute | solution.py:14
  168.1 8.3 %collective-permute-start.59 = (f32[256,256]{0,1:T(8,128)S(1)}, f32[256,256]{0,1:T(8,128)S(1)}, u32[]{:S(2)}, u32[]{:S(2)}) collective-permute-start(f32[256,256]{0,1:T(8,128)S(1)} %get-tuple-element.16), channel_id=1, source_target_pairs={{3,2},{7,6},{11,10},{15,14},{19,18},{23,22},{27,26},{31,30}} | collective-permute-start | bytes 786440 | tf_op jit(solution)/shard_map/ppermute | solution.py:14
  (32 other events, 199.9 us)

commit v20 on v17

--- a/solution.py
+++ b/solution.py
@@ -139,7 +139,10 @@
     results = []
     for part in range(SLICES):
         right_side = reduce_scatter_columns(gamma_partial[:, part * width:(part + 1) * width], "pair")
-        coefficients = solve(right_side, transfer, diag_inverse, sub_factor)
+        half = right_side.shape[1] // 2
+        coefficients = jnp.concatenate(
+            [solve(right_side[:, :half], transfer, diag_inverse, sub_factor),
+             solve(right_side[:, half:], transfer, diag_inverse, sub_factor)], axis=1)
         coeff_full = all_gather_columns(coefficients, "pair")
         partial = contract_first(screened, coeff_full)
         results.append(reduce_over_aux(partial))

time: 154 us -> 180 us (1.17)
  starting transfers between devices: 59.1 us -> 88.9 us
  waiting for transfers between devices: 67.2 us -> 55.8 us
  matrix products: 19.1 us -> 26.2 us
    ppermute x6 -> x12, waiting for transfers between devices: 17 us -> 4.85 us  [solve(): arriving = arriving + lax.ppermute(value, 'aux', [(sender, sender - 1)])]
    ppermute x6 -> x12, starting transfers between devices: 5.4 us -> 14.6 us  [solve(): incoming = incoming + lax.ppermute(value, 'aux', [(turn, turn + 1)])]
    ppermute x12, starting transfers between devices: 10.4 us -> 17.9 us  [swap(): return lax.ppermute(array, axis, [(i, i ^ bit) for i in range(count)])]
    dot_general x26 -> x44, matrix products: 17 us -> 24.1 us  [product(): jnp.dot(left, right, precision=lax.Precision.HIGH, preferred_element_type...]
    ppermute x6 -> x12, starting transfers between devices: 5.42 us -> 10.4 us  [solve(): arriving = arriving + lax.ppermute(value, 'aux', [(sender, sender - 1)])]
    ppermute x6, starting transfers between devices: 5.29 us -> 9.71 us  [reduce_over_aux(): lax.ppermute(to_left + block(index - (count - 1) + step), 'aux', leftward)]
    ppermute x6, waiting for transfers between devices: 4.44 us -> 8.49 us  [reduce_over_aux(): lax.ppermute(to_left + block(index - (count - 1) + step), 'aux', leftward)]
    ppermute x6, starting transfers between devices: 20.9 us -> 24.5 us  [reduce_over_aux(): lax.ppermute(to_right + block(index + count - 1 - step), 'aux', rightward)]
  transfers between devices with their start and end apart: 42 -> 54, of which waited for: 20 -> 17; matrix products, arithmetic and copies ran while one was open for 16% -> 18% of each run, Pallas kernels for 0% -> 0%
where the time goes in v20:
time: 180 us; the launch traced here: 179 us
  starting transfers between devices  88.9 us (49%)
  waiting for transfers between devices  55.8 us (31%)
  matrix products  26.2 us (15%)
  local copies, waits for them, and re-layouts  4.26 us (2%)
  other arithmetic  2.95 us (2%)
    ppermute x6, starting transfers between devices, reduce_over_aux(): lax.ppermute(to_right + block(index + count - 1 - step), 'aux', rightward)  24.5 us
    dot_general x44, matrix products, product(): jnp.dot(left, right, precision=lax.Precision.HIGH, preferred_element_type...  24.1 us
    ppermute x3, waiting for transfers between devices, gamma_over_aux(): from_right = lax.ppermute(from_right, 'aux', leftward)  23.4 us
    ppermute x12, starting transfers between devices, swap(): return lax.ppermute(array, axis, [(i, i ^ bit) for i in range(count)])  17.9 us
    ppermute x12, waiting for transfers between devices, swap(): return lax.ppermute(array, axis, [(i, i ^ bit) for i in range(count)])  14.8 us
    ppermute x12, starting transfers between devices, solve(): incoming = incoming + lax.ppermute(value, 'aux', [(turn, turn + 1)])  14.6 us
    ppermute x12, starting transfers between devices, solve(): arriving = arriving + lax.ppermute(value, 'aux', [(sender, sender - 1)])  10.4 us
    ppermute x6, starting transfers between devices, reduce_over_aux(): lax.ppermute(to_left + block(index - (count - 1) + step), 'aux', leftward)  9.71 us
  transfers between devices with their start and end apart: 54, of which 17 were waited for; matrix products, arithmetic and copies ran while one was open for 18% of the time, Pallas kernels for 0%

profile of v20, /device:TPU:0, one launch (start us, length us, event | category | flops | bytes accessed | tf_op | source)
XLA Modules:
  0.0 179.0 jit_solution(17601654828273198707)
XLA Ops:
  0.0 1.4 collective-permute-start.1
  1.4 6.4 %collective-permute-start = (f32[256,512]{1,0:T(8,128)}, f32[256,512]{1,0:T(8,128)}, u32[]{:S(2)}, u32[]{:S(2)}) collective-permute-start(f32[256,512]{1,0:T(8,128)} %param.6), channel_id=1, source_target_pairs={{0,1},{1,2},{2,3},{4,5},{5,6},{6,7},{8,9},{9,10},{10,11},{12,13},{... | collective-permute-start | bytes 1572872 | tf_op jit(solution)/shard_map/ppermute | solution.py:87
  7.8 2.9 %copy.8 = f32[512,1024]{0,1:T(8,128)} copy(f32[512,1024]{1,0:T(8,128)} %param.5) | data formatting | bytes 4194304 | tf_op args[0]
  11.0 1.8 %bitcast_multiply_fusion = f32[512,1024]{0,1:T(8,128)S(1)} fusion(f32[512,1024]{0,1:T(8,128)} %copy.8, f32[512,16]{0,1:T(8,128)S(1)} %reshape.6), kind=kLoop, calls=%fused_computation | loop fusion | flops 524288 | bytes 4227072 | tf_op jit(solution)/shard_map/mul | solution.py:23
  12.8 1.7 fusion.22
  14.5 2.8 %collective-permute-done.1 = f32[256,512]{1,0:T(8,128)} collective-permute-done((f32[256,512]{1,0:T(8,128)}, f32[256,512]{1,0:T(8,128)}, u32[]{:S(2)}, u32[]{:S(2)}) %collective-permute-start.1) | collective-permute-done | bytes 524320 | tf_op jit(solution)/shard_map/ppermute | solution.py:88
  19.3 1.7 convolution_add_fusion.3
  21.0 1.7 convolution_add_fusion.2
  22.6 9.8 %collective-permute-done.3 = f32[256,512]{1,0:T(8,128)S(1)} collective-permute-done((f32[256,512]{1,0:T(8,128)}, f32[256,512]{1,0:T(8,128)S(1)}, u32[]{:S(2)}, u32[]{:S(2)}) %collective-permute-start.3) | collective-permute-done | bytes 524320 | tf_op jit(solution)/shard_map/ppermute | solution.py:88
  35.8 10.8 %collective-permute-done.5 = f32[256,512]{1,0:T(8,128)S(1)} collective-permute-done((f32[256,512]{1,0:T(8,128)S(1)}, f32[256,512]{1,0:T(8,128)S(1)}, u32[]{:S(2)}, u32[]{:S(2)}) %collective-permute-start.5) | collective-permute-done | bytes 524320 | tf_op jit(solution)/shard_map/ppermute | solution.py:88
  51.2 6.3 %collective-permute-start.31 = (f32[512,64]{0,1:T(8,128)S(1)}, f32[512,64]{0,1:T(8,128)S(1)}, u32[]{:S(2)}, u32[]{:S(2)}) collective-permute-start(f32[512,64]{0,1:T(8,128)S(1)} %slice_select_fusion.2), channel_id=1, source_target_pairs={{0,8},{4,12},{8,0},{12,4},{16,24},{20,28},{24,16},{28,20},{1,9},{5... | collective-permute-start | bytes 393224 | tf_op jit(solution)/shard_map/ppermute | solution.py:15
  57.6 1.9 %collective-permute-start.8 = (f32[512,32]{0,1:T(8,128)S(1)}, f32[512,32]{0,1:T(8,128)S(1)}, u32[]{:S(2)}, u32[]{:S(2)}) collective-permute-start(f32[512,32]{0,1:T(8,128)S(1)} %slice_select_fusion.5), channel_id=1, source_target_pairs={{0,16},{4,20},{8,24},{12,28},{16,0},{20,4},{24,8},{28,12},{1,17},{... | collective-permute-start | bytes 196616 | tf_op jit(solution)/shard_map/ppermute | solution.py:15
  59.5 3.7 %collective-permute-done.31 = f32[512,64]{0,1:T(8,128)S(1)} collective-permute-done((f32[512,64]{0,1:T(8,128)S(1)}, f32[512,64]{0,1:T(8,128)S(1)}, u32[]{:S(2)}, u32[]{:S(2)}) %collective-permute-start.31) | collective-permute-done | bytes 131104 | tf_op jit(solution)/shard_map/ppermute | solution.py:15
  63.3 4.5 %collective-permute-start.32 = (f32[512,32]{0,1:T(8,128)S(1)}, f32[512,32]{0,1:T(8,128)S(1)}, u32[]{:S(2)}, u32[]{:S(2)}) collective-permute-start(f32[512,32]{0,1:T(8,128)S(1)} %slice_select_fusion.4), channel_id=1, source_target_pairs={{0,16},{4,20},{8,24},{12,28},{16,0},{20,4},{24,8},{28,12},{1,17},{... | collective-permute-start | bytes 196616 | tf_op jit(solution)/shard_map/ppermute | solution.py:15
  68.8 3.8 %collective-permute-start.9 = (f32[512,16]{0,1:T(8,128)S(1)}, f32[512,16]{0,1:T(8,128)S(1)}, u32[]{:S(2)}, u32[]{:S(2)}) collective-permute-start(f32[512,16]{0,1:T(8,128)S(1)} %convolution_bitcast_fusion.11), channel_id=1, source_target_pairs={{0,1},{4,5},{8,9},{12,13},{16,17},{20,21},{24,25},{28,29}} | collective-permute-start | bytes 98312 | tf_op jit(solution)/shard_map/ppermute | solution.py:119
  73.7 2.8 %collective-permute-start.15 = (f32[512,16]{0,1:T(8,128)S(1)}, f32[512,16]{0,1:T(8,128)S(1)}, u32[]{:S(2)}, u32[]{:S(2)}) collective-permute-start(f32[512,16]{0,1:T(8,128)S(1)} %convolution_bitcast_fusion.8), channel_id=1, source_target_pairs={{0,1},{4,5},{8,9},{12,13},{16,17},{20,21},{24,25},{28,29}} | collective-permute-start | bytes 98312 | tf_op jit(solution)/shard_map/ppermute | solution.py:119
  107.6 2.8 %collective-permute-done.14 = f32[512,16]{0,1:T(8,128)S(1)} collective-permute-done((f32[512,16]{0,1:T(8,128)S(1)}, f32[512,16]{0,1:T(8,128)S(1)}, u32[]{:S(2)}, u32[]{:S(2)}) %collective-permute-start.14) | collective-permute-done | bytes 32800 | tf_op jit(solution)/shard_map/ppermute | solution.py:127
  110.7 1.3 collective-permute-done.20
  114.1 2.7 %collective-permute-done.21 = f32[512,32]{0,1:T(8,128)S(1)} collective-permute-done((f32[512,32]{0,1:T(8,128)S(1)}, f32[512,32]{0,1:T(8,128)S(1)}, u32[]{:S(2)}, u32[]{:S(2)}) %collective-permute-start.21) | collective-permute-done | bytes 65568 | tf_op jit(solution)/shard_map/ppermute | solution.py:15
  116.8 1.5 collective-permute-start.22
  119.3 2.5 %collective-permute-done.22 = f32[512,64]{0,1:T(8,128)S(1)} collective-permute-done((f32[512,64]{0,1:T(8,128)S(1)}, f32[512,64]{0,1:T(8,128)S(1)}, u32[]{:S(2)}, u32[]{:S(2)}) %collective-permute-start.22) | collective-permute-done | bytes 131104 | tf_op jit(solution)/shard_map/ppermute | solution.py:15
  123.7 4.4 %collective-permute-done.46 = f32[512,64]{0,1:T(8,128)S(1)} collective-permute-done((f32[512,64]{0,1:T(8,128)S(1)}, f32[512,64]{0,1:T(8,128)S(1)}, u32[]{:S(2)}, u32[]{:S(2)}) %collective-permute-start.46) | collective-permute-done | bytes 131104 | tf_op jit(solution)/shard_map/ppermute | solution.py:15
  129.3 3.7 %collective-permute-start.24 = (f32[256,256]{0,1:T(8,128)S(1)}, f32[256,256]{0,1:T(8,128)S(1)}, u32[]{:S(2)}, u32[]{:S(2)}) collective-permute-start(f32[256,256]{0,1:T(8,128)S(1)} %get-tuple-element.10), channel_id=1, source_target_pairs={{0,1},{4,5},{8,9},{12,13},{16,17},{20,21},{24,25},{28,29}} | collective-permute-start | bytes 786440 | tf_op jit(solution)/shard_map/ppermute | solution.py:108
  134.8 1.3 collective-permute-start.48
  136.8 2.8 %collective-permute-done.24 = f32[256,256]{0,1:T(8,128)S(1)} collective-permute-done((f32[256,256]{0,1:T(8,128)S(1)}, f32[256,256]{0,1:T(8,128)S(1)}, u32[]{:S(2)}, u32[]{:S(2)}) %collective-permute-start.24) | collective-permute-done | bytes 262176 | tf_op jit(solution)/shard_map/ppermute | solution.py:108
  139.7 4.4 %collective-permute-start.25 = (f32[256,256]{0,1:T(8,128)S(1)}, f32[256,256]{0,1:T(8,128)S(1)}, u32[]{:S(2)}, u32[]{:S(2)}) collective-permute-start(f32[256,256]{0,1:T(8,128)S(1)} %get-tuple-element.8), channel_id=1, source_target_pairs={{0,1},{1,2},{4,5},{5,6},{8,9},{9,10},{12,13},{13,14},{16,17},{17,1... | collective-permute-start | bytes 786440 | tf_op jit(solution)/shard_map/ppermute | solution.py:108
  145.3 4.4 %collective-permute-start.49 = (f32[256,256]{0,1:T(8,128)S(1)}, f32[256,256]{0,1:T(8,128)S(1)}, u32[]{:S(2)}, u32[]{:S(2)}) collective-permute-start(f32[256,256]{0,1:T(8,128)S(1)} %get-tuple-element.18), channel_id=1, source_target_pairs={{0,1},{1,2},{4,5},{5,6},{8,9},{9,10},{12,13},{13,14},{16,17},{17,1... | collective-permute-start | bytes 786440 | tf_op jit(solution)/shard_map/ppermute | solution.py:108
  150.9 5.7 %collective-permute-start.26 = (f32[256,256]{0,1:T(8,128)S(1)}, f32[256,256]{0,1:T(8,128)S(1)}, u32[]{:S(2)}, u32[]{:S(2)}) collective-permute-start(f32[256,256]{0,1:T(8,128)S(1)} %get-tuple-element.6), channel_id=1, source_target_pairs={{0,1},{1,2},{2,3},{4,5},{5,6},{6,7},{8,9},{9,10},{10,11},{12,13},{... | collective-permute-start | bytes 786440 | tf_op jit(solution)/shard_map/ppermute | solution.py:108
  156.6 1.3 collective-permute-start.29
  158.0 5.0 %collective-permute-start.50 = (f32[256,256]{0,1:T(8,128)S(1)}, f32[256,256]{0,1:T(8,128)S(1)}, u32[]{:S(2)}, u32[]{:S(2)}) collective-permute-start(f32[256,256]{0,1:T(8,128)S(1)} %get-tuple-element.16), channel_id=1, source_target_pairs={{0,1},{1,2},{2,3},{4,5},{5,6},{6,7},{8,9},{9,10},{10,11},{12,13},{... | collective-permute-start | bytes 786440 | tf_op jit(solution)/shard_map/ppermute | solution.py:108
  163.0 5.7 %collective-permute-start.53 = (f32[256,256]{0,1:T(8,128)S(1)}, f32[256,256]{0,1:T(8,128)S(1)}, u32[]{:S(2)}, u32[]{:S(2)}) collective-permute-start(f32[256,256]{0,1:T(8,128)S(1)} %get-tuple-element.15), channel_id=1, source_target_pairs={{1,0},{2,1},{3,2},{5,4},{6,5},{7,6},{9,8},{10,9},{11,10},{13,12},{... | collective-permute-start | bytes 786440 | tf_op jit(solution)/shard_map/ppermute | solution.py:109
  169.4 8.5 %collective-permute-done.53 = f32[256,256]{0,1:T(8,128)S(1)} collective-permute-done((f32[256,256]{0,1:T(8,128)S(1)}, f32[256,256]{0,1:T(8,128)S(1)}, u32[]{:S(2)}, u32[]{:S(2)}) %collective-permute-start.53) | collective-permute-done | bytes 262176 | tf_op jit(solution)/shard_map/ppermute | solution.py:109
  (168 shorter events, 56.0 us)
Async XLA Ops:
  0.0 17.3 %collective-permute-start.1 = (f32[256,512]{1,0:T(8,128)}, f32[256,512]{1,0:T(8,128)}, u32[]{:S(2)}, u32[]{:S(2)}) collective-permute-start(f32[256,512]{1,0:T(8,128)} %param.6), channel_id=1, source_target_pairs={{1,0},{2,1},{3,2},{5,4},{6,5},{7,6},{9,8},{10,9},{11,10},{13,12},{... | collective-permute-start | bytes 1572872 | tf_op jit(solution)/shard_map/ppermute | solution.py:88
  1.4 17.2 %collective-permute-start = (f32[256,512]{1,0:T(8,128)}, f32[256,512]{1,0:T(8,128)}, u32[]{:S(2)}, u32[]{:S(2)}) collective-permute-start(f32[256,512]{1,0:T(8,128)} %param.6), channel_id=1, source_target_pairs={{0,1},{1,2},{2,3},{4,5},{5,6},{6,7},{8,9},{9,10},{10,11},{12,13},{... | collective-permute-start | bytes 1572872 | tf_op jit(solution)/shard_map/ppermute | solution.py:87
  17.3 15.2 %collective-permute-start.3 = (f32[256,512]{1,0:T(8,128)}, f32[256,512]{1,0:T(8,128)S(1)}, u32[]{:S(2)}, u32[]{:S(2)}) collective-permute-start(f32[256,512]{1,0:T(8,128)} %collective-permute-done.1), channel_id=1, source_target_pairs={{1,0},{2,1},{5,4},{6,5},{9,8},{10,9},{13,12},{14,13},{17,16},{18,1... | collective-permute-start | bytes 1572872 | tf_op jit(solution)/shard_map/ppermute | solution.py:88
  18.6 15.2 %collective-permute-start.2 = (f32[256,512]{1,0:T(8,128)}, f32[256,512]{1,0:T(8,128)S(1)}, u32[]{:S(2)}, u32[]{:S(2)}) collective-permute-start(f32[256,512]{1,0:T(8,128)} %collective-permute-done), channel_id=1, source_target_pairs={{1,2},{2,3},{5,6},{6,7},{9,10},{10,11},{13,14},{14,15},{17,18},{18... | collective-permute-start | bytes 1572872 | tf_op jit(solution)/shard_map/ppermute | solution.py:87
  32.5 14.1 %collective-permute-start.5 = (f32[256,512]{1,0:T(8,128)S(1)}, f32[256,512]{1,0:T(8,128)S(1)}, u32[]{:S(2)}, u32[]{:S(2)}) collective-permute-start(f32[256,512]{1,0:T(8,128)S(1)} %collective-permute-done.3), channel_id=1, source_target_pairs={{1,0},{5,4},{9,8},{13,12},{17,16},{21,20},{25,24},{29,28}} | collective-permute-start | bytes 1572872 | tf_op jit(solution)/shard_map/ppermute | solution.py:88
  33.8 13.4 %collective-permute-start.4 = (f32[256,512]{1,0:T(8,128)S(1)}, f32[256,512]{1,0:T(8,128)S(1)}, u32[]{:S(2)}, u32[]{:S(2)}) collective-permute-start(f32[256,512]{1,0:T(8,128)S(1)} %collective-permute-done.2), channel_id=1, source_target_pairs={{2,3},{6,7},{10,11},{14,15},{18,19},{22,23},{26,27},{30,31}} | collective-permute-start | bytes 1572872 | tf_op jit(solution)/shard_map/ppermute | solution.py:87
  50.1 7.4 %collective-permute-start.7 = (f32[512,64]{0,1:T(8,128)S(1)}, f32[512,64]{0,1:T(8,128)S(1)}, u32[]{:S(2)}, u32[]{:S(2)}) collective-permute-start(f32[512,64]{0,1:T(8,128)S(1)} %slice_select_fusion.3), channel_id=1, source_target_pairs={{0,8},{4,12},{8,0},{12,4},{16,24},{20,28},{24,16},{28,20},{1,9},{5... | collective-permute-start | bytes 393224 | tf_op jit(solution)/shard_map/ppermute | solution.py:15
  51.2 12.0 %collective-permute-start.31 = (f32[512,64]{0,1:T(8,128)S(1)}, f32[512,64]{0,1:T(8,128)S(1)}, u32[]{:S(2)}, u32[]{:S(2)}) collective-permute-start(f32[512,64]{0,1:T(8,128)S(1)} %slice_select_fusion.2), channel_id=1, source_target_pairs={{0,8},{4,12},{8,0},{12,4},{16,24},{20,28},{24,16},{28,20},{1,9},{5... | collective-permute-start | bytes 393224 | tf_op jit(solution)/shard_map/ppermute | solution.py:15
  57.6 10.1 %collective-permute-start.8 = (f32[512,32]{0,1:T(8,128)S(1)}, f32[512,32]{0,1:T(8,128)S(1)}, u32[]{:S(2)}, u32[]{:S(2)}) collective-permute-start(f32[512,32]{0,1:T(8,128)S(1)} %slice_select_fusion.5), channel_id=1, source_target_pairs={{0,16},{4,20},{8,24},{12,28},{16,0},{20,4},{24,8},{28,12},{1,17},{... | collective-permute-start | bytes 196616 | tf_op jit(solution)/shard_map/ppermute | solution.py:15
  63.3 9.4 %collective-permute-start.32 = (f32[512,32]{0,1:T(8,128)S(1)}, f32[512,32]{0,1:T(8,128)S(1)}, u32[]{:S(2)}, u32[]{:S(2)}) collective-permute-start(f32[512,32]{0,1:T(8,128)S(1)} %slice_select_fusion.4), channel_id=1, source_target_pairs={{0,16},{4,20},{8,24},{12,28},{16,0},{20,4},{24,8},{28,12},{1,17},{... | collective-permute-start | bytes 196616 | tf_op jit(solution)/shard_map/ppermute | solution.py:15
  68.8 10.3 %collective-permute-start.9 = (f32[512,16]{0,1:T(8,128)S(1)}, f32[512,16]{0,1:T(8,128)S(1)}, u32[]{:S(2)}, u32[]{:S(2)}) collective-permute-start(f32[512,16]{0,1:T(8,128)S(1)} %convolution_bitcast_fusion.11), channel_id=1, source_target_pairs={{0,1},{4,5},{8,9},{12,13},{16,17},{20,21},{24,25},{28,29}} | collective-permute-start | bytes 98312 | tf_op jit(solution)/shard_map/ppermute | solution.py:119
  73.7 6.6 %collective-permute-start.15 = (f32[512,16]{0,1:T(8,128)S(1)}, f32[512,16]{0,1:T(8,128)S(1)}, u32[]{:S(2)}, u32[]{:S(2)}) collective-permute-start(f32[512,16]{0,1:T(8,128)S(1)} %convolution_bitcast_fusion.8), channel_id=1, source_target_pairs={{0,1},{4,5},{8,9},{12,13},{16,17},{20,21},{24,25},{28,29}} | collective-permute-start | bytes 98312 | tf_op jit(solution)/shard_map/ppermute | solution.py:119
  87.0 5.8 %collective-permute-start.35 = (f32[512,16]{0,1:T(8,128)S(1)}, f32[512,16]{0,1:T(8,128)S(1)}, u32[]{:S(2)}, u32[]{:S(2)}) collective-permute-start(f32[512,16]{0,1:T(8,128)S(1)} %convolution_add_fusion.12), channel_id=1, source_target_pairs={{2,3},{6,7},{10,11},{14,15},{18,19},{22,23},{26,27},{30,31}} | collective-permute-start | bytes 98312 | tf_op jit(solution)/shard_map/ppermute | solution.py:119
  88.3 6.5 %collective-permute-start.41 = (f32[512,16]{0,1:T(8,128)S(1)}, f32[512,16]{0,1:T(8,128)S(1)}, u32[]{:S(2)}, u32[]{:S(2)}) collective-permute-start(f32[512,16]{0,1:T(8,128)S(1)} %convolution_add_fusion.7), channel_id=1, source_target_pairs={{2,3},{6,7},{10,11},{14,15},{18,19},{22,23},{26,27},{30,31}} | collective-permute-start | bytes 98312 | tf_op jit(solution)/shard_map/ppermute | solution.py:119
  90.2 6.5 %collective-permute-start.12 = (f32[512,16]{0,1:T(8,128)S(1)}, f32[512,16]{0,1:T(8,128)S(1)}, u32[]{:S(2)}, u32[]{:S(2)}) collective-permute-start(f32[512,16]{0,1:T(8,128)S(1)} %convolution_bitcast_fusion.10), channel_id=1, source_target_pairs={{3,2},{7,6},{11,10},{15,14},{19,18},{23,22},{27,26},{31,30}} | collective-permute-start | bytes 98312 | tf_op jit(solution)/shard_map/ppermute | solution.py:127
  101.2 9.2 %collective-permute-start.14 = (f32[512,16]{0,1:T(8,128)S(1)}, f32[512,16]{0,1:T(8,128)S(1)}, u32[]{:S(2)}, u32[]{:S(2)}) collective-permute-start(f32[512,16]{0,1:T(8,128)S(1)} %convolution_add_fusion.19), channel_id=1, source_target_pairs={{1,0},{5,4},{9,8},{13,12},{17,16},{21,20},{25,24},{29,28}} | collective-permute-start | bytes 98312 | tf_op jit(solution)/shard_map/ppermute | solution.py:127
  102.9 9.2 %collective-permute-start.20 = (f32[512,16]{0,1:T(8,128)S(1)}, f32[512,16]{0,1:T(8,128)S(1)}, u32[]{:S(2)}, u32[]{:S(2)}) collective-permute-start(f32[512,16]{0,1:T(8,128)S(1)} %convolution_add_fusion.14), channel_id=1, source_target_pairs={{1,0},{5,4},{9,8},{13,12},{17,16},{21,20},{25,24},{29,28}} | collective-permute-start | bytes 98312 | tf_op jit(solution)/shard_map/ppermute | solution.py:127
  104.6 9.2 %collective-permute-start.38 = (f32[512,16]{0,1:T(8,128)S(1)}, f32[512,16]{0,1:T(8,128)S(1)}, u32[]{:S(2)}, u32[]{:S(2)}) collective-permute-start(f32[512,16]{0,1:T(8,128)S(1)} %convolution_add_fusion.9), channel_id=1, source_target_pairs={{1,0},{5,4},{9,8},{13,12},{17,16},{21,20},{25,24},{29,28}} | collective-permute-start | bytes 98312 | tf_op jit(solution)/shard_map/ppermute | solution.py:127
  106.3 12.1 %collective-permute-start.44 = (f32[512,16]{0,1:T(8,128)S(1)}, f32[512,16]{0,1:T(8,128)S(1)}, u32[]{:S(2)}, u32[]{:S(2)}) collective-permute-start(f32[512,16]{0,1:T(8,128)S(1)} %convolution_add_fusion.4), channel_id=1, source_target_pairs={{1,0},{5,4},{9,8},{13,12},{17,16},{21,20},{25,24},{29,28}} | collective-permute-start | bytes 98312 | tf_op jit(solution)/shard_map/ppermute | solution.py:127
  121.8 6.4 %collective-permute-start.23 = (f32[512,128]{0,1:T(8,128)S(1)}, f32[512,128]{0,1:T(8,128)S(1)}, u32[]{:S(2)}, u32[]{:S(2)}) collective-permute-start(f32[512,128]{0,1:T(8,128)S(1)} %maximum_select_fusion.4), channel_id=1, source_target_pairs={{0,4},{4,0},{8,12},{12,8},{16,20},{20,16},{24,28},{28,24},{1,5},{5... | collective-permute-start | bytes 786440 | tf_op jit(solution)/shard_map/ppermute | solution.py:15
  129.3 10.3 %collective-permute-start.24 = (f32[256,256]{0,1:T(8,128)S(1)}, f32[256,256]{0,1:T(8,128)S(1)}, u32[]{:S(2)}, u32[]{:S(2)}) collective-permute-start(f32[256,256]{0,1:T(8,128)S(1)} %get-tuple-element.10), channel_id=1, source_target_pairs={{0,1},{4,5},{8,9},{12,13},{16,17},{20,21},{24,25},{28,29}} | collective-permute-start | bytes 786440 | tf_op jit(solution)/shard_map/ppermute | solution.py:108
  133.0 6.6 %collective-permute-start.27 = (f32[256,256]{0,1:T(8,128)S(1)}, f32[256,256]{0,1:T(8,128)S(1)}, u32[]{:S(2)}, u32[]{:S(2)}) collective-permute-start(f32[256,256]{0,1:T(8,128)S(1)} %get-tuple-element.9), channel_id=1, source_target_pairs={{3,2},{7,6},{11,10},{15,14},{19,18},{23,22},{27,26},{31,30}} | collective-permute-start | bytes 786440 | tf_op jit(solution)/shard_map/ppermute | solution.py:109
  134.8 10.4 %collective-permute-start.48 = (f32[256,256]{0,1:T(8,128)S(1)}, f32[256,256]{0,1:T(8,128)S(1)}, u32[]{:S(2)}, u32[]{:S(2)}) collective-permute-start(f32[256,256]{0,1:T(8,128)S(1)} %get-tuple-element.20), channel_id=1, source_target_pairs={{0,1},{4,5},{8,9},{12,13},{16,17},{20,21},{24,25},{28,29}} | collective-permute-start | bytes 786440 | tf_op jit(solution)/shard_map/ppermute | solution.py:108
  136.1 9.1 %collective-permute-start.51 = (f32[256,256]{0,1:T(8,128)S(1)}, f32[256,256]{0,1:T(8,128)S(1)}, u32[]{:S(2)}, u32[]{:S(2)}) collective-permute-start(f32[256,256]{0,1:T(8,128)S(1)} %get-tuple-element.19), channel_id=1, source_target_pairs={{3,2},{7,6},{11,10},{15,14},{19,18},{23,22},{27,26},{31,30}} | collective-permute-start | bytes 786440 | tf_op jit(solution)/shard_map/ppermute | solution.py:109
  139.7 11.1 %collective-permute-start.25 = (f32[256,256]{0,1:T(8,128)S(1)}, f32[256,256]{0,1:T(8,128)S(1)}, u32[]{:S(2)}, u32[]{:S(2)}) collective-permute-start(f32[256,256]{0,1:T(8,128)S(1)} %get-tuple-element.8), channel_id=1, source_target_pairs={{0,1},{1,2},{4,5},{5,6},{8,9},{9,10},{12,13},{13,14},{16,17},{17,1... | collective-permute-start | bytes 786440 | tf_op jit(solution)/shard_map/ppermute | solution.py:108
  144.1 6.7 %collective-permute-start.28 = (f32[256,256]{0,1:T(8,128)S(1)}, f32[256,256]{0,1:T(8,128)S(1)}, u32[]{:S(2)}, u32[]{:S(2)}) collective-permute-start(f32[256,256]{0,1:T(8,128)S(1)} %get-tuple-element.7), channel_id=1, source_target_pairs={{2,1},{3,2},{6,5},{7,6},{10,9},{11,10},{14,13},{15,14},{18,17},{19... | collective-permute-start | bytes 786440 | tf_op jit(solution)/shard_map/ppermute | solution.py:109
  145.3 12.6 %collective-permute-start.49 = (f32[256,256]{0,1:T(8,128)S(1)}, f32[256,256]{0,1:T(8,128)S(1)}, u32[]{:S(2)}, u32[]{:S(2)}) collective-permute-start(f32[256,256]{0,1:T(8,128)S(1)} %get-tuple-element.18), channel_id=1, source_target_pairs={{0,1},{1,2},{4,5},{5,6},{8,9},{9,10},{12,13},{13,14},{16,17},{17,1... | collective-permute-start | bytes 786440 | tf_op jit(solution)/shard_map/ppermute | solution.py:108
  149.7 8.2 %collective-permute-start.52 = (f32[256,256]{0,1:T(8,128)S(1)}, f32[256,256]{0,1:T(8,128)S(1)}, u32[]{:S(2)}, u32[]{:S(2)}) collective-permute-start(f32[256,256]{0,1:T(8,128)S(1)} %get-tuple-element.17), channel_id=1, source_target_pairs={{2,1},{3,2},{6,5},{7,6},{10,9},{11,10},{14,13},{15,14},{18,17},{19... | collective-permute-start | bytes 786440 | tf_op jit(solution)/shard_map/ppermute | solution.py:109
  150.9 17.8 %collective-permute-start.26 = (f32[256,256]{0,1:T(8,128)S(1)}, f32[256,256]{0,1:T(8,128)S(1)}, u32[]{:S(2)}, u32[]{:S(2)}) collective-permute-start(f32[256,256]{0,1:T(8,128)S(1)} %get-tuple-element.6), channel_id=1, source_target_pairs={{0,1},{1,2},{2,3},{4,5},{5,6},{6,7},{8,9},{9,10},{10,11},{12,13},{... | collective-permute-start | bytes 786440 | tf_op jit(solution)/shard_map/ppermute | solution.py:108
  156.6 12.2 %collective-permute-start.29 = (f32[256,256]{0,1:T(8,128)S(1)}, f32[256,256]{0,1:T(8,128)S(1)}, u32[]{:S(2)}, u32[]{:S(2)}) collective-permute-start(f32[256,256]{0,1:T(8,128)S(1)} %get-tuple-element.5), channel_id=1, source_target_pairs={{1,0},{2,1},{3,2},{5,4},{6,5},{7,6},{9,8},{10,9},{11,10},{13,12},{... | collective-permute-start | bytes 786440 | tf_op jit(solution)/shard_map/ppermute | solution.py:109
  158.0 11.4 %collective-permute-start.50 = (f32[256,256]{0,1:T(8,128)S(1)}, f32[256,256]{0,1:T(8,128)S(1)}, u32[]{:S(2)}, u32[]{:S(2)}) collective-permute-start(f32[256,256]{0,1:T(8,128)S(1)} %get-tuple-element.16), channel_id=1, source_target_pairs={{0,1},{1,2},{2,3},{4,5},{5,6},{6,7},{8,9},{9,10},{10,11},{12,13},{... | collective-permute-start | bytes 786440 | tf_op jit(solution)/shard_map/ppermute | solution.py:108
  163.0 14.8 %collective-permute-start.53 = (f32[256,256]{0,1:T(8,128)S(1)}, f32[256,256]{0,1:T(8,128)S(1)}, u32[]{:S(2)}, u32[]{:S(2)}) collective-permute-start(f32[256,256]{0,1:T(8,128)S(1)} %get-tuple-element.15), channel_id=1, source_target_pairs={{1,0},{2,1},{3,2},{5,4},{6,5},{7,6},{9,8},{10,9},{11,10},{13,12},{... | collective-permute-start | bytes 786440 | tf_op jit(solution)/shard_map/ppermute | solution.py:109
  (25 other events, 150.8 us)

commit v21 on v17

--- a/solution.py
+++ b/solution.py
@@ -44,10 +44,9 @@
     bit = 1
     while bit < count:
         width = current.shape[1] // 2
-        low, high = current[:, :width], current[:, width:]
-        upper = (index // bit) % 2 == 1
-        send = jnp.where(upper, low, high)
-        keep = jnp.where(upper, high, low)
+        upper = (index // bit) % 2
+        send = lax.dynamic_slice_in_dim(current, (1 - upper) * width, width, axis=1)
+        keep = lax.dynamic_slice_in_dim(current, upper * width, width, axis=1)
         current = keep + swap(send, axis, bit)
         bit *= 2
     return current

time: 154 us -> 159 us (1.032)
  waiting for transfers between devices: 67.2 us -> 64.2 us
  local copies, waits for them, and re-layouts: 4.24 us -> 6.96 us
  matrix products: 19.1 us -> 21.2 us
  other arithmetic: 2.88 us -> 4.6 us
    add x3 -> x4, other arithmetic: 0.2 us -> 2.09 us  [reduce_scatter_columns(): current = keep + swap(send, axis, bit)]
    dot_general x2, matrix products: 2.08 us -> 3.78 us  [contract_first(): lax.dot_general(left, right, (((0,), (0,)), ((), ())), precision=lax.Prec...]
    unnamed x7 -> x13, local copies, waits for them, and re-layouts: 2.92 us -> 3.72 us
  transfers between devices with their start and end apart: 42 -> 42, of which waited for: 20 -> 19; matrix products, arithmetic and copies ran while one was open for 16% -> 18% of each run, Pallas kernels for 0% -> 0%
where the time goes in v21:
time: 159 us; the launch traced here: 158 us
  waiting for transfers between devices  64.2 us (40%)
  starting transfers between devices  60.1 us (38%)
  matrix products  21.2 us (13%)
  local copies, waits for them, and re-layouts  6.96 us (4%)
  other arithmetic  4.6 us (3%)
    ppermute x3, waiting for transfers between devices, gamma_over_aux(): from_right = lax.ppermute(from_right, 'aux', leftward)  23 us
    ppermute x6, starting transfers between devices, reduce_over_aux(): lax.ppermute(to_right + block(index + count - 1 - step), 'aux', rightward)  20.9 us
    dot_general x26, matrix products, product(): jnp.dot(left, right, precision=lax.Precision.HIGH, preferred_element_type...  17.4 us
    ppermute x6, waiting for transfers between devices, solve(): arriving = arriving + lax.ppermute(value, 'aux', [(sender, sender - 1)])  15.5 us
    ppermute x12, waiting for transfers between devices, swap(): return lax.ppermute(array, axis, [(i, i ^ bit) for i in range(count)])  14.3 us
    ppermute x12, starting transfers between devices, swap(): return lax.ppermute(array, axis, [(i, i ^ bit) for i in range(count)])  11.3 us
    ppermute x3, starting transfers between devices, gamma_over_aux(): from_left = lax.ppermute(from_left, 'aux', rightward)  7.75 us
    ppermute x6, waiting for transfers between devices, reduce_over_aux(): lax.ppermute(to_right + block(index + count - 1 - step), 'aux', rightward)  6.53 us
  transfers between devices with their start and end apart: 42, of which 19 were waited for; matrix products, arithmetic and copies ran while one was open for 18% of the time, Pallas kernels for 0%

profile of v21, /device:TPU:0, one launch (start us, length us, event | category | flops | bytes accessed | tf_op | source)
XLA Modules:
  0.0 157.9 jit_solution(7736280727082821144)
XLA Ops:
  0.0 1.4 collective-permute-start.1
  1.4 6.4 %collective-permute-start = (f32[256,512]{1,0:T(8,128)}, f32[256,512]{1,0:T(8,128)}, u32[]{:S(2)}, u32[]{:S(2)}) collective-permute-start(f32[256,512]{1,0:T(8,128)} %param.6), channel_id=1, source_target_pairs={{0,1},{1,2},{2,3},{4,5},{5,6},{6,7},{8,9},{9,10},{10,11},{12,13},{... | collective-permute-start | bytes 1572872 | tf_op jit(solution)/shard_map/ppermute | solution.py:86
  7.8 2.9 %copy.8 = f32[512,1024]{0,1:T(8,128)} copy(f32[512,1024]{1,0:T(8,128)} %param.5) | data formatting | bytes 4194304 | tf_op args[0]
  10.9 1.8 %bitcast_multiply_fusion = f32[512,1024]{0,1:T(8,128)S(1)} fusion(f32[512,1024]{0,1:T(8,128)} %copy.8, f32[512,16]{0,1:T(8,128)S(1)} %reshape.6), kind=kLoop, calls=%fused_computation | loop fusion | flops 524288 | bytes 4227072 | tf_op jit(solution)/shard_map/mul | solution.py:23
  12.8 2.1 %fusion.22 = f32[512,512]{0,1:T(8,128)S(1)} fusion(f32[256,512]{1,0:T(8,128)} %param.6, f32[512,1024]{0,1:T(8,128)S(1)} %bitcast_multiply_fusion, s32[]{:T(128)S(6)} %select_n.153), kind=kOutput, calls=%fused_computation.47 | convolution fusion | flops 402653184 | bytes 2097156 | tf_op jit(solution)/shard_map/dot_general | solution.py:27
  14.9 2.4 %collective-permute-done.1 = f32[256,512]{1,0:T(8,128)} collective-permute-done((f32[256,512]{1,0:T(8,128)}, f32[256,512]{1,0:T(8,128)}, u32[]{:S(2)}, u32[]{:S(2)}) %collective-permute-start.1) | collective-permute-done | bytes 524320 | tf_op jit(solution)/shard_map/ppermute | solution.py:87
  19.3 1.7 %convolution_add_fusion.3 = f32[512,512]{0,1:T(8,128)S(1)} fusion(f32[512,512]{0,1:T(8,128)S(1)} %fusion.22, f32[256,512]{1,0:T(8,128)} %collective-permute-done, f32[512,1024]{0,1:T(8,128)S(1)} %bitcast_multiply_fusion, s32[]{:T(128)S(6)} %select_n.154), kind=kOutput, calls=%fused_computation.6 | convolution fusion | flops 402915328 | bytes 3145732 | tf_op jit(solution)/shard_map/dot_general | solution.py:27
  21.0 1.7 %convolution_add_fusion.2 = f32[512,512]{0,1:T(8,128)S(1)} fusion(f32[512,512]{0,1:T(8,128)S(1)} %convolution_add_fusion.3, f32[256,512]{1,0:T(8,128)} %collective-permute-done.1, f32[512,1024]{0,1:T(8,128)S(1)} %bitcast_multiply_fusion, s32[]{:T(128)S(6)} %select_n.155), kind=kOutput, calls=%fused_computation.5 | convolution fusion | flops 402915328 | bytes 3145732 | tf_op jit(solution)/shard_map/dot_general | solution.py:27
  22.6 9.8 %collective-permute-done.3 = f32[256,512]{1,0:T(8,128)S(1)} collective-permute-done((f32[256,512]{1,0:T(8,128)}, f32[256,512]{1,0:T(8,128)S(1)}, u32[]{:S(2)}, u32[]{:S(2)}) %collective-permute-start.3) | collective-permute-done | bytes 524320 | tf_op jit(solution)/shard_map/ppermute | solution.py:87
  35.8 10.8 %collective-permute-done.5 = f32[256,512]{1,0:T(8,128)S(1)} collective-permute-done((f32[256,512]{1,0:T(8,128)S(1)}, f32[256,512]{1,0:T(8,128)S(1)}, u32[]{:S(2)}, u32[]{:S(2)}) %collective-permute-start.5) | collective-permute-done | bytes 524320 | tf_op jit(solution)/shard_map/ppermute | solution.py:87
  56.5 3.2 %collective-permute-done.7 = f32[512,64]{0,1:T(8,128)S(1)} collective-permute-done((f32[512,64]{0,1:T(8,128)S(1)}, f32[512,64]{0,1:T(8,128)S(1)}, u32[]{:S(2)}, u32[]{:S(2)}) %collective-permute-start.7) | collective-permute-done | bytes 131104 | tf_op jit(solution)/shard_map/ppermute | solution.py:15
  62.7 1.9 %collective-permute-done.8 = f32[512,32]{0,1:T(8,128)S(1)} collective-permute-done((f32[512,32]{0,1:T(8,128)S(1)}, f32[512,32]{0,1:T(8,128)S(1)}, u32[]{:S(2)}, u32[]{:S(2)}) %collective-permute-start.8) | collective-permute-done | bytes 65568 | tf_op jit(solution)/shard_map/ppermute | solution.py:15
  65.3 1.4 collective-permute-start.9
  67.3 1.3 collective-permute-start.27
  82.5 14.0 %collective-permute-done.14 = f32[512,32]{0,1:T(8,128)S(1)} collective-permute-done((f32[512,32]{0,1:T(8,128)S(1)}, f32[512,32]{0,1:T(8,128)S(1)}, u32[]{:S(2)}, u32[]{:S(2)}) %collective-permute-start.14) | collective-permute-done | bytes 65568 | tf_op jit(solution)/shard_map/ppermute | solution.py:126
  96.9 1.9 %collective-permute-start.15 = (f32[512,32]{0,1:T(8,128)S(1)}, f32[512,32]{0,1:T(8,128)S(1)}, u32[]{:S(2)}, u32[]{:S(2)}) collective-permute-start(f32[512,32]{0,1:T(8,128)S(1)} %convolution_bitcast_fusion.3), channel_id=1, source_target_pairs={{0,16},{4,20},{8,24},{12,28},{16,0},{20,4},{24,8},{28,12},{1,17},{... | collective-permute-start | bytes 196616 | tf_op jit(solution)/shard_map/ppermute | solution.py:15
  101.6 2.2 %collective-permute-start.16 = (f32[512,64]{0,1:T(8,128)S(1)}, f32[512,64]{0,1:T(8,128)S(1)}, u32[]{:S(2)}, u32[]{:S(2)}) collective-permute-start(f32[512,64]{0,1:T(8,128)S(1)} %maximum_select_fusion.6), channel_id=1, source_target_pairs={{0,8},{4,12},{8,0},{12,4},{16,24},{20,28},{24,16},{28,20},{1,9},{5... | collective-permute-start | bytes 393224 | tf_op jit(solution)/shard_map/ppermute | solution.py:15
  103.8 1.5 collective-permute-done.32
  106.9 3.2 %collective-permute-done.33 = f32[512,32]{0,1:T(8,128)S(1)} collective-permute-done((f32[512,32]{0,1:T(8,128)S(1)}, f32[512,32]{0,1:T(8,128)S(1)}, u32[]{:S(2)}, u32[]{:S(2)}) %collective-permute-start.33) | collective-permute-done | bytes 65568 | tf_op jit(solution)/shard_map/ppermute | solution.py:15
  110.1 2.2 %collective-permute-start.34 = (f32[512,64]{0,1:T(8,128)S(1)}, f32[512,64]{0,1:T(8,128)S(1)}, u32[]{:S(2)}, u32[]{:S(2)}) collective-permute-start(f32[512,64]{0,1:T(8,128)S(1)} %maximum_select_fusion.7), channel_id=1, source_target_pairs={{0,8},{4,12},{8,0},{12,4},{16,24},{20,28},{24,16},{28,20},{1,9},{5... | collective-permute-start | bytes 393224 | tf_op jit(solution)/shard_map/ppermute | solution.py:15
  112.3 2.9 %collective-permute-done.34 = f32[512,64]{0,1:T(8,128)S(1)} collective-permute-done((f32[512,64]{0,1:T(8,128)S(1)}, f32[512,64]{0,1:T(8,128)S(1)}, u32[]{:S(2)}, u32[]{:S(2)}) %collective-permute-start.34) | collective-permute-done | bytes 131104 | tf_op jit(solution)/shard_map/ppermute | solution.py:15
  115.4 2.8 %fusion.2 = f32[1024,256]{0,1:T(8,128)S(1)} fusion(f32[512,1024]{0,1:T(8,128)} %copy-done.1, f32[512,128]{0,1:T(8,128)S(1)} %maximum_select_fusion.4, f32[512,128]{0,1:T(8,128)S(1)} %collective-permute-done.17, pred[]{:T(512)S(6)} %eq.25), kind=kOutput, calls=%fused_computation.25 | convolution fusion | flops 805699584 | bytes 3670017 | tf_op jit(solution)/shard_map/dot_general | solution.py:31
  118.2 1.8 %collective-permute-start.18 = (f32[256,256]{0,1:T(8,128)S(1)}, f32[256,256]{0,1:T(8,128)S(1)}, u32[]{:S(2)}, u32[]{:S(2)}) collective-permute-start(f32[256,256]{0,1:T(8,128)S(1)} %get-tuple-element.10), channel_id=1, source_target_pairs={{0,1},{4,5},{8,9},{12,13},{16,17},{20,21},{24,25},{28,29}} | collective-permute-start | bytes 786440 | tf_op jit(solution)/shard_map/ppermute | solution.py:107
  121.8 1.3 collective-permute-start.36
  123.8 2.8 %collective-permute-done.18 = f32[256,256]{0,1:T(8,128)S(1)} collective-permute-done((f32[256,256]{0,1:T(8,128)S(1)}, f32[256,256]{0,1:T(8,128)S(1)}, u32[]{:S(2)}, u32[]{:S(2)}) %collective-permute-start.18) | collective-permute-done | bytes 262176 | tf_op jit(solution)/shard_map/ppermute | solution.py:107
  126.7 4.4 %collective-permute-start.19 = (f32[256,256]{0,1:T(8,128)S(1)}, f32[256,256]{0,1:T(8,128)S(1)}, u32[]{:S(2)}, u32[]{:S(2)}) collective-permute-start(f32[256,256]{0,1:T(8,128)S(1)} %get-tuple-element.8), channel_id=1, source_target_pairs={{0,1},{1,2},{4,5},{5,6},{8,9},{9,10},{12,13},{13,14},{16,17},{17,1... | collective-permute-start | bytes 786440 | tf_op jit(solution)/shard_map/ppermute | solution.py:107
  132.3 4.4 %collective-permute-start.37 = (f32[256,256]{0,1:T(8,128)S(1)}, f32[256,256]{0,1:T(8,128)S(1)}, u32[]{:S(2)}, u32[]{:S(2)}) collective-permute-start(f32[256,256]{0,1:T(8,128)S(1)} %get-tuple-element.16), channel_id=1, source_target_pairs={{0,1},{1,2},{4,5},{5,6},{8,9},{9,10},{12,13},{13,14},{16,17},{17,1... | collective-permute-start | bytes 786440 | tf_op jit(solution)/shard_map/ppermute | solution.py:107
  138.0 4.4 %collective-permute-start.20 = (f32[256,256]{0,1:T(8,128)S(1)}, f32[256,256]{0,1:T(8,128)S(1)}, u32[]{:S(2)}, u32[]{:S(2)}) collective-permute-start(f32[256,256]{0,1:T(8,128)S(1)} %get-tuple-element.6), channel_id=1, source_target_pairs={{0,1},{1,2},{2,3},{4,5},{5,6},{6,7},{8,9},{9,10},{10,11},{12,13},{... | collective-permute-start | bytes 786440 | tf_op jit(solution)/shard_map/ppermute | solution.py:107
  143.8 4.6 %collective-permute-start.38 = (f32[256,256]{0,1:T(8,128)S(1)}, f32[256,256]{0,1:T(8,128)S(1)}, u32[]{:S(2)}, u32[]{:S(2)}) collective-permute-start(f32[256,256]{0,1:T(8,128)S(1)} %get-tuple-element.14), channel_id=1, source_target_pairs={{0,1},{1,2},{2,3},{4,5},{5,6},{6,7},{8,9},{9,10},{10,11},{12,13},{... | collective-permute-start | bytes 786440 | tf_op jit(solution)/shard_map/ppermute | solution.py:107
  149.7 1.5 collective-permute-done.23
  151.3 2.9 %collective-permute-done.38 = f32[256,256]{0,1:T(8,128)S(1)} collective-permute-done((f32[256,256]{0,1:T(8,128)S(1)}, f32[256,256]{0,1:T(8,128)S(1)}, u32[]{:S(2)}, u32[]{:S(2)}) %collective-permute-start.38) | collective-permute-done | bytes 262176 | tf_op jit(solution)/shard_map/ppermute | solution.py:107
  154.2 2.7 %collective-permute-done.41 = f32[256,256]{0,1:T(8,128)S(1)} collective-permute-done((f32[256,256]{0,1:T(8,128)S(1)}, f32[256,256]{0,1:T(8,128)S(1)}, u32[]{:S(2)}, u32[]{:S(2)}) %collective-permute-start.41) | collective-permute-done | bytes 262176 | tf_op jit(solution)/shard_map/ppermute | solution.py:108
  (127 shorter events, 46.6 us)
Async XLA Ops:
  0.0 17.3 %collective-permute-start.1 = (f32[256,512]{1,0:T(8,128)}, f32[256,512]{1,0:T(8,128)}, u32[]{:S(2)}, u32[]{:S(2)}) collective-permute-start(f32[256,512]{1,0:T(8,128)} %param.6), channel_id=1, source_target_pairs={{1,0},{2,1},{3,2},{5,4},{6,5},{7,6},{9,8},{10,9},{11,10},{13,12},{... | collective-permute-start | bytes 1572872 | tf_op jit(solution)/shard_map/ppermute | solution.py:87
  1.4 17.2 %collective-permute-start = (f32[256,512]{1,0:T(8,128)}, f32[256,512]{1,0:T(8,128)}, u32[]{:S(2)}, u32[]{:S(2)}) collective-permute-start(f32[256,512]{1,0:T(8,128)} %param.6), channel_id=1, source_target_pairs={{0,1},{1,2},{2,3},{4,5},{5,6},{6,7},{8,9},{9,10},{10,11},{12,13},{... | collective-permute-start | bytes 1572872 | tf_op jit(solution)/shard_map/ppermute | solution.py:86
  17.3 15.2 %collective-permute-start.3 = (f32[256,512]{1,0:T(8,128)}, f32[256,512]{1,0:T(8,128)S(1)}, u32[]{:S(2)}, u32[]{:S(2)}) collective-permute-start(f32[256,512]{1,0:T(8,128)} %collective-permute-done.1), channel_id=1, source_target_pairs={{1,0},{2,1},{5,4},{6,5},{9,8},{10,9},{13,12},{14,13},{17,16},{18,1... | collective-permute-start | bytes 1572872 | tf_op jit(solution)/shard_map/ppermute | solution.py:87
  18.6 15.2 %collective-permute-start.2 = (f32[256,512]{1,0:T(8,128)}, f32[256,512]{1,0:T(8,128)S(1)}, u32[]{:S(2)}, u32[]{:S(2)}) collective-permute-start(f32[256,512]{1,0:T(8,128)} %collective-permute-done), channel_id=1, source_target_pairs={{1,2},{2,3},{5,6},{6,7},{9,10},{10,11},{13,14},{14,15},{17,18},{18... | collective-permute-start | bytes 1572872 | tf_op jit(solution)/shard_map/ppermute | solution.py:86
  32.5 14.1 %collective-permute-start.5 = (f32[256,512]{1,0:T(8,128)S(1)}, f32[256,512]{1,0:T(8,128)S(1)}, u32[]{:S(2)}, u32[]{:S(2)}) collective-permute-start(f32[256,512]{1,0:T(8,128)S(1)} %collective-permute-done.3), channel_id=1, source_target_pairs={{1,0},{5,4},{9,8},{13,12},{17,16},{21,20},{25,24},{29,28}} | collective-permute-start | bytes 1572872 | tf_op jit(solution)/shard_map/ppermute | solution.py:87
  33.8 13.4 %collective-permute-start.4 = (f32[256,512]{1,0:T(8,128)S(1)}, f32[256,512]{1,0:T(8,128)S(1)}, u32[]{:S(2)}, u32[]{:S(2)}) collective-permute-start(f32[256,512]{1,0:T(8,128)S(1)} %collective-permute-done.2), channel_id=1, source_target_pairs={{2,3},{6,7},{10,11},{14,15},{18,19},{22,23},{26,27},{30,31}} | collective-permute-start | bytes 1572872 | tf_op jit(solution)/shard_map/ppermute | solution.py:86
  53.3 6.4 %collective-permute-start.7 = (f32[512,64]{0,1:T(8,128)S(1)}, f32[512,64]{0,1:T(8,128)S(1)}, u32[]{:S(2)}, u32[]{:S(2)}) collective-permute-start(f32[512,64]{0,1:T(8,128)S(1)} %constant_dynamic-slice_fusion.8), channel_id=1, source_target_pairs={{0,8},{4,12},{8,0},{12,4},{16,24},{20,28},{24,16},{28,20},{1,9},{5... | collective-permute-start | bytes 393224 | tf_op jit(solution)/shard_map/ppermute | solution.py:15
  55.4 6.2 %collective-permute-start.25 = (f32[512,64]{0,1:T(8,128)S(1)}, f32[512,64]{0,1:T(8,128)S(1)}, u32[]{:S(2)}, u32[]{:S(2)}) collective-permute-start(f32[512,64]{0,1:T(8,128)S(1)} %constant_dynamic-slice_fusion.3), channel_id=1, source_target_pairs={{0,8},{4,12},{8,0},{12,4},{16,24},{20,28},{24,16},{28,20},{1,9},{5... | collective-permute-start | bytes 393224 | tf_op jit(solution)/shard_map/ppermute | solution.py:15
  59.8 4.9 %collective-permute-start.8 = (f32[512,32]{0,1:T(8,128)S(1)}, f32[512,32]{0,1:T(8,128)S(1)}, u32[]{:S(2)}, u32[]{:S(2)}) collective-permute-start(f32[512,32]{0,1:T(8,128)S(1)} %constant_dynamic-slice_fusion.7), channel_id=1, source_target_pairs={{0,16},{4,20},{8,24},{12,28},{16,0},{20,4},{24,8},{28,12},{1,17},{... | collective-permute-start | bytes 196616 | tf_op jit(solution)/shard_map/ppermute | solution.py:15
  61.6 5.1 %collective-permute-start.26 = (f32[512,32]{0,1:T(8,128)S(1)}, f32[512,32]{0,1:T(8,128)S(1)}, u32[]{:S(2)}, u32[]{:S(2)}) collective-permute-start(f32[512,32]{0,1:T(8,128)S(1)} %constant_dynamic-slice_fusion.2), channel_id=1, source_target_pairs={{0,16},{4,20},{8,24},{12,28},{16,0},{20,4},{24,8},{28,12},{1,17},{... | collective-permute-start | bytes 196616 | tf_op jit(solution)/shard_map/ppermute | solution.py:15
  65.3 3.3 %collective-permute-start.9 = (f32[512,32]{0,1:T(8,128)S(1)}, f32[512,32]{0,1:T(8,128)S(1)}, u32[]{:S(2)}, u32[]{:S(2)}) collective-permute-start(f32[512,32]{0,1:T(8,128)S(1)} %convolution_bitcast_fusion.5), channel_id=1, source_target_pairs={{0,1},{4,5},{8,9},{12,13},{16,17},{20,21},{24,25},{28,29}} | collective-permute-start | bytes 196616 | tf_op jit(solution)/shard_map/ppermute | solution.py:118
  67.3 3.2 %collective-permute-start.27 = (f32[512,32]{0,1:T(8,128)S(1)}, f32[512,32]{0,1:T(8,128)S(1)}, u32[]{:S(2)}, u32[]{:S(2)}) collective-permute-start(f32[512,32]{0,1:T(8,128)S(1)} %convolution_bitcast_fusion.2), channel_id=1, source_target_pairs={{0,1},{4,5},{8,9},{12,13},{16,17},{20,21},{24,25},{28,29}} | collective-permute-start | bytes 196616 | tf_op jit(solution)/shard_map/ppermute | solution.py:118
  81.2 15.3 %collective-permute-start.14 = (f32[512,32]{0,1:T(8,128)S(1)}, f32[512,32]{0,1:T(8,128)S(1)}, u32[]{:S(2)}, u32[]{:S(2)}) collective-permute-start(f32[512,32]{0,1:T(8,128)S(1)} %convolution_add_fusion.9), channel_id=1, source_target_pairs={{1,0},{5,4},{9,8},{13,12},{17,16},{21,20},{25,24},{29,28}} | collective-permute-start | bytes 196616 | tf_op jit(solution)/shard_map/ppermute | solution.py:126
  96.9 4.7 %collective-permute-start.15 = (f32[512,32]{0,1:T(8,128)S(1)}, f32[512,32]{0,1:T(8,128)S(1)}, u32[]{:S(2)}, u32[]{:S(2)}) collective-permute-start(f32[512,32]{0,1:T(8,128)S(1)} %convolution_bitcast_fusion.3), channel_id=1, source_target_pairs={{0,16},{4,20},{8,24},{12,28},{16,0},{20,4},{24,8},{28,12},{1,17},{... | collective-permute-start | bytes 196616 | tf_op jit(solution)/shard_map/ppermute | solution.py:15
  99.2 6.2 %collective-permute-start.32 = (f32[512,32]{0,1:T(8,128)S(1)}, f32[512,32]{0,1:T(8,128)S(1)}, u32[]{:S(2)}, u32[]{:S(2)}) collective-permute-start(f32[512,32]{0,1:T(8,128)S(1)} %convolution_add_fusion.4), channel_id=1, source_target_pairs={{1,0},{5,4},{9,8},{13,12},{17,16},{21,20},{25,24},{29,28}} | collective-permute-start | bytes 196616 | tf_op jit(solution)/shard_map/ppermute | solution.py:126
  101.6 5.2 %collective-permute-start.16 = (f32[512,64]{0,1:T(8,128)S(1)}, f32[512,64]{0,1:T(8,128)S(1)}, u32[]{:S(2)}, u32[]{:S(2)}) collective-permute-start(f32[512,64]{0,1:T(8,128)S(1)} %maximum_select_fusion.6), channel_id=1, source_target_pairs={{0,8},{4,12},{8,0},{12,4},{16,24},{20,28},{24,16},{28,20},{1,9},{5... | collective-permute-start | bytes 393224 | tf_op jit(solution)/shard_map/ppermute | solution.py:15
  105.7 4.3 %collective-permute-start.33 = (f32[512,32]{0,1:T(8,128)S(1)}, f32[512,32]{0,1:T(8,128)S(1)}, u32[]{:S(2)}, u32[]{:S(2)}) collective-permute-start(f32[512,32]{0,1:T(8,128)S(1)} %convolution_bitcast_fusion), channel_id=1, source_target_pairs={{0,16},{4,20},{8,24},{12,28},{16,0},{20,4},{24,8},{28,12},{1,17},{... | collective-permute-start | bytes 196616 | tf_op jit(solution)/shard_map/ppermute | solution.py:15
  106.8 8.6 %collective-permute-start.17 = (f32[512,128]{0,1:T(8,128)S(1)}, f32[512,128]{0,1:T(8,128)S(1)}, u32[]{:S(2)}, u32[]{:S(2)}) collective-permute-start(f32[512,128]{0,1:T(8,128)S(1)} %maximum_select_fusion.4), channel_id=1, source_target_pairs={{0,4},{4,0},{8,12},{12,8},{16,20},{20,16},{24,28},{28,24},{1,5},{5... | collective-permute-start | bytes 786440 | tf_op jit(solution)/shard_map/ppermute | solution.py:15
  110.1 5.2 %collective-permute-start.34 = (f32[512,64]{0,1:T(8,128)S(1)}, f32[512,64]{0,1:T(8,128)S(1)}, u32[]{:S(2)}, u32[]{:S(2)}) collective-permute-start(f32[512,64]{0,1:T(8,128)S(1)} %maximum_select_fusion.7), channel_id=1, source_target_pairs={{0,8},{4,12},{8,0},{12,4},{16,24},{20,28},{24,16},{28,20},{1,9},{5... | collective-permute-start | bytes 393224 | tf_op jit(solution)/shard_map/ppermute | solution.py:15
  115.3 5.4 %collective-permute-start.35 = (f32[512,128]{0,1:T(8,128)S(1)}, f32[512,128]{0,1:T(8,128)S(1)}, u32[]{:S(2)}, u32[]{:S(2)}) collective-permute-start(f32[512,128]{0,1:T(8,128)S(1)} %maximum_select_fusion.5), channel_id=1, source_target_pairs={{0,4},{4,0},{8,12},{12,8},{16,20},{20,16},{24,28},{28,24},{1,5},{5... | collective-permute-start | bytes 786440 | tf_op jit(solution)/shard_map/ppermute | solution.py:15
  118.2 8.4 %collective-permute-start.18 = (f32[256,256]{0,1:T(8,128)S(1)}, f32[256,256]{0,1:T(8,128)S(1)}, u32[]{:S(2)}, u32[]{:S(2)}) collective-permute-start(f32[256,256]{0,1:T(8,128)S(1)} %get-tuple-element.10), channel_id=1, source_target_pairs={{0,1},{4,5},{8,9},{12,13},{16,17},{20,21},{24,25},{28,29}} | collective-permute-start | bytes 786440 | tf_op jit(solution)/shard_map/ppermute | solution.py:107
  120.0 6.6 %collective-permute-start.21 = (f32[256,256]{0,1:T(8,128)S(1)}, f32[256,256]{0,1:T(8,128)S(1)}, u32[]{:S(2)}, u32[]{:S(2)}) collective-permute-start(f32[256,256]{0,1:T(8,128)S(1)} %get-tuple-element.9), channel_id=1, source_target_pairs={{3,2},{7,6},{11,10},{15,14},{19,18},{23,22},{27,26},{31,30}} | collective-permute-start | bytes 786440 | tf_op jit(solution)/shard_map/ppermute | solution.py:108
  121.8 10.4 %collective-permute-start.36 = (f32[256,256]{0,1:T(8,128)S(1)}, f32[256,256]{0,1:T(8,128)S(1)}, u32[]{:S(2)}, u32[]{:S(2)}) collective-permute-start(f32[256,256]{0,1:T(8,128)S(1)} %get-tuple-element.18), channel_id=1, source_target_pairs={{0,1},{4,5},{8,9},{12,13},{16,17},{20,21},{24,25},{28,29}} | collective-permute-start | bytes 786440 | tf_op jit(solution)/shard_map/ppermute | solution.py:107
  123.1 9.1 %collective-permute-start.39 = (f32[256,256]{0,1:T(8,128)S(1)}, f32[256,256]{0,1:T(8,128)S(1)}, u32[]{:S(2)}, u32[]{:S(2)}) collective-permute-start(f32[256,256]{0,1:T(8,128)S(1)} %get-tuple-element.17), channel_id=1, source_target_pairs={{3,2},{7,6},{11,10},{15,14},{19,18},{23,22},{27,26},{31,30}} | collective-permute-start | bytes 786440 | tf_op jit(solution)/shard_map/ppermute | solution.py:108
  126.7 11.1 %collective-permute-start.19 = (f32[256,256]{0,1:T(8,128)S(1)}, f32[256,256]{0,1:T(8,128)S(1)}, u32[]{:S(2)}, u32[]{:S(2)}) collective-permute-start(f32[256,256]{0,1:T(8,128)S(1)} %get-tuple-element.8), channel_id=1, source_target_pairs={{0,1},{1,2},{4,5},{5,6},{8,9},{9,10},{12,13},{13,14},{16,17},{17,1... | collective-permute-start | bytes 786440 | tf_op jit(solution)/shard_map/ppermute | solution.py:107
  131.1 6.7 %collective-permute-start.22 = (f32[256,256]{0,1:T(8,128)S(1)}, f32[256,256]{0,1:T(8,128)S(1)}, u32[]{:S(2)}, u32[]{:S(2)}) collective-permute-start(f32[256,256]{0,1:T(8,128)S(1)} %get-tuple-element.7), channel_id=1, source_target_pairs={{2,1},{3,2},{6,5},{7,6},{10,9},{11,10},{14,13},{15,14},{18,17},{19... | collective-permute-start | bytes 786440 | tf_op jit(solution)/shard_map/ppermute | solution.py:108
  132.3 11.4 %collective-permute-start.37 = (f32[256,256]{0,1:T(8,128)S(1)}, f32[256,256]{0,1:T(8,128)S(1)}, u32[]{:S(2)}, u32[]{:S(2)}) collective-permute-start(f32[256,256]{0,1:T(8,128)S(1)} %get-tuple-element.16), channel_id=1, source_target_pairs={{0,1},{1,2},{4,5},{5,6},{8,9},{9,10},{12,13},{13,14},{16,17},{17,1... | collective-permute-start | bytes 786440 | tf_op jit(solution)/shard_map/ppermute | solution.py:107
  136.8 6.9 %collective-permute-start.40 = (f32[256,256]{0,1:T(8,128)S(1)}, f32[256,256]{0,1:T(8,128)S(1)}, u32[]{:S(2)}, u32[]{:S(2)}) collective-permute-start(f32[256,256]{0,1:T(8,128)S(1)} %get-tuple-element.15), channel_id=1, source_target_pairs={{2,1},{3,2},{6,5},{7,6},{10,9},{11,10},{14,13},{15,14},{18,17},{19... | collective-permute-start | bytes 786440 | tf_op jit(solution)/shard_map/ppermute | solution.py:108
  138.0 11.7 %collective-permute-start.20 = (f32[256,256]{0,1:T(8,128)S(1)}, f32[256,256]{0,1:T(8,128)S(1)}, u32[]{:S(2)}, u32[]{:S(2)}) collective-permute-start(f32[256,256]{0,1:T(8,128)S(1)} %get-tuple-element.6), channel_id=1, source_target_pairs={{0,1},{1,2},{2,3},{4,5},{5,6},{6,7},{8,9},{9,10},{10,11},{12,13},{... | collective-permute-start | bytes 786440 | tf_op jit(solution)/shard_map/ppermute | solution.py:107
  142.4 8.8 %collective-permute-start.23 = (f32[256,256]{0,1:T(8,128)S(1)}, f32[256,256]{0,1:T(8,128)S(1)}, u32[]{:S(2)}, u32[]{:S(2)}) collective-permute-start(f32[256,256]{0,1:T(8,128)S(1)} %get-tuple-element.5), channel_id=1, source_target_pairs={{1,0},{2,1},{3,2},{5,4},{6,5},{7,6},{9,8},{10,9},{11,10},{13,12},{... | collective-permute-start | bytes 786440 | tf_op jit(solution)/shard_map/ppermute | solution.py:108
  143.8 10.3 %collective-permute-start.38 = (f32[256,256]{0,1:T(8,128)S(1)}, f32[256,256]{0,1:T(8,128)S(1)}, u32[]{:S(2)}, u32[]{:S(2)}) collective-permute-start(f32[256,256]{0,1:T(8,128)S(1)} %get-tuple-element.14), channel_id=1, source_target_pairs={{0,1},{1,2},{2,3},{4,5},{5,6},{6,7},{8,9},{9,10},{10,11},{12,13},{... | collective-permute-start | bytes 786440 | tf_op jit(solution)/shard_map/ppermute | solution.py:107
  148.4 8.4 %collective-permute-start.41 = (f32[256,256]{0,1:T(8,128)S(1)}, f32[256,256]{0,1:T(8,128)S(1)}, u32[]{:S(2)}, u32[]{:S(2)}) collective-permute-start(f32[256,256]{0,1:T(8,128)S(1)} %get-tuple-element.13), channel_id=1, source_target_pairs={{1,0},{2,1},{3,2},{5,4},{6,5},{7,6},{9,8},{10,9},{11,10},{13,12},{... | collective-permute-start | bytes 786440 | tf_op jit(solution)/shard_map/ppermute | solution.py:108
  (16 other events, 118.4 us)

commit v22 on v17

--- a/solution.py
+++ b/solution.py
@@ -60,12 +60,11 @@
     bit = count // 2
     while bit >= 1:
         other = swap(current, axis, bit)
-        upper = (index // bit) % 2 == 1
-        current = jnp.where(
-            upper,
-            jnp.concatenate([other, current], axis=1),
-            jnp.concatenate([current, other], axis=1),
-        )
+        upper = (index // bit) % 2
+        width = current.shape[1]
+        joined = jnp.zeros((current.shape[0], 2 * width), current.dtype)
+        joined = lax.dynamic_update_slice_in_dim(joined, current, upper * width, axis=1)
+        current = lax.dynamic_update_slice_in_dim(joined, other, (1 - upper) * width, axis=1)
         bit //= 2
     return current
 

time: 154 us -> 151 us (0.981)
  waiting for transfers between devices: 67.2 us -> 58.4 us
  local copies, waits for them, and re-layouts: 4.24 us -> 8.56 us
    ppermute x12, waiting for transfers between devices: 15.3 us -> 10.1 us  [swap(): return lax.ppermute(array, axis, [(i, i ^ bit) for i in range(count)])]
    dynamic_update_slice x0 -> x9, local copies, waits for them, and re-layouts: none -> 3.45 us  [the longest x5 1.77 us: all_gather_columns(): lax.dynamic_update_slice_in_dim(joined, other, (1 - upper) * width, axis=1)]
    ppermute x6, waiting for transfers between devices: 17 us -> 13.6 us  [solve(): arriving = arriving + lax.ppermute(value, 'aux', [(sender, sender - 1)])]
  transfers between devices with their start and end apart: 42 -> 42, of which waited for: 20 -> 20; matrix products, arithmetic and copies ran while one was open for 16% -> 18% of each run, Pallas kernels for 0% -> 0%
where the time goes in v22:
time: 151 us; the launch traced here: 150 us
  starting transfers between devices  60 us (40%)
  waiting for transfers between devices  58.4 us (39%)
  matrix products  19.1 us (13%)
  local copies, waits for them, and re-layouts  8.56 us (6%)
  other arithmetic  2.76 us (2%)
    ppermute x3, waiting for transfers between devices, gamma_over_aux(): from_right = lax.ppermute(from_right, 'aux', leftward)  23.4 us
    ppermute x6, starting transfers between devices, reduce_over_aux(): lax.ppermute(to_right + block(index + count - 1 - step), 'aux', rightward)  20.8 us
    dot_general x26, matrix products, product(): jnp.dot(left, right, precision=lax.Precision.HIGH, preferred_element_type...  17 us
    ppermute x6, waiting for transfers between devices, solve(): arriving = arriving + lax.ppermute(value, 'aux', [(sender, sender - 1)])  13.6 us
    ppermute x12, starting transfers between devices, swap(): return lax.ppermute(array, axis, [(i, i ^ bit) for i in range(count)])  11.3 us
    ppermute x12, waiting for transfers between devices, swap(): return lax.ppermute(array, axis, [(i, i ^ bit) for i in range(count)])  10.1 us
    ppermute x3, starting transfers between devices, gamma_over_aux(): from_left = lax.ppermute(from_left, 'aux', rightward)  7.74 us
    ppermute x6, waiting for transfers between devices, reduce_over_aux(): lax.ppermute(to_right + block(index + count - 1 - step), 'aux', rightward)  6.86 us
  transfers between devices with their start and end apart: 42, of which 20 were waited for; matrix products, arithmetic and copies ran while one was open for 18% of the time, Pallas kernels for 0%

profile of v22, /device:TPU:0, one launch (start us, length us, event | category | flops | bytes accessed | tf_op | source)
XLA Modules:
  0.0 149.6 jit_solution(14294197100121301563)
XLA Ops:
  0.0 1.4 collective-permute-start.1
  1.4 6.4 %collective-permute-start = (f32[256,512]{1,0:T(8,128)}, f32[256,512]{1,0:T(8,128)}, u32[]{:S(2)}, u32[]{:S(2)}) collective-permute-start(f32[256,512]{1,0:T(8,128)} %param.6), channel_id=1, source_target_pairs={{0,1},{1,2},{2,3},{4,5},{5,6},{6,7},{8,9},{9,10},{10,11},{12,13},{... | collective-permute-start | bytes 1572872 | tf_op jit(solution)/shard_map/ppermute | solution.py:86
  7.8 2.9 %copy.8 = f32[512,1024]{0,1:T(8,128)} copy(f32[512,1024]{1,0:T(8,128)} %param.5) | data formatting | bytes 4194304 | tf_op args[0]
  10.9 1.8 %bitcast_multiply_fusion = f32[512,1024]{0,1:T(8,128)S(1)} fusion(f32[512,1024]{0,1:T(8,128)} %copy.8, f32[512,16]{0,1:T(8,128)S(1)} %reshape.6), kind=kLoop, calls=%fused_computation | loop fusion | flops 524288 | bytes 4227072 | tf_op jit(solution)/shard_map/mul | solution.py:23
  12.8 1.7 %fusion.10 = f32[512,512]{0,1:T(8,128)S(1)} fusion(f32[256,512]{1,0:T(8,128)} %param.6, f32[512,1024]{0,1:T(8,128)S(1)} %bitcast_multiply_fusion, s32[]{:T(128)S(6)} %select_n.177), kind=kOutput, calls=%fused_computation.33 | convolution fusion | flops 402653184 | bytes 2097156 | tf_op jit(solution)/shard_map/dot_general | solution.py:27
  14.5 2.8 %collective-permute-done.1 = f32[256,512]{1,0:T(8,128)} collective-permute-done((f32[256,512]{1,0:T(8,128)}, f32[256,512]{1,0:T(8,128)}, u32[]{:S(2)}, u32[]{:S(2)}) %collective-permute-start.1) | collective-permute-done | bytes 524320 | tf_op jit(solution)/shard_map/ppermute | solution.py:87
  19.3 1.7 %convolution_add_fusion.3 = f32[512,512]{0,1:T(8,128)S(1)} fusion(f32[512,512]{0,1:T(8,128)S(1)} %fusion.10, f32[256,512]{1,0:T(8,128)} %collective-permute-done, f32[512,1024]{0,1:T(8,128)S(1)} %bitcast_multiply_fusion, s32[]{:T(128)S(6)} %select_n.178), kind=kOutput, calls=%fused_computation.6 | convolution fusion | flops 402915328 | bytes 3145732 | tf_op jit(solution)/shard_map/dot_general | solution.py:27
  21.0 1.7 %convolution_add_fusion.2 = f32[512,512]{0,1:T(8,128)S(1)} fusion(f32[512,512]{0,1:T(8,128)S(1)} %convolution_add_fusion.3, f32[256,512]{1,0:T(8,128)} %collective-permute-done.1, f32[512,1024]{0,1:T(8,128)S(1)} %bitcast_multiply_fusion, s32[]{:T(128)S(6)} %select_n.179), kind=kOutput, calls=%fused_computation.5 | convolution fusion | flops 402915328 | bytes 3145732 | tf_op jit(solution)/shard_map/dot_general | solution.py:27
  22.6 9.8 %collective-permute-done.3 = f32[256,512]{1,0:T(8,128)S(1)} collective-permute-done((f32[256,512]{1,0:T(8,128)}, f32[256,512]{1,0:T(8,128)S(1)}, u32[]{:S(2)}, u32[]{:S(2)}) %collective-permute-start.3) | collective-permute-done | bytes 524320 | tf_op jit(solution)/shard_map/ppermute | solution.py:87
  35.8 10.8 %collective-permute-done.5 = f32[256,512]{1,0:T(8,128)S(1)} collective-permute-done((f32[256,512]{1,0:T(8,128)S(1)}, f32[256,512]{1,0:T(8,128)S(1)}, u32[]{:S(2)}, u32[]{:S(2)}) %collective-permute-start.5) | collective-permute-done | bytes 524320 | tf_op jit(solution)/shard_map/ppermute | solution.py:87
  52.3 4.2 %collective-permute-done.7 = f32[512,64]{0,1:T(8,128)S(1)} collective-permute-done((f32[512,64]{0,1:T(8,128)S(1)}, f32[512,64]{0,1:T(8,128)S(1)}, u32[]{:S(2)}, u32[]{:S(2)}) %collective-permute-start.7) | collective-permute-done | bytes 131104 | tf_op jit(solution)/shard_map/ppermute | solution.py:15
  59.7 1.7 %collective-permute-done.8 = f32[512,32]{0,1:T(8,128)S(1)} collective-permute-done((f32[512,32]{0,1:T(8,128)S(1)}, f32[512,32]{0,1:T(8,128)S(1)}, u32[]{:S(2)}, u32[]{:S(2)}) %collective-permute-start.8) | collective-permute-done | bytes 65568 | tf_op jit(solution)/shard_map/ppermute | solution.py:15
  61.9 1.4 collective-permute-start.9
  64.0 1.3 collective-permute-start.27
  77.8 1.3 collective-permute-start.14
  79.6 1.3 collective-permute-start.32
  80.9 13.1 %collective-permute-done.14 = f32[512,32]{0,1:T(8,128)S(1)} collective-permute-done((f32[512,32]{0,1:T(8,128)S(1)}, f32[512,32]{0,1:T(8,128)S(1)}, u32[]{:S(2)}, u32[]{:S(2)}) %collective-permute-start.14) | collective-permute-done | bytes 65568 | tf_op jit(solution)/shard_map/ppermute | solution.py:126
  94.4 1.6 %collective-permute-start.15 = (f32[512,32]{0,1:T(8,128)S(1)}, f32[512,32]{0,1:T(8,128)S(1)}, u32[]{:S(2)}, u32[]{:S(2)}) collective-permute-start(f32[512,32]{0,1:T(8,128)S(1)} %get-tuple-element.24), channel_id=1, source_target_pairs={{0,16},{4,20},{8,24},{12,28},{16,0},{20,4},{24,8},{28,12},{1,17},{... | collective-permute-start | bytes 196616 | tf_op jit(solution)/shard_map/ppermute | solution.py:15
  96.9 1.6 %collective-permute-start.33 = (f32[512,32]{0,1:T(8,128)S(1)}, f32[512,32]{0,1:T(8,128)S(1)}, u32[]{:S(2)}, u32[]{:S(2)}) collective-permute-start(f32[512,32]{0,1:T(8,128)S(1)} %get-tuple-element.22), channel_id=1, source_target_pairs={{0,16},{4,20},{8,24},{12,28},{16,0},{20,4},{24,8},{28,12},{1,17},{... | collective-permute-start | bytes 196616 | tf_op jit(solution)/shard_map/ppermute | solution.py:15
  98.7 1.6 %collective-permute-start.16 = (f32[512,64]{0,1:T(8,128)S(1)}, f32[512,64]{0,1:T(8,128)S(1)}, u32[]{:S(2)}, u32[]{:S(2)}) collective-permute-start(f32[512,64]{0,1:T(8,128)S(1)} %constant_dynamic-update-slice_fusion.10), channel_id=1, source_target_pairs={{0,8},{4,12},{8,0},{12,4},{16,24},{20,28},{24,16},{28,20},{1,9},{5... | collective-permute-start | bytes 393224 | tf_op jit(solution)/shard_map/ppermute | solution.py:15
  101.2 1.6 %collective-permute-start.34 = (f32[512,64]{0,1:T(8,128)S(1)}, f32[512,64]{0,1:T(8,128)S(1)}, u32[]{:S(2)}, u32[]{:S(2)}) collective-permute-start(f32[512,64]{0,1:T(8,128)S(1)} %constant_dynamic-update-slice_fusion.4), channel_id=1, source_target_pairs={{0,8},{4,12},{8,0},{12,4},{16,24},{20,28},{24,16},{28,20},{1,9},{5... | collective-permute-start | bytes 393224 | tf_op jit(solution)/shard_map/ppermute | solution.py:15
  104.9 1.3 collective-permute-done.34
  110.1 1.7 %collective-permute-start.18 = (f32[256,256]{0,1:T(8,128)S(1)}, f32[256,256]{0,1:T(8,128)S(1)}, u32[]{:S(2)}, u32[]{:S(2)}) collective-permute-start(f32[256,256]{0,1:T(8,128)S(1)} %get-tuple-element.10), channel_id=1, source_target_pairs={{0,1},{4,5},{8,9},{12,13},{16,17},{20,21},{24,25},{28,29}} | collective-permute-start | bytes 786440 | tf_op jit(solution)/shard_map/ppermute | solution.py:107
  113.6 1.3 collective-permute-start.36
  115.6 2.9 %collective-permute-done.18 = f32[256,256]{0,1:T(8,128)S(1)} collective-permute-done((f32[256,256]{0,1:T(8,128)S(1)}, f32[256,256]{0,1:T(8,128)S(1)}, u32[]{:S(2)}, u32[]{:S(2)}) %collective-permute-start.18) | collective-permute-done | bytes 262176 | tf_op jit(solution)/shard_map/ppermute | solution.py:107
  118.6 4.4 %collective-permute-start.19 = (f32[256,256]{0,1:T(8,128)S(1)}, f32[256,256]{0,1:T(8,128)S(1)}, u32[]{:S(2)}, u32[]{:S(2)}) collective-permute-start(f32[256,256]{0,1:T(8,128)S(1)} %get-tuple-element.8), channel_id=1, source_target_pairs={{0,1},{1,2},{4,5},{5,6},{8,9},{9,10},{12,13},{13,14},{16,17},{17,1... | collective-permute-start | bytes 786440 | tf_op jit(solution)/shard_map/ppermute | solution.py:107
  124.2 4.4 %collective-permute-start.37 = (f32[256,256]{0,1:T(8,128)S(1)}, f32[256,256]{0,1:T(8,128)S(1)}, u32[]{:S(2)}, u32[]{:S(2)}) collective-permute-start(f32[256,256]{0,1:T(8,128)S(1)} %get-tuple-element.18), channel_id=1, source_target_pairs={{0,1},{1,2},{4,5},{5,6},{8,9},{9,10},{12,13},{13,14},{16,17},{17,1... | collective-permute-start | bytes 786440 | tf_op jit(solution)/shard_map/ppermute | solution.py:107
  129.8 4.4 %collective-permute-start.20 = (f32[256,256]{0,1:T(8,128)S(1)}, f32[256,256]{0,1:T(8,128)S(1)}, u32[]{:S(2)}, u32[]{:S(2)}) collective-permute-start(f32[256,256]{0,1:T(8,128)S(1)} %get-tuple-element.6), channel_id=1, source_target_pairs={{0,1},{1,2},{2,3},{4,5},{5,6},{6,7},{8,9},{9,10},{10,11},{12,13},{... | collective-permute-start | bytes 786440 | tf_op jit(solution)/shard_map/ppermute | solution.py:107
  135.7 4.6 %collective-permute-start.38 = (f32[256,256]{0,1:T(8,128)S(1)}, f32[256,256]{0,1:T(8,128)S(1)}, u32[]{:S(2)}, u32[]{:S(2)}) collective-permute-start(f32[256,256]{0,1:T(8,128)S(1)} %get-tuple-element.16), channel_id=1, source_target_pairs={{0,1},{1,2},{2,3},{4,5},{5,6},{6,7},{8,9},{9,10},{10,11},{12,13},{... | collective-permute-start | bytes 786440 | tf_op jit(solution)/shard_map/ppermute | solution.py:107
  140.3 1.3 collective-permute-start.41
  142.6 3.1 %collective-permute-done.38 = f32[256,256]{0,1:T(8,128)S(1)} collective-permute-done((f32[256,256]{0,1:T(8,128)S(1)}, f32[256,256]{0,1:T(8,128)S(1)}, u32[]{:S(2)}, u32[]{:S(2)}) %collective-permute-start.38) | collective-permute-done | bytes 262176 | tf_op jit(solution)/shard_map/ppermute | solution.py:107
  145.8 2.7 %collective-permute-done.41 = f32[256,256]{0,1:T(8,128)S(1)} collective-permute-done((f32[256,256]{0,1:T(8,128)S(1)}, f32[256,256]{0,1:T(8,128)S(1)}, u32[]{:S(2)}, u32[]{:S(2)}) %collective-permute-start.41) | collective-permute-done | bytes 262176 | tf_op jit(solution)/shard_map/ppermute | solution.py:108
  (129 shorter events, 45.0 us)
Async XLA Ops:
  0.0 17.3 %collective-permute-start.1 = (f32[256,512]{1,0:T(8,128)}, f32[256,512]{1,0:T(8,128)}, u32[]{:S(2)}, u32[]{:S(2)}) collective-permute-start(f32[256,512]{1,0:T(8,128)} %param.6), channel_id=1, source_target_pairs={{1,0},{2,1},{3,2},{5,4},{6,5},{7,6},{9,8},{10,9},{11,10},{13,12},{... | collective-permute-start | bytes 1572872 | tf_op jit(solution)/shard_map/ppermute | solution.py:87
  1.4 17.2 %collective-permute-start = (f32[256,512]{1,0:T(8,128)}, f32[256,512]{1,0:T(8,128)}, u32[]{:S(2)}, u32[]{:S(2)}) collective-permute-start(f32[256,512]{1,0:T(8,128)} %param.6), channel_id=1, source_target_pairs={{0,1},{1,2},{2,3},{4,5},{5,6},{6,7},{8,9},{9,10},{10,11},{12,13},{... | collective-permute-start | bytes 1572872 | tf_op jit(solution)/shard_map/ppermute | solution.py:86
  17.3 15.2 %collective-permute-start.3 = (f32[256,512]{1,0:T(8,128)}, f32[256,512]{1,0:T(8,128)S(1)}, u32[]{:S(2)}, u32[]{:S(2)}) collective-permute-start(f32[256,512]{1,0:T(8,128)} %collective-permute-done.1), channel_id=1, source_target_pairs={{1,0},{2,1},{5,4},{6,5},{9,8},{10,9},{13,12},{14,13},{17,16},{18,1... | collective-permute-start | bytes 1572872 | tf_op jit(solution)/shard_map/ppermute | solution.py:87
  18.6 15.2 %collective-permute-start.2 = (f32[256,512]{1,0:T(8,128)}, f32[256,512]{1,0:T(8,128)S(1)}, u32[]{:S(2)}, u32[]{:S(2)}) collective-permute-start(f32[256,512]{1,0:T(8,128)} %collective-permute-done), channel_id=1, source_target_pairs={{1,2},{2,3},{5,6},{6,7},{9,10},{10,11},{13,14},{14,15},{17,18},{18... | collective-permute-start | bytes 1572872 | tf_op jit(solution)/shard_map/ppermute | solution.py:86
  32.5 14.1 %collective-permute-start.5 = (f32[256,512]{1,0:T(8,128)S(1)}, f32[256,512]{1,0:T(8,128)S(1)}, u32[]{:S(2)}, u32[]{:S(2)}) collective-permute-start(f32[256,512]{1,0:T(8,128)S(1)} %collective-permute-done.3), channel_id=1, source_target_pairs={{1,0},{5,4},{9,8},{13,12},{17,16},{21,20},{25,24},{29,28}} | collective-permute-start | bytes 1572872 | tf_op jit(solution)/shard_map/ppermute | solution.py:87
  33.8 13.4 %collective-permute-start.4 = (f32[256,512]{1,0:T(8,128)S(1)}, f32[256,512]{1,0:T(8,128)S(1)}, u32[]{:S(2)}, u32[]{:S(2)}) collective-permute-start(f32[256,512]{1,0:T(8,128)S(1)} %collective-permute-done.2), channel_id=1, source_target_pairs={{2,3},{6,7},{10,11},{14,15},{18,19},{22,23},{26,27},{30,31}} | collective-permute-start | bytes 1572872 | tf_op jit(solution)/shard_map/ppermute | solution.py:86
  50.1 6.4 %collective-permute-start.7 = (f32[512,64]{0,1:T(8,128)S(1)}, f32[512,64]{0,1:T(8,128)S(1)}, u32[]{:S(2)}, u32[]{:S(2)}) collective-permute-start(f32[512,64]{0,1:T(8,128)S(1)} %slice_select_fusion.3), channel_id=1, source_target_pairs={{0,8},{4,12},{8,0},{12,4},{16,24},{20,28},{24,16},{28,20},{1,9},{5... | collective-permute-start | bytes 393224 | tf_op jit(solution)/shard_map/ppermute | solution.py:15
  51.2 7.3 %collective-permute-start.25 = (f32[512,64]{0,1:T(8,128)S(1)}, f32[512,64]{0,1:T(8,128)S(1)}, u32[]{:S(2)}, u32[]{:S(2)}) collective-permute-start(f32[512,64]{0,1:T(8,128)S(1)} %slice_select_fusion.2), channel_id=1, source_target_pairs={{0,8},{4,12},{8,0},{12,4},{16,24},{20,28},{24,16},{28,20},{1,9},{5... | collective-permute-start | bytes 393224 | tf_op jit(solution)/shard_map/ppermute | solution.py:15
  56.6 4.8 %collective-permute-start.8 = (f32[512,32]{0,1:T(8,128)S(1)}, f32[512,32]{0,1:T(8,128)S(1)}, u32[]{:S(2)}, u32[]{:S(2)}) collective-permute-start(f32[512,32]{0,1:T(8,128)S(1)} %slice_select_fusion.5), channel_id=1, source_target_pairs={{0,16},{4,20},{8,24},{12,28},{16,0},{20,4},{24,8},{28,12},{1,17},{... | collective-permute-start | bytes 196616 | tf_op jit(solution)/shard_map/ppermute | solution.py:15
  58.6 4.8 %collective-permute-start.26 = (f32[512,32]{0,1:T(8,128)S(1)}, f32[512,32]{0,1:T(8,128)S(1)}, u32[]{:S(2)}, u32[]{:S(2)}) collective-permute-start(f32[512,32]{0,1:T(8,128)S(1)} %slice_select_fusion.4), channel_id=1, source_target_pairs={{0,16},{4,20},{8,24},{12,28},{16,0},{20,4},{24,8},{28,12},{1,17},{... | collective-permute-start | bytes 196616 | tf_op jit(solution)/shard_map/ppermute | solution.py:15
  61.9 3.4 %collective-permute-start.9 = (f32[512,32]{0,1:T(8,128)S(1)}, f32[512,32]{0,1:T(8,128)S(1)}, u32[]{:S(2)}, u32[]{:S(2)}) collective-permute-start(f32[512,32]{0,1:T(8,128)S(1)} %convolution_bitcast_fusion.5), channel_id=1, source_target_pairs={{0,1},{4,5},{8,9},{12,13},{16,17},{20,21},{24,25},{28,29}} | collective-permute-start | bytes 196616 | tf_op jit(solution)/shard_map/ppermute | solution.py:118
  64.0 3.2 %collective-permute-start.27 = (f32[512,32]{0,1:T(8,128)S(1)}, f32[512,32]{0,1:T(8,128)S(1)}, u32[]{:S(2)}, u32[]{:S(2)}) collective-permute-start(f32[512,32]{0,1:T(8,128)S(1)} %convolution_bitcast_fusion.2), channel_id=1, source_target_pairs={{0,1},{4,5},{8,9},{12,13},{16,17},{20,21},{24,25},{28,29}} | collective-permute-start | bytes 196616 | tf_op jit(solution)/shard_map/ppermute | solution.py:118
  70.3 2.9 %collective-permute-start.29 = (f32[512,32]{0,1:T(8,128)S(1)}, f32[512,32]{0,1:T(8,128)S(1)}, u32[]{:S(2)}, u32[]{:S(2)}) collective-permute-start(f32[512,32]{0,1:T(8,128)S(1)} %convolution_add_fusion.7), channel_id=1, source_target_pairs={{2,3},{6,7},{10,11},{14,15},{18,19},{22,23},{26,27},{30,31}} | collective-permute-start | bytes 196616 | tf_op jit(solution)/shard_map/ppermute | solution.py:118
  72.3 2.9 %collective-permute-start.12 = (f32[512,32]{0,1:T(8,128)S(1)}, f32[512,32]{0,1:T(8,128)S(1)}, u32[]{:S(2)}, u32[]{:S(2)}) collective-permute-start(f32[512,32]{0,1:T(8,128)S(1)} %convolution_bitcast_fusion.4), channel_id=1, source_target_pairs={{3,2},{7,6},{11,10},{15,14},{19,18},{23,22},{27,26},{31,30}} | collective-permute-start | bytes 196616 | tf_op jit(solution)/shard_map/ppermute | solution.py:126
  77.8 16.1 %collective-permute-start.14 = (f32[512,32]{0,1:T(8,128)S(1)}, f32[512,32]{0,1:T(8,128)S(1)}, u32[]{:S(2)}, u32[]{:S(2)}) collective-permute-start(f32[512,32]{0,1:T(8,128)S(1)} %convolution_add_fusion.9), channel_id=1, source_target_pairs={{1,0},{5,4},{9,8},{13,12},{17,16},{21,20},{25,24},{29,28}} | collective-permute-start | bytes 196616 | tf_op jit(solution)/shard_map/ppermute | solution.py:126
  79.6 16.9 %collective-permute-start.32 = (f32[512,32]{0,1:T(8,128)S(1)}, f32[512,32]{0,1:T(8,128)S(1)}, u32[]{:S(2)}, u32[]{:S(2)}) collective-permute-start(f32[512,32]{0,1:T(8,128)S(1)} %convolution_add_fusion.4), channel_id=1, source_target_pairs={{1,0},{5,4},{9,8},{13,12},{17,16},{21,20},{25,24},{29,28}} | collective-permute-start | bytes 196616 | tf_op jit(solution)/shard_map/ppermute | solution.py:126
  94.4 4.3 %collective-permute-start.15 = (f32[512,32]{0,1:T(8,128)S(1)}, f32[512,32]{0,1:T(8,128)S(1)}, u32[]{:S(2)}, u32[]{:S(2)}) collective-permute-start(f32[512,32]{0,1:T(8,128)S(1)} %get-tuple-element.24), channel_id=1, source_target_pairs={{0,16},{4,20},{8,24},{12,28},{16,0},{20,4},{24,8},{28,12},{1,17},{... | collective-permute-start | bytes 196616 | tf_op jit(solution)/shard_map/ppermute | solution.py:15
  96.9 4.3 %collective-permute-start.33 = (f32[512,32]{0,1:T(8,128)S(1)}, f32[512,32]{0,1:T(8,128)S(1)}, u32[]{:S(2)}, u32[]{:S(2)}) collective-permute-start(f32[512,32]{0,1:T(8,128)S(1)} %get-tuple-element.22), channel_id=1, source_target_pairs={{0,16},{4,20},{8,24},{12,28},{16,0},{20,4},{24,8},{28,12},{1,17},{... | collective-permute-start | bytes 196616 | tf_op jit(solution)/shard_map/ppermute | solution.py:15
  98.7 5.5 %collective-permute-start.16 = (f32[512,64]{0,1:T(8,128)S(1)}, f32[512,64]{0,1:T(8,128)S(1)}, u32[]{:S(2)}, u32[]{:S(2)}) collective-permute-start(f32[512,64]{0,1:T(8,128)S(1)} %constant_dynamic-update-slice_fusion.10), channel_id=1, source_target_pairs={{0,8},{4,12},{8,0},{12,4},{16,24},{20,28},{24,16},{28,20},{1,9},{5... | collective-permute-start | bytes 393224 | tf_op jit(solution)/shard_map/ppermute | solution.py:15
  101.2 5.0 %collective-permute-start.34 = (f32[512,64]{0,1:T(8,128)S(1)}, f32[512,64]{0,1:T(8,128)S(1)}, u32[]{:S(2)}, u32[]{:S(2)}) collective-permute-start(f32[512,64]{0,1:T(8,128)S(1)} %constant_dynamic-update-slice_fusion.4), channel_id=1, source_target_pairs={{0,8},{4,12},{8,0},{12,4},{16,24},{20,28},{24,16},{28,20},{1,9},{5... | collective-permute-start | bytes 393224 | tf_op jit(solution)/shard_map/ppermute | solution.py:15
  110.1 8.4 %collective-permute-start.18 = (f32[256,256]{0,1:T(8,128)S(1)}, f32[256,256]{0,1:T(8,128)S(1)}, u32[]{:S(2)}, u32[]{:S(2)}) collective-permute-start(f32[256,256]{0,1:T(8,128)S(1)} %get-tuple-element.10), channel_id=1, source_target_pairs={{0,1},{4,5},{8,9},{12,13},{16,17},{20,21},{24,25},{28,29}} | collective-permute-start | bytes 786440 | tf_op jit(solution)/shard_map/ppermute | solution.py:107
  111.9 6.6 %collective-permute-start.21 = (f32[256,256]{0,1:T(8,128)S(1)}, f32[256,256]{0,1:T(8,128)S(1)}, u32[]{:S(2)}, u32[]{:S(2)}) collective-permute-start(f32[256,256]{0,1:T(8,128)S(1)} %get-tuple-element.9), channel_id=1, source_target_pairs={{3,2},{7,6},{11,10},{15,14},{19,18},{23,22},{27,26},{31,30}} | collective-permute-start | bytes 786440 | tf_op jit(solution)/shard_map/ppermute | solution.py:108
  113.6 10.5 %collective-permute-start.36 = (f32[256,256]{0,1:T(8,128)S(1)}, f32[256,256]{0,1:T(8,128)S(1)}, u32[]{:S(2)}, u32[]{:S(2)}) collective-permute-start(f32[256,256]{0,1:T(8,128)S(1)} %get-tuple-element.20), channel_id=1, source_target_pairs={{0,1},{4,5},{8,9},{12,13},{16,17},{20,21},{24,25},{28,29}} | collective-permute-start | bytes 786440 | tf_op jit(solution)/shard_map/ppermute | solution.py:107
  115.0 9.2 %collective-permute-start.39 = (f32[256,256]{0,1:T(8,128)S(1)}, f32[256,256]{0,1:T(8,128)S(1)}, u32[]{:S(2)}, u32[]{:S(2)}) collective-permute-start(f32[256,256]{0,1:T(8,128)S(1)} %get-tuple-element.19), channel_id=1, source_target_pairs={{3,2},{7,6},{11,10},{15,14},{19,18},{23,22},{27,26},{31,30}} | collective-permute-start | bytes 786440 | tf_op jit(solution)/shard_map/ppermute | solution.py:108
  118.6 11.1 %collective-permute-start.19 = (f32[256,256]{0,1:T(8,128)S(1)}, f32[256,256]{0,1:T(8,128)S(1)}, u32[]{:S(2)}, u32[]{:S(2)}) collective-permute-start(f32[256,256]{0,1:T(8,128)S(1)} %get-tuple-element.8), channel_id=1, source_target_pairs={{0,1},{1,2},{4,5},{5,6},{8,9},{9,10},{12,13},{13,14},{16,17},{17,1... | collective-permute-start | bytes 786440 | tf_op jit(solution)/shard_map/ppermute | solution.py:107
  123.0 6.7 %collective-permute-start.22 = (f32[256,256]{0,1:T(8,128)S(1)}, f32[256,256]{0,1:T(8,128)S(1)}, u32[]{:S(2)}, u32[]{:S(2)}) collective-permute-start(f32[256,256]{0,1:T(8,128)S(1)} %get-tuple-element.7), channel_id=1, source_target_pairs={{2,1},{3,2},{6,5},{7,6},{10,9},{11,10},{14,13},{15,14},{18,17},{19... | collective-permute-start | bytes 786440 | tf_op jit(solution)/shard_map/ppermute | solution.py:108
  124.2 11.3 %collective-permute-start.37 = (f32[256,256]{0,1:T(8,128)S(1)}, f32[256,256]{0,1:T(8,128)S(1)}, u32[]{:S(2)}, u32[]{:S(2)}) collective-permute-start(f32[256,256]{0,1:T(8,128)S(1)} %get-tuple-element.18), channel_id=1, source_target_pairs={{0,1},{1,2},{4,5},{5,6},{8,9},{9,10},{12,13},{13,14},{16,17},{17,1... | collective-permute-start | bytes 786440 | tf_op jit(solution)/shard_map/ppermute | solution.py:107
  128.6 6.9 %collective-permute-start.40 = (f32[256,256]{0,1:T(8,128)S(1)}, f32[256,256]{0,1:T(8,128)S(1)}, u32[]{:S(2)}, u32[]{:S(2)}) collective-permute-start(f32[256,256]{0,1:T(8,128)S(1)} %get-tuple-element.17), channel_id=1, source_target_pairs={{2,1},{3,2},{6,5},{7,6},{10,9},{11,10},{14,13},{15,14},{18,17},{19... | collective-permute-start | bytes 786440 | tf_op jit(solution)/shard_map/ppermute | solution.py:108
  129.8 11.7 %collective-permute-start.20 = (f32[256,256]{0,1:T(8,128)S(1)}, f32[256,256]{0,1:T(8,128)S(1)}, u32[]{:S(2)}, u32[]{:S(2)}) collective-permute-start(f32[256,256]{0,1:T(8,128)S(1)} %get-tuple-element.6), channel_id=1, source_target_pairs={{0,1},{1,2},{2,3},{4,5},{5,6},{6,7},{8,9},{9,10},{10,11},{12,13},{... | collective-permute-start | bytes 786440 | tf_op jit(solution)/shard_map/ppermute | solution.py:107
  134.3 8.3 %collective-permute-start.23 = (f32[256,256]{0,1:T(8,128)S(1)}, f32[256,256]{0,1:T(8,128)S(1)}, u32[]{:S(2)}, u32[]{:S(2)}) collective-permute-start(f32[256,256]{0,1:T(8,128)S(1)} %get-tuple-element.5), channel_id=1, source_target_pairs={{1,0},{2,1},{3,2},{5,4},{6,5},{7,6},{9,8},{10,9},{11,10},{13,12},{... | collective-permute-start | bytes 786440 | tf_op jit(solution)/shard_map/ppermute | solution.py:108
  135.7 10.1 %collective-permute-start.38 = (f32[256,256]{0,1:T(8,128)S(1)}, f32[256,256]{0,1:T(8,128)S(1)}, u32[]{:S(2)}, u32[]{:S(2)}) collective-permute-start(f32[256,256]{0,1:T(8,128)S(1)} %get-tuple-element.16), channel_id=1, source_target_pairs={{0,1},{1,2},{2,3},{4,5},{5,6},{6,7},{8,9},{9,10},{10,11},{12,13},{... | collective-permute-start | bytes 786440 | tf_op jit(solution)/shard_map/ppermute | solution.py:107
  140.3 8.3 %collective-permute-start.41 = (f32[256,256]{0,1:T(8,128)S(1)}, f32[256,256]{0,1:T(8,128)S(1)}, u32[]{:S(2)}, u32[]{:S(2)}) collective-permute-start(f32[256,256]{0,1:T(8,128)S(1)} %get-tuple-element.15), channel_id=1, source_target_pairs={{1,0},{2,1},{3,2},{5,4},{6,5},{7,6},{9,8},{10,9},{11,10},{13,12},{... | collective-permute-start | bytes 786440 | tf_op jit(solution)/shard_map/ppermute | solution.py:108
  (13 other events, 73.0 us)

commit v23 on v22

--- a/solution.py
+++ b/solution.py
@@ -44,10 +44,9 @@
     bit = 1
     while bit < count:
         width = current.shape[1] // 2
-        low, high = current[:, :width], current[:, width:]
-        upper = (index // bit) % 2 == 1
-        send = jnp.where(upper, low, high)
-        keep = jnp.where(upper, high, low)
+        upper = (index // bit) % 2
+        send = lax.dynamic_slice_in_dim(current, (1 - upper) * width, width, axis=1)
+        keep = lax.dynamic_slice_in_dim(current, upper * width, width, axis=1)
         current = keep + swap(send, axis, bit)
         bit *= 2
     return current

time: 151 us -> 151 us (level)
  other arithmetic: 2.76 us -> 4.52 us
    add x3 -> x4, other arithmetic: 0.2 us -> 2.09 us  [reduce_scatter_columns(): current = keep + swap(send, axis, bit)]
    dynamic_update_slice x5 -> x6, local copies, waits for them, and re-layouts: 1.77 us -> 0.09 us  [all_gather_columns(): lax.dynamic_update_slice_in_dim(joined, other, (1 - upper) * width, axis=1)]
    dynamic_update_slice x4, local copies, waits for them, and re-layouts: 1.68 us -> 0.08 us  [all_gather_columns(): lax.dynamic_update_slice_in_dim(joined, current, upper * width, axis=1)]
    unnamed x7 -> x13, local copies, waits for them, and re-layouts: 2.93 us -> 3.72 us
  transfers between devices with their start and end apart: 42 -> 42, of which waited for: 20 -> 18; matrix products, arithmetic and copies ran while one was open for 18% -> 18% of each run, Pallas kernels for 0% -> 0%
where the time goes in v23:
time: 151 us
  starting transfers between devices  61.1 us (40%)
  waiting for transfers between devices  57.2 us (38%)
  matrix products  19.5 us (13%)
  local copies, waits for them, and re-layouts  7.29 us (5%)
  other arithmetic  4.52 us (3%)
    ppermute x3, waiting for transfers between devices, gamma_over_aux(): from_right = lax.ppermute(from_right, 'aux', leftward)  23 us
    ppermute x6, starting transfers between devices, reduce_over_aux(): lax.ppermute(to_right + block(index + count - 1 - step), 'aux', rightward)  21.1 us
    dot_general x26, matrix products, product(): jnp.dot(left, right, precision=lax.Precision.HIGH, preferred_element_type...  17.4 us
    ppermute x6, waiting for transfers between devices, solve(): arriving = arriving + lax.ppermute(value, 'aux', [(sender, sender - 1)])  13.1 us
    ppermute x12, starting transfers between devices, swap(): return lax.ppermute(array, axis, [(i, i ^ bit) for i in range(count)])  12.2 us
    ppermute x12, waiting for transfers between devices, swap(): return lax.ppermute(array, axis, [(i, i ^ bit) for i in range(count)])  9.54 us
    ppermute x3, starting transfers between devices, gamma_over_aux(): from_left = lax.ppermute(from_left, 'aux', rightward)  7.76 us
    ppermute x6, waiting for transfers between devices, reduce_over_aux(): lax.ppermute(to_right + block(index + count - 1 - step), 'aux', rightward)  6.37 us
  transfers between devices with their start and end apart: 42, of which 18 were waited for; matrix products, arithmetic and copies ran while one was open for 18% of the time, Pallas kernels for 0%

profile of v23, /device:TPU:0, one launch (start us, length us, event | category | flops | bytes accessed | tf_op | source)
XLA Modules:
  0.0 150.6 jit_solution(5038334683743712038)
XLA Ops:
  0.0 1.4 collective-permute-start.1
  1.4 6.4 %collective-permute-start = (f32[256,512]{1,0:T(8,128)}, f32[256,512]{1,0:T(8,128)}, u32[]{:S(2)}, u32[]{:S(2)}) collective-permute-start(f32[256,512]{1,0:T(8,128)} %param.6), channel_id=1, source_target_pairs={{0,1},{1,2},{2,3},{4,5},{5,6},{6,7},{8,9},{9,10},{10,11},{12,13},{... | collective-permute-start | bytes 1572872 | tf_op jit(solution)/shard_map/ppermute | solution.py:85
  7.8 2.9 %copy.8 = f32[512,1024]{0,1:T(8,128)} copy(f32[512,1024]{1,0:T(8,128)} %param.5) | data formatting | bytes 4194304 | tf_op args[0]
  11.0 1.8 %bitcast_multiply_fusion = f32[512,1024]{0,1:T(8,128)S(1)} fusion(f32[512,1024]{0,1:T(8,128)} %copy.8, f32[512,16]{0,1:T(8,128)S(1)} %reshape.6), kind=kLoop, calls=%fused_computation | loop fusion | flops 524288 | bytes 4227072 | tf_op jit(solution)/shard_map/mul | solution.py:23
  12.8 2.1 %fusion.10 = f32[512,512]{0,1:T(8,128)S(1)} fusion(f32[256,512]{1,0:T(8,128)} %param.6, f32[512,1024]{0,1:T(8,128)S(1)} %bitcast_multiply_fusion, s32[]{:T(128)S(6)} %select_n.121), kind=kOutput, calls=%fused_computation.33 | convolution fusion | flops 402653184 | bytes 2097156 | tf_op jit(solution)/shard_map/dot_general | solution.py:27
  14.9 2.4 %collective-permute-done.1 = f32[256,512]{1,0:T(8,128)} collective-permute-done((f32[256,512]{1,0:T(8,128)}, f32[256,512]{1,0:T(8,128)}, u32[]{:S(2)}, u32[]{:S(2)}) %collective-permute-start.1) | collective-permute-done | bytes 524320 | tf_op jit(solution)/shard_map/ppermute | solution.py:86
  19.3 1.7 %convolution_add_fusion.3 = f32[512,512]{0,1:T(8,128)S(1)} fusion(f32[512,512]{0,1:T(8,128)S(1)} %fusion.10, f32[256,512]{1,0:T(8,128)} %collective-permute-done, f32[512,1024]{0,1:T(8,128)S(1)} %bitcast_multiply_fusion, s32[]{:T(128)S(6)} %select_n.122), kind=kOutput, calls=%fused_computation.6 | convolution fusion | flops 402915328 | bytes 3145732 | tf_op jit(solution)/shard_map/dot_general | solution.py:27
  21.0 1.7 %convolution_add_fusion.2 = f32[512,512]{0,1:T(8,128)S(1)} fusion(f32[512,512]{0,1:T(8,128)S(1)} %convolution_add_fusion.3, f32[256,512]{1,0:T(8,128)} %collective-permute-done.1, f32[512,1024]{0,1:T(8,128)S(1)} %bitcast_multiply_fusion, s32[]{:T(128)S(6)} %select_n.123), kind=kOutput, calls=%fused_computation.5 | convolution fusion | flops 402915328 | bytes 3145732 | tf_op jit(solution)/shard_map/dot_general | solution.py:27
  22.6 9.8 %collective-permute-done.3 = f32[256,512]{1,0:T(8,128)S(1)} collective-permute-done((f32[256,512]{1,0:T(8,128)}, f32[256,512]{1,0:T(8,128)S(1)}, u32[]{:S(2)}, u32[]{:S(2)}) %collective-permute-start.3) | collective-permute-done | bytes 524320 | tf_op jit(solution)/shard_map/ppermute | solution.py:86
  35.8 10.8 %collective-permute-done.5 = f32[256,512]{1,0:T(8,128)S(1)} collective-permute-done((f32[256,512]{1,0:T(8,128)S(1)}, f32[256,512]{1,0:T(8,128)S(1)}, u32[]{:S(2)}, u32[]{:S(2)}) %collective-permute-start.5) | collective-permute-done | bytes 524320 | tf_op jit(solution)/shard_map/ppermute | solution.py:86
  56.5 3.2 %collective-permute-done.7 = f32[512,64]{0,1:T(8,128)S(1)} collective-permute-done((f32[512,64]{0,1:T(8,128)S(1)}, f32[512,64]{0,1:T(8,128)S(1)}, u32[]{:S(2)}, u32[]{:S(2)}) %collective-permute-start.7) | collective-permute-done | bytes 131104 | tf_op jit(solution)/shard_map/ppermute | solution.py:15
  62.7 1.9 %collective-permute-done.8 = f32[512,32]{0,1:T(8,128)S(1)} collective-permute-done((f32[512,32]{0,1:T(8,128)S(1)}, f32[512,32]{0,1:T(8,128)S(1)}, u32[]{:S(2)}, u32[]{:S(2)}) %collective-permute-start.8) | collective-permute-done | bytes 65568 | tf_op jit(solution)/shard_map/ppermute | solution.py:15
  65.3 1.5 collective-permute-start.9
  67.3 1.3 collective-permute-start.27
  81.2 1.3 collective-permute-start.14
  82.9 1.3 collective-permute-start.32
  84.2 12.3 %collective-permute-done.14 = f32[512,32]{0,1:T(8,128)S(1)} collective-permute-done((f32[512,32]{0,1:T(8,128)S(1)}, f32[512,32]{0,1:T(8,128)S(1)}, u32[]{:S(2)}, u32[]{:S(2)}) %collective-permute-start.14) | collective-permute-done | bytes 65568 | tf_op jit(solution)/shard_map/ppermute | solution.py:125
  96.9 1.6 %collective-permute-start.15 = (f32[512,32]{0,1:T(8,128)S(1)}, f32[512,32]{0,1:T(8,128)S(1)}, u32[]{:S(2)}, u32[]{:S(2)}) collective-permute-start(f32[512,32]{0,1:T(8,128)S(1)} %get-tuple-element.22), channel_id=1, source_target_pairs={{0,16},{4,20},{8,24},{12,28},{16,0},{20,4},{24,8},{28,12},{1,17},{... | collective-permute-start | bytes 196616 | tf_op jit(solution)/shard_map/ppermute | solution.py:15
  99.8 1.6 %collective-permute-start.33 = (f32[512,32]{0,1:T(8,128)S(1)}, f32[512,32]{0,1:T(8,128)S(1)}, u32[]{:S(2)}, u32[]{:S(2)}) collective-permute-start(f32[512,32]{0,1:T(8,128)S(1)} %get-tuple-element.20), channel_id=1, source_target_pairs={{0,16},{4,20},{8,24},{12,28},{16,0},{20,4},{24,8},{28,12},{1,17},{... | collective-permute-start | bytes 196616 | tf_op jit(solution)/shard_map/ppermute | solution.py:15
  101.4 2.4 %collective-permute-start.16 = (f32[512,64]{0,1:T(8,128)S(1)}, f32[512,64]{0,1:T(8,128)S(1)}, u32[]{:S(2)}, u32[]{:S(2)}) collective-permute-start(f32[512,64]{0,1:T(8,128)S(1)} %constant_dynamic-update-slice_fusion.10), channel_id=1, source_target_pairs={{0,8},{4,12},{8,0},{12,4},{16,24},{20,28},{24,16},{28,20},{1,9},{5... | collective-permute-start | bytes 393224 | tf_op jit(solution)/shard_map/ppermute | solution.py:15
  104.1 2.0 %collective-permute-start.34 = (f32[512,64]{0,1:T(8,128)S(1)}, f32[512,64]{0,1:T(8,128)S(1)}, u32[]{:S(2)}, u32[]{:S(2)}) collective-permute-start(f32[512,64]{0,1:T(8,128)S(1)} %constant_dynamic-update-slice_fusion.4), channel_id=1, source_target_pairs={{0,8},{4,12},{8,0},{12,4},{16,24},{20,28},{24,16},{28,20},{1,9},{5... | collective-permute-start | bytes 393224 | tf_op jit(solution)/shard_map/ppermute | solution.py:15
  106.8 2.3 %collective-permute-done.34 = f32[512,64]{0,1:T(8,128)S(1)} collective-permute-done((f32[512,64]{0,1:T(8,128)S(1)}, f32[512,64]{0,1:T(8,128)S(1)}, u32[]{:S(2)}, u32[]{:S(2)}) %collective-permute-start.34) | collective-permute-done | bytes 131104 | tf_op jit(solution)/shard_map/ppermute | solution.py:15
  110.6 1.8 %collective-permute-start.18 = (f32[256,256]{0,1:T(8,128)S(1)}, f32[256,256]{0,1:T(8,128)S(1)}, u32[]{:S(2)}, u32[]{:S(2)}) collective-permute-start(f32[256,256]{0,1:T(8,128)S(1)} %get-tuple-element.10), channel_id=1, source_target_pairs={{0,1},{4,5},{8,9},{12,13},{16,17},{20,21},{24,25},{28,29}} | collective-permute-start | bytes 786440 | tf_op jit(solution)/shard_map/ppermute | solution.py:106
  114.2 1.3 collective-permute-start.36
  116.2 2.8 %collective-permute-done.18 = f32[256,256]{0,1:T(8,128)S(1)} collective-permute-done((f32[256,256]{0,1:T(8,128)S(1)}, f32[256,256]{0,1:T(8,128)S(1)}, u32[]{:S(2)}, u32[]{:S(2)}) %collective-permute-start.18) | collective-permute-done | bytes 262176 | tf_op jit(solution)/shard_map/ppermute | solution.py:106
  119.0 4.4 %collective-permute-start.19 = (f32[256,256]{0,1:T(8,128)S(1)}, f32[256,256]{0,1:T(8,128)S(1)}, u32[]{:S(2)}, u32[]{:S(2)}) collective-permute-start(f32[256,256]{0,1:T(8,128)S(1)} %get-tuple-element.8), channel_id=1, source_target_pairs={{0,1},{1,2},{4,5},{5,6},{8,9},{9,10},{12,13},{13,14},{16,17},{17,1... | collective-permute-start | bytes 786440 | tf_op jit(solution)/shard_map/ppermute | solution.py:106
  124.7 4.4 %collective-permute-start.37 = (f32[256,256]{0,1:T(8,128)S(1)}, f32[256,256]{0,1:T(8,128)S(1)}, u32[]{:S(2)}, u32[]{:S(2)}) collective-permute-start(f32[256,256]{0,1:T(8,128)S(1)} %get-tuple-element.16), channel_id=1, source_target_pairs={{0,1},{1,2},{4,5},{5,6},{8,9},{9,10},{12,13},{13,14},{16,17},{17,1... | collective-permute-start | bytes 786440 | tf_op jit(solution)/shard_map/ppermute | solution.py:106
  130.3 4.6 %collective-permute-start.20 = (f32[256,256]{0,1:T(8,128)S(1)}, f32[256,256]{0,1:T(8,128)S(1)}, u32[]{:S(2)}, u32[]{:S(2)}) collective-permute-start(f32[256,256]{0,1:T(8,128)S(1)} %get-tuple-element.6), channel_id=1, source_target_pairs={{0,1},{1,2},{2,3},{4,5},{5,6},{6,7},{8,9},{9,10},{10,11},{12,13},{... | collective-permute-start | bytes 786440 | tf_op jit(solution)/shard_map/ppermute | solution.py:106
  136.3 4.6 %collective-permute-start.38 = (f32[256,256]{0,1:T(8,128)S(1)}, f32[256,256]{0,1:T(8,128)S(1)}, u32[]{:S(2)}, u32[]{:S(2)}) collective-permute-start(f32[256,256]{0,1:T(8,128)S(1)} %get-tuple-element.14), channel_id=1, source_target_pairs={{0,1},{1,2},{2,3},{4,5},{5,6},{6,7},{8,9},{9,10},{10,11},{12,13},{... | collective-permute-start | bytes 786440 | tf_op jit(solution)/shard_map/ppermute | solution.py:106
  142.2 1.6 %collective-permute-done.23 = f32[256,256]{0,1:T(8,128)S(1)} collective-permute-done((f32[256,256]{0,1:T(8,128)S(1)}, f32[256,256]{0,1:T(8,128)S(1)}, u32[]{:S(2)}, u32[]{:S(2)}) %collective-permute-start.23) | collective-permute-done | bytes 262176 | tf_op jit(solution)/shard_map/ppermute | solution.py:107
  143.9 2.7 %collective-permute-done.38 = f32[256,256]{0,1:T(8,128)S(1)} collective-permute-done((f32[256,256]{0,1:T(8,128)S(1)}, f32[256,256]{0,1:T(8,128)S(1)}, u32[]{:S(2)}, u32[]{:S(2)}) %collective-permute-start.38) | collective-permute-done | bytes 262176 | tf_op jit(solution)/shard_map/ppermute | solution.py:106
  146.6 2.8 %collective-permute-done.41 = f32[256,256]{0,1:T(8,128)S(1)} collective-permute-done((f32[256,256]{0,1:T(8,128)S(1)}, f32[256,256]{0,1:T(8,128)S(1)}, u32[]{:S(2)}, u32[]{:S(2)}) %collective-permute-start.41) | collective-permute-done | bytes 262176 | tf_op jit(solution)/shard_map/ppermute | solution.py:107
  (139 shorter events, 44.8 us)
Async XLA Ops:
  0.0 17.3 %collective-permute-start.1 = (f32[256,512]{1,0:T(8,128)}, f32[256,512]{1,0:T(8,128)}, u32[]{:S(2)}, u32[]{:S(2)}) collective-permute-start(f32[256,512]{1,0:T(8,128)} %param.6), channel_id=1, source_target_pairs={{1,0},{2,1},{3,2},{5,4},{6,5},{7,6},{9,8},{10,9},{11,10},{13,12},{... | collective-permute-start | bytes 1572872 | tf_op jit(solution)/shard_map/ppermute | solution.py:86
  1.4 17.2 %collective-permute-start = (f32[256,512]{1,0:T(8,128)}, f32[256,512]{1,0:T(8,128)}, u32[]{:S(2)}, u32[]{:S(2)}) collective-permute-start(f32[256,512]{1,0:T(8,128)} %param.6), channel_id=1, source_target_pairs={{0,1},{1,2},{2,3},{4,5},{5,6},{6,7},{8,9},{9,10},{10,11},{12,13},{... | collective-permute-start | bytes 1572872 | tf_op jit(solution)/shard_map/ppermute | solution.py:85
  17.3 15.2 %collective-permute-start.3 = (f32[256,512]{1,0:T(8,128)}, f32[256,512]{1,0:T(8,128)S(1)}, u32[]{:S(2)}, u32[]{:S(2)}) collective-permute-start(f32[256,512]{1,0:T(8,128)} %collective-permute-done.1), channel_id=1, source_target_pairs={{1,0},{2,1},{5,4},{6,5},{9,8},{10,9},{13,12},{14,13},{17,16},{18,1... | collective-permute-start | bytes 1572872 | tf_op jit(solution)/shard_map/ppermute | solution.py:86
  18.6 15.2 %collective-permute-start.2 = (f32[256,512]{1,0:T(8,128)}, f32[256,512]{1,0:T(8,128)S(1)}, u32[]{:S(2)}, u32[]{:S(2)}) collective-permute-start(f32[256,512]{1,0:T(8,128)} %collective-permute-done), channel_id=1, source_target_pairs={{1,2},{2,3},{5,6},{6,7},{9,10},{10,11},{13,14},{14,15},{17,18},{18... | collective-permute-start | bytes 1572872 | tf_op jit(solution)/shard_map/ppermute | solution.py:85
  32.5 14.1 %collective-permute-start.5 = (f32[256,512]{1,0:T(8,128)S(1)}, f32[256,512]{1,0:T(8,128)S(1)}, u32[]{:S(2)}, u32[]{:S(2)}) collective-permute-start(f32[256,512]{1,0:T(8,128)S(1)} %collective-permute-done.3), channel_id=1, source_target_pairs={{1,0},{5,4},{9,8},{13,12},{17,16},{21,20},{25,24},{29,28}} | collective-permute-start | bytes 1572872 | tf_op jit(solution)/shard_map/ppermute | solution.py:86
  33.8 13.4 %collective-permute-start.4 = (f32[256,512]{1,0:T(8,128)S(1)}, f32[256,512]{1,0:T(8,128)S(1)}, u32[]{:S(2)}, u32[]{:S(2)}) collective-permute-start(f32[256,512]{1,0:T(8,128)S(1)} %collective-permute-done.2), channel_id=1, source_target_pairs={{2,3},{6,7},{10,11},{14,15},{18,19},{22,23},{26,27},{30,31}} | collective-permute-start | bytes 1572872 | tf_op jit(solution)/shard_map/ppermute | solution.py:85
  53.3 6.4 %collective-permute-start.7 = (f32[512,64]{0,1:T(8,128)S(1)}, f32[512,64]{0,1:T(8,128)S(1)}, u32[]{:S(2)}, u32[]{:S(2)}) collective-permute-start(f32[512,64]{0,1:T(8,128)S(1)} %constant_dynamic-slice_fusion.8), channel_id=1, source_target_pairs={{0,8},{4,12},{8,0},{12,4},{16,24},{20,28},{24,16},{28,20},{1,9},{5... | collective-permute-start | bytes 393224 | tf_op jit(solution)/shard_map/ppermute | solution.py:15
  55.4 6.2 %collective-permute-start.25 = (f32[512,64]{0,1:T(8,128)S(1)}, f32[512,64]{0,1:T(8,128)S(1)}, u32[]{:S(2)}, u32[]{:S(2)}) collective-permute-start(f32[512,64]{0,1:T(8,128)S(1)} %constant_dynamic-slice_fusion.3), channel_id=1, source_target_pairs={{0,8},{4,12},{8,0},{12,4},{16,24},{20,28},{24,16},{28,20},{1,9},{5... | collective-permute-start | bytes 393224 | tf_op jit(solution)/shard_map/ppermute | solution.py:15
  59.7 4.9 %collective-permute-start.8 = (f32[512,32]{0,1:T(8,128)S(1)}, f32[512,32]{0,1:T(8,128)S(1)}, u32[]{:S(2)}, u32[]{:S(2)}) collective-permute-start(f32[512,32]{0,1:T(8,128)S(1)} %constant_dynamic-slice_fusion.7), channel_id=1, source_target_pairs={{0,16},{4,20},{8,24},{12,28},{16,0},{20,4},{24,8},{28,12},{1,17},{... | collective-permute-start | bytes 196616 | tf_op jit(solution)/shard_map/ppermute | solution.py:15
  61.6 5.1 %collective-permute-start.26 = (f32[512,32]{0,1:T(8,128)S(1)}, f32[512,32]{0,1:T(8,128)S(1)}, u32[]{:S(2)}, u32[]{:S(2)}) collective-permute-start(f32[512,32]{0,1:T(8,128)S(1)} %constant_dynamic-slice_fusion.2), channel_id=1, source_target_pairs={{0,16},{4,20},{8,24},{12,28},{16,0},{20,4},{24,8},{28,12},{1,17},{... | collective-permute-start | bytes 196616 | tf_op jit(solution)/shard_map/ppermute | solution.py:15
  65.3 3.4 %collective-permute-start.9 = (f32[512,32]{0,1:T(8,128)S(1)}, f32[512,32]{0,1:T(8,128)S(1)}, u32[]{:S(2)}, u32[]{:S(2)}) collective-permute-start(f32[512,32]{0,1:T(8,128)S(1)} %convolution_bitcast_fusion.5), channel_id=1, source_target_pairs={{0,1},{4,5},{8,9},{12,13},{16,17},{20,21},{24,25},{28,29}} | collective-permute-start | bytes 196616 | tf_op jit(solution)/shard_map/ppermute | solution.py:117
  67.3 3.2 %collective-permute-start.27 = (f32[512,32]{0,1:T(8,128)S(1)}, f32[512,32]{0,1:T(8,128)S(1)}, u32[]{:S(2)}, u32[]{:S(2)}) collective-permute-start(f32[512,32]{0,1:T(8,128)S(1)} %convolution_bitcast_fusion.2), channel_id=1, source_target_pairs={{0,1},{4,5},{8,9},{12,13},{16,17},{20,21},{24,25},{28,29}} | collective-permute-start | bytes 196616 | tf_op jit(solution)/shard_map/ppermute | solution.py:117
  73.6 2.9 %collective-permute-start.29 = (f32[512,32]{0,1:T(8,128)S(1)}, f32[512,32]{0,1:T(8,128)S(1)}, u32[]{:S(2)}, u32[]{:S(2)}) collective-permute-start(f32[512,32]{0,1:T(8,128)S(1)} %convolution_add_fusion.7), channel_id=1, source_target_pairs={{2,3},{6,7},{10,11},{14,15},{18,19},{22,23},{26,27},{30,31}} | collective-permute-start | bytes 196616 | tf_op jit(solution)/shard_map/ppermute | solution.py:117
  81.2 15.3 %collective-permute-start.14 = (f32[512,32]{0,1:T(8,128)S(1)}, f32[512,32]{0,1:T(8,128)S(1)}, u32[]{:S(2)}, u32[]{:S(2)}) collective-permute-start(f32[512,32]{0,1:T(8,128)S(1)} %convolution_add_fusion.9), channel_id=1, source_target_pairs={{1,0},{5,4},{9,8},{13,12},{17,16},{21,20},{25,24},{29,28}} | collective-permute-start | bytes 196616 | tf_op jit(solution)/shard_map/ppermute | solution.py:125
  82.9 16.4 %collective-permute-start.32 = (f32[512,32]{0,1:T(8,128)S(1)}, f32[512,32]{0,1:T(8,128)S(1)}, u32[]{:S(2)}, u32[]{:S(2)}) collective-permute-start(f32[512,32]{0,1:T(8,128)S(1)} %convolution_add_fusion.4), channel_id=1, source_target_pairs={{1,0},{5,4},{9,8},{13,12},{17,16},{21,20},{25,24},{29,28}} | collective-permute-start | bytes 196616 | tf_op jit(solution)/shard_map/ppermute | solution.py:125
  96.9 4.4 %collective-permute-start.15 = (f32[512,32]{0,1:T(8,128)S(1)}, f32[512,32]{0,1:T(8,128)S(1)}, u32[]{:S(2)}, u32[]{:S(2)}) collective-permute-start(f32[512,32]{0,1:T(8,128)S(1)} %get-tuple-element.22), channel_id=1, source_target_pairs={{0,16},{4,20},{8,24},{12,28},{16,0},{20,4},{24,8},{28,12},{1,17},{... | collective-permute-start | bytes 196616 | tf_op jit(solution)/shard_map/ppermute | solution.py:15
  99.8 4.3 %collective-permute-start.33 = (f32[512,32]{0,1:T(8,128)S(1)}, f32[512,32]{0,1:T(8,128)S(1)}, u32[]{:S(2)}, u32[]{:S(2)}) collective-permute-start(f32[512,32]{0,1:T(8,128)S(1)} %get-tuple-element.20), channel_id=1, source_target_pairs={{0,16},{4,20},{8,24},{12,28},{16,0},{20,4},{24,8},{28,12},{1,17},{... | collective-permute-start | bytes 196616 | tf_op jit(solution)/shard_map/ppermute | solution.py:15
  101.4 5.4 %collective-permute-start.16 = (f32[512,64]{0,1:T(8,128)S(1)}, f32[512,64]{0,1:T(8,128)S(1)}, u32[]{:S(2)}, u32[]{:S(2)}) collective-permute-start(f32[512,64]{0,1:T(8,128)S(1)} %constant_dynamic-update-slice_fusion.10), channel_id=1, source_target_pairs={{0,8},{4,12},{8,0},{12,4},{16,24},{20,28},{24,16},{28,20},{1,9},{5... | collective-permute-start | bytes 393224 | tf_op jit(solution)/shard_map/ppermute | solution.py:15
  104.1 5.0 %collective-permute-start.34 = (f32[512,64]{0,1:T(8,128)S(1)}, f32[512,64]{0,1:T(8,128)S(1)}, u32[]{:S(2)}, u32[]{:S(2)}) collective-permute-start(f32[512,64]{0,1:T(8,128)S(1)} %constant_dynamic-update-slice_fusion.4), channel_id=1, source_target_pairs={{0,8},{4,12},{8,0},{12,4},{16,24},{20,28},{24,16},{28,20},{1,9},{5... | collective-permute-start | bytes 393224 | tf_op jit(solution)/shard_map/ppermute | solution.py:15
  109.2 3.9 %collective-permute-start.35 = (f32[512,128]{0,1:T(8,128)S(1)}, f32[512,128]{0,1:T(8,128)S(1)}, u32[]{:S(2)}, u32[]{:S(2)}) collective-permute-start(f32[512,128]{0,1:T(8,128)S(1)} %constant_dynamic-update-slice_fusion.2), channel_id=1, source_target_pairs={{0,4},{4,0},{8,12},{12,8},{16,20},{20,16},{24,28},{28,24},{1,5},{5... | collective-permute-start | bytes 786440 | tf_op jit(solution)/shard_map/ppermute | solution.py:15
  110.6 8.4 %collective-permute-start.18 = (f32[256,256]{0,1:T(8,128)S(1)}, f32[256,256]{0,1:T(8,128)S(1)}, u32[]{:S(2)}, u32[]{:S(2)}) collective-permute-start(f32[256,256]{0,1:T(8,128)S(1)} %get-tuple-element.10), channel_id=1, source_target_pairs={{0,1},{4,5},{8,9},{12,13},{16,17},{20,21},{24,25},{28,29}} | collective-permute-start | bytes 786440 | tf_op jit(solution)/shard_map/ppermute | solution.py:106
  112.4 6.6 %collective-permute-start.21 = (f32[256,256]{0,1:T(8,128)S(1)}, f32[256,256]{0,1:T(8,128)S(1)}, u32[]{:S(2)}, u32[]{:S(2)}) collective-permute-start(f32[256,256]{0,1:T(8,128)S(1)} %get-tuple-element.9), channel_id=1, source_target_pairs={{3,2},{7,6},{11,10},{15,14},{19,18},{23,22},{27,26},{31,30}} | collective-permute-start | bytes 786440 | tf_op jit(solution)/shard_map/ppermute | solution.py:107
  114.2 10.4 %collective-permute-start.36 = (f32[256,256]{0,1:T(8,128)S(1)}, f32[256,256]{0,1:T(8,128)S(1)}, u32[]{:S(2)}, u32[]{:S(2)}) collective-permute-start(f32[256,256]{0,1:T(8,128)S(1)} %get-tuple-element.18), channel_id=1, source_target_pairs={{0,1},{4,5},{8,9},{12,13},{16,17},{20,21},{24,25},{28,29}} | collective-permute-start | bytes 786440 | tf_op jit(solution)/shard_map/ppermute | solution.py:106
  115.5 9.1 %collective-permute-start.39 = (f32[256,256]{0,1:T(8,128)S(1)}, f32[256,256]{0,1:T(8,128)S(1)}, u32[]{:S(2)}, u32[]{:S(2)}) collective-permute-start(f32[256,256]{0,1:T(8,128)S(1)} %get-tuple-element.17), channel_id=1, source_target_pairs={{3,2},{7,6},{11,10},{15,14},{19,18},{23,22},{27,26},{31,30}} | collective-permute-start | bytes 786440 | tf_op jit(solution)/shard_map/ppermute | solution.py:107
  119.0 11.1 %collective-permute-start.19 = (f32[256,256]{0,1:T(8,128)S(1)}, f32[256,256]{0,1:T(8,128)S(1)}, u32[]{:S(2)}, u32[]{:S(2)}) collective-permute-start(f32[256,256]{0,1:T(8,128)S(1)} %get-tuple-element.8), channel_id=1, source_target_pairs={{0,1},{1,2},{4,5},{5,6},{8,9},{9,10},{12,13},{13,14},{16,17},{17,1... | collective-permute-start | bytes 786440 | tf_op jit(solution)/shard_map/ppermute | solution.py:106
  123.5 6.7 %collective-permute-start.22 = (f32[256,256]{0,1:T(8,128)S(1)}, f32[256,256]{0,1:T(8,128)S(1)}, u32[]{:S(2)}, u32[]{:S(2)}) collective-permute-start(f32[256,256]{0,1:T(8,128)S(1)} %get-tuple-element.7), channel_id=1, source_target_pairs={{2,1},{3,2},{6,5},{7,6},{10,9},{11,10},{14,13},{15,14},{18,17},{19... | collective-permute-start | bytes 786440 | tf_op jit(solution)/shard_map/ppermute | solution.py:107
  124.7 11.5 %collective-permute-start.37 = (f32[256,256]{0,1:T(8,128)S(1)}, f32[256,256]{0,1:T(8,128)S(1)}, u32[]{:S(2)}, u32[]{:S(2)}) collective-permute-start(f32[256,256]{0,1:T(8,128)S(1)} %get-tuple-element.16), channel_id=1, source_target_pairs={{0,1},{1,2},{4,5},{5,6},{8,9},{9,10},{12,13},{13,14},{16,17},{17,1... | collective-permute-start | bytes 786440 | tf_op jit(solution)/shard_map/ppermute | solution.py:106
  129.1 7.1 %collective-permute-start.40 = (f32[256,256]{0,1:T(8,128)S(1)}, f32[256,256]{0,1:T(8,128)S(1)}, u32[]{:S(2)}, u32[]{:S(2)}) collective-permute-start(f32[256,256]{0,1:T(8,128)S(1)} %get-tuple-element.15), channel_id=1, source_target_pairs={{2,1},{3,2},{6,5},{7,6},{10,9},{11,10},{14,13},{15,14},{18,17},{19... | collective-permute-start | bytes 786440 | tf_op jit(solution)/shard_map/ppermute | solution.py:107
  130.3 11.9 %collective-permute-start.20 = (f32[256,256]{0,1:T(8,128)S(1)}, f32[256,256]{0,1:T(8,128)S(1)}, u32[]{:S(2)}, u32[]{:S(2)}) collective-permute-start(f32[256,256]{0,1:T(8,128)S(1)} %get-tuple-element.6), channel_id=1, source_target_pairs={{0,1},{1,2},{2,3},{4,5},{5,6},{6,7},{8,9},{9,10},{10,11},{12,13},{... | collective-permute-start | bytes 786440 | tf_op jit(solution)/shard_map/ppermute | solution.py:106
  134.9 8.9 %collective-permute-start.23 = (f32[256,256]{0,1:T(8,128)S(1)}, f32[256,256]{0,1:T(8,128)S(1)}, u32[]{:S(2)}, u32[]{:S(2)}) collective-permute-start(f32[256,256]{0,1:T(8,128)S(1)} %get-tuple-element.5), channel_id=1, source_target_pairs={{1,0},{2,1},{3,2},{5,4},{6,5},{7,6},{9,8},{10,9},{11,10},{13,12},{... | collective-permute-start | bytes 786440 | tf_op jit(solution)/shard_map/ppermute | solution.py:107
  136.3 10.3 %collective-permute-start.38 = (f32[256,256]{0,1:T(8,128)S(1)}, f32[256,256]{0,1:T(8,128)S(1)}, u32[]{:S(2)}, u32[]{:S(2)}) collective-permute-start(f32[256,256]{0,1:T(8,128)S(1)} %get-tuple-element.14), channel_id=1, source_target_pairs={{0,1},{1,2},{2,3},{4,5},{5,6},{6,7},{8,9},{9,10},{10,11},{12,13},{... | collective-permute-start | bytes 786440 | tf_op jit(solution)/shard_map/ppermute | solution.py:106
  140.9 8.6 %collective-permute-start.41 = (f32[256,256]{0,1:T(8,128)S(1)}, f32[256,256]{0,1:T(8,128)S(1)}, u32[]{:S(2)}, u32[]{:S(2)}) collective-permute-start(f32[256,256]{0,1:T(8,128)S(1)} %get-tuple-element.13), channel_id=1, source_target_pairs={{1,0},{2,1},{3,2},{5,4},{6,5},{7,6},{9,8},{10,9},{11,10},{13,12},{... | collective-permute-start | bytes 786440 | tf_op jit(solution)/shard_map/ppermute | solution.py:107
  (16 other events, 118.3 us)

commit v24 on v22

--- a/solution.py
+++ b/solution.py
@@ -117,8 +117,8 @@
         value = driving if turn == 0 else product(transfer, incoming) + driving
         incoming = incoming + lax.ppermute(value, "aux", [(turn, turn + 1)])
     solved = product(transfer, incoming) + driving
-    source = product(sub_factor.T, product(diag_inverse.T, solved))
     back_map = transfer.T
+    source = -product(back_map, solved)
     arriving = jnp.zeros_like(driving)
     for turn in range(chain_length - 1):
         sender = chain_length - 1 - turn

time: 151 us -> 150 us (level)
    dot_general x26 -> x24, matrix products: 17 us -> 16.3 us  [product(): jnp.dot(left, right, precision=lax.Precision.HIGH, preferred_element_type...]
  transfers between devices with their start and end apart: 42 -> 42, of which waited for: 20 -> 20; matrix products, arithmetic and copies ran while one was open for 18% -> 17% of each run, Pallas kernels for 0% -> 0%
where the time goes in v24:
time: 150 us; the launch traced here: 149 us
  starting transfers between devices  60 us (40%)
  waiting for transfers between devices  58.2 us (39%)
  matrix products  18.3 us (12%)
  local copies, waits for them, and re-layouts  8.56 us (6%)
  other arithmetic  2.76 us (2%)
    ppermute x3, waiting for transfers between devices, gamma_over_aux(): from_right = lax.ppermute(from_right, 'aux', leftward)  23.4 us
    ppermute x6, starting transfers between devices, reduce_over_aux(): lax.ppermute(to_right + block(index + count - 1 - step), 'aux', rightward)  20.8 us
    dot_general x24, matrix products, product(): jnp.dot(left, right, precision=lax.Precision.HIGH, preferred_element_type...  16.3 us
    ppermute x6, waiting for transfers between devices, solve(): arriving = arriving + lax.ppermute(value, 'aux', [(sender, sender - 1)])  13.4 us
    ppermute x12, starting transfers between devices, swap(): return lax.ppermute(array, axis, [(i, i ^ bit) for i in range(count)])  11.3 us
    ppermute x12, waiting for transfers between devices, swap(): return lax.ppermute(array, axis, [(i, i ^ bit) for i in range(count)])  10.1 us
    ppermute x3, starting transfers between devices, gamma_over_aux(): from_left = lax.ppermute(from_left, 'aux', rightward)  7.74 us
    ppermute x6, waiting for transfers between devices, reduce_over_aux(): lax.ppermute(to_right + block(index + count - 1 - step), 'aux', rightward)  6.86 us
  transfers between devices with their start and end apart: 42, of which 20 were waited for; matrix products, arithmetic and copies ran while one was open for 17% of the time, Pallas kernels for 0%

profile of v24, /device:TPU:0, one launch (start us, length us, event | category | flops | bytes accessed | tf_op | source)
XLA Modules:
  0.0 148.7 jit_solution(15799394068516240662)
XLA Ops:
  0.0 1.4 collective-permute-start.1
  1.4 6.4 %collective-permute-start = (f32[256,512]{1,0:T(8,128)}, f32[256,512]{1,0:T(8,128)}, u32[]{:S(2)}, u32[]{:S(2)}) collective-permute-start(f32[256,512]{1,0:T(8,128)} %param.6), channel_id=1, source_target_pairs={{0,1},{1,2},{2,3},{4,5},{5,6},{6,7},{8,9},{9,10},{10,11},{12,13},{... | collective-permute-start | bytes 1572872 | tf_op jit(solution)/shard_map/ppermute | solution.py:86
  7.8 2.9 %copy.8 = f32[512,1024]{0,1:T(8,128)} copy(f32[512,1024]{1,0:T(8,128)} %param.5) | data formatting | bytes 4194304 | tf_op args[0]
  10.9 1.8 %bitcast_multiply_fusion = f32[512,1024]{0,1:T(8,128)S(1)} fusion(f32[512,1024]{0,1:T(8,128)} %copy.8, f32[512,16]{0,1:T(8,128)S(1)} %reshape.6), kind=kLoop, calls=%fused_computation | loop fusion | flops 524288 | bytes 4227072 | tf_op jit(solution)/shard_map/mul | solution.py:23
  12.8 1.7 %fusion.10 = f32[512,512]{0,1:T(8,128)S(1)} fusion(f32[256,512]{1,0:T(8,128)} %param.6, f32[512,1024]{0,1:T(8,128)S(1)} %bitcast_multiply_fusion, s32[]{:T(128)S(6)} %select_n.177), kind=kOutput, calls=%fused_computation.33 | convolution fusion | flops 402653184 | bytes 2097156 | tf_op jit(solution)/shard_map/dot_general | solution.py:27
  14.5 2.8 %collective-permute-done.1 = f32[256,512]{1,0:T(8,128)} collective-permute-done((f32[256,512]{1,0:T(8,128)}, f32[256,512]{1,0:T(8,128)}, u32[]{:S(2)}, u32[]{:S(2)}) %collective-permute-start.1) | collective-permute-done | bytes 524320 | tf_op jit(solution)/shard_map/ppermute | solution.py:87
  19.3 1.7 %convolution_add_fusion.3 = f32[512,512]{0,1:T(8,128)S(1)} fusion(f32[512,512]{0,1:T(8,128)S(1)} %fusion.10, f32[256,512]{1,0:T(8,128)} %collective-permute-done, f32[512,1024]{0,1:T(8,128)S(1)} %bitcast_multiply_fusion, s32[]{:T(128)S(6)} %select_n.178), kind=kOutput, calls=%fused_computation.6 | convolution fusion | flops 402915328 | bytes 3145732 | tf_op jit(solution)/shard_map/dot_general | solution.py:27
  21.0 1.7 %convolution_add_fusion.2 = f32[512,512]{0,1:T(8,128)S(1)} fusion(f32[512,512]{0,1:T(8,128)S(1)} %convolution_add_fusion.3, f32[256,512]{1,0:T(8,128)} %collective-permute-done.1, f32[512,1024]{0,1:T(8,128)S(1)} %bitcast_multiply_fusion, s32[]{:T(128)S(6)} %select_n.179), kind=kOutput, calls=%fused_computation.5 | convolution fusion | flops 402915328 | bytes 3145732 | tf_op jit(solution)/shard_map/dot_general | solution.py:27
  22.6 9.8 %collective-permute-done.3 = f32[256,512]{1,0:T(8,128)S(1)} collective-permute-done((f32[256,512]{1,0:T(8,128)}, f32[256,512]{1,0:T(8,128)S(1)}, u32[]{:S(2)}, u32[]{:S(2)}) %collective-permute-start.3) | collective-permute-done | bytes 524320 | tf_op jit(solution)/shard_map/ppermute | solution.py:87
  35.8 10.8 %collective-permute-done.5 = f32[256,512]{1,0:T(8,128)S(1)} collective-permute-done((f32[256,512]{1,0:T(8,128)S(1)}, f32[256,512]{1,0:T(8,128)S(1)}, u32[]{:S(2)}, u32[]{:S(2)}) %collective-permute-start.5) | collective-permute-done | bytes 524320 | tf_op jit(solution)/shard_map/ppermute | solution.py:87
  52.3 4.2 %collective-permute-done.7 = f32[512,64]{0,1:T(8,128)S(1)} collective-permute-done((f32[512,64]{0,1:T(8,128)S(1)}, f32[512,64]{0,1:T(8,128)S(1)}, u32[]{:S(2)}, u32[]{:S(2)}) %collective-permute-start.7) | collective-permute-done | bytes 131104 | tf_op jit(solution)/shard_map/ppermute | solution.py:15
  59.7 1.7 %collective-permute-done.8 = f32[512,32]{0,1:T(8,128)S(1)} collective-permute-done((f32[512,32]{0,1:T(8,128)S(1)}, f32[512,32]{0,1:T(8,128)S(1)}, u32[]{:S(2)}, u32[]{:S(2)}) %collective-permute-start.8) | collective-permute-done | bytes 65568 | tf_op jit(solution)/shard_map/ppermute | solution.py:15
  61.9 1.4 collective-permute-start.9
  64.0 1.3 collective-permute-start.27
  77.1 1.3 collective-permute-start.14
  78.8 1.3 collective-permute-start.32
  80.1 13.1 %collective-permute-done.14 = f32[512,32]{0,1:T(8,128)S(1)} collective-permute-done((f32[512,32]{0,1:T(8,128)S(1)}, f32[512,32]{0,1:T(8,128)S(1)}, u32[]{:S(2)}, u32[]{:S(2)}) %collective-permute-start.14) | collective-permute-done | bytes 65568 | tf_op jit(solution)/shard_map/ppermute | solution.py:126
  93.6 1.6 %collective-permute-start.15 = (f32[512,32]{0,1:T(8,128)S(1)}, f32[512,32]{0,1:T(8,128)S(1)}, u32[]{:S(2)}, u32[]{:S(2)}) collective-permute-start(f32[512,32]{0,1:T(8,128)S(1)} %get-tuple-element.24), channel_id=1, source_target_pairs={{0,16},{4,20},{8,24},{12,28},{16,0},{20,4},{24,8},{28,12},{1,17},{... | collective-permute-start | bytes 196616 | tf_op jit(solution)/shard_map/ppermute | solution.py:15
  95.9 1.6 %collective-permute-start.33 = (f32[512,32]{0,1:T(8,128)S(1)}, f32[512,32]{0,1:T(8,128)S(1)}, u32[]{:S(2)}, u32[]{:S(2)}) collective-permute-start(f32[512,32]{0,1:T(8,128)S(1)} %get-tuple-element.22), channel_id=1, source_target_pairs={{0,16},{4,20},{8,24},{12,28},{16,0},{20,4},{24,8},{28,12},{1,17},{... | collective-permute-start | bytes 196616 | tf_op jit(solution)/shard_map/ppermute | solution.py:15
  98.0 1.6 %collective-permute-start.16 = (f32[512,64]{0,1:T(8,128)S(1)}, f32[512,64]{0,1:T(8,128)S(1)}, u32[]{:S(2)}, u32[]{:S(2)}) collective-permute-start(f32[512,64]{0,1:T(8,128)S(1)} %constant_dynamic-update-slice_fusion.10), channel_id=1, source_target_pairs={{0,8},{4,12},{8,0},{12,4},{16,24},{20,28},{24,16},{28,20},{1,9},{5... | collective-permute-start | bytes 393224 | tf_op jit(solution)/shard_map/ppermute | solution.py:15
  100.3 1.6 %collective-permute-start.34 = (f32[512,64]{0,1:T(8,128)S(1)}, f32[512,64]{0,1:T(8,128)S(1)}, u32[]{:S(2)}, u32[]{:S(2)}) collective-permute-start(f32[512,64]{0,1:T(8,128)S(1)} %constant_dynamic-update-slice_fusion.4), channel_id=1, source_target_pairs={{0,8},{4,12},{8,0},{12,4},{16,24},{20,28},{24,16},{28,20},{1,9},{5... | collective-permute-start | bytes 393224 | tf_op jit(solution)/shard_map/ppermute | solution.py:15
  104.0 1.3 collective-permute-done.34
  109.2 1.7 %collective-permute-start.18 = (f32[256,256]{0,1:T(8,128)S(1)}, f32[256,256]{0,1:T(8,128)S(1)}, u32[]{:S(2)}, u32[]{:S(2)}) collective-permute-start(f32[256,256]{0,1:T(8,128)S(1)} %get-tuple-element.10), channel_id=1, source_target_pairs={{0,1},{4,5},{8,9},{12,13},{16,17},{20,21},{24,25},{28,29}} | collective-permute-start | bytes 786440 | tf_op jit(solution)/shard_map/ppermute | solution.py:107
  112.7 1.3 collective-permute-start.36
  114.7 2.9 %collective-permute-done.18 = f32[256,256]{0,1:T(8,128)S(1)} collective-permute-done((f32[256,256]{0,1:T(8,128)S(1)}, f32[256,256]{0,1:T(8,128)S(1)}, u32[]{:S(2)}, u32[]{:S(2)}) %collective-permute-start.18) | collective-permute-done | bytes 262176 | tf_op jit(solution)/shard_map/ppermute | solution.py:107
  117.7 4.4 %collective-permute-start.19 = (f32[256,256]{0,1:T(8,128)S(1)}, f32[256,256]{0,1:T(8,128)S(1)}, u32[]{:S(2)}, u32[]{:S(2)}) collective-permute-start(f32[256,256]{0,1:T(8,128)S(1)} %get-tuple-element.8), channel_id=1, source_target_pairs={{0,1},{1,2},{4,5},{5,6},{8,9},{9,10},{12,13},{13,14},{16,17},{17,1... | collective-permute-start | bytes 786440 | tf_op jit(solution)/shard_map/ppermute | solution.py:107
  123.3 4.4 %collective-permute-start.37 = (f32[256,256]{0,1:T(8,128)S(1)}, f32[256,256]{0,1:T(8,128)S(1)}, u32[]{:S(2)}, u32[]{:S(2)}) collective-permute-start(f32[256,256]{0,1:T(8,128)S(1)} %get-tuple-element.18), channel_id=1, source_target_pairs={{0,1},{1,2},{4,5},{5,6},{8,9},{9,10},{12,13},{13,14},{16,17},{17,1... | collective-permute-start | bytes 786440 | tf_op jit(solution)/shard_map/ppermute | solution.py:107
  128.9 4.4 %collective-permute-start.20 = (f32[256,256]{0,1:T(8,128)S(1)}, f32[256,256]{0,1:T(8,128)S(1)}, u32[]{:S(2)}, u32[]{:S(2)}) collective-permute-start(f32[256,256]{0,1:T(8,128)S(1)} %get-tuple-element.6), channel_id=1, source_target_pairs={{0,1},{1,2},{2,3},{4,5},{5,6},{6,7},{8,9},{9,10},{10,11},{12,13},{... | collective-permute-start | bytes 786440 | tf_op jit(solution)/shard_map/ppermute | solution.py:107
  133.3 1.3 collective-permute-start.23
  134.8 4.6 %collective-permute-start.38 = (f32[256,256]{0,1:T(8,128)S(1)}, f32[256,256]{0,1:T(8,128)S(1)}, u32[]{:S(2)}, u32[]{:S(2)}) collective-permute-start(f32[256,256]{0,1:T(8,128)S(1)} %get-tuple-element.16), channel_id=1, source_target_pairs={{0,1},{1,2},{2,3},{4,5},{5,6},{6,7},{8,9},{9,10},{10,11},{12,13},{... | collective-permute-start | bytes 786440 | tf_op jit(solution)/shard_map/ppermute | solution.py:107
  141.7 3.1 %collective-permute-done.38 = f32[256,256]{0,1:T(8,128)S(1)} collective-permute-done((f32[256,256]{0,1:T(8,128)S(1)}, f32[256,256]{0,1:T(8,128)S(1)}, u32[]{:S(2)}, u32[]{:S(2)}) %collective-permute-start.38) | collective-permute-done | bytes 262176 | tf_op jit(solution)/shard_map/ppermute | solution.py:107
  144.9 2.7 %collective-permute-done.41 = f32[256,256]{0,1:T(8,128)S(1)} collective-permute-done((f32[256,256]{0,1:T(8,128)S(1)}, f32[256,256]{0,1:T(8,128)S(1)}, u32[]{:S(2)}, u32[]{:S(2)}) %collective-permute-start.41) | collective-permute-done | bytes 262176 | tf_op jit(solution)/shard_map/ppermute | solution.py:108
  (127 shorter events, 44.1 us)
Async XLA Ops:
  0.0 17.3 %collective-permute-start.1 = (f32[256,512]{1,0:T(8,128)}, f32[256,512]{1,0:T(8,128)}, u32[]{:S(2)}, u32[]{:S(2)}) collective-permute-start(f32[256,512]{1,0:T(8,128)} %param.6), channel_id=1, source_target_pairs={{1,0},{2,1},{3,2},{5,4},{6,5},{7,6},{9,8},{10,9},{11,10},{13,12},{... | collective-permute-start | bytes 1572872 | tf_op jit(solution)/shard_map/ppermute | solution.py:87
  1.4 17.2 %collective-permute-start = (f32[256,512]{1,0:T(8,128)}, f32[256,512]{1,0:T(8,128)}, u32[]{:S(2)}, u32[]{:S(2)}) collective-permute-start(f32[256,512]{1,0:T(8,128)} %param.6), channel_id=1, source_target_pairs={{0,1},{1,2},{2,3},{4,5},{5,6},{6,7},{8,9},{9,10},{10,11},{12,13},{... | collective-permute-start | bytes 1572872 | tf_op jit(solution)/shard_map/ppermute | solution.py:86
  17.3 15.2 %collective-permute-start.3 = (f32[256,512]{1,0:T(8,128)}, f32[256,512]{1,0:T(8,128)S(1)}, u32[]{:S(2)}, u32[]{:S(2)}) collective-permute-start(f32[256,512]{1,0:T(8,128)} %collective-permute-done.1), channel_id=1, source_target_pairs={{1,0},{2,1},{5,4},{6,5},{9,8},{10,9},{13,12},{14,13},{17,16},{18,1... | collective-permute-start | bytes 1572872 | tf_op jit(solution)/shard_map/ppermute | solution.py:87
  18.6 15.2 %collective-permute-start.2 = (f32[256,512]{1,0:T(8,128)}, f32[256,512]{1,0:T(8,128)S(1)}, u32[]{:S(2)}, u32[]{:S(2)}) collective-permute-start(f32[256,512]{1,0:T(8,128)} %collective-permute-done), channel_id=1, source_target_pairs={{1,2},{2,3},{5,6},{6,7},{9,10},{10,11},{13,14},{14,15},{17,18},{18... | collective-permute-start | bytes 1572872 | tf_op jit(solution)/shard_map/ppermute | solution.py:86
  32.5 14.1 %collective-permute-start.5 = (f32[256,512]{1,0:T(8,128)S(1)}, f32[256,512]{1,0:T(8,128)S(1)}, u32[]{:S(2)}, u32[]{:S(2)}) collective-permute-start(f32[256,512]{1,0:T(8,128)S(1)} %collective-permute-done.3), channel_id=1, source_target_pairs={{1,0},{5,4},{9,8},{13,12},{17,16},{21,20},{25,24},{29,28}} | collective-permute-start | bytes 1572872 | tf_op jit(solution)/shard_map/ppermute | solution.py:87
  33.8 13.4 %collective-permute-start.4 = (f32[256,512]{1,0:T(8,128)S(1)}, f32[256,512]{1,0:T(8,128)S(1)}, u32[]{:S(2)}, u32[]{:S(2)}) collective-permute-start(f32[256,512]{1,0:T(8,128)S(1)} %collective-permute-done.2), channel_id=1, source_target_pairs={{2,3},{6,7},{10,11},{14,15},{18,19},{22,23},{26,27},{30,31}} | collective-permute-start | bytes 1572872 | tf_op jit(solution)/shard_map/ppermute | solution.py:86
  50.1 6.4 %collective-permute-start.7 = (f32[512,64]{0,1:T(8,128)S(1)}, f32[512,64]{0,1:T(8,128)S(1)}, u32[]{:S(2)}, u32[]{:S(2)}) collective-permute-start(f32[512,64]{0,1:T(8,128)S(1)} %slice_select_fusion.3), channel_id=1, source_target_pairs={{0,8},{4,12},{8,0},{12,4},{16,24},{20,28},{24,16},{28,20},{1,9},{5... | collective-permute-start | bytes 393224 | tf_op jit(solution)/shard_map/ppermute | solution.py:15
  51.2 7.3 %collective-permute-start.25 = (f32[512,64]{0,1:T(8,128)S(1)}, f32[512,64]{0,1:T(8,128)S(1)}, u32[]{:S(2)}, u32[]{:S(2)}) collective-permute-start(f32[512,64]{0,1:T(8,128)S(1)} %slice_select_fusion.2), channel_id=1, source_target_pairs={{0,8},{4,12},{8,0},{12,4},{16,24},{20,28},{24,16},{28,20},{1,9},{5... | collective-permute-start | bytes 393224 | tf_op jit(solution)/shard_map/ppermute | solution.py:15
  56.6 4.8 %collective-permute-start.8 = (f32[512,32]{0,1:T(8,128)S(1)}, f32[512,32]{0,1:T(8,128)S(1)}, u32[]{:S(2)}, u32[]{:S(2)}) collective-permute-start(f32[512,32]{0,1:T(8,128)S(1)} %slice_select_fusion.5), channel_id=1, source_target_pairs={{0,16},{4,20},{8,24},{12,28},{16,0},{20,4},{24,8},{28,12},{1,17},{... | collective-permute-start | bytes 196616 | tf_op jit(solution)/shard_map/ppermute | solution.py:15
  58.6 4.8 %collective-permute-start.26 = (f32[512,32]{0,1:T(8,128)S(1)}, f32[512,32]{0,1:T(8,128)S(1)}, u32[]{:S(2)}, u32[]{:S(2)}) collective-permute-start(f32[512,32]{0,1:T(8,128)S(1)} %slice_select_fusion.4), channel_id=1, source_target_pairs={{0,16},{4,20},{8,24},{12,28},{16,0},{20,4},{24,8},{28,12},{1,17},{... | collective-permute-start | bytes 196616 | tf_op jit(solution)/shard_map/ppermute | solution.py:15
  61.9 3.4 %collective-permute-start.9 = (f32[512,32]{0,1:T(8,128)S(1)}, f32[512,32]{0,1:T(8,128)S(1)}, u32[]{:S(2)}, u32[]{:S(2)}) collective-permute-start(f32[512,32]{0,1:T(8,128)S(1)} %convolution_bitcast_fusion.3), channel_id=1, source_target_pairs={{0,1},{4,5},{8,9},{12,13},{16,17},{20,21},{24,25},{28,29}} | collective-permute-start | bytes 196616 | tf_op jit(solution)/shard_map/ppermute | solution.py:118
  64.0 3.2 %collective-permute-start.27 = (f32[512,32]{0,1:T(8,128)S(1)}, f32[512,32]{0,1:T(8,128)S(1)}, u32[]{:S(2)}, u32[]{:S(2)}) collective-permute-start(f32[512,32]{0,1:T(8,128)S(1)} %convolution_bitcast_fusion.1), channel_id=1, source_target_pairs={{0,1},{4,5},{8,9},{12,13},{16,17},{20,21},{24,25},{28,29}} | collective-permute-start | bytes 196616 | tf_op jit(solution)/shard_map/ppermute | solution.py:118
  65.8 2.5 %collective-permute-start.10 = (f32[512,32]{0,1:T(8,128)S(1)}, f32[512,32]{0,1:T(8,128)S(1)}, u32[]{:S(2)}, u32[]{:S(2)}) collective-permute-start(f32[512,32]{0,1:T(8,128)S(1)} %convolution_add_fusion.13), channel_id=1, source_target_pairs={{1,2},{5,6},{9,10},{13,14},{17,18},{21,22},{25,26},{29,30}} | collective-permute-start | bytes 196616 | tf_op jit(solution)/shard_map/ppermute | solution.py:118
  77.1 16.1 %collective-permute-start.14 = (f32[512,32]{0,1:T(8,128)S(1)}, f32[512,32]{0,1:T(8,128)S(1)}, u32[]{:S(2)}, u32[]{:S(2)}) collective-permute-start(f32[512,32]{0,1:T(8,128)S(1)} %convolution_add_fusion.9), channel_id=1, source_target_pairs={{1,0},{5,4},{9,8},{13,12},{17,16},{21,20},{25,24},{29,28}} | collective-permute-start | bytes 196616 | tf_op jit(solution)/shard_map/ppermute | solution.py:126
  78.8 16.7 %collective-permute-start.32 = (f32[512,32]{0,1:T(8,128)S(1)}, f32[512,32]{0,1:T(8,128)S(1)}, u32[]{:S(2)}, u32[]{:S(2)}) collective-permute-start(f32[512,32]{0,1:T(8,128)S(1)} %convolution_add_fusion.4), channel_id=1, source_target_pairs={{1,0},{5,4},{9,8},{13,12},{17,16},{21,20},{25,24},{29,28}} | collective-permute-start | bytes 196616 | tf_op jit(solution)/shard_map/ppermute | solution.py:126
  93.6 4.3 %collective-permute-start.15 = (f32[512,32]{0,1:T(8,128)S(1)}, f32[512,32]{0,1:T(8,128)S(1)}, u32[]{:S(2)}, u32[]{:S(2)}) collective-permute-start(f32[512,32]{0,1:T(8,128)S(1)} %get-tuple-element.24), channel_id=1, source_target_pairs={{0,16},{4,20},{8,24},{12,28},{16,0},{20,4},{24,8},{28,12},{1,17},{... | collective-permute-start | bytes 196616 | tf_op jit(solution)/shard_map/ppermute | solution.py:15
  95.9 4.3 %collective-permute-start.33 = (f32[512,32]{0,1:T(8,128)S(1)}, f32[512,32]{0,1:T(8,128)S(1)}, u32[]{:S(2)}, u32[]{:S(2)}) collective-permute-start(f32[512,32]{0,1:T(8,128)S(1)} %get-tuple-element.22), channel_id=1, source_target_pairs={{0,16},{4,20},{8,24},{12,28},{16,0},{20,4},{24,8},{28,12},{1,17},{... | collective-permute-start | bytes 196616 | tf_op jit(solution)/shard_map/ppermute | solution.py:15
  98.0 5.3 %collective-permute-start.16 = (f32[512,64]{0,1:T(8,128)S(1)}, f32[512,64]{0,1:T(8,128)S(1)}, u32[]{:S(2)}, u32[]{:S(2)}) collective-permute-start(f32[512,64]{0,1:T(8,128)S(1)} %constant_dynamic-update-slice_fusion.10), channel_id=1, source_target_pairs={{0,8},{4,12},{8,0},{12,4},{16,24},{20,28},{24,16},{28,20},{1,9},{5... | collective-permute-start | bytes 393224 | tf_op jit(solution)/shard_map/ppermute | solution.py:15
  100.3 5.0 %collective-permute-start.34 = (f32[512,64]{0,1:T(8,128)S(1)}, f32[512,64]{0,1:T(8,128)S(1)}, u32[]{:S(2)}, u32[]{:S(2)}) collective-permute-start(f32[512,64]{0,1:T(8,128)S(1)} %constant_dynamic-update-slice_fusion.4), channel_id=1, source_target_pairs={{0,8},{4,12},{8,0},{12,4},{16,24},{20,28},{24,16},{28,20},{1,9},{5... | collective-permute-start | bytes 393224 | tf_op jit(solution)/shard_map/ppermute | solution.py:15
  104.0 2.6 %collective-permute-start.17 = (f32[512,128]{0,1:T(8,128)}, f32[512,128]{0,1:T(8,128)}, u32[]{:S(2)}, u32[]{:S(2)}) collective-permute-start(f32[512,128]{0,1:T(8,128)} %constant_dynamic-update-slice_fusion.8), channel_id=1, source_target_pairs={{0,4},{4,0},{8,12},{12,8},{16,20},{20,16},{24,28},{28,24},{1,5},{5... | collective-permute-start | bytes 786440 | tf_op jit(solution)/shard_map/ppermute | solution.py:15
  109.2 8.4 %collective-permute-start.18 = (f32[256,256]{0,1:T(8,128)S(1)}, f32[256,256]{0,1:T(8,128)S(1)}, u32[]{:S(2)}, u32[]{:S(2)}) collective-permute-start(f32[256,256]{0,1:T(8,128)S(1)} %get-tuple-element.10), channel_id=1, source_target_pairs={{0,1},{4,5},{8,9},{12,13},{16,17},{20,21},{24,25},{28,29}} | collective-permute-start | bytes 786440 | tf_op jit(solution)/shard_map/ppermute | solution.py:107
  111.0 6.6 %collective-permute-start.21 = (f32[256,256]{0,1:T(8,128)S(1)}, f32[256,256]{0,1:T(8,128)S(1)}, u32[]{:S(2)}, u32[]{:S(2)}) collective-permute-start(f32[256,256]{0,1:T(8,128)S(1)} %get-tuple-element.9), channel_id=1, source_target_pairs={{3,2},{7,6},{11,10},{15,14},{19,18},{23,22},{27,26},{31,30}} | collective-permute-start | bytes 786440 | tf_op jit(solution)/shard_map/ppermute | solution.py:108
  112.7 10.5 %collective-permute-start.36 = (f32[256,256]{0,1:T(8,128)S(1)}, f32[256,256]{0,1:T(8,128)S(1)}, u32[]{:S(2)}, u32[]{:S(2)}) collective-permute-start(f32[256,256]{0,1:T(8,128)S(1)} %get-tuple-element.20), channel_id=1, source_target_pairs={{0,1},{4,5},{8,9},{12,13},{16,17},{20,21},{24,25},{28,29}} | collective-permute-start | bytes 786440 | tf_op jit(solution)/shard_map/ppermute | solution.py:107
  114.0 9.2 %collective-permute-start.39 = (f32[256,256]{0,1:T(8,128)S(1)}, f32[256,256]{0,1:T(8,128)S(1)}, u32[]{:S(2)}, u32[]{:S(2)}) collective-permute-start(f32[256,256]{0,1:T(8,128)S(1)} %get-tuple-element.19), channel_id=1, source_target_pairs={{3,2},{7,6},{11,10},{15,14},{19,18},{23,22},{27,26},{31,30}} | collective-permute-start | bytes 786440 | tf_op jit(solution)/shard_map/ppermute | solution.py:108
  117.7 11.1 %collective-permute-start.19 = (f32[256,256]{0,1:T(8,128)S(1)}, f32[256,256]{0,1:T(8,128)S(1)}, u32[]{:S(2)}, u32[]{:S(2)}) collective-permute-start(f32[256,256]{0,1:T(8,128)S(1)} %get-tuple-element.8), channel_id=1, source_target_pairs={{0,1},{1,2},{4,5},{5,6},{8,9},{9,10},{12,13},{13,14},{16,17},{17,1... | collective-permute-start | bytes 786440 | tf_op jit(solution)/shard_map/ppermute | solution.py:107
  122.1 6.7 %collective-permute-start.22 = (f32[256,256]{0,1:T(8,128)S(1)}, f32[256,256]{0,1:T(8,128)S(1)}, u32[]{:S(2)}, u32[]{:S(2)}) collective-permute-start(f32[256,256]{0,1:T(8,128)S(1)} %get-tuple-element.7), channel_id=1, source_target_pairs={{2,1},{3,2},{6,5},{7,6},{10,9},{11,10},{14,13},{15,14},{18,17},{19... | collective-permute-start | bytes 786440 | tf_op jit(solution)/shard_map/ppermute | solution.py:108
  123.3 11.3 %collective-permute-start.37 = (f32[256,256]{0,1:T(8,128)S(1)}, f32[256,256]{0,1:T(8,128)S(1)}, u32[]{:S(2)}, u32[]{:S(2)}) collective-permute-start(f32[256,256]{0,1:T(8,128)S(1)} %get-tuple-element.18), channel_id=1, source_target_pairs={{0,1},{1,2},{4,5},{5,6},{8,9},{9,10},{12,13},{13,14},{16,17},{17,1... | collective-permute-start | bytes 786440 | tf_op jit(solution)/shard_map/ppermute | solution.py:107
  127.7 6.9 %collective-permute-start.40 = (f32[256,256]{0,1:T(8,128)S(1)}, f32[256,256]{0,1:T(8,128)S(1)}, u32[]{:S(2)}, u32[]{:S(2)}) collective-permute-start(f32[256,256]{0,1:T(8,128)S(1)} %get-tuple-element.17), channel_id=1, source_target_pairs={{2,1},{3,2},{6,5},{7,6},{10,9},{11,10},{14,13},{15,14},{18,17},{19... | collective-permute-start | bytes 786440 | tf_op jit(solution)/shard_map/ppermute | solution.py:108
  128.9 11.7 %collective-permute-start.20 = (f32[256,256]{0,1:T(8,128)S(1)}, f32[256,256]{0,1:T(8,128)S(1)}, u32[]{:S(2)}, u32[]{:S(2)}) collective-permute-start(f32[256,256]{0,1:T(8,128)S(1)} %get-tuple-element.6), channel_id=1, source_target_pairs={{0,1},{1,2},{2,3},{4,5},{5,6},{6,7},{8,9},{9,10},{10,11},{12,13},{... | collective-permute-start | bytes 786440 | tf_op jit(solution)/shard_map/ppermute | solution.py:107
  133.3 8.3 %collective-permute-start.23 = (f32[256,256]{0,1:T(8,128)S(1)}, f32[256,256]{0,1:T(8,128)S(1)}, u32[]{:S(2)}, u32[]{:S(2)}) collective-permute-start(f32[256,256]{0,1:T(8,128)S(1)} %get-tuple-element.5), channel_id=1, source_target_pairs={{1,0},{2,1},{3,2},{5,4},{6,5},{7,6},{9,8},{10,9},{11,10},{13,12},{... | collective-permute-start | bytes 786440 | tf_op jit(solution)/shard_map/ppermute | solution.py:108
  134.8 10.1 %collective-permute-start.38 = (f32[256,256]{0,1:T(8,128)S(1)}, f32[256,256]{0,1:T(8,128)S(1)}, u32[]{:S(2)}, u32[]{:S(2)}) collective-permute-start(f32[256,256]{0,1:T(8,128)S(1)} %get-tuple-element.16), channel_id=1, source_target_pairs={{0,1},{1,2},{2,3},{4,5},{5,6},{6,7},{8,9},{9,10},{10,11},{12,13},{... | collective-permute-start | bytes 786440 | tf_op jit(solution)/shard_map/ppermute | solution.py:107
  139.3 8.3 %collective-permute-start.41 = (f32[256,256]{0,1:T(8,128)S(1)}, f32[256,256]{0,1:T(8,128)S(1)}, u32[]{:S(2)}, u32[]{:S(2)}) collective-permute-start(f32[256,256]{0,1:T(8,128)S(1)} %get-tuple-element.15), channel_id=1, source_target_pairs={{1,0},{2,1},{3,2},{5,4},{6,5},{7,6},{9,8},{10,9},{11,10},{13,12},{... | collective-permute-start | bytes 786440 | tf_op jit(solution)/shard_map/ppermute | solution.py:108
  (13 other events, 72.9 us)

commit v25 on v24

--- a/solution.py
+++ b/solution.py
@@ -85,8 +85,8 @@
         leftward = [(i + 1, i) for i in range(count - 1 - step)]
         from_left = lax.ppermute(from_left, "aux", rightward)
         from_right = lax.ppermute(from_right, "aux", leftward)
-        gamma = gamma + product(columns(index - 1 - step), from_left)
-        gamma = gamma + product(columns(index + 1 + step), from_right)
+        both_columns = jnp.concatenate([columns(index - 1 - step), columns(index + 1 + step)], axis=1)
+        gamma = gamma + product(both_columns, jnp.concatenate([from_left, from_right], axis=0))
     return gamma
 
 

time: 150 us -> 152 us (1.013)
  waiting for transfers between devices: 58.2 us -> 60 us
    ppermute x3, waiting for transfers between devices: 0.01 us -> 9.41 us  [gamma_over_aux(): from_left = lax.ppermute(from_left, 'aux', rightward)]
    ppermute x3, waiting for transfers between devices: 23.4 us -> 17.5 us  [gamma_over_aux(): from_right = lax.ppermute(from_right, 'aux', leftward)]
    dot_general x24 -> x21, matrix products: 16.3 us -> 14.9 us  [product(): jnp.dot(left, right, precision=lax.Precision.HIGH, preferred_element_type...]
    unnamed x7 -> x9, local copies, waits for them, and re-layouts: 2.93 us -> 3.63 us
  transfers between devices with their start and end apart: 42 -> 42, of which waited for: 20 -> 21; matrix products, arithmetic and copies ran while one was open for 17% -> 16% of each run, Pallas kernels for 0% -> 0%
where the time goes in v25:
time: 152 us; the launch traced here: 151 us
  starting transfers between devices  61.1 us (40%)
  waiting for transfers between devices  60 us (39%)
  matrix products  17 us (11%)
  local copies, waits for them, and re-layouts  9.59 us (6%)
  other arithmetic  2.76 us (2%)
    ppermute x6, starting transfers between devices, reduce_over_aux(): lax.ppermute(to_right + block(index + count - 1 - step), 'aux', rightward)  20.8 us
    ppermute x3, waiting for transfers between devices, gamma_over_aux(): from_right = lax.ppermute(from_right, 'aux', leftward)  17.5 us
    dot_general x21, matrix products, product(): jnp.dot(left, right, precision=lax.Precision.HIGH, preferred_element_type...  14.9 us
    ppermute x6, waiting for transfers between devices, solve(): arriving = arriving + lax.ppermute(value, 'aux', [(sender, sender - 1)])  12.7 us
    ppermute x12, starting transfers between devices, swap(): return lax.ppermute(array, axis, [(i, i ^ bit) for i in range(count)])  12.2 us
    ppermute x3, waiting for transfers between devices, gamma_over_aux(): from_left = lax.ppermute(from_left, 'aux', rightward)  9.41 us
    ppermute x12, waiting for transfers between devices, swap(): return lax.ppermute(array, axis, [(i, i ^ bit) for i in range(count)])  9.15 us
    ppermute x3, starting transfers between devices, gamma_over_aux(): from_left = lax.ppermute(from_left, 'aux', rightward)  8 us
  transfers between devices with their start and end apart: 42, of which 21 were waited for; matrix products, arithmetic and copies ran while one was open for 16% of the time, Pallas kernels for 0%

profile of v25, /device:TPU:0, one launch (start us, length us, event | category | flops | bytes accessed | tf_op | source)
XLA Modules:
  0.0 151.4 jit_solution(6372789537994122570)
XLA Ops:
  0.0 5.8 %collective-permute-start = (f32[256,512]{1,0:T(8,128)}, f32[256,512]{1,0:T(8,128)}, u32[]{:S(2)}, u32[]{:S(2)}) collective-permute-start(f32[256,512]{1,0:T(8,128)} %param.6), channel_id=1, source_target_pairs={{0,1},{1,2},{2,3},{4,5},{5,6},{6,7},{8,9},{9,10},{10,11},{12,13},{... | collective-permute-start | bytes 1572872 | tf_op jit(solution)/shard_map/ppermute | solution.py:86
  7.1 9.4 %collective-permute-done = f32[256,512]{1,0:T(8,128)} collective-permute-done((f32[256,512]{1,0:T(8,128)}, f32[256,512]{1,0:T(8,128)}, u32[]{:S(2)}, u32[]{:S(2)}) %collective-permute-start) | collective-permute-done | bytes 524320 | tf_op jit(solution)/shard_map/ppermute | solution.py:86
  16.5 1.5 collective-permute-start.2
  18.0 3.4 %collective-permute-done.1 = f32[256,512]{1,0:T(8,128)} collective-permute-done((f32[256,512]{1,0:T(8,128)}, f32[256,512]{1,0:T(8,128)}, u32[]{:S(2)}, u32[]{:S(2)}) %collective-permute-start.1) | collective-permute-done | bytes 524320 | tf_op jit(solution)/shard_map/ppermute | solution.py:87
  22.8 2.9 %copy.8 = f32[512,1024]{0,1:T(8,128)} copy(f32[512,1024]{1,0:T(8,128)} %param.5) | data formatting | bytes 4194304 | tf_op args[0]
  26.0 1.8 %bitcast_multiply_fusion = f32[512,1024]{0,1:T(8,128)S(1)} fusion(f32[512,1024]{0,1:T(8,128)} %copy.8, f32[512,16]{0,1:T(8,128)S(1)} %reshape.6), kind=kLoop, calls=%fused_computation | loop fusion | flops 524288 | bytes 4227072 | tf_op jit(solution)/shard_map/mul | solution.py:23
  30.2 6.0 %collective-permute-done.3 = f32[256,512]{1,0:T(8,128)} collective-permute-done((f32[256,512]{1,0:T(8,128)}, f32[256,512]{1,0:T(8,128)}, u32[]{:S(2)}, u32[]{:S(2)}) %collective-permute-start.3) | collective-permute-done | bytes 524320 | tf_op jit(solution)/shard_map/ppermute | solution.py:87
  37.6 2.2 %convolution_add_fusion.2 = f32[512,512]{0,1:T(8,128)S(1)} fusion(f32[512,512]{0,1:T(8,128)S(1)} %fusion.18, f32[512,256]{0,1:T(8,128)S(1)} %get-tuple-element.9, f32[512,256]{0,1:T(8,128)S(1)} %get-tuple-element.10, f32[256,512]{1,0:T(8,128)} %collective-permute-done.1, f32[256,512]{1,0:T(8,128)} %collective-permute-done), kind=kOutput, calls=%fused_computation.3 | convolution fusion | flops 806092800 | bytes 4194304 | tf_op jit(solution)/shard_map/dot_general | solution.py:27
  39.8 2.2 %convolution_add_fusion.1 = f32[512,512]{0,1:T(8,128)S(1)} fusion(f32[512,512]{0,1:T(8,128)S(1)} %convolution_add_fusion.2, f32[512,256]{0,1:T(8,128)S(1)} %get-tuple-element.7, f32[512,256]{0,1:T(8,128)S(1)} %get-tuple-element.8, f32[256,512]{1,0:T(8,128)} %collective-permute-done.3, f32[256,512]{1,0:T(8,128)} %collective-permute-done.2), kind=kOutput, calls=%fused_computation.2 | convolution fusion | flops 806092800 | bytes 4194304 | tf_op jit(solution)/shard_map/dot_general | solution.py:27
  42.1 8.0 %collective-permute-done.5 = f32[256,512]{1,0:T(8,128)S(1)} collective-permute-done((f32[256,512]{1,0:T(8,128)}, f32[256,512]{1,0:T(8,128)S(1)}, u32[]{:S(2)}, u32[]{:S(2)}) %collective-permute-start.5) | collective-permute-done | bytes 524320 | tf_op jit(solution)/shard_map/ppermute | solution.py:87
  53.4 1.6 %collective-permute-start.7 = (f32[512,64]{0,1:T(8,128)S(1)}, f32[512,64]{0,1:T(8,128)S(1)}, u32[]{:S(2)}, u32[]{:S(2)}) collective-permute-start(f32[512,64]{0,1:T(8,128)S(1)} %slice_select_fusion.3), channel_id=1, source_target_pairs={{0,8},{4,12},{8,0},{12,4},{16,24},{20,28},{24,16},{28,20},{1,9},{5... | collective-permute-start | bytes 393224 | tf_op jit(solution)/shard_map/ppermute | solution.py:15
  55.6 4.2 %collective-permute-done.7 = f32[512,64]{0,1:T(8,128)S(1)} collective-permute-done((f32[512,64]{0,1:T(8,128)S(1)}, f32[512,64]{0,1:T(8,128)S(1)}, u32[]{:S(2)}, u32[]{:S(2)}) %collective-permute-start.7) | collective-permute-done | bytes 131104 | tf_op jit(solution)/shard_map/ppermute | solution.py:15
  59.9 1.6 %collective-permute-start.8 = (f32[512,32]{0,1:T(8,128)S(1)}, f32[512,32]{0,1:T(8,128)S(1)}, u32[]{:S(2)}, u32[]{:S(2)}) collective-permute-start(f32[512,32]{0,1:T(8,128)S(1)} %slice_select_fusion.5), channel_id=1, source_target_pairs={{0,16},{4,20},{8,24},{12,28},{16,0},{20,4},{24,8},{28,12},{1,17},{... | collective-permute-start | bytes 196616 | tf_op jit(solution)/shard_map/ppermute | solution.py:15
  61.9 1.6 %collective-permute-start.26 = (f32[512,32]{0,1:T(8,128)S(1)}, f32[512,32]{0,1:T(8,128)S(1)}, u32[]{:S(2)}, u32[]{:S(2)}) collective-permute-start(f32[512,32]{0,1:T(8,128)S(1)} %slice_select_fusion.4), channel_id=1, source_target_pairs={{0,16},{4,20},{8,24},{12,28},{16,0},{20,4},{24,8},{28,12},{1,17},{... | collective-permute-start | bytes 196616 | tf_op jit(solution)/shard_map/ppermute | solution.py:15
  65.2 1.6 %collective-permute-start.9 = (f32[512,32]{0,1:T(8,128)S(1)}, f32[512,32]{0,1:T(8,128)S(1)}, u32[]{:S(2)}, u32[]{:S(2)}) collective-permute-start(f32[512,32]{0,1:T(8,128)S(1)} %convolution_bitcast_fusion.3), channel_id=1, source_target_pairs={{0,1},{4,5},{8,9},{12,13},{16,17},{20,21},{24,25},{28,29}} | collective-permute-start | bytes 196616 | tf_op jit(solution)/shard_map/ppermute | solution.py:118
  67.4 1.3 collective-permute-start.27
  80.5 1.3 collective-permute-start.14
  83.5 12.4 %collective-permute-done.14 = f32[512,32]{0,1:T(8,128)S(1)} collective-permute-done((f32[512,32]{0,1:T(8,128)S(1)}, f32[512,32]{0,1:T(8,128)S(1)}, u32[]{:S(2)}, u32[]{:S(2)}) %collective-permute-start.14) | collective-permute-done | bytes 65568 | tf_op jit(solution)/shard_map/ppermute | solution.py:126
  96.4 1.6 %collective-permute-start.15 = (f32[512,32]{0,1:T(8,128)S(1)}, f32[512,32]{0,1:T(8,128)S(1)}, u32[]{:S(2)}, u32[]{:S(2)}) collective-permute-start(f32[512,32]{0,1:T(8,128)S(1)} %get-tuple-element.30), channel_id=1, source_target_pairs={{0,16},{4,20},{8,24},{12,28},{16,0},{20,4},{24,8},{28,12},{1,17},{... | collective-permute-start | bytes 196616 | tf_op jit(solution)/shard_map/ppermute | solution.py:15
  98.7 1.6 %collective-permute-start.33 = (f32[512,32]{0,1:T(8,128)S(1)}, f32[512,32]{0,1:T(8,128)S(1)}, u32[]{:S(2)}, u32[]{:S(2)}) collective-permute-start(f32[512,32]{0,1:T(8,128)S(1)} %get-tuple-element.28), channel_id=1, source_target_pairs={{0,16},{4,20},{8,24},{12,28},{16,0},{20,4},{24,8},{28,12},{1,17},{... | collective-permute-start | bytes 196616 | tf_op jit(solution)/shard_map/ppermute | solution.py:15
  100.7 1.6 %collective-permute-start.16 = (f32[512,64]{0,1:T(8,128)S(1)}, f32[512,64]{0,1:T(8,128)S(1)}, u32[]{:S(2)}, u32[]{:S(2)}) collective-permute-start(f32[512,64]{0,1:T(8,128)S(1)} %constant_dynamic-update-slice_fusion.10), channel_id=1, source_target_pairs={{0,8},{4,12},{8,0},{12,4},{16,24},{20,28},{24,16},{28,20},{1,9},{5... | collective-permute-start | bytes 393224 | tf_op jit(solution)/shard_map/ppermute | solution.py:15
  103.0 1.6 %collective-permute-start.34 = (f32[512,64]{0,1:T(8,128)S(1)}, f32[512,64]{0,1:T(8,128)S(1)}, u32[]{:S(2)}, u32[]{:S(2)}) collective-permute-start(f32[512,64]{0,1:T(8,128)S(1)} %constant_dynamic-update-slice_fusion.4), channel_id=1, source_target_pairs={{0,8},{4,12},{8,0},{12,4},{16,24},{20,28},{24,16},{28,20},{1,9},{5... | collective-permute-start | bytes 393224 | tf_op jit(solution)/shard_map/ppermute | solution.py:15
  106.7 1.3 collective-permute-done.34
  112.0 1.7 %collective-permute-start.18 = (f32[256,256]{0,1:T(8,128)S(1)}, f32[256,256]{0,1:T(8,128)S(1)}, u32[]{:S(2)}, u32[]{:S(2)}) collective-permute-start(f32[256,256]{0,1:T(8,128)S(1)} %get-tuple-element.16), channel_id=1, source_target_pairs={{0,1},{4,5},{8,9},{12,13},{16,17},{20,21},{24,25},{28,29}} | collective-permute-start | bytes 786440 | tf_op jit(solution)/shard_map/ppermute | solution.py:107
  115.5 1.3 collective-permute-start.36
  117.5 2.9 %collective-permute-done.18 = f32[256,256]{0,1:T(8,128)S(1)} collective-permute-done((f32[256,256]{0,1:T(8,128)S(1)}, f32[256,256]{0,1:T(8,128)S(1)}, u32[]{:S(2)}, u32[]{:S(2)}) %collective-permute-start.18) | collective-permute-done | bytes 262176 | tf_op jit(solution)/shard_map/ppermute | solution.py:107
  120.4 4.4 %collective-permute-start.19 = (f32[256,256]{0,1:T(8,128)S(1)}, f32[256,256]{0,1:T(8,128)S(1)}, u32[]{:S(2)}, u32[]{:S(2)}) collective-permute-start(f32[256,256]{0,1:T(8,128)S(1)} %get-tuple-element.14), channel_id=1, source_target_pairs={{0,1},{1,2},{4,5},{5,6},{8,9},{9,10},{12,13},{13,14},{16,17},{17,1... | collective-permute-start | bytes 786440 | tf_op jit(solution)/shard_map/ppermute | solution.py:107
  126.0 4.4 %collective-permute-start.37 = (f32[256,256]{0,1:T(8,128)S(1)}, f32[256,256]{0,1:T(8,128)S(1)}, u32[]{:S(2)}, u32[]{:S(2)}) collective-permute-start(f32[256,256]{0,1:T(8,128)S(1)} %get-tuple-element.24), channel_id=1, source_target_pairs={{0,1},{1,2},{4,5},{5,6},{8,9},{9,10},{12,13},{13,14},{16,17},{17,1... | collective-permute-start | bytes 786440 | tf_op jit(solution)/shard_map/ppermute | solution.py:107
  131.7 4.4 %collective-permute-start.20 = (f32[256,256]{0,1:T(8,128)S(1)}, f32[256,256]{0,1:T(8,128)S(1)}, u32[]{:S(2)}, u32[]{:S(2)}) collective-permute-start(f32[256,256]{0,1:T(8,128)S(1)} %get-tuple-element.12), channel_id=1, source_target_pairs={{0,1},{1,2},{2,3},{4,5},{5,6},{6,7},{8,9},{9,10},{10,11},{12,13},{... | collective-permute-start | bytes 786440 | tf_op jit(solution)/shard_map/ppermute | solution.py:107
  137.5 4.6 %collective-permute-start.38 = (f32[256,256]{0,1:T(8,128)S(1)}, f32[256,256]{0,1:T(8,128)S(1)}, u32[]{:S(2)}, u32[]{:S(2)}) collective-permute-start(f32[256,256]{0,1:T(8,128)S(1)} %get-tuple-element.22), channel_id=1, source_target_pairs={{0,1},{1,2},{2,3},{4,5},{5,6},{6,7},{8,9},{9,10},{10,11},{12,13},{... | collective-permute-start | bytes 786440 | tf_op jit(solution)/shard_map/ppermute | solution.py:107
  144.5 3.1 %collective-permute-done.38 = f32[256,256]{0,1:T(8,128)S(1)} collective-permute-done((f32[256,256]{0,1:T(8,128)S(1)}, f32[256,256]{0,1:T(8,128)S(1)}, u32[]{:S(2)}, u32[]{:S(2)}) %collective-permute-start.38) | collective-permute-done | bytes 262176 | tf_op jit(solution)/shard_map/ppermute | solution.py:107
  147.6 2.7 %collective-permute-done.41 = f32[256,256]{0,1:T(8,128)S(1)} collective-permute-done((f32[256,256]{0,1:T(8,128)S(1)}, f32[256,256]{0,1:T(8,128)S(1)}, u32[]{:S(2)}, u32[]{:S(2)}) %collective-permute-start.41) | collective-permute-done | bytes 262176 | tf_op jit(solution)/shard_map/ppermute | solution.py:108
  (127 shorter events, 44.4 us)
Async XLA Ops:
  0.0 16.5 %collective-permute-start = (f32[256,512]{1,0:T(8,128)}, f32[256,512]{1,0:T(8,128)}, u32[]{:S(2)}, u32[]{:S(2)}) collective-permute-start(f32[256,512]{1,0:T(8,128)} %param.6), channel_id=1, source_target_pairs={{0,1},{1,2},{2,3},{4,5},{5,6},{6,7},{8,9},{9,10},{10,11},{12,13},{... | collective-permute-start | bytes 1572872 | tf_op jit(solution)/shard_map/ppermute | solution.py:86
  5.8 15.6 %collective-permute-start.1 = (f32[256,512]{1,0:T(8,128)}, f32[256,512]{1,0:T(8,128)}, u32[]{:S(2)}, u32[]{:S(2)}) collective-permute-start(f32[256,512]{1,0:T(8,128)} %param.6), channel_id=1, source_target_pairs={{1,0},{2,1},{3,2},{5,4},{6,5},{7,6},{9,8},{10,9},{11,10},{13,12},{... | collective-permute-start | bytes 1572872 | tf_op jit(solution)/shard_map/ppermute | solution.py:87
  16.5 13.0 %collective-permute-start.2 = (f32[256,512]{1,0:T(8,128)}, f32[256,512]{1,0:T(8,128)}, u32[]{:S(2)}, u32[]{:S(2)}) collective-permute-start(f32[256,512]{1,0:T(8,128)} %collective-permute-done), channel_id=1, source_target_pairs={{1,2},{2,3},{5,6},{6,7},{9,10},{10,11},{13,14},{14,15},{17,18},{18... | collective-permute-start | bytes 1572872 | tf_op jit(solution)/shard_map/ppermute | solution.py:86
  21.4 14.8 %collective-permute-start.3 = (f32[256,512]{1,0:T(8,128)}, f32[256,512]{1,0:T(8,128)}, u32[]{:S(2)}, u32[]{:S(2)}) collective-permute-start(f32[256,512]{1,0:T(8,128)} %collective-permute-done.1), channel_id=1, source_target_pairs={{1,0},{2,1},{5,4},{6,5},{9,8},{10,9},{13,12},{14,13},{17,16},{18,1... | collective-permute-start | bytes 1572872 | tf_op jit(solution)/shard_map/ppermute | solution.py:87
  29.5 12.5 %collective-permute-start.4 = (f32[256,512]{1,0:T(8,128)}, f32[256,512]{1,0:T(8,128)S(1)}, u32[]{:S(2)}, u32[]{:S(2)}) collective-permute-start(f32[256,512]{1,0:T(8,128)} %collective-permute-done.2), channel_id=1, source_target_pairs={{2,3},{6,7},{10,11},{14,15},{18,19},{22,23},{26,27},{30,31}} | collective-permute-start | bytes 1572872 | tf_op jit(solution)/shard_map/ppermute | solution.py:86
  36.3 13.8 %collective-permute-start.5 = (f32[256,512]{1,0:T(8,128)}, f32[256,512]{1,0:T(8,128)S(1)}, u32[]{:S(2)}, u32[]{:S(2)}) collective-permute-start(f32[256,512]{1,0:T(8,128)} %collective-permute-done.3), channel_id=1, source_target_pairs={{1,0},{5,4},{9,8},{13,12},{17,16},{21,20},{25,24},{29,28}} | collective-permute-start | bytes 1572872 | tf_op jit(solution)/shard_map/ppermute | solution.py:87
  53.4 6.4 %collective-permute-start.7 = (f32[512,64]{0,1:T(8,128)S(1)}, f32[512,64]{0,1:T(8,128)S(1)}, u32[]{:S(2)}, u32[]{:S(2)}) collective-permute-start(f32[512,64]{0,1:T(8,128)S(1)} %slice_select_fusion.3), channel_id=1, source_target_pairs={{0,8},{4,12},{8,0},{12,4},{16,24},{20,28},{24,16},{28,20},{1,9},{5... | collective-permute-start | bytes 393224 | tf_op jit(solution)/shard_map/ppermute | solution.py:15
  55.0 6.8 %collective-permute-start.25 = (f32[512,64]{0,1:T(8,128)S(1)}, f32[512,64]{0,1:T(8,128)S(1)}, u32[]{:S(2)}, u32[]{:S(2)}) collective-permute-start(f32[512,64]{0,1:T(8,128)S(1)} %slice_select_fusion.2), channel_id=1, source_target_pairs={{0,8},{4,12},{8,0},{12,4},{16,24},{20,28},{24,16},{28,20},{1,9},{5... | collective-permute-start | bytes 393224 | tf_op jit(solution)/shard_map/ppermute | solution.py:15
  59.9 4.8 %collective-permute-start.8 = (f32[512,32]{0,1:T(8,128)S(1)}, f32[512,32]{0,1:T(8,128)S(1)}, u32[]{:S(2)}, u32[]{:S(2)}) collective-permute-start(f32[512,32]{0,1:T(8,128)S(1)} %slice_select_fusion.5), channel_id=1, source_target_pairs={{0,16},{4,20},{8,24},{12,28},{16,0},{20,4},{24,8},{28,12},{1,17},{... | collective-permute-start | bytes 196616 | tf_op jit(solution)/shard_map/ppermute | solution.py:15
  61.9 4.9 %collective-permute-start.26 = (f32[512,32]{0,1:T(8,128)S(1)}, f32[512,32]{0,1:T(8,128)S(1)}, u32[]{:S(2)}, u32[]{:S(2)}) collective-permute-start(f32[512,32]{0,1:T(8,128)S(1)} %slice_select_fusion.4), channel_id=1, source_target_pairs={{0,16},{4,20},{8,24},{12,28},{16,0},{20,4},{24,8},{28,12},{1,17},{... | collective-permute-start | bytes 196616 | tf_op jit(solution)/shard_map/ppermute | solution.py:15
  65.2 3.5 %collective-permute-start.9 = (f32[512,32]{0,1:T(8,128)S(1)}, f32[512,32]{0,1:T(8,128)S(1)}, u32[]{:S(2)}, u32[]{:S(2)}) collective-permute-start(f32[512,32]{0,1:T(8,128)S(1)} %convolution_bitcast_fusion.3), channel_id=1, source_target_pairs={{0,1},{4,5},{8,9},{12,13},{16,17},{20,21},{24,25},{28,29}} | collective-permute-start | bytes 196616 | tf_op jit(solution)/shard_map/ppermute | solution.py:118
  67.4 3.2 %collective-permute-start.27 = (f32[512,32]{0,1:T(8,128)S(1)}, f32[512,32]{0,1:T(8,128)S(1)}, u32[]{:S(2)}, u32[]{:S(2)}) collective-permute-start(f32[512,32]{0,1:T(8,128)S(1)} %convolution_bitcast_fusion.1), channel_id=1, source_target_pairs={{0,1},{4,5},{8,9},{12,13},{16,17},{20,21},{24,25},{28,29}} | collective-permute-start | bytes 196616 | tf_op jit(solution)/shard_map/ppermute | solution.py:118
  69.3 2.5 %collective-permute-start.10 = (f32[512,32]{0,1:T(8,128)S(1)}, f32[512,32]{0,1:T(8,128)S(1)}, u32[]{:S(2)}, u32[]{:S(2)}) collective-permute-start(f32[512,32]{0,1:T(8,128)S(1)} %convolution_add_fusion.12), channel_id=1, source_target_pairs={{1,2},{5,6},{9,10},{13,14},{17,18},{21,22},{25,26},{29,30}} | collective-permute-start | bytes 196616 | tf_op jit(solution)/shard_map/ppermute | solution.py:118
  80.5 15.5 %collective-permute-start.14 = (f32[512,32]{0,1:T(8,128)S(1)}, f32[512,32]{0,1:T(8,128)S(1)}, u32[]{:S(2)}, u32[]{:S(2)}) collective-permute-start(f32[512,32]{0,1:T(8,128)S(1)} %convolution_add_fusion.8), channel_id=1, source_target_pairs={{1,0},{5,4},{9,8},{13,12},{17,16},{21,20},{25,24},{29,28}} | collective-permute-start | bytes 196616 | tf_op jit(solution)/shard_map/ppermute | solution.py:126
  82.2 16.0 %collective-permute-start.32 = (f32[512,32]{0,1:T(8,128)S(1)}, f32[512,32]{0,1:T(8,128)S(1)}, u32[]{:S(2)}, u32[]{:S(2)}) collective-permute-start(f32[512,32]{0,1:T(8,128)S(1)} %convolution_add_fusion.3), channel_id=1, source_target_pairs={{1,0},{5,4},{9,8},{13,12},{17,16},{21,20},{25,24},{29,28}} | collective-permute-start | bytes 196616 | tf_op jit(solution)/shard_map/ppermute | solution.py:126
  96.4 4.3 %collective-permute-start.15 = (f32[512,32]{0,1:T(8,128)S(1)}, f32[512,32]{0,1:T(8,128)S(1)}, u32[]{:S(2)}, u32[]{:S(2)}) collective-permute-start(f32[512,32]{0,1:T(8,128)S(1)} %get-tuple-element.30), channel_id=1, source_target_pairs={{0,16},{4,20},{8,24},{12,28},{16,0},{20,4},{24,8},{28,12},{1,17},{... | collective-permute-start | bytes 196616 | tf_op jit(solution)/shard_map/ppermute | solution.py:15
  98.7 4.3 %collective-permute-start.33 = (f32[512,32]{0,1:T(8,128)S(1)}, f32[512,32]{0,1:T(8,128)S(1)}, u32[]{:S(2)}, u32[]{:S(2)}) collective-permute-start(f32[512,32]{0,1:T(8,128)S(1)} %get-tuple-element.28), channel_id=1, source_target_pairs={{0,16},{4,20},{8,24},{12,28},{16,0},{20,4},{24,8},{28,12},{1,17},{... | collective-permute-start | bytes 196616 | tf_op jit(solution)/shard_map/ppermute | solution.py:15
  100.7 5.3 %collective-permute-start.16 = (f32[512,64]{0,1:T(8,128)S(1)}, f32[512,64]{0,1:T(8,128)S(1)}, u32[]{:S(2)}, u32[]{:S(2)}) collective-permute-start(f32[512,64]{0,1:T(8,128)S(1)} %constant_dynamic-update-slice_fusion.10), channel_id=1, source_target_pairs={{0,8},{4,12},{8,0},{12,4},{16,24},{20,28},{24,16},{28,20},{1,9},{5... | collective-permute-start | bytes 393224 | tf_op jit(solution)/shard_map/ppermute | solution.py:15
  103.0 5.0 %collective-permute-start.34 = (f32[512,64]{0,1:T(8,128)S(1)}, f32[512,64]{0,1:T(8,128)S(1)}, u32[]{:S(2)}, u32[]{:S(2)}) collective-permute-start(f32[512,64]{0,1:T(8,128)S(1)} %constant_dynamic-update-slice_fusion.4), channel_id=1, source_target_pairs={{0,8},{4,12},{8,0},{12,4},{16,24},{20,28},{24,16},{28,20},{1,9},{5... | collective-permute-start | bytes 393224 | tf_op jit(solution)/shard_map/ppermute | solution.py:15
  106.7 2.6 %collective-permute-start.17 = (f32[512,128]{0,1:T(8,128)}, f32[512,128]{0,1:T(8,128)}, u32[]{:S(2)}, u32[]{:S(2)}) collective-permute-start(f32[512,128]{0,1:T(8,128)} %constant_dynamic-update-slice_fusion.8), channel_id=1, source_target_pairs={{0,4},{4,0},{8,12},{12,8},{16,20},{20,16},{24,28},{28,24},{1,5},{5... | collective-permute-start | bytes 786440 | tf_op jit(solution)/shard_map/ppermute | solution.py:15
  112.0 8.4 %collective-permute-start.18 = (f32[256,256]{0,1:T(8,128)S(1)}, f32[256,256]{0,1:T(8,128)S(1)}, u32[]{:S(2)}, u32[]{:S(2)}) collective-permute-start(f32[256,256]{0,1:T(8,128)S(1)} %get-tuple-element.16), channel_id=1, source_target_pairs={{0,1},{4,5},{8,9},{12,13},{16,17},{20,21},{24,25},{28,29}} | collective-permute-start | bytes 786440 | tf_op jit(solution)/shard_map/ppermute | solution.py:107
  113.7 6.6 %collective-permute-start.21 = (f32[256,256]{0,1:T(8,128)S(1)}, f32[256,256]{0,1:T(8,128)S(1)}, u32[]{:S(2)}, u32[]{:S(2)}) collective-permute-start(f32[256,256]{0,1:T(8,128)S(1)} %get-tuple-element.15), channel_id=1, source_target_pairs={{3,2},{7,6},{11,10},{15,14},{19,18},{23,22},{27,26},{31,30}} | collective-permute-start | bytes 786440 | tf_op jit(solution)/shard_map/ppermute | solution.py:108
  115.5 10.5 %collective-permute-start.36 = (f32[256,256]{0,1:T(8,128)S(1)}, f32[256,256]{0,1:T(8,128)S(1)}, u32[]{:S(2)}, u32[]{:S(2)}) collective-permute-start(f32[256,256]{0,1:T(8,128)S(1)} %get-tuple-element.26), channel_id=1, source_target_pairs={{0,1},{4,5},{8,9},{12,13},{16,17},{20,21},{24,25},{28,29}} | collective-permute-start | bytes 786440 | tf_op jit(solution)/shard_map/ppermute | solution.py:107
  116.8 9.2 %collective-permute-start.39 = (f32[256,256]{0,1:T(8,128)S(1)}, f32[256,256]{0,1:T(8,128)S(1)}, u32[]{:S(2)}, u32[]{:S(2)}) collective-permute-start(f32[256,256]{0,1:T(8,128)S(1)} %get-tuple-element.25), channel_id=1, source_target_pairs={{3,2},{7,6},{11,10},{15,14},{19,18},{23,22},{27,26},{31,30}} | collective-permute-start | bytes 786440 | tf_op jit(solution)/shard_map/ppermute | solution.py:108
  120.4 11.1 %collective-permute-start.19 = (f32[256,256]{0,1:T(8,128)S(1)}, f32[256,256]{0,1:T(8,128)S(1)}, u32[]{:S(2)}, u32[]{:S(2)}) collective-permute-start(f32[256,256]{0,1:T(8,128)S(1)} %get-tuple-element.14), channel_id=1, source_target_pairs={{0,1},{1,2},{4,5},{5,6},{8,9},{9,10},{12,13},{13,14},{16,17},{17,1... | collective-permute-start | bytes 786440 | tf_op jit(solution)/shard_map/ppermute | solution.py:107
  124.8 6.7 %collective-permute-start.22 = (f32[256,256]{0,1:T(8,128)S(1)}, f32[256,256]{0,1:T(8,128)S(1)}, u32[]{:S(2)}, u32[]{:S(2)}) collective-permute-start(f32[256,256]{0,1:T(8,128)S(1)} %get-tuple-element.13), channel_id=1, source_target_pairs={{2,1},{3,2},{6,5},{7,6},{10,9},{11,10},{14,13},{15,14},{18,17},{19... | collective-permute-start | bytes 786440 | tf_op jit(solution)/shard_map/ppermute | solution.py:108
  126.0 11.3 %collective-permute-start.37 = (f32[256,256]{0,1:T(8,128)S(1)}, f32[256,256]{0,1:T(8,128)S(1)}, u32[]{:S(2)}, u32[]{:S(2)}) collective-permute-start(f32[256,256]{0,1:T(8,128)S(1)} %get-tuple-element.24), channel_id=1, source_target_pairs={{0,1},{1,2},{4,5},{5,6},{8,9},{9,10},{12,13},{13,14},{16,17},{17,1... | collective-permute-start | bytes 786440 | tf_op jit(solution)/shard_map/ppermute | solution.py:107
  130.5 6.9 %collective-permute-start.40 = (f32[256,256]{0,1:T(8,128)S(1)}, f32[256,256]{0,1:T(8,128)S(1)}, u32[]{:S(2)}, u32[]{:S(2)}) collective-permute-start(f32[256,256]{0,1:T(8,128)S(1)} %get-tuple-element.23), channel_id=1, source_target_pairs={{2,1},{3,2},{6,5},{7,6},{10,9},{11,10},{14,13},{15,14},{18,17},{19... | collective-permute-start | bytes 786440 | tf_op jit(solution)/shard_map/ppermute | solution.py:108
  131.7 11.7 %collective-permute-start.20 = (f32[256,256]{0,1:T(8,128)S(1)}, f32[256,256]{0,1:T(8,128)S(1)}, u32[]{:S(2)}, u32[]{:S(2)}) collective-permute-start(f32[256,256]{0,1:T(8,128)S(1)} %get-tuple-element.12), channel_id=1, source_target_pairs={{0,1},{1,2},{2,3},{4,5},{5,6},{6,7},{8,9},{9,10},{10,11},{12,13},{... | collective-permute-start | bytes 786440 | tf_op jit(solution)/shard_map/ppermute | solution.py:107
  136.1 8.3 %collective-permute-start.23 = (f32[256,256]{0,1:T(8,128)S(1)}, f32[256,256]{0,1:T(8,128)S(1)}, u32[]{:S(2)}, u32[]{:S(2)}) collective-permute-start(f32[256,256]{0,1:T(8,128)S(1)} %get-tuple-element.11), channel_id=1, source_target_pairs={{1,0},{2,1},{3,2},{5,4},{6,5},{7,6},{9,8},{10,9},{11,10},{13,12},{... | collective-permute-start | bytes 786440 | tf_op jit(solution)/shard_map/ppermute | solution.py:108
  137.5 10.1 %collective-permute-start.38 = (f32[256,256]{0,1:T(8,128)S(1)}, f32[256,256]{0,1:T(8,128)S(1)}, u32[]{:S(2)}, u32[]{:S(2)}) collective-permute-start(f32[256,256]{0,1:T(8,128)S(1)} %get-tuple-element.22), channel_id=1, source_target_pairs={{0,1},{1,2},{2,3},{4,5},{5,6},{6,7},{8,9},{9,10},{10,11},{12,13},{... | collective-permute-start | bytes 786440 | tf_op jit(solution)/shard_map/ppermute | solution.py:107
  142.1 8.3 %collective-permute-start.41 = (f32[256,256]{0,1:T(8,128)S(1)}, f32[256,256]{0,1:T(8,128)S(1)}, u32[]{:S(2)}, u32[]{:S(2)}) collective-permute-start(f32[256,256]{0,1:T(8,128)S(1)} %get-tuple-element.21), channel_id=1, source_target_pairs={{1,0},{2,1},{3,2},{5,4},{6,5},{7,6},{9,8},{10,9},{11,10},{13,12},{... | collective-permute-start | bytes 786440 | tf_op jit(solution)/shard_map/ppermute | solution.py:108
  (14 other events, 77.7 us)
